TPU v7x, 32 devices: a whole 2x2x4 slice. The times are simulated.
32 devices in a mesh: groups: 2 (over y), points: 4 (over z), centers: 4 (over x, core).
Axes of the slice: x: 2, y: 2, z: 4, core: 2. Of those that a mesh axis runs over, the one named last changes fastest.
Arguments:
- train_points: bfloat16 [8192, 512], P(('groups', 'points')), parts along dimension 0, may hold values from -6 to 6
- saved_preds: float32 [8192, 128], P(('groups', 'points')), parts along dimension 0, may hold values from -6 to 6
- targets: float32 [8192, 128], P(('groups', 'points')), parts along dimension 0, may hold values from -6 to 6
- huber_delta: float32 [256], P('groups'), parts along dimension 0, may hold values from 0.3 to 3
- center_pos: bfloat16 [16384, 512], P(('groups', 'points', 'centers')), parts along dimension 0, may hold values from -6 to 6
- coefficients: bfloat16 [16384, 128], P(('groups', 'points', 'centers')), parts along dimension 0, may hold values from -0.8984375 to 0.8984375
- spread: bfloat16 [16384], P(('groups', 'points', 'centers')), parts along dimension 0, may hold values from 0.5 to 2
Outputs:
- grad_centers: float32 [16384, 512], P(('groups', 'points', 'centers')), parts along dimension 0
- grad_coef: float32 [16384, 128], P(('groups', 'points', 'centers')), parts along dimension 0
There are 2 independent parts, one for each index of `groups`. A program takes and returns all parts, laid end to end along the dimension named above; each array names one. Nothing has to cross between parts.
All inputs are finite; a program needn't handle non-finite values.
Results may differ from a plain program's by a relative error of at most 0.0003.
Values may be sent and summed in bfloat16 or wider, within the bound.
No kernel may reach another device: no remote copies, remote signals or barrier semaphores. Data moves between devices by JAX's collectives and lax.ppermute only.
A program may use at most 64 MiB of HBM per device.

v0:
```python
import jax
import jax.numpy as jnp
from jax import lax
from jax.sharding import PartitionSpec as P


def per_device(train_points, saved_preds, targets, huber_delta, center_pos, coefficients, spread):
    n_points, in_width = train_points.shape
    whole_pos, whole_coef, whole_rates = (
        lax.all_gather(center_pos, "points", axis=0, tiled=True),
        lax.all_gather(coefficients, "points", axis=0, tiled=True),
        lax.all_gather(spread, "points", axis=0, tiled=True),
    )
    center_sq = jnp.sum(jnp.square(whole_pos.astype(jnp.float32)), axis=1)
    rates = whole_rates.astype(jnp.float32)
    panel_width = whole_pos.shape[0]
    out_width = whole_coef.shape[1]
    block_rows = min(512, n_points)
    block_count = n_points // block_rows
    point_blocks = train_points.reshape(block_count, block_rows, in_width)

    def kernel_of(row_block):
        point_sq = jnp.sum(jnp.square(row_block.astype(jnp.float32)), axis=1)
        cross = lax.dot_general(
            row_block, whole_pos, (((1,), (1,)), ((), ())), preferred_element_type=jnp.float32
        )
        dist = point_sq[:, None] + center_sq[None, :] - 2.0 * cross
        return jnp.exp(-rates[None, :] * dist / in_width).astype(jnp.bfloat16)

    kernels = lax.map(kernel_of, point_blocks)
    partial_pred = jnp.dot(
        kernels.reshape(n_points, panel_width), whole_coef, preferred_element_type=jnp.float32
    )
    panel_pred = lax.psum(partial_pred, "centers")
    residual = panel_pred + saved_preds - targets
    cotangent = (residual / jnp.sqrt(1.0 + jnp.square(residual / huber_delta[None, :]))).astype(
        jnp.bfloat16
    )
    cot_blocks = cotangent.reshape(block_count, block_rows, out_width)

    def coef_term(kernel, cot_block):
        return lax.dot_general(
            kernel, cot_block, (((0,), (0,)), ((), ())), preferred_element_type=jnp.float32
        )

    def moment_terms(kernel, cot_block, row_block):
        mixing = lax.dot_general(
            cot_block, whole_coef, (((1,), (1,)), ((), ())), preferred_element_type=jnp.float32
        )
        weights = (kernel.astype(jnp.float32) * mixing).astype(jnp.bfloat16)
        totals = jnp.sum(weights.astype(jnp.float32), axis=0)
        moment = lax.dot_general(
            weights, row_block, (((0,), (0,)), ((), ())), preferred_element_type=jnp.float32
        )
        return (moment, totals)

    zero_coef = jnp.zeros((panel_width, out_width), jnp.float32)
    zero_moment = jnp.zeros((panel_width, in_width), jnp.float32)
    zero_totals = jnp.zeros((panel_width,), jnp.float32)

    def coef_pass(coef_acc, inputs):
        row_block, stored, cot_block = inputs
        return (coef_acc + coef_term(stored, cot_block), None)

    coef_acc, _ = lax.scan(coef_pass, zero_coef, (point_blocks, kernels, cot_blocks))
    grad_coef = lax.psum_scatter(coef_acc, "points", scatter_dimension=0, tiled=True)

    def moment_pass(totals, inputs):
        moment_acc, totals_acc = totals
        row_block, stored, cot_block = inputs
        moment, row_sum = moment_terms(stored, cot_block, row_block)
        return ((moment_acc + moment, totals_acc + row_sum), None)

    (moment_acc, totals_acc), _ = lax.scan(
        moment_pass, (zero_moment, zero_totals), (point_blocks, kernels, cot_blocks)
    )
    own_moment, own_totals = (
        lax.psum_scatter(moment_acc, "points", scatter_dimension=0, tiled=True),
        lax.psum_scatter(totals_acc, "points", scatter_dimension=0, tiled=True),
    )
    own_rates = spread.astype(jnp.float32)
    grad_centers = (2.0 * own_rates / in_width)[:, None] * (
        own_moment - own_totals[:, None] * center_pos.astype(jnp.float32)
    )
    return (grad_centers, grad_coef)


def solution(mesh):
    return jax.shard_map(
        per_device,
        mesh=mesh,
        in_specs=(
            P(("groups", "points"), None),
            P(("groups", "points"), None),
            P(("groups", "points"), None),
            P("groups"),
            P(("groups", "points", "centers"), None),
            P(("groups", "points", "centers"), None),
            P(("groups", "points", "centers")),
        ),
        out_specs=(
            P(("groups", "points", "centers"), None),
            P(("groups", "points", "centers"), None),
        ),
        check_vma=False,
    )
```

profile of v0, /device:TPU:0, one launch (start us, length us, event | category | flops | bytes accessed | tf_op | source)
XLA Modules:
  0.0 246.5 jit_solution(6114186068954046954)
XLA Ops:
  7.2 0.7 all-gather.3.cloned.1.call-update
  7.9 0.0 all-reduce.3.cloned.1.call-start
  8.0 0.7 reshape.29
  8.6 13.5 %all-gather = bf16[4,1,512]{2,1,0:T(2,128)(2,1)S(1)} all-gather(bf16[1,1,512]{2,1,0:T(2,128)(2,1)S(1)} %reshape.29), channel_id=1, replica_groups=mesh['groups'=2,'points'=4,'centers'=4] {'points'}, dimensions={0}, use_global_device_ids=true | all-gather | bytes 5120 | tf_op jit(solution)/shard_map/all_gather | solution.py:12
  22.2 22.0 %all_gather.11 = bf16[2048,128]{1,0:T(8,128)(2,1)} all-gather(bf16[512,128]{1,0:T(8,128)(2,1)} %param.18), channel_id=1, replica_groups=mesh['groups'=2,'points'=4,'centers'=4] {'points'}, dimensions={0}, use_global_device_ids=true | all-gather | bytes 655360 | tf_op jit(solution)/shard_map/all_gather | solution.py:11
  44.2 22.4 %all-gather.3.cloned.1.call-done = bf16[2048,512]{1,0:T(8,128)(2,1)} async-done(((bf16[512,512]{1,0:T(8,128)(2,1)}), bf16[2048,512]{1,0:T(8,128)(2,1)}) %all-gather.3.cloned.1.call-update) | async-done | bytes 2097168 | tf_op jit(solution)/shard_map/all_gather | solution.py:10
  66.5 2.1 multiply_reduce_fusion.1
  68.6 11.9 %while.36 = (s32[]{:T(128)}, bf16[2,512,2048]{2,1,0:T(8,128)(2,1)}, f32[1,2048]{1,0:T(1,128)S(1)}, bf16[2,512,512]{2,1,0:T(8,128)(2,1)}, f32[2048]{0:T(1024)S(1)}, /*index=5*/bf16[2048,512]{1,0:T(8,128)(2,1)}, s32[]{:T(128)}) while((s32[]{:T(128)}, bf16[2,512,2048]{2,1,0:T(8,128)(2,1)}, f32[1,2048]{1,0:T(1,128)S(1)}, ...), condition=%wide.region_3.4_spmd, body=%wide.region_1.3_spmd.sunk | while | flops 1080819200 | bytes 5264465 | solution.py:30
  68.6 1.2 multiply_reduce_fusion.3
  69.8 4.7 %fusion.33 = bf16[2,512,2048]{2,1,0:T(8,128)(2,1)} fusion(bf16[2,512,2048]{2,1,0:T(8,128)(2,1)} %get-tuple-element.330, s32[]{:T(128)} %get-tuple-element.329, bf16[2048,512]{1,0:T(8,128)(2,1)} %get-tuple-element.341, f32[2048]{0:T(1024)S(1)} %get-tuple-element.340, f32[512]{0:T(512)S(1)} %multiply_reduce_fusion.3, f32[2048]{0:T(1024)S(1)} %bitcast.62, ...), kind=kOutput, calls=%fused_computation.2.clone.1 | convolution fusion | flops 1080033280 | bytes 4738048 | tf_op jit(solution)/shard_map/while/body/eval_jaxpr/dot_general | solution.py:24
  74.5 1.2 multiply_reduce_fusion.3
  75.7 4.7 %fusion.33 = bf16[2,512,2048]{2,1,0:T(8,128)(2,1)} fusion(bf16[2,512,2048]{2,1,0:T(8,128)(2,1)} %get-tuple-element.330, s32[]{:T(128)} %get-tuple-element.329, bf16[2048,512]{1,0:T(8,128)(2,1)} %get-tuple-element.341, f32[2048]{0:T(1024)S(1)} %get-tuple-element.340, f32[512]{0:T(512)S(1)} %multiply_reduce_fusion.3, f32[2048]{0:T(1024)S(1)} %bitcast.62, ...), kind=kOutput, calls=%fused_computation.2.clone.1 | convolution fusion | flops 1080033280 | bytes 4738048 | tf_op jit(solution)/shard_map/while/body/eval_jaxpr/dot_general | solution.py:24
  80.5 4.5 %fusion.17 = f32[1024,128]{1,0:T(8,128)} fusion(bf16[1024,2048]{1,0:T(8,128)(2,1)} %bitcast.58, bf16[2048,128]{1,0:T(8,128)(2,1)} %all_gather.11), kind=kOutput, calls=%fused_computation.29 | convolution fusion | flops 536870912 | bytes 5242880 | tf_op jit(solution)/shard_map/dot_general | solution.py:31
  85.0 0.0 reduce-scatter.3.cloned.1.call-start
  85.1 32.1 %all-reduce.3.cloned.1.call-done = f32[1024,128]{1,0:T(8,128)} async-done(((f32[1024,128]{1,0:T(8,128)}), f32[1024,128]{1,0:T(8,128)}) %all-reduce.3.cloned.1.call-update) | async-done | bytes 524304 | tf_op jit(solution)/shard_map/psum | solution.py:34
  117.1 1.2 multiply_convert_fusion
  118.3 13.7 %while.37 = (s32[]{:T(128)}, f32[2048,512]{1,0:T(8,128)}, f32[2048]{0:T(1024)S(1)}, bf16[2,512,2048]{2,1,0:T(8,128)(2,1)}, bf16[2,512,128]{2,1,0:T(8,128)(2,1)S(...) while((s32[]{:T(128)}, f32[2048,512]{1,0:T(8,128)}, ...), condition=%wide.region_7.8_spmd.clone, body=%wide.region_5.7_spmd.clone.sunk | while | flops 1349519360 | bytes 15893612 | solution.py:74
  118.3 2.5 %convert_reduce_fusion.2 = (f32[2048]{0:T(1024)S(1)}, bf16[512,2048]{1,0:T(8,128)(2,1)S(1)}) fusion(bf16[2048,128]{1,0:T(8,128)(2,1)} %get-tuple-element.366, bf16[2,512,128]{2,1,0:T(8,128)(2,1)S(1)} %get-tuple-element.365, s32[]{:T(128)} %get-tuple-element.352, bf16[2,512,2048]{2,1,0:T(8,128)(2,1)} %get-tuple-element.364), kind=kOutput, calls=%fused_computation.10.clone.1 | convolution fusion | flops 273676288 | bytes 4858880 | tf_op jit(solution)/shard_map/while/body/eval_jaxpr/dot_general | solution.py:47
  120.8 3.2 %select_add_fusion.4 = f32[2048,512]{1,0:T(8,128)} fusion(f32[2048,512]{1,0:T(8,128)} %get-tuple-element.353, bf16[512,2048]{1,0:T(8,128)(2,1)S(1)} %get-tuple-element.316, pred[]{:T(512)S(6)} %compare.6, bf16[2,512,512]{2,1,0:T(8,128)(2,1)S(1)} %get-tuple-element.367, s32[]{:T(128)} %get-tuple-element.352), kind=kOutput, calls=%fused_computation.9.clone.1 | convolution fusion | flops 1075838976 | bytes 11010053 | tf_op jit(solution)/shard_map/while/body/eval_jaxpr/dot_general | solution.py:52
  124.1 2.5 %convert_reduce_fusion.2 = (f32[2048]{0:T(1024)S(1)}, bf16[512,2048]{1,0:T(8,128)(2,1)S(1)}) fusion(bf16[2048,128]{1,0:T(8,128)(2,1)} %get-tuple-element.366, bf16[2,512,128]{2,1,0:T(8,128)(2,1)S(1)} %get-tuple-element.365, s32[]{:T(128)} %get-tuple-element.352, bf16[2,512,2048]{2,1,0:T(8,128)(2,1)} %get-tuple-element.364), kind=kOutput, calls=%fused_computation.10.clone.1 | convolution fusion | flops 273676288 | bytes 4858880 | tf_op jit(solution)/shard_map/while/body/eval_jaxpr/dot_general | solution.py:47
  126.6 5.4 %select_add_fusion.4 = f32[2048,512]{1,0:T(8,128)} fusion(f32[2048,512]{1,0:T(8,128)} %get-tuple-element.353, bf16[512,2048]{1,0:T(8,128)(2,1)S(1)} %get-tuple-element.316, pred[]{:T(512)S(6)} %compare.6, bf16[2,512,512]{2,1,0:T(8,128)(2,1)S(1)} %get-tuple-element.367, s32[]{:T(128)} %get-tuple-element.352), kind=kOutput, calls=%fused_computation.9.clone.1 | convolution fusion | flops 1075838976 | bytes 11010053 | tf_op jit(solution)/shard_map/while/body/eval_jaxpr/dot_general | solution.py:52
  132.1 0.0 reduce-scatter.5.cloned.1.call-start
  132.2 5.4 %while.38 = (s32[]{:T(128)}, f32[2048,128]{1,0:T(8,128)S(1)}, bf16[2,512,2048]{2,1,0:T(8,128)(2,1)}, bf16[2,512,128]{2,1,0:T(8,128)(2,1)S(1)}, s32[]{:T(128)}, /*index=5*/s32[]{:T(128)}) while((s32[]{:T(128)}, f32[2048,128]{1,0:T(8,128)S(1)}, bf16[2,512,2048]{2,1,0:T(8,128)(2,1)}, bf16[2,512,128]{2,1,0:T(8,128)(2,1)S(1)}, ...), condition=%wide.region_11.12_spmd.clone, body=%wide.region_10.11_spmd.clone.sunk | while | flops 268959744 | bytes 4326479 | solution.py:65
  132.2 2.7 %convolution_add_fusion.2 = f32[2048,128]{1,0:T(8,128)S(1)} fusion(bf16[2,512,2048]{2,1,0:T(8,128)(2,1)} %get-tuple-element.384, s32[]{:T(128)} %get-tuple-element.376, f32[2048,128]{1,0:T(8,128)S(1)} %get-tuple-element.377, pred[]{:T(512)S(6)} %compare.7, bf16[2,512,128]{2,1,0:T(8,128)(2,1)S(1)} %get-tuple-element.385), kind=kOutput, calls=%fused_computation.18.clone.1 | convolution fusion | flops 268959744 | bytes 4326401 | tf_op jit(solution)/shard_map/while/body/eval_jaxpr/dot_general | solution.py:42
  134.9 2.6 %convolution_add_fusion.2 = f32[2048,128]{1,0:T(8,128)S(1)} fusion(bf16[2,512,2048]{2,1,0:T(8,128)(2,1)} %get-tuple-element.384, s32[]{:T(128)} %get-tuple-element.376, f32[2048,128]{1,0:T(8,128)S(1)} %get-tuple-element.377, pred[]{:T(512)S(6)} %compare.7, bf16[2,512,128]{2,1,0:T(8,128)(2,1)S(1)} %get-tuple-element.385), kind=kOutput, calls=%fused_computation.18.clone.1 | convolution fusion | flops 268959744 | bytes 4326401 | tf_op jit(solution)/shard_map/while/body/eval_jaxpr/dot_general | solution.py:42
  137.6 1.0 copy-done
  138.6 0.6 dynamic-slice
  139.8 12.4 %all-reduce = f32[2048]{0:T(1024)S(1)} all-reduce(f32[2048]{0:T(1024)S(1)} %get-tuple-element.136), channel_id=3, replica_groups=mesh['groups'=2,'points'=4,'centers'=4] {'points'}, use_global_device_ids=true, to_apply=%region_9.10.clone | all-reduce | flops 2048 | bytes 16384
  152.2 0.1 dynamic-slice.1
  152.3 57.2 %reduce-scatter.3.cloned.1.call-done = f32[512,512]{1,0:T(8,128)} async-done(((f32[2048,512]{1,0:T(8,128)}), f32[512,512]{1,0:T(8,128)}) %reduce-scatter.3.cloned.1.call-update) | async-done | bytes 1048592 | tf_op jit(solution)/shard_map/reduce_scatter | solution.py:78
  209.5 2.4 subtract_multiply_fusion
  211.9 28.1 %reduce-scatter.5.cloned.1.call-done = f32[512,128]{1,0:T(8,128)} async-done(((f32[2048,128]{1,0:T(8,128)}), f32[512,128]{1,0:T(8,128)}) %reduce-scatter.5.cloned.1.call-update) | async-done | bytes 262160 | tf_op jit(solution)/shard_map/reduce_scatter | solution.py:66
  (27 shorter events, 0.2 us)
Async XLA Ops:
  7.2 59.4 %all-gather.3.cloned.1.call-start = ((), (), s32[]{:S(2)}) async-start(), calls=%async_computation.2 | async-start | bytes 2621440 | tf_op jit(solution)/shard_map/all_gather | solution.py:10
  7.9 109.2 %all-reduce.3.cloned.1.call-start = ((), (), s32[]{:S(2)}) async-start(), calls=%async_computation.3 | async-start | bytes 1048576 | tf_op jit(solution)/shard_map/psum | solution.py:34
  80.5 36.7 %copy-start.3 = (f32[1024,128]{1,0:T(8,128)S(1)}, f32[1024,128]{1,0:T(8,128)}, u32[]{:S(2)}) copy-start(f32[1024,128]{1,0:T(8,128)} %param.15) | copy-start | bytes 1572868
  80.5 36.7 %copy-start.4 = (f32[1024,128]{1,0:T(8,128)S(1)}, f32[1024,128]{1,0:T(8,128)}, u32[]{:S(2)}) copy-start(f32[1024,128]{1,0:T(8,128)} %param.14) | copy-start | bytes 1572868
  80.5 36.7 %copy-start.6 = (f32[128]{0:T(128)S(1)}, f32[128]{0:T(128)}, u32[]{:S(2)}) copy-start(f32[128]{0:T(128)} %param.16) | copy-start | bytes 1540
  80.5 37.8 %copy-start.1 = (bf16[2,512,512]{2,1,0:T(8,128)(2,1)S(1)}, bf16[2,512,512]{2,1,0:T(8,128)(2,1)}, u32[]{:S(2)}) copy-start(bf16[2,512,512]{2,1,0:T(8,128)(2,1)} %get-tuple-element.397) | copy-start | bytes 3145732
  85.0 124.5 %reduce-scatter.3.cloned.1.call-start = ((), (), s32[]{:S(2)}) async-start(), calls=%async_computation.4 | async-start | bytes 5242880 | tf_op jit(solution)/shard_map/reduce_scatter | solution.py:78
  132.1 108.0 %reduce-scatter.5.cloned.1.call-start = ((), (), s32[]{:S(2)}) async-start(), calls=%async_computation.5 | async-start | bytes 1310720 | tf_op jit(solution)/shard_map/reduce_scatter | solution.py:66
  132.1 6.4 %copy-start.7 = (u32[32]{0:T(128)S(1)}, u32[32]{0:T(128)}, u32[]{:S(2)}) copy-start(u32[32]{0:T(128)} %constant.66) | copy-start | bytes 388
  132.1 7.7 %copy-start.5 = (bf16[512]{0:T(512)(128)(2,1)S(1)}, bf16[512]{0:T(512)(128)(2,1)}, u32[]{:S(2)}) copy-start(bf16[512]{0:T(512)(128)(2,1)} %param.19) | copy-start | bytes 3076
  132.1 77.4 %copy-start.2 = (bf16[512,512]{1,0:T(8,128)(2,1)S(1)}, bf16[512,512]{1,0:T(8,128)(2,1)}, u32[]{:S(2)}) copy-start(bf16[512,512]{1,0:T(8,128)(2,1)} %param.17) | copy-start | bytes 1572868
  137.5 1.0 copy-start
Sparse Core Ops, SparseCore 0:
  9.6 56.9 all-gather.2
  85.1 31.9 all-reduce.2
  132.2 77.2 reduce-scatter.2
  212.3 27.6 reduce-scatter.4
where the time goes:
time: 247 us
  waiting for transfers between devices  140 us (57%)
  blocking collectives  47.9 us (19%)
  matrix products  32.9 us (13%)
  between operations  14.6 us (6%)
  other arithmetic  8.14 us (3%)
    reduce_scatter x1, waiting for transfers between devices, per_device(): lax.psum_scatter(moment_acc, 'points', scatter_dimension=0, tiled=True)  57.2 us
    psum x1, waiting for transfers between devices, per_device(): panel_pred = lax.psum(partial_pred, 'centers')  32.1 us
    reduce_scatter x1, waiting for transfers between devices, per_device(): lax.psum_scatter(coef_acc, 'points', scatter_dimension=0, tiled=True)  28.1 us
    all_gather x1, waiting for transfers between devices, per_device(): lax.all_gather(center_pos, 'points', axis=0, tiled=True)  22.4 us
    all_gather x1, blocking collectives, per_device(): lax.all_gather(coefficients, 'points', axis=0, tiled=True)  22 us
    all_gather x1, blocking collectives, per_device(): lax.all_gather(spread, 'points', axis=0, tiled=True)  13.5 us
    unnamed x1, blocking collectives  12.4 us
    dot_general x2, matrix products, kernel_of(): lax.dot_general(row_block, whole_pos, (((1,), (1,)), ((), ())), preferred...  9.42 us
  transfers between devices with their start and end apart: 4, of which 4 were waited for; matrix products, arithmetic and copies ran while one was open for 4% of the time, Pallas kernels for 0%

commit v1 on v0

v1 whole, which is shorter than its diff:
```python
import jax
import jax.numpy as jnp
from jax import lax
from jax.sharding import PartitionSpec as P


def swap(a, axis, size, d):
    return lax.ppermute(a, axis, [(i, i ^ d) for i in range(size)])


def solution(mesh):
    nz, nc = mesh.shape["points"], mesh.shape["centers"]

    def per_device(train_points, saved_preds, targets, huber_delta, center_pos, coefficients, spread):
        n_rows, in_width = train_points.shape
        own_centers, out_width = coefficients.shape
        piece = n_rows // nc
        c = lax.axis_index("centers")

        def row_piece(a, d):
            return lax.dynamic_slice_in_dim(a, (c ^ d) * piece, piece)

        own = row_piece(train_points, 0)
        layer = {dz: own if dz == 0 else swap(own, "points", nz, dz) for dz in range(nz)}

        spread_rows = own_centers // 128
        side = jnp.concatenate(
            [coefficients, jnp.pad(spread.reshape(spread_rows, 128), ((0, 16 - spread_rows), (0, 0)))]
        )
        pos, extra = {0: center_pos}, {0: side}
        for d in range(2, nc, 2):
            pos[d], extra[d] = swap(center_pos, "centers", nc, d), swap(side, "centers", nc, d)
        for d in range(0, nc, 2):
            pos[d + 1], extra[d + 1] = swap(pos[d], "centers", nc, 1), swap(extra[d], "centers", nc, 1)
        coef = {d: extra[d][:own_centers] for d in range(nc)}
        rate = {
            d: extra[d][own_centers : own_centers + spread_rows].reshape(own_centers).astype(jnp.float32)
            for d in range(nc)
        }
        center_sq = {d: jnp.sum(jnp.square(pos[d].astype(jnp.float32)), axis=1) for d in range(nc)}

        def partial_pred(rows):
            row_sq = jnp.sum(jnp.square(rows.astype(jnp.float32)), axis=1)
            total = 0.0
            for d in range(nc):
                cross = lax.dot_general(
                    rows, pos[d], (((1,), (1,)), ((), ())), preferred_element_type=jnp.float32
                )
                dist = row_sq[:, None] + center_sq[d][None, :] - 2.0 * cross
                kernel = jnp.exp(-rate[d][None, :] * dist / in_width).astype(jnp.bfloat16)
                total = total + jnp.dot(kernel, coef[d], preferred_element_type=jnp.float32)
            return total

        pred = partial_pred(own)
        for dz in range(1, nz):
            pred = pred + swap(partial_pred(layer[dz]), "points", nz, dz)
        residual = pred + row_piece(saved_preds, 0) - row_piece(targets, 0)
        cot = (residual / jnp.sqrt(1.0 + jnp.square(residual / huber_delta[None, :]))).astype(jnp.bfloat16)

        xs, cots = {}, {}
        for dz in range(nz):
            z_cot = cot if dz == 0 else swap(cot, "points", nz, dz)
            for d in range(0, nc, 2):
                cots[dz, d] = z_cot if d == 0 else swap(z_cot, "centers", nc, d)
                if dz:
                    xs[dz, d] = layer[dz] if d == 0 else swap(layer[dz], "centers", nc, d)
            for d in range(0, nc, 2):
                cots[dz, d + 1] = swap(cots[dz, d], "centers", nc, 1)
                if dz:
                    xs[dz, d + 1] = swap(xs[dz, d], "centers", nc, 1)
            if dz == 0:
                for d in range(nc):
                    xs[0, d] = row_piece(train_points, d)
        order = sorted(xs)
        all_x = jnp.concatenate([xs[k] for k in order])
        all_cot = jnp.concatenate([cots[k] for k in order])

        nt = (((1,), (1,)), ((), ()))
        all_sq = jnp.sum(jnp.square(all_x.astype(jnp.float32)), axis=1)
        cross = lax.dot_general(center_pos, all_x, nt, preferred_element_type=jnp.float32)
        dist = all_sq[None, :] + center_sq[0][:, None] - 2.0 * cross
        own_rate = spread.astype(jnp.float32)
        kernel = jnp.exp(-own_rate[:, None] * dist / in_width).astype(jnp.bfloat16)
        grad_coef = jnp.dot(kernel, all_cot, preferred_element_type=jnp.float32)
        mixing = lax.dot_general(coefficients, all_cot, nt, preferred_element_type=jnp.float32)
        weights = (kernel.astype(jnp.float32) * mixing).astype(jnp.bfloat16)
        totals = jnp.sum(weights.astype(jnp.float32), axis=1)
        moment = jnp.dot(weights, all_x, preferred_element_type=jnp.float32)
        grad_centers = (2.0 * own_rate / in_width)[:, None] * (
            moment - totals[:, None] * center_pos.astype(jnp.float32)
        )
        return (grad_centers, grad_coef)

    return jax.shard_map(
        per_device,
        mesh=mesh,
        in_specs=(
            P(("groups", "points"), None),
            P(("groups", "points"), None),
            P(("groups", "points"), None),
            P("groups"),
            P(("groups", "points", "centers"), None),
            P(("groups", "points", "centers"), None),
            P(("groups", "points", "centers")),
        ),
        out_specs=(
            P(("groups", "points", "centers"), None),
            P(("groups", "points", "centers"), None),
        ),
        check_vma=False,
    )
```

time: 247 us -> 125 us (0.51)
  waiting for transfers between devices: 140 us -> 24.5 us
  blocking collectives: 47.9 us -> 0 us
  starting transfers between devices: 0.16 us -> 30.6 us
  local copies, waits for them, and re-layouts: 2.35 us -> 16.9 us
  between operations: 14.6 us -> 1.02 us
  matrix products: 32.9 us -> 41 us
    reduce_scatter x2 -> x0, waiting for transfers between devices: 85.3 us -> none  [the longest x1 57.2 us: per_device(): lax.psum_scatter(moment_acc, 'points', scatter_dimension=0, tiled=True)]
    all_gather x2 -> x0, blocking collectives: 35.5 us -> none  [the longest x1 22 us: per_device(): lax.all_gather(coefficients, 'points', axis=0, tiled=True)]
    psum x1 -> x0, waiting for transfers between devices: 32.1 us -> none  [per_device(): panel_pred = lax.psum(partial_pred, 'centers')]
    ppermute x0 -> x36, starting transfers between devices: none -> 30.6 us  [swap(): return lax.ppermute(a, axis, [(i, i ^ d) for i in range(size)])]
    ppermute x0 -> x36, waiting for transfers between devices: none -> 24.5 us  [swap(): return lax.ppermute(a, axis, [(i, i ^ d) for i in range(size)])]
    all_gather x1 -> x0, waiting for transfers between devices: 22.4 us -> none  [per_device(): lax.all_gather(center_pos, 'points', axis=0, tiled=True)]
    unnamed x19 -> x63, local copies, waits for them, and re-layouts: 2.35 us -> 16.2 us
    unnamed x1 -> x0, blocking collectives: 12.4 us -> none
  transfers between devices with their start and end apart: 4 -> 36, of which waited for: 4 -> 7; matrix products, arithmetic and copies ran while one was open for 4% -> 45% of each run, Pallas kernels for 0% -> 0%
where the time goes in v1:
time: 125 us
  matrix products  41 us (33%)
  starting transfers between devices  30.6 us (24%)
  waiting for transfers between devices  24.5 us (20%)
  local copies, waits for them, and re-layouts  16.9 us (14%)
  other arithmetic  10.5 us (8%)
    ppermute x36, starting transfers between devices, swap(): return lax.ppermute(a, axis, [(i, i ^ d) for i in range(size)])  30.6 us
    dot_general x16, matrix products, partial_pred(): total = total + jnp.dot(kernel, coef[d], preferred_element_type=jnp.float32)  29.1 us
    ppermute x36, waiting for transfers between devices, swap(): return lax.ppermute(a, axis, [(i, i ^ d) for i in range(size)])  24.5 us
    unnamed x63, local copies, waits for them, and re-layouts  16.2 us
    dot_general x1, matrix products, per_device(): lax.dot_general(center_pos, all_x, nt, preferred_element_type=jnp.float32)  5.27 us
    dot_general x1, matrix products, per_device(): moment = jnp.dot(weights, all_x, preferred_element_type=jnp.float32)  3.32 us
    reduce_sum x1, other arithmetic, per_device(): all_sq = jnp.sum(jnp.square(all_x.astype(jnp.float32)), axis=1)  3.08 us
  transfers between devices with their start and end apart: 36, of which 7 were waited for; matrix products, arithmetic and copies ran while one was open for 45% of the time, Pallas kernels for 0%

profile of v1, /device:TPU:0, one launch (start us, length us, event | category | flops | bytes accessed | tf_op | source)
XLA Modules:
  0.0 124.5 jit_solution(918735201438522048)
XLA Ops:
  1.9 3.1 %collective-permute-start = (bf16[256,512]{1,0:T(8,128)(2,1)S(1)}, bf16[256,512]{1,0:T(8,128)(2,1)S(1)}, u32[]{:S(2)}, u32[]{:S(2)}) collective-permute-start(bf16[256,512]{1,0:T(8,128)(2,1)S(1)} %get-tuple-element.3), channel_id=1, source_target_pairs={{0,4},{4,0},{8,12},{12,8},{1,5},{5,1},{9,13},{13,9},{2,6},{6,2},{1... | collective-permute-start | bytes 786440 | tf_op jit(solution)/shard_map/ppermute | solution.py:8
  5.0 2.6 %collective-permute-start.4 = (bf16[256,512]{1,0:T(8,128)(2,1)S(1)}, bf16[256,512]{1,0:T(8,128)(2,1)S(1)}, u32[]{:S(2)}, u32[]{:S(2)}) collective-permute-start(bf16[256,512]{1,0:T(8,128)(2,1)S(1)} %get-tuple-element.3), channel_id=1, source_target_pairs={{0,8},{4,12},{8,0},{12,4},{1,9},{5,13},{9,1},{13,5},{2,10},{6,14},... | collective-permute-start | bytes 786440 | tf_op jit(solution)/shard_map/ppermute | solution.py:8
  12.3 1.7 %dynamic-slice_dynamic-update-slice_fusion.2 = bf16[4096,512]{1,0:T(8,128)(2,1)} fusion(bf16[4096,512]{1,0:T(8,128)(2,1)} %constant_dynamic-update-slice_fusion.12, bf16[1024,512]{1,0:T(8,128)(2,1)} %param.7, s32[]{:T(128)S(6)} %select_n.16), kind=kLoop, calls=%fused_computation.154 | loop fusion | bytes 524292
  13.9 2.2 %fusion.11 = f32[256,128]{1,0:T(8,128)} fusion(bf16[512,128]{1,0:T(8,128)(2,1)} %param.12, bf16[256,512]{1,0:T(8,128)(2,1)S(1)} %get-tuple-element.3, bf16[512,512]{1,0:T(8,128)(2,1)} %param.11, f32[512]{0:T(512)S(1)} %fusion.13, f32[256]{0:T(256)S(1)} %get-tuple-element.2, f32[512]{0:T(512)S(1)} %get-tuple-element.5), kind=kOutput, calls=%fused_computation.34 | convolution fusion | flops 168558592 | bytes 1053696 | tf_op jit(solution)/shard_map/dot_general | solution.py:51
  17.6 1.7 %collective-permute-start.14 = (bf16[528,128]{1,0:T(8,128)(2,1)S(1)}, bf16[528,128]{1,0:T(8,128)(2,1)S(1)}, u32[]{:S(2)}, u32[]{:S(2)}) collective-permute-start(bf16[528,128]{1,0:T(8,128)(2,1)S(1)} %fusion.94), channel_id=1, source_target_pairs={{0,2},{1,3},{2,0},{3,1},{4,6},{5,7},{6,4},{7,5},{8,10},{9,11},{10,... | collective-permute-start | bytes 405512 | tf_op jit(solution)/shard_map/ppermute | solution.py:8
  20.6 2.6 %collective-permute-done.14 = bf16[528,128]{1,0:T(8,128)(2,1)S(1)} collective-permute-done((bf16[528,128]{1,0:T(8,128)(2,1)S(1)}, bf16[528,128]{1,0:T(8,128)(2,1)S(1)}, u32[]{:S(2)}, u32[]{:S(2)}) %collective-permute-start.14) | collective-permute-done | bytes 135200 | tf_op jit(solution)/shard_map/ppermute | solution.py:8
  23.2 1.7 %collective-permute-start.15 = (bf16[512,512]{1,0:T(8,128)(2,1)S(1)}, bf16[512,512]{1,0:T(8,128)(2,1)S(1)}, u32[]{:S(2)}, u32[]{:S(2)}) collective-permute-start(bf16[512,512]{1,0:T(8,128)(2,1)S(1)} %copy-done.2), channel_id=1, source_target_pairs={{0,2},{1,3},{2,0},{3,1},{4,6},{5,7},{6,4},{7,5},{8,10},{9,11},{10,... | collective-permute-start | bytes 1572872 | tf_op jit(solution)/shard_map/ppermute | solution.py:8
  31.9 1.5 %collective-permute-start.6 = (bf16[256,512]{1,0:T(8,128)(2,1)S(1)}, bf16[256,512]{1,0:T(8,128)(2,1)S(1)}, u32[]{:S(2)}, u32[]{:S(2)}) collective-permute-start(bf16[256,512]{1,0:T(8,128)(2,1)S(1)} %collective-permute-done.4), channel_id=1, source_target_pairs={{0,2},{1,3},{2,0},{3,1},{4,6},{5,7},{6,4},{7,5},{8,10},{9,11},{10,... | collective-permute-start | bytes 786440 | tf_op jit(solution)/shard_map/ppermute | solution.py:8
  33.6 10.2 %collective-permute-done.2 = bf16[256,512]{1,0:T(8,128)(2,1)} collective-permute-done((bf16[256,512]{1,0:T(8,128)(2,1)S(1)}, bf16[256,512]{1,0:T(8,128)(2,1)}, u32[]{:S(2)}, u32[]{:S(2)}) %collective-permute-start.2) | collective-permute-done | bytes 262176 | tf_op jit(solution)/shard_map/ppermute | solution.py:8
  43.8 1.7 %collective-permute-start.10 = (bf16[256,512]{1,0:T(8,128)(2,1)S(1)}, bf16[256,512]{1,0:T(8,128)(2,1)S(1)}, u32[]{:S(2)}, u32[]{:S(2)}) collective-permute-start(bf16[256,512]{1,0:T(8,128)(2,1)S(1)} %collective-permute-done.8), channel_id=1, source_target_pairs={{0,2},{1,3},{2,0},{3,1},{4,6},{5,7},{6,4},{7,5},{8,10},{9,11},{10,... | collective-permute-start | bytes 786440 | tf_op jit(solution)/shard_map/ppermute | solution.py:8
  45.7 2.2 %convolution_add_fusion.8 = f32[256,128]{1,0:T(8,128)} fusion(f32[256,128]{1,0:T(8,128)} %fusion.79, bf16[256,512]{1,0:T(8,128)(2,1)S(1)} %collective-permute-done, bf16[512,512]{1,0:T(8,128)(2,1)S(1)} %collective-permute-done.13, f32[256]{0:T(256)} %copy-done.9, f32[512]{0:T(512)S(1)} %multiply_reduce_fusion.3, f32[512]{0:T(512)} %negate_bitcast_fusion.2, ...), kind=kOutput, calls=%fused_computation.43 | convolution fusion | flops 168591360 | bytes 1184768 | tf_op jit(solution)/shard_map/dot_general | solution.py:51
  47.8 2.2 %convolution_add_fusion.11 = f32[256,128]{1,0:T(8,128)} fusion(f32[256,128]{1,0:T(8,128)} %fusion.11, bf16[256,512]{1,0:T(8,128)(2,1)S(1)} %get-tuple-element.3, bf16[512,512]{1,0:T(8,128)(2,1)S(1)} %collective-permute-done.13, f32[512]{0:T(512)S(1)} %multiply_reduce_fusion.3, f32[512]{0:T(512)} %negate_bitcast_fusion.2, f32[256]{0:T(256)} %copy-done.7, ...), kind=kOutput, calls=%fused_computation.47 | convolution fusion | flops 168591360 | bytes 1184768 | tf_op jit(solution)/shard_map/dot_general | solution.py:51
  50.0 2.2 %convolution_add_fusion.7 = f32[256,128]{1,0:T(8,128)} fusion(f32[256,128]{1,0:T(8,128)} %convolution_add_fusion.8, bf16[256,512]{1,0:T(8,128)(2,1)S(1)} %collective-permute-done, bf16[512,512]{1,0:T(8,128)(2,1)S(1)} %collective-permute-done.15, f32[256]{0:T(256)} %copy-done.9, f32[512]{0:T(512)S(1)} %multiply_reduce_fusion.2, ...), kind=kOutput, calls=%fused_computation.42 | convolution fusion | flops 168591360 | bytes 1184768 | tf_op jit(solution)/shard_map/dot_general | solution.py:51
  52.2 2.2 %convolution_add_fusion.10 = f32[256,128]{1,0:T(8,128)} fusion(f32[256,128]{1,0:T(8,128)} %convolution_add_fusion.11, bf16[256,512]{1,0:T(8,128)(2,1)S(1)} %get-tuple-element.3, bf16[512,512]{1,0:T(8,128)(2,1)S(1)} %collective-permute-done.15, f32[512]{0:T(512)S(1)} %multiply_reduce_fusion.2, f32[512]{0:T(512)} %negate_bitcast_fusion.1, f32[256]{0:T(256)} %copy-done.7, ...), kind=kOutput, calls=%fused_computation.46 | convolution fusion | flops 168591360 | bytes 1184768 | tf_op jit(solution)/shard_map/dot_general | solution.py:51
  54.3 2.2 %convolution_add_fusion.5 = f32[256,128]{1,0:T(8,128)} fusion(f32[256,128]{1,0:T(8,128)} %fusion.80, bf16[256,512]{1,0:T(8,128)(2,1)S(1)} %collective-permute-done.4, bf16[512,512]{1,0:T(8,128)(2,1)S(1)} %collective-permute-done.13, f32[256]{0:T(256)} %copy-done.11, f32[512]{0:T(512)S(1)} %multiply_reduce_fusion.3, f32[512]{0:T(512)} %negate_bitcast_fusion.2, ...), kind=kOutput, calls=%fused_computation.40 | convolution fusion | flops 168591360 | bytes 1184768 | tf_op jit(solution)/shard_map/dot_general | solution.py:51
  56.5 2.2 %convolution_add_fusion.4 = f32[256,128]{1,0:T(8,128)} fusion(f32[256,128]{1,0:T(8,128)} %convolution_add_fusion.5, bf16[256,512]{1,0:T(8,128)(2,1)S(1)} %collective-permute-done.4, bf16[512,512]{1,0:T(8,128)(2,1)S(1)} %collective-permute-done.15, f32[256]{0:T(256)} %copy-done.11, f32[512]{0:T(512)S(1)} %multiply_reduce_fusion.2, ...), kind=kOutput, calls=%fused_computation.39 | convolution fusion | flops 168591360 | bytes 1184768 | tf_op jit(solution)/shard_map/dot_general | solution.py:51
  58.7 2.2 %convolution_add_fusion.2 = f32[256,128]{1,0:T(8,128)} fusion(f32[256,128]{1,0:T(8,128)} %fusion.81, bf16[256,512]{1,0:T(8,128)(2,1)S(1)} %collective-permute-done.8, bf16[512,512]{1,0:T(8,128)(2,1)S(1)} %collective-permute-done.13, f32[256]{0:T(256)} %copy-done.12, f32[512]{0:T(512)S(1)} %multiply_reduce_fusion.3, f32[512]{0:T(512)} %negate_bitcast_fusion.2, ...), kind=kOutput, calls=%fused_computation.37 | convolution fusion | flops 168591360 | bytes 1184768 | tf_op jit(solution)/shard_map/dot_general | solution.py:51
  60.8 2.2 %convolution_add_fusion.1 = f32[256,128]{1,0:T(8,128)} fusion(f32[256,128]{1,0:T(8,128)} %convolution_add_fusion.2, bf16[256,512]{1,0:T(8,128)(2,1)S(1)} %collective-permute-done.8, bf16[512,512]{1,0:T(8,128)(2,1)S(1)} %collective-permute-done.15, f32[256]{0:T(256)} %copy-done.12, f32[512]{0:T(512)S(1)} %multiply_reduce_fusion.2, ...), kind=kOutput, calls=%fused_computation.36 | convolution fusion | flops 168591360 | bytes 1184768 | tf_op jit(solution)/shard_map/dot_general | solution.py:51
  63.5 1.7 %constant_dynamic-update-slice_fusion.10 = bf16[4096,512]{1,0:T(8,128)(2,1)} fusion(bf16[4096,512]{1,0:T(8,128)(2,1)} %constant_dynamic-update-slice_fusion.11, bf16[256,512]{1,0:T(8,128)(2,1)} %collective-permute-done.1), kind=kLoop, calls=%fused_computation.179 | loop fusion | bytes 524288
  65.2 1.7 %constant_dynamic-update-slice_fusion.9 = bf16[4096,512]{1,0:T(8,128)(2,1)} fusion(bf16[4096,512]{1,0:T(8,128)(2,1)} %constant_dynamic-update-slice_fusion.10, bf16[256,512]{1,0:T(8,128)(2,1)} %collective-permute-done.2), kind=kLoop, calls=%fused_computation.178 | loop fusion | bytes 524288
  67.4 1.7 %constant_dynamic-update-slice_fusion.8 = bf16[4096,512]{1,0:T(8,128)(2,1)} fusion(bf16[4096,512]{1,0:T(8,128)(2,1)} %constant_dynamic-update-slice_fusion.9, bf16[256,512]{1,0:T(8,128)(2,1)} %collective-permute-done.3), kind=kLoop, calls=%fused_computation.177 | loop fusion | bytes 524288
  78.9 3.6 %collective-permute-start.19 = (f32[256,128]{1,0:T(8,128)S(1)}, f32[256,128]{1,0:T(8,128)S(1)}, u32[]{:S(2)}, u32[]{:S(2)}) collective-permute-start(f32[256,128]{1,0:T(8,128)S(1)} %convolution_add_fusion.3), channel_id=1, source_target_pairs={{0,8},{4,12},{8,0},{12,4},{1,9},{5,13},{9,1},{13,5},{2,10},{6,14},... | collective-permute-start | bytes 393224 | tf_op jit(solution)/shard_map/ppermute | solution.py:8
  84.2 3.1 %multiply_reduce_fusion = f32[4096]{0:T(1024)S(1)} fusion(bf16[4096,512]{1,0:T(8,128)(2,1)} %constant_dynamic-update-slice_fusion), kind=kLoop, calls=%fused_computation.8 | loop fusion | flops 6287360 | bytes 4210688 | tf_op jit(solution)/shard_map/reduce_sum | solution.py:79
  87.3 5.0 %collective-permute-done.19 = f32[256,128]{1,0:T(8,128)S(1)} collective-permute-done((f32[256,128]{1,0:T(8,128)S(1)}, f32[256,128]{1,0:T(8,128)S(1)}, u32[]{:S(2)}, u32[]{:S(2)}) %collective-permute-start.19) | collective-permute-done | bytes 131104 | tf_op jit(solution)/shard_map/ppermute | solution.py:8
  92.4 1.6 %constant_dynamic-update-slice_fusion.28 = (bf16[4096,128]{1,0:T(8,128)(2,1)S(1)}, bf16[256,128]{1,0:T(8,128)(2,1)S(1)}) fusion(f32[128]{0:T(128)S(1)} %copy-done.16, f32[1024,128]{1,0:T(8,128)} %param.9, s32[]{:T(128)S(6)} %select_n.15, f32[1024,128]{1,0:T(8,128)} %param.8, f32[256,128]{1,0:T(8,128)S(1)} %collective-permute-done.20, ...), kind=kOutput, calls=%fused_computation.197 | convolution fusion | flops 168919040 | bytes 1840644 | tf_op jit(solution)/shard_map/dot_general | solution.py:51
  94.6 2.9 %collective-permute-start.24 = (bf16[256,128]{1,0:T(8,128)(2,1)S(1)}, bf16[256,128]{1,0:T(8,128)(2,1)S(1)}, u32[]{:S(2)}, u32[]{:S(2)}) collective-permute-start(bf16[256,128]{1,0:T(8,128)(2,1)S(1)} %get-tuple-element.7), channel_id=1, source_target_pairs={{0,4},{4,0},{8,12},{12,8},{1,5},{5,1},{9,13},{13,9},{2,6},{6,2},{1... | collective-permute-start | bytes 196616 | tf_op jit(solution)/shard_map/ppermute | solution.py:8
  98.5 5.3 %fusion.4 = bf16[512,4096]{0,1:T(8,128)(2,1)S(1)} fusion(bf16[4096,512]{1,0:T(8,128)(2,1)} %constant_dynamic-update-slice_fusion, bf16[512,512]{1,0:T(8,128)(2,1)S(1)} %copy-done.2, f32[512]{0:T(512)S(1)} %fusion.13, f32[4096]{0:T(1024)S(1)} %multiply_reduce_fusion, f32[512]{0:T(512)S(1)} %copy-done.6), kind=kOutput, calls=%fused_computation.6 | convolution fusion | flops 2160066560 | bytes 8933376 | tf_op jit(solution)/shard_map/dot_general | solution.py:80
  105.3 1.6 %collective-permute-start.26 = (bf16[256,128]{1,0:T(8,128)(2,1)S(1)}, bf16[256,128]{1,0:T(8,128)(2,1)S(1)}, u32[]{:S(2)}, u32[]{:S(2)}) collective-permute-start(bf16[256,128]{1,0:T(8,128)(2,1)S(1)} %collective-permute-done.24), channel_id=1, source_target_pairs={{0,2},{1,3},{2,0},{3,1},{4,6},{5,7},{6,4},{7,5},{8,10},{9,11},{10,... | collective-permute-start | bytes 196616 | tf_op jit(solution)/shard_map/ppermute | solution.py:8
  107.4 2.5 %collective-permute-done.32 = bf16[256,128]{1,0:T(8,128)(2,1)S(1)} collective-permute-done((bf16[256,128]{1,0:T(8,128)(2,1)S(1)}, bf16[256,128]{1,0:T(8,128)(2,1)S(1)}, u32[]{:S(2)}, u32[]{:S(2)}) %collective-permute-start.32) | collective-permute-done | bytes 65568 | tf_op jit(solution)/shard_map/ppermute | solution.py:8
  112.6 1.6 %collective-permute-done.30 = bf16[256,128]{1,0:T(8,128)(2,1)S(1)} collective-permute-done((bf16[256,128]{1,0:T(8,128)(2,1)S(1)}, bf16[256,128]{1,0:T(8,128)(2,1)S(1)}, u32[]{:S(2)}, u32[]{:S(2)}) %collective-permute-start.30) | collective-permute-done | bytes 65568 | tf_op jit(solution)/shard_map/ppermute | solution.py:8
  117.0 2.0 %fusion.139 = f32[512,128]{1,0:T(8,128)} fusion(bf16[512,4096]{0,1:T(8,128)(2,1)S(1)} %fusion.4, bf16[4096,128]{1,0:T(8,128)(2,1)S(1)} %constant_dynamic-update-slice_fusion.13), kind=kOutput, calls=%fused_computation.236 | convolution fusion | flops 536870912 | bytes 5505024 | tf_op jit(solution)/shard_map/dot_general | solution.py:84
  121.2 3.3 %fusion.5 = f32[512,512]{1,0:T(8,128)} fusion(bf16[512,4096]{0,1:T(8,128)(2,1)S(1)} %get-tuple-element.9, bf16[4096,512]{1,0:T(8,128)(2,1)S(1)} %copy-done, bf16[512,512]{1,0:T(8,128)(2,1)S(1)} %copy-done.2, f32[512]{0:T(512)S(1)} %get-tuple-element.8, f32[512]{0:T(512)S(1)} %copy-done.4), kind=kOutput, calls=%fused_computation.12 | convolution fusion | flops 2148532224 | bytes 9965568 | tf_op jit(solution)/shard_map/dot_general | solution.py:88
  (139 shorter events, 39.7 us)
Async XLA Ops:
  1.9 23.6 %collective-permute-start = (bf16[256,512]{1,0:T(8,128)(2,1)S(1)}, bf16[256,512]{1,0:T(8,128)(2,1)S(1)}, u32[]{:S(2)}, u32[]{:S(2)}) collective-permute-start(bf16[256,512]{1,0:T(8,128)(2,1)S(1)} %get-tuple-element.3), channel_id=1, source_target_pairs={{0,4},{4,0},{8,12},{12,8},{1,5},{5,1},{9,13},{13,9},{2,6},{6,2},{1... | collective-permute-start | bytes 786440 | tf_op jit(solution)/shard_map/ppermute | solution.py:8
  5.0 21.9 %collective-permute-start.4 = (bf16[256,512]{1,0:T(8,128)(2,1)S(1)}, bf16[256,512]{1,0:T(8,128)(2,1)S(1)}, u32[]{:S(2)}, u32[]{:S(2)}) collective-permute-start(bf16[256,512]{1,0:T(8,128)(2,1)S(1)} %get-tuple-element.3), channel_id=1, source_target_pairs={{0,8},{4,12},{8,0},{12,4},{1,9},{5,13},{9,1},{13,5},{2,10},{6,14},... | collective-permute-start | bytes 786440 | tf_op jit(solution)/shard_map/ppermute | solution.py:8
  7.6 21.1 %collective-permute-start.8 = (bf16[256,512]{1,0:T(8,128)(2,1)S(1)}, bf16[256,512]{1,0:T(8,128)(2,1)S(1)}, u32[]{:S(2)}, u32[]{:S(2)}) collective-permute-start(bf16[256,512]{1,0:T(8,128)(2,1)S(1)} %get-tuple-element.3), channel_id=1, source_target_pairs={{0,12},{4,8},{8,4},{12,0},{1,13},{5,9},{9,5},{13,1},{2,14},{6,10},... | collective-permute-start | bytes 786440 | tf_op jit(solution)/shard_map/ppermute | solution.py:8
  8.5 9.1 %collective-permute-start.12 = (bf16[528,128]{1,0:T(8,128)(2,1)S(1)}, bf16[528,128]{1,0:T(8,128)(2,1)}, u32[]{:S(2)}, u32[]{:S(2)}) collective-permute-start(bf16[528,128]{1,0:T(8,128)(2,1)S(1)} %fusion.94), channel_id=1, source_target_pairs={{0,1},{1,0},{2,3},{3,2},{4,5},{5,4},{6,7},{7,6},{8,9},{9,8},{10,11... | collective-permute-start | bytes 405512 | tf_op jit(solution)/shard_map/ppermute | solution.py:8
  8.6 23.3 %collective-permute-start.13 = (bf16[512,512]{1,0:T(8,128)(2,1)}, bf16[512,512]{1,0:T(8,128)(2,1)S(1)}, u32[]{:S(2)}, u32[]{:S(2)}) collective-permute-start(bf16[512,512]{1,0:T(8,128)(2,1)} %param.11), channel_id=1, source_target_pairs={{0,1},{1,0},{2,3},{3,2},{4,5},{5,4},{6,7},{7,6},{8,9},{9,8},{10,11... | collective-permute-start | bytes 1572872 | tf_op jit(solution)/shard_map/ppermute | solution.py:8
  17.6 5.6 %collective-permute-start.14 = (bf16[528,128]{1,0:T(8,128)(2,1)S(1)}, bf16[528,128]{1,0:T(8,128)(2,1)S(1)}, u32[]{:S(2)}, u32[]{:S(2)}) collective-permute-start(bf16[528,128]{1,0:T(8,128)(2,1)S(1)} %fusion.94), channel_id=1, source_target_pairs={{0,2},{1,3},{2,0},{3,1},{4,6},{5,7},{6,4},{7,5},{8,10},{9,11},{10,... | collective-permute-start | bytes 405512 | tf_op jit(solution)/shard_map/ppermute | solution.py:8
  23.2 22.3 %collective-permute-start.15 = (bf16[512,512]{1,0:T(8,128)(2,1)S(1)}, bf16[512,512]{1,0:T(8,128)(2,1)S(1)}, u32[]{:S(2)}, u32[]{:S(2)}) collective-permute-start(bf16[512,512]{1,0:T(8,128)(2,1)S(1)} %copy-done.2), channel_id=1, source_target_pairs={{0,2},{1,3},{2,0},{3,1},{4,6},{5,7},{6,4},{7,5},{8,10},{9,11},{10,... | collective-permute-start | bytes 1572872 | tf_op jit(solution)/shard_map/ppermute | solution.py:8
  25.5 5.7 %collective-permute-start.16 = (bf16[528,128]{1,0:T(8,128)(2,1)S(1)}, bf16[528,128]{1,0:T(8,128)(2,1)S(1)}, u32[]{:S(2)}, u32[]{:S(2)}) collective-permute-start(bf16[528,128]{1,0:T(8,128)(2,1)S(1)} %collective-permute-done.14), channel_id=1, source_target_pairs={{0,1},{1,0},{2,3},{3,2},{4,5},{5,4},{6,7},{7,6},{8,9},{9,8},{10,11... | collective-permute-start | bytes 405512 | tf_op jit(solution)/shard_map/ppermute | solution.py:8
  26.8 36.2 %collective-permute-start.1 = (bf16[256,512]{1,0:T(8,128)(2,1)S(1)}, bf16[256,512]{1,0:T(8,128)(2,1)}, u32[]{:S(2)}, u32[]{:S(2)}) collective-permute-start(bf16[256,512]{1,0:T(8,128)(2,1)S(1)} %collective-permute-done), channel_id=1, source_target_pairs={{0,1},{1,0},{2,3},{3,2},{4,5},{5,4},{6,7},{7,6},{8,9},{9,8},{10,11... | collective-permute-start | bytes 786440 | tf_op jit(solution)/shard_map/ppermute | solution.py:8
  28.7 15.1 %collective-permute-start.2 = (bf16[256,512]{1,0:T(8,128)(2,1)S(1)}, bf16[256,512]{1,0:T(8,128)(2,1)}, u32[]{:S(2)}, u32[]{:S(2)}) collective-permute-start(bf16[256,512]{1,0:T(8,128)(2,1)S(1)} %collective-permute-done), channel_id=1, source_target_pairs={{0,2},{1,3},{2,0},{3,1},{4,6},{5,7},{6,4},{7,5},{8,10},{9,11},{10,... | collective-permute-start | bytes 786440 | tf_op jit(solution)/shard_map/ppermute | solution.py:8
  31.2 38.6 %collective-permute-start.5 = (bf16[256,512]{1,0:T(8,128)(2,1)S(1)}, bf16[256,512]{1,0:T(8,128)(2,1)S(1)}, u32[]{:S(2)}, u32[]{:S(2)}) collective-permute-start(bf16[256,512]{1,0:T(8,128)(2,1)S(1)} %collective-permute-done.4), channel_id=1, source_target_pairs={{0,1},{1,0},{2,3},{3,2},{4,5},{5,4},{6,7},{7,6},{8,9},{9,8},{10,11... | collective-permute-start | bytes 786440 | tf_op jit(solution)/shard_map/ppermute | solution.py:8
  31.9 35.0 %collective-permute-start.6 = (bf16[256,512]{1,0:T(8,128)(2,1)S(1)}, bf16[256,512]{1,0:T(8,128)(2,1)S(1)}, u32[]{:S(2)}, u32[]{:S(2)}) collective-permute-start(bf16[256,512]{1,0:T(8,128)(2,1)S(1)} %collective-permute-done.4), channel_id=1, source_target_pairs={{0,2},{1,3},{2,0},{3,1},{4,6},{5,7},{6,4},{7,5},{8,10},{9,11},{10,... | collective-permute-start | bytes 786440 | tf_op jit(solution)/shard_map/ppermute | solution.py:8
  43.8 23.1 %collective-permute-start.10 = (bf16[256,512]{1,0:T(8,128)(2,1)S(1)}, bf16[256,512]{1,0:T(8,128)(2,1)S(1)}, u32[]{:S(2)}, u32[]{:S(2)}) collective-permute-start(bf16[256,512]{1,0:T(8,128)(2,1)S(1)} %collective-permute-done.8), channel_id=1, source_target_pairs={{0,2},{1,3},{2,0},{3,1},{4,6},{5,7},{6,4},{7,5},{8,10},{9,11},{10,... | collective-permute-start | bytes 786440 | tf_op jit(solution)/shard_map/ppermute | solution.py:8
  45.5 21.9 %collective-permute-start.3 = (bf16[256,512]{1,0:T(8,128)(2,1)}, bf16[256,512]{1,0:T(8,128)(2,1)}, u32[]{:S(2)}, u32[]{:S(2)}) collective-permute-start(bf16[256,512]{1,0:T(8,128)(2,1)} %collective-permute-done.2), channel_id=1, source_target_pairs={{0,1},{1,0},{2,3},{3,2},{4,5},{5,4},{6,7},{7,6},{8,9},{9,8},{10,11... | collective-permute-start | bytes 786440 | tf_op jit(solution)/shard_map/ppermute | solution.py:8
  63.0 9.8 %collective-permute-start.9 = (bf16[256,512]{1,0:T(8,128)(2,1)S(1)}, bf16[256,512]{1,0:T(8,128)(2,1)S(1)}, u32[]{:S(2)}, u32[]{:S(2)}) collective-permute-start(bf16[256,512]{1,0:T(8,128)(2,1)S(1)} %collective-permute-done.8), channel_id=1, source_target_pairs={{0,1},{1,0},{2,3},{3,2},{4,5},{5,4},{6,7},{7,6},{8,9},{9,8},{10,11... | collective-permute-start | bytes 786440 | tf_op jit(solution)/shard_map/ppermute | solution.py:8
  66.9 8.1 %collective-permute-start.17 = (bf16[512,512]{1,0:T(8,128)(2,1)S(1)}, bf16[512,512]{1,0:T(8,128)(2,1)S(1)}, u32[]{:S(2)}, u32[]{:S(2)}) collective-permute-start(bf16[512,512]{1,0:T(8,128)(2,1)S(1)} %collective-permute-done.15), channel_id=1, source_target_pairs={{0,1},{1,0},{2,3},{3,2},{4,5},{5,4},{6,7},{7,6},{8,9},{9,8},{10,11... | collective-permute-start | bytes 1572872 | tf_op jit(solution)/shard_map/ppermute | solution.py:8
  66.9 4.4 %collective-permute-start.7 = (bf16[256,512]{1,0:T(8,128)(2,1)S(1)}, bf16[256,512]{1,0:T(8,128)(2,1)S(1)}, u32[]{:S(2)}, u32[]{:S(2)}) collective-permute-start(bf16[256,512]{1,0:T(8,128)(2,1)S(1)} %collective-permute-done.6), channel_id=1, source_target_pairs={{0,1},{1,0},{2,3},{3,2},{4,5},{5,4},{6,7},{7,6},{8,9},{9,8},{10,11... | collective-permute-start | bytes 786440 | tf_op jit(solution)/shard_map/ppermute | solution.py:8
  67.4 6.8 %collective-permute-start.11 = (bf16[256,512]{1,0:T(8,128)(2,1)S(1)}, bf16[256,512]{1,0:T(8,128)(2,1)S(1)}, u32[]{:S(2)}, u32[]{:S(2)}) collective-permute-start(bf16[256,512]{1,0:T(8,128)(2,1)S(1)} %collective-permute-done.10), channel_id=1, source_target_pairs={{0,1},{1,0},{2,3},{3,2},{4,5},{5,4},{6,7},{7,6},{8,9},{9,8},{10,11... | collective-permute-start | bytes 786440 | tf_op jit(solution)/shard_map/ppermute | solution.py:8
  76.6 10.7 %collective-permute-start.18 = (f32[256,128]{1,0:T(8,128)S(1)}, f32[256,128]{1,0:T(8,128)S(1)}, u32[]{:S(2)}, u32[]{:S(2)}) collective-permute-start(f32[256,128]{1,0:T(8,128)S(1)} %convolution_add_fusion.6), channel_id=1, source_target_pairs={{0,4},{4,0},{8,12},{12,8},{1,5},{5,1},{9,13},{13,9},{2,6},{6,2},{1... | collective-permute-start | bytes 393224 | tf_op jit(solution)/shard_map/ppermute | solution.py:8
  78.9 13.5 %collective-permute-start.19 = (f32[256,128]{1,0:T(8,128)S(1)}, f32[256,128]{1,0:T(8,128)S(1)}, u32[]{:S(2)}, u32[]{:S(2)}) collective-permute-start(f32[256,128]{1,0:T(8,128)S(1)} %convolution_add_fusion.3), channel_id=1, source_target_pairs={{0,8},{4,12},{8,0},{12,4},{1,9},{5,13},{9,1},{13,5},{2,10},{6,14},... | collective-permute-start | bytes 393224 | tf_op jit(solution)/shard_map/ppermute | solution.py:8
  83.9 8.4 %collective-permute-start.20 = (f32[256,128]{1,0:T(8,128)S(1)}, f32[256,128]{1,0:T(8,128)S(1)}, u32[]{:S(2)}, u32[]{:S(2)}) collective-permute-start(f32[256,128]{1,0:T(8,128)S(1)} %convolution_add_fusion), channel_id=1, source_target_pairs={{0,12},{4,8},{8,4},{12,0},{1,13},{5,9},{9,5},{13,1},{2,14},{6,10},... | collective-permute-start | bytes 393224 | tf_op jit(solution)/shard_map/ppermute | solution.py:8
  94.0 11.4 %collective-permute-start.21 = (bf16[256,128]{1,0:T(8,128)(2,1)S(1)}, bf16[256,128]{1,0:T(8,128)(2,1)S(1)}, u32[]{:S(2)}, u32[]{:S(2)}) collective-permute-start(bf16[256,128]{1,0:T(8,128)(2,1)S(1)} %get-tuple-element.7), channel_id=1, source_target_pairs={{0,1},{1,0},{2,3},{3,2},{4,5},{5,4},{6,7},{7,6},{8,9},{9,8},{10,11... | collective-permute-start | bytes 196616 | tf_op jit(solution)/shard_map/ppermute | solution.py:8
  94.0 12.9 %collective-permute-start.22 = (bf16[256,128]{1,0:T(8,128)(2,1)S(1)}, bf16[256,128]{1,0:T(8,128)(2,1)S(1)}, u32[]{:S(2)}, u32[]{:S(2)}) collective-permute-start(bf16[256,128]{1,0:T(8,128)(2,1)S(1)} %get-tuple-element.7), channel_id=1, source_target_pairs={{0,2},{1,3},{2,0},{3,1},{4,6},{5,7},{6,4},{7,5},{8,10},{9,11},{10,... | collective-permute-start | bytes 196616 | tf_op jit(solution)/shard_map/ppermute | solution.py:8
  94.6 10.7 %collective-permute-start.24 = (bf16[256,128]{1,0:T(8,128)(2,1)S(1)}, bf16[256,128]{1,0:T(8,128)(2,1)S(1)}, u32[]{:S(2)}, u32[]{:S(2)}) collective-permute-start(bf16[256,128]{1,0:T(8,128)(2,1)S(1)} %get-tuple-element.7), channel_id=1, source_target_pairs={{0,4},{4,0},{8,12},{12,8},{1,5},{5,1},{9,13},{13,9},{2,6},{6,2},{1... | collective-permute-start | bytes 196616 | tf_op jit(solution)/shard_map/ppermute | solution.py:8
  97.5 9.5 %collective-permute-start.28 = (bf16[256,128]{1,0:T(8,128)(2,1)S(1)}, bf16[256,128]{1,0:T(8,128)(2,1)S(1)}, u32[]{:S(2)}, u32[]{:S(2)}) collective-permute-start(bf16[256,128]{1,0:T(8,128)(2,1)S(1)} %get-tuple-element.7), channel_id=1, source_target_pairs={{0,8},{4,12},{8,0},{12,4},{1,9},{5,13},{9,1},{13,5},{2,10},{6,14},... | collective-permute-start | bytes 196616 | tf_op jit(solution)/shard_map/ppermute | solution.py:8
  103.8 6.2 %collective-permute-start.32 = (bf16[256,128]{1,0:T(8,128)(2,1)S(1)}, bf16[256,128]{1,0:T(8,128)(2,1)S(1)}, u32[]{:S(2)}, u32[]{:S(2)}) collective-permute-start(bf16[256,128]{1,0:T(8,128)(2,1)S(1)} %get-tuple-element.7), channel_id=1, source_target_pairs={{0,12},{4,8},{8,4},{12,0},{1,13},{5,9},{9,5},{13,1},{2,14},{6,10},... | collective-permute-start | bytes 196616 | tf_op jit(solution)/shard_map/ppermute | solution.py:8
  105.3 6.7 %collective-permute-start.25 = (bf16[256,128]{1,0:T(8,128)(2,1)S(1)}, bf16[256,128]{1,0:T(8,128)(2,1)S(1)}, u32[]{:S(2)}, u32[]{:S(2)}) collective-permute-start(bf16[256,128]{1,0:T(8,128)(2,1)S(1)} %collective-permute-done.24), channel_id=1, source_target_pairs={{0,1},{1,0},{2,3},{3,2},{4,5},{5,4},{6,7},{7,6},{8,9},{9,8},{10,11... | collective-permute-start | bytes 196616 | tf_op jit(solution)/shard_map/ppermute | solution.py:8
  105.3 6.8 %collective-permute-start.26 = (bf16[256,128]{1,0:T(8,128)(2,1)S(1)}, bf16[256,128]{1,0:T(8,128)(2,1)S(1)}, u32[]{:S(2)}, u32[]{:S(2)}) collective-permute-start(bf16[256,128]{1,0:T(8,128)(2,1)S(1)} %collective-permute-done.24), channel_id=1, source_target_pairs={{0,2},{1,3},{2,0},{3,1},{4,6},{5,7},{6,4},{7,5},{8,10},{9,11},{10,... | collective-permute-start | bytes 196616 | tf_op jit(solution)/shard_map/ppermute | solution.py:8
  106.9 4.6 %collective-permute-start.23 = (bf16[256,128]{1,0:T(8,128)(2,1)S(1)}, bf16[256,128]{1,0:T(8,128)(2,1)S(1)}, u32[]{:S(2)}, u32[]{:S(2)}) collective-permute-start(bf16[256,128]{1,0:T(8,128)(2,1)S(1)} %collective-permute-done.22), channel_id=1, source_target_pairs={{0,1},{1,0},{2,3},{3,2},{4,5},{5,4},{6,7},{7,6},{8,9},{9,8},{10,11... | collective-permute-start | bytes 196616 | tf_op jit(solution)/shard_map/ppermute | solution.py:8
  107.1 8.8 %collective-permute-start.29 = (bf16[256,128]{1,0:T(8,128)(2,1)S(1)}, bf16[256,128]{1,0:T(8,128)(2,1)S(1)}, u32[]{:S(2)}, u32[]{:S(2)}) collective-permute-start(bf16[256,128]{1,0:T(8,128)(2,1)S(1)} %collective-permute-done.28), channel_id=1, source_target_pairs={{0,1},{1,0},{2,3},{3,2},{4,5},{5,4},{6,7},{7,6},{8,9},{9,8},{10,11... | collective-permute-start | bytes 196616 | tf_op jit(solution)/shard_map/ppermute | solution.py:8
  110.0 4.3 %collective-permute-start.30 = (bf16[256,128]{1,0:T(8,128)(2,1)S(1)}, bf16[256,128]{1,0:T(8,128)(2,1)S(1)}, u32[]{:S(2)}, u32[]{:S(2)}) collective-permute-start(bf16[256,128]{1,0:T(8,128)(2,1)S(1)} %collective-permute-done.28), channel_id=1, source_target_pairs={{0,2},{1,3},{2,0},{3,1},{4,6},{5,7},{6,4},{7,5},{8,10},{9,11},{10,... | collective-permute-start | bytes 196616 | tf_op jit(solution)/shard_map/ppermute | solution.py:8
  111.5 4.3 %collective-permute-start.34 = (bf16[256,128]{1,0:T(8,128)(2,1)S(1)}, bf16[256,128]{1,0:T(8,128)(2,1)S(1)}, u32[]{:S(2)}, u32[]{:S(2)}) collective-permute-start(bf16[256,128]{1,0:T(8,128)(2,1)S(1)} %collective-permute-done.32), channel_id=1, source_target_pairs={{0,2},{1,3},{2,0},{3,1},{4,6},{5,7},{6,4},{7,5},{8,10},{9,11},{10,... | collective-permute-start | bytes 196616 | tf_op jit(solution)/shard_map/ppermute | solution.py:8
  (21 other events, 231.1 us)

commit v2 on v1

v2 whole, which is shorter than its diff:
```python
import functools
import math

import jax
import jax.numpy as jnp
from jax import lax
from jax.experimental import pallas as pl
from jax.experimental.pallas import tpu as pltpu
from jax.sharding import PartitionSpec as P

F32, BF16 = jnp.float32, jnp.bfloat16
ANY = pl.BlockSpec(memory_space=pl.ANY)
VMEM = pl.BlockSpec(memory_space=pltpu.VMEM)
NT = (((1,), (1,)), ((), ()))
LOG2E = math.log2(math.e)


def swap(a, axis, size, d):
    return lax.ppermute(a, axis, [(i, i ^ d) for i in range(size)])


def lane_groups(a):
    total = None
    for k in range(0, a.shape[1], 128):
        part = jnp.square(a[:, k : k + 128].astype(F32))
        total = part if total is None else total + part
    return total


def half_sq_row(a):
    return 0.5 * jnp.sum(lane_groups(a).T, axis=0, keepdims=True)


def half_sq_column(a):
    return 0.5 * jnp.sum(lane_groups(a), axis=1, keepdims=True)


def rate_row(side, n, in_width):
    rows = side[n : n + 16].astype(F32)
    row = jnp.concatenate([rows[k : k + 1] for k in range(n // 128)], axis=1)
    return row * (-2.0 * LOG2E / in_width)


def copies(pairs, sems):
    made = [pltpu.make_async_copy(src, dst, sems.at[k]) for k, (src, dst) in enumerate(pairs)]
    for copy in made:
        copy.start()
    return made


def forward(rows, blocks, sides, stats=None):
    nb, (n, in_width), out_width = len(blocks), blocks[0].shape, sides[0].shape[1]
    first = stats is None

    def body(*refs):
        rows_ref, block_refs, side_refs = refs[0], refs[1 : 1 + nb], refs[1 + nb : 1 + 2 * nb]
        if first:
            out_ref, stats_ref, pos, side, sems = refs[1 + 2 * nb :]
        else:
            stats_ref, out_ref, pos, side, sems = refs[1 + 2 * nb :]
        pairs = []
        for b in range(nb):
            pairs += [(block_refs[b], pos.at[b]), (side_refs[b], side.at[b])]
        made = copies(pairs, sems)
        x = rows_ref[...]
        row_sq = half_sq_column(x)
        total = jnp.zeros(out_ref.shape, F32)
        for b in range(nb):
            made[2 * b].wait()
            made[2 * b + 1].wait()
            if first:
                stats_ref[b, 0:1] = half_sq_row(pos[b])
                stats_ref[b, 1:2] = rate_row(side[b], n, in_width)
            cross = lax.dot_general(x, pos[b], NT, preferred_element_type=F32)
            power = (row_sq + stats_ref[b, 0:1] - cross) * stats_ref[b, 1:2]
            kernel = jnp.exp2(power).astype(BF16)
            total += jnp.dot(kernel, side[b, :n], preferred_element_type=F32)
        out_ref[...] = total

    part = jax.ShapeDtypeStruct((rows.shape[0], out_width), F32)
    stat = jax.ShapeDtypeStruct((nb, 8, n), F32)
    work = rows.shape[0] * nb * n
    return pl.pallas_call(
        body,
        out_shape=(part, stat) if first else part,
        in_specs=[VMEM] + [ANY] * (2 * nb) + ([] if first else [VMEM]),
        out_specs=(VMEM, VMEM) if first else VMEM,
        scratch_shapes=[
            pltpu.VMEM((nb, n, in_width), BF16),
            pltpu.VMEM((nb,) + sides[0].shape, BF16),
            pltpu.SemaphoreType.DMA((2 * nb,)),
        ],
        compiler_params=pltpu.CompilerParams(vmem_limit_bytes=24 << 20),
        cost_estimate=pl.CostEstimate(
            flops=2 * work * (in_width + out_width), bytes_accessed=3 << 20, transcendentals=work
        ),
        name="forward",
    )(rows, *blocks, *sides, *([] if first else [stats]))


def own_kernel(center_pos, side, local, far):
    n, in_width = center_pos.shape
    near_rows, far_rows = local.shape[0], far.shape[0]

    def body(pos_ref, side_ref, local_ref, far_ref, out_ref):
        pos = pos_ref[...]
        center_sq = half_sq_column(pos)
        rate = jnp.broadcast_to(rate_row(side_ref[...], n, in_width), (128, n)).T[:, :1]
        step = near_rows
        for start in range(0, near_rows + far_rows, step):
            x = local_ref[...] if start == 0 else far_ref[start - near_rows : start - near_rows + step]
            cross = lax.dot_general(pos, x, NT, preferred_element_type=F32)
            power = (center_sq + half_sq_row(x) - cross) * rate
            out_ref[:, start : start + step] = jnp.exp2(power).astype(BF16)

    work = n * (near_rows + far_rows)
    return pl.pallas_call(
        body,
        out_shape=jax.ShapeDtypeStruct((n, near_rows + far_rows), BF16),
        in_specs=[VMEM] * 4,
        out_specs=VMEM,
        compiler_params=pltpu.CompilerParams(vmem_limit_bytes=24 << 20),
        cost_estimate=pl.CostEstimate(
            flops=2 * work * in_width, bytes_accessed=3 << 20, transcendentals=work
        ),
        name="own_kernel",
    )(center_pos, side, local, far)


def backward(center_pos, side, locals_, fars, kernels, cots, before=None, last=False):
    n, in_width = center_pos.shape
    out_width = side.shape[1]
    groups, near_rows, points = len(kernels), locals_[0].shape[0], kernels[0].shape[1]

    def body(*refs):
        refs = list(refs)
        pos_ref, side_ref = refs[:2]
        del refs[:2]
        local_refs, far_refs, kernel_refs, cot_refs = (
            refs[k * groups : (k + 1) * groups] for k in range(4)
        )
        del refs[: 4 * groups]
        before_refs = None
        if before is not None:
            before_refs = refs[:3]
            del refs[:3]
        moment_ref, coef_ref = refs[:2]
        del refs[:2]
        if not last:
            total_ref = refs.pop(0)
        x, kernel, cot, sems = refs
        pairs = []
        for g in range(groups):
            pairs += [
                (cot_refs[g], cot.at[g]),
                (kernel_refs[g], kernel.at[g]),
                (local_refs[g], x.at[g, :near_rows]),
                (far_refs[g], x.at[g, near_rows:]),
            ]
        made = copies(pairs, sems)
        coef = side_ref[:n]
        ones = jnp.ones((points, 128), BF16)
        if before_refs is None:
            moment, grad_coef, total = 0.0, 0.0, 0.0
        else:
            moment, grad_coef, total = (ref[...] for ref in before_refs)
        for g in range(groups):
            for copy in made[4 * g : 4 * g + 4]:
                copy.wait()
            mixing = lax.dot_general(coef, cot[g], NT, preferred_element_type=F32)
            weights = (kernel[g].astype(F32) * mixing).astype(BF16)
            grad_coef += jnp.dot(kernel[g], cot[g], preferred_element_type=F32)
            total += jnp.dot(weights, ones, preferred_element_type=F32)
            moment += jnp.dot(weights, x[g], preferred_element_type=F32)
        coef_ref[...] = grad_coef
        if last:
            rate = jnp.broadcast_to(rate_row(side_ref[...], n, 2.0 * LOG2E), (128, n)).T
            scale = rate * (-2.0 / in_width)
            for k in range(0, in_width, 128):
                pos = pos_ref[:, k : k + 128].astype(F32)
                moment_ref[:, k : k + 128] = scale * (moment[:, k : k + 128] - total * pos)
        else:
            moment_ref[...] = moment
            total_ref[...] = total

    shapes = [
        jax.ShapeDtypeStruct((n, in_width), F32),
        jax.ShapeDtypeStruct((n, out_width), F32),
        jax.ShapeDtypeStruct((n, 128), F32),
    ]
    outs = 2 if last else 3
    work = n * points * groups
    return pl.pallas_call(
        body,
        out_shape=tuple(shapes[:outs]),
        in_specs=[VMEM] * 2 + [ANY] * (4 * groups) + ([] if before is None else [VMEM] * 3),
        out_specs=(VMEM,) * outs,
        scratch_shapes=[
            pltpu.VMEM((groups, points, in_width), BF16),
            pltpu.VMEM((groups, n, points), BF16),
            pltpu.VMEM((groups, points, out_width), BF16),
            pltpu.SemaphoreType.DMA((4 * groups,)),
        ],
        compiler_params=pltpu.CompilerParams(vmem_limit_bytes=40 << 20),
        cost_estimate=pl.CostEstimate(
            flops=2 * work * (in_width + 2 * out_width + 128), bytes_accessed=6 << 20, transcendentals=0
        ),
        name="backward",
    )(center_pos, side, *locals_, *fars, *kernels, *cots, *([] if before is None else before))


def solution(mesh):
    nz, nc = mesh.shape["points"], mesh.shape["centers"]

    def per_device(train_points, saved_preds, targets, huber_delta, center_pos, coefficients, spread):
        n_rows = train_points.shape[0]
        own_centers = coefficients.shape[0]
        piece = n_rows // nc
        c = lax.axis_index("centers")

        def row_piece(a, d):
            return lax.dynamic_slice_in_dim(a, (c ^ d) * piece, piece)

        own = row_piece(train_points, 0)
        layer = {dz: swap(own, "points", nz, dz) for dz in range(1, nz)}

        spread_rows = own_centers // 128
        side = jnp.concatenate(
            [coefficients, jnp.pad(spread.reshape(spread_rows, 128), ((0, 16 - spread_rows), (0, 0)))]
        )
        pos, sides = {0: center_pos}, {0: side}
        for d in range(2, nc, 2):
            pos[d], sides[d] = swap(center_pos, "centers", nc, d), swap(side, "centers", nc, d)
        for d in range(0, nc, 2):
            pos[d + 1], sides[d + 1] = swap(pos[d], "centers", nc, 1), swap(sides[d], "centers", nc, 1)
        blocks, sides = [pos[d] for d in range(nc)], [sides[d] for d in range(nc)]

        pred, stats = forward(own, blocks, sides)
        for dz in range(1, nz):
            pred = pred + swap(forward(layer[dz], blocks, sides, stats), "points", nz, dz)
        residual = pred + row_piece(saved_preds, 0) - row_piece(targets, 0)
        cot = (residual / jnp.sqrt(1.0 + jnp.square(residual / huber_delta[None, :]))).astype(BF16)

        local = {d: own if d == 0 else row_piece(train_points, d) for d in range(nc)}
        far = {0: jnp.concatenate([layer[dz] for dz in range(1, nz)])}
        cots = {0: jnp.concatenate([cot] + [swap(cot, "points", nz, dz) for dz in range(1, nz)])}
        for d in range(2, nc, 2):
            far[d], cots[d] = swap(far[0], "centers", nc, d), swap(cots[0], "centers", nc, d)
        for d in range(0, nc, 2):
            far[d + 1], cots[d + 1] = swap(far[d], "centers", nc, 1), swap(cots[d], "centers", nc, 1)

        kernels = {d: own_kernel(center_pos, side, local[d], far[d]) for d in range(nc)}
        sums = None
        for d in range(0, nc, 2):
            near = [d, d + 1]
            sums = backward(
                center_pos,
                side,
                *([group[k] for k in near] for group in (local, far, kernels, cots)),
                before=sums,
                last=d + 2 == nc,
            )
        return sums

    return jax.shard_map(
        per_device,
        mesh=mesh,
        in_specs=(
            P(("groups", "points"), None),
            P(("groups", "points"), None),
            P(("groups", "points"), None),
            P("groups"),
            P(("groups", "points", "centers"), None),
            P(("groups", "points", "centers"), None),
            P(("groups", "points", "centers")),
        ),
        out_specs=(
            P(("groups", "points", "centers"), None),
            P(("groups", "points", "centers"), None),
        ),
        check_vma=False,
    )
```

time: 125 us -> 106 us (0.85)
  matrix products: 41 us -> 0 us
  waiting for transfers between devices: 24.5 us -> 52.2 us
  Pallas kernels: 0 us -> 24.5 us
  local copies, waits for them, and re-layouts: 16.9 us -> 1.63 us
  other arithmetic: 10.5 us -> 1.08 us
  starting transfers between devices: 30.6 us -> 25.1 us
    dot_general x20 -> x0, matrix products: 41 us -> none  [the longest x16 29.1 us: partial_pred(): total = total + jnp.dot(kernel, coef[d], preferred_element_type=jnp.float32)]
    ppermute x36 -> x21, waiting for transfers between devices: 24.5 us -> 52.2 us  [swap(): return lax.ppermute(a, axis, [(i, i ^ d) for i in range(size)])]
    pallas_call x0 -> x10, Pallas kernels: none -> 24.5 us  [the longest x4 11.9 us: forward(): pl.pallas_call(body, out_shape=(part, stat) if first else part, in_specs=...]
    unnamed x63 -> x10, local copies, waits for them, and re-layouts: 16.2 us -> 0.3 us
    reduce_sum x9 -> x0, other arithmetic: 6.42 us -> none  [the longest x1 3.08 us: per_device(): all_sq = jnp.sum(jnp.square(all_x.astype(jnp.float32)), axis=1)]
    ppermute x36 -> x21, starting transfers between devices: 30.6 us -> 25.1 us  [swap(): return lax.ppermute(a, axis, [(i, i ^ d) for i in range(size)])]
    neg x3 -> x0, other arithmetic: 1.85 us -> none  [partial_pred(): kernel = jnp.exp(-rate[d][None, :] * dist / in_width).astype(jnp.bfloat16)]
    dynamic_slice x0 -> x1, local copies, waits for them, and re-layouts: none -> 1.31 us  [row_piece(): return lax.dynamic_slice_in_dim(a, (c ^ d) * piece, piece)]
  transfers between devices with their start and end apart: 36 -> 21, of which waited for: 7 -> 7; matrix products, arithmetic and copies ran while one was open for 45% -> 2% of each run, Pallas kernels for 0% -> 19%
where the time goes in v2:
time: 106 us; the launch traced here: 105 us
  waiting for transfers between devices  52.2 us (49%)
  starting transfers between devices  25.1 us (24%)
  Pallas kernels  24.5 us (23%)
  local copies, waits for them, and re-layouts  1.63 us (2%)
  other arithmetic  1.08 us (1%)
    ppermute x21, waiting for transfers between devices, swap(): return lax.ppermute(a, axis, [(i, i ^ d) for i in range(size)])  52.2 us
    ppermute x21, starting transfers between devices, swap(): return lax.ppermute(a, axis, [(i, i ^ d) for i in range(size)])  25.1 us
    pallas_call x4, Pallas kernels, forward(): pl.pallas_call(body, out_shape=(part, stat) if first else part, in_specs=...  11.9 us
    pallas_call x2, Pallas kernels, backward(): pl.pallas_call(body, out_shape=tuple(shapes[:outs]), in_specs=[VMEM] * 2...  8.33 us
    pallas_call x4, Pallas kernels, own_kernel(): pl.pallas_call(body, out_shape=jax.ShapeDtypeStruct((n, near_rows + far_r...  4.31 us
  transfers between devices with their start and end apart: 21, of which 7 were waited for; matrix products, arithmetic and copies ran while one was open for 2% of the time, Pallas kernels for 19%

profile of v2, /device:TPU:0, one launch (start us, length us, event | category | flops | bytes accessed | tf_op | source)
XLA Modules:
  0.0 105.5 jit_solution(1625419331550770067)
XLA Ops:
  0.6 3.0 %collective-permute-start.6 = (bf16[512,512]{1,0:T(8,128)(2,1)}, bf16[512,512]{1,0:T(8,128)(2,1)S(1)}, u32[]{:S(2)}, u32[]{:S(2)}) collective-permute-start(bf16[512,512]{1,0:T(8,128)(2,1)} %refs_0_.3), channel_id=1, source_target_pairs={{0,2},{1,3},{2,0},{3,1},{4,6},{5,7},{6,4},{7,5},{8,10},{9,11},{10,... | collective-permute-start | bytes 1572872 | tf_op jit(solution)/shard_map/ppermute | solution.py:19
  3.6 1.3 %constant_dynamic-slice_fusion = (bf16[256,512]{1,0:T(8,128)(2,1)S(1)}, bf16[256,512]{1,0:T(8,128)(2,1)S(1)}, bf16[256,512]{1,0:T(8,128)(2,1)S(1)}, bf16[256,512]{1,0:T(8,128)(2,1)S(1)}) fusion(bf16[1024,512]{1,0:T(8,128)(2,1)} %param.7, s32[]{:T(128)S(6)} %select_n.17, s32[]{:T(128)S(6)} %select_n.15, s32[]{:T(128)S(6)} %select_n.14, s32[]{:T(128)S(6)} %select_n.16), kind=kLoop, calls=%fused_computation.8 | loop fusion | bytes 2097168 | tf_op jit(solution)/shard_map/dynamic_slice | solution.py:222
  5.0 1.6 %collective-permute-start = (bf16[256,512]{1,0:T(8,128)(2,1)S(1)}, bf16[256,512]{1,0:T(8,128)(2,1)S(1)}, u32[]{:S(2)}, u32[]{:S(2)}) collective-permute-start(bf16[256,512]{1,0:T(8,128)(2,1)S(1)} %get-tuple-element.15.refs_0_.local_ref.refs_2_), channel_id=1, source_target_pairs={{0,4},{4,0},{8,12},{12,8},{1,5},{5,1},{9,13},{13,9},{2,6},{6,2},{1... | collective-permute-start | bytes 786440 | tf_op jit(solution)/shard_map/ppermute | solution.py:19
  6.6 2.6 %collective-permute-start.1 = (bf16[256,512]{1,0:T(8,128)(2,1)S(1)}, bf16[256,512]{1,0:T(8,128)(2,1)S(1)}, u32[]{:S(2)}, u32[]{:S(2)}) collective-permute-start(bf16[256,512]{1,0:T(8,128)(2,1)S(1)} %get-tuple-element.15.refs_0_.local_ref.refs_2_), channel_id=1, source_target_pairs={{0,8},{4,12},{8,0},{12,4},{1,9},{5,13},{9,1},{13,5},{2,10},{6,14},... | collective-permute-start | bytes 786440 | tf_op jit(solution)/shard_map/ppermute | solution.py:19
  9.4 8.1 %collective-permute-done.refs_0_ = bf16[256,512]{1,0:T(8,128)(2,1)S(1)} collective-permute-done((bf16[256,512]{1,0:T(8,128)(2,1)S(1)}, bf16[256,512]{1,0:T(8,128)(2,1)S(1)}, u32[]{:S(2)}, u32[]{:S(2)}) %collective-permute-start) | collective-permute-done | bytes 262176 | tf_op jit(solution)/shard_map/ppermute | solution.py:19
  17.6 10.4 %collective-permute-done.1.refs_0_ = bf16[256,512]{1,0:T(8,128)(2,1)S(1)} collective-permute-done((bf16[256,512]{1,0:T(8,128)(2,1)S(1)}, bf16[256,512]{1,0:T(8,128)(2,1)S(1)}, u32[]{:S(2)}, u32[]{:S(2)}) %collective-permute-start.1) | collective-permute-done | bytes 262176 | tf_op jit(solution)/shard_map/ppermute | solution.py:19
  28.1 0.6 collective-permute-start.3
  28.9 1.3 %collective-permute-start.9 = (bf16[528,128]{1,0:T(8,128)(2,1)S(1)}, bf16[528,128]{1,0:T(8,128)(2,1)S(1)}, u32[]{:S(2)}, u32[]{:S(2)}) collective-permute-start(bf16[528,128]{1,0:T(8,128)(2,1)S(1)} %fusion.1.side_ref.refs_5_.refs_1_), channel_id=1, source_target_pairs={{0,2},{1,3},{2,0},{3,1},{4,6},{5,7},{6,4},{7,5},{8,10},{9,11},{10,... | collective-permute-start | bytes 405512 | tf_op jit(solution)/shard_map/ppermute | solution.py:19
  30.2 16.9 %collective-permute-done.9.refs_7_ = bf16[528,128]{1,0:T(8,128)(2,1)S(1)} collective-permute-done((bf16[528,128]{1,0:T(8,128)(2,1)S(1)}, bf16[528,128]{1,0:T(8,128)(2,1)S(1)}, u32[]{:S(2)}, u32[]{:S(2)}) %collective-permute-start.9) | collective-permute-done | bytes 135200 | tf_op jit(solution)/shard_map/ppermute | solution.py:19
  47.2 1.3 %collective-permute-done.10.refs_8_ = bf16[528,128]{1,0:T(8,128)(2,1)S(1)} collective-permute-done((bf16[528,128]{1,0:T(8,128)(2,1)S(1)}, bf16[528,128]{1,0:T(8,128)(2,1)S(1)}, u32[]{:S(2)}, u32[]{:S(2)}) %collective-permute-start.10) | collective-permute-done | bytes 135200 | tf_op jit(solution)/shard_map/ppermute | solution.py:19
  48.5 3.0 %forward.4 = (f32[256,128]{1,0:T(8,128)S(1)}, f32[4,8,512]{2,1,0:T(8,128)S(1)}) custom-call(bf16[256,512]{1,0:T(8,128)(2,1)S(1)} %get-tuple-element.15.refs_0_.local_ref.refs_2_, bf16[512,512]{1,0:T(8,128)(2,1)S(1)} %copy-done, bf16[512,512]{1,0:T(8,128)(2,1)S(1)} %collective-permute-done.5.refs_2_, bf16[512,512]{1,0:T(8,128)(2,1)S(1)} %collective-permute-done.6.refs_3_, ...), custom_call_target="tpu_custom_call" | custom-call | flops 671088640 | bytes 3145728 | tf_op jit(solution)/shard_map/forward/pallas_call | solution.py:83
  51.5 3.0 %forward.5 = f32[256,128]{1,0:T(8,128)S(1)} custom-call(bf16[256,512]{1,0:T(8,128)(2,1)S(1)} %collective-permute-done.refs_0_, bf16[512,512]{1,0:T(8,128)(2,1)S(1)} %copy-done, bf16[512,512]{1,0:T(8,128)(2,1)S(1)} %collective-permute-done.5.refs_2_, bf16[512,512]{1,0:T(8,128)(2,1)S(1)} %collective-permute-done.6.refs_3_, ...), custom_call_target="tpu_custom_call" | custom-call | flops 671088640 | bytes 3145728 | tf_op jit(solution)/shard_map/forward/pallas_call | solution.py:83
  54.5 6.2 %collective-permute-start.11 = (f32[256,128]{1,0:T(8,128)S(1)}, f32[256,128]{1,0:T(8,128)S(1)}, u32[]{:S(2)}, u32[]{:S(2)}) collective-permute-start(f32[256,128]{1,0:T(8,128)S(1)} %forward.5), channel_id=1, source_target_pairs={{0,4},{4,0},{8,12},{12,8},{1,5},{5,1},{9,13},{13,9},{2,6},{6,2},{1... | collective-permute-start | bytes 393224 | tf_op jit(solution)/shard_map/ppermute | solution.py:19
  60.7 3.0 %forward.6 = f32[256,128]{1,0:T(8,128)S(1)} custom-call(bf16[256,512]{1,0:T(8,128)(2,1)S(1)} %collective-permute-done.1.refs_0_, bf16[512,512]{1,0:T(8,128)(2,1)S(1)} %copy-done, bf16[512,512]{1,0:T(8,128)(2,1)S(1)} %collective-permute-done.5.refs_2_, bf16[512,512]{1,0:T(8,128)(2,1)S(1)} %collective-permute-done.6.refs_3_, ...), custom_call_target="tpu_custom_call" | custom-call | flops 671088640 | bytes 3145728 | tf_op jit(solution)/shard_map/forward/pallas_call | solution.py:83
  63.6 1.1 %collective-permute-start.12 = (f32[256,128]{1,0:T(8,128)S(1)}, f32[256,128]{1,0:T(8,128)S(1)}, u32[]{:S(2)}, u32[]{:S(2)}) collective-permute-start(f32[256,128]{1,0:T(8,128)S(1)} %forward.6), channel_id=1, source_target_pairs={{0,8},{4,12},{8,0},{12,4},{1,9},{5,13},{9,1},{13,5},{2,10},{6,14},... | collective-permute-start | bytes 393224 | tf_op jit(solution)/shard_map/ppermute | solution.py:19
  64.7 3.0 %forward.7 = f32[256,128]{1,0:T(8,128)S(1)} custom-call(bf16[256,512]{1,0:T(8,128)(2,1)S(1)} %collective-permute-done.2.refs_0_, bf16[512,512]{1,0:T(8,128)(2,1)S(1)} %copy-done, bf16[512,512]{1,0:T(8,128)(2,1)S(1)} %collective-permute-done.5.refs_2_, bf16[512,512]{1,0:T(8,128)(2,1)S(1)} %collective-permute-done.6.refs_3_, ...), custom_call_target="tpu_custom_call" | custom-call | flops 671088640 | bytes 3145728 | tf_op jit(solution)/shard_map/forward/pallas_call | solution.py:83
  67.7 1.5 %collective-permute-start.13 = (f32[256,128]{1,0:T(8,128)S(1)}, f32[256,128]{1,0:T(8,128)S(1)}, u32[]{:S(2)}, u32[]{:S(2)}) collective-permute-start(f32[256,128]{1,0:T(8,128)S(1)} %forward.7), channel_id=1, source_target_pairs={{0,12},{4,8},{8,4},{12,0},{1,13},{5,9},{9,5},{13,1},{2,14},{6,10},... | collective-permute-start | bytes 393224 | tf_op jit(solution)/shard_map/ppermute | solution.py:19
  69.2 0.5 collective-permute-start.4
  69.8 5.7 %collective-permute-done.12 = f32[256,128]{1,0:T(8,128)S(1)} collective-permute-done((f32[256,128]{1,0:T(8,128)S(1)}, f32[256,128]{1,0:T(8,128)S(1)}, u32[]{:S(2)}, u32[]{:S(2)}) %collective-permute-start.12) | collective-permute-done | bytes 131104 | tf_op jit(solution)/shard_map/ppermute | solution.py:19
  75.4 1.1 multiply_convert_fusion
  76.5 3.3 %collective-permute-start.14 = (bf16[256,128]{1,0:T(8,128)(2,1)S(1)}, bf16[256,128]{1,0:T(8,128)(2,1)S(1)}, u32[]{:S(2)}, u32[]{:S(2)}) collective-permute-start(bf16[256,128]{1,0:T(8,128)(2,1)S(1)} %multiply_convert_fusion), channel_id=1, source_target_pairs={{0,4},{4,0},{8,12},{12,8},{1,5},{5,1},{9,13},{13,9},{2,6},{6,2},{1... | collective-permute-start | bytes 196616 | tf_op jit(solution)/shard_map/ppermute | solution.py:19
  79.8 1.0 collective-permute-start.15
  80.8 1.5 %collective-permute-start.16 = (bf16[256,128]{1,0:T(8,128)(2,1)S(1)}, bf16[256,128]{1,0:T(8,128)(2,1)S(1)}, u32[]{:S(2)}, u32[]{:S(2)}) collective-permute-start(bf16[256,128]{1,0:T(8,128)(2,1)S(1)} %multiply_convert_fusion), channel_id=1, source_target_pairs={{0,12},{4,8},{8,4},{12,0},{1,13},{5,9},{9,5},{13,1},{2,14},{6,10},... | collective-permute-start | bytes 196616 | tf_op jit(solution)/shard_map/ppermute | solution.py:19
  82.3 5.7 %collective-permute-done.15 = bf16[256,128]{1,0:T(8,128)(2,1)S(1)} collective-permute-done((bf16[256,128]{1,0:T(8,128)(2,1)S(1)}, bf16[256,128]{1,0:T(8,128)(2,1)S(1)}, u32[]{:S(2)}, u32[]{:S(2)}) %collective-permute-start.15) | collective-permute-done | bytes 65568 | tf_op jit(solution)/shard_map/ppermute | solution.py:19
  88.0 0.6 collective-permute-start.17
  88.6 1.1 %own_kernel.6.refs_6_ = bf16[512,1024]{1,0:T(8,128)(2,1)S(1)} custom-call(bf16[512,512]{1,0:T(8,128)(2,1)S(1)} %copy-done, bf16[528,128]{1,0:T(8,128)(2,1)S(1)} %fusion.1.side_ref.refs_5_.refs_1_, bf16[256,512]{1,0:T(8,128)(2,1)S(1)} %get-tuple-element.15.refs_0_.local_ref.refs_2_, bf16[768,512]{1,0:T(8,128)(2,1)S(1)} %constant_dynamic-update-slice_fusion.far_ref.refs_4_), custom_call_target="tpu_custom_call" | custom-call | flops 536870912 | bytes 3145728 | tf_op jit(solution)/shard_map/own_kernel/pallas_call | solution.py:117
  89.7 1.1 %own_kernel.4.refs_6_ = bf16[512,1024]{1,0:T(8,128)(2,1)S(1)} custom-call(bf16[512,512]{1,0:T(8,128)(2,1)S(1)} %copy-done, bf16[528,128]{1,0:T(8,128)(2,1)S(1)} %fusion.1.side_ref.refs_5_.refs_1_, bf16[256,512]{1,0:T(8,128)(2,1)S(1)} %get-tuple-element.14.local_ref.refs_2_, bf16[768,512]{1,0:T(8,128)(2,1)S(1)} %collective-permute-done.3.far_ref.refs_4_), custom_call_target="tpu_custom_call" | custom-call | flops 536870912 | bytes 3145728 | tf_op jit(solution)/shard_map/own_kernel/pallas_call | solution.py:117
  90.8 4.0 %collective-permute-done.17.refs_8_ = bf16[1024,128]{1,0:T(8,128)(2,1)S(1)} collective-permute-done((bf16[1024,128]{1,0:T(8,128)(2,1)S(1)}, bf16[1024,128]{1,0:T(8,128)(2,1)S(1)}, u32[]{:S(2)}, u32[]{:S(2)}) %collective-permute-start.17) | collective-permute-done | bytes 262176 | tf_op jit(solution)/shard_map/ppermute | solution.py:19
  94.8 1.1 %own_kernel.7.refs_7_ = bf16[512,1024]{1,0:T(8,128)(2,1)S(1)} custom-call(bf16[512,512]{1,0:T(8,128)(2,1)S(1)} %copy-done, bf16[528,128]{1,0:T(8,128)(2,1)S(1)} %fusion.1.side_ref.refs_5_.refs_1_, bf16[256,512]{1,0:T(8,128)(2,1)S(1)} %get-tuple-element.12.local_ref.refs_3_, bf16[768,512]{1,0:T(8,128)(2,1)S(1)} %collective-permute-done.19.far_ref.refs_5_), custom_call_target="tpu_custom_call" | custom-call | flops 536870912 | bytes 3145728 | tf_op jit(solution)/shard_map/own_kernel/pallas_call | solution.py:117
  95.9 3.7 %backward.2 = (f32[512,512]{1,0:T(8,128)S(1)}, f32[512,128]{1,0:T(8,128)S(1)}, f32[512,128]{1,0:T(8,128)S(1)}) custom-call(bf16[512,512]{1,0:T(8,128)(2,1)S(1)} %copy-done, bf16[528,128]{1,0:T(8,128)(2,1)S(1)} %fusion.1.side_ref.refs_5_.refs_1_, bf16[256,512]{1,0:T(8,128)(2,1)S(1)} %get-tuple-element.15.refs_0_.local_ref.refs_2_, ...), custom_call_target="tpu_custom_call" | custom-call | flops 1879048192 | bytes 6291456 | tf_op jit(solution)/shard_map/backward/pallas_call | solution.py:193
  99.6 1.1 %own_kernel.5.refs_7_ = bf16[512,1024]{1,0:T(8,128)(2,1)S(1)} custom-call(bf16[512,512]{1,0:T(8,128)(2,1)S(1)} %copy-done, bf16[528,128]{1,0:T(8,128)(2,1)S(1)} %fusion.1.side_ref.refs_5_.refs_1_, bf16[256,512]{1,0:T(8,128)(2,1)S(1)} %get-tuple-element.13.local_ref.refs_3_, bf16[768,512]{1,0:T(8,128)(2,1)S(1)} %collective-permute-done.4.far_ref.refs_5_), custom_call_target="tpu_custom_call" | custom-call | flops 536870912 | bytes 3145728 | tf_op jit(solution)/shard_map/own_kernel/pallas_call | solution.py:117
  100.7 4.6 %backward.3 = (f32[512,512]{1,0:T(8,128)}, f32[512,128]{1,0:T(8,128)}) custom-call(bf16[512,512]{1,0:T(8,128)(2,1)S(1)} %copy-done, bf16[528,128]{1,0:T(8,128)(2,1)S(1)} %fusion.1.side_ref.refs_5_.refs_1_, bf16[256,512]{1,0:T(8,128)(2,1)S(1)} %get-tuple-element.14.local_ref.refs_2_, bf16[256,512]{1,0:T(8,128)(2,1)S(1)} %get-tuple-element.13.local_ref.refs_3_, ...), custom_call_target="tpu_custom_call" | custom-call | flops 1879048192 | bytes 6291456 | tf_op jit(solution)/shard_map/backward/pallas_call | solution.py:193
  (35 shorter events, 0.7 us)
Async XLA Ops:
  0.6 16.9 %collective-permute-start.6 = (bf16[512,512]{1,0:T(8,128)(2,1)}, bf16[512,512]{1,0:T(8,128)(2,1)S(1)}, u32[]{:S(2)}, u32[]{:S(2)}) collective-permute-start(bf16[512,512]{1,0:T(8,128)(2,1)} %refs_0_.3), channel_id=1, source_target_pairs={{0,2},{1,3},{2,0},{3,1},{4,6},{5,7},{6,4},{7,5},{8,10},{9,11},{10,... | collective-permute-start | bytes 1572872 | tf_op jit(solution)/shard_map/ppermute | solution.py:19
  3.6 5.8 %copy-start = (bf16[512,512]{1,0:T(8,128)(2,1)S(1)}, bf16[512,512]{1,0:T(8,128)(2,1)}, u32[]{:S(2)}) copy-start(bf16[512,512]{1,0:T(8,128)(2,1)} %refs_0_.3) | copy-start | bytes 1572868
  5.0 12.5 %collective-permute-start = (bf16[256,512]{1,0:T(8,128)(2,1)S(1)}, bf16[256,512]{1,0:T(8,128)(2,1)S(1)}, u32[]{:S(2)}, u32[]{:S(2)}) collective-permute-start(bf16[256,512]{1,0:T(8,128)(2,1)S(1)} %get-tuple-element.15.refs_0_.local_ref.refs_2_), channel_id=1, source_target_pairs={{0,4},{4,0},{8,12},{12,8},{1,5},{5,1},{9,13},{13,9},{2,6},{6,2},{1... | collective-permute-start | bytes 786440 | tf_op jit(solution)/shard_map/ppermute | solution.py:19
  6.6 21.4 %collective-permute-start.1 = (bf16[256,512]{1,0:T(8,128)(2,1)S(1)}, bf16[256,512]{1,0:T(8,128)(2,1)S(1)}, u32[]{:S(2)}, u32[]{:S(2)}) collective-permute-start(bf16[256,512]{1,0:T(8,128)(2,1)S(1)} %get-tuple-element.15.refs_0_.local_ref.refs_2_), channel_id=1, source_target_pairs={{0,8},{4,12},{8,0},{12,4},{1,9},{5,13},{9,1},{13,5},{2,10},{6,14},... | collective-permute-start | bytes 786440 | tf_op jit(solution)/shard_map/ppermute | solution.py:19
  9.2 18.8 %collective-permute-start.2 = (bf16[256,512]{1,0:T(8,128)(2,1)S(1)}, bf16[256,512]{1,0:T(8,128)(2,1)S(1)}, u32[]{:S(2)}, u32[]{:S(2)}) collective-permute-start(bf16[256,512]{1,0:T(8,128)(2,1)S(1)} %get-tuple-element.15.refs_0_.local_ref.refs_2_), channel_id=1, source_target_pairs={{0,12},{4,8},{8,4},{12,0},{1,13},{5,9},{9,5},{13,1},{2,14},{6,10},... | collective-permute-start | bytes 786440 | tf_op jit(solution)/shard_map/ppermute | solution.py:19
  9.4 39.1 %collective-permute-start.5 = (bf16[512,512]{1,0:T(8,128)(2,1)S(1)}, bf16[512,512]{1,0:T(8,128)(2,1)S(1)}, u32[]{:S(2)}, u32[]{:S(2)}) collective-permute-start(bf16[512,512]{1,0:T(8,128)(2,1)S(1)} %copy-done), channel_id=1, source_target_pairs={{0,1},{1,0},{2,3},{3,2},{4,5},{5,4},{6,7},{7,6},{8,9},{9,8},{10,11... | collective-permute-start | bytes 1572872 | tf_op jit(solution)/shard_map/ppermute | solution.py:19
  17.5 31.0 %collective-permute-start.7 = (bf16[512,512]{1,0:T(8,128)(2,1)S(1)}, bf16[512,512]{1,0:T(8,128)(2,1)S(1)}, u32[]{:S(2)}, u32[]{:S(2)}) collective-permute-start(bf16[512,512]{1,0:T(8,128)(2,1)S(1)} %collective-permute-done.6.refs_3_), channel_id=1, source_target_pairs={{0,1},{1,0},{2,3},{3,2},{4,5},{5,4},{6,7},{7,6},{8,9},{9,8},{10,11... | collective-permute-start | bytes 1572872 | tf_op jit(solution)/shard_map/ppermute | solution.py:19
  28.0 0.9 copy-start.1
  28.0 0.9 copy-start.2
  28.1 41.2 %collective-permute-start.3 = (bf16[768,512]{1,0:T(8,128)(2,1)S(1)}, bf16[768,512]{1,0:T(8,128)(2,1)S(1)}, u32[]{:S(2)}, u32[]{:S(2)}) collective-permute-start(bf16[768,512]{1,0:T(8,128)(2,1)S(1)} %constant_dynamic-update-slice_fusion.far_ref.refs_4_), channel_id=1, source_target_pairs={{0,2},{1,3},{2,0},{3,1},{4,6},{5,7},{6,4},{7,5},{8,10},{9,11},{10,... | collective-permute-start | bytes 2359304 | tf_op jit(solution)/shard_map/ppermute | solution.py:19
  28.9 18.3 %collective-permute-start.9 = (bf16[528,128]{1,0:T(8,128)(2,1)S(1)}, bf16[528,128]{1,0:T(8,128)(2,1)S(1)}, u32[]{:S(2)}, u32[]{:S(2)}) collective-permute-start(bf16[528,128]{1,0:T(8,128)(2,1)S(1)} %fusion.1.side_ref.refs_5_.refs_1_), channel_id=1, source_target_pairs={{0,2},{1,3},{2,0},{3,1},{4,6},{5,7},{6,4},{7,5},{8,10},{9,11},{10,... | collective-permute-start | bytes 405512 | tf_op jit(solution)/shard_map/ppermute | solution.py:19
  30.2 16.9 %collective-permute-start.8 = (bf16[528,128]{1,0:T(8,128)(2,1)S(1)}, bf16[528,128]{1,0:T(8,128)(2,1)S(1)}, u32[]{:S(2)}, u32[]{:S(2)}) collective-permute-start(bf16[528,128]{1,0:T(8,128)(2,1)S(1)} %fusion.1.side_ref.refs_5_.refs_1_), channel_id=1, source_target_pairs={{0,1},{1,0},{2,3},{3,2},{4,5},{5,4},{6,7},{7,6},{8,9},{9,8},{10,11... | collective-permute-start | bytes 405512 | tf_op jit(solution)/shard_map/ppermute | solution.py:19
  47.2 1.4 %collective-permute-start.10 = (bf16[528,128]{1,0:T(8,128)(2,1)S(1)}, bf16[528,128]{1,0:T(8,128)(2,1)S(1)}, u32[]{:S(2)}, u32[]{:S(2)}) collective-permute-start(bf16[528,128]{1,0:T(8,128)(2,1)S(1)} %collective-permute-done.9.refs_7_), channel_id=1, source_target_pairs={{0,1},{1,0},{2,3},{3,2},{4,5},{5,4},{6,7},{7,6},{8,9},{9,8},{10,11... | collective-permute-start | bytes 405512 | tf_op jit(solution)/shard_map/ppermute | solution.py:19
  54.5 15.3 %collective-permute-start.11 = (f32[256,128]{1,0:T(8,128)S(1)}, f32[256,128]{1,0:T(8,128)S(1)}, u32[]{:S(2)}, u32[]{:S(2)}) collective-permute-start(f32[256,128]{1,0:T(8,128)S(1)} %forward.5), channel_id=1, source_target_pairs={{0,4},{4,0},{8,12},{12,8},{1,5},{5,1},{9,13},{13,9},{2,6},{6,2},{1... | collective-permute-start | bytes 393224 | tf_op jit(solution)/shard_map/ppermute | solution.py:19
  63.6 11.8 %collective-permute-start.12 = (f32[256,128]{1,0:T(8,128)S(1)}, f32[256,128]{1,0:T(8,128)S(1)}, u32[]{:S(2)}, u32[]{:S(2)}) collective-permute-start(f32[256,128]{1,0:T(8,128)S(1)} %forward.6), channel_id=1, source_target_pairs={{0,8},{4,12},{8,0},{12,4},{1,9},{5,13},{9,1},{13,5},{2,10},{6,14},... | collective-permute-start | bytes 393224 | tf_op jit(solution)/shard_map/ppermute | solution.py:19
  67.7 7.7 %copy-start.3 = (f32[128]{0:T(128)S(1)}, f32[128]{0:T(128)}, u32[]{:S(2)}) copy-start(f32[128]{0:T(128)} %param.10) | copy-start | bytes 1540
  67.7 7.7 %collective-permute-start.13 = (f32[256,128]{1,0:T(8,128)S(1)}, f32[256,128]{1,0:T(8,128)S(1)}, u32[]{:S(2)}, u32[]{:S(2)}) collective-permute-start(f32[256,128]{1,0:T(8,128)S(1)} %forward.7), channel_id=1, source_target_pairs={{0,12},{4,8},{8,4},{12,0},{1,13},{5,9},{9,5},{13,1},{2,14},{6,10},... | collective-permute-start | bytes 393224 | tf_op jit(solution)/shard_map/ppermute | solution.py:19
  69.2 25.5 %collective-permute-start.19 = (bf16[768,512]{1,0:T(8,128)(2,1)S(1)}, bf16[768,512]{1,0:T(8,128)(2,1)S(1)}, u32[]{:S(2)}, u32[]{:S(2)}) collective-permute-start(bf16[768,512]{1,0:T(8,128)(2,1)S(1)} %constant_dynamic-update-slice_fusion.far_ref.refs_4_), channel_id=1, source_target_pairs={{0,1},{1,0},{2,3},{3,2},{4,5},{5,4},{6,7},{7,6},{8,9},{9,8},{10,11... | collective-permute-start | bytes 2359304 | tf_op jit(solution)/shard_map/ppermute | solution.py:19
  69.2 30.4 %collective-permute-start.4 = (bf16[768,512]{1,0:T(8,128)(2,1)S(1)}, bf16[768,512]{1,0:T(8,128)(2,1)S(1)}, u32[]{:S(2)}, u32[]{:S(2)}) collective-permute-start(bf16[768,512]{1,0:T(8,128)(2,1)S(1)} %collective-permute-done.3.far_ref.refs_4_), channel_id=1, source_target_pairs={{0,1},{1,0},{2,3},{3,2},{4,5},{5,4},{6,7},{7,6},{8,9},{9,8},{10,11... | collective-permute-start | bytes 2359304 | tf_op jit(solution)/shard_map/ppermute | solution.py:19
  76.5 5.8 %collective-permute-start.14 = (bf16[256,128]{1,0:T(8,128)(2,1)S(1)}, bf16[256,128]{1,0:T(8,128)(2,1)S(1)}, u32[]{:S(2)}, u32[]{:S(2)}) collective-permute-start(bf16[256,128]{1,0:T(8,128)(2,1)S(1)} %multiply_convert_fusion), channel_id=1, source_target_pairs={{0,4},{4,0},{8,12},{12,8},{1,5},{5,1},{9,13},{13,9},{2,6},{6,2},{1... | collective-permute-start | bytes 196616 | tf_op jit(solution)/shard_map/ppermute | solution.py:19
  79.8 8.1 %collective-permute-start.15 = (bf16[256,128]{1,0:T(8,128)(2,1)S(1)}, bf16[256,128]{1,0:T(8,128)(2,1)S(1)}, u32[]{:S(2)}, u32[]{:S(2)}) collective-permute-start(bf16[256,128]{1,0:T(8,128)(2,1)S(1)} %multiply_convert_fusion), channel_id=1, source_target_pairs={{0,8},{4,12},{8,0},{12,4},{1,9},{5,13},{9,1},{13,5},{2,10},{6,14},... | collective-permute-start | bytes 196616 | tf_op jit(solution)/shard_map/ppermute | solution.py:19
  80.8 7.2 %collective-permute-start.16 = (bf16[256,128]{1,0:T(8,128)(2,1)S(1)}, bf16[256,128]{1,0:T(8,128)(2,1)S(1)}, u32[]{:S(2)}, u32[]{:S(2)}) collective-permute-start(bf16[256,128]{1,0:T(8,128)(2,1)S(1)} %multiply_convert_fusion), channel_id=1, source_target_pairs={{0,12},{4,8},{8,4},{12,0},{1,13},{5,9},{9,5},{13,1},{2,14},{6,10},... | collective-permute-start | bytes 196616 | tf_op jit(solution)/shard_map/ppermute | solution.py:19
  88.0 6.8 %collective-permute-start.17 = (bf16[1024,128]{1,0:T(8,128)(2,1)S(1)}, bf16[1024,128]{1,0:T(8,128)(2,1)S(1)}, u32[]{:S(2)}, u32[]{:S(2)}) collective-permute-start(bf16[1024,128]{1,0:T(8,128)(2,1)S(1)} %pad_maximum_fusion.refs_8_), channel_id=1, source_target_pairs={{0,2},{1,3},{2,0},{3,1},{4,6},{5,7},{6,4},{7,5},{8,10},{9,11},{10,... | collective-permute-start | bytes 786440 | tf_op jit(solution)/shard_map/ppermute | solution.py:19
  88.6 7.3 %collective-permute-start.20 = (bf16[1024,128]{1,0:T(8,128)(2,1)S(1)}, bf16[1024,128]{1,0:T(8,128)(2,1)S(1)}, u32[]{:S(2)}, u32[]{:S(2)}) collective-permute-start(bf16[1024,128]{1,0:T(8,128)(2,1)S(1)} %pad_maximum_fusion.refs_8_), channel_id=1, source_target_pairs={{0,1},{1,0},{2,3},{3,2},{4,5},{5,4},{6,7},{7,6},{8,9},{9,8},{10,11... | collective-permute-start | bytes 786440 | tf_op jit(solution)/shard_map/ppermute | solution.py:19
  94.8 5.9 %collective-permute-start.18 = (bf16[1024,128]{1,0:T(8,128)(2,1)S(1)}, bf16[1024,128]{1,0:T(8,128)(2,1)S(1)}, u32[]{:S(2)}, u32[]{:S(2)}) collective-permute-start(bf16[1024,128]{1,0:T(8,128)(2,1)S(1)} %collective-permute-done.17.refs_8_), channel_id=1, source_target_pairs={{0,1},{1,0},{2,3},{3,2},{4,5},{5,4},{6,7},{7,6},{8,9},{9,8},{10,11... | collective-permute-start | bytes 786440 | tf_op jit(solution)/shard_map/ppermute | solution.py:19

commit v3 on v1

v3 whole, which is shorter than its diff:
```python
import math

import jax
import jax.numpy as jnp
from jax import lax
from jax.experimental import pallas as pl
from jax.experimental.pallas import tpu as pltpu
from jax.sharding import PartitionSpec as P

F32, BF16 = jnp.float32, jnp.bfloat16
HBM = pl.BlockSpec(memory_space=pltpu.HBM)
VMEM = pl.BlockSpec(memory_space=pltpu.VMEM)
NT = (((1,), (1,)), ((), ()))
LOG2E = math.log2(math.e)


def swap(a, axis, size, d):
    return lax.ppermute(a, axis, [(i, i ^ d) for i in range(size)])


def lane_groups(a):
    total = None
    for k in range(0, a.shape[1], 128):
        part = jnp.square(a[:, k : k + 128].astype(F32))
        total = part if total is None else total + part
    return total


def half_sq_row(a):
    return 0.5 * jnp.sum(lane_groups(a).T, axis=0, keepdims=True)


def half_sq_column(a):
    return 0.5 * jnp.sum(lane_groups(a), axis=1, keepdims=True)


def column(row):
    return jnp.broadcast_to(row, (128, row.shape[1])).T


def params(mib):
    return pltpu.CompilerParams(vmem_limit_bytes=mib << 20)


def pack(train_points, center_pos, coefficients, spread, piece):
    n, in_width = center_pos.shape
    out_width = coefficients.shape[1]
    across = in_width // out_width
    q = n // across

    def body(points_ref, pos_ref, coef_ref, spread_ref, own_ref, out_ref, sem):
        start = pl.multiple_of(lax.axis_index("centers") * piece, piece)
        copy = pltpu.make_async_copy(points_ref.at[pl.ds(start, piece)], own_ref, sem)
        copy.start()
        pos = pos_ref[...]
        out_ref[:n] = pos
        for k in range(across):
            out_ref[n : n + q, k * out_width : (k + 1) * out_width] = coef_ref[k * q : (k + 1) * q]
        half = half_sq_row(pos)
        high = half.astype(BF16)
        rest = half - high.astype(F32)
        middle = rest.astype(BF16)
        low = (rest - middle.astype(F32)).astype(BF16)
        rows = [r.astype(F32) for r in (spread_ref[...], high, middle, low)]
        tail = jnp.concatenate(rows + [jnp.zeros((12, n), F32)]).astype(BF16)
        if n < in_width:
            tail = jnp.concatenate([tail, jnp.zeros((16, in_width - n), BF16)], axis=1)
        out_ref[n + q :] = tail
        copy.wait()

    return pl.pallas_call(
        body,
        out_shape=(
            jax.ShapeDtypeStruct((piece, in_width), BF16),
            jax.ShapeDtypeStruct((n + q + 16, in_width), BF16),
        ),
        in_specs=[HBM, VMEM, VMEM, VMEM],
        out_specs=(VMEM, VMEM),
        scratch_shapes=[pltpu.SemaphoreType.DMA],
        compiler_params=params(16),
        cost_estimate=pl.CostEstimate(flops=1 << 20, bytes_accessed=2 << 20, transcendentals=0),
        name="pack",
    )(train_points, center_pos, coefficients, spread.reshape(1, n))


def take(arrays, offsets, piece):
    def body(*refs):
        ins, outs, sems = refs[: len(arrays)], refs[len(arrays) : -1], refs[-1]
        made = []
        for k, d in enumerate(offsets):
            start = pl.multiple_of((lax.axis_index("centers") ^ d) * piece, piece)
            made.append(pltpu.make_async_copy(ins[k].at[pl.ds(start, piece)], outs[k], sems.at[k]))
            made[-1].start()
        for copy in made:
            copy.wait()

    return pl.pallas_call(
        body,
        out_shape=tuple(jax.ShapeDtypeStruct((piece, a.shape[1]), a.dtype) for a in arrays),
        in_specs=[HBM] * len(arrays),
        out_specs=(VMEM,) * len(arrays),
        scratch_shapes=[pltpu.SemaphoreType.DMA((len(arrays),))],
        compiler_params=params(16),
        cost_estimate=pl.CostEstimate(flops=0, bytes_accessed=2 << 20, transcendentals=0),
        name="take",
    )(*arrays)


def forward(rows, payloads, n, out_width):
    in_width = rows.shape[1]
    q = n * out_width // in_width

    def body(rows_ref, *refs):
        out_ref = refs[-1]
        x = rows_ref[...]
        row_sq = half_sq_column(x)
        total = jnp.zeros(out_ref.shape, F32)
        for ref in refs[:-1]:
            packed = ref[n : n + q]
            coef = jnp.concatenate(
                [packed[:, k : k + out_width] for k in range(0, in_width, out_width)]
            )
            tail = ref[n + q :, :n].astype(F32)
            center_sq = tail[1:2] + tail[2:3] + tail[3:4]
            rate = tail[0:1] * (-2.0 * LOG2E / in_width)
            cross = lax.dot_general(x, ref[:n], NT, preferred_element_type=F32)
            power = (row_sq + center_sq - cross) * rate
            kernel = jnp.exp2(power).astype(BF16)
            total += jnp.dot(kernel, coef, preferred_element_type=F32)
        out_ref[...] = total

    work = rows.shape[0] * len(payloads) * n
    return pl.pallas_call(
        body,
        out_shape=jax.ShapeDtypeStruct((rows.shape[0], out_width), F32),
        in_specs=[VMEM] * (1 + len(payloads)),
        out_specs=VMEM,
        compiler_params=params(16),
        cost_estimate=pl.CostEstimate(
            flops=2 * work * (in_width + out_width), bytes_accessed=3 << 20, transcendentals=work
        ),
        name="forward",
    )(rows, *payloads)


def own_kernel(center_pos, spread, blocks):
    n, in_width = center_pos.shape
    points = sum(b.shape[0] for b in blocks)

    def body(pos_ref, spread_ref, *refs):
        out_ref = refs[-1]
        pos = pos_ref[...]
        center_sq = half_sq_column(pos)
        rate = column(spread_ref[...].astype(F32) * (-2.0 * LOG2E / in_width))[:, :1]
        at = 0
        for ref in refs[:-1]:
            step = min(256, ref.shape[0])
            for start in range(0, ref.shape[0], step):
                x = ref[start : start + step]
                cross = lax.dot_general(pos, x, NT, preferred_element_type=F32)
                power = (center_sq + half_sq_row(x) - cross) * rate
                out_ref[:, at : at + step] = jnp.exp2(power).astype(BF16)
                at += step

    work = n * points
    return pl.pallas_call(
        body,
        out_shape=jax.ShapeDtypeStruct((n, points), BF16),
        in_specs=[VMEM] * (2 + len(blocks)),
        out_specs=VMEM,
        compiler_params=params(16),
        cost_estimate=pl.CostEstimate(
            flops=2 * work * in_width, bytes_accessed=3 << 20, transcendentals=work
        ),
        name="own_kernel",
    )(center_pos, spread.reshape(1, n), *blocks)


def cotangent(parts, saved, target, delta):
    def body(*refs):
        saved_ref, target_ref, delta_ref, out_ref = refs[-4:]
        pred = refs[0][...]
        for ref in refs[1:-4]:
            pred += ref[...]
        residual = pred + saved_ref[...] - target_ref[...]
        ratio = residual / delta_ref[...]
        out_ref[...] = (residual / jnp.sqrt(1.0 + ratio * ratio)).astype(BF16)

    return pl.pallas_call(
        body,
        out_shape=jax.ShapeDtypeStruct(saved.shape, BF16),
        in_specs=[VMEM] * (len(parts) + 3),
        out_specs=VMEM,
        compiler_params=params(16),
        cost_estimate=pl.CostEstimate(flops=1 << 18, bytes_accessed=1 << 20, transcendentals=1 << 16),
        name="cotangent",
    )(*parts, saved, target, delta.reshape(1, -1))


def backward(center_pos, coefficients, spread, groups, before=None, last=False):
    n, in_width = center_pos.shape
    out_width = coefficients.shape[1]
    flat = []
    for kernel, xs, cots in groups:
        flat += [kernel, *xs, *cots]
    carried = [] if before is None else list(before)
    outs = 2 if last else 3
    points = sum(kernel.shape[1] for kernel, _, _ in groups)

    def body(pos_ref, coef_in, spread_ref, *refs):
        refs, out_refs = list(refs[:-outs]), refs[-outs:]
        coef = coef_in[...]
        moment = grad_coef = total = 0.0
        if carried:
            moment, grad_coef, total = (ref[...] for ref in refs[-3:])
        for _, xs, cots in groups:
            kernel_ref = refs.pop(0)
            x_refs = [refs.pop(0) for _ in xs]
            cot_refs = [refs.pop(0) for _ in cots]
            cot = jnp.concatenate([ref[...] for ref in cot_refs])
            kernel = kernel_ref[...]
            mixing = lax.dot_general(coef, cot, NT, preferred_element_type=F32)
            weights = (kernel.astype(F32) * mixing).astype(BF16)
            ones = jnp.ones((kernel.shape[1], 128), BF16)
            grad_coef += jnp.dot(kernel, cot, preferred_element_type=F32)
            total += jnp.dot(weights, ones, preferred_element_type=F32)
            x = jnp.concatenate([ref[...] for ref in x_refs])
            moment += jnp.dot(weights, x, preferred_element_type=F32)
        out_refs[1][...] = grad_coef
        if last:
            scale = column(spread_ref[...].astype(F32)) * (2.0 / in_width)
            for k in range(0, in_width, 128):
                pos = pos_ref[:, k : k + 128].astype(F32)
                out_refs[0][:, k : k + 128] = scale * (moment[:, k : k + 128] - total * pos)
        else:
            out_refs[0][...] = moment
            out_refs[2][...] = total

    shapes = [
        jax.ShapeDtypeStruct((n, in_width), F32),
        jax.ShapeDtypeStruct((n, out_width), F32),
        jax.ShapeDtypeStruct((n, 128), F32),
    ]
    work = n * points
    return pl.pallas_call(
        body,
        out_shape=tuple(shapes[:outs]),
        in_specs=[VMEM] * (3 + len(flat) + len(carried)),
        out_specs=(VMEM,) * outs,
        compiler_params=params(24),
        cost_estimate=pl.CostEstimate(
            flops=2 * work * (in_width + 2 * out_width + 128), bytes_accessed=6 << 20, transcendentals=0
        ),
        name="backward",
    )(center_pos, coefficients, spread.reshape(1, n), *flat, *carried)


def solution(mesh):
    nz, nc = mesh.shape["points"], mesh.shape["centers"]

    def per_device(train_points, saved_preds, targets, huber_delta, center_pos, coefficients, spread):
        n_rows = train_points.shape[0]
        n, out_width = coefficients.shape
        piece = n_rows // nc

        own, payload = pack(train_points, center_pos, coefficients, spread, piece)

        layer = {0: own}
        for dz in range(2, nz, 2):
            layer[dz] = swap(own, "points", nz, dz)
        for dz in range(1, nz, 2):
            layer[dz] = swap(layer[dz - 1], "points", nz, 1)

        payloads = {0: payload}
        for d in range(2, nc, 2):
            payloads[d] = swap(payload, "centers", nc, d)
        for d in range(0, nc, 2):
            payloads[d + 1] = swap(payloads[d], "centers", nc, 1)
        payloads = [payloads[d] for d in range(nc)]

        saved, target, *local = take(
            [saved_preds, targets] + [train_points] * (nc - 1), [0, 0, *range(1, nc)], piece
        )
        local = [own, *local]

        parts = [forward(layer[dz], payloads, n, out_width) for dz in range(nz)]
        parts = [parts[0]] + [swap(parts[dz], "points", nz, dz) for dz in range(1, nz)]
        cot = cotangent(parts, saved, target, huber_delta)

        far = {0: jnp.concatenate([layer[dz] for dz in range(1, nz)])}
        cots = {0: jnp.concatenate([cot] + [swap(cot, "points", nz, dz) for dz in range(1, nz)])}
        for d in range(2, nc, 2):
            far[d], cots[d] = swap(far[0], "centers", nc, d), swap(cots[0], "centers", nc, d)
        for d in range(0, nc, 2):
            far[d + 1], cots[d + 1] = swap(far[d], "centers", nc, 1), swap(cots[d], "centers", nc, 1)

        kernels = {d: own_kernel(center_pos, spread, [local[d], far[d]]) for d in range(nc)}
        sums = None
        for d in range(0, nc, 2):
            groups = [(kernels[k], [local[k], far[k]], [cots[k]]) for k in (d, d + 1)]
            sums = backward(center_pos, coefficients, spread, groups, before=sums, last=d + 2 == nc)
        return sums

    return jax.shard_map(
        per_device,
        mesh=mesh,
        in_specs=(
            P(("groups", "points"), None),
            P(("groups", "points"), None),
            P(("groups", "points"), None),
            P("groups"),
            P(("groups", "points", "centers"), None),
            P(("groups", "points", "centers"), None),
            P(("groups", "points", "centers")),
        ),
        out_specs=(
            P(("groups", "points", "centers"), None),
            P(("groups", "points", "centers"), None),
        ),
        check_vma=False,
    )
```

time: 125 us -> 78.5 us (0.63)
  matrix products: 41 us -> 0 us
  Pallas kernels: 0 us -> 17.4 us
  local copies, waits for them, and re-layouts: 16.9 us -> 4.58 us
  other arithmetic: 10.5 us -> 0.02 us
  waiting for transfers between devices: 24.5 us -> 34.6 us
  starting transfers between devices: 30.6 us -> 20.7 us
    dot_general x20 -> x0, matrix products: 41 us -> none  [the longest x16 29.1 us: partial_pred(): total = total + jnp.dot(kernel, coef[d], preferred_element_type=jnp.float32)]
    pallas_call x0 -> x13, Pallas kernels: none -> 17.4 us  [the longest x2 6.91 us: backward(): pl.pallas_call(body, out_shape=tuple(shapes[:outs]), in_specs=[VMEM] * (3...]
    unnamed x63 -> x20, local copies, waits for them, and re-layouts: 16.2 us -> 3.88 us
    ppermute x36 -> x18, waiting for transfers between devices: 24.5 us -> 34.6 us  [swap(): return lax.ppermute(a, axis, [(i, i ^ d) for i in range(size)])]
    ppermute x36 -> x18, starting transfers between devices: 30.6 us -> 20.7 us  [swap(): return lax.ppermute(a, axis, [(i, i ^ d) for i in range(size)])]
    reduce_sum x9 -> x0, other arithmetic: 6.42 us -> none  [the longest x1 3.08 us: per_device(): all_sq = jnp.sum(jnp.square(all_x.astype(jnp.float32)), axis=1)]
    neg x3 -> x0, other arithmetic: 1.85 us -> none  [partial_pred(): kernel = jnp.exp(-rate[d][None, :] * dist / in_width).astype(jnp.bfloat16)]
    div x1 -> x0, other arithmetic: 1.26 us -> none  [per_device(): 2.0 * own_rate / in_width]
  transfers between devices with their start and end apart: 36 -> 18, of which waited for: 7 -> 7; matrix products, arithmetic and copies ran while one was open for 45% -> 0% of each run, Pallas kernels for 0% -> 17%
where the time goes in v3:
time: 78.5 us; the launch traced here: 78.2 us
  waiting for transfers between devices  34.6 us (44%)
  starting transfers between devices  20.7 us (26%)
  Pallas kernels  17.4 us (22%)
  local copies, waits for them, and re-layouts  4.58 us (6%)
  between operations  0.86 us (1%)
    ppermute x18, waiting for transfers between devices, swap(): return lax.ppermute(a, axis, [(i, i ^ d) for i in range(size)])  34.6 us
    ppermute x18, starting transfers between devices, swap(): return lax.ppermute(a, axis, [(i, i ^ d) for i in range(size)])  20.7 us
    pallas_call x2, Pallas kernels, backward(): pl.pallas_call(body, out_shape=tuple(shapes[:outs]), in_specs=[VMEM] * (3...  6.91 us
    pallas_call x4, Pallas kernels, forward(): pl.pallas_call(body, out_shape=jax.ShapeDtypeStruct((rows.shape[0], out_w...  5.26 us
    pallas_call x4, Pallas kernels, own_kernel(): pl.pallas_call(body, out_shape=jax.ShapeDtypeStruct((n, points), BF16), i...  4.28 us
    unnamed x20, local copies, waits for them, and re-layouts  3.88 us
  transfers between devices with their start and end apart: 18, of which 7 were waited for; matrix products, arithmetic and copies ran while one was open for 0% of the time, Pallas kernels for 17%

profile of v3, /device:TPU:0, one launch (start us, length us, event | category | flops | bytes accessed | tf_op | source)
XLA Modules:
  0.0 78.2 jit_solution(13107012100044108916)
XLA Ops:
  0.6 0.7 reshape.4.spread_ref
  1.3 1.2 %copy-done = bf16[1024,512]{1,0:T(8,128)(2,1)S(1)} copy-done((bf16[1024,512]{1,0:T(8,128)(2,1)S(1)}, bf16[1024,512]{1,0:T(8,128)(2,1)}, u32[]{:S(2)}) %copy-start) | copy-done | bytes 1048600
  2.5 1.0 %copy-done.2 = bf16[512,512]{1,0:T(8,128)(2,1)S(1)} copy-done((bf16[512,512]{1,0:T(8,128)(2,1)S(1)}, bf16[512,512]{1,0:T(8,128)(2,1)}, u32[]{:S(2)}) %copy-start.2) | copy-done | bytes 524312
  3.6 0.9 %copy-done.6 = bf16[512,128]{1,0:T(8,128)(2,1)S(1)} copy-done((bf16[512,128]{1,0:T(8,128)(2,1)S(1)}, bf16[512,128]{1,0:T(8,128)(2,1)}, u32[]{:S(2)}) %copy-start.6) | copy-done | bytes 131096
  4.7 3.0 %collective-permute-start.5 = (bf16[656,512]{1,0:T(8,128)(2,1)S(1)}, bf16[656,512]{1,0:T(8,128)(2,1)S(1)}, u32[]{:S(2)}, u32[]{:S(2)}) collective-permute-start(bf16[656,512]{1,0:T(8,128)(2,1)S(1)} %get-tuple-element.14.refs_0_), channel_id=1, source_target_pairs={{0,2},{1,3},{2,0},{3,1},{4,6},{5,7},{6,4},{7,5},{8,10},{9,11},{10,... | collective-permute-start | bytes 2015240 | tf_op jit(solution)/shard_map/ppermute | solution.py:18
  7.7 2.6 %collective-permute-start.1 = (bf16[256,512]{1,0:T(8,128)(2,1)S(1)}, bf16[256,512]{1,0:T(8,128)(2,1)S(1)}, u32[]{:S(2)}, u32[]{:S(2)}) collective-permute-start(bf16[256,512]{1,0:T(8,128)(2,1)S(1)} %get-tuple-element.13.rows_ref.refs_0_.refs_1_), channel_id=1, source_target_pairs={{0,8},{4,12},{8,0},{12,4},{1,9},{5,13},{9,1},{13,5},{2,10},{6,14},... | collective-permute-start | bytes 786440 | tf_op jit(solution)/shard_map/ppermute | solution.py:18
  10.3 1.6 %collective-permute-start = (bf16[256,512]{1,0:T(8,128)(2,1)S(1)}, bf16[256,512]{1,0:T(8,128)(2,1)S(1)}, u32[]{:S(2)}, u32[]{:S(2)}) collective-permute-start(bf16[256,512]{1,0:T(8,128)(2,1)S(1)} %get-tuple-element.13.rows_ref.refs_0_.refs_1_), channel_id=1, source_target_pairs={{0,4},{4,0},{8,12},{12,8},{1,5},{5,1},{9,13},{13,9},{2,6},{6,2},{1... | collective-permute-start | bytes 786440 | tf_op jit(solution)/shard_map/ppermute | solution.py:18
  11.9 10.2 %collective-permute-done.1.rows_ref = bf16[256,512]{1,0:T(8,128)(2,1)S(1)} collective-permute-done((bf16[256,512]{1,0:T(8,128)(2,1)S(1)}, bf16[256,512]{1,0:T(8,128)(2,1)S(1)}, u32[]{:S(2)}, u32[]{:S(2)}) %collective-permute-start.1) | collective-permute-done | bytes 262176 | tf_op jit(solution)/shard_map/ppermute | solution.py:18
  22.1 0.6 collective-permute-start.2
  23.3 5.9 %collective-permute-done.2.rows_ref = bf16[256,512]{1,0:T(8,128)(2,1)S(1)} collective-permute-done((bf16[256,512]{1,0:T(8,128)(2,1)S(1)}, bf16[256,512]{1,0:T(8,128)(2,1)S(1)}, u32[]{:S(2)}, u32[]{:S(2)}) %collective-permute-start.2) | collective-permute-done | bytes 262176 | tf_op jit(solution)/shard_map/ppermute | solution.py:18
  29.2 0.6 collective-permute-start.3
  29.8 1.3 %forward.7 = f32[256,128]{1,0:T(8,128)S(1)} custom-call(bf16[256,512]{1,0:T(8,128)(2,1)S(1)} %collective-permute-done.2.rows_ref, bf16[656,512]{1,0:T(8,128)(2,1)S(1)} %get-tuple-element.14.refs_0_, bf16[656,512]{1,0:T(8,128)(2,1)S(1)} %collective-permute-done.4.refs_1_, bf16[656,512]{1,0:T(8,128)(2,1)S(1)} %collective-permute-done.5.refs_2_, ...), custom_call_target="tpu_custom_call" | custom-call | flops 671088640 | bytes 3145728 | tf_op jit(solution)/shard_map/forward/pallas_call | solution.py:133
  31.1 4.6 %collective-permute-start.9 = (f32[256,128]{1,0:T(8,128)S(1)}, f32[256,128]{1,0:T(8,128)S(1)}, u32[]{:S(2)}, u32[]{:S(2)}) collective-permute-start(f32[256,128]{1,0:T(8,128)S(1)} %forward.7), channel_id=1, source_target_pairs={{0,12},{4,8},{8,4},{12,0},{1,13},{5,9},{9,5},{13,1},{2,14},{6,10},... | collective-permute-start | bytes 393224 | tf_op jit(solution)/shard_map/ppermute | solution.py:18
  35.7 1.3 %forward.5 = f32[256,128]{1,0:T(8,128)S(1)} custom-call(bf16[256,512]{1,0:T(8,128)(2,1)S(1)} %collective-permute-done.rows_ref, bf16[656,512]{1,0:T(8,128)(2,1)S(1)} %get-tuple-element.14.refs_0_, bf16[656,512]{1,0:T(8,128)(2,1)S(1)} %collective-permute-done.4.refs_1_, bf16[656,512]{1,0:T(8,128)(2,1)S(1)} %collective-permute-done.5.refs_2_, ...), custom_call_target="tpu_custom_call" | custom-call | flops 671088640 | bytes 3145728 | tf_op jit(solution)/shard_map/forward/pallas_call | solution.py:133
  37.2 1.3 %forward.6 = f32[256,128]{1,0:T(8,128)S(1)} custom-call(bf16[256,512]{1,0:T(8,128)(2,1)S(1)} %collective-permute-done.1.rows_ref, bf16[656,512]{1,0:T(8,128)(2,1)S(1)} %get-tuple-element.14.refs_0_, bf16[656,512]{1,0:T(8,128)(2,1)S(1)} %collective-permute-done.4.refs_1_, bf16[656,512]{1,0:T(8,128)(2,1)S(1)} %collective-permute-done.5.refs_2_, ...), custom_call_target="tpu_custom_call" | custom-call | flops 671088640 | bytes 3145728 | tf_op jit(solution)/shard_map/forward/pallas_call | solution.py:133
  38.5 0.6 collective-permute-start.8
  39.1 8.0 %collective-permute-done.3.refs_1_.refs_2_ = bf16[768,512]{1,0:T(8,128)(2,1)S(1)} collective-permute-done((bf16[768,512]{1,0:T(8,128)(2,1)S(1)}, bf16[768,512]{1,0:T(8,128)(2,1)S(1)}, u32[]{:S(2)}, u32[]{:S(2)}) %collective-permute-start.3) | collective-permute-done | bytes 786464 | tf_op jit(solution)/shard_map/ppermute | solution.py:18
  47.2 0.6 take.1
  47.8 1.3 %forward.4.refs_0_ = f32[256,128]{1,0:T(8,128)S(1)} custom-call(bf16[256,512]{1,0:T(8,128)(2,1)S(1)} %get-tuple-element.13.rows_ref.refs_0_.refs_1_, bf16[656,512]{1,0:T(8,128)(2,1)S(1)} %get-tuple-element.14.refs_0_, bf16[656,512]{1,0:T(8,128)(2,1)S(1)} %collective-permute-done.4.refs_1_, bf16[656,512]{1,0:T(8,128)(2,1)S(1)} %collective-permute-done.5.refs_2_, ...), custom_call_target="tpu_custom_call" | custom-call | flops 671088640 | bytes 3145728 | tf_op jit(solution)/shard_map/forward/pallas_call | solution.py:133
  49.2 0.6 copy-done.8
  49.9 2.5 %collective-permute-start.10 = (bf16[256,128]{1,0:T(8,128)(2,1)S(1)}, bf16[256,128]{1,0:T(8,128)(2,1)S(1)}, u32[]{:S(2)}, u32[]{:S(2)}) collective-permute-start(bf16[256,128]{1,0:T(8,128)(2,1)S(1)} %cotangent.1), channel_id=1, source_target_pairs={{0,4},{4,0},{8,12},{12,8},{1,5},{5,1},{9,13},{13,9},{2,6},{6,2},{1... | collective-permute-start | bytes 196616 | tf_op jit(solution)/shard_map/ppermute | solution.py:18
  52.5 3.4 %collective-permute-start.11 = (bf16[256,128]{1,0:T(8,128)(2,1)S(1)}, bf16[256,128]{1,0:T(8,128)(2,1)S(1)}, u32[]{:S(2)}, u32[]{:S(2)}) collective-permute-start(bf16[256,128]{1,0:T(8,128)(2,1)S(1)} %cotangent.1), channel_id=1, source_target_pairs={{0,8},{4,12},{8,0},{12,4},{1,9},{5,13},{9,1},{13,5},{2,10},{6,14},... | collective-permute-start | bytes 196616 | tf_op jit(solution)/shard_map/ppermute | solution.py:18
  55.9 2.9 %collective-permute-done.11 = bf16[256,128]{1,0:T(8,128)(2,1)S(1)} collective-permute-done((bf16[256,128]{1,0:T(8,128)(2,1)S(1)}, bf16[256,128]{1,0:T(8,128)(2,1)S(1)}, u32[]{:S(2)}, u32[]{:S(2)}) %collective-permute-start.11) | collective-permute-done | bytes 65568 | tf_op jit(solution)/shard_map/ppermute | solution.py:18
  58.8 3.1 %collective-permute-done.12 = bf16[256,128]{1,0:T(8,128)(2,1)S(1)} collective-permute-done((bf16[256,128]{1,0:T(8,128)(2,1)S(1)}, bf16[256,128]{1,0:T(8,128)(2,1)S(1)}, u32[]{:S(2)}, u32[]{:S(2)}) %collective-permute-start.12) | collective-permute-done | bytes 65568 | tf_op jit(solution)/shard_map/ppermute | solution.py:18
  62.0 0.6 collective-permute-start.13
  62.6 1.1 %own_kernel.6.refs_0_ = bf16[512,1024]{1,0:T(8,128)(2,1)S(1)} custom-call(bf16[512,512]{1,0:T(8,128)(2,1)S(1)} %copy-done.3, bf16[1,512]{1,0:T(2,128)(2,1)S(1)} %reshape.4.spread_ref, bf16[256,512]{1,0:T(8,128)(2,1)S(1)} %get-tuple-element.13.rows_ref.refs_0_.refs_1_, bf16[768,512]{1,0:T(8,128)(2,1)S(1)} %constant_dynamic-update-slice_fusion.refs_1_.refs_2_), custom_call_target="tpu_custom_call" | custom-call | flops 536870912 | bytes 3145728 | tf_op jit(solution)/shard_map/own_kernel/pallas_call | solution.py:166
  63.7 1.1 %own_kernel.4.refs_0_ = bf16[512,1024]{1,0:T(8,128)(2,1)S(1)} custom-call(bf16[512,512]{1,0:T(8,128)(2,1)S(1)} %copy-done.3, bf16[1,512]{1,0:T(2,128)(2,1)S(1)} %reshape.4.spread_ref, bf16[256,512]{1,0:T(8,128)(2,1)S(1)} %get-tuple-element.12.refs_0_.refs_1_, bf16[768,512]{1,0:T(8,128)(2,1)S(1)} %collective-permute-done.3.refs_1_.refs_2_), custom_call_target="tpu_custom_call" | custom-call | flops 536870912 | bytes 3145728 | tf_op jit(solution)/shard_map/own_kernel/pallas_call | solution.py:166
  64.7 4.3 %collective-permute-done.13.refs_3_ = bf16[1024,128]{1,0:T(8,128)(2,1)S(1)} collective-permute-done((bf16[1024,128]{1,0:T(8,128)(2,1)S(1)}, bf16[1024,128]{1,0:T(8,128)(2,1)S(1)}, u32[]{:S(2)}, u32[]{:S(2)}) %collective-permute-start.13) | collective-permute-done | bytes 262176 | tf_op jit(solution)/shard_map/ppermute | solution.py:18
  69.0 1.1 %own_kernel.7.refs_4_ = bf16[512,1024]{1,0:T(8,128)(2,1)S(1)} custom-call(bf16[512,512]{1,0:T(8,128)(2,1)S(1)} %copy-done.3, bf16[1,512]{1,0:T(2,128)(2,1)S(1)} %reshape.4.spread_ref, bf16[256,512]{1,0:T(8,128)(2,1)S(1)} %get-tuple-element.18.refs_0_.refs_5_, bf16[768,512]{1,0:T(8,128)(2,1)S(1)} %collective-permute-done.16.refs_1_.refs_6_), custom_call_target="tpu_custom_call" | custom-call | flops 536870912 | bytes 3145728 | tf_op jit(solution)/shard_map/own_kernel/pallas_call | solution.py:166
  70.1 2.9 %backward.2 = (f32[512,512]{1,0:T(8,128)S(1)}, f32[512,128]{1,0:T(8,128)S(1)}, f32[512,128]{1,0:T(8,128)S(1)}) custom-call(bf16[512,512]{1,0:T(8,128)(2,1)S(1)} %copy-done.3, bf16[512,128]{1,0:T(8,128)(2,1)S(1)} %copy-done.7, bf16[1,512]{1,0:T(2,128)(2,1)S(1)} %reshape.4.spread_ref, bf16[512,1024]{1,0:T(8,128)(2,1)S(1)} %own_kernel.6.refs_0_, ...), custom_call_target="tpu_custom_call" | custom-call | flops 1879048192 | bytes 6291456 | tf_op jit(solution)/shard_map/backward/pallas_call | solution.py:245
  73.1 1.1 %own_kernel.5.refs_4_ = bf16[512,1024]{1,0:T(8,128)(2,1)S(1)} custom-call(bf16[512,512]{1,0:T(8,128)(2,1)S(1)} %copy-done.3, bf16[1,512]{1,0:T(2,128)(2,1)S(1)} %reshape.4.spread_ref, bf16[256,512]{1,0:T(8,128)(2,1)S(1)} %get-tuple-element.17.refs_0_.refs_5_, bf16[768,512]{1,0:T(8,128)(2,1)S(1)} %collective-permute-done.14.refs_1_.refs_6_), custom_call_target="tpu_custom_call" | custom-call | flops 536870912 | bytes 3145728 | tf_op jit(solution)/shard_map/own_kernel/pallas_call | solution.py:166
  74.1 4.0 %backward.3 = (f32[512,512]{1,0:T(8,128)}, f32[512,128]{1,0:T(8,128)}) custom-call(bf16[512,512]{1,0:T(8,128)(2,1)S(1)} %copy-done.3, bf16[512,128]{1,0:T(8,128)(2,1)S(1)} %copy-done.7, bf16[1,512]{1,0:T(2,128)(2,1)S(1)} %reshape.4.spread_ref, bf16[512,1024]{1,0:T(8,128)(2,1)S(1)} %own_kernel.4.refs_0_, ...), custom_call_target="tpu_custom_call" | custom-call | flops 1879048192 | bytes 6291456 | tf_op jit(solution)/shard_map/backward/pallas_call | solution.py:245
  (40 shorter events, 1.2 us)
Async XLA Ops:
  1.3 1.2 %copy-start = (bf16[1024,512]{1,0:T(8,128)(2,1)S(1)}, bf16[1024,512]{1,0:T(8,128)(2,1)}, u32[]{:S(2)}) copy-start(bf16[1024,512]{1,0:T(8,128)(2,1)} %points_ref.1) | copy-start | bytes 3145732
  2.5 1.0 %copy-start.2 = (bf16[512,512]{1,0:T(8,128)(2,1)S(1)}, bf16[512,512]{1,0:T(8,128)(2,1)}, u32[]{:S(2)}) copy-start(bf16[512,512]{1,0:T(8,128)(2,1)} %pos_ref.13) | copy-start | bytes 1572868
  3.6 0.9 %copy-start.6 = (bf16[512,128]{1,0:T(8,128)(2,1)S(1)}, bf16[512,128]{1,0:T(8,128)(2,1)}, u32[]{:S(2)}) copy-start(bf16[512,128]{1,0:T(8,128)(2,1)} %coef_in.3) | copy-start | bytes 393220
  4.7 18.1 %collective-permute-start.5 = (bf16[656,512]{1,0:T(8,128)(2,1)S(1)}, bf16[656,512]{1,0:T(8,128)(2,1)S(1)}, u32[]{:S(2)}, u32[]{:S(2)}) collective-permute-start(bf16[656,512]{1,0:T(8,128)(2,1)S(1)} %get-tuple-element.14.refs_0_), channel_id=1, source_target_pairs={{0,2},{1,3},{2,0},{3,1},{4,6},{5,7},{6,4},{7,5},{8,10},{9,11},{10,... | collective-permute-start | bytes 2015240 | tf_op jit(solution)/shard_map/ppermute | solution.py:18
  7.7 14.4 %collective-permute-start.1 = (bf16[256,512]{1,0:T(8,128)(2,1)S(1)}, bf16[256,512]{1,0:T(8,128)(2,1)S(1)}, u32[]{:S(2)}, u32[]{:S(2)}) collective-permute-start(bf16[256,512]{1,0:T(8,128)(2,1)S(1)} %get-tuple-element.13.rows_ref.refs_0_.refs_1_), channel_id=1, source_target_pairs={{0,8},{4,12},{8,0},{12,4},{1,9},{5,13},{9,1},{13,5},{2,10},{6,14},... | collective-permute-start | bytes 786440 | tf_op jit(solution)/shard_map/ppermute | solution.py:18
  10.3 12.4 %collective-permute-start = (bf16[256,512]{1,0:T(8,128)(2,1)S(1)}, bf16[256,512]{1,0:T(8,128)(2,1)S(1)}, u32[]{:S(2)}, u32[]{:S(2)}) collective-permute-start(bf16[256,512]{1,0:T(8,128)(2,1)S(1)} %get-tuple-element.13.rows_ref.refs_0_.refs_1_), channel_id=1, source_target_pairs={{0,4},{4,0},{8,12},{12,8},{1,5},{5,1},{9,13},{13,9},{2,6},{6,2},{1... | collective-permute-start | bytes 786440 | tf_op jit(solution)/shard_map/ppermute | solution.py:18
  22.1 7.1 %collective-permute-start.2 = (bf16[256,512]{1,0:T(8,128)(2,1)S(1)}, bf16[256,512]{1,0:T(8,128)(2,1)S(1)}, u32[]{:S(2)}, u32[]{:S(2)}) collective-permute-start(bf16[256,512]{1,0:T(8,128)(2,1)S(1)} %collective-permute-done.1.rows_ref), channel_id=1, source_target_pairs={{0,4},{4,0},{8,12},{12,8},{1,5},{5,1},{9,13},{13,9},{2,6},{6,2},{1... | collective-permute-start | bytes 786440 | tf_op jit(solution)/shard_map/ppermute | solution.py:18
  22.7 7.1 %collective-permute-start.4 = (bf16[656,512]{1,0:T(8,128)(2,1)S(1)}, bf16[656,512]{1,0:T(8,128)(2,1)S(1)}, u32[]{:S(2)}, u32[]{:S(2)}) collective-permute-start(bf16[656,512]{1,0:T(8,128)(2,1)S(1)} %get-tuple-element.14.refs_0_), channel_id=1, source_target_pairs={{0,1},{1,0},{2,3},{3,2},{4,5},{5,4},{6,7},{7,6},{8,9},{9,8},{10,11... | collective-permute-start | bytes 2015240 | tf_op jit(solution)/shard_map/ppermute | solution.py:18
  22.8 7.0 %collective-permute-start.6 = (bf16[656,512]{1,0:T(8,128)(2,1)S(1)}, bf16[656,512]{1,0:T(8,128)(2,1)S(1)}, u32[]{:S(2)}, u32[]{:S(2)}) collective-permute-start(bf16[656,512]{1,0:T(8,128)(2,1)S(1)} %collective-permute-done.5.refs_2_), channel_id=1, source_target_pairs={{0,1},{1,0},{2,3},{3,2},{4,5},{5,4},{6,7},{7,6},{8,9},{9,8},{10,11... | collective-permute-start | bytes 2015240 | tf_op jit(solution)/shard_map/ppermute | solution.py:18
  29.2 17.9 %collective-permute-start.3 = (bf16[768,512]{1,0:T(8,128)(2,1)S(1)}, bf16[768,512]{1,0:T(8,128)(2,1)S(1)}, u32[]{:S(2)}, u32[]{:S(2)}) collective-permute-start(bf16[768,512]{1,0:T(8,128)(2,1)S(1)} %constant_dynamic-update-slice_fusion.refs_1_.refs_2_), channel_id=1, source_target_pairs={{0,2},{1,3},{2,0},{3,1},{4,6},{5,7},{6,4},{7,5},{8,10},{9,11},{10,... | collective-permute-start | bytes 2359304 | tf_op jit(solution)/shard_map/ppermute | solution.py:18
  29.8 39.2 %collective-permute-start.16 = (bf16[768,512]{1,0:T(8,128)(2,1)S(1)}, bf16[768,512]{1,0:T(8,128)(2,1)S(1)}, u32[]{:S(2)}, u32[]{:S(2)}) collective-permute-start(bf16[768,512]{1,0:T(8,128)(2,1)S(1)} %constant_dynamic-update-slice_fusion.refs_1_.refs_2_), channel_id=1, source_target_pairs={{0,1},{1,0},{2,3},{3,2},{4,5},{5,4},{6,7},{7,6},{8,9},{9,8},{10,11... | collective-permute-start | bytes 2359304 | tf_op jit(solution)/shard_map/ppermute | solution.py:18
  31.1 18.0 %collective-permute-start.9 = (f32[256,128]{1,0:T(8,128)S(1)}, f32[256,128]{1,0:T(8,128)S(1)}, u32[]{:S(2)}, u32[]{:S(2)}) collective-permute-start(f32[256,128]{1,0:T(8,128)S(1)} %forward.7), channel_id=1, source_target_pairs={{0,12},{4,8},{8,4},{12,0},{1,13},{5,9},{9,5},{13,1},{2,14},{6,10},... | collective-permute-start | bytes 393224 | tf_op jit(solution)/shard_map/ppermute | solution.py:18
  37.1 10.1 %copy-start.1 = (bf16[1024,512]{1,0:T(8,128)(2,1)S(1)}, bf16[1024,512]{1,0:T(8,128)(2,1)}, u32[]{:S(2)}) copy-start(bf16[1024,512]{1,0:T(8,128)(2,1)} %points_ref.1) | copy-start | bytes 3145732
  37.1 10.1 %copy-start.4 = (f32[1024,128]{1,0:T(8,128)S(1)}, f32[1024,128]{1,0:T(8,128)}, u32[]{:S(2)}) copy-start(f32[1024,128]{1,0:T(8,128)} %refs_0_.1) | copy-start | bytes 1572868
  37.1 10.1 %copy-start.5 = (f32[1024,128]{1,0:T(8,128)S(1)}, f32[1024,128]{1,0:T(8,128)}, u32[]{:S(2)}) copy-start(f32[1024,128]{1,0:T(8,128)} %refs_1_.1) | copy-start | bytes 1572868
  37.1 12.1 %collective-permute-start.7 = (f32[256,128]{1,0:T(8,128)S(1)}, f32[256,128]{1,0:T(8,128)S(1)}, u32[]{:S(2)}, u32[]{:S(2)}) collective-permute-start(f32[256,128]{1,0:T(8,128)S(1)} %forward.5), channel_id=1, source_target_pairs={{0,4},{4,0},{8,12},{12,8},{1,5},{5,1},{9,13},{13,9},{2,6},{6,2},{1... | collective-permute-start | bytes 393224 | tf_op jit(solution)/shard_map/ppermute | solution.py:18
  38.5 10.7 %collective-permute-start.8 = (f32[256,128]{1,0:T(8,128)S(1)}, f32[256,128]{1,0:T(8,128)S(1)}, u32[]{:S(2)}, u32[]{:S(2)}) collective-permute-start(f32[256,128]{1,0:T(8,128)S(1)} %forward.6), channel_id=1, source_target_pairs={{0,8},{4,12},{8,0},{12,4},{1,9},{5,13},{9,1},{13,5},{2,10},{6,14},... | collective-permute-start | bytes 393224 | tf_op jit(solution)/shard_map/ppermute | solution.py:18
  47.1 25.9 %collective-permute-start.14 = (bf16[768,512]{1,0:T(8,128)(2,1)S(1)}, bf16[768,512]{1,0:T(8,128)(2,1)S(1)}, u32[]{:S(2)}, u32[]{:S(2)}) collective-permute-start(bf16[768,512]{1,0:T(8,128)(2,1)S(1)} %collective-permute-done.3.refs_1_.refs_2_), channel_id=1, source_target_pairs={{0,1},{1,0},{2,3},{3,2},{4,5},{5,4},{6,7},{7,6},{8,9},{9,8},{10,11... | collective-permute-start | bytes 2359304 | tf_op jit(solution)/shard_map/ppermute | solution.py:18
  49.2 0.7 copy-start.8
  49.8 12.8 %copy-start.3 = (bf16[512,512]{1,0:T(8,128)(2,1)S(1)}, bf16[512,512]{1,0:T(8,128)(2,1)}, u32[]{:S(2)}) copy-start(bf16[512,512]{1,0:T(8,128)(2,1)} %pos_ref.13) | copy-start | bytes 1572868
  49.9 6.0 %collective-permute-start.10 = (bf16[256,128]{1,0:T(8,128)(2,1)S(1)}, bf16[256,128]{1,0:T(8,128)(2,1)S(1)}, u32[]{:S(2)}, u32[]{:S(2)}) collective-permute-start(bf16[256,128]{1,0:T(8,128)(2,1)S(1)} %cotangent.1), channel_id=1, source_target_pairs={{0,4},{4,0},{8,12},{12,8},{1,5},{5,1},{9,13},{13,9},{2,6},{6,2},{1... | collective-permute-start | bytes 196616 | tf_op jit(solution)/shard_map/ppermute | solution.py:18
  52.5 6.4 %collective-permute-start.11 = (bf16[256,128]{1,0:T(8,128)(2,1)S(1)}, bf16[256,128]{1,0:T(8,128)(2,1)S(1)}, u32[]{:S(2)}, u32[]{:S(2)}) collective-permute-start(bf16[256,128]{1,0:T(8,128)(2,1)S(1)} %cotangent.1), channel_id=1, source_target_pairs={{0,8},{4,12},{8,0},{12,4},{1,9},{5,13},{9,1},{13,5},{2,10},{6,14},... | collective-permute-start | bytes 196616 | tf_op jit(solution)/shard_map/ppermute | solution.py:18
  55.8 6.1 %collective-permute-start.12 = (bf16[256,128]{1,0:T(8,128)(2,1)S(1)}, bf16[256,128]{1,0:T(8,128)(2,1)S(1)}, u32[]{:S(2)}, u32[]{:S(2)}) collective-permute-start(bf16[256,128]{1,0:T(8,128)(2,1)S(1)} %cotangent.1), channel_id=1, source_target_pairs={{0,12},{4,8},{8,4},{12,0},{1,13},{5,9},{9,5},{13,1},{2,14},{6,10},... | collective-permute-start | bytes 196616 | tf_op jit(solution)/shard_map/ppermute | solution.py:18
  62.0 7.1 %collective-permute-start.13 = (bf16[1024,128]{1,0:T(8,128)(2,1)S(1)}, bf16[1024,128]{1,0:T(8,128)(2,1)S(1)}, u32[]{:S(2)}, u32[]{:S(2)}) collective-permute-start(bf16[1024,128]{1,0:T(8,128)(2,1)S(1)} %pad_maximum_fusion.refs_3_), channel_id=1, source_target_pairs={{0,2},{1,3},{2,0},{3,1},{4,6},{5,7},{6,4},{7,5},{8,10},{9,11},{10,... | collective-permute-start | bytes 786440 | tf_op jit(solution)/shard_map/ppermute | solution.py:18
  62.6 7.5 %collective-permute-start.17 = (bf16[1024,128]{1,0:T(8,128)(2,1)S(1)}, bf16[1024,128]{1,0:T(8,128)(2,1)S(1)}, u32[]{:S(2)}, u32[]{:S(2)}) collective-permute-start(bf16[1024,128]{1,0:T(8,128)(2,1)S(1)} %pad_maximum_fusion.refs_3_), channel_id=1, source_target_pairs={{0,1},{1,0},{2,3},{3,2},{4,5},{5,4},{6,7},{7,6},{8,9},{9,8},{10,11... | collective-permute-start | bytes 786440 | tf_op jit(solution)/shard_map/ppermute | solution.py:18
  69.0 5.1 %collective-permute-start.15 = (bf16[1024,128]{1,0:T(8,128)(2,1)S(1)}, bf16[1024,128]{1,0:T(8,128)(2,1)S(1)}, u32[]{:S(2)}, u32[]{:S(2)}) collective-permute-start(bf16[1024,128]{1,0:T(8,128)(2,1)S(1)} %collective-permute-done.13.refs_3_), channel_id=1, source_target_pairs={{0,1},{1,0},{2,3},{3,2},{4,5},{5,4},{6,7},{7,6},{8,9},{9,8},{10,11... | collective-permute-start | bytes 786440 | tf_op jit(solution)/shard_map/ppermute | solution.py:18
  69.0 1.1 %copy-start.7 = (bf16[512,128]{1,0:T(8,128)(2,1)S(1)}, bf16[512,128]{1,0:T(8,128)(2,1)}, u32[]{:S(2)}) copy-start(bf16[512,128]{1,0:T(8,128)(2,1)} %coef_in.3) | copy-start | bytes 393220

commit v4 on v3

--- a/solution.py
+++ b/solution.py
@@ -12,10 +12,16 @@
 VMEM = pl.BlockSpec(memory_space=pltpu.VMEM)
 NT = (((1,), (1,)), ((), ()))
 LOG2E = math.log2(math.e)
+COVER = 8
+BRIEF = pl.CostEstimate(flops=1, bytes_accessed=1, transcendentals=0)
 
 
 def swap(a, axis, size, d):
     return lax.ppermute(a, axis, [(i, i ^ d) for i in range(size)])
+
+
+def after(a, *others):
+    return lax.optimization_barrier((a, *others))[0]
 
 
 def lane_groups(a):
@@ -48,12 +54,19 @@
     across = in_width // out_width
     q = n // across
 
-    def body(points_ref, pos_ref, coef_ref, spread_ref, own_ref, out_ref, sem):
+    def body(points_ref, pos_in, coef_in, spread_ref, own_ref, out_ref, coef_ref, sems):
         start = pl.multiple_of(lax.axis_index("centers") * piece, piece)
-        copy = pltpu.make_async_copy(points_ref.at[pl.ds(start, piece)], own_ref, sem)
-        copy.start()
-        pos = pos_ref[...]
-        out_ref[:n] = pos
+        pairs = [
+            (pos_in, out_ref.at[:n]),
+            (coef_in, coef_ref),
+            (points_ref.at[pl.ds(start, piece)], own_ref),
+        ]
+        made = [pltpu.make_async_copy(*pair, sems.at[k]) for k, pair in enumerate(pairs)]
+        for copy in made:
+            copy.start()
+        for copy in made:
+            copy.wait()
+        pos = out_ref[:n]
         for k in range(across):
             out_ref[n : n + q, k * out_width : (k + 1) * out_width] = coef_ref[k * q : (k + 1) * q]
         half = half_sq_row(pos)
@@ -66,7 +79,6 @@
         if n < in_width:
             tail = jnp.concatenate([tail, jnp.zeros((16, in_width - n), BF16)], axis=1)
         out_ref[n + q :] = tail
-        copy.wait()
 
     return pl.pallas_call(
         body,
@@ -74,39 +86,41 @@
             jax.ShapeDtypeStruct((piece, in_width), BF16),
             jax.ShapeDtypeStruct((n + q + 16, in_width), BF16),
         ),
-        in_specs=[HBM, VMEM, VMEM, VMEM],
+        in_specs=[HBM, HBM, HBM, VMEM],
         out_specs=(VMEM, VMEM),
-        scratch_shapes=[pltpu.SemaphoreType.DMA],
-        compiler_params=params(16),
-        cost_estimate=pl.CostEstimate(flops=1 << 20, bytes_accessed=2 << 20, transcendentals=0),
+        scratch_shapes=[pltpu.VMEM((n, out_width), BF16), pltpu.SemaphoreType.DMA((3,))],
+        compiler_params=params(62),
+        cost_estimate=BRIEF,
         name="pack",
     )(train_points, center_pos, coefficients, spread.reshape(1, n))
 
 
-def take(arrays, offsets, piece):
+def take(arrays, offsets, piece, row):
     def body(*refs):
-        ins, outs, sems = refs[: len(arrays)], refs[len(arrays) : -1], refs[-1]
+        row_ref, ins, outs, sems = refs[0], refs[1 : len(arrays) + 1], refs[len(arrays) + 1 : -1], refs[-1]
         made = []
         for k, d in enumerate(offsets):
             start = pl.multiple_of((lax.axis_index("centers") ^ d) * piece, piece)
             made.append(pltpu.make_async_copy(ins[k].at[pl.ds(start, piece)], outs[k], sems.at[k]))
             made[-1].start()
+        outs[-1][...] = row_ref[...]
         for copy in made:
             copy.wait()
 
     return pl.pallas_call(
         body,
-        out_shape=tuple(jax.ShapeDtypeStruct((piece, a.shape[1]), a.dtype) for a in arrays),
-        in_specs=[HBM] * len(arrays),
-        out_specs=(VMEM,) * len(arrays),
+        out_shape=tuple(jax.ShapeDtypeStruct((piece, a.shape[1]), a.dtype) for a in arrays)
+        + (jax.ShapeDtypeStruct((1, row.shape[0]), row.dtype),),
+        in_specs=[VMEM] + [HBM] * len(arrays),
+        out_specs=(VMEM,) * (len(arrays) + 1),
         scratch_shapes=[pltpu.SemaphoreType.DMA((len(arrays),))],
         compiler_params=params(16),
-        cost_estimate=pl.CostEstimate(flops=0, bytes_accessed=2 << 20, transcendentals=0),
+        cost_estimate=BRIEF,
         name="take",
-    )(*arrays)
-
-
-def forward(rows, payloads, n, out_width):
+    )(row.reshape(1, -1), *arrays)
+
+
+def forward(rows, payloads, n, out_width, before=()):
     in_width = rows.shape[1]
     q = n * out_width // in_width
 
@@ -115,7 +129,9 @@
         x = rows_ref[...]
         row_sq = half_sq_column(x)
         total = jnp.zeros(out_ref.shape, F32)
-        for ref in refs[:-1]:
+        for ref in refs[len(payloads) : -1]:
+            total += ref[...]
+        for ref in refs[: len(payloads)]:
             packed = ref[n : n + q]
             coef = jnp.concatenate(
                 [packed[:, k : k + out_width] for k in range(0, in_width, out_width)]
@@ -133,14 +149,14 @@
     return pl.pallas_call(
         body,
         out_shape=jax.ShapeDtypeStruct((rows.shape[0], out_width), F32),
-        in_specs=[VMEM] * (1 + len(payloads)),
+        in_specs=[VMEM] * (1 + len(payloads) + len(before)),
         out_specs=VMEM,
         compiler_params=params(16),
         cost_estimate=pl.CostEstimate(
-            flops=2 * work * (in_width + out_width), bytes_accessed=3 << 20, transcendentals=work
+            flops=COVER * 2 * work * (in_width + out_width), bytes_accessed=3 << 20, transcendentals=work
         ),
         name="forward",
-    )(rows, *payloads)
+    )(rows, *payloads, *before)
 
 
 def own_kernel(center_pos, spread, blocks):
@@ -162,16 +178,13 @@
                 out_ref[:, at : at + step] = jnp.exp2(power).astype(BF16)
                 at += step
 
-    work = n * points
     return pl.pallas_call(
         body,
         out_shape=jax.ShapeDtypeStruct((n, points), BF16),
         in_specs=[VMEM] * (2 + len(blocks)),
         out_specs=VMEM,
         compiler_params=params(16),
-        cost_estimate=pl.CostEstimate(
-            flops=2 * work * in_width, bytes_accessed=3 << 20, transcendentals=work
-        ),
+        cost_estimate=BRIEF,
         name="own_kernel",
     )(center_pos, spread.reshape(1, n), *blocks)
 
@@ -192,9 +205,9 @@
         in_specs=[VMEM] * (len(parts) + 3),
         out_specs=VMEM,
         compiler_params=params(16),
-        cost_estimate=pl.CostEstimate(flops=1 << 18, bytes_accessed=1 << 20, transcendentals=1 << 16),
+        cost_estimate=BRIEF,
         name="cotangent",
-    )(*parts, saved, target, delta.reshape(1, -1))
+    )(*parts, saved, target, delta)
 
 
 def backward(center_pos, coefficients, spread, groups, before=None, last=False):
@@ -241,16 +254,13 @@
         jax.ShapeDtypeStruct((n, out_width), F32),
         jax.ShapeDtypeStruct((n, 128), F32),
     ]
-    work = n * points
     return pl.pallas_call(
         body,
         out_shape=tuple(shapes[:outs]),
         in_specs=[VMEM] * (3 + len(flat) + len(carried)),
         out_specs=(VMEM,) * outs,
         compiler_params=params(24),
-        cost_estimate=pl.CostEstimate(
-            flops=2 * work * (in_width + 2 * out_width + 128), bytes_accessed=6 << 20, transcendentals=0
-        ),
+        cost_estimate=BRIEF,
         name="backward",
     )(center_pos, coefficients, spread.reshape(1, n), *flat, *carried)
 
@@ -268,37 +278,68 @@
         layer = {0: own}
         for dz in range(2, nz, 2):
             layer[dz] = swap(own, "points", nz, dz)
-        for dz in range(1, nz, 2):
+        layer[1] = swap(own, "points", nz, 1)
+
+        payloads = {0: payload}
+        for d in range(2, nc, 2):
+            payloads[d] = swap(payload, "centers", nc, d)
+        payloads[1] = swap(payload, "centers", nc, 1)
+        near = [payloads[0], payloads[1]]
+        parts = {dz: forward(layer[dz], near, n, out_width) for dz in (*range(2, nz, 2), 1)}
+        for dz in range(3, nz, 2):
             layer[dz] = swap(layer[dz - 1], "points", nz, 1)
-
-        payloads = {0: payload}
-        for d in range(2, nc, 2):
-            payloads[d] = swap(payload, "centers", nc, d)
-        for d in range(0, nc, 2):
-            payloads[d + 1] = swap(payloads[d], "centers", nc, 1)
-        payloads = [payloads[d] for d in range(nc)]
-
-        saved, target, *local = take(
-            [saved_preds, targets] + [train_points] * (nc - 1), [0, 0, *range(1, nc)], piece
+        for d in range(2, nc, 2):
+            payloads[d + 1] = swap(after(payloads[d], layer[2]), "centers", nc, 1)
+        rest = [payloads[d] for d in range(2, nc)]
+
+        saved, target, *local, delta = take(
+            [saved_preds, targets] + [train_points] * (nc - 1), [0, 0, *range(1, nc)], piece, huber_delta
         )
         local = [own, *local]
 
-        parts = [forward(layer[dz], payloads, n, out_width) for dz in range(nz)]
-        parts = [parts[0]] + [swap(parts[dz], "points", nz, dz) for dz in range(1, nz)]
-        cot = cotangent(parts, saved, target, huber_delta)
-
-        far = {0: jnp.concatenate([layer[dz] for dz in range(1, nz)])}
-        cots = {0: jnp.concatenate([cot] + [swap(cot, "points", nz, dz) for dz in range(1, nz)])}
-        for d in range(2, nc, 2):
-            far[d], cots[d] = swap(far[0], "centers", nc, d), swap(cots[0], "centers", nc, d)
+        received = {}
+        for dz in range(2, nz, 2):
+            parts[dz] = forward(layer[dz], rest, n, out_width, [parts[dz]])
+            received[dz] = swap(parts[dz], "points", nz, dz)
+        for dz in range(3, nz, 2):
+            parts[dz] = forward(after(layer[dz], parts[dz - 1]), near + rest, n, out_width)
+            received[dz] = swap(parts[dz], "points", nz, dz)
+        parts[1] = forward(layer[1], rest, n, out_width, [after(parts[1], parts[nz - 1])])
+        received[1] = swap(parts[1], "points", nz, 1)
+        soon = [received.pop(dz) for dz in range(2, nz, 2)]
+        parts[0] = forward(after(own, parts[1]), near + rest, n, out_width, soon)
+
+        early = {0: jnp.concatenate([layer[dz] for dz in range(1, nz - 1)])}
+        late = {0: after(layer[nz - 1], parts[0])}
+        for d in range(2, nc, 2):
+            early[d] = swap(after(early[0], payloads[d]), "centers", nc, d)
+            late[d] = swap(late[0], "centers", nc, d)
+        early[1] = swap(after(early[0], payloads[nc - 1]), "centers", nc, 1)
+        late[1] = swap(late[0], "centers", nc, 1)
+        kernels = {d: own_kernel(center_pos, spread, [local[d], early[d], late[d]]) for d in (0, 1)}
+
+        cot = cotangent([parts[0], *received.values()], saved, target, delta)
+
+        for d in range(2, nc, 2):
+            early[d + 1] = swap(after(early[d], cot), "centers", nc, 1)
+            late[d + 1] = swap(after(late[d], cot), "centers", nc, 1)
+            for k in (d, d + 1):
+                kernels[k] = own_kernel(center_pos, spread, [local[k], early[k], late[k]])
+
+        cots = {0: [cot] + [swap(cot, "points", nz, dz) for dz in range(1, nz)]}
+        for d in range(2, nc, 2):
+            held = after(cots[0][2], kernels[0], kernels[1])
+            cots[d] = [swap(a, "centers", nc, d) for a in (*cots[0][:2], held, *cots[0][3:])]
         for d in range(0, nc, 2):
-            far[d + 1], cots[d + 1] = swap(far[d], "centers", nc, 1), swap(cots[d], "centers", nc, 1)
-
-        kernels = {d: own_kernel(center_pos, spread, [local[d], far[d]]) for d in range(nc)}
-        sums = None
-        for d in range(0, nc, 2):
-            groups = [(kernels[k], [local[k], far[k]], [cots[k]]) for k in (d, d + 1)]
-            sums = backward(center_pos, coefficients, spread, groups, before=sums, last=d + 2 == nc)
+            cots[d + 1] = [swap(jnp.concatenate(cots[d]), "centers", nc, 1)]
+
+        def group(d):
+            return (kernels[d], [local[d], early[d], late[d]], cots[d])
+
+        kernels[0] = after(kernels[0], *(kernels[d] for d in range(1, nc)))
+        sums = backward(center_pos, coefficients, spread, [group(0), group(1)])
+        for d in range(2, nc):
+            sums = backward(center_pos, coefficients, spread, [group(d)], before=sums, last=d + 1 == nc)
         return sums
 
     return jax.shard_map(

time: 78.5 us -> 72.7 us (0.926)
  waiting for transfers between devices: 34.6 us -> 23.7 us
  starting transfers between devices: 20.7 us -> 25.9 us
  local copies, waits for them, and re-layouts: 4.58 us -> 1.36 us
  Pallas kernels: 17.4 us -> 20.6 us
    ppermute x18 -> x24, waiting for transfers between devices: 34.6 us -> 23.7 us  [swap(): return lax.ppermute(a, axis, [(i, i ^ d) for i in range(size)])]
    ppermute x18 -> x24, starting transfers between devices: 20.7 us -> 25.9 us  [swap(): return lax.ppermute(a, axis, [(i, i ^ d) for i in range(size)])]
    unnamed x20 -> x19, local copies, waits for them, and re-layouts: 3.88 us -> 0.07 us
    pallas_call x1, Pallas kernels: 0.23 us -> 2.87 us  [pack(): pl.pallas_call(body, out_shape=(jax.ShapeDtypeStruct((piece, in_width), B...]
    pallas_call x4 -> x6, Pallas kernels: 5.26 us -> 5.7 us  [forward(): pl.pallas_call(body, out_shape=jax.ShapeDtypeStruct((rows.shape[0], out_w...]
    pallas_call x2 -> x3, Pallas kernels: 6.91 us -> 7.02 us  [backward(): pl.pallas_call(body, out_shape=tuple(shapes[:outs]), in_specs=[VMEM] * (3...]
  transfers between devices with their start and end apart: 18 -> 24, of which waited for: 7 -> 10; matrix products, arithmetic and copies ran while one was open for 0% -> 0% of each run, Pallas kernels for 17% -> 21%
where the time goes in v4:
time: 72.7 us; the launch traced here: 72.4 us
  starting transfers between devices  25.9 us (36%)
  waiting for transfers between devices  23.7 us (33%)
  Pallas kernels  20.6 us (28%)
  local copies, waits for them, and re-layouts  1.36 us (2%)
  between operations  0.93 us (1%)
    ppermute x24, starting transfers between devices, swap(): return lax.ppermute(a, axis, [(i, i ^ d) for i in range(size)])  25.9 us
    ppermute x24, waiting for transfers between devices, swap(): return lax.ppermute(a, axis, [(i, i ^ d) for i in range(size)])  23.7 us
    pallas_call x3, Pallas kernels, backward(): pl.pallas_call(body, out_shape=tuple(shapes[:outs]), in_specs=[VMEM] * (3...  7.02 us
    pallas_call x6, Pallas kernels, forward(): pl.pallas_call(body, out_shape=jax.ShapeDtypeStruct((rows.shape[0], out_w...  5.7 us
    pallas_call x4, Pallas kernels, own_kernel(): pl.pallas_call(body, out_shape=jax.ShapeDtypeStruct((n, points), BF16), i...  4.25 us
    pallas_call x1, Pallas kernels, pack(): pl.pallas_call(body, out_shape=(jax.ShapeDtypeStruct((piece, in_width), B...  2.87 us
  transfers between devices with their start and end apart: 24, of which 10 were waited for; matrix products, arithmetic and copies ran while one was open for 0% of the time, Pallas kernels for 21%

profile of v4, /device:TPU:0, one launch (start us, length us, event | category | flops | bytes accessed | tf_op | source)
XLA Modules:
  0.0 72.4 jit_solution(18192133440931613074)
XLA Ops:
  0.6 1.3 %reshape.4.spread_ref = bf16[1,512]{1,0:T(2,128)(2,1)} reshape(bf16[512]{0:T(512)(128)(2,1)} %param.13) | data formatting | bytes 2048 | tf_op jit(solution)/shard_map/reshape | solution.py:265
  1.9 2.9 %pack.1 = (bf16[256,512]{1,0:T(8,128)(2,1)}, bf16[656,512]{1,0:T(8,128)(2,1)}) custom-call(bf16[1024,512]{1,0:T(8,128)(2,1)} %points_ref.1, bf16[512,512]{1,0:T(8,128)(2,1)} %pos_ref.13, bf16[512,128]{1,0:T(8,128)(2,1)} %coef_in.7, bf16[1,512]{1,0:T(2,128)(2,1)} %reshape.4.spread_ref), custom_call_target="tpu_custom_call" | custom-call | flops 1 | bytes 1 | tf_op jit(solution)/shard_map/pack/pallas_call | solution.py:83
  4.8 3.0 %collective-permute-start.2 = (bf16[656,512]{1,0:T(8,128)(2,1)}, bf16[656,512]{1,0:T(8,128)(2,1)S(1)}, u32[]{:S(2)}, u32[]{:S(2)}) collective-permute-start(bf16[656,512]{1,0:T(8,128)(2,1)} %get-tuple-element.29.refs_0_), channel_id=1, source_target_pairs={{0,2},{1,3},{2,0},{3,1},{4,6},{5,7},{6,4},{7,5},{8,10},{9,11},{10,... | collective-permute-start | bytes 2015240 | tf_op jit(solution)/shard_map/ppermute | solution.py:20
  7.8 2.6 %collective-permute-start.1 = (bf16[256,512]{1,0:T(8,128)(2,1)}, bf16[256,512]{1,0:T(8,128)(2,1)S(1)}, u32[]{:S(2)}, u32[]{:S(2)}) collective-permute-start(bf16[256,512]{1,0:T(8,128)(2,1)} %get-tuple-element.34.rows_ref.refs_0_.refs_1_), channel_id=1, source_target_pairs={{0,8},{4,12},{8,0},{12,4},{1,9},{5,13},{9,1},{13,5},{2,10},{6,14},... | collective-permute-start | bytes 786440 | tf_op jit(solution)/shard_map/ppermute | solution.py:20
  10.4 1.6 %collective-permute-start = (bf16[256,512]{1,0:T(8,128)(2,1)}, bf16[256,512]{1,0:T(8,128)(2,1)S(1)}, u32[]{:S(2)}, u32[]{:S(2)}) collective-permute-start(bf16[256,512]{1,0:T(8,128)(2,1)} %get-tuple-element.34.rows_ref.refs_0_.refs_1_), channel_id=1, source_target_pairs={{0,4},{4,0},{8,12},{12,8},{1,5},{5,1},{9,13},{13,9},{2,6},{6,2},{1... | collective-permute-start | bytes 786440 | tf_op jit(solution)/shard_map/ppermute | solution.py:20
  12.0 11.4 %collective-permute-done.1.rows_ref = bf16[256,512]{1,0:T(8,128)(2,1)S(1)} collective-permute-done((bf16[256,512]{1,0:T(8,128)(2,1)}, bf16[256,512]{1,0:T(8,128)(2,1)S(1)}, u32[]{:S(2)}, u32[]{:S(2)}) %collective-permute-start.1) | collective-permute-done | bytes 262176 | tf_op jit(solution)/shard_map/ppermute | solution.py:20
  24.1 0.9 %collective-permute-start.3 = (bf16[512,512]{1,0:T(8,128)(2,1)S(1)}, bf16[512,512]{1,0:T(8,128)(2,1)S(1)}, u32[]{:S(2)}, u32[]{:S(2)}) collective-permute-start(bf16[512,512]{1,0:T(8,128)(2,1)S(1)} %constant_dynamic-update-slice_fusion.refs_1_.refs_2_), channel_id=1, source_target_pairs={{0,2},{1,3},{2,0},{3,1},{4,6},{5,7},{6,4},{7,5},{8,10},{9,11},{10,... | collective-permute-start | bytes 1572872 | tf_op jit(solution)/shard_map/ppermute | solution.py:20
  27.2 3.1 %collective-permute-start.7 = (f32[256,128]{1,0:T(8,128)S(1)}, f32[256,128]{1,0:T(8,128)S(1)}, u32[]{:S(2)}, u32[]{:S(2)}) collective-permute-start(f32[256,128]{1,0:T(8,128)S(1)} %forward.8), channel_id=1, source_target_pairs={{0,8},{4,12},{8,0},{12,4},{1,9},{5,13},{9,1},{13,5},{2,10},{6,14},... | collective-permute-start | bytes 393224 | tf_op jit(solution)/shard_map/ppermute | solution.py:20
  30.3 0.9 %collective-permute-done.6.rows_ref.refs_2_.refs_3_ = bf16[256,512]{1,0:T(8,128)(2,1)S(1)} collective-permute-done((bf16[256,512]{1,0:T(8,128)(2,1)S(1)}, bf16[256,512]{1,0:T(8,128)(2,1)S(1)}, u32[]{:S(2)}, u32[]{:S(2)}) %collective-permute-start.6) | collective-permute-done | bytes 262176 | tf_op jit(solution)/shard_map/ppermute | solution.py:20
  31.2 1.3 %forward.9 = f32[256,128]{1,0:T(8,128)S(1)} custom-call(bf16[256,512]{1,0:T(8,128)(2,1)S(1)} %collective-permute-done.6.rows_ref.refs_2_.refs_3_, bf16[656,512]{1,0:T(8,128)(2,1)S(1)} %copy-done.8, bf16[656,512]{1,0:T(8,128)(2,1)S(1)} %collective-permute-done.5.refs_1_, bf16[656,512]{1,0:T(8,128)(2,1)S(1)} %collective-permute-done.2.refs_0_.refs_2_, ...), custom_call_target="tpu_custom_call" | custom-call | flops 5368709120 | bytes 3145728 | tf_op jit(solution)/shard_map/forward/pallas_call | solution.py:149
  32.5 0.8 %forward.10 = f32[256,128]{1,0:T(8,128)S(1)} custom-call(bf16[256,512]{1,0:T(8,128)(2,1)S(1)} %collective-permute-done.rows_ref, bf16[656,512]{1,0:T(8,128)(2,1)S(1)} %collective-permute-done.2.refs_0_.refs_2_, bf16[656,512]{1,0:T(8,128)(2,1)S(1)} %collective-permute-done.4.refs_1_.refs_3_, f32[256,128]{1,0:T(8,128)S(1)} %forward.6.refs_2_), custom_call_target="tpu_custom_call" | custom-call | flops 2684354560 | bytes 3145728 | tf_op jit(solution)/shard_map/forward/pallas_call | solution.py:149
  33.4 1.1 %collective-permute-start.9 = (f32[256,128]{1,0:T(8,128)S(1)}, f32[256,128]{1,0:T(8,128)S(1)}, u32[]{:S(2)}, u32[]{:S(2)}) collective-permute-start(f32[256,128]{1,0:T(8,128)S(1)} %forward.10), channel_id=1, source_target_pairs={{0,4},{4,0},{8,12},{12,8},{1,5},{5,1},{9,13},{13,9},{2,6},{6,2},{1... | collective-permute-start | bytes 393224 | tf_op jit(solution)/shard_map/ppermute | solution.py:20
  34.5 2.6 %collective-permute-done.7.refs_4_ = f32[256,128]{1,0:T(8,128)S(1)} collective-permute-done((f32[256,128]{1,0:T(8,128)S(1)}, f32[256,128]{1,0:T(8,128)S(1)}, u32[]{:S(2)}, u32[]{:S(2)}) %collective-permute-start.7) | collective-permute-done | bytes 131104 | tf_op jit(solution)/shard_map/ppermute | solution.py:20
  37.1 1.4 %forward.11.refs_0_ = f32[256,128]{1,0:T(8,128)S(1)} custom-call(bf16[256,512]{1,0:T(8,128)(2,1)S(1)} %copy-done.3, bf16[656,512]{1,0:T(8,128)(2,1)S(1)} %copy-done.8, bf16[656,512]{1,0:T(8,128)(2,1)S(1)} %collective-permute-done.5.refs_1_, bf16[656,512]{1,0:T(8,128)(2,1)S(1)} %collective-permute-done.2.refs_0_.refs_2_, ...), custom_call_target="tpu_custom_call" | custom-call | flops 5368709120 | bytes 3145728 | tf_op jit(solution)/shard_map/forward/pallas_call | solution.py:149
  38.6 1.6 %collective-permute-start.11 = (bf16[256,512]{1,0:T(8,128)(2,1)S(1)}, bf16[256,512]{1,0:T(8,128)(2,1)S(1)}, u32[]{:S(2)}, u32[]{:S(2)}) collective-permute-start(bf16[256,512]{1,0:T(8,128)(2,1)S(1)} %collective-permute-done.6.rows_ref.refs_2_.refs_3_), channel_id=1, source_target_pairs={{0,2},{1,3},{2,0},{3,1},{4,6},{5,7},{6,4},{7,5},{8,10},{9,11},{10,... | collective-permute-start | bytes 786440 | tf_op jit(solution)/shard_map/ppermute | solution.py:20
  40.1 2.9 %collective-permute-start.8 = (f32[256,128]{1,0:T(8,128)S(1)}, f32[256,128]{1,0:T(8,128)S(1)}, u32[]{:S(2)}, u32[]{:S(2)}) collective-permute-start(f32[256,128]{1,0:T(8,128)S(1)} %forward.9), channel_id=1, source_target_pairs={{0,12},{4,8},{8,4},{12,0},{1,13},{5,9},{9,5},{13,1},{2,14},{6,10},... | collective-permute-start | bytes 393224 | tf_op jit(solution)/shard_map/ppermute | solution.py:20
  43.7 3.9 %collective-permute-done.8.refs_1_ = f32[256,128]{1,0:T(8,128)S(1)} collective-permute-done((f32[256,128]{1,0:T(8,128)S(1)}, f32[256,128]{1,0:T(8,128)S(1)}, u32[]{:S(2)}, u32[]{:S(2)}) %collective-permute-start.8) | collective-permute-done | bytes 131104 | tf_op jit(solution)/shard_map/ppermute | solution.py:20
  47.7 0.9 %collective-permute-start.14 = (bf16[256,128]{1,0:T(8,128)(2,1)S(1)}, bf16[256,128]{1,0:T(8,128)(2,1)S(1)}, u32[]{:S(2)}, u32[]{:S(2)}) collective-permute-start(bf16[256,128]{1,0:T(8,128)(2,1)S(1)} %cotangent.1.refs_4_), channel_id=1, source_target_pairs={{0,4},{4,0},{8,12},{12,8},{1,5},{5,1},{9,13},{13,9},{2,6},{6,2},{1... | collective-permute-start | bytes 196616 | tf_op jit(solution)/shard_map/ppermute | solution.py:20
  48.6 2.0 %collective-permute-start.16 = (bf16[256,128]{1,0:T(8,128)(2,1)S(1)}, bf16[256,128]{1,0:T(8,128)(2,1)S(1)}, u32[]{:S(2)}, u32[]{:S(2)}) collective-permute-start(bf16[256,128]{1,0:T(8,128)(2,1)S(1)} %cotangent.1.refs_4_), channel_id=1, source_target_pairs={{0,8},{4,12},{8,0},{12,4},{1,9},{5,13},{9,1},{13,5},{2,10},{6,14},... | collective-permute-start | bytes 196616 | tf_op jit(solution)/shard_map/ppermute | solution.py:20
  50.6 1.5 %collective-permute-start.20 = (bf16[256,128]{1,0:T(8,128)(2,1)S(1)}, bf16[256,128]{1,0:T(8,128)(2,1)S(1)}, u32[]{:S(2)}, u32[]{:S(2)}) collective-permute-start(bf16[256,128]{1,0:T(8,128)(2,1)S(1)} %cotangent.1.refs_4_), channel_id=1, source_target_pairs={{0,12},{4,8},{8,4},{12,0},{1,13},{5,9},{9,5},{13,1},{2,14},{6,10},... | collective-permute-start | bytes 196616 | tf_op jit(solution)/shard_map/ppermute | solution.py:20
  52.2 1.1 %own_kernel.5.refs_0_ = bf16[512,1024]{1,0:T(8,128)(2,1)S(1)} custom-call(bf16[512,512]{1,0:T(8,128)(2,1)S(1)} %copy-done, bf16[1,512]{1,0:T(2,128)(2,1)S(1)} %copy-done.6, bf16[256,512]{1,0:T(8,128)(2,1)S(1)} %copy-done.3, bf16[512,512]{1,0:T(8,128)(2,1)S(1)} %constant_dynamic-update-slice_fusion.refs_1_.refs_2_, ...), custom_call_target="tpu_custom_call" | custom-call | flops 1 | bytes 1 | tf_op jit(solution)/shard_map/own_kernel/pallas_call | solution.py:181
  53.2 1.1 %own_kernel.6.refs_8_ = bf16[512,1024]{1,0:T(8,128)(2,1)S(1)} custom-call(bf16[512,512]{1,0:T(8,128)(2,1)S(1)} %copy-done, bf16[1,512]{1,0:T(2,128)(2,1)S(1)} %copy-done.6, bf16[256,512]{1,0:T(8,128)(2,1)S(1)} %get-tuple-element.41.refs_0_.refs_9_, bf16[512,512]{1,0:T(8,128)(2,1)S(1)} %collective-permute-done.17.refs_1_.refs_10_, ...), custom_call_target="tpu_custom_call" | custom-call | flops 1 | bytes 1 | tf_op jit(solution)/shard_map/own_kernel/pallas_call | solution.py:181
  55.2 1.2 %collective-permute-start.15 = (bf16[256,128]{1,0:T(8,128)(2,1)S(1)}, bf16[256,128]{1,0:T(8,128)(2,1)S(1)}, u32[]{:S(2)}, u32[]{:S(2)}) collective-permute-start(bf16[256,128]{1,0:T(8,128)(2,1)S(1)} %collective-permute-done.14.refs_5_), channel_id=1, source_target_pairs={{0,2},{1,3},{2,0},{3,1},{4,6},{5,7},{6,4},{7,5},{8,10},{9,11},{10,... | collective-permute-start | bytes 196616 | tf_op jit(solution)/shard_map/ppermute | solution.py:20
  56.7 1.4 %collective-permute-start.21 = (bf16[256,128]{1,0:T(8,128)(2,1)S(1)}, bf16[256,128]{1,0:T(8,128)(2,1)S(1)}, u32[]{:S(2)}, u32[]{:S(2)}) collective-permute-start(bf16[256,128]{1,0:T(8,128)(2,1)S(1)} %collective-permute-done.20.refs_7_), channel_id=1, source_target_pairs={{0,2},{1,3},{2,0},{3,1},{4,6},{5,7},{6,4},{7,5},{8,10},{9,11},{10,... | collective-permute-start | bytes 196616 | tf_op jit(solution)/shard_map/ppermute | solution.py:20
  59.3 1.4 %collective-permute-done.15.refs_5_ = bf16[256,128]{1,0:T(8,128)(2,1)S(1)} collective-permute-done((bf16[256,128]{1,0:T(8,128)(2,1)S(1)}, bf16[256,128]{1,0:T(8,128)(2,1)S(1)}, u32[]{:S(2)}, u32[]{:S(2)}) %collective-permute-start.15) | collective-permute-done | bytes 65568 | tf_op jit(solution)/shard_map/ppermute | solution.py:20
  60.7 1.4 %collective-permute-done.21.refs_7_ = bf16[256,128]{1,0:T(8,128)(2,1)S(1)} collective-permute-done((bf16[256,128]{1,0:T(8,128)(2,1)S(1)}, bf16[256,128]{1,0:T(8,128)(2,1)S(1)}, u32[]{:S(2)}, u32[]{:S(2)}) %collective-permute-start.21) | collective-permute-done | bytes 65568 | tf_op jit(solution)/shard_map/ppermute | solution.py:20
  62.1 1.0 %collective-permute-done.19.refs_6_ = bf16[256,128]{1,0:T(8,128)(2,1)S(1)} collective-permute-done((bf16[256,128]{1,0:T(8,128)(2,1)S(1)}, bf16[256,128]{1,0:T(8,128)(2,1)S(1)}, u32[]{:S(2)}, u32[]{:S(2)}) %collective-permute-start.19) | collective-permute-done | bytes 65568 | tf_op jit(solution)/shard_map/ppermute | solution.py:20
  63.2 1.1 %own_kernel.7.refs_0_ = bf16[512,1024]{1,0:T(8,128)(2,1)S(1)} custom-call(bf16[512,512]{1,0:T(8,128)(2,1)S(1)} %copy-done, bf16[1,512]{1,0:T(2,128)(2,1)S(1)} %copy-done.6, bf16[256,512]{1,0:T(8,128)(2,1)S(1)} %get-tuple-element.44.refs_0_.refs_1_, bf16[512,512]{1,0:T(8,128)(2,1)S(1)} %collective-permute-done.3.refs_1_.refs_2_, ...), custom_call_target="tpu_custom_call" | custom-call | flops 1 | bytes 1 | tf_op jit(solution)/shard_map/own_kernel/pallas_call | solution.py:181
  64.3 1.1 %own_kernel.4.refs_0_ = bf16[512,1024]{1,0:T(8,128)(2,1)S(1)} custom-call(bf16[512,512]{1,0:T(8,128)(2,1)S(1)} %copy-done, bf16[1,512]{1,0:T(2,128)(2,1)S(1)} %copy-done.6, bf16[256,512]{1,0:T(8,128)(2,1)S(1)} %get-tuple-element.27.refs_0_.refs_1_, bf16[512,512]{1,0:T(8,128)(2,1)S(1)} %collective-permute-done.10.refs_1_.refs_2_, ...), custom_call_target="tpu_custom_call" | custom-call | flops 1 | bytes 1 | tf_op jit(solution)/shard_map/own_kernel/pallas_call | solution.py:181
  65.4 2.9 %backward.3 = (f32[512,512]{1,0:T(8,128)S(1)}, f32[512,128]{1,0:T(8,128)S(1)}, f32[512,128]{1,0:T(8,128)S(1)}) custom-call(bf16[512,512]{1,0:T(8,128)(2,1)S(1)} %copy-done, bf16[512,128]{1,0:T(8,128)(2,1)S(1)} %copy-done.2, bf16[1,512]{1,0:T(2,128)(2,1)S(1)} %copy-done.6, bf16[512,1024]{1,0:T(8,128)(2,1)S(1)} %own_kernel.5.refs_0_, ...), custom_call_target="tpu_custom_call" | custom-call | flops 1 | bytes 1 | tf_op jit(solution)/shard_map/backward/pallas_call | solution.py:257
  68.3 1.5 %backward.4 = (f32[512,512]{1,0:T(8,128)S(1)}, f32[512,128]{1,0:T(8,128)S(1)}, f32[512,128]{1,0:T(8,128)S(1)}) custom-call(bf16[512,512]{1,0:T(8,128)(2,1)S(1)} %copy-done, bf16[512,128]{1,0:T(8,128)(2,1)S(1)} %copy-done.2, bf16[1,512]{1,0:T(2,128)(2,1)S(1)} %copy-done.6, bf16[512,1024]{1,0:T(8,128)(2,1)S(1)} %own_kernel.7.refs_0_, ...), custom_call_target="tpu_custom_call" | custom-call | flops 1 | bytes 1 | tf_op jit(solution)/shard_map/backward/pallas_call | solution.py:257
  69.9 2.6 %backward.5 = (f32[512,512]{1,0:T(8,128)}, f32[512,128]{1,0:T(8,128)}) custom-call(bf16[512,512]{1,0:T(8,128)(2,1)S(1)} %copy-done, bf16[512,128]{1,0:T(8,128)(2,1)S(1)} %copy-done.2, bf16[1,512]{1,0:T(2,128)(2,1)S(1)} %copy-done.6, bf16[512,1024]{1,0:T(8,128)(2,1)S(1)} %own_kernel.4.refs_0_, bf16[256,512]{1,0:T(8,128)(2,1)S(1)} %get-tuple-element.27.refs_0_.refs_1_, ...), custom_call_target="tpu_custom_call" | custom-call | flops 1 | bytes 1 | tf_op jit(solution)/shard_map/backward/pallas_call | solution.py:257
  (55 shorter events, 6.3 us)
Async XLA Ops:
  4.8 20.2 %copy-start.8 = (bf16[656,512]{1,0:T(8,128)(2,1)S(1)}, bf16[656,512]{1,0:T(8,128)(2,1)}, u32[]{:S(2)}) copy-start(bf16[656,512]{1,0:T(8,128)(2,1)} %get-tuple-element.29.refs_0_) | copy-start | bytes 2015236
  4.8 19.2 %collective-permute-start.2 = (bf16[656,512]{1,0:T(8,128)(2,1)}, bf16[656,512]{1,0:T(8,128)(2,1)S(1)}, u32[]{:S(2)}, u32[]{:S(2)}) collective-permute-start(bf16[656,512]{1,0:T(8,128)(2,1)} %get-tuple-element.29.refs_0_), channel_id=1, source_target_pairs={{0,2},{1,3},{2,0},{3,1},{4,6},{5,7},{6,4},{7,5},{8,10},{9,11},{10,... | collective-permute-start | bytes 2015240 | tf_op jit(solution)/shard_map/ppermute | solution.py:20
  7.8 17.2 %collective-permute-start.5 = (bf16[656,512]{1,0:T(8,128)(2,1)}, bf16[656,512]{1,0:T(8,128)(2,1)S(1)}, u32[]{:S(2)}, u32[]{:S(2)}) collective-permute-start(bf16[656,512]{1,0:T(8,128)(2,1)} %get-tuple-element.29.refs_0_), channel_id=1, source_target_pairs={{0,1},{1,0},{2,3},{3,2},{4,5},{5,4},{6,7},{7,6},{8,9},{9,8},{10,11... | collective-permute-start | bytes 2015240 | tf_op jit(solution)/shard_map/ppermute | solution.py:20
  7.8 15.6 %collective-permute-start.1 = (bf16[256,512]{1,0:T(8,128)(2,1)}, bf16[256,512]{1,0:T(8,128)(2,1)S(1)}, u32[]{:S(2)}, u32[]{:S(2)}) collective-permute-start(bf16[256,512]{1,0:T(8,128)(2,1)} %get-tuple-element.34.rows_ref.refs_0_.refs_1_), channel_id=1, source_target_pairs={{0,8},{4,12},{8,0},{12,4},{1,9},{5,13},{9,1},{13,5},{2,10},{6,14},... | collective-permute-start | bytes 786440 | tf_op jit(solution)/shard_map/ppermute | solution.py:20
  10.4 13.6 %collective-permute-start = (bf16[256,512]{1,0:T(8,128)(2,1)}, bf16[256,512]{1,0:T(8,128)(2,1)S(1)}, u32[]{:S(2)}, u32[]{:S(2)}) collective-permute-start(bf16[256,512]{1,0:T(8,128)(2,1)} %get-tuple-element.34.rows_ref.refs_0_.refs_1_), channel_id=1, source_target_pairs={{0,4},{4,0},{8,12},{12,8},{1,5},{5,1},{9,13},{13,9},{2,6},{6,2},{1... | collective-permute-start | bytes 786440 | tf_op jit(solution)/shard_map/ppermute | solution.py:20
  23.3 7.9 %collective-permute-start.6 = (bf16[256,512]{1,0:T(8,128)(2,1)S(1)}, bf16[256,512]{1,0:T(8,128)(2,1)S(1)}, u32[]{:S(2)}, u32[]{:S(2)}) collective-permute-start(bf16[256,512]{1,0:T(8,128)(2,1)S(1)} %collective-permute-done.1.rows_ref), channel_id=1, source_target_pairs={{0,4},{4,0},{8,12},{12,8},{1,5},{5,1},{9,13},{13,9},{2,6},{6,2},{1... | collective-permute-start | bytes 786440 | tf_op jit(solution)/shard_map/ppermute | solution.py:20
  24.0 2.4 %collective-permute-start.4 = (bf16[656,512]{1,0:T(8,128)(2,1)S(1)}, bf16[656,512]{1,0:T(8,128)(2,1)S(1)}, u32[]{:S(2)}, u32[]{:S(2)}) collective-permute-start(bf16[656,512]{1,0:T(8,128)(2,1)S(1)} %collective-permute-done.2.refs_0_.refs_2_), channel_id=1, source_target_pairs={{0,1},{1,0},{2,3},{3,2},{4,5},{5,4},{6,7},{7,6},{8,9},{9,8},{10,11... | collective-permute-start | bytes 2015240 | tf_op jit(solution)/shard_map/ppermute | solution.py:20
  24.1 24.6 %collective-permute-start.3 = (bf16[512,512]{1,0:T(8,128)(2,1)S(1)}, bf16[512,512]{1,0:T(8,128)(2,1)S(1)}, u32[]{:S(2)}, u32[]{:S(2)}) collective-permute-start(bf16[512,512]{1,0:T(8,128)(2,1)S(1)} %constant_dynamic-update-slice_fusion.refs_1_.refs_2_), channel_id=1, source_target_pairs={{0,2},{1,3},{2,0},{3,1},{4,6},{5,7},{6,4},{7,5},{8,10},{9,11},{10,... | collective-permute-start | bytes 1572872 | tf_op jit(solution)/shard_map/ppermute | solution.py:20
  27.2 9.9 %collective-permute-start.7 = (f32[256,128]{1,0:T(8,128)S(1)}, f32[256,128]{1,0:T(8,128)S(1)}, u32[]{:S(2)}, u32[]{:S(2)}) collective-permute-start(f32[256,128]{1,0:T(8,128)S(1)} %forward.8), channel_id=1, source_target_pairs={{0,8},{4,12},{8,0},{12,4},{1,9},{5,13},{9,1},{13,5},{2,10},{6,14},... | collective-permute-start | bytes 393224 | tf_op jit(solution)/shard_map/ppermute | solution.py:20
  32.5 4.6 %copy-start.3 = (bf16[256,512]{1,0:T(8,128)(2,1)S(1)}, bf16[256,512]{1,0:T(8,128)(2,1)}, u32[]{:S(2)}) copy-start(bf16[256,512]{1,0:T(8,128)(2,1)} %get-tuple-element.34.rows_ref.refs_0_.refs_1_) | copy-start | bytes 786436
  33.3 9.7 %copy-start.1 = (bf16[1024,512]{1,0:T(8,128)(2,1)S(1)}, bf16[1024,512]{1,0:T(8,128)(2,1)}, u32[]{:S(2)}) copy-start(bf16[1024,512]{1,0:T(8,128)(2,1)} %points_ref.1) | copy-start | bytes 3145732
  33.4 9.7 %copy-start.4 = (f32[1024,128]{1,0:T(8,128)S(1)}, f32[1024,128]{1,0:T(8,128)}, u32[]{:S(2)}) copy-start(f32[1024,128]{1,0:T(8,128)} %refs_1_.1) | copy-start | bytes 1572868
  33.4 9.7 %copy-start.5 = (f32[1024,128]{1,0:T(8,128)S(1)}, f32[1024,128]{1,0:T(8,128)}, u32[]{:S(2)}) copy-start(f32[1024,128]{1,0:T(8,128)} %refs_2_.1) | copy-start | bytes 1572868
  33.4 6.8 %collective-permute-start.9 = (f32[256,128]{1,0:T(8,128)S(1)}, f32[256,128]{1,0:T(8,128)S(1)}, u32[]{:S(2)}, u32[]{:S(2)}) collective-permute-start(f32[256,128]{1,0:T(8,128)S(1)} %forward.10), channel_id=1, source_target_pairs={{0,4},{4,0},{8,12},{12,8},{1,5},{5,1},{9,13},{13,9},{2,6},{6,2},{1... | collective-permute-start | bytes 393224 | tf_op jit(solution)/shard_map/ppermute | solution.py:20
  34.5 17.6 %collective-permute-start.17 = (bf16[512,512]{1,0:T(8,128)(2,1)S(1)}, bf16[512,512]{1,0:T(8,128)(2,1)S(1)}, u32[]{:S(2)}, u32[]{:S(2)}) collective-permute-start(bf16[512,512]{1,0:T(8,128)(2,1)S(1)} %constant_dynamic-update-slice_fusion.refs_1_.refs_2_), channel_id=1, source_target_pairs={{0,1},{1,0},{2,3},{3,2},{4,5},{5,4},{6,7},{7,6},{8,9},{9,8},{10,11... | collective-permute-start | bytes 1572872 | tf_op jit(solution)/shard_map/ppermute | solution.py:20
  38.5 4.5 %copy-start.7 = (f32[128]{0:T(128)S(1)}, f32[128]{0:T(128)}, u32[]{:S(2)}) copy-start(f32[128]{0:T(128)} %param.10) | copy-start | bytes 1540
  38.5 12.2 %collective-permute-start.18 = (bf16[256,512]{1,0:T(8,128)(2,1)S(1)}, bf16[256,512]{1,0:T(8,128)(2,1)S(1)}, u32[]{:S(2)}, u32[]{:S(2)}) collective-permute-start(bf16[256,512]{1,0:T(8,128)(2,1)S(1)} %collective-permute-done.6.rows_ref.refs_2_.refs_3_), channel_id=1, source_target_pairs={{0,1},{1,0},{2,3},{3,2},{4,5},{5,4},{6,7},{7,6},{8,9},{9,8},{10,11... | collective-permute-start | bytes 786440 | tf_op jit(solution)/shard_map/ppermute | solution.py:20
  38.6 19.5 %collective-permute-start.11 = (bf16[256,512]{1,0:T(8,128)(2,1)S(1)}, bf16[256,512]{1,0:T(8,128)(2,1)S(1)}, u32[]{:S(2)}, u32[]{:S(2)}) collective-permute-start(bf16[256,512]{1,0:T(8,128)(2,1)S(1)} %collective-permute-done.6.rows_ref.refs_2_.refs_3_), channel_id=1, source_target_pairs={{0,2},{1,3},{2,0},{3,1},{4,6},{5,7},{6,4},{7,5},{8,10},{9,11},{10,... | collective-permute-start | bytes 786440 | tf_op jit(solution)/shard_map/ppermute | solution.py:20
  40.1 7.5 %collective-permute-start.8 = (f32[256,128]{1,0:T(8,128)S(1)}, f32[256,128]{1,0:T(8,128)S(1)}, u32[]{:S(2)}, u32[]{:S(2)}) collective-permute-start(f32[256,128]{1,0:T(8,128)S(1)} %forward.9), channel_id=1, source_target_pairs={{0,12},{4,8},{8,4},{12,0},{1,13},{5,9},{9,5},{13,1},{2,14},{6,10},... | collective-permute-start | bytes 393224 | tf_op jit(solution)/shard_map/ppermute | solution.py:20
  43.7 8.5 %copy-start = (bf16[512,512]{1,0:T(8,128)(2,1)S(1)}, bf16[512,512]{1,0:T(8,128)(2,1)}, u32[]{:S(2)}) copy-start(bf16[512,512]{1,0:T(8,128)(2,1)} %pos_ref.13) | copy-start | bytes 1572868
  47.6 4.6 %copy-start.6 = (bf16[1,512]{1,0:T(2,128)(2,1)S(1)}, bf16[1,512]{1,0:T(2,128)(2,1)}, u32[]{:S(2)}) copy-start(bf16[1,512]{1,0:T(2,128)(2,1)} %reshape.4.spread_ref) | copy-start | bytes 3076
  47.7 6.6 %collective-permute-start.14 = (bf16[256,128]{1,0:T(8,128)(2,1)S(1)}, bf16[256,128]{1,0:T(8,128)(2,1)S(1)}, u32[]{:S(2)}, u32[]{:S(2)}) collective-permute-start(bf16[256,128]{1,0:T(8,128)(2,1)S(1)} %cotangent.1.refs_4_), channel_id=1, source_target_pairs={{0,4},{4,0},{8,12},{12,8},{1,5},{5,1},{9,13},{13,9},{2,6},{6,2},{1... | collective-permute-start | bytes 196616 | tf_op jit(solution)/shard_map/ppermute | solution.py:20
  48.6 6.6 %collective-permute-start.16 = (bf16[256,128]{1,0:T(8,128)(2,1)S(1)}, bf16[256,128]{1,0:T(8,128)(2,1)S(1)}, u32[]{:S(2)}, u32[]{:S(2)}) collective-permute-start(bf16[256,128]{1,0:T(8,128)(2,1)S(1)} %cotangent.1.refs_4_), channel_id=1, source_target_pairs={{0,8},{4,12},{8,0},{12,4},{1,9},{5,13},{9,1},{13,5},{2,10},{6,14},... | collective-permute-start | bytes 196616 | tf_op jit(solution)/shard_map/ppermute | solution.py:20
  50.6 6.1 %collective-permute-start.20 = (bf16[256,128]{1,0:T(8,128)(2,1)S(1)}, bf16[256,128]{1,0:T(8,128)(2,1)S(1)}, u32[]{:S(2)}, u32[]{:S(2)}) collective-permute-start(bf16[256,128]{1,0:T(8,128)(2,1)S(1)} %cotangent.1.refs_4_), channel_id=1, source_target_pairs={{0,12},{4,8},{8,4},{12,0},{1,13},{5,9},{9,5},{13,1},{2,14},{6,10},... | collective-permute-start | bytes 196616 | tf_op jit(solution)/shard_map/ppermute | solution.py:20
  52.2 12.1 %collective-permute-start.10 = (bf16[512,512]{1,0:T(8,128)(2,1)S(1)}, bf16[512,512]{1,0:T(8,128)(2,1)S(1)}, u32[]{:S(2)}, u32[]{:S(2)}) collective-permute-start(bf16[512,512]{1,0:T(8,128)(2,1)S(1)} %collective-permute-done.3.refs_1_.refs_2_), channel_id=1, source_target_pairs={{0,1},{1,0},{2,3},{3,2},{4,5},{5,4},{6,7},{7,6},{8,9},{9,8},{10,11... | collective-permute-start | bytes 1572872 | tf_op jit(solution)/shard_map/ppermute | solution.py:20
  54.3 5.0 %collective-permute-start.13 = (bf16[256,128]{1,0:T(8,128)(2,1)S(1)}, bf16[256,128]{1,0:T(8,128)(2,1)S(1)}, u32[]{:S(2)}, u32[]{:S(2)}) collective-permute-start(bf16[256,128]{1,0:T(8,128)(2,1)S(1)} %cotangent.1.refs_4_), channel_id=1, source_target_pairs={{0,2},{1,3},{2,0},{3,1},{4,6},{5,7},{6,4},{7,5},{8,10},{9,11},{10,... | collective-permute-start | bytes 196616 | tf_op jit(solution)/shard_map/ppermute | solution.py:20
  55.2 5.5 %collective-permute-start.15 = (bf16[256,128]{1,0:T(8,128)(2,1)S(1)}, bf16[256,128]{1,0:T(8,128)(2,1)S(1)}, u32[]{:S(2)}, u32[]{:S(2)}) collective-permute-start(bf16[256,128]{1,0:T(8,128)(2,1)S(1)} %collective-permute-done.14.refs_5_), channel_id=1, source_target_pairs={{0,2},{1,3},{2,0},{3,1},{4,6},{5,7},{6,4},{7,5},{8,10},{9,11},{10,... | collective-permute-start | bytes 196616 | tf_op jit(solution)/shard_map/ppermute | solution.py:20
  56.7 5.4 %collective-permute-start.21 = (bf16[256,128]{1,0:T(8,128)(2,1)S(1)}, bf16[256,128]{1,0:T(8,128)(2,1)S(1)}, u32[]{:S(2)}, u32[]{:S(2)}) collective-permute-start(bf16[256,128]{1,0:T(8,128)(2,1)S(1)} %collective-permute-done.20.refs_7_), channel_id=1, source_target_pairs={{0,2},{1,3},{2,0},{3,1},{4,6},{5,7},{6,4},{7,5},{8,10},{9,11},{10,... | collective-permute-start | bytes 196616 | tf_op jit(solution)/shard_map/ppermute | solution.py:20
  58.1 5.0 %collective-permute-start.19 = (bf16[256,128]{1,0:T(8,128)(2,1)S(1)}, bf16[256,128]{1,0:T(8,128)(2,1)S(1)}, u32[]{:S(2)}, u32[]{:S(2)}) collective-permute-start(bf16[256,128]{1,0:T(8,128)(2,1)S(1)} %collective-permute-done.16.refs_6_), channel_id=1, source_target_pairs={{0,2},{1,3},{2,0},{3,1},{4,6},{5,7},{6,4},{7,5},{8,10},{9,11},{10,... | collective-permute-start | bytes 196616 | tf_op jit(solution)/shard_map/ppermute | solution.py:20
  59.3 6.1 %collective-permute-start.23 = (bf16[1024,128]{1,0:T(8,128)(2,1)S(1)}, bf16[1024,128]{1,0:T(8,128)(2,1)S(1)}, u32[]{:S(2)}, u32[]{:S(2)}) collective-permute-start(bf16[1024,128]{1,0:T(8,128)(2,1)S(1)} %pad_maximum_fusion.1), channel_id=1, source_target_pairs={{0,1},{1,0},{2,3},{3,2},{4,5},{5,4},{6,7},{7,6},{8,9},{9,8},{10,11... | collective-permute-start | bytes 786440 | tf_op jit(solution)/shard_map/ppermute | solution.py:20
  60.7 3.6 %collective-permute-start.12 = (bf16[256,512]{1,0:T(8,128)(2,1)S(1)}, bf16[256,512]{1,0:T(8,128)(2,1)S(1)}, u32[]{:S(2)}, u32[]{:S(2)}) collective-permute-start(bf16[256,512]{1,0:T(8,128)(2,1)S(1)} %collective-permute-done.11.refs_2_.refs_3_), channel_id=1, source_target_pairs={{0,1},{1,0},{2,3},{3,2},{4,5},{5,4},{6,7},{7,6},{8,9},{9,8},{10,11... | collective-permute-start | bytes 786440 | tf_op jit(solution)/shard_map/ppermute | solution.py:20
  63.1 6.7 %collective-permute-start.22 = (bf16[1024,128]{1,0:T(8,128)(2,1)S(1)}, bf16[1024,128]{1,0:T(8,128)(2,1)S(1)}, u32[]{:S(2)}, u32[]{:S(2)}) collective-permute-start(bf16[1024,128]{1,0:T(8,128)(2,1)S(1)} %pad_maximum_fusion), channel_id=1, source_target_pairs={{0,1},{1,0},{2,3},{3,2},{4,5},{5,4},{6,7},{7,6},{8,9},{9,8},{10,11... | collective-permute-start | bytes 786440 | tf_op jit(solution)/shard_map/ppermute | solution.py:20
  (1 other events, 1.1 us)

commit v5 on v4

--- a/solution.py
+++ b/solution.py
@@ -12,7 +12,7 @@
 VMEM = pl.BlockSpec(memory_space=pltpu.VMEM)
 NT = (((1,), (1,)), ((), ()))
 LOG2E = math.log2(math.e)
-COVER = 8
+COVER = pl.CostEstimate(flops=1 << 34, bytes_accessed=1 << 20, transcendentals=1 << 20)
 BRIEF = pl.CostEstimate(flops=1, bytes_accessed=1, transcendentals=0)
 
 
@@ -120,63 +120,60 @@
     )(row.reshape(1, -1), *arrays)
 
 
-def forward(rows, payloads, n, out_width, before=()):
-    in_width = rows.shape[1]
+def partial_pred(x, refs, n, out_width, total):
+    in_width = x.shape[1]
     q = n * out_width // in_width
-
+    row_sq = half_sq_column(x)
+    for ref in refs:
+        packed = ref[n : n + q]
+        coef = jnp.concatenate([packed[:, k : k + out_width] for k in range(0, in_width, out_width)])
+        tail = ref[n + q :, :n].astype(F32)
+        center_sq = tail[1:2] + tail[2:3] + tail[3:4]
+        rate = tail[0:1] * (-2.0 * LOG2E / in_width)
+        cross = lax.dot_general(x, ref[:n], NT, preferred_element_type=F32)
+        power = (row_sq + center_sq - cross) * rate
+        kernel = jnp.exp2(power).astype(BF16)
+        new = jnp.dot(kernel, coef, preferred_element_type=F32)
+        total = new if total is None else total + new
+    return total
+
+
+def own_values(pos_ref, spread_ref, refs, out_ref):
+    pos = pos_ref[...]
+    center_sq = half_sq_column(pos)
+    rate = column(spread_ref[...].astype(F32) * (-2.0 * LOG2E / pos.shape[1]))[:, :1]
+    at = 0
+    for ref in refs:
+        step = min(256, ref.shape[0])
+        for start in range(0, ref.shape[0], step):
+            x = ref[start : start + step]
+            cross = lax.dot_general(pos, x, NT, preferred_element_type=F32)
+            power = (center_sq + half_sq_row(x) - cross) * rate
+            out_ref[:, at : at + step] = jnp.exp2(power).astype(BF16)
+            at += step
+
+
+def forward(rows, payloads, n, out_width):
     def body(rows_ref, *refs):
-        out_ref = refs[-1]
-        x = rows_ref[...]
-        row_sq = half_sq_column(x)
-        total = jnp.zeros(out_ref.shape, F32)
-        for ref in refs[len(payloads) : -1]:
-            total += ref[...]
-        for ref in refs[: len(payloads)]:
-            packed = ref[n : n + q]
-            coef = jnp.concatenate(
-                [packed[:, k : k + out_width] for k in range(0, in_width, out_width)]
-            )
-            tail = ref[n + q :, :n].astype(F32)
-            center_sq = tail[1:2] + tail[2:3] + tail[3:4]
-            rate = tail[0:1] * (-2.0 * LOG2E / in_width)
-            cross = lax.dot_general(x, ref[:n], NT, preferred_element_type=F32)
-            power = (row_sq + center_sq - cross) * rate
-            kernel = jnp.exp2(power).astype(BF16)
-            total += jnp.dot(kernel, coef, preferred_element_type=F32)
-        out_ref[...] = total
-
-    work = rows.shape[0] * len(payloads) * n
+        refs[-1][...] = partial_pred(rows_ref[...], refs[:-1], n, out_width, None)
+
     return pl.pallas_call(
         body,
         out_shape=jax.ShapeDtypeStruct((rows.shape[0], out_width), F32),
-        in_specs=[VMEM] * (1 + len(payloads) + len(before)),
+        in_specs=[VMEM] * (1 + len(payloads)),
         out_specs=VMEM,
         compiler_params=params(16),
-        cost_estimate=pl.CostEstimate(
-            flops=COVER * 2 * work * (in_width + out_width), bytes_accessed=3 << 20, transcendentals=work
-        ),
+        cost_estimate=COVER,
         name="forward",
-    )(rows, *payloads, *before)
+    )(rows, *payloads)
 
 
 def own_kernel(center_pos, spread, blocks):
-    n, in_width = center_pos.shape
+    n = center_pos.shape[0]
     points = sum(b.shape[0] for b in blocks)
 
     def body(pos_ref, spread_ref, *refs):
-        out_ref = refs[-1]
-        pos = pos_ref[...]
-        center_sq = half_sq_column(pos)
-        rate = column(spread_ref[...].astype(F32) * (-2.0 * LOG2E / in_width))[:, :1]
-        at = 0
-        for ref in refs[:-1]:
-            step = min(256, ref.shape[0])
-            for start in range(0, ref.shape[0], step):
-                x = ref[start : start + step]
-                cross = lax.dot_general(pos, x, NT, preferred_element_type=F32)
-                power = (center_sq + half_sq_row(x) - cross) * rate
-                out_ref[:, at : at + step] = jnp.exp2(power).astype(BF16)
-                at += step
+        own_values(pos_ref, spread_ref, refs[:-1], refs[-1])
 
     return pl.pallas_call(
         body,
@@ -187,6 +184,35 @@
         cost_estimate=BRIEF,
         name="own_kernel",
     )(center_pos, spread.reshape(1, n), *blocks)
+
+
+def own_rows(rows, payloads, out_width, received, center_pos, spread, blocks):
+    n = center_pos.shape[0]
+    points = sum(b.shape[0] for b in blocks)
+    ends = [1, 1 + len(payloads)]
+    ends.append(ends[-1] + len(received))
+
+    def body(*refs):
+        total = None
+        for ref in refs[ends[1] : ends[2]]:
+            total = ref[...] if total is None else total + ref[...]
+        refs[-2][...] = partial_pred(refs[0][...], refs[1 : ends[1]], n, out_width, total)
+        pos_ref, spread_ref, *block_refs = refs[ends[2] : -2]
+        own_values(pos_ref, spread_ref, block_refs, refs[-1])
+
+    ins = [rows, *payloads, *received, center_pos, spread.reshape(1, n), *blocks]
+    return pl.pallas_call(
+        body,
+        out_shape=(
+            jax.ShapeDtypeStruct((rows.shape[0], out_width), F32),
+            jax.ShapeDtypeStruct((n, points), BF16),
+        ),
+        in_specs=[VMEM] * len(ins),
+        out_specs=(VMEM, VMEM),
+        compiler_params=params(16),
+        cost_estimate=COVER,
+        name="own_rows",
+    )(*ins)
 
 
 def cotangent(parts, saved, target, delta):
@@ -223,9 +249,13 @@
     def body(pos_ref, coef_in, spread_ref, *refs):
         refs, out_refs = list(refs[:-outs]), refs[-outs:]
         coef = coef_in[...]
-        moment = grad_coef = total = 0.0
+        moment = grad_coef = total = None
         if carried:
-            moment, grad_coef, total = (ref[...] for ref in refs[-3:])
+            moment, grad_coef, total = refs[-3:]
+
+        def plus(old, new):
+            return new if old is None else old[...] + new
+
         for _, xs, cots in groups:
             kernel_ref = refs.pop(0)
             x_refs = [refs.pop(0) for _ in xs]
@@ -234,14 +264,17 @@
             kernel = kernel_ref[...]
             mixing = lax.dot_general(coef, cot, NT, preferred_element_type=F32)
             weights = (kernel.astype(F32) * mixing).astype(BF16)
-            ones = jnp.ones((kernel.shape[1], 128), BF16)
-            grad_coef += jnp.dot(kernel, cot, preferred_element_type=F32)
-            total += jnp.dot(weights, ones, preferred_element_type=F32)
+            grad_coef = plus(grad_coef, jnp.dot(kernel, cot, preferred_element_type=F32))
+            lanes = weights[:, :128].astype(F32)
+            for k in range(128, kernel.shape[1], 128):
+                lanes += weights[:, k : k + 128].astype(F32)
+            total = plus(total, lanes)
             x = jnp.concatenate([ref[...] for ref in x_refs])
-            moment += jnp.dot(weights, x, preferred_element_type=F32)
+            moment = plus(moment, jnp.dot(weights, x, preferred_element_type=F32))
         out_refs[1][...] = grad_coef
         if last:
             scale = column(spread_ref[...].astype(F32)) * (2.0 / in_width)
+            total = jnp.sum(total, axis=1, keepdims=True)
             for k in range(0, in_width, 128):
                 pos = pos_ref[:, k : k + 128].astype(F32)
                 out_refs[0][:, k : k + 128] = scale * (moment[:, k : k + 128] - total * pos)
@@ -284,62 +317,68 @@
         for d in range(2, nc, 2):
             payloads[d] = swap(payload, "centers", nc, d)
         payloads[1] = swap(payload, "centers", nc, 1)
-        near = [payloads[0], payloads[1]]
-        parts = {dz: forward(layer[dz], near, n, out_width) for dz in (*range(2, nz, 2), 1)}
         for dz in range(3, nz, 2):
             layer[dz] = swap(layer[dz - 1], "points", nz, 1)
         for d in range(2, nc, 2):
-            payloads[d + 1] = swap(after(payloads[d], layer[2]), "centers", nc, 1)
-        rest = [payloads[d] for d in range(2, nc)]
+            payloads[d + 1] = swap(after(payloads[d], layer[1], layer[2]), "centers", nc, 1)
+        blocks = [payloads[d] for d in range(nc)]
 
         saved, target, *local, delta = take(
             [saved_preds, targets] + [train_points] * (nc - 1), [0, 0, *range(1, nc)], piece, huber_delta
         )
         local = [own, *local]
 
-        received = {}
+        early = {0: jnp.concatenate([layer[dz] for dz in range(1, nz - 1)])}
+        for d in range(2, nc, 2):
+            early[d] = swap(after(early[0], payloads[d]), "centers", nc, d)
+        early[1] = swap(after(early[0], payloads[2]), "centers", nc, 1)
+
+        parts, received = {}, {}
         for dz in range(2, nz, 2):
-            parts[dz] = forward(layer[dz], rest, n, out_width, [parts[dz]])
+            parts[dz] = forward(after(layer[dz], saved), blocks, n, out_width)
             received[dz] = swap(parts[dz], "points", nz, dz)
         for dz in range(3, nz, 2):
-            parts[dz] = forward(after(layer[dz], parts[dz - 1]), near + rest, n, out_width)
+            parts[dz] = forward(after(layer[dz], parts[dz - 1], early[1]), blocks, n, out_width)
             received[dz] = swap(parts[dz], "points", nz, dz)
-        parts[1] = forward(layer[1], rest, n, out_width, [after(parts[1], parts[nz - 1])])
+        parts[1] = forward(after(layer[1], parts[nz - 1]), blocks, n, out_width)
         received[1] = swap(parts[1], "points", nz, 1)
         soon = [received.pop(dz) for dz in range(2, nz, 2)]
-        parts[0] = forward(after(own, parts[1]), near + rest, n, out_width, soon)
-
-        early = {0: jnp.concatenate([layer[dz] for dz in range(1, nz - 1)])}
-        late = {0: after(layer[nz - 1], parts[0])}
+        own = after(own, parts[1])
+        kernels, late = {}, {0: layer[nz - 1]}
+        parts[0], kernels[0] = own_rows(
+            own, blocks, out_width, soon, center_pos, spread, [local[0], early[0], late[0]]
+        )
+        late[0] = after(late[0], parts[0])
+        for d in (1, *range(2, nc, 2)):
+            late[d] = swap(late[0], "centers", nc, d)
         for d in range(2, nc, 2):
-            early[d] = swap(after(early[0], payloads[d]), "centers", nc, d)
-            late[d] = swap(late[0], "centers", nc, d)
-        early[1] = swap(after(early[0], payloads[nc - 1]), "centers", nc, 1)
-        late[1] = swap(late[0], "centers", nc, 1)
-        kernels = {d: own_kernel(center_pos, spread, [local[d], early[d], late[d]]) for d in (0, 1)}
-
+            early[d + 1] = swap(after(early[d], parts[0]), "centers", nc, 1)
         cot = cotangent([parts[0], *received.values()], saved, target, delta)
 
+        kernels[1] = own_kernel(center_pos, spread, [local[1], early[1], late[1]])
+        far = [swap(cot, "points", nz, dz) for dz in range(2, nz)]
+        far = jnp.concatenate([swap(after(cot, kernels[1]), "points", nz, 1), *far])
+        cots = {0: [cot, far]}
         for d in range(2, nc, 2):
-            early[d + 1] = swap(after(early[d], cot), "centers", nc, 1)
-            late[d + 1] = swap(after(late[d], cot), "centers", nc, 1)
-            for k in (d, d + 1):
-                kernels[k] = own_kernel(center_pos, spread, [local[k], early[k], late[k]])
-
-        cots = {0: [cot] + [swap(cot, "points", nz, dz) for dz in range(1, nz)]}
-        for d in range(2, nc, 2):
-            held = after(cots[0][2], kernels[0], kernels[1])
-            cots[d] = [swap(a, "centers", nc, d) for a in (*cots[0][:2], held, *cots[0][3:])]
-        for d in range(0, nc, 2):
-            cots[d + 1] = [swap(jnp.concatenate(cots[d]), "centers", nc, 1)]
-
-        def group(d):
-            return (kernels[d], [local[d], early[d], late[d]], cots[d])
-
-        kernels[0] = after(kernels[0], *(kernels[d] for d in range(1, nc)))
-        sums = backward(center_pos, coefficients, spread, [group(0), group(1)])
-        for d in range(2, nc):
-            sums = backward(center_pos, coefficients, spread, [group(d)], before=sums, last=d + 1 == nc)
+            cots[d] = [swap(a, "centers", nc, d) for a in (cot, far)]
+        cots[1] = [swap(jnp.concatenate(cots[0]), "centers", nc, 1)]
+
+        sums = None
+        for d in range(nc):
+            if d == 2:
+                ready = [sums[0], *(kernels[k] for k in range(2, nc))]
+                for k in range(2, nc, 2):
+                    cots[k] = [after(a, *ready) for a in cots[k]]
+                    cots[k + 1] = [swap(jnp.concatenate(cots[k]), "centers", nc, 1)]
+            group = (kernels[d], [local[d], early[d], late[d]], cots[d])
+            sums = backward(
+                center_pos, coefficients, spread, [group], before=sums, last=d + 1 == nc
+            )
+            if d == 0:
+                for k in range(2, nc, 2):
+                    late[k + 1] = swap(after(late[k], sums[0]), "centers", nc, 1)
+                    for j in (k, k + 1):
+                        kernels[j] = own_kernel(center_pos, spread, [local[j], early[j], late[j]])
         return sums
 
     return jax.shard_map(

time: 72.7 us -> 76.4 us (1.051)
  waiting for transfers between devices: 23.7 us -> 28.4 us
  local copies, waits for them, and re-layouts: 1.36 us -> 3.37 us
  starting transfers between devices: 25.9 us -> 24.2 us
  Pallas kernels: 20.6 us -> 19.4 us
    ppermute x24 -> x22, waiting for transfers between devices: 23.7 us -> 28.4 us  [swap(): return lax.ppermute(a, axis, [(i, i ^ d) for i in range(size)])]
    pallas_call x0 -> x1, Pallas kernels: none -> 2.33 us  [own_rows(): pl.pallas_call(body, out_shape=(jax.ShapeDtypeStruct((rows.shape[0], out_...]
    unnamed x19 -> x21, local copies, waits for them, and re-layouts: 0.07 us -> 1.97 us
    ppermute x24 -> x22, starting transfers between devices: 25.9 us -> 24.2 us  [swap(): return lax.ppermute(a, axis, [(i, i ^ d) for i in range(size)])]
    pallas_call x6 -> x3, Pallas kernels: 5.7 us -> 4.02 us  [forward(): pl.pallas_call(body, out_shape=jax.ShapeDtypeStruct((rows.shape[0], out_w...]
    pallas_call x4 -> x3, Pallas kernels: 4.25 us -> 3.19 us  [own_kernel(): pl.pallas_call(body, out_shape=jax.ShapeDtypeStruct((n, points), BF16), i...]
    pallas_call x3 -> x4, Pallas kernels: 7.02 us -> 6.4 us  [backward(): pl.pallas_call(body, out_shape=tuple(shapes[:outs]), in_specs=[VMEM] * (3...]
  transfers between devices with their start and end apart: 24 -> 22, of which waited for: 10 -> 12; matrix products, arithmetic and copies ran while one was open for 0% -> 0% of each run, Pallas kernels for 21% -> 18%
where the time goes in v5:
time: 76.4 us; the launch traced here: 76.2 us
  waiting for transfers between devices  28.4 us (37%)
  starting transfers between devices  24.2 us (32%)
  Pallas kernels  19.4 us (25%)
  local copies, waits for them, and re-layouts  3.37 us (4%)
  between operations  0.9 us (1%)
    ppermute x22, waiting for transfers between devices, swap(): return lax.ppermute(a, axis, [(i, i ^ d) for i in range(size)])  28.4 us
    ppermute x22, starting transfers between devices, swap(): return lax.ppermute(a, axis, [(i, i ^ d) for i in range(size)])  24.2 us
    pallas_call x4, Pallas kernels, backward(): pl.pallas_call(body, out_shape=tuple(shapes[:outs]), in_specs=[VMEM] * (3...  6.4 us
    pallas_call x3, Pallas kernels, forward(): pl.pallas_call(body, out_shape=jax.ShapeDtypeStruct((rows.shape[0], out_w...  4.02 us
    pallas_call x3, Pallas kernels, own_kernel(): pl.pallas_call(body, out_shape=jax.ShapeDtypeStruct((n, points), BF16), i...  3.19 us
    pallas_call x1, Pallas kernels, pack(): pl.pallas_call(body, out_shape=(jax.ShapeDtypeStruct((piece, in_width), B...  2.93 us
    pallas_call x1, Pallas kernels, own_rows(): pl.pallas_call(body, out_shape=(jax.ShapeDtypeStruct((rows.shape[0], out_...  2.33 us
    unnamed x21, local copies, waits for them, and re-layouts  1.97 us
  transfers between devices with their start and end apart: 22, of which 12 were waited for; matrix products, arithmetic and copies ran while one was open for 0% of the time, Pallas kernels for 18%

profile of v5, /device:TPU:0, one launch (start us, length us, event | category | flops | bytes accessed | tf_op | source)
XLA Modules:
  0.0 76.2 jit_solution(5768796331709366922)
XLA Ops:
  0.6 1.4 %reshape.4.spread_ref.refs_7_ = bf16[1,512]{1,0:T(2,128)(2,1)} reshape(bf16[512]{0:T(512)(128)(2,1)} %param.13) | data formatting | bytes 2048 | tf_op jit(solution)/shard_map/reshape | solution.py:298
  2.0 2.9 %pack.1 = (bf16[256,512]{1,0:T(8,128)(2,1)}, bf16[656,512]{1,0:T(8,128)(2,1)}) custom-call(bf16[1024,512]{1,0:T(8,128)(2,1)} %points_ref.1, bf16[512,512]{1,0:T(8,128)(2,1)} %pos_ref.13, bf16[512,128]{1,0:T(8,128)(2,1)} %coef_in.9, bf16[1,512]{1,0:T(2,128)(2,1)} %reshape.4.spread_ref.refs_7_), custom_call_target="tpu_custom_call" | custom-call | flops 1 | bytes 1 | tf_op jit(solution)/shard_map/pack/pallas_call | solution.py:83
  4.9 3.0 %collective-permute-start.2 = (bf16[656,512]{1,0:T(8,128)(2,1)}, bf16[656,512]{1,0:T(8,128)(2,1)S(1)}, u32[]{:S(2)}, u32[]{:S(2)}) collective-permute-start(bf16[656,512]{1,0:T(8,128)(2,1)} %get-tuple-element.35.refs_0_.refs_1_), channel_id=1, source_target_pairs={{0,2},{1,3},{2,0},{3,1},{4,6},{5,7},{6,4},{7,5},{8,10},{9,11},{10,... | collective-permute-start | bytes 2015240 | tf_op jit(solution)/shard_map/ppermute | solution.py:20
  7.9 2.6 %collective-permute-start.1 = (bf16[256,512]{1,0:T(8,128)(2,1)}, bf16[256,512]{1,0:T(8,128)(2,1)S(1)}, u32[]{:S(2)}, u32[]{:S(2)}) collective-permute-start(bf16[256,512]{1,0:T(8,128)(2,1)} %get-tuple-element.42.refs_0_.refs_8_.refs_1_), channel_id=1, source_target_pairs={{0,8},{4,12},{8,0},{12,4},{1,9},{5,13},{9,1},{13,5},{2,10},{6,14},... | collective-permute-start | bytes 786440 | tf_op jit(solution)/shard_map/ppermute | solution.py:20
  10.5 1.6 %collective-permute-start = (bf16[256,512]{1,0:T(8,128)(2,1)}, bf16[256,512]{1,0:T(8,128)(2,1)S(1)}, u32[]{:S(2)}, u32[]{:S(2)}) collective-permute-start(bf16[256,512]{1,0:T(8,128)(2,1)} %get-tuple-element.42.refs_0_.refs_8_.refs_1_), channel_id=1, source_target_pairs={{0,4},{4,0},{8,12},{12,8},{1,5},{5,1},{9,13},{13,9},{2,6},{6,2},{1... | collective-permute-start | bytes 786440 | tf_op jit(solution)/shard_map/ppermute | solution.py:20
  12.1 10.4 %collective-permute-done.1.rows_ref = bf16[256,512]{1,0:T(8,128)(2,1)S(1)} collective-permute-done((bf16[256,512]{1,0:T(8,128)(2,1)}, bf16[256,512]{1,0:T(8,128)(2,1)S(1)}, u32[]{:S(2)}, u32[]{:S(2)}) %collective-permute-start.1) | collective-permute-done | bytes 262176 | tf_op jit(solution)/shard_map/ppermute | solution.py:20
  23.3 1.0 %copy-done.4 = f32[1024,128]{1,0:T(8,128)S(1)} copy-done((f32[1024,128]{1,0:T(8,128)S(1)}, f32[1024,128]{1,0:T(8,128)}, u32[]{:S(2)}) %copy-start.4) | copy-done | bytes 524312
  24.7 1.9 %collective-permute-start.4 = (bf16[256,512]{1,0:T(8,128)(2,1)S(1)}, bf16[256,512]{1,0:T(8,128)(2,1)S(1)}, u32[]{:S(2)}, u32[]{:S(2)}) collective-permute-start(bf16[256,512]{1,0:T(8,128)(2,1)S(1)} %collective-permute-done.1.rows_ref), channel_id=1, source_target_pairs={{0,4},{4,0},{8,12},{12,8},{1,5},{5,1},{9,13},{13,9},{2,6},{6,2},{1... | collective-permute-start | bytes 786440 | tf_op jit(solution)/shard_map/ppermute | solution.py:20
  27.0 1.5 %collective-permute-start.3 = (bf16[512,512]{1,0:T(8,128)(2,1)S(1)}, bf16[512,512]{1,0:T(8,128)(2,1)S(1)}, u32[]{:S(2)}, u32[]{:S(2)}) collective-permute-start(bf16[512,512]{1,0:T(8,128)(2,1)S(1)} %constant_dynamic-update-slice_fusion.refs_9_.refs_2_), channel_id=1, source_target_pairs={{0,2},{1,3},{2,0},{3,1},{4,6},{5,7},{6,4},{7,5},{8,10},{9,11},{10,... | collective-permute-start | bytes 1572872 | tf_op jit(solution)/shard_map/ppermute | solution.py:20
  28.5 1.3 %forward.3 = f32[256,128]{1,0:T(8,128)S(1)} custom-call(bf16[256,512]{1,0:T(8,128)(2,1)S(1)} %collective-permute-done.1.rows_ref, bf16[656,512]{1,0:T(8,128)(2,1)S(1)} %copy-done.8, bf16[656,512]{1,0:T(8,128)(2,1)S(1)} %collective-permute-done.5.refs_1_.refs_2_, bf16[656,512]{1,0:T(8,128)(2,1)S(1)} %collective-permute-done.2.refs_2_.refs_3_, ...), custom_call_target="tpu_custom_call" | custom-call | flops 17179869184 | bytes 1048576 | tf_op jit(solution)/shard_map/forward/pallas_call | solution.py:160
  29.8 2.7 %collective-permute-start.8 = (f32[256,128]{1,0:T(8,128)S(1)}, f32[256,128]{1,0:T(8,128)S(1)}, u32[]{:S(2)}, u32[]{:S(2)}) collective-permute-start(f32[256,128]{1,0:T(8,128)S(1)} %forward.3), channel_id=1, source_target_pairs={{0,8},{4,12},{8,0},{12,4},{1,9},{5,13},{9,1},{13,5},{2,10},{6,14},... | collective-permute-start | bytes 393224 | tf_op jit(solution)/shard_map/ppermute | solution.py:20
  32.5 3.2 %collective-permute-done.4.rows_ref.refs_10_.refs_3_ = bf16[256,512]{1,0:T(8,128)(2,1)S(1)} collective-permute-done((bf16[256,512]{1,0:T(8,128)(2,1)S(1)}, bf16[256,512]{1,0:T(8,128)(2,1)S(1)}, u32[]{:S(2)}, u32[]{:S(2)}) %collective-permute-start.4) | collective-permute-done | bytes 262176 | tf_op jit(solution)/shard_map/ppermute | solution.py:20
  35.7 1.3 %forward.4 = f32[256,128]{1,0:T(8,128)S(1)} custom-call(bf16[256,512]{1,0:T(8,128)(2,1)S(1)} %collective-permute-done.4.rows_ref.refs_10_.refs_3_, bf16[656,512]{1,0:T(8,128)(2,1)S(1)} %copy-done.8, bf16[656,512]{1,0:T(8,128)(2,1)S(1)} %collective-permute-done.5.refs_1_.refs_2_, bf16[656,512]{1,0:T(8,128)(2,1)S(1)} %collective-permute-done.2.refs_2_.refs_3_, ...), custom_call_target="tpu_custom_call" | custom-call | flops 17179869184 | bytes 1048576 | tf_op jit(solution)/shard_map/forward/pallas_call | solution.py:160
  37.1 1.3 %forward.5 = f32[256,128]{1,0:T(8,128)S(1)} custom-call(bf16[256,512]{1,0:T(8,128)(2,1)S(1)} %collective-permute-done.rows_ref, bf16[656,512]{1,0:T(8,128)(2,1)S(1)} %copy-done.8, bf16[656,512]{1,0:T(8,128)(2,1)S(1)} %collective-permute-done.5.refs_1_.refs_2_, bf16[656,512]{1,0:T(8,128)(2,1)S(1)} %collective-permute-done.2.refs_2_.refs_3_, ...), custom_call_target="tpu_custom_call" | custom-call | flops 17179869184 | bytes 1048576 | tf_op jit(solution)/shard_map/forward/pallas_call | solution.py:160
  39.1 2.3 %own_rows.1 = (f32[256,128]{1,0:T(8,128)S(1)}, bf16[512,1024]{1,0:T(8,128)(2,1)S(1)}) custom-call(bf16[256,512]{1,0:T(8,128)(2,1)S(1)} %copy-done.5, bf16[656,512]{1,0:T(8,128)(2,1)S(1)} %copy-done.8, bf16[656,512]{1,0:T(8,128)(2,1)S(1)} %collective-permute-done.5.refs_1_.refs_2_, bf16[656,512]{1,0:T(8,128)(2,1)S(1)} %collective-permute-done.2.refs_2_.refs_3_, ...), custom_call_target="tpu_custom_call" | custom-call | flops 17179869184 | bytes 1048576 | tf_op jit(solution)/shard_map/own_rows/pallas_call | solution.py:204
  41.8 2.3 %collective-permute-start.11 = (f32[256,128]{1,0:T(8,128)S(1)}, f32[256,128]{1,0:T(8,128)S(1)}, u32[]{:S(2)}, u32[]{:S(2)}) collective-permute-start(f32[256,128]{1,0:T(8,128)S(1)} %forward.4), channel_id=1, source_target_pairs={{0,12},{4,8},{8,4},{12,0},{1,13},{5,9},{9,5},{13,1},{2,14},{6,10},... | collective-permute-start | bytes 393224 | tf_op jit(solution)/shard_map/ppermute | solution.py:20
  44.1 3.3 %collective-permute-done.12.refs_2_ = f32[256,128]{1,0:T(8,128)S(1)} collective-permute-done((f32[256,128]{1,0:T(8,128)S(1)}, f32[256,128]{1,0:T(8,128)S(1)}, u32[]{:S(2)}, u32[]{:S(2)}) %collective-permute-start.12) | collective-permute-done | bytes 131104 | tf_op jit(solution)/shard_map/ppermute | solution.py:20
  47.4 3.6 %collective-permute-done.11.refs_1_ = f32[256,128]{1,0:T(8,128)S(1)} collective-permute-done((f32[256,128]{1,0:T(8,128)S(1)}, f32[256,128]{1,0:T(8,128)S(1)}, u32[]{:S(2)}, u32[]{:S(2)}) %collective-permute-start.11) | collective-permute-done | bytes 131104 | tf_op jit(solution)/shard_map/ppermute | solution.py:20
  51.1 2.0 %collective-permute-start.15 = (bf16[256,128]{1,0:T(8,128)(2,1)S(1)}, bf16[256,128]{1,0:T(8,128)(2,1)S(1)}, u32[]{:S(2)}, u32[]{:S(2)}) collective-permute-start(bf16[256,128]{1,0:T(8,128)(2,1)S(1)} %cotangent.1.refs_4_), channel_id=1, source_target_pairs={{0,8},{4,12},{8,0},{12,4},{1,9},{5,13},{9,1},{13,5},{2,10},{6,14},... | collective-permute-start | bytes 196616 | tf_op jit(solution)/shard_map/ppermute | solution.py:20
  53.1 1.4 %collective-permute-start.16 = (bf16[256,128]{1,0:T(8,128)(2,1)S(1)}, bf16[256,128]{1,0:T(8,128)(2,1)S(1)}, u32[]{:S(2)}, u32[]{:S(2)}) collective-permute-start(bf16[256,128]{1,0:T(8,128)(2,1)S(1)} %cotangent.1.refs_4_), channel_id=1, source_target_pairs={{0,12},{4,8},{8,4},{12,0},{1,13},{5,9},{9,5},{13,1},{2,14},{6,10},... | collective-permute-start | bytes 196616 | tf_op jit(solution)/shard_map/ppermute | solution.py:20
  54.5 1.1 %own_kernel.3.refs_0_ = bf16[512,1024]{1,0:T(8,128)(2,1)S(1)} custom-call(bf16[512,512]{1,0:T(8,128)(2,1)S(1)} %copy-done, bf16[1,512]{1,0:T(2,128)(2,1)S(1)} %copy-done.6, bf16[256,512]{1,0:T(8,128)(2,1)S(1)} %get-tuple-element.49.refs_0_.refs_1_, bf16[512,512]{1,0:T(8,128)(2,1)S(1)} %collective-permute-done.7.refs_1_.refs_2_, ...), custom_call_target="tpu_custom_call" | custom-call | flops 1 | bytes 1 | tf_op jit(solution)/shard_map/own_kernel/pallas_call | solution.py:178
  55.8 2.2 %collective-permute-start.10 = (bf16[256,512]{1,0:T(8,128)(2,1)S(1)}, bf16[256,512]{1,0:T(8,128)(2,1)S(1)}, u32[]{:S(2)}, u32[]{:S(2)}) collective-permute-start(bf16[256,512]{1,0:T(8,128)(2,1)S(1)} %collective-permute-done.4.rows_ref.refs_10_.refs_3_), channel_id=1, source_target_pairs={{0,2},{1,3},{2,0},{3,1},{4,6},{5,7},{6,4},{7,5},{8,10},{9,11},{10,... | collective-permute-start | bytes 786440 | tf_op jit(solution)/shard_map/ppermute | solution.py:20
  58.0 1.2 %collective-permute-done.16 = bf16[256,128]{1,0:T(8,128)(2,1)S(1)} collective-permute-done((bf16[256,128]{1,0:T(8,128)(2,1)S(1)}, bf16[256,128]{1,0:T(8,128)(2,1)S(1)}, u32[]{:S(2)}, u32[]{:S(2)}) %collective-permute-start.16) | collective-permute-done | bytes 65568 | tf_op jit(solution)/shard_map/ppermute | solution.py:20
  61.0 1.3 %backward.4 = (f32[512,512]{1,0:T(8,128)S(1)}, f32[512,128]{1,0:T(8,128)S(1)}, f32[512,128]{1,0:T(8,128)S(1)}) custom-call(bf16[512,512]{1,0:T(8,128)(2,1)S(1)} %copy-done, bf16[512,128]{1,0:T(8,128)(2,1)S(1)} %copy-done.2, bf16[1,512]{1,0:T(2,128)(2,1)S(1)} %copy-done.6, bf16[512,1024]{1,0:T(8,128)(2,1)S(1)} %get-tuple-element.46.refs_0_, ...), custom_call_target="tpu_custom_call" | custom-call | flops 1 | bytes 1 | tf_op jit(solution)/shard_map/backward/pallas_call | solution.py:290
  62.3 1.2 %collective-permute-done.10.refs_2_.refs_3_ = bf16[256,512]{1,0:T(8,128)(2,1)S(1)} collective-permute-done((bf16[256,512]{1,0:T(8,128)(2,1)S(1)}, bf16[256,512]{1,0:T(8,128)(2,1)S(1)}, u32[]{:S(2)}, u32[]{:S(2)}) %collective-permute-start.10) | collective-permute-done | bytes 262176 | tf_op jit(solution)/shard_map/ppermute | solution.py:20
  63.4 1.7 %collective-permute-start.20 = (bf16[768,128]{1,0:T(8,128)(2,1)S(1)}, bf16[768,128]{1,0:T(8,128)(2,1)S(1)}, u32[]{:S(2)}, u32[]{:S(2)}) collective-permute-start(bf16[768,128]{1,0:T(8,128)(2,1)S(1)} %constant_dynamic-update-slice_fusion.2.refs_5_), channel_id=1, source_target_pairs={{0,2},{1,3},{2,0},{3,1},{4,6},{5,7},{6,4},{7,5},{8,10},{9,11},{10,... | collective-permute-start | bytes 589832 | tf_op jit(solution)/shard_map/ppermute | solution.py:20
  65.5 1.1 %own_kernel.5.refs_0_ = bf16[512,1024]{1,0:T(8,128)(2,1)S(1)} custom-call(bf16[512,512]{1,0:T(8,128)(2,1)S(1)} %copy-done, bf16[1,512]{1,0:T(2,128)(2,1)S(1)} %copy-done.6, bf16[256,512]{1,0:T(8,128)(2,1)S(1)} %get-tuple-element.56.refs_0_.refs_1_, bf16[512,512]{1,0:T(8,128)(2,1)S(1)} %collective-permute-done.3.refs_1_.refs_2_, ...), custom_call_target="tpu_custom_call" | custom-call | flops 1 | bytes 1 | tf_op jit(solution)/shard_map/own_kernel/pallas_call | solution.py:178
  66.6 1.3 %backward.5 = (f32[512,512]{1,0:T(8,128)S(1)}, f32[512,128]{1,0:T(8,128)S(1)}, f32[512,128]{1,0:T(8,128)S(1)}) custom-call(bf16[512,512]{1,0:T(8,128)(2,1)S(1)} %copy-done, bf16[512,128]{1,0:T(8,128)(2,1)S(1)} %copy-done.2, bf16[1,512]{1,0:T(2,128)(2,1)S(1)} %copy-done.6, bf16[512,1024]{1,0:T(8,128)(2,1)S(1)} %own_kernel.3.refs_0_, ...), custom_call_target="tpu_custom_call" | custom-call | flops 1 | bytes 1 | tf_op jit(solution)/shard_map/backward/pallas_call | solution.py:290
  67.9 1.1 %own_kernel.4.refs_0_ = bf16[512,1024]{1,0:T(8,128)(2,1)S(1)} custom-call(bf16[512,512]{1,0:T(8,128)(2,1)S(1)} %copy-done, bf16[1,512]{1,0:T(2,128)(2,1)S(1)} %copy-done.6, bf16[256,512]{1,0:T(8,128)(2,1)S(1)} %get-tuple-element.33.refs_0_.refs_1_, bf16[512,512]{1,0:T(8,128)(2,1)S(1)} %collective-permute-done.9.refs_1_.refs_2_, ...), custom_call_target="tpu_custom_call" | custom-call | flops 1 | bytes 1 | tf_op jit(solution)/shard_map/own_kernel/pallas_call | solution.py:178
  69.0 3.2 %collective-permute-done.18.refs_4_ = bf16[256,128]{1,0:T(8,128)(2,1)S(1)} collective-permute-done((bf16[256,128]{1,0:T(8,128)(2,1)S(1)}, bf16[256,128]{1,0:T(8,128)(2,1)S(1)}, u32[]{:S(2)}, u32[]{:S(2)}) %collective-permute-start.18) | collective-permute-done | bytes 65568 | tf_op jit(solution)/shard_map/ppermute | solution.py:20
  72.3 1.3 %backward.6 = (f32[512,512]{1,0:T(8,128)S(1)}, f32[512,128]{1,0:T(8,128)S(1)}, f32[512,128]{1,0:T(8,128)S(1)}) custom-call(bf16[512,512]{1,0:T(8,128)(2,1)S(1)} %copy-done, bf16[512,128]{1,0:T(8,128)(2,1)S(1)} %copy-done.2, bf16[1,512]{1,0:T(2,128)(2,1)S(1)} %copy-done.6, bf16[512,1024]{1,0:T(8,128)(2,1)S(1)} %own_kernel.5.refs_0_, ...), custom_call_target="tpu_custom_call" | custom-call | flops 1 | bytes 1 | tf_op jit(solution)/shard_map/backward/pallas_call | solution.py:290
  73.8 2.4 %backward.7 = (f32[512,512]{1,0:T(8,128)}, f32[512,128]{1,0:T(8,128)}) custom-call(bf16[512,512]{1,0:T(8,128)(2,1)S(1)} %copy-done, bf16[512,128]{1,0:T(8,128)(2,1)S(1)} %copy-done.2, bf16[1,512]{1,0:T(2,128)(2,1)S(1)} %copy-done.6, bf16[512,1024]{1,0:T(8,128)(2,1)S(1)} %own_kernel.4.refs_0_, bf16[256,512]{1,0:T(8,128)(2,1)S(1)} %get-tuple-element.33.refs_0_.refs_1_, ...), custom_call_target="tpu_custom_call" | custom-call | flops 1 | bytes 1 | tf_op jit(solution)/shard_map/backward/pallas_call | solution.py:290
  (52 shorter events, 5.0 us)
Async XLA Ops:
  0.6 22.6 %copy-start.1 = (bf16[1024,512]{1,0:T(8,128)(2,1)S(1)}, bf16[1024,512]{1,0:T(8,128)(2,1)}, u32[]{:S(2)}) copy-start(bf16[1024,512]{1,0:T(8,128)(2,1)} %points_ref.1) | copy-start | bytes 3145732
  2.0 21.2 %copy-start.3 = (f32[1024,128]{1,0:T(8,128)S(1)}, f32[1024,128]{1,0:T(8,128)}, u32[]{:S(2)}) copy-start(f32[1024,128]{1,0:T(8,128)} %refs_1_.1) | copy-start | bytes 1572868
  4.9 18.3 %collective-permute-start.2 = (bf16[656,512]{1,0:T(8,128)(2,1)}, bf16[656,512]{1,0:T(8,128)(2,1)S(1)}, u32[]{:S(2)}, u32[]{:S(2)}) collective-permute-start(bf16[656,512]{1,0:T(8,128)(2,1)} %get-tuple-element.35.refs_0_.refs_1_), channel_id=1, source_target_pairs={{0,2},{1,3},{2,0},{3,1},{4,6},{5,7},{6,4},{7,5},{8,10},{9,11},{10,... | collective-permute-start | bytes 2015240 | tf_op jit(solution)/shard_map/ppermute | solution.py:20
  7.9 15.3 %copy-start.7 = (f32[128]{0:T(128)S(1)}, f32[128]{0:T(128)}, u32[]{:S(2)}) copy-start(f32[128]{0:T(128)} %param.10) | copy-start | bytes 1540
  7.9 14.6 %collective-permute-start.1 = (bf16[256,512]{1,0:T(8,128)(2,1)}, bf16[256,512]{1,0:T(8,128)(2,1)S(1)}, u32[]{:S(2)}, u32[]{:S(2)}) collective-permute-start(bf16[256,512]{1,0:T(8,128)(2,1)} %get-tuple-element.42.refs_0_.refs_8_.refs_1_), channel_id=1, source_target_pairs={{0,8},{4,12},{8,0},{12,4},{1,9},{5,13},{9,1},{13,5},{2,10},{6,14},... | collective-permute-start | bytes 786440 | tf_op jit(solution)/shard_map/ppermute | solution.py:20
  10.5 12.2 %collective-permute-start = (bf16[256,512]{1,0:T(8,128)(2,1)}, bf16[256,512]{1,0:T(8,128)(2,1)S(1)}, u32[]{:S(2)}, u32[]{:S(2)}) collective-permute-start(bf16[256,512]{1,0:T(8,128)(2,1)} %get-tuple-element.42.refs_0_.refs_8_.refs_1_), channel_id=1, source_target_pairs={{0,4},{4,0},{8,12},{12,8},{1,5},{5,1},{9,13},{13,9},{2,6},{6,2},{1... | collective-permute-start | bytes 786440 | tf_op jit(solution)/shard_map/ppermute | solution.py:20
  12.1 16.3 %collective-permute-start.5 = (bf16[656,512]{1,0:T(8,128)(2,1)}, bf16[656,512]{1,0:T(8,128)(2,1)S(1)}, u32[]{:S(2)}, u32[]{:S(2)}) collective-permute-start(bf16[656,512]{1,0:T(8,128)(2,1)} %get-tuple-element.35.refs_0_.refs_1_), channel_id=1, source_target_pairs={{0,1},{1,0},{2,3},{3,2},{4,5},{5,4},{6,7},{7,6},{8,9},{9,8},{10,11... | collective-permute-start | bytes 2015240 | tf_op jit(solution)/shard_map/ppermute | solution.py:20
  23.2 5.2 %collective-permute-start.6 = (bf16[656,512]{1,0:T(8,128)(2,1)S(1)}, bf16[656,512]{1,0:T(8,128)(2,1)S(1)}, u32[]{:S(2)}, u32[]{:S(2)}) collective-permute-start(bf16[656,512]{1,0:T(8,128)(2,1)S(1)} %collective-permute-done.2.refs_2_.refs_3_), channel_id=1, source_target_pairs={{0,1},{1,0},{2,3},{3,2},{4,5},{5,4},{6,7},{7,6},{8,9},{9,8},{10,11... | collective-permute-start | bytes 2015240 | tf_op jit(solution)/shard_map/ppermute | solution.py:20
  23.3 1.0 %copy-start.4 = (f32[1024,128]{1,0:T(8,128)S(1)}, f32[1024,128]{1,0:T(8,128)}, u32[]{:S(2)}) copy-start(f32[1024,128]{1,0:T(8,128)} %refs_2_.1) | copy-start | bytes 1572868
  24.7 3.7 %copy-start.8 = (bf16[656,512]{1,0:T(8,128)(2,1)S(1)}, bf16[656,512]{1,0:T(8,128)(2,1)}, u32[]{:S(2)}) copy-start(bf16[656,512]{1,0:T(8,128)(2,1)} %get-tuple-element.35.refs_0_.refs_1_) | copy-start | bytes 2015236
  24.7 10.9 %collective-permute-start.4 = (bf16[256,512]{1,0:T(8,128)(2,1)S(1)}, bf16[256,512]{1,0:T(8,128)(2,1)S(1)}, u32[]{:S(2)}, u32[]{:S(2)}) collective-permute-start(bf16[256,512]{1,0:T(8,128)(2,1)S(1)} %collective-permute-done.1.rows_ref), channel_id=1, source_target_pairs={{0,4},{4,0},{8,12},{12,8},{1,5},{5,1},{9,13},{13,9},{2,6},{6,2},{1... | collective-permute-start | bytes 786440 | tf_op jit(solution)/shard_map/ppermute | solution.py:20
  26.7 9.0 %collective-permute-start.7 = (bf16[512,512]{1,0:T(8,128)(2,1)S(1)}, bf16[512,512]{1,0:T(8,128)(2,1)S(1)}, u32[]{:S(2)}, u32[]{:S(2)}) collective-permute-start(bf16[512,512]{1,0:T(8,128)(2,1)S(1)} %constant_dynamic-update-slice_fusion.refs_9_.refs_2_), channel_id=1, source_target_pairs={{0,1},{1,0},{2,3},{3,2},{4,5},{5,4},{6,7},{7,6},{8,9},{9,8},{10,11... | collective-permute-start | bytes 1572872 | tf_op jit(solution)/shard_map/ppermute | solution.py:20
  27.0 31.1 %collective-permute-start.3 = (bf16[512,512]{1,0:T(8,128)(2,1)S(1)}, bf16[512,512]{1,0:T(8,128)(2,1)S(1)}, u32[]{:S(2)}, u32[]{:S(2)}) collective-permute-start(bf16[512,512]{1,0:T(8,128)(2,1)S(1)} %constant_dynamic-update-slice_fusion.refs_9_.refs_2_), channel_id=1, source_target_pairs={{0,2},{1,3},{2,0},{3,1},{4,6},{5,7},{6,4},{7,5},{8,10},{9,11},{10,... | collective-permute-start | bytes 1572872 | tf_op jit(solution)/shard_map/ppermute | solution.py:20
  29.8 9.3 %collective-permute-start.8 = (f32[256,128]{1,0:T(8,128)S(1)}, f32[256,128]{1,0:T(8,128)S(1)}, u32[]{:S(2)}, u32[]{:S(2)}) collective-permute-start(f32[256,128]{1,0:T(8,128)S(1)} %forward.3), channel_id=1, source_target_pairs={{0,8},{4,12},{8,0},{12,4},{1,9},{5,13},{9,1},{13,5},{2,10},{6,14},... | collective-permute-start | bytes 393224 | tf_op jit(solution)/shard_map/ppermute | solution.py:20
  37.0 2.0 %copy-start = (bf16[512,512]{1,0:T(8,128)(2,1)S(1)}, bf16[512,512]{1,0:T(8,128)(2,1)}, u32[]{:S(2)}) copy-start(bf16[512,512]{1,0:T(8,128)(2,1)} %pos_ref.13) | copy-start | bytes 1572868
  37.0 2.0 %copy-start.5 = (bf16[256,512]{1,0:T(8,128)(2,1)S(1)}, bf16[256,512]{1,0:T(8,128)(2,1)}, u32[]{:S(2)}) copy-start(bf16[256,512]{1,0:T(8,128)(2,1)} %get-tuple-element.42.refs_0_.refs_8_.refs_1_) | copy-start | bytes 786436
  37.1 2.0 %copy-start.6 = (bf16[1,512]{1,0:T(2,128)(2,1)S(1)}, bf16[1,512]{1,0:T(2,128)(2,1)}, u32[]{:S(2)}) copy-start(bf16[1,512]{1,0:T(2,128)(2,1)} %reshape.4.spread_ref.refs_7_) | copy-start | bytes 3076
  41.4 13.1 %collective-permute-start.13 = (bf16[256,512]{1,0:T(8,128)(2,1)S(1)}, bf16[256,512]{1,0:T(8,128)(2,1)S(1)}, u32[]{:S(2)}, u32[]{:S(2)}) collective-permute-start(bf16[256,512]{1,0:T(8,128)(2,1)S(1)} %collective-permute-done.4.rows_ref.refs_10_.refs_3_), channel_id=1, source_target_pairs={{0,1},{1,0},{2,3},{3,2},{4,5},{5,4},{6,7},{7,6},{8,9},{9,8},{10,11... | collective-permute-start | bytes 786440 | tf_op jit(solution)/shard_map/ppermute | solution.py:20
  41.5 5.9 %collective-permute-start.12 = (f32[256,128]{1,0:T(8,128)S(1)}, f32[256,128]{1,0:T(8,128)S(1)}, u32[]{:S(2)}, u32[]{:S(2)}) collective-permute-start(f32[256,128]{1,0:T(8,128)S(1)} %forward.5), channel_id=1, source_target_pairs={{0,4},{4,0},{8,12},{12,8},{1,5},{5,1},{9,13},{13,9},{2,6},{6,2},{1... | collective-permute-start | bytes 393224 | tf_op jit(solution)/shard_map/ppermute | solution.py:20
  41.8 9.3 %collective-permute-start.11 = (f32[256,128]{1,0:T(8,128)S(1)}, f32[256,128]{1,0:T(8,128)S(1)}, u32[]{:S(2)}, u32[]{:S(2)}) collective-permute-start(f32[256,128]{1,0:T(8,128)S(1)} %forward.4), channel_id=1, source_target_pairs={{0,12},{4,8},{8,4},{12,0},{1,13},{5,9},{9,5},{13,1},{2,14},{6,10},... | collective-permute-start | bytes 393224 | tf_op jit(solution)/shard_map/ppermute | solution.py:20
  51.1 6.9 %collective-permute-start.15 = (bf16[256,128]{1,0:T(8,128)(2,1)S(1)}, bf16[256,128]{1,0:T(8,128)(2,1)S(1)}, u32[]{:S(2)}, u32[]{:S(2)}) collective-permute-start(bf16[256,128]{1,0:T(8,128)(2,1)S(1)} %cotangent.1.refs_4_), channel_id=1, source_target_pairs={{0,8},{4,12},{8,0},{12,4},{1,9},{5,13},{9,1},{13,5},{2,10},{6,14},... | collective-permute-start | bytes 196616 | tf_op jit(solution)/shard_map/ppermute | solution.py:20
  53.1 6.2 %collective-permute-start.16 = (bf16[256,128]{1,0:T(8,128)(2,1)S(1)}, bf16[256,128]{1,0:T(8,128)(2,1)S(1)}, u32[]{:S(2)}, u32[]{:S(2)}) collective-permute-start(bf16[256,128]{1,0:T(8,128)(2,1)S(1)} %cotangent.1.refs_4_), channel_id=1, source_target_pairs={{0,12},{4,8},{8,4},{12,0},{1,13},{5,9},{9,5},{13,1},{2,14},{6,10},... | collective-permute-start | bytes 196616 | tf_op jit(solution)/shard_map/ppermute | solution.py:20
  55.6 4.4 %collective-permute-start.14 = (bf16[256,128]{1,0:T(8,128)(2,1)S(1)}, bf16[256,128]{1,0:T(8,128)(2,1)S(1)}, u32[]{:S(2)}, u32[]{:S(2)}) collective-permute-start(bf16[256,128]{1,0:T(8,128)(2,1)S(1)} %cotangent.1.refs_4_), channel_id=1, source_target_pairs={{0,4},{4,0},{8,12},{12,8},{1,5},{5,1},{9,13},{13,9},{2,6},{6,2},{1... | collective-permute-start | bytes 196616 | tf_op jit(solution)/shard_map/ppermute | solution.py:20
  55.8 7.6 %collective-permute-start.10 = (bf16[256,512]{1,0:T(8,128)(2,1)S(1)}, bf16[256,512]{1,0:T(8,128)(2,1)S(1)}, u32[]{:S(2)}, u32[]{:S(2)}) collective-permute-start(bf16[256,512]{1,0:T(8,128)(2,1)S(1)} %collective-permute-done.4.rows_ref.refs_10_.refs_3_), channel_id=1, source_target_pairs={{0,2},{1,3},{2,0},{3,1},{4,6},{5,7},{6,4},{7,5},{8,10},{9,11},{10,... | collective-permute-start | bytes 786440 | tf_op jit(solution)/shard_map/ppermute | solution.py:20
  58.0 9.9 %collective-permute-start.9 = (bf16[512,512]{1,0:T(8,128)(2,1)S(1)}, bf16[512,512]{1,0:T(8,128)(2,1)S(1)}, u32[]{:S(2)}, u32[]{:S(2)}) collective-permute-start(bf16[512,512]{1,0:T(8,128)(2,1)S(1)} %collective-permute-done.3.refs_1_.refs_2_), channel_id=1, source_target_pairs={{0,1},{1,0},{2,3},{3,2},{4,5},{5,4},{6,7},{7,6},{8,9},{9,8},{10,11... | collective-permute-start | bytes 1572872 | tf_op jit(solution)/shard_map/ppermute | solution.py:20
  60.0 6.5 %collective-permute-start.19 = (bf16[1024,128]{1,0:T(8,128)(2,1)S(1)}, bf16[1024,128]{1,0:T(8,128)(2,1)S(1)}, u32[]{:S(2)}, u32[]{:S(2)}) collective-permute-start(bf16[1024,128]{1,0:T(8,128)(2,1)S(1)} %pad_maximum_fusion), channel_id=1, source_target_pairs={{0,1},{1,0},{2,3},{3,2},{4,5},{5,4},{6,7},{7,6},{8,9},{9,8},{10,11... | collective-permute-start | bytes 786440 | tf_op jit(solution)/shard_map/ppermute | solution.py:20
  60.1 0.9 %copy-start.2 = (bf16[512,128]{1,0:T(8,128)(2,1)S(1)}, bf16[512,128]{1,0:T(8,128)(2,1)}, u32[]{:S(2)}) copy-start(bf16[512,128]{1,0:T(8,128)(2,1)} %coef_in.9) | copy-start | bytes 393220
  63.4 4.5 %collective-permute-start.17 = (bf16[256,512]{1,0:T(8,128)(2,1)S(1)}, bf16[256,512]{1,0:T(8,128)(2,1)S(1)}, u32[]{:S(2)}, u32[]{:S(2)}) collective-permute-start(bf16[256,512]{1,0:T(8,128)(2,1)S(1)} %collective-permute-done.10.refs_2_.refs_3_), channel_id=1, source_target_pairs={{0,1},{1,0},{2,3},{3,2},{4,5},{5,4},{6,7},{7,6},{8,9},{9,8},{10,11... | collective-permute-start | bytes 786440 | tf_op jit(solution)/shard_map/ppermute | solution.py:20
  63.4 8.7 %collective-permute-start.20 = (bf16[768,128]{1,0:T(8,128)(2,1)S(1)}, bf16[768,128]{1,0:T(8,128)(2,1)S(1)}, u32[]{:S(2)}, u32[]{:S(2)}) collective-permute-start(bf16[768,128]{1,0:T(8,128)(2,1)S(1)} %constant_dynamic-update-slice_fusion.2.refs_5_), channel_id=1, source_target_pairs={{0,2},{1,3},{2,0},{3,1},{4,6},{5,7},{6,4},{7,5},{8,10},{9,11},{10,... | collective-permute-start | bytes 589832 | tf_op jit(solution)/shard_map/ppermute | solution.py:20
  65.2 7.0 %collective-permute-start.18 = (bf16[256,128]{1,0:T(8,128)(2,1)S(1)}, bf16[256,128]{1,0:T(8,128)(2,1)S(1)}, u32[]{:S(2)}, u32[]{:S(2)}) collective-permute-start(bf16[256,128]{1,0:T(8,128)(2,1)S(1)} %cotangent.1.refs_4_), channel_id=1, source_target_pairs={{0,2},{1,3},{2,0},{3,1},{4,6},{5,7},{6,4},{7,5},{8,10},{9,11},{10,... | collective-permute-start | bytes 196616 | tf_op jit(solution)/shard_map/ppermute | solution.py:20
  72.2 1.6 %collective-permute-start.21 = (bf16[1024,128]{1,0:T(8,128)(2,1)S(1)}, bf16[1024,128]{1,0:T(8,128)(2,1)S(1)}, u32[]{:S(2)}, u32[]{:S(2)}) collective-permute-start(bf16[1024,128]{1,0:T(8,128)(2,1)S(1)} %pad_maximum_fusion.1), channel_id=1, source_target_pairs={{0,1},{1,0},{2,3},{3,2},{4,5},{5,4},{6,7},{7,6},{8,9},{9,8},{10,11... | collective-permute-start | bytes 786440 | tf_op jit(solution)/shard_map/ppermute | solution.py:20

commit v6 on v5

v6 whole, which is shorter than its diff:
```python
import math

import jax
import jax.numpy as jnp
from jax import lax
from jax.experimental import pallas as pl
from jax.experimental.pallas import tpu as pltpu
from jax.sharding import PartitionSpec as P

F32, BF16 = jnp.float32, jnp.bfloat16
HBM = pl.BlockSpec(memory_space=pltpu.HBM)
VMEM = pl.BlockSpec(memory_space=pltpu.VMEM)
NT = (((1,), (1,)), ((), ()))
LOG2E = math.log2(math.e)
COVER = pl.CostEstimate(flops=1 << 34, bytes_accessed=1 << 20, transcendentals=1 << 20)
BRIEF = pl.CostEstimate(flops=1, bytes_accessed=1, transcendentals=0)


def swap(a, axis, size, d):
    return lax.ppermute(a, axis, [(i, i ^ d) for i in range(size)])


def after(a, *others):
    return lax.optimization_barrier((a, *others))[0]


def lane_groups(a):
    total = None
    for k in range(0, a.shape[1], 128):
        part = jnp.square(a[:, k : k + 128].astype(F32))
        total = part if total is None else total + part
    return total


def half_sq_row(a):
    return 0.5 * jnp.sum(lane_groups(a).T, axis=0, keepdims=True)


def half_sq_column(a):
    return 0.5 * jnp.sum(lane_groups(a), axis=1, keepdims=True)


def column(row):
    return jnp.broadcast_to(row, (128, row.shape[1])).T


def params(mib):
    return pltpu.CompilerParams(vmem_limit_bytes=mib << 20)


def pack(center_pos, coefficients, spread, delta):
    n, in_width = center_pos.shape
    out_width = coefficients.shape[1]
    across = in_width // out_width
    q = n // across

    def body(pos_ref, coef_ref, spread_ref, delta_ref, out_ref, row_ref):
        row_ref[...] = delta_ref[...]
        for k in range(across):
            out_ref[:q, k * out_width : (k + 1) * out_width] = coef_ref[k * q : (k + 1) * q]
        half = half_sq_row(pos_ref[...])
        high = half.astype(BF16)
        rest = half - high.astype(F32)
        middle = rest.astype(BF16)
        low = (rest - middle.astype(F32)).astype(BF16)
        rows = [r.astype(F32) for r in (spread_ref[...], high, middle, low)]
        tail = jnp.concatenate(rows + [jnp.zeros((12, n), F32)]).astype(BF16)
        if n < in_width:
            tail = jnp.concatenate([tail, jnp.zeros((16, in_width - n), BF16)], axis=1)
        out_ref[q:] = tail

    return pl.pallas_call(
        body,
        out_shape=(
            jax.ShapeDtypeStruct((q + 16, in_width), BF16),
            jax.ShapeDtypeStruct((1, delta.shape[0]), F32),
        ),
        in_specs=[VMEM] * 4,
        out_specs=(VMEM, VMEM),
        compiler_params=params(16),
        cost_estimate=BRIEF,
        name="pack",
    )(center_pos, coefficients, spread.reshape(1, n), delta.reshape(1, -1))


def take(arrays, offsets, piece, mib=16):
    def body(*refs):
        ins, outs, sems = refs[: len(arrays)], refs[len(arrays) : -1], refs[-1]
        made = []
        for k, d in enumerate(offsets):
            start = pl.multiple_of((lax.axis_index("centers") ^ d) * piece, piece)
            made.append(pltpu.make_async_copy(ins[k].at[pl.ds(start, piece)], outs[k], sems.at[k]))
            made[-1].start()
        for copy in made:
            copy.wait()

    return pl.pallas_call(
        body,
        out_shape=tuple(jax.ShapeDtypeStruct((piece, a.shape[1]), a.dtype) for a in arrays),
        in_specs=[HBM] * len(arrays),
        out_specs=(VMEM,) * len(arrays),
        scratch_shapes=[pltpu.SemaphoreType.DMA((len(arrays),))],
        compiler_params=params(mib),
        cost_estimate=BRIEF,
        name="take",
    )(*arrays)


def partial_pred(x, refs, total):
    in_width = x.shape[1]
    row_sq = half_sq_column(x)
    for pos_ref, side_ref in zip(refs[::2], refs[1::2]):
        n, q = pos_ref.shape[0], side_ref.shape[0] - 16
        out_width = q * in_width // n
        packed = side_ref[:q]
        coef = jnp.concatenate([packed[:, k : k + out_width] for k in range(0, in_width, out_width)])
        tail = side_ref[q:, :n].astype(F32)
        center_sq = tail[1:2] + tail[2:3] + tail[3:4]
        rate = tail[0:1] * (-2.0 * LOG2E / in_width)
        cross = lax.dot_general(x, pos_ref[...], NT, preferred_element_type=F32)
        power = (row_sq + center_sq - cross) * rate
        kernel = jnp.exp2(power).astype(BF16)
        new = jnp.dot(kernel, coef, preferred_element_type=F32)
        total = new if total is None else total + new
    return total


def own_values(pos_ref, spread_ref, refs, out_ref):
    pos = pos_ref[...]
    center_sq = half_sq_column(pos)
    rate = column(spread_ref[...].astype(F32) * (-2.0 * LOG2E / pos.shape[1]))[:, :1]
    at = 0
    for ref in refs:
        step = min(256, ref.shape[0])
        for start in range(0, ref.shape[0], step):
            x = ref[start : start + step]
            cross = lax.dot_general(pos, x, NT, preferred_element_type=F32)
            power = (center_sq + half_sq_row(x) - cross) * rate
            out_ref[:, at : at + step] = jnp.exp2(power).astype(BF16)
            at += step


def forward(rows, centers, out_width, cost):
    counts = [r.shape[0] for r in rows]

    def body(*refs):
        row_refs, refs, outs = refs[: len(rows)], refs[len(rows) : -len(rows)], refs[-len(rows) :]
        x = jnp.concatenate([ref[...] for ref in row_refs])
        total = partial_pred(x, refs, None)
        at = 0
        for ref, count in zip(outs, counts):
            ref[...] = total[at : at + count]
            at += count

    return pl.pallas_call(
        body,
        out_shape=tuple(jax.ShapeDtypeStruct((count, out_width), F32) for count in counts),
        in_specs=[VMEM] * (len(rows) + len(centers)),
        out_specs=(VMEM,) * len(rows),
        compiler_params=params(24),
        cost_estimate=cost,
        name="forward",
    )(*rows, *centers)


def own_kernel(center_pos, spread, blocks):
    n = center_pos.shape[0]
    points = sum(b.shape[0] for b in blocks)

    def body(pos_ref, spread_ref, *refs):
        own_values(pos_ref, spread_ref, refs[:-1], refs[-1])

    return pl.pallas_call(
        body,
        out_shape=jax.ShapeDtypeStruct((n, points), BF16),
        in_specs=[VMEM] * (2 + len(blocks)),
        out_specs=VMEM,
        compiler_params=params(16),
        cost_estimate=BRIEF,
        name="own_kernel",
    )(center_pos, spread.reshape(1, n), *blocks)


def own_rows(rows, centers, out_width, received, center_pos, spread, more):
    n = center_pos.shape[0]
    ends = [1, 1 + len(centers)]
    ends.append(ends[-1] + len(received))

    def body(*refs):
        outs, refs = refs[-1 - len(more) :], refs[: -1 - len(more)]
        total = None
        for ref in refs[ends[1] : ends[2]]:
            total = ref[...] if total is None else total + ref[...]
        outs[0][...] = partial_pred(refs[0][...], refs[1 : ends[1]], total)
        pos_ref, spread_ref, *block_refs = refs[ends[2] :]
        for k, blocks in enumerate(more):
            own_values(pos_ref, spread_ref, block_refs[: len(blocks)], outs[1 + k])
            del block_refs[: len(blocks)]

    ins = [rows, *centers, *received, center_pos, spread.reshape(1, n)]
    ins += [block for blocks in more for block in blocks]
    return pl.pallas_call(
        body,
        out_shape=(jax.ShapeDtypeStruct((rows.shape[0], out_width), F32),)
        + tuple(jax.ShapeDtypeStruct((n, sum(b.shape[0] for b in blocks)), BF16) for blocks in more),
        in_specs=[VMEM] * len(ins),
        out_specs=(VMEM,) * (1 + len(more)),
        compiler_params=params(16),
        cost_estimate=COVER,
        name="own_rows",
    )(*ins)


def cotangent(parts, saved, target, delta):
    def body(*refs):
        saved_ref, target_ref, delta_ref, out_ref = refs[-4:]
        pred = refs[0][...]
        for ref in refs[1:-4]:
            pred += ref[...]
        residual = pred + saved_ref[...] - target_ref[...]
        ratio = residual / delta_ref[...]
        out_ref[...] = (residual / jnp.sqrt(1.0 + ratio * ratio)).astype(BF16)

    return pl.pallas_call(
        body,
        out_shape=jax.ShapeDtypeStruct(saved.shape, BF16),
        in_specs=[VMEM] * (len(parts) + 3),
        out_specs=VMEM,
        compiler_params=params(16),
        cost_estimate=BRIEF,
        name="cotangent",
    )(*parts, saved, target, delta)


def backward(center_pos, coefficients, spread, groups, before=None, last=False, more=()):
    n, in_width = center_pos.shape
    out_width = coefficients.shape[1]
    flat = []
    for kernel, xs, cots in groups:
        flat += [kernel, *xs, *cots]
    carried = [] if before is None else list(before)
    outs = (2 if last else 3) + len(more)
    wanted = [block for blocks in more for block in blocks]
    points = sum(kernel.shape[1] for kernel, _, _ in groups)

    def body(pos_ref, coef_in, spread_ref, *refs):
        refs, out_refs = list(refs[:-outs]), refs[-outs:]
        coef = coef_in[...]
        moment = grad_coef = total = None
        if carried:
            moment, grad_coef, total = refs[len(flat) : len(flat) + 3]
        block_refs = refs[len(flat) + len(carried) :]
        for k, blocks in enumerate(more):
            own_values(pos_ref, spread_ref, block_refs[: len(blocks)], out_refs[3 + k])
            del block_refs[: len(blocks)]

        def plus(old, new):
            return new if old is None else old[...] + new

        for _, xs, cots in groups:
            kernel_ref = refs.pop(0)
            x_refs = [refs.pop(0) for _ in xs]
            cot_refs = [refs.pop(0) for _ in cots]
            cot = jnp.concatenate([ref[...] for ref in cot_refs])
            kernel = kernel_ref[...]
            mixing = lax.dot_general(coef, cot, NT, preferred_element_type=F32)
            weights = (kernel.astype(F32) * mixing).astype(BF16)
            grad_coef = plus(grad_coef, jnp.dot(kernel, cot, preferred_element_type=F32))
            lanes = weights[:, :128].astype(F32)
            for k in range(128, kernel.shape[1], 128):
                lanes += weights[:, k : k + 128].astype(F32)
            total = plus(total, lanes)
            x = jnp.concatenate([ref[...] for ref in x_refs])
            moment = plus(moment, jnp.dot(weights, x, preferred_element_type=F32))
        out_refs[1][...] = grad_coef
        if last:
            scale = column(spread_ref[...].astype(F32)) * (2.0 / in_width)
            total = jnp.sum(total, axis=1, keepdims=True)
            for k in range(0, in_width, 128):
                pos = pos_ref[:, k : k + 128].astype(F32)
                out_refs[0][:, k : k + 128] = scale * (moment[:, k : k + 128] - total * pos)
        else:
            out_refs[0][...] = moment
            out_refs[2][...] = total

    shapes = [
        jax.ShapeDtypeStruct((n, in_width), F32),
        jax.ShapeDtypeStruct((n, out_width), F32),
        jax.ShapeDtypeStruct((n, 128), F32),
    ]
    return pl.pallas_call(
        body,
        out_shape=tuple(shapes[: 2 if last else 3])
        + tuple(jax.ShapeDtypeStruct((n, sum(b.shape[0] for b in blocks)), BF16) for blocks in more),
        in_specs=[VMEM] * (3 + len(flat) + len(carried) + len(wanted)),
        out_specs=(VMEM,) * outs,
        compiler_params=params(24),
        cost_estimate=COVER if more else BRIEF,
        name="backward",
    )(center_pos, coefficients, spread.reshape(1, n), *flat, *carried, *wanted)


def solution(mesh):
    nz, nc = mesh.shape["points"], mesh.shape["centers"]

    def per_device(train_points, saved_preds, targets, huber_delta, center_pos, coefficients, spread):
        n_rows = train_points.shape[0]
        n, out_width = coefficients.shape
        piece = n_rows // nc

        (own,) = take([train_points], [0], piece, 62)

        layer = {0: own}
        for dz in range(2, nz, 2):
            layer[dz] = swap(own, "points", nz, dz)
        layer[1] = swap(own, "points", nz, 1)

        pos, side = {0: center_pos}, {}
        for d in range(2, nc, 2):
            pos[d] = swap(center_pos, "centers", nc, d)
        pos[1] = swap(center_pos, "centers", nc, 1)
        side[0], delta = pack(after(center_pos, own), coefficients, spread, huber_delta)
        for d in range(2, nc, 2):
            side[d] = swap(side[0], "centers", nc, d)
        side[1] = swap(side[0], "centers", nc, 1)
        for dz in range(3, nz, 2):
            layer[dz] = swap(layer[dz - 1], "points", nz, 1)
        for d in range(2, nc, 2):
            here = (layer[1], layer[2], side[d])
            pos[d + 1] = swap(after(pos[d], *here), "centers", nc, 1)
            side[d + 1] = swap(after(side[d], *here), "centers", nc, 1)
        centers = [a for d in range(nc) for a in (pos[d], side[d])]

        saved, target, *local = take(
            [saved_preds, targets] + [train_points] * (nc - 1), [0, 0, *range(1, nc)], piece
        )
        local = [own, *local]

        early = {0: jnp.concatenate([layer[dz] for dz in range(1, nz - 1)])}
        for d in range(2, nc, 2):
            early[d] = swap(after(early[0], side[d]), "centers", nc, d)
        early[1] = swap(after(early[0], side[nc - 1]), "centers", nc, 1)

        first, second = [*range(2, nz, 2), 1], range(3, nz, 2)
        rows = [after(layer[dz], saved) for dz in first]
        parts = dict(zip(first, forward(rows, centers, out_width, BRIEF)))
        rows = [after(layer[dz], *parts.values(), early[1]) for dz in second]
        received = {dz: swap(parts[dz], "points", nz, dz) for dz in first}
        parts.update(zip(second, forward(rows, centers, out_width, COVER)))
        soon = list(received.values())
        received = [swap(parts[dz], "points", nz, dz) for dz in second]
        last = parts[nz - 1]
        late = {0: layer[nz - 1]}
        for d in (1, *range(2, nc, 2)):
            late[d] = swap(after(late[0], last, *soon), "centers", nc, d)
        near = [[local[d], early[d], late[d]] for d in (0, 1)]
        kernels = {}
        parts[0], kernels[0], kernels[1] = own_rows(
            after(own, last), centers, out_width, soon, center_pos, spread, near
        )
        for d in range(2, nc, 2):
            early[d + 1] = swap(after(early[d], last), "centers", nc, 1)
        cot = cotangent([parts[0], *received], saved, target, delta)

        far = [swap(cot, "points", nz, dz) for dz in range(1, nz)]
        cots = {0: [jnp.concatenate([cot, *far])]}
        for d in range(2, nc, 2):
            cots[d] = [swap(cots[0][0], "centers", nc, d)]
            late[d + 1] = swap(after(late[d], far[0]), "centers", nc, 1)
        cots[1] = [swap(cots[0][0], "centers", nc, 1)]

        points = {d: [local[d], early[d], late[d]] for d in range(nc)}
        groups = [(kernels[d], points[d], cots[d]) for d in (0, 1)]
        rest = range(2, nc)
        *sums, a, b = backward(
            center_pos, coefficients, spread, groups, more=[points[2], points[3]]
        )
        kernels[2], kernels[3] = a, b
        for d in range(4, nc):
            kernels[d] = own_kernel(center_pos, spread, points[d])
        for d in range(2, nc, 2):
            cots[d] = [after(cots[d][0], sums[0])]
            cots[d + 1] = [swap(cots[d][0], "centers", nc, 1)]
        for d in rest:
            group = (kernels[d], points[d], cots[d])
            sums = backward(
                center_pos, coefficients, spread, [group], before=sums, last=d + 1 == nc
            )
        return sums

    return jax.shard_map(
        per_device,
        mesh=mesh,
        in_specs=(
            P(("groups", "points"), None),
            P(("groups", "points"), None),
            P(("groups", "points"), None),
            P("groups"),
            P(("groups", "points", "centers"), None),
            P(("groups", "points", "centers"), None),
            P(("groups", "points", "centers")),
        ),
        out_specs=(
            P(("groups", "points", "centers"), None),
            P(("groups", "points", "centers"), None),
        ),
        check_vma=False,
    )
```

time: 76.4 us -> 67.7 us (0.89)
  local copies, waits for them, and re-layouts: 3.37 us -> 0.08 us
  waiting for transfers between devices: 28.4 us -> 25.4 us
  Pallas kernels: 19.4 us -> 17.6 us
    pallas_call x11 -> x6, Pallas kernels: 16.5 us -> 12.2 us  [the longest x3 8.42 us: backward(): pl.pallas_call(body, out_shape=tuple(shapes[:2 if last else 3]) + tuple((...]
    ppermute x22 -> x24, waiting for transfers between devices: 28.4 us -> 25.4 us  [swap(): return lax.ppermute(a, axis, [(i, i ^ d) for i in range(size)])]
    unnamed x21 -> x17, local copies, waits for them, and re-layouts: 1.97 us -> 0.05 us
    pallas_call x1 -> x2, Pallas kernels: 0.42 us -> 2.18 us  [take(): pl.pallas_call(body, out_shape=tuple((jax.ShapeDtypeStruct((piece, a.shap...]
    reshape x1, local copies, waits for them, and re-layouts: 1.36 us -> 0.01 us  [backward(): spread.reshape(1, n)]
    pallas_call x1, Pallas kernels: 2.33 us -> 3.11 us  [own_rows(): pl.pallas_call(body, out_shape=(jax.ShapeDtypeStruct((rows.shape[0], out_...]
    ppermute x22 -> x24, starting transfers between devices: 24.2 us -> 23.7 us  [swap(): return lax.ppermute(a, axis, [(i, i ^ d) for i in range(size)])]
  transfers between devices with their start and end apart: 22 -> 24, of which waited for: 12 -> 12; matrix products, arithmetic and copies ran while one was open for 0% -> 0% of each run, Pallas kernels for 18% -> 23%
where the time goes in v6:
time: 67.7 us; the launch traced here: 67.5 us
  waiting for transfers between devices  25.4 us (38%)
  starting transfers between devices  23.7 us (35%)
  Pallas kernels  17.6 us (26%)
  between operations  0.81 us (1%)
    ppermute x24, waiting for transfers between devices, swap(): return lax.ppermute(a, axis, [(i, i ^ d) for i in range(size)])  25.4 us
    ppermute x24, starting transfers between devices, swap(): return lax.ppermute(a, axis, [(i, i ^ d) for i in range(size)])  23.7 us
    pallas_call x3, Pallas kernels, backward(): pl.pallas_call(body, out_shape=tuple(shapes[:2 if last else 3]) + tuple((...  8.42 us
    pallas_call x2, Pallas kernels, forward(): pl.pallas_call(body, out_shape=tuple((jax.ShapeDtypeStruct((count, out_wi...  3.56 us
    pallas_call x1, Pallas kernels, own_rows(): pl.pallas_call(body, out_shape=(jax.ShapeDtypeStruct((rows.shape[0], out_...  3.11 us
    pallas_call x2, Pallas kernels, take(): pl.pallas_call(body, out_shape=tuple((jax.ShapeDtypeStruct((piece, a.shap...  2.18 us
  transfers between devices with their start and end apart: 24, of which 12 were waited for; matrix products, arithmetic and copies ran while one was open for 0% of the time, Pallas kernels for 23%

profile of v6, /device:TPU:0, one launch (start us, length us, event | category | flops | bytes accessed | tf_op | source)
XLA Modules:
  0.0 67.5 jit_solution(5651404520279377336)
XLA Ops:
  0.7 3.0 %collective-permute-start.5 = (bf16[512,512]{1,0:T(8,128)(2,1)}, bf16[512,512]{1,0:T(8,128)(2,1)S(1)}, u32[]{:S(2)}, u32[]{:S(2)}) collective-permute-start(bf16[512,512]{1,0:T(8,128)(2,1)} %pos_ref.6), channel_id=1, source_target_pairs={{0,2},{1,3},{2,0},{3,1},{4,6},{5,7},{6,4},{7,5},{8,10},{9,11},{10,... | collective-permute-start | bytes 1572872 | tf_op jit(solution)/shard_map/ppermute | solution.py:20
  3.7 1.7 %take.2.refs_0_.refs_13_.refs_1_ = bf16[256,512]{1,0:T(8,128)(2,1)} custom-call(bf16[1024,512]{1,0:T(8,128)(2,1)} %refs_4_.1), custom_call_target="tpu_custom_call" | custom-call | flops 1 | bytes 1 | tf_op jit(solution)/shard_map/take/pallas_call | solution.py:97
  5.4 2.7 %collective-permute-start = (bf16[256,512]{1,0:T(8,128)(2,1)}, bf16[256,512]{1,0:T(8,128)(2,1)S(1)}, u32[]{:S(2)}, u32[]{:S(2)}) collective-permute-start(bf16[256,512]{1,0:T(8,128)(2,1)} %take.2.refs_0_.refs_13_.refs_1_), channel_id=1, source_target_pairs={{0,8},{4,12},{8,0},{12,4},{1,9},{5,13},{9,1},{13,5},{2,10},{6,14},... | collective-permute-start | bytes 786440 | tf_op jit(solution)/shard_map/ppermute | solution.py:20
  8.1 1.6 %collective-permute-start.2 = (bf16[256,512]{1,0:T(8,128)(2,1)}, bf16[256,512]{1,0:T(8,128)(2,1)S(1)}, u32[]{:S(2)}, u32[]{:S(2)}) collective-permute-start(bf16[256,512]{1,0:T(8,128)(2,1)} %take.2.refs_0_.refs_13_.refs_1_), channel_id=1, source_target_pairs={{0,4},{4,0},{8,12},{12,8},{1,5},{5,1},{9,13},{13,9},{2,6},{6,2},{1... | collective-permute-start | bytes 786440 | tf_op jit(solution)/shard_map/ppermute | solution.py:20
  9.9 0.6 collective-permute-start.6
  10.5 8.5 %collective-permute-done.6.refs_7_.refs_6_ = bf16[144,512]{1,0:T(8,128)(2,1)S(1)} collective-permute-done((bf16[144,512]{1,0:T(8,128)(2,1)S(1)}, bf16[144,512]{1,0:T(8,128)(2,1)S(1)}, u32[]{:S(2)}, u32[]{:S(2)}) %collective-permute-start.6) | collective-permute-done | bytes 147488 | tf_op jit(solution)/shard_map/ppermute | solution.py:20
  19.0 1.1 %collective-permute-done.refs_0_ = bf16[256,512]{1,0:T(8,128)(2,1)S(1)} collective-permute-done((bf16[256,512]{1,0:T(8,128)(2,1)}, bf16[256,512]{1,0:T(8,128)(2,1)S(1)}, u32[]{:S(2)}, u32[]{:S(2)}) %collective-permute-start) | collective-permute-done | bytes 262176 | tf_op jit(solution)/shard_map/ppermute | solution.py:20
  20.3 0.6 collective-permute-start.7
  20.9 0.7 %collective-permute-done.8.refs_9_.refs_8_ = bf16[144,512]{1,0:T(8,128)(2,1)S(1)} collective-permute-done((bf16[144,512]{1,0:T(8,128)(2,1)S(1)}, bf16[144,512]{1,0:T(8,128)(2,1)S(1)}, u32[]{:S(2)}, u32[]{:S(2)}) %collective-permute-start.8) | collective-permute-done | bytes 147488 | tf_op jit(solution)/shard_map/ppermute | solution.py:20
  21.8 1.5 %collective-permute-start.1 = (bf16[256,512]{1,0:T(8,128)(2,1)S(1)}, bf16[256,512]{1,0:T(8,128)(2,1)S(1)}, u32[]{:S(2)}, u32[]{:S(2)}) collective-permute-start(bf16[256,512]{1,0:T(8,128)(2,1)S(1)} %collective-permute-done.refs_0_), channel_id=1, source_target_pairs={{0,4},{4,0},{8,12},{12,8},{1,5},{5,1},{9,13},{13,9},{2,6},{6,2},{1... | collective-permute-start | bytes 786440 | tf_op jit(solution)/shard_map/ppermute | solution.py:20
  23.3 0.5 take.3
  23.8 0.8 %collective-permute-done.4.refs_5_.refs_4_ = bf16[144,512]{1,0:T(8,128)(2,1)S(1)} collective-permute-done((bf16[144,512]{1,0:T(8,128)(2,1)S(1)}, bf16[144,512]{1,0:T(8,128)(2,1)S(1)}, u32[]{:S(2)}, u32[]{:S(2)}) %collective-permute-start.4) | collective-permute-done | bytes 147488 | tf_op jit(solution)/shard_map/ppermute | solution.py:20
  24.6 0.6 collective-permute-start.18
  25.2 2.2 %forward.2 = (f32[256,128]{1,0:T(8,128)S(1)}, f32[256,128]{1,0:T(8,128)S(1)}) custom-call(bf16[256,512]{1,0:T(8,128)(2,1)S(1)} %collective-permute-done.refs_0_, bf16[256,512]{1,0:T(8,128)(2,1)S(1)} %collective-permute-done.2.refs_1_, bf16[512,512]{1,0:T(8,128)(2,1)S(1)} %copy-done.1, bf16[144,512]{1,0:T(8,128)(2,1)S(1)} %get-tuple-element.39.refs_3_.refs_2_, ...), custom_call_target="tpu_custom_call" | custom-call | flops 1 | bytes 1 | tf_op jit(solution)/shard_map/forward/pallas_call | solution.py:155
  27.4 2.7 %collective-permute-start.10 = (f32[256,128]{1,0:T(8,128)S(1)}, f32[256,128]{1,0:T(8,128)S(1)}, u32[]{:S(2)}, u32[]{:S(2)}) collective-permute-start(f32[256,128]{1,0:T(8,128)S(1)} %get-tuple-element.42), channel_id=1, source_target_pairs={{0,8},{4,12},{8,0},{12,4},{1,9},{5,13},{9,1},{13,5},{2,10},{6,14},... | collective-permute-start | bytes 393224 | tf_op jit(solution)/shard_map/ppermute | solution.py:20
  30.1 0.6 collective-permute-start.11
  30.7 1.3 %forward.3 = f32[256,128]{1,0:T(8,128)S(1)} custom-call(bf16[256,512]{1,0:T(8,128)(2,1)S(1)} %collective-permute-done.1.refs_0_.refs_15_.refs_3_, bf16[512,512]{1,0:T(8,128)(2,1)S(1)} %copy-done.1, bf16[144,512]{1,0:T(8,128)(2,1)S(1)} %get-tuple-element.39.refs_3_.refs_2_, bf16[512,512]{1,0:T(8,128)(2,1)S(1)} %collective-permute-done.3.refs_4_.refs_3_, ...), custom_call_target="tpu_custom_call" | custom-call | flops 17179869184 | bytes 1048576 | tf_op jit(solution)/shard_map/forward/pallas_call | solution.py:155
  32.0 4.6 %collective-permute-done.10.refs_9_ = f32[256,128]{1,0:T(8,128)S(1)} collective-permute-done((f32[256,128]{1,0:T(8,128)S(1)}, f32[256,128]{1,0:T(8,128)S(1)}, u32[]{:S(2)}, u32[]{:S(2)}) %collective-permute-start.10) | collective-permute-done | bytes 131104 | tf_op jit(solution)/shard_map/ppermute | solution.py:20
  36.6 0.3 collective-permute-done.11.refs_10_
  36.8 2.3 %collective-permute-start.13 = (f32[256,128]{1,0:T(8,128)S(1)}, f32[256,128]{1,0:T(8,128)S(1)}, u32[]{:S(2)}, u32[]{:S(2)}) collective-permute-start(f32[256,128]{1,0:T(8,128)S(1)} %forward.3), channel_id=1, source_target_pairs={{0,12},{4,8},{8,4},{12,0},{1,13},{5,9},{9,5},{13,1},{2,14},{6,10},... | collective-permute-start | bytes 393224 | tf_op jit(solution)/shard_map/ppermute | solution.py:20
  39.4 1.1 %collective-permute-start.19 = (bf16[256,512]{1,0:T(8,128)(2,1)S(1)}, bf16[256,512]{1,0:T(8,128)(2,1)S(1)}, u32[]{:S(2)}, u32[]{:S(2)}) collective-permute-start(bf16[256,512]{1,0:T(8,128)(2,1)S(1)} %collective-permute-done.1.refs_0_.refs_15_.refs_3_), channel_id=1, source_target_pairs={{0,2},{1,3},{2,0},{3,1},{4,6},{5,7},{6,4},{7,5},{8,10},{9,11},{10,... | collective-permute-start | bytes 786440 | tf_op jit(solution)/shard_map/ppermute | solution.py:20
  40.5 3.1 %own_rows.1 = (f32[256,128]{1,0:T(8,128)S(1)}, bf16[512,1024]{1,0:T(8,128)(2,1)S(1)}, bf16[512,1024]{1,0:T(8,128)(2,1)S(1)}) custom-call(bf16[256,512]{1,0:T(8,128)(2,1)S(1)} %copy-done.5, bf16[512,512]{1,0:T(8,128)(2,1)S(1)} %copy-done.1, bf16[144,512]{1,0:T(8,128)(2,1)S(1)} %get-tuple-element.39.refs_3_.refs_2_, ...), custom_call_target="tpu_custom_call" | custom-call | flops 17179869184 | bytes 1048576 | tf_op jit(solution)/shard_map/own_rows/pallas_call | solution.py:202
  43.6 1.0 %collective-permute-done.13.refs_1_ = f32[256,128]{1,0:T(8,128)S(1)} collective-permute-done((f32[256,128]{1,0:T(8,128)S(1)}, f32[256,128]{1,0:T(8,128)S(1)}, u32[]{:S(2)}, u32[]{:S(2)}) %collective-permute-start.13) | collective-permute-done | bytes 131104 | tf_op jit(solution)/shard_map/ppermute | solution.py:20
  44.8 2.3 %collective-permute-start.14 = (bf16[256,128]{1,0:T(8,128)(2,1)S(1)}, bf16[256,128]{1,0:T(8,128)(2,1)S(1)}, u32[]{:S(2)}, u32[]{:S(2)}) collective-permute-start(bf16[256,128]{1,0:T(8,128)(2,1)S(1)} %cotangent.1), channel_id=1, source_target_pairs={{0,4},{4,0},{8,12},{12,8},{1,5},{5,1},{9,13},{13,9},{2,6},{6,2},{1... | collective-permute-start | bytes 196616 | tf_op jit(solution)/shard_map/ppermute | solution.py:20
  47.1 0.6 collective-permute-start.15
  47.7 1.8 %collective-permute-start.16 = (bf16[256,128]{1,0:T(8,128)(2,1)S(1)}, bf16[256,128]{1,0:T(8,128)(2,1)S(1)}, u32[]{:S(2)}, u32[]{:S(2)}) collective-permute-start(bf16[256,128]{1,0:T(8,128)(2,1)S(1)} %cotangent.1), channel_id=1, source_target_pairs={{0,12},{4,8},{8,4},{12,0},{1,13},{5,9},{9,5},{13,1},{2,14},{6,10},... | collective-permute-start | bytes 196616 | tf_op jit(solution)/shard_map/ppermute | solution.py:20
  49.6 5.3 %collective-permute-done.15 = bf16[256,128]{1,0:T(8,128)(2,1)S(1)} collective-permute-done((bf16[256,128]{1,0:T(8,128)(2,1)S(1)}, bf16[256,128]{1,0:T(8,128)(2,1)S(1)}, u32[]{:S(2)}, u32[]{:S(2)}) %collective-permute-start.15) | collective-permute-done | bytes 65568 | tf_op jit(solution)/shard_map/ppermute | solution.py:20
  54.9 1.3 %collective-permute-start.22 = (bf16[1024,128]{1,0:T(8,128)(2,1)S(1)}, bf16[1024,128]{1,0:T(8,128)(2,1)S(1)}, u32[]{:S(2)}, u32[]{:S(2)}) collective-permute-start(bf16[1024,128]{1,0:T(8,128)(2,1)S(1)} %pad_maximum_fusion.refs_4_), channel_id=1, source_target_pairs={{0,2},{1,3},{2,0},{3,1},{4,6},{5,7},{6,4},{7,5},{8,10},{9,11},{10,... | collective-permute-start | bytes 786440 | tf_op jit(solution)/shard_map/ppermute | solution.py:20
  56.4 4.8 %backward.3 = (f32[512,512]{1,0:T(8,128)S(1)}, f32[512,128]{1,0:T(8,128)S(1)}, f32[512,128]{1,0:T(8,128)S(1)}, bf16[512,1024]{1,0:T(8,128)(2,1)S(1)}, bf16[512,1024]{1,0:T(8,128)(2,1)S(1)}) custom-call(bf16[512,512]{1,0:T(8,128)(2,1)S(1)} %copy-done.1, bf16[512,128]{1,0:T(8,128)(2,1)S(1)} %copy-done.2, bf16[1,512]{1,0:T(2,128)(2,1)S(1)} %reshape.12.spread_ref.refs_12_, ...), custom_call_target="tpu_custom_call" | custom-call | flops 17179869184 | bytes 1048576 | tf_op jit(solution)/shard_map/backward/pallas_call | solution.py:291
  61.2 2.4 %collective-permute-done.22.refs_4_ = bf16[1024,128]{1,0:T(8,128)(2,1)S(1)} collective-permute-done((bf16[1024,128]{1,0:T(8,128)(2,1)S(1)}, bf16[1024,128]{1,0:T(8,128)(2,1)S(1)}, u32[]{:S(2)}, u32[]{:S(2)}) %collective-permute-start.22) | collective-permute-done | bytes 262176 | tf_op jit(solution)/shard_map/ppermute | solution.py:20
  63.6 1.3 %backward.4 = (f32[512,512]{1,0:T(8,128)S(1)}, f32[512,128]{1,0:T(8,128)S(1)}, f32[512,128]{1,0:T(8,128)S(1)}) custom-call(bf16[512,512]{1,0:T(8,128)(2,1)S(1)} %copy-done.1, bf16[512,128]{1,0:T(8,128)(2,1)S(1)} %copy-done.2, bf16[1,512]{1,0:T(2,128)(2,1)S(1)} %reshape.12.spread_ref.refs_12_, bf16[512,1024]{1,0:T(8,128)(2,1)S(1)} %get-tuple-element.62.refs_0_, ...), custom_call_target="tpu_custom_call" | custom-call | flops 1 | bytes 1 | tf_op jit(solution)/shard_map/backward/pallas_call | solution.py:291
  65.2 2.4 %backward.5 = (f32[512,512]{1,0:T(8,128)}, f32[512,128]{1,0:T(8,128)}) custom-call(bf16[512,512]{1,0:T(8,128)(2,1)S(1)} %copy-done.1, bf16[512,128]{1,0:T(8,128)(2,1)S(1)} %copy-done.2, bf16[1,512]{1,0:T(2,128)(2,1)S(1)} %reshape.12.spread_ref.refs_12_, bf16[512,1024]{1,0:T(8,128)(2,1)S(1)} %get-tuple-element.59.refs_0_, ...), custom_call_target="tpu_custom_call" | custom-call | flops 1 | bytes 1 | tf_op jit(solution)/shard_map/backward/pallas_call | solution.py:291
  (46 shorter events, 1.6 us)
Async XLA Ops:
  0.6 9.0 %copy-start.1 = (bf16[512,512]{1,0:T(8,128)(2,1)S(1)}, bf16[512,512]{1,0:T(8,128)(2,1)}, u32[]{:S(2)}) copy-start(bf16[512,512]{1,0:T(8,128)(2,1)} %pos_ref.6) | copy-start | bytes 1572868
  0.6 9.0 %copy-start.7 = (bf16[512]{0:T(512)(128)(2,1)S(1)}, bf16[512]{0:T(512)(128)(2,1)}, u32[]{:S(2)}) copy-start(bf16[512]{0:T(512)(128)(2,1)} %param.13) | copy-start | bytes 3076
  0.7 9.0 %copy-start.2 = (bf16[512,128]{1,0:T(8,128)(2,1)S(1)}, bf16[512,128]{1,0:T(8,128)(2,1)}, u32[]{:S(2)}) copy-start(bf16[512,128]{1,0:T(8,128)(2,1)} %coef_in.5) | copy-start | bytes 393220
  0.7 19.6 %collective-permute-start.5 = (bf16[512,512]{1,0:T(8,128)(2,1)}, bf16[512,512]{1,0:T(8,128)(2,1)S(1)}, u32[]{:S(2)}, u32[]{:S(2)}) collective-permute-start(bf16[512,512]{1,0:T(8,128)(2,1)} %pos_ref.6), channel_id=1, source_target_pairs={{0,2},{1,3},{2,0},{3,1},{4,6},{5,7},{6,4},{7,5},{8,10},{9,11},{10,... | collective-permute-start | bytes 1572872 | tf_op jit(solution)/shard_map/ppermute | solution.py:20
  3.7 6.0 %copy-start.6 = (f32[128]{0:T(128)S(1)}, f32[128]{0:T(128)}, u32[]{:S(2)}) copy-start(f32[128]{0:T(128)} %param.10) | copy-start | bytes 1540
  3.7 19.6 %copy-start.4 = (f32[1024,128]{1,0:T(8,128)S(1)}, f32[1024,128]{1,0:T(8,128)}, u32[]{:S(2)}) copy-start(f32[1024,128]{1,0:T(8,128)} %refs_1_.3) | copy-start | bytes 1572868
  5.4 17.9 %copy-start = (bf16[1024,512]{1,0:T(8,128)(2,1)S(1)}, bf16[1024,512]{1,0:T(8,128)(2,1)}, u32[]{:S(2)}) copy-start(bf16[1024,512]{1,0:T(8,128)(2,1)} %refs_4_.1) | copy-start | bytes 3145732
  5.4 14.7 %collective-permute-start = (bf16[256,512]{1,0:T(8,128)(2,1)}, bf16[256,512]{1,0:T(8,128)(2,1)S(1)}, u32[]{:S(2)}, u32[]{:S(2)}) collective-permute-start(bf16[256,512]{1,0:T(8,128)(2,1)} %take.2.refs_0_.refs_13_.refs_1_), channel_id=1, source_target_pairs={{0,8},{4,12},{8,0},{12,4},{1,9},{5,13},{9,1},{13,5},{2,10},{6,14},... | collective-permute-start | bytes 786440 | tf_op jit(solution)/shard_map/ppermute | solution.py:20
  8.1 12.2 %collective-permute-start.2 = (bf16[256,512]{1,0:T(8,128)(2,1)}, bf16[256,512]{1,0:T(8,128)(2,1)S(1)}, u32[]{:S(2)}, u32[]{:S(2)}) collective-permute-start(bf16[256,512]{1,0:T(8,128)(2,1)} %take.2.refs_0_.refs_13_.refs_1_), channel_id=1, source_target_pairs={{0,4},{4,0},{8,12},{12,8},{1,5},{5,1},{9,13},{13,9},{2,6},{6,2},{1... | collective-permute-start | bytes 786440 | tf_op jit(solution)/shard_map/ppermute | solution.py:20
  9.9 13.4 %copy-start.3 = (f32[1024,128]{1,0:T(8,128)S(1)}, f32[1024,128]{1,0:T(8,128)}, u32[]{:S(2)}) copy-start(f32[1024,128]{1,0:T(8,128)} %refs_0_.3) | copy-start | bytes 1572868
  9.9 9.1 %collective-permute-start.6 = (bf16[144,512]{1,0:T(8,128)(2,1)S(1)}, bf16[144,512]{1,0:T(8,128)(2,1)S(1)}, u32[]{:S(2)}, u32[]{:S(2)}) collective-permute-start(bf16[144,512]{1,0:T(8,128)(2,1)S(1)} %get-tuple-element.39.refs_3_.refs_2_), channel_id=1, source_target_pairs={{0,2},{1,3},{2,0},{3,1},{4,6},{5,7},{6,4},{7,5},{8,10},{9,11},{10,... | collective-permute-start | bytes 442376 | tf_op jit(solution)/shard_map/ppermute | solution.py:20
  10.5 14.7 %collective-permute-start.3 = (bf16[512,512]{1,0:T(8,128)(2,1)S(1)}, bf16[512,512]{1,0:T(8,128)(2,1)S(1)}, u32[]{:S(2)}, u32[]{:S(2)}) collective-permute-start(bf16[512,512]{1,0:T(8,128)(2,1)S(1)} %copy-done.1), channel_id=1, source_target_pairs={{0,1},{1,0},{2,3},{3,2},{4,5},{5,4},{6,7},{7,6},{8,9},{9,8},{10,11... | collective-permute-start | bytes 1572872 | tf_op jit(solution)/shard_map/ppermute | solution.py:20
  20.3 1.4 %collective-permute-start.8 = (bf16[144,512]{1,0:T(8,128)(2,1)S(1)}, bf16[144,512]{1,0:T(8,128)(2,1)S(1)}, u32[]{:S(2)}, u32[]{:S(2)}) collective-permute-start(bf16[144,512]{1,0:T(8,128)(2,1)S(1)} %collective-permute-done.6.refs_7_.refs_6_), channel_id=1, source_target_pairs={{0,1},{1,0},{2,3},{3,2},{4,5},{5,4},{6,7},{7,6},{8,9},{9,8},{10,11... | collective-permute-start | bytes 442376 | tf_op jit(solution)/shard_map/ppermute | solution.py:20
  20.3 4.9 %collective-permute-start.7 = (bf16[512,512]{1,0:T(8,128)(2,1)S(1)}, bf16[512,512]{1,0:T(8,128)(2,1)S(1)}, u32[]{:S(2)}, u32[]{:S(2)}) collective-permute-start(bf16[512,512]{1,0:T(8,128)(2,1)S(1)} %collective-permute-done.5.refs_6_.refs_5_), channel_id=1, source_target_pairs={{0,1},{1,0},{2,3},{3,2},{4,5},{5,4},{6,7},{7,6},{8,9},{9,8},{10,11... | collective-permute-start | bytes 1572872 | tf_op jit(solution)/shard_map/ppermute | solution.py:20
  21.6 9.1 %collective-permute-start.9 = (bf16[512,512]{1,0:T(8,128)(2,1)S(1)}, bf16[512,512]{1,0:T(8,128)(2,1)S(1)}, u32[]{:S(2)}, u32[]{:S(2)}) collective-permute-start(bf16[512,512]{1,0:T(8,128)(2,1)S(1)} %constant_dynamic-update-slice_fusion.refs_14_.refs_2_), channel_id=1, source_target_pairs={{0,1},{1,0},{2,3},{3,2},{4,5},{5,4},{6,7},{7,6},{8,9},{9,8},{10,11... | collective-permute-start | bytes 1572872 | tf_op jit(solution)/shard_map/ppermute | solution.py:20
  21.8 8.9 %collective-permute-start.1 = (bf16[256,512]{1,0:T(8,128)(2,1)S(1)}, bf16[256,512]{1,0:T(8,128)(2,1)S(1)}, u32[]{:S(2)}, u32[]{:S(2)}) collective-permute-start(bf16[256,512]{1,0:T(8,128)(2,1)S(1)} %collective-permute-done.refs_0_), channel_id=1, source_target_pairs={{0,4},{4,0},{8,12},{12,8},{1,5},{5,1},{9,13},{13,9},{2,6},{6,2},{1... | collective-permute-start | bytes 786440 | tf_op jit(solution)/shard_map/ppermute | solution.py:20
  23.2 1.4 %collective-permute-start.4 = (bf16[144,512]{1,0:T(8,128)(2,1)S(1)}, bf16[144,512]{1,0:T(8,128)(2,1)S(1)}, u32[]{:S(2)}, u32[]{:S(2)}) collective-permute-start(bf16[144,512]{1,0:T(8,128)(2,1)S(1)} %get-tuple-element.39.refs_3_.refs_2_), channel_id=1, source_target_pairs={{0,1},{1,0},{2,3},{3,2},{4,5},{5,4},{6,7},{7,6},{8,9},{9,8},{10,11... | collective-permute-start | bytes 442376 | tf_op jit(solution)/shard_map/ppermute | solution.py:20
  24.6 14.6 %collective-permute-start.18 = (bf16[512,512]{1,0:T(8,128)(2,1)S(1)}, bf16[512,512]{1,0:T(8,128)(2,1)S(1)}, u32[]{:S(2)}, u32[]{:S(2)}) collective-permute-start(bf16[512,512]{1,0:T(8,128)(2,1)S(1)} %constant_dynamic-update-slice_fusion.refs_14_.refs_2_), channel_id=1, source_target_pairs={{0,2},{1,3},{2,0},{3,1},{4,6},{5,7},{6,4},{7,5},{8,10},{9,11},{10,... | collective-permute-start | bytes 1572872 | tf_op jit(solution)/shard_map/ppermute | solution.py:20
  27.4 9.1 %collective-permute-start.10 = (f32[256,128]{1,0:T(8,128)S(1)}, f32[256,128]{1,0:T(8,128)S(1)}, u32[]{:S(2)}, u32[]{:S(2)}) collective-permute-start(f32[256,128]{1,0:T(8,128)S(1)} %get-tuple-element.42), channel_id=1, source_target_pairs={{0,8},{4,12},{8,0},{12,4},{1,9},{5,13},{9,1},{13,5},{2,10},{6,14},... | collective-permute-start | bytes 393224 | tf_op jit(solution)/shard_map/ppermute | solution.py:20
  30.1 10.4 %copy-start.5 = (bf16[256,512]{1,0:T(8,128)(2,1)S(1)}, bf16[256,512]{1,0:T(8,128)(2,1)}, u32[]{:S(2)}) copy-start(bf16[256,512]{1,0:T(8,128)(2,1)} %take.2.refs_0_.refs_13_.refs_1_) | copy-start | bytes 786436
  30.1 6.7 %collective-permute-start.11 = (f32[256,128]{1,0:T(8,128)S(1)}, f32[256,128]{1,0:T(8,128)S(1)}, u32[]{:S(2)}, u32[]{:S(2)}) collective-permute-start(f32[256,128]{1,0:T(8,128)S(1)} %get-tuple-element.43), channel_id=1, source_target_pairs={{0,4},{4,0},{8,12},{12,8},{1,5},{5,1},{9,13},{13,9},{2,6},{6,2},{1... | collective-permute-start | bytes 393224 | tf_op jit(solution)/shard_map/ppermute | solution.py:20
  36.8 3.7 %collective-permute-start.12 = (bf16[256,512]{1,0:T(8,128)(2,1)S(1)}, bf16[256,512]{1,0:T(8,128)(2,1)S(1)}, u32[]{:S(2)}, u32[]{:S(2)}) collective-permute-start(bf16[256,512]{1,0:T(8,128)(2,1)S(1)} %collective-permute-done.1.refs_0_.refs_15_.refs_3_), channel_id=1, source_target_pairs={{0,1},{1,0},{2,3},{3,2},{4,5},{5,4},{6,7},{7,6},{8,9},{9,8},{10,11... | collective-permute-start | bytes 786440 | tf_op jit(solution)/shard_map/ppermute | solution.py:20
  36.8 7.8 %collective-permute-start.13 = (f32[256,128]{1,0:T(8,128)S(1)}, f32[256,128]{1,0:T(8,128)S(1)}, u32[]{:S(2)}, u32[]{:S(2)}) collective-permute-start(f32[256,128]{1,0:T(8,128)S(1)} %forward.3), channel_id=1, source_target_pairs={{0,12},{4,8},{8,4},{12,0},{1,13},{5,9},{9,5},{13,1},{2,14},{6,10},... | collective-permute-start | bytes 393224 | tf_op jit(solution)/shard_map/ppermute | solution.py:20
  39.2 17.0 %collective-permute-start.20 = (bf16[512,512]{1,0:T(8,128)(2,1)S(1)}, bf16[512,512]{1,0:T(8,128)(2,1)S(1)}, u32[]{:S(2)}, u32[]{:S(2)}) collective-permute-start(bf16[512,512]{1,0:T(8,128)(2,1)S(1)} %collective-permute-done.18.refs_11_.refs_2_), channel_id=1, source_target_pairs={{0,1},{1,0},{2,3},{3,2},{4,5},{5,4},{6,7},{7,6},{8,9},{9,8},{10,11... | collective-permute-start | bytes 1572872 | tf_op jit(solution)/shard_map/ppermute | solution.py:20
  39.4 10.1 %collective-permute-start.19 = (bf16[256,512]{1,0:T(8,128)(2,1)S(1)}, bf16[256,512]{1,0:T(8,128)(2,1)S(1)}, u32[]{:S(2)}, u32[]{:S(2)}) collective-permute-start(bf16[256,512]{1,0:T(8,128)(2,1)S(1)} %collective-permute-done.1.refs_0_.refs_15_.refs_3_), channel_id=1, source_target_pairs={{0,2},{1,3},{2,0},{3,1},{4,6},{5,7},{6,4},{7,5},{8,10},{9,11},{10,... | collective-permute-start | bytes 786440 | tf_op jit(solution)/shard_map/ppermute | solution.py:20
  44.8 4.8 %collective-permute-start.14 = (bf16[256,128]{1,0:T(8,128)(2,1)S(1)}, bf16[256,128]{1,0:T(8,128)(2,1)S(1)}, u32[]{:S(2)}, u32[]{:S(2)}) collective-permute-start(bf16[256,128]{1,0:T(8,128)(2,1)S(1)} %cotangent.1), channel_id=1, source_target_pairs={{0,4},{4,0},{8,12},{12,8},{1,5},{5,1},{9,13},{13,9},{2,6},{6,2},{1... | collective-permute-start | bytes 196616 | tf_op jit(solution)/shard_map/ppermute | solution.py:20
  47.1 7.7 %collective-permute-start.15 = (bf16[256,128]{1,0:T(8,128)(2,1)S(1)}, bf16[256,128]{1,0:T(8,128)(2,1)S(1)}, u32[]{:S(2)}, u32[]{:S(2)}) collective-permute-start(bf16[256,128]{1,0:T(8,128)(2,1)S(1)} %cotangent.1), channel_id=1, source_target_pairs={{0,8},{4,12},{8,0},{12,4},{1,9},{5,13},{9,1},{13,5},{2,10},{6,14},... | collective-permute-start | bytes 196616 | tf_op jit(solution)/shard_map/ppermute | solution.py:20
  47.7 7.1 %collective-permute-start.16 = (bf16[256,128]{1,0:T(8,128)(2,1)S(1)}, bf16[256,128]{1,0:T(8,128)(2,1)S(1)}, u32[]{:S(2)}, u32[]{:S(2)}) collective-permute-start(bf16[256,128]{1,0:T(8,128)(2,1)S(1)} %cotangent.1), channel_id=1, source_target_pairs={{0,12},{4,8},{8,4},{12,0},{1,13},{5,9},{9,5},{13,1},{2,14},{6,10},... | collective-permute-start | bytes 196616 | tf_op jit(solution)/shard_map/ppermute | solution.py:20
  49.5 6.7 %collective-permute-start.21 = (bf16[256,512]{1,0:T(8,128)(2,1)S(1)}, bf16[256,512]{1,0:T(8,128)(2,1)S(1)}, u32[]{:S(2)}, u32[]{:S(2)}) collective-permute-start(bf16[256,512]{1,0:T(8,128)(2,1)S(1)} %collective-permute-done.19.refs_12_.refs_3_), channel_id=1, source_target_pairs={{0,1},{1,0},{2,3},{3,2},{4,5},{5,4},{6,7},{7,6},{8,9},{9,8},{10,11... | collective-permute-start | bytes 786440 | tf_op jit(solution)/shard_map/ppermute | solution.py:20
  54.8 1.6 %collective-permute-start.17 = (bf16[1024,128]{1,0:T(8,128)(2,1)S(1)}, bf16[1024,128]{1,0:T(8,128)(2,1)S(1)}, u32[]{:S(2)}, u32[]{:S(2)}) collective-permute-start(bf16[1024,128]{1,0:T(8,128)(2,1)S(1)} %pad_maximum_fusion.refs_4_), channel_id=1, source_target_pairs={{0,1},{1,0},{2,3},{3,2},{4,5},{5,4},{6,7},{7,6},{8,9},{9,8},{10,11... | collective-permute-start | bytes 786440 | tf_op jit(solution)/shard_map/ppermute | solution.py:20
  54.9 8.7 %collective-permute-start.22 = (bf16[1024,128]{1,0:T(8,128)(2,1)S(1)}, bf16[1024,128]{1,0:T(8,128)(2,1)S(1)}, u32[]{:S(2)}, u32[]{:S(2)}) collective-permute-start(bf16[1024,128]{1,0:T(8,128)(2,1)S(1)} %pad_maximum_fusion.refs_4_), channel_id=1, source_target_pairs={{0,2},{1,3},{2,0},{3,1},{4,6},{5,7},{6,4},{7,5},{8,10},{9,11},{10,... | collective-permute-start | bytes 786440 | tf_op jit(solution)/shard_map/ppermute | solution.py:20
  63.6 1.5 %collective-permute-start.23 = (bf16[1024,128]{1,0:T(8,128)(2,1)S(1)}, bf16[1024,128]{1,0:T(8,128)(2,1)S(1)}, u32[]{:S(2)}, u32[]{:S(2)}) collective-permute-start(bf16[1024,128]{1,0:T(8,128)(2,1)S(1)} %collective-permute-done.22.refs_4_), channel_id=1, source_target_pairs={{0,1},{1,0},{2,3},{3,2},{4,5},{5,4},{6,7},{7,6},{8,9},{9,8},{10,11... | collective-permute-start | bytes 786440 | tf_op jit(solution)/shard_map/ppermute | solution.py:20

commit v7 on v6

--- a/solution.py
+++ b/solution.py
@@ -83,7 +83,7 @@
     )(center_pos, coefficients, spread.reshape(1, n), delta.reshape(1, -1))
 
 
-def take(arrays, offsets, piece, mib=16):
+def take(arrays, offsets, piece, space=VMEM):
     def body(*refs):
         ins, outs, sems = refs[: len(arrays)], refs[len(arrays) : -1], refs[-1]
         made = []
@@ -98,9 +98,9 @@
         body,
         out_shape=tuple(jax.ShapeDtypeStruct((piece, a.shape[1]), a.dtype) for a in arrays),
         in_specs=[HBM] * len(arrays),
-        out_specs=(VMEM,) * len(arrays),
+        out_specs=(space,) * len(arrays),
         scratch_shapes=[pltpu.SemaphoreType.DMA((len(arrays),))],
-        compiler_params=params(mib),
+        compiler_params=params(16 if space is VMEM else 62),
         cost_estimate=BRIEF,
         name="take",
     )(*arrays)
@@ -125,19 +125,24 @@
     return total
 
 
-def own_values(pos_ref, spread_ref, refs, out_ref):
+def own_values(pos_ref, spread_ref, refs):
     pos = pos_ref[...]
     center_sq = half_sq_column(pos)
     rate = column(spread_ref[...].astype(F32) * (-2.0 * LOG2E / pos.shape[1]))[:, :1]
-    at = 0
     for ref in refs:
         step = min(256, ref.shape[0])
         for start in range(0, ref.shape[0], step):
             x = ref[start : start + step]
             cross = lax.dot_general(pos, x, NT, preferred_element_type=F32)
             power = (center_sq + half_sq_row(x) - cross) * rate
-            out_ref[:, at : at + step] = jnp.exp2(power).astype(BF16)
-            at += step
+            yield jnp.exp2(power).astype(BF16)
+
+
+def store_values(pos_ref, spread_ref, refs, out_ref):
+    at = 0
+    for part in own_values(pos_ref, spread_ref, refs):
+        out_ref[:, at : at + part.shape[1]] = part
+        at += part.shape[1]
 
 
 def forward(rows, centers, out_width, cost):
@@ -168,7 +173,7 @@
     points = sum(b.shape[0] for b in blocks)
 
     def body(pos_ref, spread_ref, *refs):
-        own_values(pos_ref, spread_ref, refs[:-1], refs[-1])
+        store_values(pos_ref, spread_ref, refs[:-1], refs[-1])
 
     return pl.pallas_call(
         body,
@@ -194,7 +199,7 @@
         outs[0][...] = partial_pred(refs[0][...], refs[1 : ends[1]], total)
         pos_ref, spread_ref, *block_refs = refs[ends[2] :]
         for k, blocks in enumerate(more):
-            own_values(pos_ref, spread_ref, block_refs[: len(blocks)], outs[1 + k])
+            store_values(pos_ref, spread_ref, block_refs[: len(blocks)], outs[1 + k])
             del block_refs[: len(blocks)]
 
     ins = [rows, *centers, *received, center_pos, spread.reshape(1, n)]
@@ -232,65 +237,51 @@
     )(*parts, saved, target, delta)
 
 
-def backward(center_pos, coefficients, spread, groups, before=None, last=False, more=()):
+def group_terms(coef, kernel, x, cot):
+    mixing = lax.dot_general(coef, cot, NT, preferred_element_type=F32)
+    weights = (kernel.astype(F32) * mixing).astype(BF16)
+    lanes = weights[:, :128].astype(F32)
+    for k in range(128, kernel.shape[1], 128):
+        lanes += weights[:, k : k + 128].astype(F32)
+    return (
+        jnp.dot(weights, x, preferred_element_type=F32),
+        jnp.dot(kernel, cot, preferred_element_type=F32),
+        lanes,
+    )
+
+
+def backward(center_pos, coefficients, spread, groups, before=None, more=()):
     n, in_width = center_pos.shape
     out_width = coefficients.shape[1]
     flat = []
-    for kernel, xs, cots in groups:
-        flat += [kernel, *xs, *cots]
+    for kernel, xs, cot in groups:
+        flat += [*xs, cot] if kernel is None else [kernel, *xs, cot]
     carried = [] if before is None else list(before)
-    outs = (2 if last else 3) + len(more)
+    outs = 3 + len(more)
     wanted = [block for blocks in more for block in blocks]
-    points = sum(kernel.shape[1] for kernel, _, _ in groups)
-
-    def body(pos_ref, coef_in, spread_ref, *refs):
+
+    def body(pos_ref, coef_ref, spread_ref, *refs):
         refs, out_refs = list(refs[:-outs]), refs[-outs:]
-        coef = coef_in[...]
-        moment = grad_coef = total = None
-        if carried:
-            moment, grad_coef, total = refs[len(flat) : len(flat) + 3]
+        coef = coef_ref[...]
+        sums = [ref[...] for ref in refs[len(flat) : len(flat) + 3]] if carried else None
         block_refs = refs[len(flat) + len(carried) :]
         for k, blocks in enumerate(more):
-            own_values(pos_ref, spread_ref, block_refs[: len(blocks)], out_refs[3 + k])
+            store_values(pos_ref, spread_ref, block_refs[: len(blocks)], out_refs[3 + k])
             del block_refs[: len(blocks)]
-
-        def plus(old, new):
-            return new if old is None else old[...] + new
-
-        for _, xs, cots in groups:
-            kernel_ref = refs.pop(0)
+        for given, xs, _ in groups:
+            kernel = None if given is None else refs.pop(0)[...]
             x_refs = [refs.pop(0) for _ in xs]
-            cot_refs = [refs.pop(0) for _ in cots]
-            cot = jnp.concatenate([ref[...] for ref in cot_refs])
-            kernel = kernel_ref[...]
-            mixing = lax.dot_general(coef, cot, NT, preferred_element_type=F32)
-            weights = (kernel.astype(F32) * mixing).astype(BF16)
-            grad_coef = plus(grad_coef, jnp.dot(kernel, cot, preferred_element_type=F32))
-            lanes = weights[:, :128].astype(F32)
-            for k in range(128, kernel.shape[1], 128):
-                lanes += weights[:, k : k + 128].astype(F32)
-            total = plus(total, lanes)
+            if given is None:
+                kernel = jnp.concatenate(list(own_values(pos_ref, spread_ref, x_refs)), axis=1)
             x = jnp.concatenate([ref[...] for ref in x_refs])
-            moment = plus(moment, jnp.dot(weights, x, preferred_element_type=F32))
-        out_refs[1][...] = grad_coef
-        if last:
-            scale = column(spread_ref[...].astype(F32)) * (2.0 / in_width)
-            total = jnp.sum(total, axis=1, keepdims=True)
-            for k in range(0, in_width, 128):
-                pos = pos_ref[:, k : k + 128].astype(F32)
-                out_refs[0][:, k : k + 128] = scale * (moment[:, k : k + 128] - total * pos)
-        else:
-            out_refs[0][...] = moment
-            out_refs[2][...] = total
-
-    shapes = [
-        jax.ShapeDtypeStruct((n, in_width), F32),
-        jax.ShapeDtypeStruct((n, out_width), F32),
-        jax.ShapeDtypeStruct((n, 128), F32),
-    ]
-    return pl.pallas_call(
-        body,
-        out_shape=tuple(shapes[: 2 if last else 3])
+            terms = group_terms(coef, kernel, x, refs.pop(0)[...])
+            sums = terms if sums is None else [a + b for a, b in zip(sums, terms)]
+        for ref, value in zip(out_refs[:3], sums):
+            ref[...] = value
+
+    return pl.pallas_call(
+        body,
+        out_shape=tuple(jax.ShapeDtypeStruct((n, width), F32) for width in (in_width, out_width, 128))
         + tuple(jax.ShapeDtypeStruct((n, sum(b.shape[0] for b in blocks)), BF16) for blocks in more),
         in_specs=[VMEM] * (3 + len(flat) + len(carried) + len(wanted)),
         out_specs=(VMEM,) * outs,
@@ -300,6 +291,53 @@
     )(center_pos, coefficients, spread.reshape(1, n), *flat, *carried, *wanted)
 
 
+def finish(center_pos, coefficients, spread, group, before):
+    n, in_width = center_pos.shape
+    out_width = coefficients.shape[1]
+    kernel, xs, cot = group
+    step = min(n, 256)
+
+    def body(pos_ref, coef_ref, spread_ref, kernel_ref, cot_ref, *refs):
+        x_refs, refs = refs[: len(xs)], refs[len(xs) :]
+        moment_ref, grad_ref, lanes_ref, centers_out, coef_out, centers_buf, coef_buf, sems = refs
+        x = jnp.concatenate([ref[...] for ref in x_refs])
+        cot = cot_ref[...]
+        scale = column(spread_ref[...].astype(F32)) * (2.0 / in_width)
+        made = []
+        for k, start in enumerate(range(0, n, step)):
+            rows = slice(start, start + step)
+            moment, grad, lanes = group_terms(coef_ref[rows], kernel_ref[rows], x, cot)
+            coef_buf[rows] = grad_ref[rows] + grad
+            moment += moment_ref[rows]
+            total = jnp.sum(lanes_ref[rows] + lanes, axis=1, keepdims=True)
+            for at in range(0, in_width, 128):
+                pos = pos_ref[rows, at : at + 128].astype(F32)
+                centers_buf[rows, at : at + 128] = scale[rows] * (moment[:, at : at + 128] - total * pos)
+            pairs = [(centers_buf, centers_out), (coef_buf, coef_out)]
+            for j, (src, dst) in enumerate(pairs):
+                copy = pltpu.make_async_copy(src.at[rows], dst.at[rows], sems.at[2 * k + j])
+                copy.start()
+                made.append(copy)
+        for copy in made:
+            copy.wait()
+
+    ins = [center_pos, coefficients, spread.reshape(1, n), kernel, cot, *xs, *before]
+    return pl.pallas_call(
+        body,
+        out_shape=tuple(jax.ShapeDtypeStruct((n, width), F32) for width in (in_width, out_width)),
+        in_specs=[VMEM] * len(ins),
+        out_specs=(HBM, HBM),
+        scratch_shapes=[
+            pltpu.VMEM((n, in_width), F32),
+            pltpu.VMEM((n, out_width), F32),
+            pltpu.SemaphoreType.DMA((2 * pl.cdiv(n, step),)),
+        ],
+        compiler_params=params(24),
+        cost_estimate=BRIEF,
+        name="finish",
+    )(*ins)
+
+
 def solution(mesh):
     nz, nc = mesh.shape["points"], mesh.shape["centers"]
 
@@ -308,7 +346,7 @@
         n, out_width = coefficients.shape
         piece = n_rows // nc
 
-        (own,) = take([train_points], [0], piece, 62)
+        (own,) = take([train_points], [0], piece, HBM)
 
         layer = {0: own}
         for dz in range(2, nz, 2):
@@ -350,43 +388,44 @@
         soon = list(received.values())
         received = [swap(parts[dz], "points", nz, dz) for dz in second]
         last = parts[nz - 1]
-        late = {0: layer[nz - 1]}
-        for d in (1, *range(2, nc, 2)):
-            late[d] = swap(after(late[0], last, *soon), "centers", nc, d)
-        near = [[local[d], early[d], late[d]] for d in (0, 1)]
-        kernels = {}
-        parts[0], kernels[0], kernels[1] = own_rows(
-            after(own, last), centers, out_width, soon, center_pos, spread, near
+        kernels, late = {1: None}, {0: layer[nz - 1]}
+        parts[0], kernels[0] = own_rows(
+            after(own, last),
+            centers,
+            out_width,
+            soon,
+            center_pos,
+            spread,
+            [[local[0], early[0], late[0]]],
         )
         for d in range(2, nc, 2):
-            early[d + 1] = swap(after(early[d], last), "centers", nc, 1)
+            late[d] = swap(after(late[0], parts[0]), "centers", nc, d)
+            early[d + 1] = swap(after(early[d], parts[0]), "centers", nc, 1)
+        late[1] = swap(after(late[0], parts[0]), "centers", nc, 1)
         cot = cotangent([parts[0], *received], saved, target, delta)
 
         far = [swap(cot, "points", nz, dz) for dz in range(1, nz)]
-        cots = {0: [jnp.concatenate([cot, *far])]}
-        for d in range(2, nc, 2):
-            cots[d] = [swap(cots[0][0], "centers", nc, d)]
+        cots = {0: jnp.concatenate([cot, *far])}
+        for d in range(2, nc, 2):
+            cots[d] = swap(cots[0], "centers", nc, d)
             late[d + 1] = swap(after(late[d], far[0]), "centers", nc, 1)
-        cots[1] = [swap(cots[0][0], "centers", nc, 1)]
+        cots[1] = swap(cots[0], "centers", nc, 1)
 
         points = {d: [local[d], early[d], late[d]] for d in range(nc)}
         groups = [(kernels[d], points[d], cots[d]) for d in (0, 1)]
-        rest = range(2, nc)
-        *sums, a, b = backward(
+        *sums, kernels[2], kernels[3] = backward(
             center_pos, coefficients, spread, groups, more=[points[2], points[3]]
         )
-        kernels[2], kernels[3] = a, b
         for d in range(4, nc):
             kernels[d] = own_kernel(center_pos, spread, points[d])
         for d in range(2, nc, 2):
-            cots[d] = [after(cots[d][0], sums[0])]
-            cots[d + 1] = [swap(cots[d][0], "centers", nc, 1)]
-        for d in rest:
+            cots[d] = after(cots[d], sums[0])
+            cots[d + 1] = swap(cots[d], "centers", nc, 1)
+        for d in range(2, nc - 1):
             group = (kernels[d], points[d], cots[d])
-            sums = backward(
-                center_pos, coefficients, spread, [group], before=sums, last=d + 1 == nc
-            )
-        return sums
+            sums = backward(center_pos, coefficients, spread, [group], before=sums)
+        group = (kernels[nc - 1], points[nc - 1], cots[nc - 1])
+        return finish(center_pos, coefficients, spread, group, sums)
 
     return jax.shard_map(
         per_device,

time: 67.7 us -> 73.1 us (1.080)
  Pallas kernels: 17.6 us -> 24.7 us
  waiting for transfers between devices: 25.4 us -> 19.6 us
  starting transfers between devices: 23.7 us -> 27.8 us
    pallas_call x2, Pallas kernels: 2.18 us -> 9.51 us  [take(): pl.pallas_call(body, out_shape=tuple((jax.ShapeDtypeStruct((piece, a.shap...]
    ppermute x24, waiting for transfers between devices: 25.4 us -> 19.6 us  [swap(): return lax.ppermute(a, axis, [(i, i ^ d) for i in range(size)])]
    ppermute x24, starting transfers between devices: 23.7 us -> 27.8 us  [swap(): return lax.ppermute(a, axis, [(i, i ^ d) for i in range(size)])]
    pallas_call x1, Pallas kernels: 3.11 us -> 2.26 us  [own_rows(): pl.pallas_call(body, out_shape=(jax.ShapeDtypeStruct((rows.shape[0], out_...]
  transfers between devices with their start and end apart: 24 -> 24, of which waited for: 12 -> 12; matrix products, arithmetic and copies ran while one was open for 0% -> 0% of each run, Pallas kernels for 23% -> 31%
where the time goes in v7:
time: 73.1 us; the launch traced here: 73 us
  starting transfers between devices  27.8 us (38%)
  Pallas kernels  24.7 us (34%)
  waiting for transfers between devices  19.6 us (27%)
  between operations  0.83 us (1%)
    ppermute x24, starting transfers between devices, swap(): return lax.ppermute(a, axis, [(i, i ^ d) for i in range(size)])  27.8 us
    ppermute x24, waiting for transfers between devices, swap(): return lax.ppermute(a, axis, [(i, i ^ d) for i in range(size)])  19.6 us
    pallas_call x2, Pallas kernels, take(): pl.pallas_call(body, out_shape=tuple((jax.ShapeDtypeStruct((piece, a.shap...  9.51 us
    pallas_call x2, Pallas kernels, backward(): pl.pallas_call(body, out_shape=tuple((jax.ShapeDtypeStruct((n, width), F3...  6.84 us
    pallas_call x2, Pallas kernels, forward(): pl.pallas_call(body, out_shape=tuple((jax.ShapeDtypeStruct((count, out_wi...  3.55 us
    pallas_call x1, Pallas kernels, finish(): pl.pallas_call(body, out_shape=tuple((jax.ShapeDtypeStruct((n, width), F3...  2.26 us
    pallas_call x1, Pallas kernels, own_rows(): pl.pallas_call(body, out_shape=(jax.ShapeDtypeStruct((rows.shape[0], out_...  2.26 us
  transfers between devices with their start and end apart: 24, of which 12 were waited for; matrix products, arithmetic and copies ran while one was open for 0% of the time, Pallas kernels for 31%

profile of v7, /device:TPU:0, one launch (start us, length us, event | category | flops | bytes accessed | tf_op | source)
XLA Modules:
  0.0 73.0 jit_solution(2336686680917016179)
XLA Ops:
  0.7 3.0 %collective-permute-start.5 = (bf16[512,512]{1,0:T(8,128)(2,1)}, bf16[512,512]{1,0:T(8,128)(2,1)S(1)}, u32[]{:S(2)}, u32[]{:S(2)}) collective-permute-start(bf16[512,512]{1,0:T(8,128)(2,1)} %pos_ref.6), channel_id=1, source_target_pairs={{0,2},{1,3},{2,0},{3,1},{4,6},{5,7},{6,4},{7,5},{8,10},{9,11},{10,... | collective-permute-start | bytes 1572872 | tf_op jit(solution)/shard_map/ppermute | solution.py:20
  3.7 9.0 %take.2.refs_0_.refs_13_.refs_1_ = bf16[256,512]{1,0:T(8,128)(2,1)} custom-call(bf16[1024,512]{1,0:T(8,128)(2,1)} %refs_4_.1), custom_call_target="tpu_custom_call" | custom-call | flops 1 | bytes 1 | tf_op jit(solution)/shard_map/take/pallas_call | solution.py:97
  12.7 2.7 %collective-permute-start = (bf16[256,512]{1,0:T(8,128)(2,1)}, bf16[256,512]{1,0:T(8,128)(2,1)S(1)}, u32[]{:S(2)}, u32[]{:S(2)}) collective-permute-start(bf16[256,512]{1,0:T(8,128)(2,1)} %take.2.refs_0_.refs_13_.refs_1_), channel_id=1, source_target_pairs={{0,8},{4,12},{8,0},{12,4},{1,9},{5,13},{9,1},{13,5},{2,10},{6,14},... | collective-permute-start | bytes 786440 | tf_op jit(solution)/shard_map/ppermute | solution.py:20
  15.4 1.6 %collective-permute-start.2 = (bf16[256,512]{1,0:T(8,128)(2,1)}, bf16[256,512]{1,0:T(8,128)(2,1)S(1)}, u32[]{:S(2)}, u32[]{:S(2)}) collective-permute-start(bf16[256,512]{1,0:T(8,128)(2,1)} %take.2.refs_0_.refs_13_.refs_1_), channel_id=1, source_target_pairs={{0,4},{4,0},{8,12},{12,8},{1,5},{5,1},{9,13},{13,9},{2,6},{6,2},{1... | collective-permute-start | bytes 786440 | tf_op jit(solution)/shard_map/ppermute | solution.py:20
  17.2 0.6 collective-permute-start.6
  17.8 4.6 %collective-permute-done.6.refs_7_.refs_6_ = bf16[144,512]{1,0:T(8,128)(2,1)S(1)} collective-permute-done((bf16[144,512]{1,0:T(8,128)(2,1)S(1)}, bf16[144,512]{1,0:T(8,128)(2,1)S(1)}, u32[]{:S(2)}, u32[]{:S(2)}) %collective-permute-start.6) | collective-permute-done | bytes 147488 | tf_op jit(solution)/shard_map/ppermute | solution.py:20
  22.4 5.0 %collective-permute-done.refs_0_ = bf16[256,512]{1,0:T(8,128)(2,1)S(1)} collective-permute-done((bf16[256,512]{1,0:T(8,128)(2,1)}, bf16[256,512]{1,0:T(8,128)(2,1)S(1)}, u32[]{:S(2)}, u32[]{:S(2)}) %collective-permute-start) | collective-permute-done | bytes 262176 | tf_op jit(solution)/shard_map/ppermute | solution.py:20
  27.6 0.6 collective-permute-start.7
  28.2 0.7 %collective-permute-done.8.refs_9_.refs_8_ = bf16[144,512]{1,0:T(8,128)(2,1)S(1)} collective-permute-done((bf16[144,512]{1,0:T(8,128)(2,1)S(1)}, bf16[144,512]{1,0:T(8,128)(2,1)S(1)}, u32[]{:S(2)}, u32[]{:S(2)}) %collective-permute-start.8) | collective-permute-done | bytes 147488 | tf_op jit(solution)/shard_map/ppermute | solution.py:20
  29.1 1.5 %collective-permute-start.1 = (bf16[256,512]{1,0:T(8,128)(2,1)S(1)}, bf16[256,512]{1,0:T(8,128)(2,1)S(1)}, u32[]{:S(2)}, u32[]{:S(2)}) collective-permute-start(bf16[256,512]{1,0:T(8,128)(2,1)S(1)} %collective-permute-done.refs_0_), channel_id=1, source_target_pairs={{0,4},{4,0},{8,12},{12,8},{1,5},{5,1},{9,13},{13,9},{2,6},{6,2},{1... | collective-permute-start | bytes 786440 | tf_op jit(solution)/shard_map/ppermute | solution.py:20
  30.6 0.5 take.3
  31.1 0.8 %collective-permute-done.4.refs_5_.refs_4_ = bf16[144,512]{1,0:T(8,128)(2,1)S(1)} collective-permute-done((bf16[144,512]{1,0:T(8,128)(2,1)S(1)}, bf16[144,512]{1,0:T(8,128)(2,1)S(1)}, u32[]{:S(2)}, u32[]{:S(2)}) %collective-permute-start.4) | collective-permute-done | bytes 147488 | tf_op jit(solution)/shard_map/ppermute | solution.py:20
  31.9 0.5 collective-permute-start.18
  32.5 2.2 %forward.2 = (f32[256,128]{1,0:T(8,128)S(1)}, f32[256,128]{1,0:T(8,128)S(1)}) custom-call(bf16[256,512]{1,0:T(8,128)(2,1)S(1)} %collective-permute-done.refs_0_, bf16[256,512]{1,0:T(8,128)(2,1)S(1)} %collective-permute-done.2.refs_1_, bf16[512,512]{1,0:T(8,128)(2,1)S(1)} %copy-done.1, bf16[144,512]{1,0:T(8,128)(2,1)S(1)} %get-tuple-element.38.refs_3_.refs_2_, ...), custom_call_target="tpu_custom_call" | custom-call | flops 1 | bytes 1 | tf_op jit(solution)/shard_map/forward/pallas_call | solution.py:160
  34.7 2.4 %collective-permute-start.10 = (f32[256,128]{1,0:T(8,128)S(1)}, f32[256,128]{1,0:T(8,128)S(1)}, u32[]{:S(2)}, u32[]{:S(2)}) collective-permute-start(f32[256,128]{1,0:T(8,128)S(1)} %get-tuple-element.41), channel_id=1, source_target_pairs={{0,8},{4,12},{8,0},{12,4},{1,9},{5,13},{9,1},{13,5},{2,10},{6,14},... | collective-permute-start | bytes 393224 | tf_op jit(solution)/shard_map/ppermute | solution.py:20
  37.1 0.6 collective-permute-start.11
  37.7 1.3 %forward.3 = f32[256,128]{1,0:T(8,128)S(1)} custom-call(bf16[256,512]{1,0:T(8,128)(2,1)S(1)} %collective-permute-done.1.refs_0_.refs_15_.refs_3_, bf16[512,512]{1,0:T(8,128)(2,1)S(1)} %copy-done.1, bf16[144,512]{1,0:T(8,128)(2,1)S(1)} %get-tuple-element.38.refs_3_.refs_2_, bf16[512,512]{1,0:T(8,128)(2,1)S(1)} %collective-permute-done.3.refs_4_.refs_3_, ...), custom_call_target="tpu_custom_call" | custom-call | flops 17179869184 | bytes 1048576 | tf_op jit(solution)/shard_map/forward/pallas_call | solution.py:160
  39.0 4.8 %collective-permute-start.12 = (f32[256,128]{1,0:T(8,128)S(1)}, f32[256,128]{1,0:T(8,128)S(1)}, u32[]{:S(2)}, u32[]{:S(2)}) collective-permute-start(f32[256,128]{1,0:T(8,128)S(1)} %forward.3), channel_id=1, source_target_pairs={{0,12},{4,8},{8,4},{12,0},{1,13},{5,9},{9,5},{13,1},{2,14},{6,10},... | collective-permute-start | bytes 393224 | tf_op jit(solution)/shard_map/ppermute | solution.py:20
  43.8 1.0 %collective-permute-done.10.refs_9_ = f32[256,128]{1,0:T(8,128)S(1)} collective-permute-done((f32[256,128]{1,0:T(8,128)S(1)}, f32[256,128]{1,0:T(8,128)S(1)}, u32[]{:S(2)}, u32[]{:S(2)}) %collective-permute-start.10) | collective-permute-done | bytes 131104 | tf_op jit(solution)/shard_map/ppermute | solution.py:20
  44.8 2.3 %own_rows.1 = (f32[256,128]{1,0:T(8,128)S(1)}, bf16[512,1024]{1,0:T(8,128)(2,1)S(1)}) custom-call(bf16[256,512]{1,0:T(8,128)(2,1)S(1)} %copy-done.5, bf16[512,512]{1,0:T(8,128)(2,1)S(1)} %copy-done.1, bf16[144,512]{1,0:T(8,128)(2,1)S(1)} %get-tuple-element.38.refs_3_.refs_2_, bf16[512,512]{1,0:T(8,128)(2,1)S(1)} %collective-permute-done.3.refs_4_.refs_3_, ...), custom_call_target="tpu_custom_call" | custom-call | flops 17179869184 | bytes 1048576 | tf_op jit(solution)/shard_map/own_rows/pallas_call | solution.py:207
  47.1 4.3 %collective-permute-start.19 = (bf16[256,512]{1,0:T(8,128)(2,1)S(1)}, bf16[256,512]{1,0:T(8,128)(2,1)S(1)}, u32[]{:S(2)}, u32[]{:S(2)}) collective-permute-start(bf16[256,512]{1,0:T(8,128)(2,1)S(1)} %collective-permute-done.1.refs_0_.refs_15_.refs_3_), channel_id=1, source_target_pairs={{0,2},{1,3},{2,0},{3,1},{4,6},{5,7},{6,4},{7,5},{8,10},{9,11},{10,... | collective-permute-start | bytes 786440 | tf_op jit(solution)/shard_map/ppermute | solution.py:20
  51.6 1.1 %collective-permute-start.14 = (bf16[256,128]{1,0:T(8,128)(2,1)S(1)}, bf16[256,128]{1,0:T(8,128)(2,1)S(1)}, u32[]{:S(2)}, u32[]{:S(2)}) collective-permute-start(bf16[256,128]{1,0:T(8,128)(2,1)S(1)} %cotangent.1), channel_id=1, source_target_pairs={{0,8},{4,12},{8,0},{12,4},{1,9},{5,13},{9,1},{13,5},{2,10},{6,14},... | collective-permute-start | bytes 196616 | tf_op jit(solution)/shard_map/ppermute | solution.py:20
  52.7 3.2 %collective-permute-start.15 = (bf16[256,128]{1,0:T(8,128)(2,1)S(1)}, bf16[256,128]{1,0:T(8,128)(2,1)S(1)}, u32[]{:S(2)}, u32[]{:S(2)}) collective-permute-start(bf16[256,128]{1,0:T(8,128)(2,1)S(1)} %cotangent.1), channel_id=1, source_target_pairs={{0,12},{4,8},{8,4},{12,0},{1,13},{5,9},{9,5},{13,1},{2,14},{6,10},... | collective-permute-start | bytes 196616 | tf_op jit(solution)/shard_map/ppermute | solution.py:20
  56.0 1.2 %collective-permute-done.13 = bf16[256,128]{1,0:T(8,128)(2,1)S(1)} collective-permute-done((bf16[256,128]{1,0:T(8,128)(2,1)S(1)}, bf16[256,128]{1,0:T(8,128)(2,1)S(1)}, u32[]{:S(2)}, u32[]{:S(2)}) %collective-permute-start.13) | collective-permute-done | bytes 65568 | tf_op jit(solution)/shard_map/ppermute | solution.py:20
  57.2 3.1 %collective-permute-done.14 = bf16[256,128]{1,0:T(8,128)(2,1)S(1)} collective-permute-done((bf16[256,128]{1,0:T(8,128)(2,1)S(1)}, bf16[256,128]{1,0:T(8,128)(2,1)S(1)}, u32[]{:S(2)}, u32[]{:S(2)}) %collective-permute-start.14) | collective-permute-done | bytes 65568 | tf_op jit(solution)/shard_map/ppermute | solution.py:20
  60.4 0.5 collective-permute-start.21
  61.0 0.9 %collective-permute-done.17.refs_8_ = bf16[1024,128]{1,0:T(8,128)(2,1)S(1)} collective-permute-done((bf16[1024,128]{1,0:T(8,128)(2,1)S(1)}, bf16[1024,128]{1,0:T(8,128)(2,1)S(1)}, u32[]{:S(2)}, u32[]{:S(2)}) %collective-permute-start.17) | collective-permute-done | bytes 262176 | tf_op jit(solution)/shard_map/ppermute | solution.py:20
  61.9 0.4 collective-permute-done.21.refs_14_.refs_2_
  62.3 5.6 %backward.2 = (f32[512,512]{1,0:T(8,128)S(1)}, f32[512,128]{1,0:T(8,128)S(1)}, f32[512,128]{1,0:T(8,128)S(1)}, bf16[512,1024]{1,0:T(8,128)(2,1)S(1)}, bf16[512,1024]{1,0:T(8,128)(2,1)S(1)}) custom-call(bf16[512,512]{1,0:T(8,128)(2,1)S(1)} %copy-done.1, bf16[512,128]{1,0:T(8,128)(2,1)S(1)} %copy-done.2, bf16[1,512]{1,0:T(2,128)(2,1)S(1)} %reshape.12.spread_ref.refs_12_, ...), custom_call_target="tpu_custom_call" | custom-call | flops 17179869184 | bytes 1048576 | tf_op jit(solution)/shard_map/backward/pallas_call | solution.py:282
  67.9 1.3 %collective-permute-done.22.refs_4_ = bf16[1024,128]{1,0:T(8,128)(2,1)S(1)} collective-permute-done((bf16[1024,128]{1,0:T(8,128)(2,1)S(1)}, bf16[1024,128]{1,0:T(8,128)(2,1)S(1)}, u32[]{:S(2)}, u32[]{:S(2)}) %collective-permute-start.22) | collective-permute-done | bytes 262176 | tf_op jit(solution)/shard_map/ppermute | solution.py:20
  69.2 1.3 %backward.3 = (f32[512,512]{1,0:T(8,128)S(1)}, f32[512,128]{1,0:T(8,128)S(1)}, f32[512,128]{1,0:T(8,128)S(1)}) custom-call(bf16[512,512]{1,0:T(8,128)(2,1)S(1)} %copy-done.1, bf16[512,128]{1,0:T(8,128)(2,1)S(1)} %copy-done.2, bf16[1,512]{1,0:T(2,128)(2,1)S(1)} %reshape.12.spread_ref.refs_12_, bf16[512,1024]{1,0:T(8,128)(2,1)S(1)} %get-tuple-element.60.refs_0_, ...), custom_call_target="tpu_custom_call" | custom-call | flops 1 | bytes 1 | tf_op jit(solution)/shard_map/backward/pallas_call | solution.py:282
  70.7 2.3 %finish.1 = (f32[512,512]{1,0:T(8,128)}, f32[512,128]{1,0:T(8,128)}) custom-call(bf16[512,512]{1,0:T(8,128)(2,1)S(1)} %copy-done.1, bf16[512,128]{1,0:T(8,128)(2,1)S(1)} %copy-done.2, bf16[1,512]{1,0:T(2,128)(2,1)S(1)} %reshape.12.spread_ref.refs_12_, bf16[512,1024]{1,0:T(8,128)(2,1)S(1)} %get-tuple-element.57.kernel_ref, ...), custom_call_target="tpu_custom_call" | custom-call | flops 1 | bytes 1 | tf_op jit(solution)/shard_map/finish/pallas_call | solution.py:325
  (46 shorter events, 1.3 us)
Async XLA Ops:
  0.6 16.3 %copy-start.1 = (bf16[512,512]{1,0:T(8,128)(2,1)S(1)}, bf16[512,512]{1,0:T(8,128)(2,1)}, u32[]{:S(2)}) copy-start(bf16[512,512]{1,0:T(8,128)(2,1)} %pos_ref.6) | copy-start | bytes 1572868
  0.6 16.3 %copy-start.7 = (bf16[512]{0:T(512)(128)(2,1)S(1)}, bf16[512]{0:T(512)(128)(2,1)}, u32[]{:S(2)}) copy-start(bf16[512]{0:T(512)(128)(2,1)} %param.13) | copy-start | bytes 3076
  0.7 16.3 %copy-start.2 = (bf16[512,128]{1,0:T(8,128)(2,1)S(1)}, bf16[512,128]{1,0:T(8,128)(2,1)}, u32[]{:S(2)}) copy-start(bf16[512,128]{1,0:T(8,128)(2,1)} %coef_ref.7) | copy-start | bytes 393220
  0.7 27.0 %collective-permute-start.5 = (bf16[512,512]{1,0:T(8,128)(2,1)}, bf16[512,512]{1,0:T(8,128)(2,1)S(1)}, u32[]{:S(2)}, u32[]{:S(2)}) collective-permute-start(bf16[512,512]{1,0:T(8,128)(2,1)} %pos_ref.6), channel_id=1, source_target_pairs={{0,2},{1,3},{2,0},{3,1},{4,6},{5,7},{6,4},{7,5},{8,10},{9,11},{10,... | collective-permute-start | bytes 1572872 | tf_op jit(solution)/shard_map/ppermute | solution.py:20
  3.7 13.3 %copy-start.6 = (f32[128]{0:T(128)S(1)}, f32[128]{0:T(128)}, u32[]{:S(2)}) copy-start(f32[128]{0:T(128)} %param.10) | copy-start | bytes 1540
  3.7 27.0 %copy-start.4 = (f32[1024,128]{1,0:T(8,128)S(1)}, f32[1024,128]{1,0:T(8,128)}, u32[]{:S(2)}) copy-start(f32[1024,128]{1,0:T(8,128)} %refs_1_.3) | copy-start | bytes 1572868
  12.7 17.9 %copy-start = (bf16[1024,512]{1,0:T(8,128)(2,1)S(1)}, bf16[1024,512]{1,0:T(8,128)(2,1)}, u32[]{:S(2)}) copy-start(bf16[1024,512]{1,0:T(8,128)(2,1)} %refs_4_.1) | copy-start | bytes 3145732
  12.7 14.7 %collective-permute-start = (bf16[256,512]{1,0:T(8,128)(2,1)}, bf16[256,512]{1,0:T(8,128)(2,1)S(1)}, u32[]{:S(2)}, u32[]{:S(2)}) collective-permute-start(bf16[256,512]{1,0:T(8,128)(2,1)} %take.2.refs_0_.refs_13_.refs_1_), channel_id=1, source_target_pairs={{0,8},{4,12},{8,0},{12,4},{1,9},{5,13},{9,1},{13,5},{2,10},{6,14},... | collective-permute-start | bytes 786440 | tf_op jit(solution)/shard_map/ppermute | solution.py:20
  15.4 12.2 %collective-permute-start.2 = (bf16[256,512]{1,0:T(8,128)(2,1)}, bf16[256,512]{1,0:T(8,128)(2,1)S(1)}, u32[]{:S(2)}, u32[]{:S(2)}) collective-permute-start(bf16[256,512]{1,0:T(8,128)(2,1)} %take.2.refs_0_.refs_13_.refs_1_), channel_id=1, source_target_pairs={{0,4},{4,0},{8,12},{12,8},{1,5},{5,1},{9,13},{13,9},{2,6},{6,2},{1... | collective-permute-start | bytes 786440 | tf_op jit(solution)/shard_map/ppermute | solution.py:20
  17.2 13.4 %copy-start.3 = (f32[1024,128]{1,0:T(8,128)S(1)}, f32[1024,128]{1,0:T(8,128)}, u32[]{:S(2)}) copy-start(f32[1024,128]{1,0:T(8,128)} %refs_0_.3) | copy-start | bytes 1572868
  17.2 5.2 %collective-permute-start.6 = (bf16[144,512]{1,0:T(8,128)(2,1)S(1)}, bf16[144,512]{1,0:T(8,128)(2,1)S(1)}, u32[]{:S(2)}, u32[]{:S(2)}) collective-permute-start(bf16[144,512]{1,0:T(8,128)(2,1)S(1)} %get-tuple-element.38.refs_3_.refs_2_), channel_id=1, source_target_pairs={{0,2},{1,3},{2,0},{3,1},{4,6},{5,7},{6,4},{7,5},{8,10},{9,11},{10,... | collective-permute-start | bytes 442376 | tf_op jit(solution)/shard_map/ppermute | solution.py:20
  17.8 14.7 %collective-permute-start.3 = (bf16[512,512]{1,0:T(8,128)(2,1)S(1)}, bf16[512,512]{1,0:T(8,128)(2,1)S(1)}, u32[]{:S(2)}, u32[]{:S(2)}) collective-permute-start(bf16[512,512]{1,0:T(8,128)(2,1)S(1)} %copy-done.1), channel_id=1, source_target_pairs={{0,1},{1,0},{2,3},{3,2},{4,5},{5,4},{6,7},{7,6},{8,9},{9,8},{10,11... | collective-permute-start | bytes 1572872 | tf_op jit(solution)/shard_map/ppermute | solution.py:20
  27.6 1.4 %collective-permute-start.8 = (bf16[144,512]{1,0:T(8,128)(2,1)S(1)}, bf16[144,512]{1,0:T(8,128)(2,1)S(1)}, u32[]{:S(2)}, u32[]{:S(2)}) collective-permute-start(bf16[144,512]{1,0:T(8,128)(2,1)S(1)} %collective-permute-done.6.refs_7_.refs_6_), channel_id=1, source_target_pairs={{0,1},{1,0},{2,3},{3,2},{4,5},{5,4},{6,7},{7,6},{8,9},{9,8},{10,11... | collective-permute-start | bytes 442376 | tf_op jit(solution)/shard_map/ppermute | solution.py:20
  27.6 4.8 %collective-permute-start.7 = (bf16[512,512]{1,0:T(8,128)(2,1)S(1)}, bf16[512,512]{1,0:T(8,128)(2,1)S(1)}, u32[]{:S(2)}, u32[]{:S(2)}) collective-permute-start(bf16[512,512]{1,0:T(8,128)(2,1)S(1)} %collective-permute-done.5.refs_6_.refs_5_), channel_id=1, source_target_pairs={{0,1},{1,0},{2,3},{3,2},{4,5},{5,4},{6,7},{7,6},{8,9},{9,8},{10,11... | collective-permute-start | bytes 1572872 | tf_op jit(solution)/shard_map/ppermute | solution.py:20
  29.0 8.7 %collective-permute-start.9 = (bf16[512,512]{1,0:T(8,128)(2,1)S(1)}, bf16[512,512]{1,0:T(8,128)(2,1)S(1)}, u32[]{:S(2)}, u32[]{:S(2)}) collective-permute-start(bf16[512,512]{1,0:T(8,128)(2,1)S(1)} %constant_dynamic-update-slice_fusion.refs_14_.refs_2_), channel_id=1, source_target_pairs={{0,1},{1,0},{2,3},{3,2},{4,5},{5,4},{6,7},{7,6},{8,9},{9,8},{10,11... | collective-permute-start | bytes 1572872 | tf_op jit(solution)/shard_map/ppermute | solution.py:20
  29.1 8.6 %collective-permute-start.1 = (bf16[256,512]{1,0:T(8,128)(2,1)S(1)}, bf16[256,512]{1,0:T(8,128)(2,1)S(1)}, u32[]{:S(2)}, u32[]{:S(2)}) collective-permute-start(bf16[256,512]{1,0:T(8,128)(2,1)S(1)} %collective-permute-done.refs_0_), channel_id=1, source_target_pairs={{0,4},{4,0},{8,12},{12,8},{1,5},{5,1},{9,13},{13,9},{2,6},{6,2},{1... | collective-permute-start | bytes 786440 | tf_op jit(solution)/shard_map/ppermute | solution.py:20
  30.6 1.4 %collective-permute-start.4 = (bf16[144,512]{1,0:T(8,128)(2,1)S(1)}, bf16[144,512]{1,0:T(8,128)(2,1)S(1)}, u32[]{:S(2)}, u32[]{:S(2)}) collective-permute-start(bf16[144,512]{1,0:T(8,128)(2,1)S(1)} %get-tuple-element.38.refs_3_.refs_2_), channel_id=1, source_target_pairs={{0,1},{1,0},{2,3},{3,2},{4,5},{5,4},{6,7},{7,6},{8,9},{9,8},{10,11... | collective-permute-start | bytes 442376 | tf_op jit(solution)/shard_map/ppermute | solution.py:20
  31.9 19.5 %collective-permute-start.18 = (bf16[512,512]{1,0:T(8,128)(2,1)S(1)}, bf16[512,512]{1,0:T(8,128)(2,1)S(1)}, u32[]{:S(2)}, u32[]{:S(2)}) collective-permute-start(bf16[512,512]{1,0:T(8,128)(2,1)S(1)} %constant_dynamic-update-slice_fusion.refs_14_.refs_2_), channel_id=1, source_target_pairs={{0,2},{1,3},{2,0},{3,1},{4,6},{5,7},{6,4},{7,5},{8,10},{9,11},{10,... | collective-permute-start | bytes 1572872 | tf_op jit(solution)/shard_map/ppermute | solution.py:20
  34.7 10.1 %collective-permute-start.10 = (f32[256,128]{1,0:T(8,128)S(1)}, f32[256,128]{1,0:T(8,128)S(1)}, u32[]{:S(2)}, u32[]{:S(2)}) collective-permute-start(f32[256,128]{1,0:T(8,128)S(1)} %get-tuple-element.41), channel_id=1, source_target_pairs={{0,8},{4,12},{8,0},{12,4},{1,9},{5,13},{9,1},{13,5},{2,10},{6,14},... | collective-permute-start | bytes 393224 | tf_op jit(solution)/shard_map/ppermute | solution.py:20
  37.1 7.7 %copy-start.5 = (bf16[256,512]{1,0:T(8,128)(2,1)S(1)}, bf16[256,512]{1,0:T(8,128)(2,1)}, u32[]{:S(2)}) copy-start(bf16[256,512]{1,0:T(8,128)(2,1)} %take.2.refs_0_.refs_13_.refs_1_) | copy-start | bytes 786436
  37.1 7.7 %collective-permute-start.11 = (f32[256,128]{1,0:T(8,128)S(1)}, f32[256,128]{1,0:T(8,128)S(1)}, u32[]{:S(2)}, u32[]{:S(2)}) collective-permute-start(f32[256,128]{1,0:T(8,128)S(1)} %get-tuple-element.42), channel_id=1, source_target_pairs={{0,4},{4,0},{8,12},{12,8},{1,5},{5,1},{9,13},{13,9},{2,6},{6,2},{1... | collective-permute-start | bytes 393224 | tf_op jit(solution)/shard_map/ppermute | solution.py:20
  39.0 12.4 %collective-permute-start.12 = (f32[256,128]{1,0:T(8,128)S(1)}, f32[256,128]{1,0:T(8,128)S(1)}, u32[]{:S(2)}, u32[]{:S(2)}) collective-permute-start(f32[256,128]{1,0:T(8,128)S(1)} %forward.3), channel_id=1, source_target_pairs={{0,12},{4,8},{8,4},{12,0},{1,13},{5,9},{9,5},{13,1},{2,14},{6,10},... | collective-permute-start | bytes 393224 | tf_op jit(solution)/shard_map/ppermute | solution.py:20
  47.1 13.3 %collective-permute-start.19 = (bf16[256,512]{1,0:T(8,128)(2,1)S(1)}, bf16[256,512]{1,0:T(8,128)(2,1)S(1)}, u32[]{:S(2)}, u32[]{:S(2)}) collective-permute-start(bf16[256,512]{1,0:T(8,128)(2,1)S(1)} %collective-permute-done.1.refs_0_.refs_15_.refs_3_), channel_id=1, source_target_pairs={{0,2},{1,3},{2,0},{3,1},{4,6},{5,7},{6,4},{7,5},{8,10},{9,11},{10,... | collective-permute-start | bytes 786440 | tf_op jit(solution)/shard_map/ppermute | solution.py:20
  51.4 10.9 %collective-permute-start.20 = (bf16[512,512]{1,0:T(8,128)(2,1)S(1)}, bf16[512,512]{1,0:T(8,128)(2,1)S(1)}, u32[]{:S(2)}, u32[]{:S(2)}) collective-permute-start(bf16[512,512]{1,0:T(8,128)(2,1)S(1)} %collective-permute-done.18.refs_10_.refs_2_), channel_id=1, source_target_pairs={{0,1},{1,0},{2,3},{3,2},{4,5},{5,4},{6,7},{7,6},{8,9},{9,8},{10,11... | collective-permute-start | bytes 1572872 | tf_op jit(solution)/shard_map/ppermute | solution.py:20
  51.5 5.6 %collective-permute-start.13 = (bf16[256,128]{1,0:T(8,128)(2,1)S(1)}, bf16[256,128]{1,0:T(8,128)(2,1)S(1)}, u32[]{:S(2)}, u32[]{:S(2)}) collective-permute-start(bf16[256,128]{1,0:T(8,128)(2,1)S(1)} %cotangent.1), channel_id=1, source_target_pairs={{0,4},{4,0},{8,12},{12,8},{1,5},{5,1},{9,13},{13,9},{2,6},{6,2},{1... | collective-permute-start | bytes 196616 | tf_op jit(solution)/shard_map/ppermute | solution.py:20
  51.6 8.7 %collective-permute-start.14 = (bf16[256,128]{1,0:T(8,128)(2,1)S(1)}, bf16[256,128]{1,0:T(8,128)(2,1)S(1)}, u32[]{:S(2)}, u32[]{:S(2)}) collective-permute-start(bf16[256,128]{1,0:T(8,128)(2,1)S(1)} %cotangent.1), channel_id=1, source_target_pairs={{0,8},{4,12},{8,0},{12,4},{1,9},{5,13},{9,1},{13,5},{2,10},{6,14},... | collective-permute-start | bytes 196616 | tf_op jit(solution)/shard_map/ppermute | solution.py:20
  52.7 7.6 %collective-permute-start.15 = (bf16[256,128]{1,0:T(8,128)(2,1)S(1)}, bf16[256,128]{1,0:T(8,128)(2,1)S(1)}, u32[]{:S(2)}, u32[]{:S(2)}) collective-permute-start(bf16[256,128]{1,0:T(8,128)(2,1)S(1)} %cotangent.1), channel_id=1, source_target_pairs={{0,12},{4,8},{8,4},{12,0},{1,13},{5,9},{9,5},{13,1},{2,14},{6,10},... | collective-permute-start | bytes 196616 | tf_op jit(solution)/shard_map/ppermute | solution.py:20
  57.2 3.8 %collective-permute-start.16 = (bf16[256,512]{1,0:T(8,128)(2,1)S(1)}, bf16[256,512]{1,0:T(8,128)(2,1)S(1)}, u32[]{:S(2)}, u32[]{:S(2)}) collective-permute-start(bf16[256,512]{1,0:T(8,128)(2,1)S(1)} %collective-permute-done.1.refs_0_.refs_15_.refs_3_), channel_id=1, source_target_pairs={{0,1},{1,0},{2,3},{3,2},{4,5},{5,4},{6,7},{7,6},{8,9},{9,8},{10,11... | collective-permute-start | bytes 786440 | tf_op jit(solution)/shard_map/ppermute | solution.py:20
  60.3 1.6 %collective-permute-start.17 = (bf16[1024,128]{1,0:T(8,128)(2,1)S(1)}, bf16[1024,128]{1,0:T(8,128)(2,1)S(1)}, u32[]{:S(2)}, u32[]{:S(2)}) collective-permute-start(bf16[1024,128]{1,0:T(8,128)(2,1)S(1)} %pad_maximum_fusion.refs_4_), channel_id=1, source_target_pairs={{0,1},{1,0},{2,3},{3,2},{4,5},{5,4},{6,7},{7,6},{8,9},{9,8},{10,11... | collective-permute-start | bytes 786440 | tf_op jit(solution)/shard_map/ppermute | solution.py:20
  60.4 1.9 %collective-permute-start.21 = (bf16[256,512]{1,0:T(8,128)(2,1)S(1)}, bf16[256,512]{1,0:T(8,128)(2,1)S(1)}, u32[]{:S(2)}, u32[]{:S(2)}) collective-permute-start(bf16[256,512]{1,0:T(8,128)(2,1)S(1)} %collective-permute-done.19.refs_11_.refs_3_), channel_id=1, source_target_pairs={{0,1},{1,0},{2,3},{3,2},{4,5},{5,4},{6,7},{7,6},{8,9},{9,8},{10,11... | collective-permute-start | bytes 786440 | tf_op jit(solution)/shard_map/ppermute | solution.py:20
  60.9 8.3 %collective-permute-start.22 = (bf16[1024,128]{1,0:T(8,128)(2,1)S(1)}, bf16[1024,128]{1,0:T(8,128)(2,1)S(1)}, u32[]{:S(2)}, u32[]{:S(2)}) collective-permute-start(bf16[1024,128]{1,0:T(8,128)(2,1)S(1)} %pad_maximum_fusion.refs_4_), channel_id=1, source_target_pairs={{0,2},{1,3},{2,0},{3,1},{4,6},{5,7},{6,4},{7,5},{8,10},{9,11},{10,... | collective-permute-start | bytes 786440 | tf_op jit(solution)/shard_map/ppermute | solution.py:20
  69.2 1.5 %collective-permute-start.23 = (bf16[1024,128]{1,0:T(8,128)(2,1)S(1)}, bf16[1024,128]{1,0:T(8,128)(2,1)S(1)}, u32[]{:S(2)}, u32[]{:S(2)}) collective-permute-start(bf16[1024,128]{1,0:T(8,128)(2,1)S(1)} %collective-permute-done.22.refs_4_), channel_id=1, source_target_pairs={{0,1},{1,0},{2,3},{3,2},{4,5},{5,4},{6,7},{7,6},{8,9},{9,8},{10,11... | collective-permute-start | bytes 786440 | tf_op jit(solution)/shard_map/ppermute | solution.py:20

commit v8 on v7

--- a/solution.py
+++ b/solution.py
@@ -83,7 +83,7 @@
     )(center_pos, coefficients, spread.reshape(1, n), delta.reshape(1, -1))
 
 
-def take(arrays, offsets, piece, space=VMEM):
+def take(arrays, offsets, piece):
     def body(*refs):
         ins, outs, sems = refs[: len(arrays)], refs[len(arrays) : -1], refs[-1]
         made = []
@@ -98,9 +98,9 @@
         body,
         out_shape=tuple(jax.ShapeDtypeStruct((piece, a.shape[1]), a.dtype) for a in arrays),
         in_specs=[HBM] * len(arrays),
-        out_specs=(space,) * len(arrays),
+        out_specs=(VMEM,) * len(arrays),
         scratch_shapes=[pltpu.SemaphoreType.DMA((len(arrays),))],
-        compiler_params=params(16 if space is VMEM else 62),
+        compiler_params=params(16),
         cost_estimate=BRIEF,
         name="take",
     )(*arrays)
@@ -346,7 +346,7 @@
         n, out_width = coefficients.shape
         piece = n_rows // nc
 
-        (own,) = take([train_points], [0], piece, HBM)
+        own = lax.dynamic_slice_in_dim(train_points, lax.axis_index("centers") * piece, piece)
 
         layer = {0: own}
         for dz in range(2, nz, 2):
@@ -399,16 +399,23 @@
             [[local[0], early[0], late[0]]],
         )
         for d in range(2, nc, 2):
-            late[d] = swap(after(late[0], parts[0]), "centers", nc, d)
+            late[d] = swap(after(late[0], last, *soon), "centers", nc, d)
             early[d + 1] = swap(after(early[d], parts[0]), "centers", nc, 1)
         late[1] = swap(after(late[0], parts[0]), "centers", nc, 1)
         cot = cotangent([parts[0], *received], saved, target, delta)
 
-        far = [swap(cot, "points", nz, dz) for dz in range(1, nz)]
-        cots = {0: jnp.concatenate([cot, *far])}
-        for d in range(2, nc, 2):
-            cots[d] = swap(cots[0], "centers", nc, d)
-            late[d + 1] = swap(after(late[d], far[0]), "centers", nc, 1)
+        far = {dz: swap(cot, "points", nz, dz) for dz in range(2, nz, 2)}
+        held = after(cot, *(late[d] for d in range(2, nc, 2)))
+        far[1] = swap(held, "points", nz, 1)
+        far.update({dz: swap(far[dz - 1], "points", nz, 1) for dz in range(3, nz, 2)})
+        ahead = {d: swap(cot, "centers", nc, d) for d in range(2, nc, 2)}
+        far[1] = after(far[1], *ahead.values())
+        far = jnp.concatenate([far[dz] for dz in range(1, nz)])
+        cots = {0: jnp.concatenate([cot, far])}
+        across = {}
+        for d in range(2, nc, 2):
+            across[d] = [ahead[d], swap(far, "centers", nc, d)]
+            late[d + 1] = swap(after(late[d], far), "centers", nc, 1)
         cots[1] = swap(cots[0], "centers", nc, 1)
 
         points = {d: [local[d], early[d], late[d]] for d in range(nc)}
@@ -419,7 +426,7 @@
         for d in range(4, nc):
             kernels[d] = own_kernel(center_pos, spread, points[d])
         for d in range(2, nc, 2):
-            cots[d] = after(cots[d], sums[0])
+            cots[d] = jnp.concatenate([after(a, sums[0]) for a in across[d]])
             cots[d + 1] = swap(cots[d], "centers", nc, 1)
         for d in range(2, nc - 1):
             group = (kernels[d], points[d], cots[d])

time: 73.1 us -> 65.7 us (0.90)
  Pallas kernels: 24.7 us -> 15.8 us
  starting transfers between devices: 27.8 us -> 22.4 us
  local copies, waits for them, and re-layouts: 0.08 us -> 4.46 us
  waiting for transfers between devices: 19.6 us -> 21.9 us
    pallas_call x2 -> x1, Pallas kernels: 9.51 us -> 0.42 us  [take(): pl.pallas_call(body, out_shape=tuple((jax.ShapeDtypeStruct((piece, a.shap...]
    ppermute x24 -> x25, starting transfers between devices: 27.8 us -> 22.4 us  [swap(): return lax.ppermute(a, axis, [(i, i ^ d) for i in range(size)])]
    unnamed x17 -> x18, local copies, waits for them, and re-layouts: 0.05 us -> 2.66 us
    ppermute x24 -> x25, waiting for transfers between devices: 19.6 us -> 21.9 us  [swap(): return lax.ppermute(a, axis, [(i, i ^ d) for i in range(size)])]
    dynamic_slice x0 -> x1, local copies, waits for them, and re-layouts: none -> 1.06 us  [per_device(): lax.dynamic_slice_in_dim(train_points, lax.axis_index('centers') * piece,...]
  transfers between devices with their start and end apart: 24 -> 25, of which waited for: 12 -> 10; matrix products, arithmetic and copies ran while one was open for 0% -> 3% of each run, Pallas kernels for 31% -> 21%
where the time goes in v8:
time: 65.7 us; the launch traced here: 65.4 us
  starting transfers between devices  22.4 us (34%)
  waiting for transfers between devices  21.9 us (33%)
  Pallas kernels  15.8 us (24%)
  local copies, waits for them, and re-layouts  4.46 us (7%)
  between operations  0.83 us (1%)
    ppermute x25, starting transfers between devices, swap(): return lax.ppermute(a, axis, [(i, i ^ d) for i in range(size)])  22.4 us
    ppermute x25, waiting for transfers between devices, swap(): return lax.ppermute(a, axis, [(i, i ^ d) for i in range(size)])  21.9 us
    pallas_call x2, Pallas kernels, backward(): pl.pallas_call(body, out_shape=tuple((jax.ShapeDtypeStruct((n, width), F3...  7 us
    pallas_call x2, Pallas kernels, forward(): pl.pallas_call(body, out_shape=tuple((jax.ShapeDtypeStruct((count, out_wi...  3.55 us
    unnamed x18, local copies, waits for them, and re-layouts  2.66 us
    pallas_call x1, Pallas kernels, finish(): pl.pallas_call(body, out_shape=tuple((jax.ShapeDtypeStruct((n, width), F3...  2.32 us
    pallas_call x1, Pallas kernels, own_rows(): pl.pallas_call(body, out_shape=(jax.ShapeDtypeStruct((rows.shape[0], out_...  2.27 us
  transfers between devices with their start and end apart: 25, of which 10 were waited for; matrix products, arithmetic and copies ran while one was open for 3% of the time, Pallas kernels for 21%

profile of v8, /device:TPU:0, one launch (start us, length us, event | category | flops | bytes accessed | tf_op | source)
XLA Modules:
  0.0 65.4 jit_solution(12620298588031254512)
XLA Ops:
  0.6 3.0 %collective-permute-start.5 = (bf16[512,512]{1,0:T(8,128)(2,1)}, bf16[512,512]{1,0:T(8,128)(2,1)S(1)}, u32[]{:S(2)}, u32[]{:S(2)}) collective-permute-start(bf16[512,512]{1,0:T(8,128)(2,1)} %pos_ref.6), channel_id=1, source_target_pairs={{0,2},{1,3},{2,0},{3,1},{4,6},{5,7},{6,4},{7,5},{8,10},{9,11},{10,... | collective-permute-start | bytes 1572872 | tf_op jit(solution)/shard_map/ppermute | solution.py:20
  3.6 1.1 %constant_dynamic-slice_fusion.refs_0_.refs_13_.refs_1_ = bf16[256,512]{1,0:T(8,128)(2,1)S(1)} fusion(bf16[1024,512]{1,0:T(8,128)(2,1)} %refs_4_.1, s32[]{:T(128)S(6)} %select_n.3), kind=kLoop, calls=%fused_computation.8 | loop fusion | bytes 524292 | tf_op jit(solution)/shard_map/dynamic_slice | solution.py:349
  4.7 1.6 %collective-permute-start.2 = (bf16[256,512]{1,0:T(8,128)(2,1)S(1)}, bf16[256,512]{1,0:T(8,128)(2,1)S(1)}, u32[]{:S(2)}, u32[]{:S(2)}) collective-permute-start(bf16[256,512]{1,0:T(8,128)(2,1)S(1)} %constant_dynamic-slice_fusion.refs_0_.refs_13_.refs_1_), channel_id=1, source_target_pairs={{0,4},{4,0},{8,12},{12,8},{1,5},{5,1},{9,13},{13,9},{2,6},{6,2},{1... | collective-permute-start | bytes 786440 | tf_op jit(solution)/shard_map/ppermute | solution.py:20
  6.3 2.6 %collective-permute-start = (bf16[256,512]{1,0:T(8,128)(2,1)S(1)}, bf16[256,512]{1,0:T(8,128)(2,1)S(1)}, u32[]{:S(2)}, u32[]{:S(2)}) collective-permute-start(bf16[256,512]{1,0:T(8,128)(2,1)S(1)} %constant_dynamic-slice_fusion.refs_0_.refs_13_.refs_1_), channel_id=1, source_target_pairs={{0,8},{4,12},{8,0},{12,4},{1,9},{5,13},{9,1},{13,5},{2,10},{6,14},... | collective-permute-start | bytes 786440 | tf_op jit(solution)/shard_map/ppermute | solution.py:20
  8.9 0.7 %reshape.12.spread_ref.refs_12_ = bf16[1,512]{1,0:T(2,128)(2,1)S(1)} reshape(bf16[512]{0:T(512)(128)(2,1)} %param.13) | data formatting | bytes 2048 | tf_op jit(solution)/shard_map/reshape | solution.py:324
  9.6 0.9 %copy-done.2 = bf16[512,128]{1,0:T(8,128)(2,1)S(1)} copy-done((bf16[512,128]{1,0:T(8,128)(2,1)S(1)}, bf16[512,128]{1,0:T(8,128)(2,1)}, u32[]{:S(2)}) %copy-start.2) | copy-done | bytes 131096
  10.5 0.7 copy-done.6
  11.4 0.6 collective-permute-start.6
  12.0 6.9 %collective-permute-done.6.refs_7_.refs_6_ = bf16[144,512]{1,0:T(8,128)(2,1)S(1)} collective-permute-done((bf16[144,512]{1,0:T(8,128)(2,1)S(1)}, bf16[144,512]{1,0:T(8,128)(2,1)S(1)}, u32[]{:S(2)}, u32[]{:S(2)}) %collective-permute-start.6) | collective-permute-done | bytes 147488 | tf_op jit(solution)/shard_map/ppermute | solution.py:20
  18.9 1.5 %collective-permute-done.refs_0_ = bf16[256,512]{1,0:T(8,128)(2,1)S(1)} collective-permute-done((bf16[256,512]{1,0:T(8,128)(2,1)S(1)}, bf16[256,512]{1,0:T(8,128)(2,1)S(1)}, u32[]{:S(2)}, u32[]{:S(2)}) %collective-permute-start) | collective-permute-done | bytes 262176 | tf_op jit(solution)/shard_map/ppermute | solution.py:20
  20.4 0.6 collective-permute-start.7
  21.0 0.7 %collective-permute-done.8.refs_9_.refs_8_ = bf16[144,512]{1,0:T(8,128)(2,1)S(1)} collective-permute-done((bf16[144,512]{1,0:T(8,128)(2,1)S(1)}, bf16[144,512]{1,0:T(8,128)(2,1)S(1)}, u32[]{:S(2)}, u32[]{:S(2)}) %collective-permute-start.8) | collective-permute-done | bytes 147488 | tf_op jit(solution)/shard_map/ppermute | solution.py:20
  22.5 1.0 %copy-done.5 = f32[1024,128]{1,0:T(8,128)S(1)} copy-done((f32[1024,128]{1,0:T(8,128)S(1)}, f32[1024,128]{1,0:T(8,128)}, u32[]{:S(2)}) %copy-start.5) | copy-done | bytes 524312
  23.9 1.5 %collective-permute-start.20 = (bf16[512,512]{1,0:T(8,128)(2,1)S(1)}, bf16[512,512]{1,0:T(8,128)(2,1)S(1)}, u32[]{:S(2)}, u32[]{:S(2)}) collective-permute-start(bf16[512,512]{1,0:T(8,128)(2,1)S(1)} %constant_dynamic-update-slice_fusion.refs_14_.refs_2_), channel_id=1, source_target_pairs={{0,2},{1,3},{2,0},{3,1},{4,6},{5,7},{6,4},{7,5},{8,10},{9,11},{10,... | collective-permute-start | bytes 1572872 | tf_op jit(solution)/shard_map/ppermute | solution.py:20
  25.4 2.2 %forward.2 = (f32[256,128]{1,0:T(8,128)S(1)}, f32[256,128]{1,0:T(8,128)S(1)}) custom-call(bf16[256,512]{1,0:T(8,128)(2,1)S(1)} %collective-permute-done.refs_0_, bf16[256,512]{1,0:T(8,128)(2,1)S(1)} %collective-permute-done.2.refs_1_, bf16[512,512]{1,0:T(8,128)(2,1)S(1)} %copy-done.1, bf16[144,512]{1,0:T(8,128)(2,1)S(1)} %get-tuple-element.42.refs_3_.refs_2_, ...), custom_call_target="tpu_custom_call" | custom-call | flops 1 | bytes 1 | tf_op jit(solution)/shard_map/forward/pallas_call | solution.py:160
  27.7 2.7 %collective-permute-start.10 = (f32[256,128]{1,0:T(8,128)S(1)}, f32[256,128]{1,0:T(8,128)S(1)}, u32[]{:S(2)}, u32[]{:S(2)}) collective-permute-start(f32[256,128]{1,0:T(8,128)S(1)} %get-tuple-element.45), channel_id=1, source_target_pairs={{0,8},{4,12},{8,0},{12,4},{1,9},{5,13},{9,1},{13,5},{2,10},{6,14},... | collective-permute-start | bytes 393224 | tf_op jit(solution)/shard_map/ppermute | solution.py:20
  30.8 1.3 %forward.3 = f32[256,128]{1,0:T(8,128)S(1)} custom-call(bf16[256,512]{1,0:T(8,128)(2,1)S(1)} %collective-permute-done.1.refs_0_.refs_15_.refs_3_, bf16[512,512]{1,0:T(8,128)(2,1)S(1)} %copy-done.1, bf16[144,512]{1,0:T(8,128)(2,1)S(1)} %get-tuple-element.42.refs_3_.refs_2_, bf16[512,512]{1,0:T(8,128)(2,1)S(1)} %collective-permute-done.3.refs_4_.refs_3_, ...), custom_call_target="tpu_custom_call" | custom-call | flops 17179869184 | bytes 1048576 | tf_op jit(solution)/shard_map/forward/pallas_call | solution.py:160
  32.1 2.3 %collective-permute-start.12 = (f32[256,128]{1,0:T(8,128)S(1)}, f32[256,128]{1,0:T(8,128)S(1)}, u32[]{:S(2)}, u32[]{:S(2)}) collective-permute-start(f32[256,128]{1,0:T(8,128)S(1)} %forward.3), channel_id=1, source_target_pairs={{0,12},{4,8},{8,4},{12,0},{1,13},{5,9},{9,5},{13,1},{2,14},{6,10},... | collective-permute-start | bytes 393224 | tf_op jit(solution)/shard_map/ppermute | solution.py:20
  34.4 3.7 %collective-permute-done.10.refs_9_ = f32[256,128]{1,0:T(8,128)S(1)} collective-permute-done((f32[256,128]{1,0:T(8,128)S(1)}, f32[256,128]{1,0:T(8,128)S(1)}, u32[]{:S(2)}, u32[]{:S(2)}) %collective-permute-start.10) | collective-permute-done | bytes 131104 | tf_op jit(solution)/shard_map/ppermute | solution.py:20
  38.1 2.9 %collective-permute-done.11.refs_10_ = f32[256,128]{1,0:T(8,128)S(1)} collective-permute-done((f32[256,128]{1,0:T(8,128)S(1)}, f32[256,128]{1,0:T(8,128)S(1)}, u32[]{:S(2)}, u32[]{:S(2)}) %collective-permute-start.11) | collective-permute-done | bytes 131104 | tf_op jit(solution)/shard_map/ppermute | solution.py:20
  41.0 2.3 %own_rows.1 = (f32[256,128]{1,0:T(8,128)S(1)}, bf16[512,1024]{1,0:T(8,128)(2,1)S(1)}) custom-call(bf16[256,512]{1,0:T(8,128)(2,1)S(1)} %constant_dynamic-slice_fusion.refs_0_.refs_13_.refs_1_, bf16[512,512]{1,0:T(8,128)(2,1)S(1)} %copy-done.1, bf16[144,512]{1,0:T(8,128)(2,1)S(1)} %get-tuple-element.42.refs_3_.refs_2_, ...), custom_call_target="tpu_custom_call" | custom-call | flops 17179869184 | bytes 1048576 | tf_op jit(solution)/shard_map/own_rows/pallas_call | solution.py:207
  43.4 1.0 %collective-permute-start.16 = (bf16[256,128]{1,0:T(8,128)(2,1)S(1)}, bf16[256,128]{1,0:T(8,128)(2,1)S(1)}, u32[]{:S(2)}, u32[]{:S(2)}) collective-permute-start(bf16[256,128]{1,0:T(8,128)(2,1)S(1)} %cotangent.1), channel_id=1, source_target_pairs={{0,8},{4,12},{8,0},{12,4},{1,9},{5,13},{9,1},{13,5},{2,10},{6,14},... | collective-permute-start | bytes 196616 | tf_op jit(solution)/shard_map/ppermute | solution.py:20
  44.4 1.1 %collective-permute-start.15 = (bf16[256,128]{1,0:T(8,128)(2,1)S(1)}, bf16[256,128]{1,0:T(8,128)(2,1)S(1)}, u32[]{:S(2)}, u32[]{:S(2)}) collective-permute-start(bf16[256,128]{1,0:T(8,128)(2,1)S(1)} %cotangent.1), channel_id=1, source_target_pairs={{0,2},{1,3},{2,0},{3,1},{4,6},{5,7},{6,4},{7,5},{8,10},{9,11},{10,... | collective-permute-start | bytes 196616 | tf_op jit(solution)/shard_map/ppermute | solution.py:20
  45.5 2.5 %collective-permute-done.13.refs_11_.refs_3_ = bf16[256,512]{1,0:T(8,128)(2,1)S(1)} collective-permute-done((bf16[256,512]{1,0:T(8,128)(2,1)S(1)}, bf16[256,512]{1,0:T(8,128)(2,1)S(1)}, u32[]{:S(2)}, u32[]{:S(2)}) %collective-permute-start.13) | collective-permute-done | bytes 262176 | tf_op jit(solution)/shard_map/ppermute | solution.py:20
  49.0 1.6 %collective-permute-start.17 = (bf16[256,128]{1,0:T(8,128)(2,1)S(1)}, bf16[256,128]{1,0:T(8,128)(2,1)S(1)}, u32[]{:S(2)}, u32[]{:S(2)}) collective-permute-start(bf16[256,128]{1,0:T(8,128)(2,1)S(1)} %collective-permute-done.16), channel_id=1, source_target_pairs={{0,4},{4,0},{8,12},{12,8},{1,5},{5,1},{9,13},{13,9},{2,6},{6,2},{1... | collective-permute-start | bytes 196616 | tf_op jit(solution)/shard_map/ppermute | solution.py:20
  50.6 2.3 %collective-permute-done.14 = bf16[256,128]{1,0:T(8,128)(2,1)S(1)} collective-permute-done((bf16[256,128]{1,0:T(8,128)(2,1)S(1)}, bf16[256,128]{1,0:T(8,128)(2,1)S(1)}, u32[]{:S(2)}, u32[]{:S(2)}) %collective-permute-start.14) | collective-permute-done | bytes 65568 | tf_op jit(solution)/shard_map/ppermute | solution.py:20
  52.9 0.7 %collective-permute-done.17 = bf16[256,128]{1,0:T(8,128)(2,1)S(1)} collective-permute-done((bf16[256,128]{1,0:T(8,128)(2,1)S(1)}, bf16[256,128]{1,0:T(8,128)(2,1)S(1)}, u32[]{:S(2)}, u32[]{:S(2)}) %collective-permute-start.17) | collective-permute-done | bytes 65568 | tf_op jit(solution)/shard_map/ppermute | solution.py:20
  53.7 0.6 collective-permute-start.19
  54.3 1.5 %collective-permute-start.23 = (bf16[768,128]{1,0:T(8,128)(2,1)S(1)}, bf16[768,128]{1,0:T(8,128)(2,1)S(1)}, u32[]{:S(2)}, u32[]{:S(2)}) collective-permute-start(bf16[768,128]{1,0:T(8,128)(2,1)S(1)} %constant_dynamic-update-slice_fusion.2), channel_id=1, source_target_pairs={{0,2},{1,3},{2,0},{3,1},{4,6},{5,7},{6,4},{7,5},{8,10},{9,11},{10,... | collective-permute-start | bytes 589832 | tf_op jit(solution)/shard_map/ppermute | solution.py:20
  55.8 5.7 %backward.2 = (f32[512,512]{1,0:T(8,128)S(1)}, f32[512,128]{1,0:T(8,128)S(1)}, f32[512,128]{1,0:T(8,128)S(1)}, bf16[512,1024]{1,0:T(8,128)(2,1)S(1)}, bf16[512,1024]{1,0:T(8,128)(2,1)S(1)}) custom-call(bf16[512,512]{1,0:T(8,128)(2,1)S(1)} %copy-done.1, bf16[512,128]{1,0:T(8,128)(2,1)S(1)} %copy-done.3, bf16[1,512]{1,0:T(2,128)(2,1)S(1)} %reshape.12.spread_ref.refs_12_, ...), custom_call_target="tpu_custom_call" | custom-call | flops 17179869184 | bytes 1048576 | tf_op jit(solution)/shard_map/backward/pallas_call | solution.py:282
  61.6 1.3 %backward.3 = (f32[512,512]{1,0:T(8,128)S(1)}, f32[512,128]{1,0:T(8,128)S(1)}, f32[512,128]{1,0:T(8,128)S(1)}) custom-call(bf16[512,512]{1,0:T(8,128)(2,1)S(1)} %copy-done.1, bf16[512,128]{1,0:T(8,128)(2,1)S(1)} %copy-done.3, bf16[1,512]{1,0:T(2,128)(2,1)S(1)} %reshape.12.spread_ref.refs_12_, bf16[512,1024]{1,0:T(8,128)(2,1)S(1)} %get-tuple-element.68.refs_0_, ...), custom_call_target="tpu_custom_call" | custom-call | flops 1 | bytes 1 | tf_op jit(solution)/shard_map/backward/pallas_call | solution.py:282
  63.1 2.3 %finish.1 = (f32[512,512]{1,0:T(8,128)}, f32[512,128]{1,0:T(8,128)}) custom-call(bf16[512,512]{1,0:T(8,128)(2,1)S(1)} %copy-done.1, bf16[512,128]{1,0:T(8,128)(2,1)S(1)} %copy-done.3, bf16[1,512]{1,0:T(2,128)(2,1)S(1)} %reshape.12.spread_ref.refs_12_, bf16[512,1024]{1,0:T(8,128)(2,1)S(1)} %get-tuple-element.64.kernel_ref, ...), custom_call_target="tpu_custom_call" | custom-call | flops 1 | bytes 1 | tf_op jit(solution)/shard_map/finish/pallas_call | solution.py:325
  (51 shorter events, 3.3 us)
Async XLA Ops:
  0.6 9.0 %copy-start.1 = (bf16[512,512]{1,0:T(8,128)(2,1)S(1)}, bf16[512,512]{1,0:T(8,128)(2,1)}, u32[]{:S(2)}) copy-start(bf16[512,512]{1,0:T(8,128)(2,1)} %pos_ref.6) | copy-start | bytes 1572868
  0.6 19.8 %collective-permute-start.5 = (bf16[512,512]{1,0:T(8,128)(2,1)}, bf16[512,512]{1,0:T(8,128)(2,1)S(1)}, u32[]{:S(2)}, u32[]{:S(2)}) collective-permute-start(bf16[512,512]{1,0:T(8,128)(2,1)} %pos_ref.6), channel_id=1, source_target_pairs={{0,2},{1,3},{2,0},{3,1},{4,6},{5,7},{6,4},{7,5},{8,10},{9,11},{10,... | collective-permute-start | bytes 1572872 | tf_op jit(solution)/shard_map/ppermute | solution.py:20
  3.6 18.8 %copy-start = (bf16[1024,512]{1,0:T(8,128)(2,1)S(1)}, bf16[1024,512]{1,0:T(8,128)(2,1)}, u32[]{:S(2)}) copy-start(bf16[1024,512]{1,0:T(8,128)(2,1)} %refs_4_.1) | copy-start | bytes 3145732
  4.7 14.2 %collective-permute-start.2 = (bf16[256,512]{1,0:T(8,128)(2,1)S(1)}, bf16[256,512]{1,0:T(8,128)(2,1)S(1)}, u32[]{:S(2)}, u32[]{:S(2)}) collective-permute-start(bf16[256,512]{1,0:T(8,128)(2,1)S(1)} %constant_dynamic-slice_fusion.refs_0_.refs_13_.refs_1_), channel_id=1, source_target_pairs={{0,4},{4,0},{8,12},{12,8},{1,5},{5,1},{9,13},{13,9},{2,6},{6,2},{1... | collective-permute-start | bytes 786440 | tf_op jit(solution)/shard_map/ppermute | solution.py:20
  6.3 14.0 %collective-permute-start = (bf16[256,512]{1,0:T(8,128)(2,1)S(1)}, bf16[256,512]{1,0:T(8,128)(2,1)S(1)}, u32[]{:S(2)}, u32[]{:S(2)}) collective-permute-start(bf16[256,512]{1,0:T(8,128)(2,1)S(1)} %constant_dynamic-slice_fusion.refs_0_.refs_13_.refs_1_), channel_id=1, source_target_pairs={{0,8},{4,12},{8,0},{12,4},{1,9},{5,13},{9,1},{13,5},{2,10},{6,14},... | collective-permute-start | bytes 786440 | tf_op jit(solution)/shard_map/ppermute | solution.py:20
  9.6 0.9 %copy-start.2 = (bf16[512,128]{1,0:T(8,128)(2,1)S(1)}, bf16[512,128]{1,0:T(8,128)(2,1)}, u32[]{:S(2)}) copy-start(bf16[512,128]{1,0:T(8,128)(2,1)} %coef_ref.7) | copy-start | bytes 393220
  10.5 0.7 %copy-start.6 = (f32[128]{0:T(128)S(1)}, f32[128]{0:T(128)}, u32[]{:S(2)}) copy-start(f32[128]{0:T(128)} %param.10) | copy-start | bytes 1540
  11.4 11.1 %copy-start.4 = (f32[1024,128]{1,0:T(8,128)S(1)}, f32[1024,128]{1,0:T(8,128)}, u32[]{:S(2)}) copy-start(f32[1024,128]{1,0:T(8,128)} %refs_0_.1) | copy-start | bytes 1572868
  11.4 7.6 %collective-permute-start.6 = (bf16[144,512]{1,0:T(8,128)(2,1)S(1)}, bf16[144,512]{1,0:T(8,128)(2,1)S(1)}, u32[]{:S(2)}, u32[]{:S(2)}) collective-permute-start(bf16[144,512]{1,0:T(8,128)(2,1)S(1)} %get-tuple-element.42.refs_3_.refs_2_), channel_id=1, source_target_pairs={{0,2},{1,3},{2,0},{3,1},{4,6},{5,7},{6,4},{7,5},{8,10},{9,11},{10,... | collective-permute-start | bytes 442376 | tf_op jit(solution)/shard_map/ppermute | solution.py:20
  12.0 13.4 %collective-permute-start.3 = (bf16[512,512]{1,0:T(8,128)(2,1)S(1)}, bf16[512,512]{1,0:T(8,128)(2,1)S(1)}, u32[]{:S(2)}, u32[]{:S(2)}) collective-permute-start(bf16[512,512]{1,0:T(8,128)(2,1)S(1)} %copy-done.1), channel_id=1, source_target_pairs={{0,1},{1,0},{2,3},{3,2},{4,5},{5,4},{6,7},{7,6},{8,9},{9,8},{10,11... | collective-permute-start | bytes 1572872 | tf_op jit(solution)/shard_map/ppermute | solution.py:20
  20.4 1.4 %collective-permute-start.8 = (bf16[144,512]{1,0:T(8,128)(2,1)S(1)}, bf16[144,512]{1,0:T(8,128)(2,1)S(1)}, u32[]{:S(2)}, u32[]{:S(2)}) collective-permute-start(bf16[144,512]{1,0:T(8,128)(2,1)S(1)} %collective-permute-done.6.refs_7_.refs_6_), channel_id=1, source_target_pairs={{0,1},{1,0},{2,3},{3,2},{4,5},{5,4},{6,7},{7,6},{8,9},{9,8},{10,11... | collective-permute-start | bytes 442376 | tf_op jit(solution)/shard_map/ppermute | solution.py:20
  20.4 5.0 %collective-permute-start.7 = (bf16[512,512]{1,0:T(8,128)(2,1)S(1)}, bf16[512,512]{1,0:T(8,128)(2,1)S(1)}, u32[]{:S(2)}, u32[]{:S(2)}) collective-permute-start(bf16[512,512]{1,0:T(8,128)(2,1)S(1)} %collective-permute-done.5.refs_6_.refs_5_), channel_id=1, source_target_pairs={{0,1},{1,0},{2,3},{3,2},{4,5},{5,4},{6,7},{7,6},{8,9},{9,8},{10,11... | collective-permute-start | bytes 1572872 | tf_op jit(solution)/shard_map/ppermute | solution.py:20
  21.8 9.0 %collective-permute-start.9 = (bf16[512,512]{1,0:T(8,128)(2,1)S(1)}, bf16[512,512]{1,0:T(8,128)(2,1)S(1)}, u32[]{:S(2)}, u32[]{:S(2)}) collective-permute-start(bf16[512,512]{1,0:T(8,128)(2,1)S(1)} %constant_dynamic-update-slice_fusion.refs_14_.refs_2_), channel_id=1, source_target_pairs={{0,1},{1,0},{2,3},{3,2},{4,5},{5,4},{6,7},{7,6},{8,9},{9,8},{10,11... | collective-permute-start | bytes 1572872 | tf_op jit(solution)/shard_map/ppermute | solution.py:20
  21.9 8.9 %collective-permute-start.1 = (bf16[256,512]{1,0:T(8,128)(2,1)S(1)}, bf16[256,512]{1,0:T(8,128)(2,1)S(1)}, u32[]{:S(2)}, u32[]{:S(2)}) collective-permute-start(bf16[256,512]{1,0:T(8,128)(2,1)S(1)} %collective-permute-done.refs_0_), channel_id=1, source_target_pairs={{0,4},{4,0},{8,12},{12,8},{1,5},{5,1},{9,13},{13,9},{2,6},{6,2},{1... | collective-permute-start | bytes 786440 | tf_op jit(solution)/shard_map/ppermute | solution.py:20
  22.4 1.5 %collective-permute-start.4 = (bf16[144,512]{1,0:T(8,128)(2,1)S(1)}, bf16[144,512]{1,0:T(8,128)(2,1)S(1)}, u32[]{:S(2)}, u32[]{:S(2)}) collective-permute-start(bf16[144,512]{1,0:T(8,128)(2,1)S(1)} %get-tuple-element.42.refs_3_.refs_2_), channel_id=1, source_target_pairs={{0,1},{1,0},{2,3},{3,2},{4,5},{5,4},{6,7},{7,6},{8,9},{9,8},{10,11... | collective-permute-start | bytes 442376 | tf_op jit(solution)/shard_map/ppermute | solution.py:20
  22.5 1.0 %copy-start.5 = (f32[1024,128]{1,0:T(8,128)S(1)}, f32[1024,128]{1,0:T(8,128)}, u32[]{:S(2)}) copy-start(f32[1024,128]{1,0:T(8,128)} %refs_1_.3) | copy-start | bytes 1572868
  23.9 24.1 %collective-permute-start.20 = (bf16[512,512]{1,0:T(8,128)(2,1)S(1)}, bf16[512,512]{1,0:T(8,128)(2,1)S(1)}, u32[]{:S(2)}, u32[]{:S(2)}) collective-permute-start(bf16[512,512]{1,0:T(8,128)(2,1)S(1)} %constant_dynamic-update-slice_fusion.refs_14_.refs_2_), channel_id=1, source_target_pairs={{0,2},{1,3},{2,0},{3,1},{4,6},{5,7},{6,4},{7,5},{8,10},{9,11},{10,... | collective-permute-start | bytes 1572872 | tf_op jit(solution)/shard_map/ppermute | solution.py:20
  27.7 10.4 %collective-permute-start.10 = (f32[256,128]{1,0:T(8,128)S(1)}, f32[256,128]{1,0:T(8,128)S(1)}, u32[]{:S(2)}, u32[]{:S(2)}) collective-permute-start(f32[256,128]{1,0:T(8,128)S(1)} %get-tuple-element.45), channel_id=1, source_target_pairs={{0,8},{4,12},{8,0},{12,4},{1,9},{5,13},{9,1},{13,5},{2,10},{6,14},... | collective-permute-start | bytes 393224 | tf_op jit(solution)/shard_map/ppermute | solution.py:20
  30.3 10.7 %collective-permute-start.11 = (f32[256,128]{1,0:T(8,128)S(1)}, f32[256,128]{1,0:T(8,128)S(1)}, u32[]{:S(2)}, u32[]{:S(2)}) collective-permute-start(f32[256,128]{1,0:T(8,128)S(1)} %get-tuple-element.46), channel_id=1, source_target_pairs={{0,4},{4,0},{8,12},{12,8},{1,5},{5,1},{9,13},{13,9},{2,6},{6,2},{1... | collective-permute-start | bytes 393224 | tf_op jit(solution)/shard_map/ppermute | solution.py:20
  32.1 11.2 %collective-permute-start.12 = (f32[256,128]{1,0:T(8,128)S(1)}, f32[256,128]{1,0:T(8,128)S(1)}, u32[]{:S(2)}, u32[]{:S(2)}) collective-permute-start(f32[256,128]{1,0:T(8,128)S(1)} %forward.3), channel_id=1, source_target_pairs={{0,12},{4,8},{8,4},{12,0},{1,13},{5,9},{9,5},{13,1},{2,14},{6,10},... | collective-permute-start | bytes 393224 | tf_op jit(solution)/shard_map/ppermute | solution.py:20
  41.0 7.1 %collective-permute-start.13 = (bf16[256,512]{1,0:T(8,128)(2,1)S(1)}, bf16[256,512]{1,0:T(8,128)(2,1)S(1)}, u32[]{:S(2)}, u32[]{:S(2)}) collective-permute-start(bf16[256,512]{1,0:T(8,128)(2,1)S(1)} %collective-permute-done.1.refs_0_.refs_15_.refs_3_), channel_id=1, source_target_pairs={{0,2},{1,3},{2,0},{3,1},{4,6},{5,7},{6,4},{7,5},{8,10},{9,11},{10,... | collective-permute-start | bytes 786440 | tf_op jit(solution)/shard_map/ppermute | solution.py:20
  43.4 5.6 %collective-permute-start.16 = (bf16[256,128]{1,0:T(8,128)(2,1)S(1)}, bf16[256,128]{1,0:T(8,128)(2,1)S(1)}, u32[]{:S(2)}, u32[]{:S(2)}) collective-permute-start(bf16[256,128]{1,0:T(8,128)(2,1)S(1)} %cotangent.1), channel_id=1, source_target_pairs={{0,8},{4,12},{8,0},{12,4},{1,9},{5,13},{9,1},{13,5},{2,10},{6,14},... | collective-permute-start | bytes 196616 | tf_op jit(solution)/shard_map/ppermute | solution.py:20
  44.4 6.2 %collective-permute-start.15 = (bf16[256,128]{1,0:T(8,128)(2,1)S(1)}, bf16[256,128]{1,0:T(8,128)(2,1)S(1)}, u32[]{:S(2)}, u32[]{:S(2)}) collective-permute-start(bf16[256,128]{1,0:T(8,128)(2,1)S(1)} %cotangent.1), channel_id=1, source_target_pairs={{0,2},{1,3},{2,0},{3,1},{4,6},{5,7},{6,4},{7,5},{8,10},{9,11},{10,... | collective-permute-start | bytes 196616 | tf_op jit(solution)/shard_map/ppermute | solution.py:20
  48.1 4.8 %collective-permute-start.14 = (bf16[256,128]{1,0:T(8,128)(2,1)S(1)}, bf16[256,128]{1,0:T(8,128)(2,1)S(1)}, u32[]{:S(2)}, u32[]{:S(2)}) collective-permute-start(bf16[256,128]{1,0:T(8,128)(2,1)S(1)} %cotangent.1), channel_id=1, source_target_pairs={{0,4},{4,0},{8,12},{12,8},{1,5},{5,1},{9,13},{13,9},{2,6},{6,2},{1... | collective-permute-start | bytes 196616 | tf_op jit(solution)/shard_map/ppermute | solution.py:20
  48.1 7.7 %collective-permute-start.18 = (bf16[256,512]{1,0:T(8,128)(2,1)S(1)}, bf16[256,512]{1,0:T(8,128)(2,1)S(1)}, u32[]{:S(2)}, u32[]{:S(2)}) collective-permute-start(bf16[256,512]{1,0:T(8,128)(2,1)S(1)} %collective-permute-done.1.refs_0_.refs_15_.refs_3_), channel_id=1, source_target_pairs={{0,1},{1,0},{2,3},{3,2},{4,5},{5,4},{6,7},{7,6},{8,9},{9,8},{10,11... | collective-permute-start | bytes 786440 | tf_op jit(solution)/shard_map/ppermute | solution.py:20
  48.1 7.7 %collective-permute-start.21 = (bf16[512,512]{1,0:T(8,128)(2,1)S(1)}, bf16[512,512]{1,0:T(8,128)(2,1)S(1)}, u32[]{:S(2)}, u32[]{:S(2)}) collective-permute-start(bf16[512,512]{1,0:T(8,128)(2,1)S(1)} %collective-permute-done.20.refs_10_.refs_2_), channel_id=1, source_target_pairs={{0,1},{1,0},{2,3},{3,2},{4,5},{5,4},{6,7},{7,6},{8,9},{9,8},{10,11... | collective-permute-start | bytes 1572872 | tf_op jit(solution)/shard_map/ppermute | solution.py:20
  49.0 4.6 %collective-permute-start.17 = (bf16[256,128]{1,0:T(8,128)(2,1)S(1)}, bf16[256,128]{1,0:T(8,128)(2,1)S(1)}, u32[]{:S(2)}, u32[]{:S(2)}) collective-permute-start(bf16[256,128]{1,0:T(8,128)(2,1)S(1)} %collective-permute-done.16), channel_id=1, source_target_pairs={{0,4},{4,0},{8,12},{12,8},{1,5},{5,1},{9,13},{13,9},{2,6},{6,2},{1... | collective-permute-start | bytes 196616 | tf_op jit(solution)/shard_map/ppermute | solution.py:20
  53.6 2.2 %copy-start.3 = (bf16[512,128]{1,0:T(8,128)(2,1)S(1)}, bf16[512,128]{1,0:T(8,128)(2,1)}, u32[]{:S(2)}) copy-start(bf16[512,128]{1,0:T(8,128)(2,1)} %coef_ref.7) | copy-start | bytes 393220
  53.6 2.1 %collective-permute-start.22 = (bf16[256,512]{1,0:T(8,128)(2,1)S(1)}, bf16[256,512]{1,0:T(8,128)(2,1)S(1)}, u32[]{:S(2)}, u32[]{:S(2)}) collective-permute-start(bf16[256,512]{1,0:T(8,128)(2,1)S(1)} %collective-permute-done.13.refs_11_.refs_3_), channel_id=1, source_target_pairs={{0,1},{1,0},{2,3},{3,2},{4,5},{5,4},{6,7},{7,6},{8,9},{9,8},{10,11... | collective-permute-start | bytes 786440 | tf_op jit(solution)/shard_map/ppermute | solution.py:20
  53.7 2.0 %collective-permute-start.19 = (bf16[1024,128]{1,0:T(8,128)(2,1)S(1)}, bf16[1024,128]{1,0:T(8,128)(2,1)S(1)}, u32[]{:S(2)}, u32[]{:S(2)}) collective-permute-start(bf16[1024,128]{1,0:T(8,128)(2,1)S(1)} %pad_maximum_fusion.refs_4_), channel_id=1, source_target_pairs={{0,1},{1,0},{2,3},{3,2},{4,5},{5,4},{6,7},{7,6},{8,9},{9,8},{10,11... | collective-permute-start | bytes 786440 | tf_op jit(solution)/shard_map/ppermute | solution.py:20
  54.3 7.2 %collective-permute-start.23 = (bf16[768,128]{1,0:T(8,128)(2,1)S(1)}, bf16[768,128]{1,0:T(8,128)(2,1)S(1)}, u32[]{:S(2)}, u32[]{:S(2)}) collective-permute-start(bf16[768,128]{1,0:T(8,128)(2,1)S(1)} %constant_dynamic-update-slice_fusion.2), channel_id=1, source_target_pairs={{0,2},{1,3},{2,0},{3,1},{4,6},{5,7},{6,4},{7,5},{8,10},{9,11},{10,... | collective-permute-start | bytes 589832 | tf_op jit(solution)/shard_map/ppermute | solution.py:20
  61.5 1.6 %collective-permute-start.24 = (bf16[1024,128]{1,0:T(8,128)(2,1)S(1)}, bf16[1024,128]{1,0:T(8,128)(2,1)S(1)}, u32[]{:S(2)}, u32[]{:S(2)}) collective-permute-start(bf16[1024,128]{1,0:T(8,128)(2,1)S(1)} %constant_dynamic-update-slice_fusion.5.refs_4_), channel_id=1, source_target_pairs={{0,1},{1,0},{2,3},{3,2},{4,5},{5,4},{6,7},{7,6},{8,9},{9,8},{10,11... | collective-permute-start | bytes 786440 | tf_op jit(solution)/shard_map/ppermute | solution.py:20

commit v9 on v8

--- a/solution.py
+++ b/solution.py
@@ -363,16 +363,14 @@
         side[1] = swap(side[0], "centers", nc, 1)
         for dz in range(3, nz, 2):
             layer[dz] = swap(layer[dz - 1], "points", nz, 1)
-        for d in range(2, nc, 2):
-            here = (layer[1], layer[2], side[d])
-            pos[d + 1] = swap(after(pos[d], *here), "centers", nc, 1)
-            side[d + 1] = swap(after(side[d], *here), "centers", nc, 1)
-        centers = [a for d in range(nc) for a in (pos[d], side[d])]
-
         saved, target, *local = take(
             [saved_preds, targets] + [train_points] * (nc - 1), [0, 0, *range(1, nc)], piece
         )
         local = [own, *local]
+        for d in range(2, nc, 2):
+            pos[d + 1] = swap(after(pos[d], layer[1], saved), "centers", nc, 1)
+            side[d + 1] = swap(after(side[d], layer[2]), "centers", nc, 1)
+        centers = [a for d in range(nc) for a in (pos[d], side[d])]
 
         early = {0: jnp.concatenate([layer[dz] for dz in range(1, nz - 1)])}
         for d in range(2, nc, 2):
@@ -380,13 +378,13 @@
         early[1] = swap(after(early[0], side[nc - 1]), "centers", nc, 1)
 
         first, second = [*range(2, nz, 2), 1], range(3, nz, 2)
-        rows = [after(layer[dz], saved) for dz in first]
+        rows = [layer[dz] for dz in first]
         parts = dict(zip(first, forward(rows, centers, out_width, BRIEF)))
         rows = [after(layer[dz], *parts.values(), early[1]) for dz in second]
         received = {dz: swap(parts[dz], "points", nz, dz) for dz in first}
         parts.update(zip(second, forward(rows, centers, out_width, COVER)))
-        soon = list(received.values())
-        received = [swap(parts[dz], "points", nz, dz) for dz in second]
+        soon = [received[dz] for dz in range(2, nz, 2)]
+        received = [received[1]] + [swap(parts[dz], "points", nz, dz) for dz in second]
         last = parts[nz - 1]
         kernels, late = {1: None}, {0: layer[nz - 1]}
         parts[0], kernels[0] = own_rows(
@@ -399,14 +397,13 @@
             [[local[0], early[0], late[0]]],
         )
         for d in range(2, nc, 2):
-            late[d] = swap(after(late[0], last, *soon), "centers", nc, d)
+            late[d] = swap(after(late[0], parts[0]), "centers", nc, d)
             early[d + 1] = swap(after(early[d], parts[0]), "centers", nc, 1)
         late[1] = swap(after(late[0], parts[0]), "centers", nc, 1)
         cot = cotangent([parts[0], *received], saved, target, delta)
 
         far = {dz: swap(cot, "points", nz, dz) for dz in range(2, nz, 2)}
-        held = after(cot, *(late[d] for d in range(2, nc, 2)))
-        far[1] = swap(held, "points", nz, 1)
+        far[1] = swap(cot, "points", nz, 1)
         far.update({dz: swap(far[dz - 1], "points", nz, 1) for dz in range(3, nz, 2)})
         ahead = {d: swap(cot, "centers", nc, d) for d in range(2, nc, 2)}
         far[1] = after(far[1], *ahead.values())

time: 65.7 us -> 71.5 us (1.088)
  Pallas kernels: 15.8 us -> 23.4 us
  waiting for transfers between devices: 21.9 us -> 14.7 us
  starting transfers between devices: 22.4 us -> 26.6 us
  local copies, waits for them, and re-layouts: 4.46 us -> 5.4 us
    ppermute x25, waiting for transfers between devices: 21.9 us -> 14.7 us  [swap(): return lax.ppermute(a, axis, [(i, i ^ d) for i in range(size)])]
    ppermute x25, starting transfers between devices: 22.4 us -> 26.6 us  [swap(): return lax.ppermute(a, axis, [(i, i ^ d) for i in range(size)])]
    pallas_call x2, Pallas kernels: 3.55 us -> 5.62 us  [forward(): pl.pallas_call(body, out_shape=tuple((jax.ShapeDtypeStruct((count, out_wi...]
    pallas_call x2, Pallas kernels: 7 us -> 9.05 us  [backward(): pl.pallas_call(body, out_shape=tuple((jax.ShapeDtypeStruct((n, width), F3...]
    pallas_call x1, Pallas kernels: 2.27 us -> 3.6 us  [own_rows(): pl.pallas_call(body, out_shape=(jax.ShapeDtypeStruct((rows.shape[0], out_...]
    pallas_call x1, Pallas kernels: 2.32 us -> 3.38 us  [finish(): pl.pallas_call(body, out_shape=tuple((jax.ShapeDtypeStruct((n, width), F3...]
    pallas_call x1, Pallas kernels: 0.19 us -> 1.25 us  [pack(): pl.pallas_call(body, out_shape=(jax.ShapeDtypeStruct((q + 16, in_width),...]
    unnamed x18 -> x16, local copies, waits for them, and re-layouts: 2.66 us -> 3.69 us
  transfers between devices with their start and end apart: 25 -> 25, of which waited for: 10 -> 10; matrix products, arithmetic and copies ran while one was open for 3% -> 2% of each run, Pallas kernels for 21% -> 28%
where the time goes in v9:
time: 71.5 us; the launch traced here: 70.9 us
  starting transfers between devices  26.6 us (37%)
  Pallas kernels  23.4 us (33%)
  waiting for transfers between devices  14.7 us (21%)
  local copies, waits for them, and re-layouts  5.4 us (8%)
  between operations  0.83 us (1%)
    ppermute x25, starting transfers between devices, swap(): return lax.ppermute(a, axis, [(i, i ^ d) for i in range(size)])  26.6 us
    ppermute x25, waiting for transfers between devices, swap(): return lax.ppermute(a, axis, [(i, i ^ d) for i in range(size)])  14.7 us
    pallas_call x2, Pallas kernels, backward(): pl.pallas_call(body, out_shape=tuple((jax.ShapeDtypeStruct((n, width), F3...  9.05 us
    pallas_call x2, Pallas kernels, forward(): pl.pallas_call(body, out_shape=tuple((jax.ShapeDtypeStruct((count, out_wi...  5.62 us
    unnamed x16, local copies, waits for them, and re-layouts  3.69 us
    pallas_call x1, Pallas kernels, own_rows(): pl.pallas_call(body, out_shape=(jax.ShapeDtypeStruct((rows.shape[0], out_...  3.6 us
    pallas_call x1, Pallas kernels, finish(): pl.pallas_call(body, out_shape=tuple((jax.ShapeDtypeStruct((n, width), F3...  3.38 us
  transfers between devices with their start and end apart: 25, of which 10 were waited for; matrix products, arithmetic and copies ran while one was open for 2% of the time, Pallas kernels for 28%

profile of v9, /device:TPU:0, one launch (start us, length us, event | category | flops | bytes accessed | tf_op | source)
XLA Modules:
  0.0 70.9 jit_solution(17047670432955227916)
XLA Ops:
  0.6 3.0 %collective-permute-start.5 = (bf16[512,512]{1,0:T(8,128)(2,1)}, bf16[512,512]{1,0:T(8,128)(2,1)S(1)}, u32[]{:S(2)}, u32[]{:S(2)}) collective-permute-start(bf16[512,512]{1,0:T(8,128)(2,1)} %pos_ref.6), channel_id=1, source_target_pairs={{0,2},{1,3},{2,0},{3,1},{4,6},{5,7},{6,4},{7,5},{8,10},{9,11},{10,... | collective-permute-start | bytes 1572872 | tf_op jit(solution)/shard_map/ppermute | solution.py:20
  3.6 1.0 %constant_dynamic-slice_fusion.refs_0_.refs_12_.refs_1_ = bf16[256,512]{1,0:T(8,128)(2,1)S(1)} fusion(bf16[1024,512]{1,0:T(8,128)(2,1)} %refs_4_.1, s32[]{:T(128)S(6)} %select_n.3), kind=kLoop, calls=%fused_computation.8 | loop fusion | bytes 524292 | tf_op jit(solution)/shard_map/dynamic_slice | solution.py:349
  4.6 2.7 %collective-permute-start = (bf16[256,512]{1,0:T(8,128)(2,1)S(1)}, bf16[256,512]{1,0:T(8,128)(2,1)S(1)}, u32[]{:S(2)}, u32[]{:S(2)}) collective-permute-start(bf16[256,512]{1,0:T(8,128)(2,1)S(1)} %constant_dynamic-slice_fusion.refs_0_.refs_12_.refs_1_), channel_id=1, source_target_pairs={{0,8},{4,12},{8,0},{12,4},{1,9},{5,13},{9,1},{13,5},{2,10},{6,14},... | collective-permute-start | bytes 786440 | tf_op jit(solution)/shard_map/ppermute | solution.py:20
  7.3 1.6 %collective-permute-start.2 = (bf16[256,512]{1,0:T(8,128)(2,1)S(1)}, bf16[256,512]{1,0:T(8,128)(2,1)S(1)}, u32[]{:S(2)}, u32[]{:S(2)}) collective-permute-start(bf16[256,512]{1,0:T(8,128)(2,1)S(1)} %constant_dynamic-slice_fusion.refs_0_.refs_12_.refs_1_), channel_id=1, source_target_pairs={{0,4},{4,0},{8,12},{12,8},{1,5},{5,1},{9,13},{13,9},{2,6},{6,2},{1... | collective-permute-start | bytes 786440 | tf_op jit(solution)/shard_map/ppermute | solution.py:20
  8.8 0.7 reshape.12.spread_ref.refs_11_
  9.5 0.9 %copy-done.1 = bf16[512,128]{1,0:T(8,128)(2,1)S(1)} copy-done((bf16[512,128]{1,0:T(8,128)(2,1)S(1)}, bf16[512,128]{1,0:T(8,128)(2,1)}, u32[]{:S(2)}) %copy-start.1) | copy-done | bytes 131096
  10.4 0.7 copy-done.5
  11.1 1.2 %pack.1 = (bf16[144,512]{1,0:T(8,128)(2,1)S(1)}, f32[1,128]{1,0:T(1,128)S(1)}) custom-call(bf16[512,512]{1,0:T(8,128)(2,1)} %pos_ref.6, bf16[512,128]{1,0:T(8,128)(2,1)S(1)} %copy-done.1, bf16[1,512]{1,0:T(2,128)(2,1)S(1)} %reshape.12.spread_ref.refs_11_, f32[1,128]{1,0:T(1,128)S(1)} %bitcast.1), custom_call_target="tpu_custom_call" | custom-call | flops 1 | bytes 1 | tf_op jit(solution)/shard_map/pack/pallas_call | solution.py:72
  12.3 0.6 collective-permute-start.6
  12.9 1.0 %copy-done.3 = f32[1024,128]{1,0:T(8,128)S(1)} copy-done((f32[1024,128]{1,0:T(8,128)S(1)}, f32[1024,128]{1,0:T(8,128)}, u32[]{:S(2)}) %copy-start.3) | copy-done | bytes 524312
  14.0 1.0 %copy-done.4 = f32[1024,128]{1,0:T(8,128)S(1)} copy-done((f32[1024,128]{1,0:T(8,128)S(1)}, f32[1024,128]{1,0:T(8,128)}, u32[]{:S(2)}) %copy-start.4) | copy-done | bytes 524312
  15.4 3.5 %collective-permute-done.6.refs_7_.refs_6_ = bf16[144,512]{1,0:T(8,128)(2,1)S(1)} collective-permute-done((bf16[144,512]{1,0:T(8,128)(2,1)S(1)}, bf16[144,512]{1,0:T(8,128)(2,1)S(1)}, u32[]{:S(2)}, u32[]{:S(2)}) %collective-permute-start.6) | collective-permute-done | bytes 147488 | tf_op jit(solution)/shard_map/ppermute | solution.py:20
  19.7 0.7 %collective-permute-done.8.refs_9_.refs_8_ = bf16[144,512]{1,0:T(8,128)(2,1)S(1)} collective-permute-done((bf16[144,512]{1,0:T(8,128)(2,1)S(1)}, bf16[144,512]{1,0:T(8,128)(2,1)S(1)}, u32[]{:S(2)}, u32[]{:S(2)}) %collective-permute-start.8) | collective-permute-done | bytes 147488 | tf_op jit(solution)/shard_map/ppermute | solution.py:20
  20.6 1.7 %collective-permute-start.1 = (bf16[256,512]{1,0:T(8,128)(2,1)S(1)}, bf16[256,512]{1,0:T(8,128)(2,1)S(1)}, u32[]{:S(2)}, u32[]{:S(2)}) collective-permute-start(bf16[256,512]{1,0:T(8,128)(2,1)S(1)} %collective-permute-done.refs_0_), channel_id=1, source_target_pairs={{0,4},{4,0},{8,12},{12,8},{1,5},{5,1},{9,13},{13,9},{2,6},{6,2},{1... | collective-permute-start | bytes 786440 | tf_op jit(solution)/shard_map/ppermute | solution.py:20
  22.4 1.3 %collective-permute-done.4.refs_5_.refs_4_ = bf16[144,512]{1,0:T(8,128)(2,1)S(1)} collective-permute-done((bf16[144,512]{1,0:T(8,128)(2,1)S(1)}, bf16[144,512]{1,0:T(8,128)(2,1)S(1)}, u32[]{:S(2)}, u32[]{:S(2)}) %collective-permute-start.4) | collective-permute-done | bytes 147488 | tf_op jit(solution)/shard_map/ppermute | solution.py:20
  23.7 1.5 %collective-permute-start.19 = (bf16[512,512]{1,0:T(8,128)(2,1)S(1)}, bf16[512,512]{1,0:T(8,128)(2,1)S(1)}, u32[]{:S(2)}, u32[]{:S(2)}) collective-permute-start(bf16[512,512]{1,0:T(8,128)(2,1)S(1)} %constant_dynamic-update-slice_fusion.refs_13_.refs_2_), channel_id=1, source_target_pairs={{0,2},{1,3},{2,0},{3,1},{4,6},{5,7},{6,4},{7,5},{8,10},{9,11},{10,... | collective-permute-start | bytes 1572872 | tf_op jit(solution)/shard_map/ppermute | solution.py:20
  25.2 3.3 %forward.2 = (f32[256,128]{1,0:T(8,128)S(1)}, f32[256,128]{1,0:T(8,128)S(1)}) custom-call(bf16[256,512]{1,0:T(8,128)(2,1)S(1)} %collective-permute-done.refs_0_, bf16[256,512]{1,0:T(8,128)(2,1)S(1)} %collective-permute-done.2.refs_1_, bf16[512,512]{1,0:T(8,128)(2,1)} %pos_ref.6, bf16[144,512]{1,0:T(8,128)(2,1)S(1)} %get-tuple-element.35.refs_3_.refs_2_, ...), custom_call_target="tpu_custom_call" | custom-call | flops 1 | bytes 1 | tf_op jit(solution)/shard_map/forward/pallas_call | solution.py:160
  28.5 2.7 %collective-permute-start.10 = (f32[256,128]{1,0:T(8,128)S(1)}, f32[256,128]{1,0:T(8,128)S(1)}, u32[]{:S(2)}, u32[]{:S(2)}) collective-permute-start(f32[256,128]{1,0:T(8,128)S(1)} %get-tuple-element.39), channel_id=1, source_target_pairs={{0,8},{4,12},{8,0},{12,4},{1,9},{5,13},{9,1},{13,5},{2,10},{6,14},... | collective-permute-start | bytes 393224 | tf_op jit(solution)/shard_map/ppermute | solution.py:20
  31.1 2.3 %forward.3 = f32[256,128]{1,0:T(8,128)S(1)} custom-call(bf16[256,512]{1,0:T(8,128)(2,1)S(1)} %collective-permute-done.1.refs_0_.refs_14_.refs_3_, bf16[512,512]{1,0:T(8,128)(2,1)} %pos_ref.6, bf16[144,512]{1,0:T(8,128)(2,1)S(1)} %get-tuple-element.35.refs_3_.refs_2_, bf16[512,512]{1,0:T(8,128)(2,1)S(1)} %collective-permute-done.3.refs_4_.refs_3_, ...), custom_call_target="tpu_custom_call" | custom-call | flops 17179869184 | bytes 1048576 | tf_op jit(solution)/shard_map/forward/pallas_call | solution.py:160
  33.5 1.8 %collective-permute-start.12 = (f32[256,128]{1,0:T(8,128)S(1)}, f32[256,128]{1,0:T(8,128)S(1)}, u32[]{:S(2)}, u32[]{:S(2)}) collective-permute-start(f32[256,128]{1,0:T(8,128)S(1)} %forward.3), channel_id=1, source_target_pairs={{0,12},{4,8},{8,4},{12,0},{1,13},{5,9},{9,5},{13,1},{2,14},{6,10},... | collective-permute-start | bytes 393224 | tf_op jit(solution)/shard_map/ppermute | solution.py:20
  35.3 2.3 %collective-permute-done.10.refs_9_ = f32[256,128]{1,0:T(8,128)S(1)} collective-permute-done((f32[256,128]{1,0:T(8,128)S(1)}, f32[256,128]{1,0:T(8,128)S(1)}, u32[]{:S(2)}, u32[]{:S(2)}) %collective-permute-start.10) | collective-permute-done | bytes 131104 | tf_op jit(solution)/shard_map/ppermute | solution.py:20
  37.6 3.6 %own_rows.1 = (f32[256,128]{1,0:T(8,128)S(1)}, bf16[512,1024]{1,0:T(8,128)(2,1)S(1)}) custom-call(bf16[256,512]{1,0:T(8,128)(2,1)S(1)} %constant_dynamic-slice_fusion.refs_0_.refs_12_.refs_1_, bf16[512,512]{1,0:T(8,128)(2,1)} %pos_ref.6, bf16[144,512]{1,0:T(8,128)(2,1)S(1)} %get-tuple-element.35.refs_3_.refs_2_, ...), custom_call_target="tpu_custom_call" | custom-call | flops 17179869184 | bytes 1048576 | tf_op jit(solution)/shard_map/own_rows/pallas_call | solution.py:207
  41.8 1.4 %collective-permute-done.11.refs_1_ = f32[256,128]{1,0:T(8,128)S(1)} collective-permute-done((f32[256,128]{1,0:T(8,128)S(1)}, f32[256,128]{1,0:T(8,128)S(1)}, u32[]{:S(2)}, u32[]{:S(2)}) %collective-permute-start.11) | collective-permute-done | bytes 131104 | tf_op jit(solution)/shard_map/ppermute | solution.py:20
  43.2 1.0 %collective-permute-start.14 = (bf16[256,128]{1,0:T(8,128)(2,1)S(1)}, bf16[256,128]{1,0:T(8,128)(2,1)S(1)}, u32[]{:S(2)}, u32[]{:S(2)}) collective-permute-start(bf16[256,128]{1,0:T(8,128)(2,1)S(1)} %cotangent.1), channel_id=1, source_target_pairs={{0,2},{1,3},{2,0},{3,1},{4,6},{5,7},{6,4},{7,5},{8,10},{9,11},{10,... | collective-permute-start | bytes 196616 | tf_op jit(solution)/shard_map/ppermute | solution.py:20
  44.2 0.7 collective-permute-start.13
  44.9 3.5 %collective-permute-start.15 = (bf16[256,128]{1,0:T(8,128)(2,1)S(1)}, bf16[256,128]{1,0:T(8,128)(2,1)S(1)}, u32[]{:S(2)}, u32[]{:S(2)}) collective-permute-start(bf16[256,128]{1,0:T(8,128)(2,1)S(1)} %cotangent.1), channel_id=1, source_target_pairs={{0,8},{4,12},{8,0},{12,4},{1,9},{5,13},{9,1},{13,5},{2,10},{6,14},... | collective-permute-start | bytes 196616 | tf_op jit(solution)/shard_map/ppermute | solution.py:20
  48.4 1.9 %collective-permute-start.20 = (bf16[256,512]{1,0:T(8,128)(2,1)S(1)}, bf16[256,512]{1,0:T(8,128)(2,1)S(1)}, u32[]{:S(2)}, u32[]{:S(2)}) collective-permute-start(bf16[256,512]{1,0:T(8,128)(2,1)S(1)} %collective-permute-done.1.refs_0_.refs_14_.refs_3_), channel_id=1, source_target_pairs={{0,2},{1,3},{2,0},{3,1},{4,6},{5,7},{6,4},{7,5},{8,10},{9,11},{10,... | collective-permute-start | bytes 786440 | tf_op jit(solution)/shard_map/ppermute | solution.py:20
  51.5 4.1 %collective-permute-done.16 = bf16[256,128]{1,0:T(8,128)(2,1)S(1)} collective-permute-done((bf16[256,128]{1,0:T(8,128)(2,1)S(1)}, bf16[256,128]{1,0:T(8,128)(2,1)S(1)}, u32[]{:S(2)}, u32[]{:S(2)}) %collective-permute-start.16) | collective-permute-done | bytes 65568 | tf_op jit(solution)/shard_map/ppermute | solution.py:20
  56.3 1.9 %collective-permute-start.23 = (bf16[768,128]{1,0:T(8,128)(2,1)S(1)}, bf16[768,128]{1,0:T(8,128)(2,1)S(1)}, u32[]{:S(2)}, u32[]{:S(2)}) collective-permute-start(bf16[768,128]{1,0:T(8,128)(2,1)S(1)} %constant_dynamic-update-slice_fusion.2), channel_id=1, source_target_pairs={{0,2},{1,3},{2,0},{3,1},{4,6},{5,7},{6,4},{7,5},{8,10},{9,11},{10,... | collective-permute-start | bytes 589832 | tf_op jit(solution)/shard_map/ppermute | solution.py:20
  58.3 6.7 %backward.2 = (f32[512,512]{1,0:T(8,128)S(1)}, f32[512,128]{1,0:T(8,128)S(1)}, f32[512,128]{1,0:T(8,128)S(1)}, bf16[512,1024]{1,0:T(8,128)(2,1)S(1)}, bf16[512,1024]{1,0:T(8,128)(2,1)S(1)}) custom-call(bf16[512,512]{1,0:T(8,128)(2,1)} %pos_ref.6, bf16[512,128]{1,0:T(8,128)(2,1)S(1)} %copy-done.2, bf16[1,512]{1,0:T(2,128)(2,1)S(1)} %reshape.12.spread_ref.refs_11_, ...), custom_call_target="tpu_custom_call" | custom-call | flops 17179869184 | bytes 1048576 | tf_op jit(solution)/shard_map/backward/pallas_call | solution.py:282
  65.1 2.4 %backward.3 = (f32[512,512]{1,0:T(8,128)S(1)}, f32[512,128]{1,0:T(8,128)S(1)}, f32[512,128]{1,0:T(8,128)S(1)}) custom-call(bf16[512,512]{1,0:T(8,128)(2,1)} %pos_ref.6, bf16[512,128]{1,0:T(8,128)(2,1)S(1)} %copy-done.2, bf16[1,512]{1,0:T(2,128)(2,1)S(1)} %reshape.12.spread_ref.refs_11_, bf16[512,1024]{1,0:T(8,128)(2,1)S(1)} %get-tuple-element.60.refs_0_, ...), custom_call_target="tpu_custom_call" | custom-call | flops 1 | bytes 1 | tf_op jit(solution)/shard_map/backward/pallas_call | solution.py:282
  67.5 3.4 %finish.1 = (f32[512,512]{1,0:T(8,128)}, f32[512,128]{1,0:T(8,128)}) custom-call(bf16[512,512]{1,0:T(8,128)(2,1)} %pos_ref.6, bf16[512,128]{1,0:T(8,128)(2,1)S(1)} %copy-done.2, bf16[1,512]{1,0:T(2,128)(2,1)S(1)} %reshape.12.spread_ref.refs_11_, bf16[512,1024]{1,0:T(8,128)(2,1)S(1)} %get-tuple-element.56.kernel_ref, ...), custom_call_target="tpu_custom_call" | custom-call | flops 1 | bytes 1 | tf_op jit(solution)/shard_map/finish/pallas_call | solution.py:325
  (49 shorter events, 3.9 us)
Async XLA Ops:
  0.6 12.3 %copy-start = (bf16[1024,512]{1,0:T(8,128)(2,1)S(1)}, bf16[1024,512]{1,0:T(8,128)(2,1)}, u32[]{:S(2)}) copy-start(bf16[1024,512]{1,0:T(8,128)(2,1)} %refs_4_.1) | copy-start | bytes 3145732
  0.6 18.7 %collective-permute-start.5 = (bf16[512,512]{1,0:T(8,128)(2,1)}, bf16[512,512]{1,0:T(8,128)(2,1)S(1)}, u32[]{:S(2)}, u32[]{:S(2)}) collective-permute-start(bf16[512,512]{1,0:T(8,128)(2,1)} %pos_ref.6), channel_id=1, source_target_pairs={{0,2},{1,3},{2,0},{3,1},{4,6},{5,7},{6,4},{7,5},{8,10},{9,11},{10,... | collective-permute-start | bytes 1572872 | tf_op jit(solution)/shard_map/ppermute | solution.py:20
  4.6 14.5 %collective-permute-start = (bf16[256,512]{1,0:T(8,128)(2,1)S(1)}, bf16[256,512]{1,0:T(8,128)(2,1)S(1)}, u32[]{:S(2)}, u32[]{:S(2)}) collective-permute-start(bf16[256,512]{1,0:T(8,128)(2,1)S(1)} %constant_dynamic-slice_fusion.refs_0_.refs_12_.refs_1_), channel_id=1, source_target_pairs={{0,8},{4,12},{8,0},{12,4},{1,9},{5,13},{9,1},{13,5},{2,10},{6,14},... | collective-permute-start | bytes 786440 | tf_op jit(solution)/shard_map/ppermute | solution.py:20
  7.3 12.0 %collective-permute-start.2 = (bf16[256,512]{1,0:T(8,128)(2,1)S(1)}, bf16[256,512]{1,0:T(8,128)(2,1)S(1)}, u32[]{:S(2)}, u32[]{:S(2)}) collective-permute-start(bf16[256,512]{1,0:T(8,128)(2,1)S(1)} %constant_dynamic-slice_fusion.refs_0_.refs_12_.refs_1_), channel_id=1, source_target_pairs={{0,4},{4,0},{8,12},{12,8},{1,5},{5,1},{9,13},{13,9},{2,6},{6,2},{1... | collective-permute-start | bytes 786440 | tf_op jit(solution)/shard_map/ppermute | solution.py:20
  9.5 0.9 %copy-start.1 = (bf16[512,128]{1,0:T(8,128)(2,1)S(1)}, bf16[512,128]{1,0:T(8,128)(2,1)}, u32[]{:S(2)}) copy-start(bf16[512,128]{1,0:T(8,128)(2,1)} %coef_ref.7) | copy-start | bytes 393220
  10.4 0.7 copy-start.5
  12.3 6.6 %collective-permute-start.6 = (bf16[144,512]{1,0:T(8,128)(2,1)S(1)}, bf16[144,512]{1,0:T(8,128)(2,1)S(1)}, u32[]{:S(2)}, u32[]{:S(2)}) collective-permute-start(bf16[144,512]{1,0:T(8,128)(2,1)S(1)} %get-tuple-element.35.refs_3_.refs_2_), channel_id=1, source_target_pairs={{0,2},{1,3},{2,0},{3,1},{4,6},{5,7},{6,4},{7,5},{8,10},{9,11},{10,... | collective-permute-start | bytes 442376 | tf_op jit(solution)/shard_map/ppermute | solution.py:20
  12.9 12.2 %collective-permute-start.3 = (bf16[512,512]{1,0:T(8,128)(2,1)}, bf16[512,512]{1,0:T(8,128)(2,1)S(1)}, u32[]{:S(2)}, u32[]{:S(2)}) collective-permute-start(bf16[512,512]{1,0:T(8,128)(2,1)} %pos_ref.6), channel_id=1, source_target_pairs={{0,1},{1,0},{2,3},{3,2},{4,5},{5,4},{6,7},{7,6},{8,9},{9,8},{10,11... | collective-permute-start | bytes 1572872 | tf_op jit(solution)/shard_map/ppermute | solution.py:20
  12.9 1.0 %copy-start.3 = (f32[1024,128]{1,0:T(8,128)S(1)}, f32[1024,128]{1,0:T(8,128)}, u32[]{:S(2)}) copy-start(f32[1024,128]{1,0:T(8,128)} %refs_0_.1) | copy-start | bytes 1572868
  14.0 1.0 %copy-start.4 = (f32[1024,128]{1,0:T(8,128)S(1)}, f32[1024,128]{1,0:T(8,128)}, u32[]{:S(2)}) copy-start(f32[1024,128]{1,0:T(8,128)} %refs_1_.3) | copy-start | bytes 1572868
  19.1 1.4 %collective-permute-start.8 = (bf16[144,512]{1,0:T(8,128)(2,1)S(1)}, bf16[144,512]{1,0:T(8,128)(2,1)S(1)}, u32[]{:S(2)}, u32[]{:S(2)}) collective-permute-start(bf16[144,512]{1,0:T(8,128)(2,1)S(1)} %collective-permute-done.6.refs_7_.refs_6_), channel_id=1, source_target_pairs={{0,1},{1,0},{2,3},{3,2},{4,5},{5,4},{6,7},{7,6},{8,9},{9,8},{10,11... | collective-permute-start | bytes 442376 | tf_op jit(solution)/shard_map/ppermute | solution.py:20
  19.3 5.9 %collective-permute-start.7 = (bf16[512,512]{1,0:T(8,128)(2,1)S(1)}, bf16[512,512]{1,0:T(8,128)(2,1)S(1)}, u32[]{:S(2)}, u32[]{:S(2)}) collective-permute-start(bf16[512,512]{1,0:T(8,128)(2,1)S(1)} %collective-permute-done.5.refs_6_.refs_5_), channel_id=1, source_target_pairs={{0,1},{1,0},{2,3},{3,2},{4,5},{5,4},{6,7},{7,6},{8,9},{9,8},{10,11... | collective-permute-start | bytes 1572872 | tf_op jit(solution)/shard_map/ppermute | solution.py:20
  20.4 10.7 %collective-permute-start.9 = (bf16[512,512]{1,0:T(8,128)(2,1)S(1)}, bf16[512,512]{1,0:T(8,128)(2,1)S(1)}, u32[]{:S(2)}, u32[]{:S(2)}) collective-permute-start(bf16[512,512]{1,0:T(8,128)(2,1)S(1)} %constant_dynamic-update-slice_fusion.refs_13_.refs_2_), channel_id=1, source_target_pairs={{0,1},{1,0},{2,3},{3,2},{4,5},{5,4},{6,7},{7,6},{8,9},{9,8},{10,11... | collective-permute-start | bytes 1572872 | tf_op jit(solution)/shard_map/ppermute | solution.py:20
  20.6 10.5 %collective-permute-start.1 = (bf16[256,512]{1,0:T(8,128)(2,1)S(1)}, bf16[256,512]{1,0:T(8,128)(2,1)S(1)}, u32[]{:S(2)}, u32[]{:S(2)}) collective-permute-start(bf16[256,512]{1,0:T(8,128)(2,1)S(1)} %collective-permute-done.refs_0_), channel_id=1, source_target_pairs={{0,4},{4,0},{8,12},{12,8},{1,5},{5,1},{9,13},{13,9},{2,6},{6,2},{1... | collective-permute-start | bytes 786440 | tf_op jit(solution)/shard_map/ppermute | solution.py:20
  22.3 1.4 %collective-permute-start.4 = (bf16[144,512]{1,0:T(8,128)(2,1)S(1)}, bf16[144,512]{1,0:T(8,128)(2,1)S(1)}, u32[]{:S(2)}, u32[]{:S(2)}) collective-permute-start(bf16[144,512]{1,0:T(8,128)(2,1)S(1)} %get-tuple-element.35.refs_3_.refs_2_), channel_id=1, source_target_pairs={{0,1},{1,0},{2,3},{3,2},{4,5},{5,4},{6,7},{7,6},{8,9},{9,8},{10,11... | collective-permute-start | bytes 442376 | tf_op jit(solution)/shard_map/ppermute | solution.py:20
  23.7 26.7 %collective-permute-start.19 = (bf16[512,512]{1,0:T(8,128)(2,1)S(1)}, bf16[512,512]{1,0:T(8,128)(2,1)S(1)}, u32[]{:S(2)}, u32[]{:S(2)}) collective-permute-start(bf16[512,512]{1,0:T(8,128)(2,1)S(1)} %constant_dynamic-update-slice_fusion.refs_13_.refs_2_), channel_id=1, source_target_pairs={{0,2},{1,3},{2,0},{3,1},{4,6},{5,7},{6,4},{7,5},{8,10},{9,11},{10,... | collective-permute-start | bytes 1572872 | tf_op jit(solution)/shard_map/ppermute | solution.py:20
  28.5 9.2 %collective-permute-start.10 = (f32[256,128]{1,0:T(8,128)S(1)}, f32[256,128]{1,0:T(8,128)S(1)}, u32[]{:S(2)}, u32[]{:S(2)}) collective-permute-start(f32[256,128]{1,0:T(8,128)S(1)} %get-tuple-element.39), channel_id=1, source_target_pairs={{0,8},{4,12},{8,0},{12,4},{1,9},{5,13},{9,1},{13,5},{2,10},{6,14},... | collective-permute-start | bytes 393224 | tf_op jit(solution)/shard_map/ppermute | solution.py:20
  33.5 8.3 %collective-permute-start.12 = (f32[256,128]{1,0:T(8,128)S(1)}, f32[256,128]{1,0:T(8,128)S(1)}, u32[]{:S(2)}, u32[]{:S(2)}) collective-permute-start(f32[256,128]{1,0:T(8,128)S(1)} %forward.3), channel_id=1, source_target_pairs={{0,12},{4,8},{8,4},{12,0},{1,13},{5,9},{9,5},{13,1},{2,14},{6,10},... | collective-permute-start | bytes 393224 | tf_op jit(solution)/shard_map/ppermute | solution.py:20
  35.3 7.8 %collective-permute-start.11 = (f32[256,128]{1,0:T(8,128)S(1)}, f32[256,128]{1,0:T(8,128)S(1)}, u32[]{:S(2)}, u32[]{:S(2)}) collective-permute-start(f32[256,128]{1,0:T(8,128)S(1)} %get-tuple-element.40), channel_id=1, source_target_pairs={{0,4},{4,0},{8,12},{12,8},{1,5},{5,1},{9,13},{13,9},{2,6},{6,2},{1... | collective-permute-start | bytes 393224 | tf_op jit(solution)/shard_map/ppermute | solution.py:20
  43.2 7.1 %collective-permute-start.14 = (bf16[256,128]{1,0:T(8,128)(2,1)S(1)}, bf16[256,128]{1,0:T(8,128)(2,1)S(1)}, u32[]{:S(2)}, u32[]{:S(2)}) collective-permute-start(bf16[256,128]{1,0:T(8,128)(2,1)S(1)} %cotangent.1), channel_id=1, source_target_pairs={{0,2},{1,3},{2,0},{3,1},{4,6},{5,7},{6,4},{7,5},{8,10},{9,11},{10,... | collective-permute-start | bytes 196616 | tf_op jit(solution)/shard_map/ppermute | solution.py:20
  44.2 6.7 %collective-permute-start.13 = (bf16[256,128]{1,0:T(8,128)(2,1)S(1)}, bf16[256,128]{1,0:T(8,128)(2,1)S(1)}, u32[]{:S(2)}, u32[]{:S(2)}) collective-permute-start(bf16[256,128]{1,0:T(8,128)(2,1)S(1)} %cotangent.1), channel_id=1, source_target_pairs={{0,4},{4,0},{8,12},{12,8},{1,5},{5,1},{9,13},{13,9},{2,6},{6,2},{1... | collective-permute-start | bytes 196616 | tf_op jit(solution)/shard_map/ppermute | solution.py:20
  44.9 6.5 %collective-permute-start.15 = (bf16[256,128]{1,0:T(8,128)(2,1)S(1)}, bf16[256,128]{1,0:T(8,128)(2,1)S(1)}, u32[]{:S(2)}, u32[]{:S(2)}) collective-permute-start(bf16[256,128]{1,0:T(8,128)(2,1)S(1)} %cotangent.1), channel_id=1, source_target_pairs={{0,8},{4,12},{8,0},{12,4},{1,9},{5,13},{9,1},{13,5},{2,10},{6,14},... | collective-permute-start | bytes 196616 | tf_op jit(solution)/shard_map/ppermute | solution.py:20
  48.4 7.3 %collective-permute-start.20 = (bf16[256,512]{1,0:T(8,128)(2,1)S(1)}, bf16[256,512]{1,0:T(8,128)(2,1)S(1)}, u32[]{:S(2)}, u32[]{:S(2)}) collective-permute-start(bf16[256,512]{1,0:T(8,128)(2,1)S(1)} %collective-permute-done.1.refs_0_.refs_14_.refs_3_), channel_id=1, source_target_pairs={{0,2},{1,3},{2,0},{3,1},{4,6},{5,7},{6,4},{7,5},{8,10},{9,11},{10,... | collective-permute-start | bytes 786440 | tf_op jit(solution)/shard_map/ppermute | solution.py:20
  50.3 7.9 %collective-permute-start.17 = (bf16[256,512]{1,0:T(8,128)(2,1)S(1)}, bf16[256,512]{1,0:T(8,128)(2,1)S(1)}, u32[]{:S(2)}, u32[]{:S(2)}) collective-permute-start(bf16[256,512]{1,0:T(8,128)(2,1)S(1)} %collective-permute-done.1.refs_0_.refs_14_.refs_3_), channel_id=1, source_target_pairs={{0,1},{1,0},{2,3},{3,2},{4,5},{5,4},{6,7},{7,6},{8,9},{9,8},{10,11... | collective-permute-start | bytes 786440 | tf_op jit(solution)/shard_map/ppermute | solution.py:20
  50.3 7.9 %collective-permute-start.21 = (bf16[512,512]{1,0:T(8,128)(2,1)S(1)}, bf16[512,512]{1,0:T(8,128)(2,1)S(1)}, u32[]{:S(2)}, u32[]{:S(2)}) collective-permute-start(bf16[512,512]{1,0:T(8,128)(2,1)S(1)} %collective-permute-done.19.refs_10_.refs_2_), channel_id=1, source_target_pairs={{0,1},{1,0},{2,3},{3,2},{4,5},{5,4},{6,7},{7,6},{8,9},{9,8},{10,11... | collective-permute-start | bytes 1572872 | tf_op jit(solution)/shard_map/ppermute | solution.py:20
  51.3 4.3 %collective-permute-start.16 = (bf16[256,128]{1,0:T(8,128)(2,1)S(1)}, bf16[256,128]{1,0:T(8,128)(2,1)S(1)}, u32[]{:S(2)}, u32[]{:S(2)}) collective-permute-start(bf16[256,128]{1,0:T(8,128)(2,1)S(1)} %collective-permute-done.15), channel_id=1, source_target_pairs={{0,4},{4,0},{8,12},{12,8},{1,5},{5,1},{9,13},{13,9},{2,6},{6,2},{1... | collective-permute-start | bytes 196616 | tf_op jit(solution)/shard_map/ppermute | solution.py:20
  55.6 2.6 %copy-start.2 = (bf16[512,128]{1,0:T(8,128)(2,1)S(1)}, bf16[512,128]{1,0:T(8,128)(2,1)}, u32[]{:S(2)}) copy-start(bf16[512,128]{1,0:T(8,128)(2,1)} %coef_ref.7) | copy-start | bytes 393220
  55.6 2.6 %collective-permute-start.18 = (bf16[1024,128]{1,0:T(8,128)(2,1)S(1)}, bf16[1024,128]{1,0:T(8,128)(2,1)S(1)}, u32[]{:S(2)}, u32[]{:S(2)}) collective-permute-start(bf16[1024,128]{1,0:T(8,128)(2,1)S(1)} %pad_maximum_fusion.refs_4_), channel_id=1, source_target_pairs={{0,1},{1,0},{2,3},{3,2},{4,5},{5,4},{6,7},{7,6},{8,9},{9,8},{10,11... | collective-permute-start | bytes 786440 | tf_op jit(solution)/shard_map/ppermute | solution.py:20
  55.7 2.5 %collective-permute-start.22 = (bf16[256,512]{1,0:T(8,128)(2,1)S(1)}, bf16[256,512]{1,0:T(8,128)(2,1)S(1)}, u32[]{:S(2)}, u32[]{:S(2)}) collective-permute-start(bf16[256,512]{1,0:T(8,128)(2,1)S(1)} %collective-permute-done.20.refs_11_.refs_3_), channel_id=1, source_target_pairs={{0,1},{1,0},{2,3},{3,2},{4,5},{5,4},{6,7},{7,6},{8,9},{9,8},{10,11... | collective-permute-start | bytes 786440 | tf_op jit(solution)/shard_map/ppermute | solution.py:20
  56.3 8.7 %collective-permute-start.23 = (bf16[768,128]{1,0:T(8,128)(2,1)S(1)}, bf16[768,128]{1,0:T(8,128)(2,1)S(1)}, u32[]{:S(2)}, u32[]{:S(2)}) collective-permute-start(bf16[768,128]{1,0:T(8,128)(2,1)S(1)} %constant_dynamic-update-slice_fusion.2), channel_id=1, source_target_pairs={{0,2},{1,3},{2,0},{3,1},{4,6},{5,7},{6,4},{7,5},{8,10},{9,11},{10,... | collective-permute-start | bytes 589832 | tf_op jit(solution)/shard_map/ppermute | solution.py:20
  65.0 2.4 %collective-permute-start.24 = (bf16[1024,128]{1,0:T(8,128)(2,1)S(1)}, bf16[1024,128]{1,0:T(8,128)(2,1)S(1)}, u32[]{:S(2)}, u32[]{:S(2)}) collective-permute-start(bf16[1024,128]{1,0:T(8,128)(2,1)S(1)} %constant_dynamic-update-slice_fusion.5.refs_4_), channel_id=1, source_target_pairs={{0,1},{1,0},{2,3},{3,2},{4,5},{5,4},{6,7},{7,6},{8,9},{9,8},{10,11... | collective-permute-start | bytes 786440 | tf_op jit(solution)/shard_map/ppermute | solution.py:20

commit v10 on v9

--- a/solution.py
+++ b/solution.py
@@ -54,11 +54,15 @@
     across = in_width // out_width
     q = n // across
 
-    def body(pos_ref, coef_ref, spread_ref, delta_ref, out_ref, row_ref):
+    def body(pos_ref, coef_ref, spread_ref, delta_ref, own_pos, out_ref, row_ref, own_spread, own_coef):
         row_ref[...] = delta_ref[...]
+        own_spread[...] = spread_ref[...]
+        own_coef[...] = coef_ref[...]
+        pos = pos_ref[...]
+        own_pos[...] = pos
         for k in range(across):
             out_ref[:q, k * out_width : (k + 1) * out_width] = coef_ref[k * q : (k + 1) * q]
-        half = half_sq_row(pos_ref[...])
+        half = half_sq_row(pos)
         high = half.astype(BF16)
         rest = half - high.astype(F32)
         middle = rest.astype(BF16)
@@ -72,11 +76,14 @@
     return pl.pallas_call(
         body,
         out_shape=(
+            jax.ShapeDtypeStruct((n, in_width), BF16),
             jax.ShapeDtypeStruct((q + 16, in_width), BF16),
             jax.ShapeDtypeStruct((1, delta.shape[0]), F32),
+            jax.ShapeDtypeStruct((1, n), BF16),
+            jax.ShapeDtypeStruct((n, out_width), BF16),
         ),
         in_specs=[VMEM] * 4,
-        out_specs=(VMEM, VMEM),
+        out_specs=(VMEM,) * 5,
         compiler_params=params(16),
         cost_estimate=BRIEF,
         name="pack",
@@ -169,7 +176,7 @@
 
 
 def own_kernel(center_pos, spread, blocks):
-    n = center_pos.shape[0]
+    n = spread.shape[1]
     points = sum(b.shape[0] for b in blocks)
 
     def body(pos_ref, spread_ref, *refs):
@@ -183,11 +190,11 @@
         compiler_params=params(16),
         cost_estimate=BRIEF,
         name="own_kernel",
-    )(center_pos, spread.reshape(1, n), *blocks)
+    )(center_pos, spread, *blocks)
 
 
 def own_rows(rows, centers, out_width, received, center_pos, spread, more):
-    n = center_pos.shape[0]
+    n = spread.shape[1]
     ends = [1, 1 + len(centers)]
     ends.append(ends[-1] + len(received))
 
@@ -202,7 +209,7 @@
             store_values(pos_ref, spread_ref, block_refs[: len(blocks)], outs[1 + k])
             del block_refs[: len(blocks)]
 
-    ins = [rows, *centers, *received, center_pos, spread.reshape(1, n)]
+    ins = [rows, *centers, *received, center_pos, spread]
     ins += [block for blocks in more for block in blocks]
     return pl.pallas_call(
         body,
@@ -251,8 +258,7 @@
 
 
 def backward(center_pos, coefficients, spread, groups, before=None, more=()):
-    n, in_width = center_pos.shape
-    out_width = coefficients.shape[1]
+    (n, out_width), in_width = coefficients.shape, center_pos.shape[1]
     flat = []
     for kernel, xs, cot in groups:
         flat += [*xs, cot] if kernel is None else [kernel, *xs, cot]
@@ -288,12 +294,11 @@
         compiler_params=params(24),
         cost_estimate=COVER if more else BRIEF,
         name="backward",
-    )(center_pos, coefficients, spread.reshape(1, n), *flat, *carried, *wanted)
+    )(center_pos, coefficients, spread, *flat, *carried, *wanted)
 
 
 def finish(center_pos, coefficients, spread, group, before):
-    n, in_width = center_pos.shape
-    out_width = coefficients.shape[1]
+    (n, out_width), in_width = coefficients.shape, center_pos.shape[1]
     kernel, xs, cot = group
     step = min(n, 256)
 
@@ -321,7 +326,7 @@
         for copy in made:
             copy.wait()
 
-    ins = [center_pos, coefficients, spread.reshape(1, n), kernel, cot, *xs, *before]
+    ins = [center_pos, coefficients, spread, kernel, cot, *xs, *before]
     return pl.pallas_call(
         body,
         out_shape=tuple(jax.ShapeDtypeStruct((n, width), F32) for width in (in_width, out_width)),
@@ -353,14 +358,15 @@
             layer[dz] = swap(own, "points", nz, dz)
         layer[1] = swap(own, "points", nz, 1)
 
-        pos, side = {0: center_pos}, {}
+        pos, side = {1: swap(center_pos, "centers", nc, 1)}, {}
         for d in range(2, nc, 2):
             pos[d] = swap(center_pos, "centers", nc, d)
-        pos[1] = swap(center_pos, "centers", nc, 1)
-        side[0], delta = pack(after(center_pos, own), coefficients, spread, huber_delta)
+        center_pos, side[0], delta, spread, coefficients = pack(
+            after(center_pos, own), coefficients, spread, huber_delta
+        )
+        pos[0], side[1] = center_pos, swap(side[0], "centers", nc, 1)
         for d in range(2, nc, 2):
             side[d] = swap(side[0], "centers", nc, d)
-        side[1] = swap(side[0], "centers", nc, 1)
         for dz in range(3, nz, 2):
             layer[dz] = swap(layer[dz - 1], "points", nz, 1)
         saved, target, *local = take(
@@ -369,12 +375,10 @@
         local = [own, *local]
         for d in range(2, nc, 2):
             pos[d + 1] = swap(after(pos[d], layer[1], saved), "centers", nc, 1)
-            side[d + 1] = swap(after(side[d], layer[2]), "centers", nc, 1)
+            side[d + 1] = swap(after(side[d], layer[2], side[1]), "centers", nc, 1)
         centers = [a for d in range(nc) for a in (pos[d], side[d])]
 
         early = {0: jnp.concatenate([layer[dz] for dz in range(1, nz - 1)])}
-        for d in range(2, nc, 2):
-            early[d] = swap(after(early[0], side[d]), "centers", nc, d)
         early[1] = swap(after(early[0], side[nc - 1]), "centers", nc, 1)
 
         first, second = [*range(2, nz, 2), 1], range(3, nz, 2)
@@ -397,6 +401,7 @@
             [[local[0], early[0], late[0]]],
         )
         for d in range(2, nc, 2):
+            early[d] = swap(after(early[0], last), "centers", nc, d)
             late[d] = swap(after(late[0], parts[0]), "centers", nc, d)
             early[d + 1] = swap(after(early[d], parts[0]), "centers", nc, 1)
         late[1] = swap(after(late[0], parts[0]), "centers", nc, 1)

time: 71.5 us -> 70.1 us (0.980)
  Pallas kernels: 23.4 us -> 15.8 us
  waiting for transfers between devices: 14.7 us -> 20.4 us
  local copies, waits for them, and re-layouts: 5.4 us -> 6.44 us
    ppermute x25, waiting for transfers between devices: 14.7 us -> 20.4 us  [swap(): return lax.ppermute(a, axis, [(i, i ^ d) for i in range(size)])]
    pallas_call x2, Pallas kernels: 9.05 us -> 6.93 us  [backward(): pl.pallas_call(body, out_shape=tuple((jax.ShapeDtypeStruct((n, width), F3...]
    pallas_call x2, Pallas kernels: 5.62 us -> 3.56 us  [forward(): pl.pallas_call(body, out_shape=tuple((jax.ShapeDtypeStruct((count, out_wi...]
    pallas_call x1, Pallas kernels: 3.6 us -> 2.28 us  [own_rows(): pl.pallas_call(body, out_shape=(jax.ShapeDtypeStruct((rows.shape[0], out_...]
    pallas_call x1, Pallas kernels: 3.38 us -> 2.31 us  [finish(): pl.pallas_call(body, out_shape=tuple((jax.ShapeDtypeStruct((n, width), F3...]
    unnamed x16 -> x18, local copies, waits for them, and re-layouts: 3.69 us -> 4.74 us
    pallas_call x1, Pallas kernels: 1.25 us -> 0.22 us  [pack(): pl.pallas_call(body, out_shape=(jax.ShapeDtypeStruct((n, in_width), BF16)...]
  transfers between devices with their start and end apart: 25 -> 25, of which waited for: 10 -> 9; matrix products, arithmetic and copies ran while one was open for 2% -> 2% of each run, Pallas kernels for 28% -> 19%
where the time goes in v10:
time: 70.1 us; the launch traced here: 69.8 us
  starting transfers between devices  26.3 us (38%)
  waiting for transfers between devices  20.4 us (29%)
  Pallas kernels  15.8 us (23%)
  local copies, waits for them, and re-layouts  6.44 us (9%)
  between operations  0.81 us (1%)
    ppermute x25, starting transfers between devices, swap(): return lax.ppermute(a, axis, [(i, i ^ d) for i in range(size)])  26.3 us
    ppermute x25, waiting for transfers between devices, swap(): return lax.ppermute(a, axis, [(i, i ^ d) for i in range(size)])  20.4 us
    pallas_call x2, Pallas kernels, backward(): pl.pallas_call(body, out_shape=tuple((jax.ShapeDtypeStruct((n, width), F3...  6.93 us
    unnamed x18, local copies, waits for them, and re-layouts  4.74 us
    pallas_call x2, Pallas kernels, forward(): pl.pallas_call(body, out_shape=tuple((jax.ShapeDtypeStruct((count, out_wi...  3.56 us
    pallas_call x1, Pallas kernels, finish(): pl.pallas_call(body, out_shape=tuple((jax.ShapeDtypeStruct((n, width), F3...  2.31 us
    pallas_call x1, Pallas kernels, own_rows(): pl.pallas_call(body, out_shape=(jax.ShapeDtypeStruct((rows.shape[0], out_...  2.28 us
  transfers between devices with their start and end apart: 25, of which 9 were waited for; matrix products, arithmetic and copies ran while one was open for 2% of the time, Pallas kernels for 19%

profile of v10, /device:TPU:0, one launch (start us, length us, event | category | flops | bytes accessed | tf_op | source)
XLA Modules:
  0.0 69.8 jit_solution(18097210116237481038)
XLA Ops:
  0.6 3.0 %collective-permute-start.5 = (bf16[512,512]{1,0:T(8,128)(2,1)}, bf16[512,512]{1,0:T(8,128)(2,1)S(1)}, u32[]{:S(2)}, u32[]{:S(2)}) collective-permute-start(bf16[512,512]{1,0:T(8,128)(2,1)} %pos_ref), channel_id=1, source_target_pairs={{0,2},{1,3},{2,0},{3,1},{4,6},{5,7},{6,4},{7,5},{8,10},{9,11},{10,... | collective-permute-start | bytes 1572872 | tf_op jit(solution)/shard_map/ppermute | solution.py:20
  3.6 1.0 %constant_dynamic-slice_fusion.refs_0_.refs_12_.refs_1_ = bf16[256,512]{1,0:T(8,128)(2,1)S(1)} fusion(bf16[1024,512]{1,0:T(8,128)(2,1)} %refs_4_.1, s32[]{:T(128)S(6)} %select_n.3), kind=kLoop, calls=%fused_computation.8 | loop fusion | bytes 524292 | tf_op jit(solution)/shard_map/dynamic_slice | solution.py:354
  4.6 2.7 %collective-permute-start = (bf16[256,512]{1,0:T(8,128)(2,1)S(1)}, bf16[256,512]{1,0:T(8,128)(2,1)S(1)}, u32[]{:S(2)}, u32[]{:S(2)}) collective-permute-start(bf16[256,512]{1,0:T(8,128)(2,1)S(1)} %constant_dynamic-slice_fusion.refs_0_.refs_12_.refs_1_), channel_id=1, source_target_pairs={{0,8},{4,12},{8,0},{12,4},{1,9},{5,13},{9,1},{13,5},{2,10},{6,14},... | collective-permute-start | bytes 786440 | tf_op jit(solution)/shard_map/ppermute | solution.py:20
  7.3 1.6 %collective-permute-start.2 = (bf16[256,512]{1,0:T(8,128)(2,1)S(1)}, bf16[256,512]{1,0:T(8,128)(2,1)S(1)}, u32[]{:S(2)}, u32[]{:S(2)}) collective-permute-start(bf16[256,512]{1,0:T(8,128)(2,1)S(1)} %constant_dynamic-slice_fusion.refs_0_.refs_12_.refs_1_), channel_id=1, source_target_pairs={{0,4},{4,0},{8,12},{12,8},{1,5},{5,1},{9,13},{13,9},{2,6},{6,2},{1... | collective-permute-start | bytes 786440 | tf_op jit(solution)/shard_map/ppermute | solution.py:20
  8.8 0.7 reshape.10.spread_ref
  9.5 1.0 %copy-done.1 = bf16[512,512]{1,0:T(8,128)(2,1)S(1)} copy-done((bf16[512,512]{1,0:T(8,128)(2,1)S(1)}, bf16[512,512]{1,0:T(8,128)(2,1)}, u32[]{:S(2)}) %copy-start.1) | copy-done | bytes 524312
  10.6 0.9 %copy-done.5 = bf16[512,128]{1,0:T(8,128)(2,1)S(1)} copy-done((bf16[512,128]{1,0:T(8,128)(2,1)S(1)}, bf16[512,128]{1,0:T(8,128)(2,1)}, u32[]{:S(2)}) %copy-start.5) | copy-done | bytes 131096
  11.5 0.7 copy-done.6
  13.0 1.0 %copy-done.3 = f32[1024,128]{1,0:T(8,128)S(1)} copy-done((f32[1024,128]{1,0:T(8,128)S(1)}, f32[1024,128]{1,0:T(8,128)}, u32[]{:S(2)}) %copy-start.3) | copy-done | bytes 524312
  14.0 1.0 %copy-done.4 = f32[1024,128]{1,0:T(8,128)S(1)} copy-done((f32[1024,128]{1,0:T(8,128)S(1)}, f32[1024,128]{1,0:T(8,128)}, u32[]{:S(2)}) %copy-start.4) | copy-done | bytes 524312
  15.5 3.5 %collective-permute-done.6.refs_7_.refs_6_ = bf16[144,512]{1,0:T(8,128)(2,1)S(1)} collective-permute-done((bf16[144,512]{1,0:T(8,128)(2,1)S(1)}, bf16[144,512]{1,0:T(8,128)(2,1)S(1)}, u32[]{:S(2)}, u32[]{:S(2)}) %collective-permute-start.6) | collective-permute-done | bytes 147488 | tf_op jit(solution)/shard_map/ppermute | solution.py:20
  19.7 1.4 %collective-permute-done.8.refs_9_.refs_8_ = bf16[144,512]{1,0:T(8,128)(2,1)S(1)} collective-permute-done((bf16[144,512]{1,0:T(8,128)(2,1)S(1)}, bf16[144,512]{1,0:T(8,128)(2,1)S(1)}, u32[]{:S(2)}, u32[]{:S(2)}) %collective-permute-start.8) | collective-permute-done | bytes 147488 | tf_op jit(solution)/shard_map/ppermute | solution.py:20
  21.2 1.8 %collective-permute-start.1 = (bf16[256,512]{1,0:T(8,128)(2,1)S(1)}, bf16[256,512]{1,0:T(8,128)(2,1)S(1)}, u32[]{:S(2)}, u32[]{:S(2)}) collective-permute-start(bf16[256,512]{1,0:T(8,128)(2,1)S(1)} %collective-permute-done.refs_0_), channel_id=1, source_target_pairs={{0,4},{4,0},{8,12},{12,8},{1,5},{5,1},{9,13},{13,9},{2,6},{6,2},{1... | collective-permute-start | bytes 786440 | tf_op jit(solution)/shard_map/ppermute | solution.py:20
  23.0 2.2 %forward.2 = (f32[256,128]{1,0:T(8,128)S(1)}, f32[256,128]{1,0:T(8,128)S(1)}) custom-call(bf16[256,512]{1,0:T(8,128)(2,1)S(1)} %collective-permute-done.refs_0_, bf16[256,512]{1,0:T(8,128)(2,1)S(1)} %collective-permute-done.2.refs_1_, bf16[512,512]{1,0:T(8,128)(2,1)S(1)} %get-tuple-element.38.refs_2_.refs_1_.refs_10_.pos_ref, ...), custom_call_target="tpu_custom_call" | custom-call | flops 1 | bytes 1 | tf_op jit(solution)/shard_map/forward/pallas_call | solution.py:167
  25.3 2.7 %collective-permute-start.10 = (f32[256,128]{1,0:T(8,128)S(1)}, f32[256,128]{1,0:T(8,128)S(1)}, u32[]{:S(2)}, u32[]{:S(2)}) collective-permute-start(f32[256,128]{1,0:T(8,128)S(1)} %get-tuple-element.45), channel_id=1, source_target_pairs={{0,8},{4,12},{8,0},{12,4},{1,9},{5,13},{9,1},{13,5},{2,10},{6,14},... | collective-permute-start | bytes 393224 | tf_op jit(solution)/shard_map/ppermute | solution.py:20
  28.0 4.7 %collective-permute-done.1.refs_0_.refs_14_.refs_3_ = bf16[256,512]{1,0:T(8,128)(2,1)S(1)} collective-permute-done((bf16[256,512]{1,0:T(8,128)(2,1)S(1)}, bf16[256,512]{1,0:T(8,128)(2,1)S(1)}, u32[]{:S(2)}, u32[]{:S(2)}) %collective-permute-start.1) | collective-permute-done | bytes 262176 | tf_op jit(solution)/shard_map/ppermute | solution.py:20
  32.7 1.3 %forward.3 = f32[256,128]{1,0:T(8,128)S(1)} custom-call(bf16[256,512]{1,0:T(8,128)(2,1)S(1)} %collective-permute-done.1.refs_0_.refs_14_.refs_3_, bf16[512,512]{1,0:T(8,128)(2,1)S(1)} %get-tuple-element.38.refs_2_.refs_1_.refs_10_.pos_ref, bf16[144,512]{1,0:T(8,128)(2,1)S(1)} %get-tuple-element.41.refs_3_.refs_2_, ...), custom_call_target="tpu_custom_call" | custom-call | flops 17179869184 | bytes 1048576 | tf_op jit(solution)/shard_map/forward/pallas_call | solution.py:167
  34.0 2.9 %collective-permute-start.12 = (f32[256,128]{1,0:T(8,128)S(1)}, f32[256,128]{1,0:T(8,128)S(1)}, u32[]{:S(2)}, u32[]{:S(2)}) collective-permute-start(f32[256,128]{1,0:T(8,128)S(1)} %forward.3), channel_id=1, source_target_pairs={{0,12},{4,8},{8,4},{12,0},{1,13},{5,9},{9,5},{13,1},{2,14},{6,10},... | collective-permute-start | bytes 393224 | tf_op jit(solution)/shard_map/ppermute | solution.py:20
  36.9 1.5 %collective-permute-start.19 = (bf16[512,512]{1,0:T(8,128)(2,1)S(1)}, bf16[512,512]{1,0:T(8,128)(2,1)S(1)}, u32[]{:S(2)}, u32[]{:S(2)}) collective-permute-start(bf16[512,512]{1,0:T(8,128)(2,1)S(1)} %constant_dynamic-update-slice_fusion.refs_13_.refs_2_), channel_id=1, source_target_pairs={{0,2},{1,3},{2,0},{3,1},{4,6},{5,7},{6,4},{7,5},{8,10},{9,11},{10,... | collective-permute-start | bytes 1572872 | tf_op jit(solution)/shard_map/ppermute | solution.py:20
  38.4 2.3 %own_rows.1 = (f32[256,128]{1,0:T(8,128)S(1)}, bf16[512,1024]{1,0:T(8,128)(2,1)S(1)}) custom-call(bf16[256,512]{1,0:T(8,128)(2,1)S(1)} %constant_dynamic-slice_fusion.refs_0_.refs_12_.refs_1_, bf16[512,512]{1,0:T(8,128)(2,1)S(1)} %get-tuple-element.38.refs_2_.refs_1_.refs_10_.pos_ref, bf16[144,512]{1,0:T(8,128)(2,1)S(1)} %get-tuple-element.41.refs_3_.refs_2_, ...), custom_call_target="tpu_custom_call" | custom-call | flops 17179869184 | bytes 1048576 | tf_op jit(solution)/shard_map/own_rows/pallas_call | solution.py:214
  40.7 1.6 %collective-permute-done.12.refs_2_ = f32[256,128]{1,0:T(8,128)S(1)} collective-permute-done((f32[256,128]{1,0:T(8,128)S(1)}, f32[256,128]{1,0:T(8,128)S(1)}, u32[]{:S(2)}, u32[]{:S(2)}) %collective-permute-start.12) | collective-permute-done | bytes 131104 | tf_op jit(solution)/shard_map/ppermute | solution.py:20
  42.3 1.5 %collective-permute-done.11.refs_1_ = f32[256,128]{1,0:T(8,128)S(1)} collective-permute-done((f32[256,128]{1,0:T(8,128)S(1)}, f32[256,128]{1,0:T(8,128)S(1)}, u32[]{:S(2)}, u32[]{:S(2)}) %collective-permute-start.11) | collective-permute-done | bytes 131104 | tf_op jit(solution)/shard_map/ppermute | solution.py:20
  43.9 1.6 %collective-permute-start.14 = (bf16[256,128]{1,0:T(8,128)(2,1)S(1)}, bf16[256,128]{1,0:T(8,128)(2,1)S(1)}, u32[]{:S(2)}, u32[]{:S(2)}) collective-permute-start(bf16[256,128]{1,0:T(8,128)(2,1)S(1)} %cotangent.1), channel_id=1, source_target_pairs={{0,2},{1,3},{2,0},{3,1},{4,6},{5,7},{6,4},{7,5},{8,10},{9,11},{10,... | collective-permute-start | bytes 196616 | tf_op jit(solution)/shard_map/ppermute | solution.py:20
  45.4 0.9 %collective-permute-start.13 = (bf16[256,128]{1,0:T(8,128)(2,1)S(1)}, bf16[256,128]{1,0:T(8,128)(2,1)S(1)}, u32[]{:S(2)}, u32[]{:S(2)}) collective-permute-start(bf16[256,128]{1,0:T(8,128)(2,1)S(1)} %cotangent.1), channel_id=1, source_target_pairs={{0,4},{4,0},{8,12},{12,8},{1,5},{5,1},{9,13},{13,9},{2,6},{6,2},{1... | collective-permute-start | bytes 196616 | tf_op jit(solution)/shard_map/ppermute | solution.py:20
  46.3 1.5 %collective-permute-start.15 = (bf16[256,128]{1,0:T(8,128)(2,1)S(1)}, bf16[256,128]{1,0:T(8,128)(2,1)S(1)}, u32[]{:S(2)}, u32[]{:S(2)}) collective-permute-start(bf16[256,128]{1,0:T(8,128)(2,1)S(1)} %cotangent.1), channel_id=1, source_target_pairs={{0,8},{4,12},{8,0},{12,4},{1,9},{5,13},{9,1},{13,5},{2,10},{6,14},... | collective-permute-start | bytes 196616 | tf_op jit(solution)/shard_map/ppermute | solution.py:20
  48.2 4.9 %collective-permute-done.14 = bf16[256,128]{1,0:T(8,128)(2,1)S(1)} collective-permute-done((bf16[256,128]{1,0:T(8,128)(2,1)S(1)}, bf16[256,128]{1,0:T(8,128)(2,1)S(1)}, u32[]{:S(2)}, u32[]{:S(2)}) %collective-permute-start.14) | collective-permute-done | bytes 65568 | tf_op jit(solution)/shard_map/ppermute | solution.py:20
  53.2 2.1 %collective-permute-start.16 = (bf16[256,128]{1,0:T(8,128)(2,1)S(1)}, bf16[256,128]{1,0:T(8,128)(2,1)S(1)}, u32[]{:S(2)}, u32[]{:S(2)}) collective-permute-start(bf16[256,128]{1,0:T(8,128)(2,1)S(1)} %collective-permute-done.15), channel_id=1, source_target_pairs={{0,4},{4,0},{8,12},{12,8},{1,5},{5,1},{9,13},{13,9},{2,6},{6,2},{1... | collective-permute-start | bytes 196616 | tf_op jit(solution)/shard_map/ppermute | solution.py:20
  55.5 2.4 %collective-permute-done.16 = bf16[256,128]{1,0:T(8,128)(2,1)S(1)} collective-permute-done((bf16[256,128]{1,0:T(8,128)(2,1)S(1)}, bf16[256,128]{1,0:T(8,128)(2,1)S(1)}, u32[]{:S(2)}, u32[]{:S(2)}) %collective-permute-start.16) | collective-permute-done | bytes 65568 | tf_op jit(solution)/shard_map/ppermute | solution.py:20
  58.6 1.5 %collective-permute-start.23 = (bf16[768,128]{1,0:T(8,128)(2,1)S(1)}, bf16[768,128]{1,0:T(8,128)(2,1)S(1)}, u32[]{:S(2)}, u32[]{:S(2)}) collective-permute-start(bf16[768,128]{1,0:T(8,128)(2,1)S(1)} %constant_dynamic-update-slice_fusion.2), channel_id=1, source_target_pairs={{0,2},{1,3},{2,0},{3,1},{4,6},{5,7},{6,4},{7,5},{8,10},{9,11},{10,... | collective-permute-start | bytes 589832 | tf_op jit(solution)/shard_map/ppermute | solution.py:20
  60.1 5.6 %backward.2 = (f32[512,512]{1,0:T(8,128)S(1)}, f32[512,128]{1,0:T(8,128)S(1)}, f32[512,128]{1,0:T(8,128)S(1)}, bf16[512,1024]{1,0:T(8,128)(2,1)S(1)}, bf16[512,1024]{1,0:T(8,128)(2,1)S(1)}) custom-call(bf16[512,512]{1,0:T(8,128)(2,1)S(1)} %get-tuple-element.38.refs_2_.refs_1_.refs_10_.pos_ref, bf16[512,128]{1,0:T(8,128)(2,1)S(1)} %get-tuple-element.39.coef_ref, ...), custom_call_target="tpu_custom_call" | custom-call | flops 17179869184 | bytes 1048576 | tf_op jit(solution)/shard_map/backward/pallas_call | solution.py:288
  65.9 1.3 %backward.3 = (f32[512,512]{1,0:T(8,128)S(1)}, f32[512,128]{1,0:T(8,128)S(1)}, f32[512,128]{1,0:T(8,128)S(1)}) custom-call(bf16[512,512]{1,0:T(8,128)(2,1)S(1)} %get-tuple-element.38.refs_2_.refs_1_.refs_10_.pos_ref, bf16[512,128]{1,0:T(8,128)(2,1)S(1)} %get-tuple-element.39.coef_ref, bf16[1,512]{1,0:T(2,128)(2,1)S(1)} %get-tuple-element.40.refs_11_.spread_ref, ...), custom_call_target="tpu_custom_call" | custom-call | flops 1 | bytes 1 | tf_op jit(solution)/shard_map/backward/pallas_call | solution.py:288
  67.4 2.3 %finish.1 = (f32[512,512]{1,0:T(8,128)}, f32[512,128]{1,0:T(8,128)}) custom-call(bf16[512,512]{1,0:T(8,128)(2,1)S(1)} %get-tuple-element.38.refs_2_.refs_1_.refs_10_.pos_ref, bf16[512,128]{1,0:T(8,128)(2,1)S(1)} %get-tuple-element.39.coef_ref, bf16[1,512]{1,0:T(2,128)(2,1)S(1)} %get-tuple-element.40.refs_11_.spread_ref, ...), custom_call_target="tpu_custom_call" | custom-call | flops 1 | bytes 1 | tf_op jit(solution)/shard_map/finish/pallas_call | solution.py:330
  (51 shorter events, 3.9 us)
Async XLA Ops:
  0.6 12.3 %copy-start = (bf16[1024,512]{1,0:T(8,128)(2,1)S(1)}, bf16[1024,512]{1,0:T(8,128)(2,1)}, u32[]{:S(2)}) copy-start(bf16[1024,512]{1,0:T(8,128)(2,1)} %refs_4_.1) | copy-start | bytes 3145732
  0.6 18.9 %collective-permute-start.5 = (bf16[512,512]{1,0:T(8,128)(2,1)}, bf16[512,512]{1,0:T(8,128)(2,1)S(1)}, u32[]{:S(2)}, u32[]{:S(2)}) collective-permute-start(bf16[512,512]{1,0:T(8,128)(2,1)} %pos_ref), channel_id=1, source_target_pairs={{0,2},{1,3},{2,0},{3,1},{4,6},{5,7},{6,4},{7,5},{8,10},{9,11},{10,... | collective-permute-start | bytes 1572872 | tf_op jit(solution)/shard_map/ppermute | solution.py:20
  4.6 14.5 %collective-permute-start = (bf16[256,512]{1,0:T(8,128)(2,1)S(1)}, bf16[256,512]{1,0:T(8,128)(2,1)S(1)}, u32[]{:S(2)}, u32[]{:S(2)}) collective-permute-start(bf16[256,512]{1,0:T(8,128)(2,1)S(1)} %constant_dynamic-slice_fusion.refs_0_.refs_12_.refs_1_), channel_id=1, source_target_pairs={{0,8},{4,12},{8,0},{12,4},{1,9},{5,13},{9,1},{13,5},{2,10},{6,14},... | collective-permute-start | bytes 786440 | tf_op jit(solution)/shard_map/ppermute | solution.py:20
  7.3 12.2 %collective-permute-start.2 = (bf16[256,512]{1,0:T(8,128)(2,1)S(1)}, bf16[256,512]{1,0:T(8,128)(2,1)S(1)}, u32[]{:S(2)}, u32[]{:S(2)}) collective-permute-start(bf16[256,512]{1,0:T(8,128)(2,1)S(1)} %constant_dynamic-slice_fusion.refs_0_.refs_12_.refs_1_), channel_id=1, source_target_pairs={{0,4},{4,0},{8,12},{12,8},{1,5},{5,1},{9,13},{13,9},{2,6},{6,2},{1... | collective-permute-start | bytes 786440 | tf_op jit(solution)/shard_map/ppermute | solution.py:20
  9.5 1.0 %copy-start.1 = (bf16[512,512]{1,0:T(8,128)(2,1)S(1)}, bf16[512,512]{1,0:T(8,128)(2,1)}, u32[]{:S(2)}) copy-start(bf16[512,512]{1,0:T(8,128)(2,1)} %pos_ref) | copy-start | bytes 1572868
  10.6 0.9 %copy-start.5 = (bf16[512,128]{1,0:T(8,128)(2,1)S(1)}, bf16[512,128]{1,0:T(8,128)(2,1)}, u32[]{:S(2)}) copy-start(bf16[512,128]{1,0:T(8,128)(2,1)} %coef_ref.1) | copy-start | bytes 393220
  11.5 0.7 copy-start.6
  12.3 6.6 %copy-start.2 = (bf16[512,512]{1,0:T(8,128)(2,1)S(1)}, bf16[512,512]{1,0:T(8,128)(2,1)}, u32[]{:S(2)}) copy-start(bf16[512,512]{1,0:T(8,128)(2,1)} %pos_ref) | copy-start | bytes 1572868
  12.4 6.6 %collective-permute-start.6 = (bf16[144,512]{1,0:T(8,128)(2,1)S(1)}, bf16[144,512]{1,0:T(8,128)(2,1)S(1)}, u32[]{:S(2)}, u32[]{:S(2)}) collective-permute-start(bf16[144,512]{1,0:T(8,128)(2,1)S(1)} %get-tuple-element.41.refs_3_.refs_2_), channel_id=1, source_target_pairs={{0,2},{1,3},{2,0},{3,1},{4,6},{5,7},{6,4},{7,5},{8,10},{9,11},{10,... | collective-permute-start | bytes 442376 | tf_op jit(solution)/shard_map/ppermute | solution.py:20
  13.0 6.0 %collective-permute-start.4 = (bf16[144,512]{1,0:T(8,128)(2,1)S(1)}, bf16[144,512]{1,0:T(8,128)(2,1)S(1)}, u32[]{:S(2)}, u32[]{:S(2)}) collective-permute-start(bf16[144,512]{1,0:T(8,128)(2,1)S(1)} %get-tuple-element.41.refs_3_.refs_2_), channel_id=1, source_target_pairs={{0,1},{1,0},{2,3},{3,2},{4,5},{5,4},{6,7},{7,6},{8,9},{9,8},{10,11... | collective-permute-start | bytes 442376 | tf_op jit(solution)/shard_map/ppermute | solution.py:20
  13.0 1.0 %copy-start.3 = (f32[1024,128]{1,0:T(8,128)S(1)}, f32[1024,128]{1,0:T(8,128)}, u32[]{:S(2)}) copy-start(f32[1024,128]{1,0:T(8,128)} %refs_0_.1) | copy-start | bytes 1572868
  14.0 1.0 %copy-start.4 = (f32[1024,128]{1,0:T(8,128)S(1)}, f32[1024,128]{1,0:T(8,128)}, u32[]{:S(2)}) copy-start(f32[1024,128]{1,0:T(8,128)} %refs_1_.1) | copy-start | bytes 1572868
  18.9 4.1 %collective-permute-start.3 = (bf16[512,512]{1,0:T(8,128)(2,1)S(1)}, bf16[512,512]{1,0:T(8,128)(2,1)S(1)}, u32[]{:S(2)}, u32[]{:S(2)}) collective-permute-start(bf16[512,512]{1,0:T(8,128)(2,1)S(1)} %copy-done.2), channel_id=1, source_target_pairs={{0,1},{1,0},{2,3},{3,2},{4,5},{5,4},{6,7},{7,6},{8,9},{9,8},{10,11... | collective-permute-start | bytes 1572872 | tf_op jit(solution)/shard_map/ppermute | solution.py:20
  19.1 2.0 %collective-permute-start.8 = (bf16[144,512]{1,0:T(8,128)(2,1)S(1)}, bf16[144,512]{1,0:T(8,128)(2,1)S(1)}, u32[]{:S(2)}, u32[]{:S(2)}) collective-permute-start(bf16[144,512]{1,0:T(8,128)(2,1)S(1)} %collective-permute-done.6.refs_7_.refs_6_), channel_id=1, source_target_pairs={{0,1},{1,0},{2,3},{3,2},{4,5},{5,4},{6,7},{7,6},{8,9},{9,8},{10,11... | collective-permute-start | bytes 442376 | tf_op jit(solution)/shard_map/ppermute | solution.py:20
  19.5 3.5 %collective-permute-start.7 = (bf16[512,512]{1,0:T(8,128)(2,1)S(1)}, bf16[512,512]{1,0:T(8,128)(2,1)S(1)}, u32[]{:S(2)}, u32[]{:S(2)}) collective-permute-start(bf16[512,512]{1,0:T(8,128)(2,1)S(1)} %collective-permute-done.5.refs_6_.refs_5_), channel_id=1, source_target_pairs={{0,1},{1,0},{2,3},{3,2},{4,5},{5,4},{6,7},{7,6},{8,9},{9,8},{10,11... | collective-permute-start | bytes 1572872 | tf_op jit(solution)/shard_map/ppermute | solution.py:20
  21.1 11.6 %collective-permute-start.9 = (bf16[512,512]{1,0:T(8,128)(2,1)S(1)}, bf16[512,512]{1,0:T(8,128)(2,1)S(1)}, u32[]{:S(2)}, u32[]{:S(2)}) collective-permute-start(bf16[512,512]{1,0:T(8,128)(2,1)S(1)} %constant_dynamic-update-slice_fusion.refs_13_.refs_2_), channel_id=1, source_target_pairs={{0,1},{1,0},{2,3},{3,2},{4,5},{5,4},{6,7},{7,6},{8,9},{9,8},{10,11... | collective-permute-start | bytes 1572872 | tf_op jit(solution)/shard_map/ppermute | solution.py:20
  21.2 11.5 %collective-permute-start.1 = (bf16[256,512]{1,0:T(8,128)(2,1)S(1)}, bf16[256,512]{1,0:T(8,128)(2,1)S(1)}, u32[]{:S(2)}, u32[]{:S(2)}) collective-permute-start(bf16[256,512]{1,0:T(8,128)(2,1)S(1)} %collective-permute-done.refs_0_), channel_id=1, source_target_pairs={{0,4},{4,0},{8,12},{12,8},{1,5},{5,1},{9,13},{13,9},{2,6},{6,2},{1... | collective-permute-start | bytes 786440 | tf_op jit(solution)/shard_map/ppermute | solution.py:20
  25.3 13.1 %collective-permute-start.10 = (f32[256,128]{1,0:T(8,128)S(1)}, f32[256,128]{1,0:T(8,128)S(1)}, u32[]{:S(2)}, u32[]{:S(2)}) collective-permute-start(f32[256,128]{1,0:T(8,128)S(1)} %get-tuple-element.45), channel_id=1, source_target_pairs={{0,8},{4,12},{8,0},{12,4},{1,9},{5,13},{9,1},{13,5},{2,10},{6,14},... | collective-permute-start | bytes 393224 | tf_op jit(solution)/shard_map/ppermute | solution.py:20
  34.0 8.3 %collective-permute-start.12 = (f32[256,128]{1,0:T(8,128)S(1)}, f32[256,128]{1,0:T(8,128)S(1)}, u32[]{:S(2)}, u32[]{:S(2)}) collective-permute-start(f32[256,128]{1,0:T(8,128)S(1)} %forward.3), channel_id=1, source_target_pairs={{0,12},{4,8},{8,4},{12,0},{1,13},{5,9},{9,5},{13,1},{2,14},{6,10},... | collective-permute-start | bytes 393224 | tf_op jit(solution)/shard_map/ppermute | solution.py:20
  36.9 6.9 %collective-permute-start.11 = (f32[256,128]{1,0:T(8,128)S(1)}, f32[256,128]{1,0:T(8,128)S(1)}, u32[]{:S(2)}, u32[]{:S(2)}) collective-permute-start(f32[256,128]{1,0:T(8,128)S(1)} %get-tuple-element.46), channel_id=1, source_target_pairs={{0,4},{4,0},{8,12},{12,8},{1,5},{5,1},{9,13},{13,9},{2,6},{6,2},{1... | collective-permute-start | bytes 393224 | tf_op jit(solution)/shard_map/ppermute | solution.py:20
  36.9 18.4 %collective-permute-start.19 = (bf16[512,512]{1,0:T(8,128)(2,1)S(1)}, bf16[512,512]{1,0:T(8,128)(2,1)S(1)}, u32[]{:S(2)}, u32[]{:S(2)}) collective-permute-start(bf16[512,512]{1,0:T(8,128)(2,1)S(1)} %constant_dynamic-update-slice_fusion.refs_13_.refs_2_), channel_id=1, source_target_pairs={{0,2},{1,3},{2,0},{3,1},{4,6},{5,7},{6,4},{7,5},{8,10},{9,11},{10,... | collective-permute-start | bytes 1572872 | tf_op jit(solution)/shard_map/ppermute | solution.py:20
  43.9 9.3 %collective-permute-start.14 = (bf16[256,128]{1,0:T(8,128)(2,1)S(1)}, bf16[256,128]{1,0:T(8,128)(2,1)S(1)}, u32[]{:S(2)}, u32[]{:S(2)}) collective-permute-start(bf16[256,128]{1,0:T(8,128)(2,1)S(1)} %cotangent.1), channel_id=1, source_target_pairs={{0,2},{1,3},{2,0},{3,1},{4,6},{5,7},{6,4},{7,5},{8,10},{9,11},{10,... | collective-permute-start | bytes 196616 | tf_op jit(solution)/shard_map/ppermute | solution.py:20
  45.4 7.7 %collective-permute-start.13 = (bf16[256,128]{1,0:T(8,128)(2,1)S(1)}, bf16[256,128]{1,0:T(8,128)(2,1)S(1)}, u32[]{:S(2)}, u32[]{:S(2)}) collective-permute-start(bf16[256,128]{1,0:T(8,128)(2,1)S(1)} %cotangent.1), channel_id=1, source_target_pairs={{0,4},{4,0},{8,12},{12,8},{1,5},{5,1},{9,13},{13,9},{2,6},{6,2},{1... | collective-permute-start | bytes 196616 | tf_op jit(solution)/shard_map/ppermute | solution.py:20
  46.3 6.9 %collective-permute-start.15 = (bf16[256,128]{1,0:T(8,128)(2,1)S(1)}, bf16[256,128]{1,0:T(8,128)(2,1)S(1)}, u32[]{:S(2)}, u32[]{:S(2)}) collective-permute-start(bf16[256,128]{1,0:T(8,128)(2,1)S(1)} %cotangent.1), channel_id=1, source_target_pairs={{0,8},{4,12},{8,0},{12,4},{1,9},{5,13},{9,1},{13,5},{2,10},{6,14},... | collective-permute-start | bytes 196616 | tf_op jit(solution)/shard_map/ppermute | solution.py:20
  47.8 10.3 %collective-permute-start.20 = (bf16[256,512]{1,0:T(8,128)(2,1)S(1)}, bf16[256,512]{1,0:T(8,128)(2,1)S(1)}, u32[]{:S(2)}, u32[]{:S(2)}) collective-permute-start(bf16[256,512]{1,0:T(8,128)(2,1)S(1)} %collective-permute-done.1.refs_0_.refs_14_.refs_3_), channel_id=1, source_target_pairs={{0,2},{1,3},{2,0},{3,1},{4,6},{5,7},{6,4},{7,5},{8,10},{9,11},{10,... | collective-permute-start | bytes 786440 | tf_op jit(solution)/shard_map/ppermute | solution.py:20
  53.1 7.0 %collective-permute-start.17 = (bf16[256,512]{1,0:T(8,128)(2,1)S(1)}, bf16[256,512]{1,0:T(8,128)(2,1)S(1)}, u32[]{:S(2)}, u32[]{:S(2)}) collective-permute-start(bf16[256,512]{1,0:T(8,128)(2,1)S(1)} %collective-permute-done.1.refs_0_.refs_14_.refs_3_), channel_id=1, source_target_pairs={{0,1},{1,0},{2,3},{3,2},{4,5},{5,4},{6,7},{7,6},{8,9},{9,8},{10,11... | collective-permute-start | bytes 786440 | tf_op jit(solution)/shard_map/ppermute | solution.py:20
  53.2 4.8 %collective-permute-start.16 = (bf16[256,128]{1,0:T(8,128)(2,1)S(1)}, bf16[256,128]{1,0:T(8,128)(2,1)S(1)}, u32[]{:S(2)}, u32[]{:S(2)}) collective-permute-start(bf16[256,128]{1,0:T(8,128)(2,1)S(1)} %collective-permute-done.15), channel_id=1, source_target_pairs={{0,4},{4,0},{8,12},{12,8},{1,5},{5,1},{9,13},{13,9},{2,6},{6,2},{1... | collective-permute-start | bytes 196616 | tf_op jit(solution)/shard_map/ppermute | solution.py:20
  55.3 4.9 %collective-permute-start.21 = (bf16[512,512]{1,0:T(8,128)(2,1)S(1)}, bf16[512,512]{1,0:T(8,128)(2,1)S(1)}, u32[]{:S(2)}, u32[]{:S(2)}) collective-permute-start(bf16[512,512]{1,0:T(8,128)(2,1)S(1)} %collective-permute-done.19.refs_10_.refs_2_), channel_id=1, source_target_pairs={{0,1},{1,0},{2,3},{3,2},{4,5},{5,4},{6,7},{7,6},{8,9},{9,8},{10,11... | collective-permute-start | bytes 1572872 | tf_op jit(solution)/shard_map/ppermute | solution.py:20
  58.0 2.2 %collective-permute-start.18 = (bf16[1024,128]{1,0:T(8,128)(2,1)S(1)}, bf16[1024,128]{1,0:T(8,128)(2,1)S(1)}, u32[]{:S(2)}, u32[]{:S(2)}) collective-permute-start(bf16[1024,128]{1,0:T(8,128)(2,1)S(1)} %pad_maximum_fusion.refs_4_), channel_id=1, source_target_pairs={{0,1},{1,0},{2,3},{3,2},{4,5},{5,4},{6,7},{7,6},{8,9},{9,8},{10,11... | collective-permute-start | bytes 786440 | tf_op jit(solution)/shard_map/ppermute | solution.py:20
  58.1 2.1 %collective-permute-start.22 = (bf16[256,512]{1,0:T(8,128)(2,1)S(1)}, bf16[256,512]{1,0:T(8,128)(2,1)S(1)}, u32[]{:S(2)}, u32[]{:S(2)}) collective-permute-start(bf16[256,512]{1,0:T(8,128)(2,1)S(1)} %collective-permute-done.20.refs_11_.refs_3_), channel_id=1, source_target_pairs={{0,1},{1,0},{2,3},{3,2},{4,5},{5,4},{6,7},{7,6},{8,9},{9,8},{10,11... | collective-permute-start | bytes 786440 | tf_op jit(solution)/shard_map/ppermute | solution.py:20
  58.6 7.2 %collective-permute-start.23 = (bf16[768,128]{1,0:T(8,128)(2,1)S(1)}, bf16[768,128]{1,0:T(8,128)(2,1)S(1)}, u32[]{:S(2)}, u32[]{:S(2)}) collective-permute-start(bf16[768,128]{1,0:T(8,128)(2,1)S(1)} %constant_dynamic-update-slice_fusion.2), channel_id=1, source_target_pairs={{0,2},{1,3},{2,0},{3,1},{4,6},{5,7},{6,4},{7,5},{8,10},{9,11},{10,... | collective-permute-start | bytes 589832 | tf_op jit(solution)/shard_map/ppermute | solution.py:20
  65.8 1.6 %collective-permute-start.24 = (bf16[1024,128]{1,0:T(8,128)(2,1)S(1)}, bf16[1024,128]{1,0:T(8,128)(2,1)S(1)}, u32[]{:S(2)}, u32[]{:S(2)}) collective-permute-start(bf16[1024,128]{1,0:T(8,128)(2,1)S(1)} %constant_dynamic-update-slice_fusion.5.refs_4_), channel_id=1, source_target_pairs={{0,1},{1,0},{2,3},{3,2},{4,5},{5,4},{6,7},{7,6},{8,9},{9,8},{10,11... | collective-permute-start | bytes 786440 | tf_op jit(solution)/shard_map/ppermute | solution.py:20

commit v11 on v10

--- a/solution.py
+++ b/solution.py
@@ -401,8 +401,8 @@
             [[local[0], early[0], late[0]]],
         )
         for d in range(2, nc, 2):
-            early[d] = swap(after(early[0], last), "centers", nc, d)
-            late[d] = swap(after(late[0], parts[0]), "centers", nc, d)
+            early[d] = swap(after(early[0], side[d]), "centers", nc, d)
+            late[d] = swap(after(late[0], last, *soon), "centers", nc, d)
             early[d + 1] = swap(after(early[d], parts[0]), "centers", nc, 1)
         late[1] = swap(after(late[0], parts[0]), "centers", nc, 1)
         cot = cotangent([parts[0], *received], saved, target, delta)
@@ -410,7 +410,7 @@
         far = {dz: swap(cot, "points", nz, dz) for dz in range(2, nz, 2)}
         far[1] = swap(cot, "points", nz, 1)
         far.update({dz: swap(far[dz - 1], "points", nz, 1) for dz in range(3, nz, 2)})
-        ahead = {d: swap(cot, "centers", nc, d) for d in range(2, nc, 2)}
+        ahead = {d: swap(after(cot, late[d]), "centers", nc, d) for d in range(2, nc, 2)}
         far[1] = after(far[1], *ahead.values())
         far = jnp.concatenate([far[dz] for dz in range(1, nz)])
         cots = {0: jnp.concatenate([cot, far])}

time: 70.1 us -> 66 us (0.942)
  waiting for transfers between devices: 20.4 us -> 10.6 us
  starting transfers between devices: 26.3 us -> 32 us
    ppermute x25, waiting for transfers between devices: 20.4 us -> 10.6 us  [swap(): return lax.ppermute(a, axis, [(i, i ^ d) for i in range(size)])]
    ppermute x25, starting transfers between devices: 26.3 us -> 32 us  [swap(): return lax.ppermute(a, axis, [(i, i ^ d) for i in range(size)])]
  transfers between devices with their start and end apart: 25 -> 25, of which waited for: 9 -> 9; matrix products, arithmetic and copies ran while one was open for 2% -> 3% of each run, Pallas kernels for 19% -> 21%
where the time goes in v11:
time: 66 us; the launch traced here: 65.7 us
  starting transfers between devices  32 us (48%)
  Pallas kernels  15.8 us (24%)
  waiting for transfers between devices  10.6 us (16%)
  local copies, waits for them, and re-layouts  6.44 us (10%)
  between operations  0.81 us (1%)
    ppermute x25, starting transfers between devices, swap(): return lax.ppermute(a, axis, [(i, i ^ d) for i in range(size)])  32 us
    ppermute x25, waiting for transfers between devices, swap(): return lax.ppermute(a, axis, [(i, i ^ d) for i in range(size)])  10.6 us
    pallas_call x2, Pallas kernels, backward(): pl.pallas_call(body, out_shape=tuple((jax.ShapeDtypeStruct((n, width), F3...  6.97 us
    unnamed x18, local copies, waits for them, and re-layouts  4.74 us
    pallas_call x2, Pallas kernels, forward(): pl.pallas_call(body, out_shape=tuple((jax.ShapeDtypeStruct((count, out_wi...  3.56 us
    pallas_call x1, Pallas kernels, finish(): pl.pallas_call(body, out_shape=tuple((jax.ShapeDtypeStruct((n, width), F3...  2.31 us
    pallas_call x1, Pallas kernels, own_rows(): pl.pallas_call(body, out_shape=(jax.ShapeDtypeStruct((rows.shape[0], out_...  2.28 us
  transfers between devices with their start and end apart: 25, of which 9 were waited for; matrix products, arithmetic and copies ran while one was open for 3% of the time, Pallas kernels for 21%

profile of v11, /device:TPU:0, one launch (start us, length us, event | category | flops | bytes accessed | tf_op | source)
XLA Modules:
  0.0 65.7 jit_solution(4023034797641409502)
XLA Ops:
  0.6 3.0 %collective-permute-start.5 = (bf16[512,512]{1,0:T(8,128)(2,1)}, bf16[512,512]{1,0:T(8,128)(2,1)S(1)}, u32[]{:S(2)}, u32[]{:S(2)}) collective-permute-start(bf16[512,512]{1,0:T(8,128)(2,1)} %pos_ref), channel_id=1, source_target_pairs={{0,2},{1,3},{2,0},{3,1},{4,6},{5,7},{6,4},{7,5},{8,10},{9,11},{10,... | collective-permute-start | bytes 1572872 | tf_op jit(solution)/shard_map/ppermute | solution.py:20
  3.6 1.0 %constant_dynamic-slice_fusion.refs_0_.refs_12_.refs_1_ = bf16[256,512]{1,0:T(8,128)(2,1)S(1)} fusion(bf16[1024,512]{1,0:T(8,128)(2,1)} %refs_4_.1, s32[]{:T(128)S(6)} %select_n.3), kind=kLoop, calls=%fused_computation.8 | loop fusion | bytes 524292 | tf_op jit(solution)/shard_map/dynamic_slice | solution.py:354
  4.6 2.7 %collective-permute-start = (bf16[256,512]{1,0:T(8,128)(2,1)S(1)}, bf16[256,512]{1,0:T(8,128)(2,1)S(1)}, u32[]{:S(2)}, u32[]{:S(2)}) collective-permute-start(bf16[256,512]{1,0:T(8,128)(2,1)S(1)} %constant_dynamic-slice_fusion.refs_0_.refs_12_.refs_1_), channel_id=1, source_target_pairs={{0,8},{4,12},{8,0},{12,4},{1,9},{5,13},{9,1},{13,5},{2,10},{6,14},... | collective-permute-start | bytes 786440 | tf_op jit(solution)/shard_map/ppermute | solution.py:20
  7.3 1.6 %collective-permute-start.2 = (bf16[256,512]{1,0:T(8,128)(2,1)S(1)}, bf16[256,512]{1,0:T(8,128)(2,1)S(1)}, u32[]{:S(2)}, u32[]{:S(2)}) collective-permute-start(bf16[256,512]{1,0:T(8,128)(2,1)S(1)} %constant_dynamic-slice_fusion.refs_0_.refs_12_.refs_1_), channel_id=1, source_target_pairs={{0,4},{4,0},{8,12},{12,8},{1,5},{5,1},{9,13},{13,9},{2,6},{6,2},{1... | collective-permute-start | bytes 786440 | tf_op jit(solution)/shard_map/ppermute | solution.py:20
  8.8 0.7 %reshape.10.spread_ref = bf16[1,512]{1,0:T(2,128)(2,1)S(1)} reshape(bf16[512]{0:T(512)(128)(2,1)} %param.13) | data formatting | bytes 2048 | tf_op jit(solution)/shard_map/reshape | solution.py:90
  9.5 1.0 %copy-done.1 = bf16[512,512]{1,0:T(8,128)(2,1)S(1)} copy-done((bf16[512,512]{1,0:T(8,128)(2,1)S(1)}, bf16[512,512]{1,0:T(8,128)(2,1)}, u32[]{:S(2)}) %copy-start.1) | copy-done | bytes 524312
  10.6 0.9 %copy-done.5 = bf16[512,128]{1,0:T(8,128)(2,1)S(1)} copy-done((bf16[512,128]{1,0:T(8,128)(2,1)S(1)}, bf16[512,128]{1,0:T(8,128)(2,1)}, u32[]{:S(2)}) %copy-start.5) | copy-done | bytes 131096
  11.5 0.7 copy-done.6
  12.4 0.6 collective-permute-start.6
  13.0 1.0 %copy-done.3 = f32[1024,128]{1,0:T(8,128)S(1)} copy-done((f32[1024,128]{1,0:T(8,128)S(1)}, f32[1024,128]{1,0:T(8,128)}, u32[]{:S(2)}) %copy-start.3) | copy-done | bytes 524312
  14.0 1.0 %copy-done.4 = f32[1024,128]{1,0:T(8,128)S(1)} copy-done((f32[1024,128]{1,0:T(8,128)S(1)}, f32[1024,128]{1,0:T(8,128)}, u32[]{:S(2)}) %copy-start.4) | copy-done | bytes 524312
  15.5 3.5 %collective-permute-done.6.refs_7_.refs_6_ = bf16[144,512]{1,0:T(8,128)(2,1)S(1)} collective-permute-done((bf16[144,512]{1,0:T(8,128)(2,1)S(1)}, bf16[144,512]{1,0:T(8,128)(2,1)S(1)}, u32[]{:S(2)}, u32[]{:S(2)}) %collective-permute-start.6) | collective-permute-done | bytes 147488 | tf_op jit(solution)/shard_map/ppermute | solution.py:20
  19.7 1.4 %collective-permute-done.8.refs_9_.refs_8_ = bf16[144,512]{1,0:T(8,128)(2,1)S(1)} collective-permute-done((bf16[144,512]{1,0:T(8,128)(2,1)S(1)}, bf16[144,512]{1,0:T(8,128)(2,1)S(1)}, u32[]{:S(2)}, u32[]{:S(2)}) %collective-permute-start.8) | collective-permute-done | bytes 147488 | tf_op jit(solution)/shard_map/ppermute | solution.py:20
  21.2 1.8 %collective-permute-start.1 = (bf16[256,512]{1,0:T(8,128)(2,1)S(1)}, bf16[256,512]{1,0:T(8,128)(2,1)S(1)}, u32[]{:S(2)}, u32[]{:S(2)}) collective-permute-start(bf16[256,512]{1,0:T(8,128)(2,1)S(1)} %collective-permute-done.refs_0_), channel_id=1, source_target_pairs={{0,4},{4,0},{8,12},{12,8},{1,5},{5,1},{9,13},{13,9},{2,6},{6,2},{1... | collective-permute-start | bytes 786440 | tf_op jit(solution)/shard_map/ppermute | solution.py:20
  23.0 1.5 %collective-permute-start.20 = (bf16[512,512]{1,0:T(8,128)(2,1)S(1)}, bf16[512,512]{1,0:T(8,128)(2,1)S(1)}, u32[]{:S(2)}, u32[]{:S(2)}) collective-permute-start(bf16[512,512]{1,0:T(8,128)(2,1)S(1)} %constant_dynamic-update-slice_fusion.refs_13_.refs_2_), channel_id=1, source_target_pairs={{0,2},{1,3},{2,0},{3,1},{4,6},{5,7},{6,4},{7,5},{8,10},{9,11},{10,... | collective-permute-start | bytes 1572872 | tf_op jit(solution)/shard_map/ppermute | solution.py:20
  24.5 2.2 %forward.2 = (f32[256,128]{1,0:T(8,128)S(1)}, f32[256,128]{1,0:T(8,128)S(1)}) custom-call(bf16[256,512]{1,0:T(8,128)(2,1)S(1)} %collective-permute-done.refs_0_, bf16[256,512]{1,0:T(8,128)(2,1)S(1)} %collective-permute-done.2.refs_1_, bf16[512,512]{1,0:T(8,128)(2,1)S(1)} %get-tuple-element.40.refs_2_.refs_1_.refs_10_.pos_ref, ...), custom_call_target="tpu_custom_call" | custom-call | flops 1 | bytes 1 | tf_op jit(solution)/shard_map/forward/pallas_call | solution.py:167
  26.8 2.7 %collective-permute-start.10 = (f32[256,128]{1,0:T(8,128)S(1)}, f32[256,128]{1,0:T(8,128)S(1)}, u32[]{:S(2)}, u32[]{:S(2)}) collective-permute-start(f32[256,128]{1,0:T(8,128)S(1)} %get-tuple-element.47), channel_id=1, source_target_pairs={{0,8},{4,12},{8,0},{12,4},{1,9},{5,13},{9,1},{13,5},{2,10},{6,14},... | collective-permute-start | bytes 393224 | tf_op jit(solution)/shard_map/ppermute | solution.py:20
  29.9 1.3 %forward.3 = f32[256,128]{1,0:T(8,128)S(1)} custom-call(bf16[256,512]{1,0:T(8,128)(2,1)S(1)} %collective-permute-done.1.refs_0_.refs_14_.refs_3_, bf16[512,512]{1,0:T(8,128)(2,1)S(1)} %get-tuple-element.40.refs_2_.refs_1_.refs_10_.pos_ref, bf16[144,512]{1,0:T(8,128)(2,1)S(1)} %get-tuple-element.43.refs_3_.refs_2_, ...), custom_call_target="tpu_custom_call" | custom-call | flops 17179869184 | bytes 1048576 | tf_op jit(solution)/shard_map/forward/pallas_call | solution.py:167
  31.2 4.9 %collective-permute-start.12 = (f32[256,128]{1,0:T(8,128)S(1)}, f32[256,128]{1,0:T(8,128)S(1)}, u32[]{:S(2)}, u32[]{:S(2)}) collective-permute-start(f32[256,128]{1,0:T(8,128)S(1)} %forward.3), channel_id=1, source_target_pairs={{0,12},{4,8},{8,4},{12,0},{1,13},{5,9},{9,5},{13,1},{2,14},{6,10},... | collective-permute-start | bytes 393224 | tf_op jit(solution)/shard_map/ppermute | solution.py:20
  36.5 1.8 %collective-permute-start.14 = (bf16[256,512]{1,0:T(8,128)(2,1)S(1)}, bf16[256,512]{1,0:T(8,128)(2,1)S(1)}, u32[]{:S(2)}, u32[]{:S(2)}) collective-permute-start(bf16[256,512]{1,0:T(8,128)(2,1)S(1)} %collective-permute-done.1.refs_0_.refs_14_.refs_3_), channel_id=1, source_target_pairs={{0,2},{1,3},{2,0},{3,1},{4,6},{5,7},{6,4},{7,5},{8,10},{9,11},{10,... | collective-permute-start | bytes 786440 | tf_op jit(solution)/shard_map/ppermute | solution.py:20
  38.3 2.3 %own_rows.1 = (f32[256,128]{1,0:T(8,128)S(1)}, bf16[512,1024]{1,0:T(8,128)(2,1)S(1)}) custom-call(bf16[256,512]{1,0:T(8,128)(2,1)S(1)} %constant_dynamic-slice_fusion.refs_0_.refs_12_.refs_1_, bf16[512,512]{1,0:T(8,128)(2,1)S(1)} %get-tuple-element.40.refs_2_.refs_1_.refs_10_.pos_ref, bf16[144,512]{1,0:T(8,128)(2,1)S(1)} %get-tuple-element.43.refs_3_.refs_2_, ...), custom_call_target="tpu_custom_call" | custom-call | flops 17179869184 | bytes 1048576 | tf_op jit(solution)/shard_map/own_rows/pallas_call | solution.py:214
  40.6 1.6 %collective-permute-done.11.refs_1_ = f32[256,128]{1,0:T(8,128)S(1)} collective-permute-done((f32[256,128]{1,0:T(8,128)S(1)}, f32[256,128]{1,0:T(8,128)S(1)}, u32[]{:S(2)}, u32[]{:S(2)}) %collective-permute-start.11) | collective-permute-done | bytes 131104 | tf_op jit(solution)/shard_map/ppermute | solution.py:20
  42.3 0.6 collective-permute-start.16
  42.9 2.3 %collective-permute-start.13 = (bf16[256,128]{1,0:T(8,128)(2,1)S(1)}, bf16[256,128]{1,0:T(8,128)(2,1)S(1)}, u32[]{:S(2)}, u32[]{:S(2)}) collective-permute-start(bf16[256,128]{1,0:T(8,128)(2,1)S(1)} %cotangent.1), channel_id=1, source_target_pairs={{0,4},{4,0},{8,12},{12,8},{1,5},{5,1},{9,13},{13,9},{2,6},{6,2},{1... | collective-permute-start | bytes 196616 | tf_op jit(solution)/shard_map/ppermute | solution.py:20
  45.2 2.3 %collective-permute-start.15 = (bf16[256,128]{1,0:T(8,128)(2,1)S(1)}, bf16[256,128]{1,0:T(8,128)(2,1)S(1)}, u32[]{:S(2)}, u32[]{:S(2)}) collective-permute-start(bf16[256,128]{1,0:T(8,128)(2,1)S(1)} %cotangent.1), channel_id=1, source_target_pairs={{0,2},{1,3},{2,0},{3,1},{4,6},{5,7},{6,4},{7,5},{8,10},{9,11},{10,... | collective-permute-start | bytes 196616 | tf_op jit(solution)/shard_map/ppermute | solution.py:20
  48.0 1.2 %collective-permute-start.17 = (bf16[256,128]{1,0:T(8,128)(2,1)S(1)}, bf16[256,128]{1,0:T(8,128)(2,1)S(1)}, u32[]{:S(2)}, u32[]{:S(2)}) collective-permute-start(bf16[256,128]{1,0:T(8,128)(2,1)S(1)} %collective-permute-done.16), channel_id=1, source_target_pairs={{0,4},{4,0},{8,12},{12,8},{1,5},{5,1},{9,13},{13,9},{2,6},{6,2},{1... | collective-permute-start | bytes 196616 | tf_op jit(solution)/shard_map/ppermute | solution.py:20
  49.7 2.5 %collective-permute-done.17 = bf16[256,128]{1,0:T(8,128)(2,1)S(1)} collective-permute-done((bf16[256,128]{1,0:T(8,128)(2,1)S(1)}, bf16[256,128]{1,0:T(8,128)(2,1)S(1)}, u32[]{:S(2)}, u32[]{:S(2)}) %collective-permute-start.17) | collective-permute-done | bytes 65568 | tf_op jit(solution)/shard_map/ppermute | solution.py:20
  52.4 0.6 collective-permute-start.19
  52.9 3.1 %collective-permute-start.23 = (bf16[768,128]{1,0:T(8,128)(2,1)S(1)}, bf16[768,128]{1,0:T(8,128)(2,1)S(1)}, u32[]{:S(2)}, u32[]{:S(2)}) collective-permute-start(bf16[768,128]{1,0:T(8,128)(2,1)S(1)} %constant_dynamic-update-slice_fusion.2), channel_id=1, source_target_pairs={{0,2},{1,3},{2,0},{3,1},{4,6},{5,7},{6,4},{7,5},{8,10},{9,11},{10,... | collective-permute-start | bytes 589832 | tf_op jit(solution)/shard_map/ppermute | solution.py:20
  56.1 5.7 %backward.2 = (f32[512,512]{1,0:T(8,128)S(1)}, f32[512,128]{1,0:T(8,128)S(1)}, f32[512,128]{1,0:T(8,128)S(1)}, bf16[512,1024]{1,0:T(8,128)(2,1)S(1)}, bf16[512,1024]{1,0:T(8,128)(2,1)S(1)}) custom-call(bf16[512,512]{1,0:T(8,128)(2,1)S(1)} %get-tuple-element.40.refs_2_.refs_1_.refs_10_.pos_ref, bf16[512,128]{1,0:T(8,128)(2,1)S(1)} %get-tuple-element.41.coef_ref, ...), custom_call_target="tpu_custom_call" | custom-call | flops 17179869184 | bytes 1048576 | tf_op jit(solution)/shard_map/backward/pallas_call | solution.py:288
  61.9 1.3 %backward.3 = (f32[512,512]{1,0:T(8,128)S(1)}, f32[512,128]{1,0:T(8,128)S(1)}, f32[512,128]{1,0:T(8,128)S(1)}) custom-call(bf16[512,512]{1,0:T(8,128)(2,1)S(1)} %get-tuple-element.40.refs_2_.refs_1_.refs_10_.pos_ref, bf16[512,128]{1,0:T(8,128)(2,1)S(1)} %get-tuple-element.41.coef_ref, bf16[1,512]{1,0:T(2,128)(2,1)S(1)} %get-tuple-element.42.refs_11_.spread_ref, ...), custom_call_target="tpu_custom_call" | custom-call | flops 1 | bytes 1 | tf_op jit(solution)/shard_map/backward/pallas_call | solution.py:288
  63.4 2.3 %finish.1 = (f32[512,512]{1,0:T(8,128)}, f32[512,128]{1,0:T(8,128)}) custom-call(bf16[512,512]{1,0:T(8,128)(2,1)S(1)} %get-tuple-element.40.refs_2_.refs_1_.refs_10_.pos_ref, bf16[512,128]{1,0:T(8,128)(2,1)S(1)} %get-tuple-element.41.coef_ref, bf16[1,512]{1,0:T(2,128)(2,1)S(1)} %get-tuple-element.42.refs_11_.spread_ref, ...), custom_call_target="tpu_custom_call" | custom-call | flops 1 | bytes 1 | tf_op jit(solution)/shard_map/finish/pallas_call | solution.py:330
  (51 shorter events, 3.9 us)
Async XLA Ops:
  0.6 12.3 %copy-start = (bf16[1024,512]{1,0:T(8,128)(2,1)S(1)}, bf16[1024,512]{1,0:T(8,128)(2,1)}, u32[]{:S(2)}) copy-start(bf16[1024,512]{1,0:T(8,128)(2,1)} %refs_4_.1) | copy-start | bytes 3145732
  0.6 18.9 %collective-permute-start.5 = (bf16[512,512]{1,0:T(8,128)(2,1)}, bf16[512,512]{1,0:T(8,128)(2,1)S(1)}, u32[]{:S(2)}, u32[]{:S(2)}) collective-permute-start(bf16[512,512]{1,0:T(8,128)(2,1)} %pos_ref), channel_id=1, source_target_pairs={{0,2},{1,3},{2,0},{3,1},{4,6},{5,7},{6,4},{7,5},{8,10},{9,11},{10,... | collective-permute-start | bytes 1572872 | tf_op jit(solution)/shard_map/ppermute | solution.py:20
  4.6 14.5 %collective-permute-start = (bf16[256,512]{1,0:T(8,128)(2,1)S(1)}, bf16[256,512]{1,0:T(8,128)(2,1)S(1)}, u32[]{:S(2)}, u32[]{:S(2)}) collective-permute-start(bf16[256,512]{1,0:T(8,128)(2,1)S(1)} %constant_dynamic-slice_fusion.refs_0_.refs_12_.refs_1_), channel_id=1, source_target_pairs={{0,8},{4,12},{8,0},{12,4},{1,9},{5,13},{9,1},{13,5},{2,10},{6,14},... | collective-permute-start | bytes 786440 | tf_op jit(solution)/shard_map/ppermute | solution.py:20
  7.3 12.2 %collective-permute-start.2 = (bf16[256,512]{1,0:T(8,128)(2,1)S(1)}, bf16[256,512]{1,0:T(8,128)(2,1)S(1)}, u32[]{:S(2)}, u32[]{:S(2)}) collective-permute-start(bf16[256,512]{1,0:T(8,128)(2,1)S(1)} %constant_dynamic-slice_fusion.refs_0_.refs_12_.refs_1_), channel_id=1, source_target_pairs={{0,4},{4,0},{8,12},{12,8},{1,5},{5,1},{9,13},{13,9},{2,6},{6,2},{1... | collective-permute-start | bytes 786440 | tf_op jit(solution)/shard_map/ppermute | solution.py:20
  9.5 1.0 %copy-start.1 = (bf16[512,512]{1,0:T(8,128)(2,1)S(1)}, bf16[512,512]{1,0:T(8,128)(2,1)}, u32[]{:S(2)}) copy-start(bf16[512,512]{1,0:T(8,128)(2,1)} %pos_ref) | copy-start | bytes 1572868
  10.6 0.9 %copy-start.5 = (bf16[512,128]{1,0:T(8,128)(2,1)S(1)}, bf16[512,128]{1,0:T(8,128)(2,1)}, u32[]{:S(2)}) copy-start(bf16[512,128]{1,0:T(8,128)(2,1)} %coef_ref.1) | copy-start | bytes 393220
  11.5 0.7 copy-start.6
  12.3 6.6 %copy-start.2 = (bf16[512,512]{1,0:T(8,128)(2,1)S(1)}, bf16[512,512]{1,0:T(8,128)(2,1)}, u32[]{:S(2)}) copy-start(bf16[512,512]{1,0:T(8,128)(2,1)} %pos_ref) | copy-start | bytes 1572868
  12.4 6.6 %collective-permute-start.6 = (bf16[144,512]{1,0:T(8,128)(2,1)S(1)}, bf16[144,512]{1,0:T(8,128)(2,1)S(1)}, u32[]{:S(2)}, u32[]{:S(2)}) collective-permute-start(bf16[144,512]{1,0:T(8,128)(2,1)S(1)} %get-tuple-element.43.refs_3_.refs_2_), channel_id=1, source_target_pairs={{0,2},{1,3},{2,0},{3,1},{4,6},{5,7},{6,4},{7,5},{8,10},{9,11},{10,... | collective-permute-start | bytes 442376 | tf_op jit(solution)/shard_map/ppermute | solution.py:20
  13.0 6.0 %collective-permute-start.4 = (bf16[144,512]{1,0:T(8,128)(2,1)S(1)}, bf16[144,512]{1,0:T(8,128)(2,1)S(1)}, u32[]{:S(2)}, u32[]{:S(2)}) collective-permute-start(bf16[144,512]{1,0:T(8,128)(2,1)S(1)} %get-tuple-element.43.refs_3_.refs_2_), channel_id=1, source_target_pairs={{0,1},{1,0},{2,3},{3,2},{4,5},{5,4},{6,7},{7,6},{8,9},{9,8},{10,11... | collective-permute-start | bytes 442376 | tf_op jit(solution)/shard_map/ppermute | solution.py:20
  13.0 1.0 %copy-start.3 = (f32[1024,128]{1,0:T(8,128)S(1)}, f32[1024,128]{1,0:T(8,128)}, u32[]{:S(2)}) copy-start(f32[1024,128]{1,0:T(8,128)} %refs_0_.1) | copy-start | bytes 1572868
  14.0 1.0 %copy-start.4 = (f32[1024,128]{1,0:T(8,128)S(1)}, f32[1024,128]{1,0:T(8,128)}, u32[]{:S(2)}) copy-start(f32[1024,128]{1,0:T(8,128)} %refs_1_.1) | copy-start | bytes 1572868
  18.9 5.6 %collective-permute-start.3 = (bf16[512,512]{1,0:T(8,128)(2,1)S(1)}, bf16[512,512]{1,0:T(8,128)(2,1)S(1)}, u32[]{:S(2)}, u32[]{:S(2)}) collective-permute-start(bf16[512,512]{1,0:T(8,128)(2,1)S(1)} %copy-done.2), channel_id=1, source_target_pairs={{0,1},{1,0},{2,3},{3,2},{4,5},{5,4},{6,7},{7,6},{8,9},{9,8},{10,11... | collective-permute-start | bytes 1572872 | tf_op jit(solution)/shard_map/ppermute | solution.py:20
  19.1 2.0 %collective-permute-start.8 = (bf16[144,512]{1,0:T(8,128)(2,1)S(1)}, bf16[144,512]{1,0:T(8,128)(2,1)S(1)}, u32[]{:S(2)}, u32[]{:S(2)}) collective-permute-start(bf16[144,512]{1,0:T(8,128)(2,1)S(1)} %collective-permute-done.6.refs_7_.refs_6_), channel_id=1, source_target_pairs={{0,1},{1,0},{2,3},{3,2},{4,5},{5,4},{6,7},{7,6},{8,9},{9,8},{10,11... | collective-permute-start | bytes 442376 | tf_op jit(solution)/shard_map/ppermute | solution.py:20
  19.5 5.0 %collective-permute-start.7 = (bf16[512,512]{1,0:T(8,128)(2,1)S(1)}, bf16[512,512]{1,0:T(8,128)(2,1)S(1)}, u32[]{:S(2)}, u32[]{:S(2)}) collective-permute-start(bf16[512,512]{1,0:T(8,128)(2,1)S(1)} %collective-permute-done.5.refs_6_.refs_5_), channel_id=1, source_target_pairs={{0,1},{1,0},{2,3},{3,2},{4,5},{5,4},{6,7},{7,6},{8,9},{9,8},{10,11... | collective-permute-start | bytes 1572872 | tf_op jit(solution)/shard_map/ppermute | solution.py:20
  21.1 8.8 %collective-permute-start.9 = (bf16[512,512]{1,0:T(8,128)(2,1)S(1)}, bf16[512,512]{1,0:T(8,128)(2,1)S(1)}, u32[]{:S(2)}, u32[]{:S(2)}) collective-permute-start(bf16[512,512]{1,0:T(8,128)(2,1)S(1)} %constant_dynamic-update-slice_fusion.refs_13_.refs_2_), channel_id=1, source_target_pairs={{0,1},{1,0},{2,3},{3,2},{4,5},{5,4},{6,7},{7,6},{8,9},{9,8},{10,11... | collective-permute-start | bytes 1572872 | tf_op jit(solution)/shard_map/ppermute | solution.py:20
  21.2 8.7 %collective-permute-start.1 = (bf16[256,512]{1,0:T(8,128)(2,1)S(1)}, bf16[256,512]{1,0:T(8,128)(2,1)S(1)}, u32[]{:S(2)}, u32[]{:S(2)}) collective-permute-start(bf16[256,512]{1,0:T(8,128)(2,1)S(1)} %collective-permute-done.refs_0_), channel_id=1, source_target_pairs={{0,4},{4,0},{8,12},{12,8},{1,5},{5,1},{9,13},{13,9},{2,6},{6,2},{1... | collective-permute-start | bytes 786440 | tf_op jit(solution)/shard_map/ppermute | solution.py:20
  23.0 24.4 %collective-permute-start.20 = (bf16[512,512]{1,0:T(8,128)(2,1)S(1)}, bf16[512,512]{1,0:T(8,128)(2,1)S(1)}, u32[]{:S(2)}, u32[]{:S(2)}) collective-permute-start(bf16[512,512]{1,0:T(8,128)(2,1)S(1)} %constant_dynamic-update-slice_fusion.refs_13_.refs_2_), channel_id=1, source_target_pairs={{0,2},{1,3},{2,0},{3,1},{4,6},{5,7},{6,4},{7,5},{8,10},{9,11},{10,... | collective-permute-start | bytes 1572872 | tf_op jit(solution)/shard_map/ppermute | solution.py:20
  26.8 9.7 %collective-permute-start.10 = (f32[256,128]{1,0:T(8,128)S(1)}, f32[256,128]{1,0:T(8,128)S(1)}, u32[]{:S(2)}, u32[]{:S(2)}) collective-permute-start(f32[256,128]{1,0:T(8,128)S(1)} %get-tuple-element.47), channel_id=1, source_target_pairs={{0,8},{4,12},{8,0},{12,4},{1,9},{5,13},{9,1},{13,5},{2,10},{6,14},... | collective-permute-start | bytes 393224 | tf_op jit(solution)/shard_map/ppermute | solution.py:20
  31.2 9.4 %collective-permute-start.12 = (f32[256,128]{1,0:T(8,128)S(1)}, f32[256,128]{1,0:T(8,128)S(1)}, u32[]{:S(2)}, u32[]{:S(2)}) collective-permute-start(f32[256,128]{1,0:T(8,128)S(1)} %forward.3), channel_id=1, source_target_pairs={{0,12},{4,8},{8,4},{12,0},{1,13},{5,9},{9,5},{13,1},{2,14},{6,10},... | collective-permute-start | bytes 393224 | tf_op jit(solution)/shard_map/ppermute | solution.py:20
  36.1 6.1 %collective-permute-start.11 = (f32[256,128]{1,0:T(8,128)S(1)}, f32[256,128]{1,0:T(8,128)S(1)}, u32[]{:S(2)}, u32[]{:S(2)}) collective-permute-start(f32[256,128]{1,0:T(8,128)S(1)} %get-tuple-element.48), channel_id=1, source_target_pairs={{0,4},{4,0},{8,12},{12,8},{1,5},{5,1},{9,13},{13,9},{2,6},{6,2},{1... | collective-permute-start | bytes 393224 | tf_op jit(solution)/shard_map/ppermute | solution.py:20
  36.5 8.7 %collective-permute-start.14 = (bf16[256,512]{1,0:T(8,128)(2,1)S(1)}, bf16[256,512]{1,0:T(8,128)(2,1)S(1)}, u32[]{:S(2)}, u32[]{:S(2)}) collective-permute-start(bf16[256,512]{1,0:T(8,128)(2,1)S(1)} %collective-permute-done.1.refs_0_.refs_14_.refs_3_), channel_id=1, source_target_pairs={{0,2},{1,3},{2,0},{3,1},{4,6},{5,7},{6,4},{7,5},{8,10},{9,11},{10,... | collective-permute-start | bytes 786440 | tf_op jit(solution)/shard_map/ppermute | solution.py:20
  42.3 5.7 %collective-permute-start.16 = (bf16[256,128]{1,0:T(8,128)(2,1)S(1)}, bf16[256,128]{1,0:T(8,128)(2,1)S(1)}, u32[]{:S(2)}, u32[]{:S(2)}) collective-permute-start(bf16[256,128]{1,0:T(8,128)(2,1)S(1)} %cotangent.1), channel_id=1, source_target_pairs={{0,8},{4,12},{8,0},{12,4},{1,9},{5,13},{9,1},{13,5},{2,10},{6,14},... | collective-permute-start | bytes 196616 | tf_op jit(solution)/shard_map/ppermute | solution.py:20
  42.9 6.3 %collective-permute-start.13 = (bf16[256,128]{1,0:T(8,128)(2,1)S(1)}, bf16[256,128]{1,0:T(8,128)(2,1)S(1)}, u32[]{:S(2)}, u32[]{:S(2)}) collective-permute-start(bf16[256,128]{1,0:T(8,128)(2,1)S(1)} %cotangent.1), channel_id=1, source_target_pairs={{0,4},{4,0},{8,12},{12,8},{1,5},{5,1},{9,13},{13,9},{2,6},{6,2},{1... | collective-permute-start | bytes 196616 | tf_op jit(solution)/shard_map/ppermute | solution.py:20
  45.2 4.5 %collective-permute-start.15 = (bf16[256,128]{1,0:T(8,128)(2,1)S(1)}, bf16[256,128]{1,0:T(8,128)(2,1)S(1)}, u32[]{:S(2)}, u32[]{:S(2)}) collective-permute-start(bf16[256,128]{1,0:T(8,128)(2,1)S(1)} %cotangent.1), channel_id=1, source_target_pairs={{0,2},{1,3},{2,0},{3,1},{4,6},{5,7},{6,4},{7,5},{8,10},{9,11},{10,... | collective-permute-start | bytes 196616 | tf_op jit(solution)/shard_map/ppermute | solution.py:20
  47.5 8.6 %collective-permute-start.18 = (bf16[256,512]{1,0:T(8,128)(2,1)S(1)}, bf16[256,512]{1,0:T(8,128)(2,1)S(1)}, u32[]{:S(2)}, u32[]{:S(2)}) collective-permute-start(bf16[256,512]{1,0:T(8,128)(2,1)S(1)} %collective-permute-done.1.refs_0_.refs_14_.refs_3_), channel_id=1, source_target_pairs={{0,1},{1,0},{2,3},{3,2},{4,5},{5,4},{6,7},{7,6},{8,9},{9,8},{10,11... | collective-permute-start | bytes 786440 | tf_op jit(solution)/shard_map/ppermute | solution.py:20
  47.5 8.6 %collective-permute-start.21 = (bf16[512,512]{1,0:T(8,128)(2,1)S(1)}, bf16[512,512]{1,0:T(8,128)(2,1)S(1)}, u32[]{:S(2)}, u32[]{:S(2)}) collective-permute-start(bf16[512,512]{1,0:T(8,128)(2,1)S(1)} %collective-permute-done.20.refs_10_.refs_2_), channel_id=1, source_target_pairs={{0,1},{1,0},{2,3},{3,2},{4,5},{5,4},{6,7},{7,6},{8,9},{9,8},{10,11... | collective-permute-start | bytes 1572872 | tf_op jit(solution)/shard_map/ppermute | solution.py:20
  48.0 4.3 %collective-permute-start.17 = (bf16[256,128]{1,0:T(8,128)(2,1)S(1)}, bf16[256,128]{1,0:T(8,128)(2,1)S(1)}, u32[]{:S(2)}, u32[]{:S(2)}) collective-permute-start(bf16[256,128]{1,0:T(8,128)(2,1)S(1)} %collective-permute-done.16), channel_id=1, source_target_pairs={{0,4},{4,0},{8,12},{12,8},{1,5},{5,1},{9,13},{13,9},{2,6},{6,2},{1... | collective-permute-start | bytes 196616 | tf_op jit(solution)/shard_map/ppermute | solution.py:20
  52.3 3.8 %collective-permute-start.22 = (bf16[256,512]{1,0:T(8,128)(2,1)S(1)}, bf16[256,512]{1,0:T(8,128)(2,1)S(1)}, u32[]{:S(2)}, u32[]{:S(2)}) collective-permute-start(bf16[256,512]{1,0:T(8,128)(2,1)S(1)} %collective-permute-done.14.refs_11_.refs_3_), channel_id=1, source_target_pairs={{0,1},{1,0},{2,3},{3,2},{4,5},{5,4},{6,7},{7,6},{8,9},{9,8},{10,11... | collective-permute-start | bytes 786440 | tf_op jit(solution)/shard_map/ppermute | solution.py:20
  52.4 3.7 %collective-permute-start.19 = (bf16[1024,128]{1,0:T(8,128)(2,1)S(1)}, bf16[1024,128]{1,0:T(8,128)(2,1)S(1)}, u32[]{:S(2)}, u32[]{:S(2)}) collective-permute-start(bf16[1024,128]{1,0:T(8,128)(2,1)S(1)} %pad_maximum_fusion.refs_4_), channel_id=1, source_target_pairs={{0,1},{1,0},{2,3},{3,2},{4,5},{5,4},{6,7},{7,6},{8,9},{9,8},{10,11... | collective-permute-start | bytes 786440 | tf_op jit(solution)/shard_map/ppermute | solution.py:20
  52.9 8.8 %collective-permute-start.23 = (bf16[768,128]{1,0:T(8,128)(2,1)S(1)}, bf16[768,128]{1,0:T(8,128)(2,1)S(1)}, u32[]{:S(2)}, u32[]{:S(2)}) collective-permute-start(bf16[768,128]{1,0:T(8,128)(2,1)S(1)} %constant_dynamic-update-slice_fusion.2), channel_id=1, source_target_pairs={{0,2},{1,3},{2,0},{3,1},{4,6},{5,7},{6,4},{7,5},{8,10},{9,11},{10,... | collective-permute-start | bytes 589832 | tf_op jit(solution)/shard_map/ppermute | solution.py:20
  61.8 1.6 %collective-permute-start.24 = (bf16[1024,128]{1,0:T(8,128)(2,1)S(1)}, bf16[1024,128]{1,0:T(8,128)(2,1)S(1)}, u32[]{:S(2)}, u32[]{:S(2)}) collective-permute-start(bf16[1024,128]{1,0:T(8,128)(2,1)S(1)} %constant_dynamic-update-slice_fusion.5.refs_4_), channel_id=1, source_target_pairs={{0,1},{1,0},{2,3},{3,2},{4,5},{5,4},{6,7},{7,6},{8,9},{9,8},{10,11... | collective-permute-start | bytes 786440 | tf_op jit(solution)/shard_map/ppermute | solution.py:20

commit v12 on v11

--- a/solution.py
+++ b/solution.py
@@ -374,18 +374,19 @@
         )
         local = [own, *local]
         for d in range(2, nc, 2):
-            pos[d + 1] = swap(after(pos[d], layer[1], saved), "centers", nc, 1)
+            pos[d + 1] = swap(after(pos[d], layer[1], layer[2], side[1], side[d], saved), "centers", nc, 1)
             side[d + 1] = swap(after(side[d], layer[2], side[1]), "centers", nc, 1)
         centers = [a for d in range(nc) for a in (pos[d], side[d])]
 
         early = {0: jnp.concatenate([layer[dz] for dz in range(1, nz - 1)])}
-        early[1] = swap(after(early[0], side[nc - 1]), "centers", nc, 1)
-
-        first, second = [*range(2, nz, 2), 1], range(3, nz, 2)
-        rows = [layer[dz] for dz in first]
-        parts = dict(zip(first, forward(rows, centers, out_width, BRIEF)))
-        rows = [after(layer[dz], *parts.values(), early[1]) for dz in second]
+
+        first, second = range(2, nz, 2), range(3, nz, 2)
+        parts = dict(zip(first, forward([layer[dz] for dz in first], centers, out_width, BRIEF)))
         received = {dz: swap(parts[dz], "points", nz, dz) for dz in first}
+        rows = [after(layer[1], *parts.values())]
+        (parts[1],) = forward(rows, centers, out_width, COVER)
+        received[1] = swap(parts[1], "points", nz, 1)
+        rows = [after(layer[dz], *parts.values()) for dz in second]
         parts.update(zip(second, forward(rows, centers, out_width, COVER)))
         soon = [received[dz] for dz in range(2, nz, 2)]
         received = [received[1]] + [swap(parts[dz], "points", nz, dz) for dz in second]
@@ -404,6 +405,7 @@
             early[d] = swap(after(early[0], side[d]), "centers", nc, d)
             late[d] = swap(after(late[0], last, *soon), "centers", nc, d)
             early[d + 1] = swap(after(early[d], parts[0]), "centers", nc, 1)
+        early[1] = swap(after(early[0], parts[0]), "centers", nc, 1)
         late[1] = swap(after(late[0], parts[0]), "centers", nc, 1)
         cot = cotangent([parts[0], *received], saved, target, delta)
 

time: 66 us -> 65.4 us (level)
  starting transfers between devices: 32 us -> 23.3 us
  waiting for transfers between devices: 10.6 us -> 18.2 us
    ppermute x25, starting transfers between devices: 32 us -> 23.3 us  [swap(): return lax.ppermute(a, axis, [(i, i ^ d) for i in range(size)])]
    ppermute x25, waiting for transfers between devices: 10.6 us -> 18.2 us  [swap(): return lax.ppermute(a, axis, [(i, i ^ d) for i in range(size)])]
    pallas_call x2 -> x3, Pallas kernels: 3.56 us -> 3.93 us  [forward(): pl.pallas_call(body, out_shape=tuple((jax.ShapeDtypeStruct((count, out_wi...]
where the time goes in v12:
time: 65.4 us; the launch traced here: 65.1 us
  starting transfers between devices  23.3 us (36%)
  waiting for transfers between devices  18.2 us (28%)
  Pallas kernels  16.2 us (25%)
  local copies, waits for them, and re-layouts  6.45 us (10%)
  between operations  0.82 us (1%)
    ppermute x25, starting transfers between devices, swap(): return lax.ppermute(a, axis, [(i, i ^ d) for i in range(size)])  23.3 us
    ppermute x25, waiting for transfers between devices, swap(): return lax.ppermute(a, axis, [(i, i ^ d) for i in range(size)])  18.2 us
    pallas_call x2, Pallas kernels, backward(): pl.pallas_call(body, out_shape=tuple((jax.ShapeDtypeStruct((n, width), F3...  6.98 us
    unnamed x18, local copies, waits for them, and re-layouts  4.74 us
    pallas_call x3, Pallas kernels, forward(): pl.pallas_call(body, out_shape=tuple((jax.ShapeDtypeStruct((count, out_wi...  3.93 us
    pallas_call x1, Pallas kernels, finish(): pl.pallas_call(body, out_shape=tuple((jax.ShapeDtypeStruct((n, width), F3...  2.32 us
    pallas_call x1, Pallas kernels, own_rows(): pl.pallas_call(body, out_shape=(jax.ShapeDtypeStruct((rows.shape[0], out_...  2.28 us
  transfers between devices with their start and end apart: 25, of which 9 were waited for; matrix products, arithmetic and copies ran while one was open for 3% of the time, Pallas kernels for 21%

profile of v12, /device:TPU:0, one launch (start us, length us, event | category | flops | bytes accessed | tf_op | source)
XLA Modules:
  0.0 65.1 jit_solution(11053752862093128206)
XLA Ops:
  0.6 3.0 %collective-permute-start.4 = (bf16[512,512]{1,0:T(8,128)(2,1)}, bf16[512,512]{1,0:T(8,128)(2,1)S(1)}, u32[]{:S(2)}, u32[]{:S(2)}) collective-permute-start(bf16[512,512]{1,0:T(8,128)(2,1)} %pos_ref), channel_id=1, source_target_pairs={{0,2},{1,3},{2,0},{3,1},{4,6},{5,7},{6,4},{7,5},{8,10},{9,11},{10,... | collective-permute-start | bytes 1572872 | tf_op jit(solution)/shard_map/ppermute | solution.py:20
  3.6 1.0 %constant_dynamic-slice_fusion.refs_0_.refs_12_.refs_1_ = bf16[256,512]{1,0:T(8,128)(2,1)S(1)} fusion(bf16[1024,512]{1,0:T(8,128)(2,1)} %refs_4_.1, s32[]{:T(128)S(6)} %select_n.3), kind=kLoop, calls=%fused_computation.8 | loop fusion | bytes 524292 | tf_op jit(solution)/shard_map/dynamic_slice | solution.py:354
  4.6 1.6 %collective-permute-start.6 = (bf16[256,512]{1,0:T(8,128)(2,1)S(1)}, bf16[256,512]{1,0:T(8,128)(2,1)S(1)}, u32[]{:S(2)}, u32[]{:S(2)}) collective-permute-start(bf16[256,512]{1,0:T(8,128)(2,1)S(1)} %constant_dynamic-slice_fusion.refs_0_.refs_12_.refs_1_), channel_id=1, source_target_pairs={{0,4},{4,0},{8,12},{12,8},{1,5},{5,1},{9,13},{13,9},{2,6},{6,2},{1... | collective-permute-start | bytes 786440 | tf_op jit(solution)/shard_map/ppermute | solution.py:20
  6.3 2.6 %collective-permute-start = (bf16[256,512]{1,0:T(8,128)(2,1)S(1)}, bf16[256,512]{1,0:T(8,128)(2,1)S(1)}, u32[]{:S(2)}, u32[]{:S(2)}) collective-permute-start(bf16[256,512]{1,0:T(8,128)(2,1)S(1)} %constant_dynamic-slice_fusion.refs_0_.refs_12_.refs_1_), channel_id=1, source_target_pairs={{0,8},{4,12},{8,0},{12,4},{1,9},{5,13},{9,1},{13,5},{2,10},{6,14},... | collective-permute-start | bytes 786440 | tf_op jit(solution)/shard_map/ppermute | solution.py:20
  8.8 0.7 %reshape.10.spread_ref = bf16[1,512]{1,0:T(2,128)(2,1)S(1)} reshape(bf16[512]{0:T(512)(128)(2,1)} %param.13) | data formatting | bytes 2048 | tf_op jit(solution)/shard_map/reshape | solution.py:90
  9.5 1.0 %copy-done.1 = bf16[512,512]{1,0:T(8,128)(2,1)S(1)} copy-done((bf16[512,512]{1,0:T(8,128)(2,1)S(1)}, bf16[512,512]{1,0:T(8,128)(2,1)}, u32[]{:S(2)}) %copy-start.1) | copy-done | bytes 524312
  10.6 0.9 %copy-done.5 = bf16[512,128]{1,0:T(8,128)(2,1)S(1)} copy-done((bf16[512,128]{1,0:T(8,128)(2,1)S(1)}, bf16[512,128]{1,0:T(8,128)(2,1)}, u32[]{:S(2)}) %copy-start.5) | copy-done | bytes 131096
  11.5 0.7 %copy-done.6 = f32[128]{0:T(128)S(1)} copy-done((f32[128]{0:T(128)S(1)}, f32[128]{0:T(128)}, u32[]{:S(2)}) %copy-start.6) | copy-done | bytes 536
  12.4 0.6 collective-permute-start.5
  13.0 1.0 %copy-done.3 = f32[1024,128]{1,0:T(8,128)S(1)} copy-done((f32[1024,128]{1,0:T(8,128)S(1)}, f32[1024,128]{1,0:T(8,128)}, u32[]{:S(2)}) %copy-start.3) | copy-done | bytes 524312
  14.0 1.0 %copy-done.4 = f32[1024,128]{1,0:T(8,128)S(1)} copy-done((f32[1024,128]{1,0:T(8,128)S(1)}, f32[1024,128]{1,0:T(8,128)}, u32[]{:S(2)}) %copy-start.4) | copy-done | bytes 524312
  15.5 3.5 %collective-permute-done.5.refs_6_ = bf16[144,512]{1,0:T(8,128)(2,1)S(1)} collective-permute-done((bf16[144,512]{1,0:T(8,128)(2,1)S(1)}, bf16[144,512]{1,0:T(8,128)(2,1)S(1)}, u32[]{:S(2)}, u32[]{:S(2)}) %collective-permute-start.5) | collective-permute-done | bytes 147488 | tf_op jit(solution)/shard_map/ppermute | solution.py:20
  19.0 1.3 %collective-permute-done.refs_0_ = bf16[256,512]{1,0:T(8,128)(2,1)S(1)} collective-permute-done((bf16[256,512]{1,0:T(8,128)(2,1)S(1)}, bf16[256,512]{1,0:T(8,128)(2,1)S(1)}, u32[]{:S(2)}, u32[]{:S(2)}) %collective-permute-start) | collective-permute-done | bytes 262176 | tf_op jit(solution)/shard_map/ppermute | solution.py:20
  20.9 0.6 collective-permute-start.20
  21.5 1.6 %collective-permute-start.1 = (bf16[256,512]{1,0:T(8,128)(2,1)S(1)}, bf16[256,512]{1,0:T(8,128)(2,1)S(1)}, u32[]{:S(2)}, u32[]{:S(2)}) collective-permute-start(bf16[256,512]{1,0:T(8,128)(2,1)S(1)} %collective-permute-done.refs_0_), channel_id=1, source_target_pairs={{0,4},{4,0},{8,12},{12,8},{1,5},{5,1},{9,13},{13,9},{2,6},{6,2},{1... | collective-permute-start | bytes 786440 | tf_op jit(solution)/shard_map/ppermute | solution.py:20
  23.1 1.3 %forward.3 = f32[256,128]{1,0:T(8,128)S(1)} custom-call(bf16[256,512]{1,0:T(8,128)(2,1)S(1)} %collective-permute-done.refs_0_, bf16[512,512]{1,0:T(8,128)(2,1)S(1)} %get-tuple-element.39.refs_1_.refs_10_.pos_ref, bf16[144,512]{1,0:T(8,128)(2,1)S(1)} %get-tuple-element.42.refs_2_, bf16[512,512]{1,0:T(8,128)(2,1)S(1)} %collective-permute-done.2.refs_3_, ...), custom_call_target="tpu_custom_call" | custom-call | flops 1 | bytes 1 | tf_op jit(solution)/shard_map/forward/pallas_call | solution.py:167
  24.4 2.7 %collective-permute-start.9 = (f32[256,128]{1,0:T(8,128)S(1)}, f32[256,128]{1,0:T(8,128)S(1)}, u32[]{:S(2)}, u32[]{:S(2)}) collective-permute-start(f32[256,128]{1,0:T(8,128)S(1)} %forward.3), channel_id=1, source_target_pairs={{0,8},{4,12},{8,0},{12,4},{1,9},{5,13},{9,1},{13,5},{2,10},{6,14},... | collective-permute-start | bytes 393224 | tf_op jit(solution)/shard_map/ppermute | solution.py:20
  27.0 1.3 %forward.4 = f32[256,128]{1,0:T(8,128)S(1)} custom-call(bf16[256,512]{1,0:T(8,128)(2,1)S(1)} %collective-permute-done.6.refs_0_, bf16[512,512]{1,0:T(8,128)(2,1)S(1)} %get-tuple-element.39.refs_1_.refs_10_.pos_ref, bf16[144,512]{1,0:T(8,128)(2,1)S(1)} %get-tuple-element.42.refs_2_, bf16[512,512]{1,0:T(8,128)(2,1)S(1)} %collective-permute-done.2.refs_3_, ...), custom_call_target="tpu_custom_call" | custom-call | flops 17179869184 | bytes 1048576 | tf_op jit(solution)/shard_map/forward/pallas_call | solution.py:167
  28.4 4.3 %collective-permute-done.1.refs_0_.refs_14_.refs_3_ = bf16[256,512]{1,0:T(8,128)(2,1)S(1)} collective-permute-done((bf16[256,512]{1,0:T(8,128)(2,1)S(1)}, bf16[256,512]{1,0:T(8,128)(2,1)S(1)}, u32[]{:S(2)}, u32[]{:S(2)}) %collective-permute-start.1) | collective-permute-done | bytes 262176 | tf_op jit(solution)/shard_map/ppermute | solution.py:20
  32.7 1.3 %forward.5 = f32[256,128]{1,0:T(8,128)S(1)} custom-call(bf16[256,512]{1,0:T(8,128)(2,1)S(1)} %collective-permute-done.1.refs_0_.refs_14_.refs_3_, bf16[512,512]{1,0:T(8,128)(2,1)S(1)} %get-tuple-element.39.refs_1_.refs_10_.pos_ref, bf16[144,512]{1,0:T(8,128)(2,1)S(1)} %get-tuple-element.42.refs_2_, bf16[512,512]{1,0:T(8,128)(2,1)S(1)} %collective-permute-done.2.refs_3_, ...), custom_call_target="tpu_custom_call" | custom-call | flops 17179869184 | bytes 1048576 | tf_op jit(solution)/shard_map/forward/pallas_call | solution.py:167
  34.0 3.5 %collective-permute-start.11 = (f32[256,128]{1,0:T(8,128)S(1)}, f32[256,128]{1,0:T(8,128)S(1)}, u32[]{:S(2)}, u32[]{:S(2)}) collective-permute-start(f32[256,128]{1,0:T(8,128)S(1)} %forward.5), channel_id=1, source_target_pairs={{0,12},{4,8},{8,4},{12,0},{1,13},{5,9},{9,5},{13,1},{2,14},{6,10},... | collective-permute-start | bytes 393224 | tf_op jit(solution)/shard_map/ppermute | solution.py:20
  37.5 2.3 %own_rows.1 = (f32[256,128]{1,0:T(8,128)S(1)}, bf16[512,1024]{1,0:T(8,128)(2,1)S(1)}) custom-call(bf16[256,512]{1,0:T(8,128)(2,1)S(1)} %constant_dynamic-slice_fusion.refs_0_.refs_12_.refs_1_, bf16[512,512]{1,0:T(8,128)(2,1)S(1)} %get-tuple-element.39.refs_1_.refs_10_.pos_ref, bf16[144,512]{1,0:T(8,128)(2,1)S(1)} %get-tuple-element.42.refs_2_, ...), custom_call_target="tpu_custom_call" | custom-call | flops 17179869184 | bytes 1048576 | tf_op jit(solution)/shard_map/own_rows/pallas_call | solution.py:214
  39.7 2.3 %collective-permute-done.11.refs_2_ = f32[256,128]{1,0:T(8,128)S(1)} collective-permute-done((f32[256,128]{1,0:T(8,128)S(1)}, f32[256,128]{1,0:T(8,128)S(1)}, u32[]{:S(2)}, u32[]{:S(2)}) %collective-permute-start.11) | collective-permute-done | bytes 131104 | tf_op jit(solution)/shard_map/ppermute | solution.py:20
  42.1 1.4 %collective-permute-done.10.refs_1_ = f32[256,128]{1,0:T(8,128)S(1)} collective-permute-done((f32[256,128]{1,0:T(8,128)S(1)}, f32[256,128]{1,0:T(8,128)S(1)}, u32[]{:S(2)}, u32[]{:S(2)}) %collective-permute-start.10) | collective-permute-done | bytes 131104 | tf_op jit(solution)/shard_map/ppermute | solution.py:20
  44.2 2.0 %collective-permute-start.12 = (bf16[256,128]{1,0:T(8,128)(2,1)S(1)}, bf16[256,128]{1,0:T(8,128)(2,1)S(1)}, u32[]{:S(2)}, u32[]{:S(2)}) collective-permute-start(bf16[256,128]{1,0:T(8,128)(2,1)S(1)} %cotangent.1), channel_id=1, source_target_pairs={{0,4},{4,0},{8,12},{12,8},{1,5},{5,1},{9,13},{13,9},{2,6},{6,2},{1... | collective-permute-start | bytes 196616 | tf_op jit(solution)/shard_map/ppermute | solution.py:20
  46.9 2.0 %collective-permute-done.15 = bf16[256,128]{1,0:T(8,128)(2,1)S(1)} collective-permute-done((bf16[256,128]{1,0:T(8,128)(2,1)S(1)}, bf16[256,128]{1,0:T(8,128)(2,1)S(1)}, u32[]{:S(2)}, u32[]{:S(2)}) %collective-permute-start.15) | collective-permute-done | bytes 65568 | tf_op jit(solution)/shard_map/ppermute | solution.py:20
  49.1 1.3 %collective-permute-start.16 = (bf16[256,128]{1,0:T(8,128)(2,1)S(1)}, bf16[256,128]{1,0:T(8,128)(2,1)S(1)}, u32[]{:S(2)}, u32[]{:S(2)}) collective-permute-start(bf16[256,128]{1,0:T(8,128)(2,1)S(1)} %collective-permute-done.15), channel_id=1, source_target_pairs={{0,4},{4,0},{8,12},{12,8},{1,5},{5,1},{9,13},{13,9},{2,6},{6,2},{1... | collective-permute-start | bytes 196616 | tf_op jit(solution)/shard_map/ppermute | solution.py:20
  50.5 2.9 %collective-permute-done.16 = bf16[256,128]{1,0:T(8,128)(2,1)S(1)} collective-permute-done((bf16[256,128]{1,0:T(8,128)(2,1)S(1)}, bf16[256,128]{1,0:T(8,128)(2,1)S(1)}, u32[]{:S(2)}, u32[]{:S(2)}) %collective-permute-start.16) | collective-permute-done | bytes 65568 | tf_op jit(solution)/shard_map/ppermute | solution.py:20
  54.1 1.1 %collective-permute-start.23 = (bf16[768,128]{1,0:T(8,128)(2,1)S(1)}, bf16[768,128]{1,0:T(8,128)(2,1)S(1)}, u32[]{:S(2)}, u32[]{:S(2)}) collective-permute-start(bf16[768,128]{1,0:T(8,128)(2,1)S(1)} %constant_dynamic-update-slice_fusion.2), channel_id=1, source_target_pairs={{0,2},{1,3},{2,0},{3,1},{4,6},{5,7},{6,4},{7,5},{8,10},{9,11},{10,... | collective-permute-start | bytes 589832 | tf_op jit(solution)/shard_map/ppermute | solution.py:20
  55.4 5.7 %backward.2 = (f32[512,512]{1,0:T(8,128)S(1)}, f32[512,128]{1,0:T(8,128)S(1)}, f32[512,128]{1,0:T(8,128)S(1)}, bf16[512,1024]{1,0:T(8,128)(2,1)S(1)}, bf16[512,1024]{1,0:T(8,128)(2,1)S(1)}) custom-call(bf16[512,512]{1,0:T(8,128)(2,1)S(1)} %get-tuple-element.39.refs_1_.refs_10_.pos_ref, bf16[512,128]{1,0:T(8,128)(2,1)S(1)} %get-tuple-element.40.coef_ref, ...), custom_call_target="tpu_custom_call" | custom-call | flops 17179869184 | bytes 1048576 | tf_op jit(solution)/shard_map/backward/pallas_call | solution.py:288
  61.4 1.3 %backward.3 = (f32[512,512]{1,0:T(8,128)S(1)}, f32[512,128]{1,0:T(8,128)S(1)}, f32[512,128]{1,0:T(8,128)S(1)}) custom-call(bf16[512,512]{1,0:T(8,128)(2,1)S(1)} %get-tuple-element.39.refs_1_.refs_10_.pos_ref, bf16[512,128]{1,0:T(8,128)(2,1)S(1)} %get-tuple-element.40.coef_ref, bf16[1,512]{1,0:T(2,128)(2,1)S(1)} %get-tuple-element.41.refs_11_.spread_ref, ...), custom_call_target="tpu_custom_call" | custom-call | flops 1 | bytes 1 | tf_op jit(solution)/shard_map/backward/pallas_call | solution.py:288
  62.8 2.3 %finish.1 = (f32[512,512]{1,0:T(8,128)}, f32[512,128]{1,0:T(8,128)}) custom-call(bf16[512,512]{1,0:T(8,128)(2,1)S(1)} %get-tuple-element.39.refs_1_.refs_10_.pos_ref, bf16[512,128]{1,0:T(8,128)(2,1)S(1)} %get-tuple-element.40.coef_ref, bf16[1,512]{1,0:T(2,128)(2,1)S(1)} %get-tuple-element.41.refs_11_.spread_ref, ...), custom_call_target="tpu_custom_call" | custom-call | flops 1 | bytes 1 | tf_op jit(solution)/shard_map/finish/pallas_call | solution.py:330
  (52 shorter events, 4.0 us)
Async XLA Ops:
  0.6 12.3 %copy-start = (bf16[1024,512]{1,0:T(8,128)(2,1)S(1)}, bf16[1024,512]{1,0:T(8,128)(2,1)}, u32[]{:S(2)}) copy-start(bf16[1024,512]{1,0:T(8,128)(2,1)} %refs_4_.1) | copy-start | bytes 3145732
  0.6 19.7 %collective-permute-start.4 = (bf16[512,512]{1,0:T(8,128)(2,1)}, bf16[512,512]{1,0:T(8,128)(2,1)S(1)}, u32[]{:S(2)}, u32[]{:S(2)}) collective-permute-start(bf16[512,512]{1,0:T(8,128)(2,1)} %pos_ref), channel_id=1, source_target_pairs={{0,2},{1,3},{2,0},{3,1},{4,6},{5,7},{6,4},{7,5},{8,10},{9,11},{10,... | collective-permute-start | bytes 1572872 | tf_op jit(solution)/shard_map/ppermute | solution.py:20
  4.6 14.3 %collective-permute-start.6 = (bf16[256,512]{1,0:T(8,128)(2,1)S(1)}, bf16[256,512]{1,0:T(8,128)(2,1)S(1)}, u32[]{:S(2)}, u32[]{:S(2)}) collective-permute-start(bf16[256,512]{1,0:T(8,128)(2,1)S(1)} %constant_dynamic-slice_fusion.refs_0_.refs_12_.refs_1_), channel_id=1, source_target_pairs={{0,4},{4,0},{8,12},{12,8},{1,5},{5,1},{9,13},{13,9},{2,6},{6,2},{1... | collective-permute-start | bytes 786440 | tf_op jit(solution)/shard_map/ppermute | solution.py:20
  6.3 14.0 %collective-permute-start = (bf16[256,512]{1,0:T(8,128)(2,1)S(1)}, bf16[256,512]{1,0:T(8,128)(2,1)S(1)}, u32[]{:S(2)}, u32[]{:S(2)}) collective-permute-start(bf16[256,512]{1,0:T(8,128)(2,1)S(1)} %constant_dynamic-slice_fusion.refs_0_.refs_12_.refs_1_), channel_id=1, source_target_pairs={{0,8},{4,12},{8,0},{12,4},{1,9},{5,13},{9,1},{13,5},{2,10},{6,14},... | collective-permute-start | bytes 786440 | tf_op jit(solution)/shard_map/ppermute | solution.py:20
  9.5 1.0 %copy-start.1 = (bf16[512,512]{1,0:T(8,128)(2,1)S(1)}, bf16[512,512]{1,0:T(8,128)(2,1)}, u32[]{:S(2)}) copy-start(bf16[512,512]{1,0:T(8,128)(2,1)} %pos_ref) | copy-start | bytes 1572868
  10.6 0.9 %copy-start.5 = (bf16[512,128]{1,0:T(8,128)(2,1)S(1)}, bf16[512,128]{1,0:T(8,128)(2,1)}, u32[]{:S(2)}) copy-start(bf16[512,128]{1,0:T(8,128)(2,1)} %coef_ref.1) | copy-start | bytes 393220
  11.5 0.7 %copy-start.6 = (f32[128]{0:T(128)S(1)}, f32[128]{0:T(128)}, u32[]{:S(2)}) copy-start(f32[128]{0:T(128)} %param.10) | copy-start | bytes 1540
  12.3 6.6 %copy-start.2 = (bf16[512,512]{1,0:T(8,128)(2,1)S(1)}, bf16[512,512]{1,0:T(8,128)(2,1)}, u32[]{:S(2)}) copy-start(bf16[512,512]{1,0:T(8,128)(2,1)} %pos_ref) | copy-start | bytes 1572868
  12.4 6.6 %collective-permute-start.5 = (bf16[144,512]{1,0:T(8,128)(2,1)S(1)}, bf16[144,512]{1,0:T(8,128)(2,1)S(1)}, u32[]{:S(2)}, u32[]{:S(2)}) collective-permute-start(bf16[144,512]{1,0:T(8,128)(2,1)S(1)} %get-tuple-element.42.refs_2_), channel_id=1, source_target_pairs={{0,2},{1,3},{2,0},{3,1},{4,6},{5,7},{6,4},{7,5},{8,10},{9,11},{10,... | collective-permute-start | bytes 442376 | tf_op jit(solution)/shard_map/ppermute | solution.py:20
  13.0 6.0 %collective-permute-start.3 = (bf16[144,512]{1,0:T(8,128)(2,1)S(1)}, bf16[144,512]{1,0:T(8,128)(2,1)S(1)}, u32[]{:S(2)}, u32[]{:S(2)}) collective-permute-start(bf16[144,512]{1,0:T(8,128)(2,1)S(1)} %get-tuple-element.42.refs_2_), channel_id=1, source_target_pairs={{0,1},{1,0},{2,3},{3,2},{4,5},{5,4},{6,7},{7,6},{8,9},{9,8},{10,11... | collective-permute-start | bytes 442376 | tf_op jit(solution)/shard_map/ppermute | solution.py:20
  13.0 1.0 %copy-start.3 = (f32[1024,128]{1,0:T(8,128)S(1)}, f32[1024,128]{1,0:T(8,128)}, u32[]{:S(2)}) copy-start(f32[1024,128]{1,0:T(8,128)} %refs_0_.1) | copy-start | bytes 1572868
  14.0 1.0 %copy-start.4 = (f32[1024,128]{1,0:T(8,128)S(1)}, f32[1024,128]{1,0:T(8,128)}, u32[]{:S(2)}) copy-start(f32[1024,128]{1,0:T(8,128)} %refs_1_.1) | copy-start | bytes 1572868
  18.9 4.1 %collective-permute-start.2 = (bf16[512,512]{1,0:T(8,128)(2,1)S(1)}, bf16[512,512]{1,0:T(8,128)(2,1)S(1)}, u32[]{:S(2)}, u32[]{:S(2)}) collective-permute-start(bf16[512,512]{1,0:T(8,128)(2,1)S(1)} %copy-done.2), channel_id=1, source_target_pairs={{0,1},{1,0},{2,3},{3,2},{4,5},{5,4},{6,7},{7,6},{8,9},{9,8},{10,11... | collective-permute-start | bytes 1572872 | tf_op jit(solution)/shard_map/ppermute | solution.py:20
  20.3 2.8 %collective-permute-start.7 = (bf16[512,512]{1,0:T(8,128)(2,1)S(1)}, bf16[512,512]{1,0:T(8,128)(2,1)S(1)}, u32[]{:S(2)}, u32[]{:S(2)}) collective-permute-start(bf16[512,512]{1,0:T(8,128)(2,1)S(1)} %collective-permute-done.4.refs_5_), channel_id=1, source_target_pairs={{0,1},{1,0},{2,3},{3,2},{4,5},{5,4},{6,7},{7,6},{8,9},{9,8},{10,11... | collective-permute-start | bytes 1572872 | tf_op jit(solution)/shard_map/ppermute | solution.py:20
  20.3 2.7 %collective-permute-start.8 = (bf16[144,512]{1,0:T(8,128)(2,1)S(1)}, bf16[144,512]{1,0:T(8,128)(2,1)S(1)}, u32[]{:S(2)}, u32[]{:S(2)}) collective-permute-start(bf16[144,512]{1,0:T(8,128)(2,1)S(1)} %collective-permute-done.5.refs_6_), channel_id=1, source_target_pairs={{0,1},{1,0},{2,3},{3,2},{4,5},{5,4},{6,7},{7,6},{8,9},{9,8},{10,11... | collective-permute-start | bytes 442376 | tf_op jit(solution)/shard_map/ppermute | solution.py:20
  20.9 25.5 %collective-permute-start.20 = (bf16[512,512]{1,0:T(8,128)(2,1)S(1)}, bf16[512,512]{1,0:T(8,128)(2,1)S(1)}, u32[]{:S(2)}, u32[]{:S(2)}) collective-permute-start(bf16[512,512]{1,0:T(8,128)(2,1)S(1)} %constant_dynamic-update-slice_fusion.refs_13_.refs_2_), channel_id=1, source_target_pairs={{0,2},{1,3},{2,0},{3,1},{4,6},{5,7},{6,4},{7,5},{8,10},{9,11},{10,... | collective-permute-start | bytes 1572872 | tf_op jit(solution)/shard_map/ppermute | solution.py:20
  21.5 11.2 %collective-permute-start.1 = (bf16[256,512]{1,0:T(8,128)(2,1)S(1)}, bf16[256,512]{1,0:T(8,128)(2,1)S(1)}, u32[]{:S(2)}, u32[]{:S(2)}) collective-permute-start(bf16[256,512]{1,0:T(8,128)(2,1)S(1)} %collective-permute-done.refs_0_), channel_id=1, source_target_pairs={{0,4},{4,0},{8,12},{12,8},{1,5},{5,1},{9,13},{13,9},{2,6},{6,2},{1... | collective-permute-start | bytes 786440 | tf_op jit(solution)/shard_map/ppermute | solution.py:20
  24.4 13.1 %collective-permute-start.9 = (f32[256,128]{1,0:T(8,128)S(1)}, f32[256,128]{1,0:T(8,128)S(1)}, u32[]{:S(2)}, u32[]{:S(2)}) collective-permute-start(f32[256,128]{1,0:T(8,128)S(1)} %forward.3), channel_id=1, source_target_pairs={{0,8},{4,12},{8,0},{12,4},{1,9},{5,13},{9,1},{13,5},{2,10},{6,14},... | collective-permute-start | bytes 393224 | tf_op jit(solution)/shard_map/ppermute | solution.py:20
  34.0 8.1 %collective-permute-start.11 = (f32[256,128]{1,0:T(8,128)S(1)}, f32[256,128]{1,0:T(8,128)S(1)}, u32[]{:S(2)}, u32[]{:S(2)}) collective-permute-start(f32[256,128]{1,0:T(8,128)S(1)} %forward.5), channel_id=1, source_target_pairs={{0,12},{4,8},{8,4},{12,0},{1,13},{5,9},{9,5},{13,1},{2,14},{6,10},... | collective-permute-start | bytes 393224 | tf_op jit(solution)/shard_map/ppermute | solution.py:20
  37.4 6.0 %collective-permute-start.10 = (f32[256,128]{1,0:T(8,128)S(1)}, f32[256,128]{1,0:T(8,128)S(1)}, u32[]{:S(2)}, u32[]{:S(2)}) collective-permute-start(f32[256,128]{1,0:T(8,128)S(1)} %forward.4), channel_id=1, source_target_pairs={{0,4},{4,0},{8,12},{12,8},{1,5},{5,1},{9,13},{13,9},{2,6},{6,2},{1... | collective-permute-start | bytes 393224 | tf_op jit(solution)/shard_map/ppermute | solution.py:20
  37.4 8.7 %collective-permute-start.13 = (bf16[256,512]{1,0:T(8,128)(2,1)S(1)}, bf16[256,512]{1,0:T(8,128)(2,1)S(1)}, u32[]{:S(2)}, u32[]{:S(2)}) collective-permute-start(bf16[256,512]{1,0:T(8,128)(2,1)S(1)} %collective-permute-done.1.refs_0_.refs_14_.refs_3_), channel_id=1, source_target_pairs={{0,2},{1,3},{2,0},{3,1},{4,6},{5,7},{6,4},{7,5},{8,10},{9,11},{10,... | collective-permute-start | bytes 786440 | tf_op jit(solution)/shard_map/ppermute | solution.py:20
  43.6 5.3 %collective-permute-start.15 = (bf16[256,128]{1,0:T(8,128)(2,1)S(1)}, bf16[256,128]{1,0:T(8,128)(2,1)S(1)}, u32[]{:S(2)}, u32[]{:S(2)}) collective-permute-start(bf16[256,128]{1,0:T(8,128)(2,1)S(1)} %cotangent.1), channel_id=1, source_target_pairs={{0,8},{4,12},{8,0},{12,4},{1,9},{5,13},{9,1},{13,5},{2,10},{6,14},... | collective-permute-start | bytes 196616 | tf_op jit(solution)/shard_map/ppermute | solution.py:20
  44.2 5.0 %collective-permute-start.12 = (bf16[256,128]{1,0:T(8,128)(2,1)S(1)}, bf16[256,128]{1,0:T(8,128)(2,1)S(1)}, u32[]{:S(2)}, u32[]{:S(2)}) collective-permute-start(bf16[256,128]{1,0:T(8,128)(2,1)S(1)} %cotangent.1), channel_id=1, source_target_pairs={{0,4},{4,0},{8,12},{12,8},{1,5},{5,1},{9,13},{13,9},{2,6},{6,2},{1... | collective-permute-start | bytes 196616 | tf_op jit(solution)/shard_map/ppermute | solution.py:20
  46.2 4.3 %collective-permute-start.14 = (bf16[256,128]{1,0:T(8,128)(2,1)S(1)}, bf16[256,128]{1,0:T(8,128)(2,1)S(1)}, u32[]{:S(2)}, u32[]{:S(2)}) collective-permute-start(bf16[256,128]{1,0:T(8,128)(2,1)S(1)} %cotangent.1), channel_id=1, source_target_pairs={{0,2},{1,3},{2,0},{3,1},{4,6},{5,7},{6,4},{7,5},{8,10},{9,11},{10,... | collective-permute-start | bytes 196616 | tf_op jit(solution)/shard_map/ppermute | solution.py:20
  46.4 7.7 %collective-permute-start.18 = (bf16[256,512]{1,0:T(8,128)(2,1)S(1)}, bf16[256,512]{1,0:T(8,128)(2,1)S(1)}, u32[]{:S(2)}, u32[]{:S(2)}) collective-permute-start(bf16[256,512]{1,0:T(8,128)(2,1)S(1)} %collective-permute-done.1.refs_0_.refs_14_.refs_3_), channel_id=1, source_target_pairs={{0,1},{1,0},{2,3},{3,2},{4,5},{5,4},{6,7},{7,6},{8,9},{9,8},{10,11... | collective-permute-start | bytes 786440 | tf_op jit(solution)/shard_map/ppermute | solution.py:20
  46.4 8.8 %collective-permute-start.17 = (bf16[512,512]{1,0:T(8,128)(2,1)S(1)}, bf16[512,512]{1,0:T(8,128)(2,1)S(1)}, u32[]{:S(2)}, u32[]{:S(2)}) collective-permute-start(bf16[512,512]{1,0:T(8,128)(2,1)S(1)} %constant_dynamic-update-slice_fusion.refs_13_.refs_2_), channel_id=1, source_target_pairs={{0,1},{1,0},{2,3},{3,2},{4,5},{5,4},{6,7},{7,6},{8,9},{9,8},{10,11... | collective-permute-start | bytes 1572872 | tf_op jit(solution)/shard_map/ppermute | solution.py:20
  48.9 6.3 %collective-permute-start.21 = (bf16[512,512]{1,0:T(8,128)(2,1)S(1)}, bf16[512,512]{1,0:T(8,128)(2,1)S(1)}, u32[]{:S(2)}, u32[]{:S(2)}) collective-permute-start(bf16[512,512]{1,0:T(8,128)(2,1)S(1)} %collective-permute-done.20.refs_10_.refs_2_), channel_id=1, source_target_pairs={{0,1},{1,0},{2,3},{3,2},{4,5},{5,4},{6,7},{7,6},{8,9},{9,8},{10,11... | collective-permute-start | bytes 1572872 | tf_op jit(solution)/shard_map/ppermute | solution.py:20
  49.1 4.3 %collective-permute-start.16 = (bf16[256,128]{1,0:T(8,128)(2,1)S(1)}, bf16[256,128]{1,0:T(8,128)(2,1)S(1)}, u32[]{:S(2)}, u32[]{:S(2)}) collective-permute-start(bf16[256,128]{1,0:T(8,128)(2,1)S(1)} %collective-permute-done.15), channel_id=1, source_target_pairs={{0,4},{4,0},{8,12},{12,8},{1,5},{5,1},{9,13},{13,9},{2,6},{6,2},{1... | collective-permute-start | bytes 196616 | tf_op jit(solution)/shard_map/ppermute | solution.py:20
  53.4 1.8 %collective-permute-start.22 = (bf16[256,512]{1,0:T(8,128)(2,1)S(1)}, bf16[256,512]{1,0:T(8,128)(2,1)S(1)}, u32[]{:S(2)}, u32[]{:S(2)}) collective-permute-start(bf16[256,512]{1,0:T(8,128)(2,1)S(1)} %collective-permute-done.13.refs_11_.refs_3_), channel_id=1, source_target_pairs={{0,1},{1,0},{2,3},{3,2},{4,5},{5,4},{6,7},{7,6},{8,9},{9,8},{10,11... | collective-permute-start | bytes 786440 | tf_op jit(solution)/shard_map/ppermute | solution.py:20
  53.5 1.9 %collective-permute-start.19 = (bf16[1024,128]{1,0:T(8,128)(2,1)S(1)}, bf16[1024,128]{1,0:T(8,128)(2,1)S(1)}, u32[]{:S(2)}, u32[]{:S(2)}) collective-permute-start(bf16[1024,128]{1,0:T(8,128)(2,1)S(1)} %pad_maximum_fusion.refs_4_), channel_id=1, source_target_pairs={{0,1},{1,0},{2,3},{3,2},{4,5},{5,4},{6,7},{7,6},{8,9},{9,8},{10,11... | collective-permute-start | bytes 786440 | tf_op jit(solution)/shard_map/ppermute | solution.py:20
  54.1 7.0 %collective-permute-start.23 = (bf16[768,128]{1,0:T(8,128)(2,1)S(1)}, bf16[768,128]{1,0:T(8,128)(2,1)S(1)}, u32[]{:S(2)}, u32[]{:S(2)}) collective-permute-start(bf16[768,128]{1,0:T(8,128)(2,1)S(1)} %constant_dynamic-update-slice_fusion.2), channel_id=1, source_target_pairs={{0,2},{1,3},{2,0},{3,1},{4,6},{5,7},{6,4},{7,5},{8,10},{9,11},{10,... | collective-permute-start | bytes 589832 | tf_op jit(solution)/shard_map/ppermute | solution.py:20
  61.1 1.6 %collective-permute-start.24 = (bf16[1024,128]{1,0:T(8,128)(2,1)S(1)}, bf16[1024,128]{1,0:T(8,128)(2,1)S(1)}, u32[]{:S(2)}, u32[]{:S(2)}) collective-permute-start(bf16[1024,128]{1,0:T(8,128)(2,1)S(1)} %constant_dynamic-update-slice_fusion.5.refs_4_), channel_id=1, source_target_pairs={{0,1},{1,0},{2,3},{3,2},{4,5},{5,4},{6,7},{7,6},{8,9},{9,8},{10,11... | collective-permute-start | bytes 786440 | tf_op jit(solution)/shard_map/ppermute | solution.py:20

commit v13 on v12

--- a/solution.py
+++ b/solution.py
@@ -388,8 +388,8 @@
         received[1] = swap(parts[1], "points", nz, 1)
         rows = [after(layer[dz], *parts.values()) for dz in second]
         parts.update(zip(second, forward(rows, centers, out_width, COVER)))
-        soon = [received[dz] for dz in range(2, nz, 2)]
-        received = [received[1]] + [swap(parts[dz], "points", nz, dz) for dz in second]
+        soon = list(received.values())
+        received = [swap(parts[dz], "points", nz, dz) for dz in second]
         last = parts[nz - 1]
         kernels, late = {1: None}, {0: layer[nz - 1]}
         parts[0], kernels[0] = own_rows(

time: 65.4 us -> 65.2 us (level)
  waiting for transfers between devices: 18.2 us -> 14.8 us
  starting transfers between devices: 23.3 us -> 26.6 us
    ppermute x25, waiting for transfers between devices: 18.2 us -> 14.8 us  [swap(): return lax.ppermute(a, axis, [(i, i ^ d) for i in range(size)])]
    ppermute x25, starting transfers between devices: 23.3 us -> 26.6 us  [swap(): return lax.ppermute(a, axis, [(i, i ^ d) for i in range(size)])]
  transfers between devices with their start and end apart: 25 -> 25, of which waited for: 9 -> 8; matrix products, arithmetic and copies ran while one was open for 3% -> 3% of each run, Pallas kernels for 21% -> 21%
where the time goes in v13:
time: 65.2 us; the launch traced here: 64.9 us
  starting transfers between devices  26.6 us (41%)
  Pallas kernels  16.2 us (25%)
  waiting for transfers between devices  14.8 us (23%)
  local copies, waits for them, and re-layouts  6.45 us (10%)
  between operations  0.83 us (1%)
    ppermute x25, starting transfers between devices, swap(): return lax.ppermute(a, axis, [(i, i ^ d) for i in range(size)])  26.6 us
    ppermute x25, waiting for transfers between devices, swap(): return lax.ppermute(a, axis, [(i, i ^ d) for i in range(size)])  14.8 us
    pallas_call x2, Pallas kernels, backward(): pl.pallas_call(body, out_shape=tuple((jax.ShapeDtypeStruct((n, width), F3...  6.98 us
    unnamed x18, local copies, waits for them, and re-layouts  4.74 us
    pallas_call x3, Pallas kernels, forward(): pl.pallas_call(body, out_shape=tuple((jax.ShapeDtypeStruct((count, out_wi...  3.93 us
    pallas_call x1, Pallas kernels, finish(): pl.pallas_call(body, out_shape=tuple((jax.ShapeDtypeStruct((n, width), F3...  2.33 us
    pallas_call x1, Pallas kernels, own_rows(): pl.pallas_call(body, out_shape=(jax.ShapeDtypeStruct((rows.shape[0], out_...  2.28 us
  transfers between devices with their start and end apart: 25, of which 8 were waited for; matrix products, arithmetic and copies ran while one was open for 3% of the time, Pallas kernels for 21%

profile of v13, /device:TPU:0, one launch (start us, length us, event | category | flops | bytes accessed | tf_op | source)
XLA Modules:
  0.0 64.9 jit_solution(926708139463217885)
XLA Ops:
  0.6 3.0 %collective-permute-start.4 = (bf16[512,512]{1,0:T(8,128)(2,1)}, bf16[512,512]{1,0:T(8,128)(2,1)S(1)}, u32[]{:S(2)}, u32[]{:S(2)}) collective-permute-start(bf16[512,512]{1,0:T(8,128)(2,1)} %pos_ref), channel_id=1, source_target_pairs={{0,2},{1,3},{2,0},{3,1},{4,6},{5,7},{6,4},{7,5},{8,10},{9,11},{10,... | collective-permute-start | bytes 1572872 | tf_op jit(solution)/shard_map/ppermute | solution.py:20
  3.6 1.0 %constant_dynamic-slice_fusion.refs_0_.refs_13_.refs_1_ = bf16[256,512]{1,0:T(8,128)(2,1)S(1)} fusion(bf16[1024,512]{1,0:T(8,128)(2,1)} %refs_4_.1, s32[]{:T(128)S(6)} %select_n.3), kind=kLoop, calls=%fused_computation.8 | loop fusion | bytes 524292 | tf_op jit(solution)/shard_map/dynamic_slice | solution.py:354
  4.6 1.6 %collective-permute-start.6 = (bf16[256,512]{1,0:T(8,128)(2,1)S(1)}, bf16[256,512]{1,0:T(8,128)(2,1)S(1)}, u32[]{:S(2)}, u32[]{:S(2)}) collective-permute-start(bf16[256,512]{1,0:T(8,128)(2,1)S(1)} %constant_dynamic-slice_fusion.refs_0_.refs_13_.refs_1_), channel_id=1, source_target_pairs={{0,4},{4,0},{8,12},{12,8},{1,5},{5,1},{9,13},{13,9},{2,6},{6,2},{1... | collective-permute-start | bytes 786440 | tf_op jit(solution)/shard_map/ppermute | solution.py:20
  6.3 2.6 %collective-permute-start = (bf16[256,512]{1,0:T(8,128)(2,1)S(1)}, bf16[256,512]{1,0:T(8,128)(2,1)S(1)}, u32[]{:S(2)}, u32[]{:S(2)}) collective-permute-start(bf16[256,512]{1,0:T(8,128)(2,1)S(1)} %constant_dynamic-slice_fusion.refs_0_.refs_13_.refs_1_), channel_id=1, source_target_pairs={{0,8},{4,12},{8,0},{12,4},{1,9},{5,13},{9,1},{13,5},{2,10},{6,14},... | collective-permute-start | bytes 786440 | tf_op jit(solution)/shard_map/ppermute | solution.py:20
  8.8 0.7 %reshape.10.spread_ref = bf16[1,512]{1,0:T(2,128)(2,1)S(1)} reshape(bf16[512]{0:T(512)(128)(2,1)} %param.13) | data formatting | bytes 2048 | tf_op jit(solution)/shard_map/reshape | solution.py:90
  9.5 1.0 %copy-done.1 = bf16[512,512]{1,0:T(8,128)(2,1)S(1)} copy-done((bf16[512,512]{1,0:T(8,128)(2,1)S(1)}, bf16[512,512]{1,0:T(8,128)(2,1)}, u32[]{:S(2)}) %copy-start.1) | copy-done | bytes 524312
  10.6 0.9 %copy-done.5 = bf16[512,128]{1,0:T(8,128)(2,1)S(1)} copy-done((bf16[512,128]{1,0:T(8,128)(2,1)S(1)}, bf16[512,128]{1,0:T(8,128)(2,1)}, u32[]{:S(2)}) %copy-start.5) | copy-done | bytes 131096
  11.5 0.7 %copy-done.6 = f32[128]{0:T(128)S(1)} copy-done((f32[128]{0:T(128)S(1)}, f32[128]{0:T(128)}, u32[]{:S(2)}) %copy-start.6) | copy-done | bytes 536
  12.4 0.6 collective-permute-start.5
  13.0 1.0 %copy-done.3 = f32[1024,128]{1,0:T(8,128)S(1)} copy-done((f32[1024,128]{1,0:T(8,128)S(1)}, f32[1024,128]{1,0:T(8,128)}, u32[]{:S(2)}) %copy-start.3) | copy-done | bytes 524312
  14.0 1.0 %copy-done.4 = f32[1024,128]{1,0:T(8,128)S(1)} copy-done((f32[1024,128]{1,0:T(8,128)S(1)}, f32[1024,128]{1,0:T(8,128)}, u32[]{:S(2)}) %copy-start.4) | copy-done | bytes 524312
  15.5 3.5 %collective-permute-done.5.refs_6_ = bf16[144,512]{1,0:T(8,128)(2,1)S(1)} collective-permute-done((bf16[144,512]{1,0:T(8,128)(2,1)S(1)}, bf16[144,512]{1,0:T(8,128)(2,1)S(1)}, u32[]{:S(2)}, u32[]{:S(2)}) %collective-permute-start.5) | collective-permute-done | bytes 147488 | tf_op jit(solution)/shard_map/ppermute | solution.py:20
  19.0 1.3 %collective-permute-done.refs_0_ = bf16[256,512]{1,0:T(8,128)(2,1)S(1)} collective-permute-done((bf16[256,512]{1,0:T(8,128)(2,1)S(1)}, bf16[256,512]{1,0:T(8,128)(2,1)S(1)}, u32[]{:S(2)}, u32[]{:S(2)}) %collective-permute-start) | collective-permute-done | bytes 262176 | tf_op jit(solution)/shard_map/ppermute | solution.py:20
  20.9 0.6 collective-permute-start.20
  21.5 1.6 %collective-permute-start.1 = (bf16[256,512]{1,0:T(8,128)(2,1)S(1)}, bf16[256,512]{1,0:T(8,128)(2,1)S(1)}, u32[]{:S(2)}, u32[]{:S(2)}) collective-permute-start(bf16[256,512]{1,0:T(8,128)(2,1)S(1)} %collective-permute-done.refs_0_), channel_id=1, source_target_pairs={{0,4},{4,0},{8,12},{12,8},{1,5},{5,1},{9,13},{13,9},{2,6},{6,2},{1... | collective-permute-start | bytes 786440 | tf_op jit(solution)/shard_map/ppermute | solution.py:20
  23.1 1.3 %forward.3 = f32[256,128]{1,0:T(8,128)S(1)} custom-call(bf16[256,512]{1,0:T(8,128)(2,1)S(1)} %collective-permute-done.refs_0_, bf16[512,512]{1,0:T(8,128)(2,1)S(1)} %get-tuple-element.39.refs_1_.refs_11_.pos_ref, bf16[144,512]{1,0:T(8,128)(2,1)S(1)} %get-tuple-element.42.refs_2_, bf16[512,512]{1,0:T(8,128)(2,1)S(1)} %collective-permute-done.2.refs_3_, ...), custom_call_target="tpu_custom_call" | custom-call | flops 1 | bytes 1 | tf_op jit(solution)/shard_map/forward/pallas_call | solution.py:167
  24.4 2.7 %collective-permute-start.9 = (f32[256,128]{1,0:T(8,128)S(1)}, f32[256,128]{1,0:T(8,128)S(1)}, u32[]{:S(2)}, u32[]{:S(2)}) collective-permute-start(f32[256,128]{1,0:T(8,128)S(1)} %forward.3), channel_id=1, source_target_pairs={{0,8},{4,12},{8,0},{12,4},{1,9},{5,13},{9,1},{13,5},{2,10},{6,14},... | collective-permute-start | bytes 393224 | tf_op jit(solution)/shard_map/ppermute | solution.py:20
  27.0 1.3 %forward.4 = f32[256,128]{1,0:T(8,128)S(1)} custom-call(bf16[256,512]{1,0:T(8,128)(2,1)S(1)} %collective-permute-done.6.refs_0_, bf16[512,512]{1,0:T(8,128)(2,1)S(1)} %get-tuple-element.39.refs_1_.refs_11_.pos_ref, bf16[144,512]{1,0:T(8,128)(2,1)S(1)} %get-tuple-element.42.refs_2_, bf16[512,512]{1,0:T(8,128)(2,1)S(1)} %collective-permute-done.2.refs_3_, ...), custom_call_target="tpu_custom_call" | custom-call | flops 17179869184 | bytes 1048576 | tf_op jit(solution)/shard_map/forward/pallas_call | solution.py:167
  28.4 0.6 collective-permute-start.10
  29.0 4.4 %collective-permute-done.1.refs_0_.refs_15_.refs_3_ = bf16[256,512]{1,0:T(8,128)(2,1)S(1)} collective-permute-done((bf16[256,512]{1,0:T(8,128)(2,1)S(1)}, bf16[256,512]{1,0:T(8,128)(2,1)S(1)}, u32[]{:S(2)}, u32[]{:S(2)}) %collective-permute-start.1) | collective-permute-done | bytes 262176 | tf_op jit(solution)/shard_map/ppermute | solution.py:20
  33.4 1.3 %forward.5 = f32[256,128]{1,0:T(8,128)S(1)} custom-call(bf16[256,512]{1,0:T(8,128)(2,1)S(1)} %collective-permute-done.1.refs_0_.refs_15_.refs_3_, bf16[512,512]{1,0:T(8,128)(2,1)S(1)} %get-tuple-element.39.refs_1_.refs_11_.pos_ref, bf16[144,512]{1,0:T(8,128)(2,1)S(1)} %get-tuple-element.42.refs_2_, bf16[512,512]{1,0:T(8,128)(2,1)S(1)} %collective-permute-done.2.refs_3_, ...), custom_call_target="tpu_custom_call" | custom-call | flops 17179869184 | bytes 1048576 | tf_op jit(solution)/shard_map/forward/pallas_call | solution.py:167
  34.7 3.7 %collective-permute-start.11 = (f32[256,128]{1,0:T(8,128)S(1)}, f32[256,128]{1,0:T(8,128)S(1)}, u32[]{:S(2)}, u32[]{:S(2)}) collective-permute-start(f32[256,128]{1,0:T(8,128)S(1)} %forward.5), channel_id=1, source_target_pairs={{0,12},{4,8},{8,4},{12,0},{1,13},{5,9},{9,5},{13,1},{2,14},{6,10},... | collective-permute-start | bytes 393224 | tf_op jit(solution)/shard_map/ppermute | solution.py:20
  38.4 2.3 %own_rows.1 = (f32[256,128]{1,0:T(8,128)S(1)}, bf16[512,1024]{1,0:T(8,128)(2,1)S(1)}) custom-call(bf16[256,512]{1,0:T(8,128)(2,1)S(1)} %constant_dynamic-slice_fusion.refs_0_.refs_13_.refs_1_, bf16[512,512]{1,0:T(8,128)(2,1)S(1)} %get-tuple-element.39.refs_1_.refs_11_.pos_ref, bf16[144,512]{1,0:T(8,128)(2,1)S(1)} %get-tuple-element.42.refs_2_, ...), custom_call_target="tpu_custom_call" | custom-call | flops 17179869184 | bytes 1048576 | tf_op jit(solution)/shard_map/own_rows/pallas_call | solution.py:214
  40.7 1.0 %collective-permute-done.11.refs_1_ = f32[256,128]{1,0:T(8,128)S(1)} collective-permute-done((f32[256,128]{1,0:T(8,128)S(1)}, f32[256,128]{1,0:T(8,128)S(1)}, u32[]{:S(2)}, u32[]{:S(2)}) %collective-permute-start.11) | collective-permute-done | bytes 131104 | tf_op jit(solution)/shard_map/ppermute | solution.py:20
  41.8 1.3 %collective-permute-start.15 = (bf16[256,128]{1,0:T(8,128)(2,1)S(1)}, bf16[256,128]{1,0:T(8,128)(2,1)S(1)}, u32[]{:S(2)}, u32[]{:S(2)}) collective-permute-start(bf16[256,128]{1,0:T(8,128)(2,1)S(1)} %cotangent.1), channel_id=1, source_target_pairs={{0,8},{4,12},{8,0},{12,4},{1,9},{5,13},{9,1},{13,5},{2,10},{6,14},... | collective-permute-start | bytes 196616 | tf_op jit(solution)/shard_map/ppermute | solution.py:20
  43.0 3.7 %collective-permute-start.12 = (bf16[256,128]{1,0:T(8,128)(2,1)S(1)}, bf16[256,128]{1,0:T(8,128)(2,1)S(1)}, u32[]{:S(2)}, u32[]{:S(2)}) collective-permute-start(bf16[256,128]{1,0:T(8,128)(2,1)S(1)} %cotangent.1), channel_id=1, source_target_pairs={{0,4},{4,0},{8,12},{12,8},{1,5},{5,1},{9,13},{13,9},{2,6},{6,2},{1... | collective-permute-start | bytes 196616 | tf_op jit(solution)/shard_map/ppermute | solution.py:20
  47.4 1.6 %collective-permute-done.12 = bf16[256,128]{1,0:T(8,128)(2,1)S(1)} collective-permute-done((bf16[256,128]{1,0:T(8,128)(2,1)S(1)}, bf16[256,128]{1,0:T(8,128)(2,1)S(1)}, u32[]{:S(2)}, u32[]{:S(2)}) %collective-permute-start.12) | collective-permute-done | bytes 65568 | tf_op jit(solution)/shard_map/ppermute | solution.py:20
  48.9 2.0 %collective-permute-start.16 = (bf16[256,128]{1,0:T(8,128)(2,1)S(1)}, bf16[256,128]{1,0:T(8,128)(2,1)S(1)}, u32[]{:S(2)}, u32[]{:S(2)}) collective-permute-start(bf16[256,128]{1,0:T(8,128)(2,1)S(1)} %collective-permute-done.15), channel_id=1, source_target_pairs={{0,4},{4,0},{8,12},{12,8},{1,5},{5,1},{9,13},{13,9},{2,6},{6,2},{1... | collective-permute-start | bytes 196616 | tf_op jit(solution)/shard_map/ppermute | solution.py:20
  51.0 2.2 %collective-permute-done.16 = bf16[256,128]{1,0:T(8,128)(2,1)S(1)} collective-permute-done((bf16[256,128]{1,0:T(8,128)(2,1)S(1)}, bf16[256,128]{1,0:T(8,128)(2,1)S(1)}, u32[]{:S(2)}, u32[]{:S(2)}) %collective-permute-start.16) | collective-permute-done | bytes 65568 | tf_op jit(solution)/shard_map/ppermute | solution.py:20
  55.2 5.7 %backward.2 = (f32[512,512]{1,0:T(8,128)S(1)}, f32[512,128]{1,0:T(8,128)S(1)}, f32[512,128]{1,0:T(8,128)S(1)}, bf16[512,1024]{1,0:T(8,128)(2,1)S(1)}, bf16[512,1024]{1,0:T(8,128)(2,1)S(1)}) custom-call(bf16[512,512]{1,0:T(8,128)(2,1)S(1)} %get-tuple-element.39.refs_1_.refs_11_.pos_ref, bf16[512,128]{1,0:T(8,128)(2,1)S(1)} %get-tuple-element.40.coef_ref, ...), custom_call_target="tpu_custom_call" | custom-call | flops 17179869184 | bytes 1048576 | tf_op jit(solution)/shard_map/backward/pallas_call | solution.py:288
  61.2 1.3 %backward.3 = (f32[512,512]{1,0:T(8,128)S(1)}, f32[512,128]{1,0:T(8,128)S(1)}, f32[512,128]{1,0:T(8,128)S(1)}) custom-call(bf16[512,512]{1,0:T(8,128)(2,1)S(1)} %get-tuple-element.39.refs_1_.refs_11_.pos_ref, bf16[512,128]{1,0:T(8,128)(2,1)S(1)} %get-tuple-element.40.coef_ref, bf16[1,512]{1,0:T(2,128)(2,1)S(1)} %get-tuple-element.41.refs_12_.spread_ref, ...), custom_call_target="tpu_custom_call" | custom-call | flops 1 | bytes 1 | tf_op jit(solution)/shard_map/backward/pallas_call | solution.py:288
  62.6 2.3 %finish.1 = (f32[512,512]{1,0:T(8,128)}, f32[512,128]{1,0:T(8,128)}) custom-call(bf16[512,512]{1,0:T(8,128)(2,1)S(1)} %get-tuple-element.39.refs_1_.refs_11_.pos_ref, bf16[512,128]{1,0:T(8,128)(2,1)S(1)} %get-tuple-element.40.coef_ref, bf16[1,512]{1,0:T(2,128)(2,1)S(1)} %get-tuple-element.41.refs_12_.spread_ref, ...), custom_call_target="tpu_custom_call" | custom-call | flops 1 | bytes 1 | tf_op jit(solution)/shard_map/finish/pallas_call | solution.py:330
  (52 shorter events, 4.3 us)
Async XLA Ops:
  0.6 12.3 %copy-start = (bf16[1024,512]{1,0:T(8,128)(2,1)S(1)}, bf16[1024,512]{1,0:T(8,128)(2,1)}, u32[]{:S(2)}) copy-start(bf16[1024,512]{1,0:T(8,128)(2,1)} %refs_4_.1) | copy-start | bytes 3145732
  0.6 19.7 %collective-permute-start.4 = (bf16[512,512]{1,0:T(8,128)(2,1)}, bf16[512,512]{1,0:T(8,128)(2,1)S(1)}, u32[]{:S(2)}, u32[]{:S(2)}) collective-permute-start(bf16[512,512]{1,0:T(8,128)(2,1)} %pos_ref), channel_id=1, source_target_pairs={{0,2},{1,3},{2,0},{3,1},{4,6},{5,7},{6,4},{7,5},{8,10},{9,11},{10,... | collective-permute-start | bytes 1572872 | tf_op jit(solution)/shard_map/ppermute | solution.py:20
  4.6 14.3 %collective-permute-start.6 = (bf16[256,512]{1,0:T(8,128)(2,1)S(1)}, bf16[256,512]{1,0:T(8,128)(2,1)S(1)}, u32[]{:S(2)}, u32[]{:S(2)}) collective-permute-start(bf16[256,512]{1,0:T(8,128)(2,1)S(1)} %constant_dynamic-slice_fusion.refs_0_.refs_13_.refs_1_), channel_id=1, source_target_pairs={{0,4},{4,0},{8,12},{12,8},{1,5},{5,1},{9,13},{13,9},{2,6},{6,2},{1... | collective-permute-start | bytes 786440 | tf_op jit(solution)/shard_map/ppermute | solution.py:20
  6.3 14.0 %collective-permute-start = (bf16[256,512]{1,0:T(8,128)(2,1)S(1)}, bf16[256,512]{1,0:T(8,128)(2,1)S(1)}, u32[]{:S(2)}, u32[]{:S(2)}) collective-permute-start(bf16[256,512]{1,0:T(8,128)(2,1)S(1)} %constant_dynamic-slice_fusion.refs_0_.refs_13_.refs_1_), channel_id=1, source_target_pairs={{0,8},{4,12},{8,0},{12,4},{1,9},{5,13},{9,1},{13,5},{2,10},{6,14},... | collective-permute-start | bytes 786440 | tf_op jit(solution)/shard_map/ppermute | solution.py:20
  9.5 1.0 %copy-start.1 = (bf16[512,512]{1,0:T(8,128)(2,1)S(1)}, bf16[512,512]{1,0:T(8,128)(2,1)}, u32[]{:S(2)}) copy-start(bf16[512,512]{1,0:T(8,128)(2,1)} %pos_ref) | copy-start | bytes 1572868
  10.6 0.9 %copy-start.5 = (bf16[512,128]{1,0:T(8,128)(2,1)S(1)}, bf16[512,128]{1,0:T(8,128)(2,1)}, u32[]{:S(2)}) copy-start(bf16[512,128]{1,0:T(8,128)(2,1)} %coef_ref.1) | copy-start | bytes 393220
  11.5 0.7 %copy-start.6 = (f32[128]{0:T(128)S(1)}, f32[128]{0:T(128)}, u32[]{:S(2)}) copy-start(f32[128]{0:T(128)} %param.10) | copy-start | bytes 1540
  12.3 6.6 %copy-start.2 = (bf16[512,512]{1,0:T(8,128)(2,1)S(1)}, bf16[512,512]{1,0:T(8,128)(2,1)}, u32[]{:S(2)}) copy-start(bf16[512,512]{1,0:T(8,128)(2,1)} %pos_ref) | copy-start | bytes 1572868
  12.4 6.6 %collective-permute-start.5 = (bf16[144,512]{1,0:T(8,128)(2,1)S(1)}, bf16[144,512]{1,0:T(8,128)(2,1)S(1)}, u32[]{:S(2)}, u32[]{:S(2)}) collective-permute-start(bf16[144,512]{1,0:T(8,128)(2,1)S(1)} %get-tuple-element.42.refs_2_), channel_id=1, source_target_pairs={{0,2},{1,3},{2,0},{3,1},{4,6},{5,7},{6,4},{7,5},{8,10},{9,11},{10,... | collective-permute-start | bytes 442376 | tf_op jit(solution)/shard_map/ppermute | solution.py:20
  13.0 6.0 %collective-permute-start.3 = (bf16[144,512]{1,0:T(8,128)(2,1)S(1)}, bf16[144,512]{1,0:T(8,128)(2,1)S(1)}, u32[]{:S(2)}, u32[]{:S(2)}) collective-permute-start(bf16[144,512]{1,0:T(8,128)(2,1)S(1)} %get-tuple-element.42.refs_2_), channel_id=1, source_target_pairs={{0,1},{1,0},{2,3},{3,2},{4,5},{5,4},{6,7},{7,6},{8,9},{9,8},{10,11... | collective-permute-start | bytes 442376 | tf_op jit(solution)/shard_map/ppermute | solution.py:20
  13.0 1.0 %copy-start.3 = (f32[1024,128]{1,0:T(8,128)S(1)}, f32[1024,128]{1,0:T(8,128)}, u32[]{:S(2)}) copy-start(f32[1024,128]{1,0:T(8,128)} %refs_0_.1) | copy-start | bytes 1572868
  14.0 1.0 %copy-start.4 = (f32[1024,128]{1,0:T(8,128)S(1)}, f32[1024,128]{1,0:T(8,128)}, u32[]{:S(2)}) copy-start(f32[1024,128]{1,0:T(8,128)} %refs_1_.1) | copy-start | bytes 1572868
  18.9 4.1 %collective-permute-start.2 = (bf16[512,512]{1,0:T(8,128)(2,1)S(1)}, bf16[512,512]{1,0:T(8,128)(2,1)S(1)}, u32[]{:S(2)}, u32[]{:S(2)}) collective-permute-start(bf16[512,512]{1,0:T(8,128)(2,1)S(1)} %copy-done.2), channel_id=1, source_target_pairs={{0,1},{1,0},{2,3},{3,2},{4,5},{5,4},{6,7},{7,6},{8,9},{9,8},{10,11... | collective-permute-start | bytes 1572872 | tf_op jit(solution)/shard_map/ppermute | solution.py:20
  20.3 2.8 %collective-permute-start.7 = (bf16[512,512]{1,0:T(8,128)(2,1)S(1)}, bf16[512,512]{1,0:T(8,128)(2,1)S(1)}, u32[]{:S(2)}, u32[]{:S(2)}) collective-permute-start(bf16[512,512]{1,0:T(8,128)(2,1)S(1)} %collective-permute-done.4.refs_5_), channel_id=1, source_target_pairs={{0,1},{1,0},{2,3},{3,2},{4,5},{5,4},{6,7},{7,6},{8,9},{9,8},{10,11... | collective-permute-start | bytes 1572872 | tf_op jit(solution)/shard_map/ppermute | solution.py:20
  20.3 2.7 %collective-permute-start.8 = (bf16[144,512]{1,0:T(8,128)(2,1)S(1)}, bf16[144,512]{1,0:T(8,128)(2,1)S(1)}, u32[]{:S(2)}, u32[]{:S(2)}) collective-permute-start(bf16[144,512]{1,0:T(8,128)(2,1)S(1)} %collective-permute-done.5.refs_6_), channel_id=1, source_target_pairs={{0,1},{1,0},{2,3},{3,2},{4,5},{5,4},{6,7},{7,6},{8,9},{9,8},{10,11... | collective-permute-start | bytes 442376 | tf_op jit(solution)/shard_map/ppermute | solution.py:20
  20.9 25.8 %collective-permute-start.20 = (bf16[512,512]{1,0:T(8,128)(2,1)S(1)}, bf16[512,512]{1,0:T(8,128)(2,1)S(1)}, u32[]{:S(2)}, u32[]{:S(2)}) collective-permute-start(bf16[512,512]{1,0:T(8,128)(2,1)S(1)} %constant_dynamic-update-slice_fusion.refs_14_.refs_2_), channel_id=1, source_target_pairs={{0,2},{1,3},{2,0},{3,1},{4,6},{5,7},{6,4},{7,5},{8,10},{9,11},{10,... | collective-permute-start | bytes 1572872 | tf_op jit(solution)/shard_map/ppermute | solution.py:20
  21.5 12.0 %collective-permute-start.1 = (bf16[256,512]{1,0:T(8,128)(2,1)S(1)}, bf16[256,512]{1,0:T(8,128)(2,1)S(1)}, u32[]{:S(2)}, u32[]{:S(2)}) collective-permute-start(bf16[256,512]{1,0:T(8,128)(2,1)S(1)} %collective-permute-done.refs_0_), channel_id=1, source_target_pairs={{0,4},{4,0},{8,12},{12,8},{1,5},{5,1},{9,13},{13,9},{2,6},{6,2},{1... | collective-permute-start | bytes 786440 | tf_op jit(solution)/shard_map/ppermute | solution.py:20
  24.4 14.0 %collective-permute-start.9 = (f32[256,128]{1,0:T(8,128)S(1)}, f32[256,128]{1,0:T(8,128)S(1)}, u32[]{:S(2)}, u32[]{:S(2)}) collective-permute-start(f32[256,128]{1,0:T(8,128)S(1)} %forward.3), channel_id=1, source_target_pairs={{0,8},{4,12},{8,0},{12,4},{1,9},{5,13},{9,1},{13,5},{2,10},{6,14},... | collective-permute-start | bytes 393224 | tf_op jit(solution)/shard_map/ppermute | solution.py:20
  28.4 10.1 %collective-permute-start.10 = (f32[256,128]{1,0:T(8,128)S(1)}, f32[256,128]{1,0:T(8,128)S(1)}, u32[]{:S(2)}, u32[]{:S(2)}) collective-permute-start(f32[256,128]{1,0:T(8,128)S(1)} %forward.4), channel_id=1, source_target_pairs={{0,4},{4,0},{8,12},{12,8},{1,5},{5,1},{9,13},{13,9},{2,6},{6,2},{1... | collective-permute-start | bytes 393224 | tf_op jit(solution)/shard_map/ppermute | solution.py:20
  34.7 6.9 %collective-permute-start.11 = (f32[256,128]{1,0:T(8,128)S(1)}, f32[256,128]{1,0:T(8,128)S(1)}, u32[]{:S(2)}, u32[]{:S(2)}) collective-permute-start(f32[256,128]{1,0:T(8,128)S(1)} %forward.5), channel_id=1, source_target_pairs={{0,12},{4,8},{8,4},{12,0},{1,13},{5,9},{9,5},{13,1},{2,14},{6,10},... | collective-permute-start | bytes 393224 | tf_op jit(solution)/shard_map/ppermute | solution.py:20
  38.4 8.3 %collective-permute-start.13 = (bf16[256,512]{1,0:T(8,128)(2,1)S(1)}, bf16[256,512]{1,0:T(8,128)(2,1)S(1)}, u32[]{:S(2)}, u32[]{:S(2)}) collective-permute-start(bf16[256,512]{1,0:T(8,128)(2,1)S(1)} %collective-permute-done.1.refs_0_.refs_15_.refs_3_), channel_id=1, source_target_pairs={{0,2},{1,3},{2,0},{3,1},{4,6},{5,7},{6,4},{7,5},{8,10},{9,11},{10,... | collective-permute-start | bytes 786440 | tf_op jit(solution)/shard_map/ppermute | solution.py:20
  41.8 5.5 %collective-permute-start.15 = (bf16[256,128]{1,0:T(8,128)(2,1)S(1)}, bf16[256,128]{1,0:T(8,128)(2,1)S(1)}, u32[]{:S(2)}, u32[]{:S(2)}) collective-permute-start(bf16[256,128]{1,0:T(8,128)(2,1)S(1)} %cotangent.1), channel_id=1, source_target_pairs={{0,8},{4,12},{8,0},{12,4},{1,9},{5,13},{9,1},{13,5},{2,10},{6,14},... | collective-permute-start | bytes 196616 | tf_op jit(solution)/shard_map/ppermute | solution.py:20
  43.0 5.9 %collective-permute-start.12 = (bf16[256,128]{1,0:T(8,128)(2,1)S(1)}, bf16[256,128]{1,0:T(8,128)(2,1)S(1)}, u32[]{:S(2)}, u32[]{:S(2)}) collective-permute-start(bf16[256,128]{1,0:T(8,128)(2,1)S(1)} %cotangent.1), channel_id=1, source_target_pairs={{0,4},{4,0},{8,12},{12,8},{1,5},{5,1},{9,13},{13,9},{2,6},{6,2},{1... | collective-permute-start | bytes 196616 | tf_op jit(solution)/shard_map/ppermute | solution.py:20
  46.7 4.3 %collective-permute-start.14 = (bf16[256,128]{1,0:T(8,128)(2,1)S(1)}, bf16[256,128]{1,0:T(8,128)(2,1)S(1)}, u32[]{:S(2)}, u32[]{:S(2)}) collective-permute-start(bf16[256,128]{1,0:T(8,128)(2,1)S(1)} %cotangent.1), channel_id=1, source_target_pairs={{0,2},{1,3},{2,0},{3,1},{4,6},{5,7},{6,4},{7,5},{8,10},{9,11},{10,... | collective-permute-start | bytes 196616 | tf_op jit(solution)/shard_map/ppermute | solution.py:20
  46.7 7.2 %collective-permute-start.18 = (bf16[256,512]{1,0:T(8,128)(2,1)S(1)}, bf16[256,512]{1,0:T(8,128)(2,1)S(1)}, u32[]{:S(2)}, u32[]{:S(2)}) collective-permute-start(bf16[256,512]{1,0:T(8,128)(2,1)S(1)} %collective-permute-done.1.refs_0_.refs_15_.refs_3_), channel_id=1, source_target_pairs={{0,1},{1,0},{2,3},{3,2},{4,5},{5,4},{6,7},{7,6},{8,9},{9,8},{10,11... | collective-permute-start | bytes 786440 | tf_op jit(solution)/shard_map/ppermute | solution.py:20
  46.8 7.7 %collective-permute-start.17 = (bf16[512,512]{1,0:T(8,128)(2,1)S(1)}, bf16[512,512]{1,0:T(8,128)(2,1)S(1)}, u32[]{:S(2)}, u32[]{:S(2)}) collective-permute-start(bf16[512,512]{1,0:T(8,128)(2,1)S(1)} %constant_dynamic-update-slice_fusion.refs_14_.refs_2_), channel_id=1, source_target_pairs={{0,1},{1,0},{2,3},{3,2},{4,5},{5,4},{6,7},{7,6},{8,9},{9,8},{10,11... | collective-permute-start | bytes 1572872 | tf_op jit(solution)/shard_map/ppermute | solution.py:20
  47.3 7.2 %collective-permute-start.21 = (bf16[512,512]{1,0:T(8,128)(2,1)S(1)}, bf16[512,512]{1,0:T(8,128)(2,1)S(1)}, u32[]{:S(2)}, u32[]{:S(2)}) collective-permute-start(bf16[512,512]{1,0:T(8,128)(2,1)S(1)} %collective-permute-done.20.refs_10_.refs_2_), channel_id=1, source_target_pairs={{0,1},{1,0},{2,3},{3,2},{4,5},{5,4},{6,7},{7,6},{8,9},{9,8},{10,11... | collective-permute-start | bytes 1572872 | tf_op jit(solution)/shard_map/ppermute | solution.py:20
  48.9 4.3 %collective-permute-start.16 = (bf16[256,128]{1,0:T(8,128)(2,1)S(1)}, bf16[256,128]{1,0:T(8,128)(2,1)S(1)}, u32[]{:S(2)}, u32[]{:S(2)}) collective-permute-start(bf16[256,128]{1,0:T(8,128)(2,1)S(1)} %collective-permute-done.15), channel_id=1, source_target_pairs={{0,4},{4,0},{8,12},{12,8},{1,5},{5,1},{9,13},{13,9},{2,6},{6,2},{1... | collective-permute-start | bytes 196616 | tf_op jit(solution)/shard_map/ppermute | solution.py:20
  53.2 1.6 %collective-permute-start.22 = (bf16[256,512]{1,0:T(8,128)(2,1)S(1)}, bf16[256,512]{1,0:T(8,128)(2,1)S(1)}, u32[]{:S(2)}, u32[]{:S(2)}) collective-permute-start(bf16[256,512]{1,0:T(8,128)(2,1)S(1)} %collective-permute-done.13.refs_11_.refs_3_), channel_id=1, source_target_pairs={{0,1},{1,0},{2,3},{3,2},{4,5},{5,4},{6,7},{7,6},{8,9},{9,8},{10,11... | collective-permute-start | bytes 786440 | tf_op jit(solution)/shard_map/ppermute | solution.py:20
  53.3 1.9 %collective-permute-start.19 = (bf16[1024,128]{1,0:T(8,128)(2,1)S(1)}, bf16[1024,128]{1,0:T(8,128)(2,1)S(1)}, u32[]{:S(2)}, u32[]{:S(2)}) collective-permute-start(bf16[1024,128]{1,0:T(8,128)(2,1)S(1)} %pad_maximum_fusion.refs_4_), channel_id=1, source_target_pairs={{0,1},{1,0},{2,3},{3,2},{4,5},{5,4},{6,7},{7,6},{8,9},{9,8},{10,11... | collective-permute-start | bytes 786440 | tf_op jit(solution)/shard_map/ppermute | solution.py:20
  53.9 7.0 %collective-permute-start.23 = (bf16[768,128]{1,0:T(8,128)(2,1)S(1)}, bf16[768,128]{1,0:T(8,128)(2,1)S(1)}, u32[]{:S(2)}, u32[]{:S(2)}) collective-permute-start(bf16[768,128]{1,0:T(8,128)(2,1)S(1)} %constant_dynamic-update-slice_fusion.2), channel_id=1, source_target_pairs={{0,2},{1,3},{2,0},{3,1},{4,6},{5,7},{6,4},{7,5},{8,10},{9,11},{10,... | collective-permute-start | bytes 589832 | tf_op jit(solution)/shard_map/ppermute | solution.py:20
  60.9 1.6 %collective-permute-start.24 = (bf16[1024,128]{1,0:T(8,128)(2,1)S(1)}, bf16[1024,128]{1,0:T(8,128)(2,1)S(1)}, u32[]{:S(2)}, u32[]{:S(2)}) collective-permute-start(bf16[1024,128]{1,0:T(8,128)(2,1)S(1)} %constant_dynamic-update-slice_fusion.5.refs_4_), channel_id=1, source_target_pairs={{0,1},{1,0},{2,3},{3,2},{4,5},{5,4},{6,7},{7,6},{8,9},{9,8},{10,11... | collective-permute-start | bytes 786440 | tf_op jit(solution)/shard_map/ppermute | solution.py:20

commit v14 on v13

--- a/solution.py
+++ b/solution.py
@@ -411,7 +411,10 @@
 
         far = {dz: swap(cot, "points", nz, dz) for dz in range(2, nz, 2)}
         far[1] = swap(cot, "points", nz, 1)
-        far.update({dz: swap(far[dz - 1], "points", nz, 1) for dz in range(3, nz, 2)})
+        for d in range(2, nc, 2):
+            kernels[d] = own_kernel(center_pos, spread, [local[d], early[d], late[d]])
+        held = [kernels[d] for d in range(2, nc, 2)]
+        far.update({dz: swap(after(far[dz - 1], *held), "points", nz, 1) for dz in range(3, nz, 2)})
         ahead = {d: swap(after(cot, late[d]), "centers", nc, d) for d in range(2, nc, 2)}
         far[1] = after(far[1], *ahead.values())
         far = jnp.concatenate([far[dz] for dz in range(1, nz)])
@@ -424,10 +427,10 @@
 
         points = {d: [local[d], early[d], late[d]] for d in range(nc)}
         groups = [(kernels[d], points[d], cots[d]) for d in (0, 1)]
-        *sums, kernels[2], kernels[3] = backward(
-            center_pos, coefficients, spread, groups, more=[points[2], points[3]]
+        *sums, kernels[3] = backward(
+            center_pos, coefficients, spread, groups, more=[points[3]]
         )
-        for d in range(4, nc):
+        for d in range(5, nc, 2):
             kernels[d] = own_kernel(center_pos, spread, points[d])
         for d in range(2, nc, 2):
             cots[d] = jnp.concatenate([after(a, sums[0]) for a in across[d]])

time: 65.2 us -> 65.1 us (level)
  waiting for transfers between devices: 14.8 us -> 13.5 us
  starting transfers between devices: 26.6 us -> 27.6 us
    ppermute x25, waiting for transfers between devices: 14.8 us -> 13.5 us  [swap(): return lax.ppermute(a, axis, [(i, i ^ d) for i in range(size)])]
    pallas_call x0 -> x1, Pallas kernels: none -> 1.06 us  [own_kernel(): pl.pallas_call(body, out_shape=jax.ShapeDtypeStruct((n, points), BF16), i...]
    ppermute x25, starting transfers between devices: 26.6 us -> 27.6 us  [swap(): return lax.ppermute(a, axis, [(i, i ^ d) for i in range(size)])]
    pallas_call x2, Pallas kernels: 6.98 us -> 6.09 us  [backward(): pl.pallas_call(body, out_shape=tuple((jax.ShapeDtypeStruct((n, width), F3...]
  transfers between devices with their start and end apart: 25 -> 25, of which waited for: 8 -> 8; matrix products, arithmetic and copies ran while one was open for 3% -> 3% of each run, Pallas kernels for 21% -> 22%
where the time goes in v14:
time: 65.1 us; the launch traced here: 64.7 us
  starting transfers between devices  27.6 us (42%)
  Pallas kernels  16.4 us (25%)
  waiting for transfers between devices  13.5 us (21%)
  local copies, waits for them, and re-layouts  6.44 us (10%)
  between operations  0.84 us (1%)
    ppermute x25, starting transfers between devices, swap(): return lax.ppermute(a, axis, [(i, i ^ d) for i in range(size)])  27.6 us
    ppermute x25, waiting for transfers between devices, swap(): return lax.ppermute(a, axis, [(i, i ^ d) for i in range(size)])  13.5 us
    pallas_call x2, Pallas kernels, backward(): pl.pallas_call(body, out_shape=tuple((jax.ShapeDtypeStruct((n, width), F3...  6.09 us
    unnamed x18, local copies, waits for them, and re-layouts  4.74 us
    pallas_call x3, Pallas kernels, forward(): pl.pallas_call(body, out_shape=tuple((jax.ShapeDtypeStruct((count, out_wi...  3.93 us
    pallas_call x1, Pallas kernels, finish(): pl.pallas_call(body, out_shape=tuple((jax.ShapeDtypeStruct((n, width), F3...  2.31 us
    pallas_call x1, Pallas kernels, own_rows(): pl.pallas_call(body, out_shape=(jax.ShapeDtypeStruct((rows.shape[0], out_...  2.3 us
  transfers between devices with their start and end apart: 25, of which 8 were waited for; matrix products, arithmetic and copies ran while one was open for 3% of the time, Pallas kernels for 22%

profile of v14, /device:TPU:0, one launch (start us, length us, event | category | flops | bytes accessed | tf_op | source)
XLA Modules:
  0.0 64.7 jit_solution(11451861662436669419)
XLA Ops:
  0.6 3.0 %collective-permute-start.4 = (bf16[512,512]{1,0:T(8,128)(2,1)}, bf16[512,512]{1,0:T(8,128)(2,1)S(1)}, u32[]{:S(2)}, u32[]{:S(2)}) collective-permute-start(bf16[512,512]{1,0:T(8,128)(2,1)} %pos_ref), channel_id=1, source_target_pairs={{0,2},{1,3},{2,0},{3,1},{4,6},{5,7},{6,4},{7,5},{8,10},{9,11},{10,... | collective-permute-start | bytes 1572872 | tf_op jit(solution)/shard_map/ppermute | solution.py:20
  3.6 1.0 %constant_dynamic-slice_fusion.refs_0_.refs_13_.refs_1_ = bf16[256,512]{1,0:T(8,128)(2,1)S(1)} fusion(bf16[1024,512]{1,0:T(8,128)(2,1)} %refs_4_.1, s32[]{:T(128)S(6)} %select_n.3), kind=kLoop, calls=%fused_computation.8 | loop fusion | bytes 524292 | tf_op jit(solution)/shard_map/dynamic_slice | solution.py:354
  4.6 1.6 %collective-permute-start.6 = (bf16[256,512]{1,0:T(8,128)(2,1)S(1)}, bf16[256,512]{1,0:T(8,128)(2,1)S(1)}, u32[]{:S(2)}, u32[]{:S(2)}) collective-permute-start(bf16[256,512]{1,0:T(8,128)(2,1)S(1)} %constant_dynamic-slice_fusion.refs_0_.refs_13_.refs_1_), channel_id=1, source_target_pairs={{0,4},{4,0},{8,12},{12,8},{1,5},{5,1},{9,13},{13,9},{2,6},{6,2},{1... | collective-permute-start | bytes 786440 | tf_op jit(solution)/shard_map/ppermute | solution.py:20
  6.3 2.6 %collective-permute-start = (bf16[256,512]{1,0:T(8,128)(2,1)S(1)}, bf16[256,512]{1,0:T(8,128)(2,1)S(1)}, u32[]{:S(2)}, u32[]{:S(2)}) collective-permute-start(bf16[256,512]{1,0:T(8,128)(2,1)S(1)} %constant_dynamic-slice_fusion.refs_0_.refs_13_.refs_1_), channel_id=1, source_target_pairs={{0,8},{4,12},{8,0},{12,4},{1,9},{5,13},{9,1},{13,5},{2,10},{6,14},... | collective-permute-start | bytes 786440 | tf_op jit(solution)/shard_map/ppermute | solution.py:20
  8.8 0.7 %reshape.10.spread_ref = bf16[1,512]{1,0:T(2,128)(2,1)S(1)} reshape(bf16[512]{0:T(512)(128)(2,1)} %param.13) | data formatting | bytes 2048 | tf_op jit(solution)/shard_map/reshape | solution.py:90
  9.5 1.0 %copy-done.1 = bf16[512,512]{1,0:T(8,128)(2,1)S(1)} copy-done((bf16[512,512]{1,0:T(8,128)(2,1)S(1)}, bf16[512,512]{1,0:T(8,128)(2,1)}, u32[]{:S(2)}) %copy-start.1) | copy-done | bytes 524312
  10.6 0.9 %copy-done.5 = bf16[512,128]{1,0:T(8,128)(2,1)S(1)} copy-done((bf16[512,128]{1,0:T(8,128)(2,1)S(1)}, bf16[512,128]{1,0:T(8,128)(2,1)}, u32[]{:S(2)}) %copy-start.5) | copy-done | bytes 131096
  11.5 0.7 %copy-done.6 = f32[128]{0:T(128)S(1)} copy-done((f32[128]{0:T(128)S(1)}, f32[128]{0:T(128)}, u32[]{:S(2)}) %copy-start.6) | copy-done | bytes 536
  13.0 1.0 %copy-done.3 = f32[1024,128]{1,0:T(8,128)S(1)} copy-done((f32[1024,128]{1,0:T(8,128)S(1)}, f32[1024,128]{1,0:T(8,128)}, u32[]{:S(2)}) %copy-start.3) | copy-done | bytes 524312
  14.0 1.0 %copy-done.4 = f32[1024,128]{1,0:T(8,128)S(1)} copy-done((f32[1024,128]{1,0:T(8,128)S(1)}, f32[1024,128]{1,0:T(8,128)}, u32[]{:S(2)}) %copy-start.4) | copy-done | bytes 524312
  15.5 3.5 %collective-permute-done.5.refs_6_ = bf16[144,512]{1,0:T(8,128)(2,1)S(1)} collective-permute-done((bf16[144,512]{1,0:T(8,128)(2,1)S(1)}, bf16[144,512]{1,0:T(8,128)(2,1)S(1)}, u32[]{:S(2)}, u32[]{:S(2)}) %collective-permute-start.5) | collective-permute-done | bytes 147488 | tf_op jit(solution)/shard_map/ppermute | solution.py:20
  19.0 1.3 %collective-permute-done.refs_0_ = bf16[256,512]{1,0:T(8,128)(2,1)S(1)} collective-permute-done((bf16[256,512]{1,0:T(8,128)(2,1)S(1)}, bf16[256,512]{1,0:T(8,128)(2,1)S(1)}, u32[]{:S(2)}, u32[]{:S(2)}) %collective-permute-start) | collective-permute-done | bytes 262176 | tf_op jit(solution)/shard_map/ppermute | solution.py:20
  20.9 0.6 collective-permute-start.16
  21.5 1.6 %collective-permute-start.1 = (bf16[256,512]{1,0:T(8,128)(2,1)S(1)}, bf16[256,512]{1,0:T(8,128)(2,1)S(1)}, u32[]{:S(2)}, u32[]{:S(2)}) collective-permute-start(bf16[256,512]{1,0:T(8,128)(2,1)S(1)} %collective-permute-done.refs_0_), channel_id=1, source_target_pairs={{0,4},{4,0},{8,12},{12,8},{1,5},{5,1},{9,13},{13,9},{2,6},{6,2},{1... | collective-permute-start | bytes 786440 | tf_op jit(solution)/shard_map/ppermute | solution.py:20
  23.1 1.3 %forward.3 = f32[256,128]{1,0:T(8,128)S(1)} custom-call(bf16[256,512]{1,0:T(8,128)(2,1)S(1)} %collective-permute-done.refs_0_, bf16[512,512]{1,0:T(8,128)(2,1)S(1)} %get-tuple-element.39.refs_1_.refs_11_.pos_ref, bf16[144,512]{1,0:T(8,128)(2,1)S(1)} %get-tuple-element.42.refs_2_, bf16[512,512]{1,0:T(8,128)(2,1)S(1)} %collective-permute-done.2.refs_3_, ...), custom_call_target="tpu_custom_call" | custom-call | flops 1 | bytes 1 | tf_op jit(solution)/shard_map/forward/pallas_call | solution.py:167
  24.4 2.7 %collective-permute-start.9 = (f32[256,128]{1,0:T(8,128)S(1)}, f32[256,128]{1,0:T(8,128)S(1)}, u32[]{:S(2)}, u32[]{:S(2)}) collective-permute-start(f32[256,128]{1,0:T(8,128)S(1)} %forward.3), channel_id=1, source_target_pairs={{0,8},{4,12},{8,0},{12,4},{1,9},{5,13},{9,1},{13,5},{2,10},{6,14},... | collective-permute-start | bytes 393224 | tf_op jit(solution)/shard_map/ppermute | solution.py:20
  27.0 1.3 %forward.4 = f32[256,128]{1,0:T(8,128)S(1)} custom-call(bf16[256,512]{1,0:T(8,128)(2,1)S(1)} %collective-permute-done.6.refs_0_, bf16[512,512]{1,0:T(8,128)(2,1)S(1)} %get-tuple-element.39.refs_1_.refs_11_.pos_ref, bf16[144,512]{1,0:T(8,128)(2,1)S(1)} %get-tuple-element.42.refs_2_, bf16[512,512]{1,0:T(8,128)(2,1)S(1)} %collective-permute-done.2.refs_3_, ...), custom_call_target="tpu_custom_call" | custom-call | flops 17179869184 | bytes 1048576 | tf_op jit(solution)/shard_map/forward/pallas_call | solution.py:167
  28.4 0.6 %collective-permute-start.10 = (f32[256,128]{1,0:T(8,128)S(1)}, f32[256,128]{1,0:T(8,128)S(1)}, u32[]{:S(2)}, u32[]{:S(2)}) collective-permute-start(f32[256,128]{1,0:T(8,128)S(1)} %forward.4), channel_id=1, source_target_pairs={{0,4},{4,0},{8,12},{12,8},{1,5},{5,1},{9,13},{13,9},{2,6},{6,2},{1... | collective-permute-start | bytes 393224 | tf_op jit(solution)/shard_map/ppermute | solution.py:20
  29.0 4.4 %collective-permute-done.1.refs_0_.refs_15_.refs_3_ = bf16[256,512]{1,0:T(8,128)(2,1)S(1)} collective-permute-done((bf16[256,512]{1,0:T(8,128)(2,1)S(1)}, bf16[256,512]{1,0:T(8,128)(2,1)S(1)}, u32[]{:S(2)}, u32[]{:S(2)}) %collective-permute-start.1) | collective-permute-done | bytes 262176 | tf_op jit(solution)/shard_map/ppermute | solution.py:20
  33.4 1.3 %forward.5 = f32[256,128]{1,0:T(8,128)S(1)} custom-call(bf16[256,512]{1,0:T(8,128)(2,1)S(1)} %collective-permute-done.1.refs_0_.refs_15_.refs_3_, bf16[512,512]{1,0:T(8,128)(2,1)S(1)} %get-tuple-element.39.refs_1_.refs_11_.pos_ref, bf16[144,512]{1,0:T(8,128)(2,1)S(1)} %get-tuple-element.42.refs_2_, bf16[512,512]{1,0:T(8,128)(2,1)S(1)} %collective-permute-done.2.refs_3_, ...), custom_call_target="tpu_custom_call" | custom-call | flops 17179869184 | bytes 1048576 | tf_op jit(solution)/shard_map/forward/pallas_call | solution.py:167
  34.7 3.7 %collective-permute-start.11 = (f32[256,128]{1,0:T(8,128)S(1)}, f32[256,128]{1,0:T(8,128)S(1)}, u32[]{:S(2)}, u32[]{:S(2)}) collective-permute-start(f32[256,128]{1,0:T(8,128)S(1)} %forward.5), channel_id=1, source_target_pairs={{0,12},{4,8},{8,4},{12,0},{1,13},{5,9},{9,5},{13,1},{2,14},{6,10},... | collective-permute-start | bytes 393224 | tf_op jit(solution)/shard_map/ppermute | solution.py:20
  38.4 2.3 %own_rows.1 = (f32[256,128]{1,0:T(8,128)S(1)}, bf16[512,1024]{1,0:T(8,128)(2,1)S(1)}) custom-call(bf16[256,512]{1,0:T(8,128)(2,1)S(1)} %constant_dynamic-slice_fusion.refs_0_.refs_13_.refs_1_, bf16[512,512]{1,0:T(8,128)(2,1)S(1)} %get-tuple-element.39.refs_1_.refs_11_.pos_ref, bf16[144,512]{1,0:T(8,128)(2,1)S(1)} %get-tuple-element.42.refs_2_, ...), custom_call_target="tpu_custom_call" | custom-call | flops 17179869184 | bytes 1048576 | tf_op jit(solution)/shard_map/own_rows/pallas_call | solution.py:214
  40.7 0.9 %collective-permute-done.11.refs_1_ = f32[256,128]{1,0:T(8,128)S(1)} collective-permute-done((f32[256,128]{1,0:T(8,128)S(1)}, f32[256,128]{1,0:T(8,128)S(1)}, u32[]{:S(2)}, u32[]{:S(2)}) %collective-permute-start.11) | collective-permute-done | bytes 131104 | tf_op jit(solution)/shard_map/ppermute | solution.py:20
  41.8 1.3 %collective-permute-start.15 = (bf16[256,128]{1,0:T(8,128)(2,1)S(1)}, bf16[256,128]{1,0:T(8,128)(2,1)S(1)}, u32[]{:S(2)}, u32[]{:S(2)}) collective-permute-start(bf16[256,128]{1,0:T(8,128)(2,1)S(1)} %cotangent.1), channel_id=1, source_target_pairs={{0,8},{4,12},{8,0},{12,4},{1,9},{5,13},{9,1},{13,5},{2,10},{6,14},... | collective-permute-start | bytes 196616 | tf_op jit(solution)/shard_map/ppermute | solution.py:20
  43.1 3.7 %collective-permute-start.12 = (bf16[256,128]{1,0:T(8,128)(2,1)S(1)}, bf16[256,128]{1,0:T(8,128)(2,1)S(1)}, u32[]{:S(2)}, u32[]{:S(2)}) collective-permute-start(bf16[256,128]{1,0:T(8,128)(2,1)S(1)} %cotangent.1), channel_id=1, source_target_pairs={{0,4},{4,0},{8,12},{12,8},{1,5},{5,1},{9,13},{13,9},{2,6},{6,2},{1... | collective-permute-start | bytes 196616 | tf_op jit(solution)/shard_map/ppermute | solution.py:20
  47.3 1.1 %own_kernel.1.refs_0_ = bf16[512,1024]{1,0:T(8,128)(2,1)S(1)} custom-call(bf16[512,512]{1,0:T(8,128)(2,1)S(1)} %get-tuple-element.39.refs_1_.refs_11_.pos_ref, bf16[1,512]{1,0:T(2,128)(2,1)S(1)} %get-tuple-element.41.refs_12_.spread_ref, bf16[256,512]{1,0:T(8,128)(2,1)S(1)} %get-tuple-element.56.refs_0_.refs_1_, ...), custom_call_target="tpu_custom_call" | custom-call | flops 1 | bytes 1 | tf_op jit(solution)/shard_map/own_kernel/pallas_call | solution.py:185
  49.0 2.0 %collective-permute-start.17 = (bf16[256,128]{1,0:T(8,128)(2,1)S(1)}, bf16[256,128]{1,0:T(8,128)(2,1)S(1)}, u32[]{:S(2)}, u32[]{:S(2)}) collective-permute-start(bf16[256,128]{1,0:T(8,128)(2,1)S(1)} %collective-permute-done.15), channel_id=1, source_target_pairs={{0,4},{4,0},{8,12},{12,8},{1,5},{5,1},{9,13},{13,9},{2,6},{6,2},{1... | collective-permute-start | bytes 196616 | tf_op jit(solution)/shard_map/ppermute | solution.py:20
  51.0 2.2 %collective-permute-done.17 = bf16[256,128]{1,0:T(8,128)(2,1)S(1)} collective-permute-done((bf16[256,128]{1,0:T(8,128)(2,1)S(1)}, bf16[256,128]{1,0:T(8,128)(2,1)S(1)}, u32[]{:S(2)}, u32[]{:S(2)}) %collective-permute-start.17) | collective-permute-done | bytes 65568 | tf_op jit(solution)/shard_map/ppermute | solution.py:20
  53.9 1.7 %collective-permute-start.23 = (bf16[768,128]{1,0:T(8,128)(2,1)S(1)}, bf16[768,128]{1,0:T(8,128)(2,1)S(1)}, u32[]{:S(2)}, u32[]{:S(2)}) collective-permute-start(bf16[768,128]{1,0:T(8,128)(2,1)S(1)} %constant_dynamic-update-slice_fusion.2), channel_id=1, source_target_pairs={{0,2},{1,3},{2,0},{3,1},{4,6},{5,7},{6,4},{7,5},{8,10},{9,11},{10,... | collective-permute-start | bytes 589832 | tf_op jit(solution)/shard_map/ppermute | solution.py:20
  55.6 4.8 %backward.2 = (f32[512,512]{1,0:T(8,128)S(1)}, f32[512,128]{1,0:T(8,128)S(1)}, f32[512,128]{1,0:T(8,128)S(1)}, bf16[512,1024]{1,0:T(8,128)(2,1)S(1)}) custom-call(bf16[512,512]{1,0:T(8,128)(2,1)S(1)} %get-tuple-element.39.refs_1_.refs_11_.pos_ref, bf16[512,128]{1,0:T(8,128)(2,1)S(1)} %get-tuple-element.40.coef_ref, ...), custom_call_target="tpu_custom_call" | custom-call | flops 17179869184 | bytes 1048576 | tf_op jit(solution)/shard_map/backward/pallas_call | solution.py:288
  60.9 1.3 %backward.3 = (f32[512,512]{1,0:T(8,128)S(1)}, f32[512,128]{1,0:T(8,128)S(1)}, f32[512,128]{1,0:T(8,128)S(1)}) custom-call(bf16[512,512]{1,0:T(8,128)(2,1)S(1)} %get-tuple-element.39.refs_1_.refs_11_.pos_ref, bf16[512,128]{1,0:T(8,128)(2,1)S(1)} %get-tuple-element.40.coef_ref, bf16[1,512]{1,0:T(2,128)(2,1)S(1)} %get-tuple-element.41.refs_12_.spread_ref, ...), custom_call_target="tpu_custom_call" | custom-call | flops 1 | bytes 1 | tf_op jit(solution)/shard_map/backward/pallas_call | solution.py:288
  62.4 2.3 %finish.1 = (f32[512,512]{1,0:T(8,128)}, f32[512,128]{1,0:T(8,128)}) custom-call(bf16[512,512]{1,0:T(8,128)(2,1)S(1)} %get-tuple-element.39.refs_1_.refs_11_.pos_ref, bf16[512,128]{1,0:T(8,128)(2,1)S(1)} %get-tuple-element.40.coef_ref, bf16[1,512]{1,0:T(2,128)(2,1)S(1)} %get-tuple-element.41.refs_12_.spread_ref, ...), custom_call_target="tpu_custom_call" | custom-call | flops 1 | bytes 1 | tf_op jit(solution)/shard_map/finish/pallas_call | solution.py:330
  (53 shorter events, 4.5 us)
Async XLA Ops:
  0.6 12.3 %copy-start = (bf16[1024,512]{1,0:T(8,128)(2,1)S(1)}, bf16[1024,512]{1,0:T(8,128)(2,1)}, u32[]{:S(2)}) copy-start(bf16[1024,512]{1,0:T(8,128)(2,1)} %refs_4_.1) | copy-start | bytes 3145732
  0.6 19.7 %collective-permute-start.4 = (bf16[512,512]{1,0:T(8,128)(2,1)}, bf16[512,512]{1,0:T(8,128)(2,1)S(1)}, u32[]{:S(2)}, u32[]{:S(2)}) collective-permute-start(bf16[512,512]{1,0:T(8,128)(2,1)} %pos_ref), channel_id=1, source_target_pairs={{0,2},{1,3},{2,0},{3,1},{4,6},{5,7},{6,4},{7,5},{8,10},{9,11},{10,... | collective-permute-start | bytes 1572872 | tf_op jit(solution)/shard_map/ppermute | solution.py:20
  4.6 14.3 %collective-permute-start.6 = (bf16[256,512]{1,0:T(8,128)(2,1)S(1)}, bf16[256,512]{1,0:T(8,128)(2,1)S(1)}, u32[]{:S(2)}, u32[]{:S(2)}) collective-permute-start(bf16[256,512]{1,0:T(8,128)(2,1)S(1)} %constant_dynamic-slice_fusion.refs_0_.refs_13_.refs_1_), channel_id=1, source_target_pairs={{0,4},{4,0},{8,12},{12,8},{1,5},{5,1},{9,13},{13,9},{2,6},{6,2},{1... | collective-permute-start | bytes 786440 | tf_op jit(solution)/shard_map/ppermute | solution.py:20
  6.3 14.0 %collective-permute-start = (bf16[256,512]{1,0:T(8,128)(2,1)S(1)}, bf16[256,512]{1,0:T(8,128)(2,1)S(1)}, u32[]{:S(2)}, u32[]{:S(2)}) collective-permute-start(bf16[256,512]{1,0:T(8,128)(2,1)S(1)} %constant_dynamic-slice_fusion.refs_0_.refs_13_.refs_1_), channel_id=1, source_target_pairs={{0,8},{4,12},{8,0},{12,4},{1,9},{5,13},{9,1},{13,5},{2,10},{6,14},... | collective-permute-start | bytes 786440 | tf_op jit(solution)/shard_map/ppermute | solution.py:20
  9.5 1.0 %copy-start.1 = (bf16[512,512]{1,0:T(8,128)(2,1)S(1)}, bf16[512,512]{1,0:T(8,128)(2,1)}, u32[]{:S(2)}) copy-start(bf16[512,512]{1,0:T(8,128)(2,1)} %pos_ref) | copy-start | bytes 1572868
  10.6 0.9 %copy-start.5 = (bf16[512,128]{1,0:T(8,128)(2,1)S(1)}, bf16[512,128]{1,0:T(8,128)(2,1)}, u32[]{:S(2)}) copy-start(bf16[512,128]{1,0:T(8,128)(2,1)} %coef_ref.1) | copy-start | bytes 393220
  11.5 0.7 %copy-start.6 = (f32[128]{0:T(128)S(1)}, f32[128]{0:T(128)}, u32[]{:S(2)}) copy-start(f32[128]{0:T(128)} %param.10) | copy-start | bytes 1540
  12.3 6.6 %copy-start.2 = (bf16[512,512]{1,0:T(8,128)(2,1)S(1)}, bf16[512,512]{1,0:T(8,128)(2,1)}, u32[]{:S(2)}) copy-start(bf16[512,512]{1,0:T(8,128)(2,1)} %pos_ref) | copy-start | bytes 1572868
  12.4 6.6 %collective-permute-start.5 = (bf16[144,512]{1,0:T(8,128)(2,1)S(1)}, bf16[144,512]{1,0:T(8,128)(2,1)S(1)}, u32[]{:S(2)}, u32[]{:S(2)}) collective-permute-start(bf16[144,512]{1,0:T(8,128)(2,1)S(1)} %get-tuple-element.42.refs_2_), channel_id=1, source_target_pairs={{0,2},{1,3},{2,0},{3,1},{4,6},{5,7},{6,4},{7,5},{8,10},{9,11},{10,... | collective-permute-start | bytes 442376 | tf_op jit(solution)/shard_map/ppermute | solution.py:20
  13.0 6.0 %collective-permute-start.3 = (bf16[144,512]{1,0:T(8,128)(2,1)S(1)}, bf16[144,512]{1,0:T(8,128)(2,1)S(1)}, u32[]{:S(2)}, u32[]{:S(2)}) collective-permute-start(bf16[144,512]{1,0:T(8,128)(2,1)S(1)} %get-tuple-element.42.refs_2_), channel_id=1, source_target_pairs={{0,1},{1,0},{2,3},{3,2},{4,5},{5,4},{6,7},{7,6},{8,9},{9,8},{10,11... | collective-permute-start | bytes 442376 | tf_op jit(solution)/shard_map/ppermute | solution.py:20
  13.0 1.0 %copy-start.3 = (f32[1024,128]{1,0:T(8,128)S(1)}, f32[1024,128]{1,0:T(8,128)}, u32[]{:S(2)}) copy-start(f32[1024,128]{1,0:T(8,128)} %refs_0_.1) | copy-start | bytes 1572868
  14.0 1.0 %copy-start.4 = (f32[1024,128]{1,0:T(8,128)S(1)}, f32[1024,128]{1,0:T(8,128)}, u32[]{:S(2)}) copy-start(f32[1024,128]{1,0:T(8,128)} %refs_1_.1) | copy-start | bytes 1572868
  18.9 4.1 %collective-permute-start.2 = (bf16[512,512]{1,0:T(8,128)(2,1)S(1)}, bf16[512,512]{1,0:T(8,128)(2,1)S(1)}, u32[]{:S(2)}, u32[]{:S(2)}) collective-permute-start(bf16[512,512]{1,0:T(8,128)(2,1)S(1)} %copy-done.2), channel_id=1, source_target_pairs={{0,1},{1,0},{2,3},{3,2},{4,5},{5,4},{6,7},{7,6},{8,9},{9,8},{10,11... | collective-permute-start | bytes 1572872 | tf_op jit(solution)/shard_map/ppermute | solution.py:20
  20.3 2.8 %collective-permute-start.7 = (bf16[512,512]{1,0:T(8,128)(2,1)S(1)}, bf16[512,512]{1,0:T(8,128)(2,1)S(1)}, u32[]{:S(2)}, u32[]{:S(2)}) collective-permute-start(bf16[512,512]{1,0:T(8,128)(2,1)S(1)} %collective-permute-done.4.refs_5_), channel_id=1, source_target_pairs={{0,1},{1,0},{2,3},{3,2},{4,5},{5,4},{6,7},{7,6},{8,9},{9,8},{10,11... | collective-permute-start | bytes 1572872 | tf_op jit(solution)/shard_map/ppermute | solution.py:20
  20.3 2.7 %collective-permute-start.8 = (bf16[144,512]{1,0:T(8,128)(2,1)S(1)}, bf16[144,512]{1,0:T(8,128)(2,1)S(1)}, u32[]{:S(2)}, u32[]{:S(2)}) collective-permute-start(bf16[144,512]{1,0:T(8,128)(2,1)S(1)} %collective-permute-done.5.refs_6_), channel_id=1, source_target_pairs={{0,1},{1,0},{2,3},{3,2},{4,5},{5,4},{6,7},{7,6},{8,9},{9,8},{10,11... | collective-permute-start | bytes 442376 | tf_op jit(solution)/shard_map/ppermute | solution.py:20
  20.9 25.9 %collective-permute-start.16 = (bf16[512,512]{1,0:T(8,128)(2,1)S(1)}, bf16[512,512]{1,0:T(8,128)(2,1)S(1)}, u32[]{:S(2)}, u32[]{:S(2)}) collective-permute-start(bf16[512,512]{1,0:T(8,128)(2,1)S(1)} %constant_dynamic-update-slice_fusion.refs_14_.refs_2_), channel_id=1, source_target_pairs={{0,2},{1,3},{2,0},{3,1},{4,6},{5,7},{6,4},{7,5},{8,10},{9,11},{10,... | collective-permute-start | bytes 1572872 | tf_op jit(solution)/shard_map/ppermute | solution.py:20
  21.5 12.0 %collective-permute-start.1 = (bf16[256,512]{1,0:T(8,128)(2,1)S(1)}, bf16[256,512]{1,0:T(8,128)(2,1)S(1)}, u32[]{:S(2)}, u32[]{:S(2)}) collective-permute-start(bf16[256,512]{1,0:T(8,128)(2,1)S(1)} %collective-permute-done.refs_0_), channel_id=1, source_target_pairs={{0,4},{4,0},{8,12},{12,8},{1,5},{5,1},{9,13},{13,9},{2,6},{6,2},{1... | collective-permute-start | bytes 786440 | tf_op jit(solution)/shard_map/ppermute | solution.py:20
  24.4 14.0 %collective-permute-start.9 = (f32[256,128]{1,0:T(8,128)S(1)}, f32[256,128]{1,0:T(8,128)S(1)}, u32[]{:S(2)}, u32[]{:S(2)}) collective-permute-start(f32[256,128]{1,0:T(8,128)S(1)} %forward.3), channel_id=1, source_target_pairs={{0,8},{4,12},{8,0},{12,4},{1,9},{5,13},{9,1},{13,5},{2,10},{6,14},... | collective-permute-start | bytes 393224 | tf_op jit(solution)/shard_map/ppermute | solution.py:20
  28.4 10.1 %collective-permute-start.10 = (f32[256,128]{1,0:T(8,128)S(1)}, f32[256,128]{1,0:T(8,128)S(1)}, u32[]{:S(2)}, u32[]{:S(2)}) collective-permute-start(f32[256,128]{1,0:T(8,128)S(1)} %forward.4), channel_id=1, source_target_pairs={{0,4},{4,0},{8,12},{12,8},{1,5},{5,1},{9,13},{13,9},{2,6},{6,2},{1... | collective-permute-start | bytes 393224 | tf_op jit(solution)/shard_map/ppermute | solution.py:20
  34.7 6.9 %collective-permute-start.11 = (f32[256,128]{1,0:T(8,128)S(1)}, f32[256,128]{1,0:T(8,128)S(1)}, u32[]{:S(2)}, u32[]{:S(2)}) collective-permute-start(f32[256,128]{1,0:T(8,128)S(1)} %forward.5), channel_id=1, source_target_pairs={{0,12},{4,8},{8,4},{12,0},{1,13},{5,9},{9,5},{13,1},{2,14},{6,10},... | collective-permute-start | bytes 393224 | tf_op jit(solution)/shard_map/ppermute | solution.py:20
  38.4 8.3 %collective-permute-start.13 = (bf16[256,512]{1,0:T(8,128)(2,1)S(1)}, bf16[256,512]{1,0:T(8,128)(2,1)S(1)}, u32[]{:S(2)}, u32[]{:S(2)}) collective-permute-start(bf16[256,512]{1,0:T(8,128)(2,1)S(1)} %collective-permute-done.1.refs_0_.refs_15_.refs_3_), channel_id=1, source_target_pairs={{0,2},{1,3},{2,0},{3,1},{4,6},{5,7},{6,4},{7,5},{8,10},{9,11},{10,... | collective-permute-start | bytes 786440 | tf_op jit(solution)/shard_map/ppermute | solution.py:20
  41.8 6.6 %collective-permute-start.15 = (bf16[256,128]{1,0:T(8,128)(2,1)S(1)}, bf16[256,128]{1,0:T(8,128)(2,1)S(1)}, u32[]{:S(2)}, u32[]{:S(2)}) collective-permute-start(bf16[256,128]{1,0:T(8,128)(2,1)S(1)} %cotangent.1), channel_id=1, source_target_pairs={{0,8},{4,12},{8,0},{12,4},{1,9},{5,13},{9,1},{13,5},{2,10},{6,14},... | collective-permute-start | bytes 196616 | tf_op jit(solution)/shard_map/ppermute | solution.py:20
  43.1 5.9 %collective-permute-start.12 = (bf16[256,128]{1,0:T(8,128)(2,1)S(1)}, bf16[256,128]{1,0:T(8,128)(2,1)S(1)}, u32[]{:S(2)}, u32[]{:S(2)}) collective-permute-start(bf16[256,128]{1,0:T(8,128)(2,1)S(1)} %cotangent.1), channel_id=1, source_target_pairs={{0,4},{4,0},{8,12},{12,8},{1,5},{5,1},{9,13},{13,9},{2,6},{6,2},{1... | collective-permute-start | bytes 196616 | tf_op jit(solution)/shard_map/ppermute | solution.py:20
  46.7 4.3 %collective-permute-start.14 = (bf16[256,128]{1,0:T(8,128)(2,1)S(1)}, bf16[256,128]{1,0:T(8,128)(2,1)S(1)}, u32[]{:S(2)}, u32[]{:S(2)}) collective-permute-start(bf16[256,128]{1,0:T(8,128)(2,1)S(1)} %cotangent.1), channel_id=1, source_target_pairs={{0,2},{1,3},{2,0},{3,1},{4,6},{5,7},{6,4},{7,5},{8,10},{9,11},{10,... | collective-permute-start | bytes 196616 | tf_op jit(solution)/shard_map/ppermute | solution.py:20
  46.7 7.2 %collective-permute-start.19 = (bf16[256,512]{1,0:T(8,128)(2,1)S(1)}, bf16[256,512]{1,0:T(8,128)(2,1)S(1)}, u32[]{:S(2)}, u32[]{:S(2)}) collective-permute-start(bf16[256,512]{1,0:T(8,128)(2,1)S(1)} %collective-permute-done.1.refs_0_.refs_15_.refs_3_), channel_id=1, source_target_pairs={{0,1},{1,0},{2,3},{3,2},{4,5},{5,4},{6,7},{7,6},{8,9},{9,8},{10,11... | collective-permute-start | bytes 786440 | tf_op jit(solution)/shard_map/ppermute | solution.py:20
  46.8 8.8 %collective-permute-start.18 = (bf16[512,512]{1,0:T(8,128)(2,1)S(1)}, bf16[512,512]{1,0:T(8,128)(2,1)S(1)}, u32[]{:S(2)}, u32[]{:S(2)}) collective-permute-start(bf16[512,512]{1,0:T(8,128)(2,1)S(1)} %constant_dynamic-update-slice_fusion.refs_14_.refs_2_), channel_id=1, source_target_pairs={{0,1},{1,0},{2,3},{3,2},{4,5},{5,4},{6,7},{7,6},{8,9},{9,8},{10,11... | collective-permute-start | bytes 1572872 | tf_op jit(solution)/shard_map/ppermute | solution.py:20
  48.4 7.2 %collective-permute-start.21 = (bf16[512,512]{1,0:T(8,128)(2,1)S(1)}, bf16[512,512]{1,0:T(8,128)(2,1)S(1)}, u32[]{:S(2)}, u32[]{:S(2)}) collective-permute-start(bf16[512,512]{1,0:T(8,128)(2,1)S(1)} %collective-permute-done.16.refs_1_.refs_2_), channel_id=1, source_target_pairs={{0,1},{1,0},{2,3},{3,2},{4,5},{5,4},{6,7},{7,6},{8,9},{9,8},{10,11... | collective-permute-start | bytes 1572872 | tf_op jit(solution)/shard_map/ppermute | solution.py:20
  49.0 4.3 %collective-permute-start.17 = (bf16[256,128]{1,0:T(8,128)(2,1)S(1)}, bf16[256,128]{1,0:T(8,128)(2,1)S(1)}, u32[]{:S(2)}, u32[]{:S(2)}) collective-permute-start(bf16[256,128]{1,0:T(8,128)(2,1)S(1)} %collective-permute-done.15), channel_id=1, source_target_pairs={{0,4},{4,0},{8,12},{12,8},{1,5},{5,1},{9,13},{13,9},{2,6},{6,2},{1... | collective-permute-start | bytes 196616 | tf_op jit(solution)/shard_map/ppermute | solution.py:20
  53.2 2.4 %collective-permute-start.22 = (bf16[256,512]{1,0:T(8,128)(2,1)S(1)}, bf16[256,512]{1,0:T(8,128)(2,1)S(1)}, u32[]{:S(2)}, u32[]{:S(2)}) collective-permute-start(bf16[256,512]{1,0:T(8,128)(2,1)S(1)} %collective-permute-done.13.refs_2_.refs_3_), channel_id=1, source_target_pairs={{0,1},{1,0},{2,3},{3,2},{4,5},{5,4},{6,7},{7,6},{8,9},{9,8},{10,11... | collective-permute-start | bytes 786440 | tf_op jit(solution)/shard_map/ppermute | solution.py:20
  53.3 2.3 %collective-permute-start.20 = (bf16[1024,128]{1,0:T(8,128)(2,1)S(1)}, bf16[1024,128]{1,0:T(8,128)(2,1)S(1)}, u32[]{:S(2)}, u32[]{:S(2)}) collective-permute-start(bf16[1024,128]{1,0:T(8,128)(2,1)S(1)} %pad_maximum_fusion.refs_4_), channel_id=1, source_target_pairs={{0,1},{1,0},{2,3},{3,2},{4,5},{5,4},{6,7},{7,6},{8,9},{9,8},{10,11... | collective-permute-start | bytes 786440 | tf_op jit(solution)/shard_map/ppermute | solution.py:20
  53.9 6.9 %collective-permute-start.23 = (bf16[768,128]{1,0:T(8,128)(2,1)S(1)}, bf16[768,128]{1,0:T(8,128)(2,1)S(1)}, u32[]{:S(2)}, u32[]{:S(2)}) collective-permute-start(bf16[768,128]{1,0:T(8,128)(2,1)S(1)} %constant_dynamic-update-slice_fusion.2), channel_id=1, source_target_pairs={{0,2},{1,3},{2,0},{3,1},{4,6},{5,7},{6,4},{7,5},{8,10},{9,11},{10,... | collective-permute-start | bytes 589832 | tf_op jit(solution)/shard_map/ppermute | solution.py:20
  60.8 1.6 %collective-permute-start.24 = (bf16[1024,128]{1,0:T(8,128)(2,1)S(1)}, bf16[1024,128]{1,0:T(8,128)(2,1)S(1)}, u32[]{:S(2)}, u32[]{:S(2)}) collective-permute-start(bf16[1024,128]{1,0:T(8,128)(2,1)S(1)} %constant_dynamic-update-slice_fusion.5.refs_4_), channel_id=1, source_target_pairs={{0,1},{1,0},{2,3},{3,2},{4,5},{5,4},{6,7},{7,6},{8,9},{9,8},{10,11... | collective-permute-start | bytes 786440 | tf_op jit(solution)/shard_map/ppermute | solution.py:20

commit v15 on v13

--- a/solution.py
+++ b/solution.py
@@ -409,9 +409,7 @@
         late[1] = swap(after(late[0], parts[0]), "centers", nc, 1)
         cot = cotangent([parts[0], *received], saved, target, delta)
 
-        far = {dz: swap(cot, "points", nz, dz) for dz in range(2, nz, 2)}
-        far[1] = swap(cot, "points", nz, 1)
-        far.update({dz: swap(far[dz - 1], "points", nz, 1) for dz in range(3, nz, 2)})
+        far = {dz: swap(cot, "points", nz, dz) for dz in (*range(2, nz), 1)}
         ahead = {d: swap(after(cot, late[d]), "centers", nc, d) for d in range(2, nc, 2)}
         far[1] = after(far[1], *ahead.values())
         far = jnp.concatenate([far[dz] for dz in range(1, nz)])

time: 65.2 us -> 65.4 us (level)
  waiting for transfers between devices: 14.8 us -> 17.9 us
  starting transfers between devices: 26.6 us -> 23.6 us
    ppermute x25, waiting for transfers between devices: 14.8 us -> 17.9 us  [swap(): return lax.ppermute(a, axis, [(i, i ^ d) for i in range(size)])]
    ppermute x25, starting transfers between devices: 26.6 us -> 23.6 us  [swap(): return lax.ppermute(a, axis, [(i, i ^ d) for i in range(size)])]
where the time goes in v15:
time: 65.4 us; the launch traced here: 65.1 us
  starting transfers between devices  23.6 us (36%)
  waiting for transfers between devices  17.9 us (27%)
  Pallas kernels  16.2 us (25%)
  local copies, waits for them, and re-layouts  6.45 us (10%)
  between operations  0.85 us (1%)
    ppermute x25, starting transfers between devices, swap(): return lax.ppermute(a, axis, [(i, i ^ d) for i in range(size)])  23.6 us
    ppermute x25, waiting for transfers between devices, swap(): return lax.ppermute(a, axis, [(i, i ^ d) for i in range(size)])  17.9 us
    pallas_call x2, Pallas kernels, backward(): pl.pallas_call(body, out_shape=tuple((jax.ShapeDtypeStruct((n, width), F3...  6.99 us
    unnamed x18, local copies, waits for them, and re-layouts  4.74 us
    pallas_call x3, Pallas kernels, forward(): pl.pallas_call(body, out_shape=tuple((jax.ShapeDtypeStruct((count, out_wi...  3.93 us
    pallas_call x1, Pallas kernels, finish(): pl.pallas_call(body, out_shape=tuple((jax.ShapeDtypeStruct((n, width), F3...  2.31 us
    pallas_call x1, Pallas kernels, own_rows(): pl.pallas_call(body, out_shape=(jax.ShapeDtypeStruct((rows.shape[0], out_...  2.28 us
  transfers between devices with their start and end apart: 25, of which 8 were waited for; matrix products, arithmetic and copies ran while one was open for 3% of the time, Pallas kernels for 21%

profile of v15, /device:TPU:0, one launch (start us, length us, event | category | flops | bytes accessed | tf_op | source)
XLA Modules:
  0.0 65.1 jit_solution(8145050627618583514)
XLA Ops:
  0.6 3.0 %collective-permute-start.4 = (bf16[512,512]{1,0:T(8,128)(2,1)}, bf16[512,512]{1,0:T(8,128)(2,1)S(1)}, u32[]{:S(2)}, u32[]{:S(2)}) collective-permute-start(bf16[512,512]{1,0:T(8,128)(2,1)} %pos_ref), channel_id=1, source_target_pairs={{0,2},{1,3},{2,0},{3,1},{4,6},{5,7},{6,4},{7,5},{8,10},{9,11},{10,... | collective-permute-start | bytes 1572872 | tf_op jit(solution)/shard_map/ppermute | solution.py:20
  3.6 1.0 %constant_dynamic-slice_fusion.refs_0_.refs_13_.refs_1_ = bf16[256,512]{1,0:T(8,128)(2,1)S(1)} fusion(bf16[1024,512]{1,0:T(8,128)(2,1)} %refs_4_.1, s32[]{:T(128)S(6)} %select_n.3), kind=kLoop, calls=%fused_computation.8 | loop fusion | bytes 524292 | tf_op jit(solution)/shard_map/dynamic_slice | solution.py:354
  4.6 1.6 %collective-permute-start.6 = (bf16[256,512]{1,0:T(8,128)(2,1)S(1)}, bf16[256,512]{1,0:T(8,128)(2,1)S(1)}, u32[]{:S(2)}, u32[]{:S(2)}) collective-permute-start(bf16[256,512]{1,0:T(8,128)(2,1)S(1)} %constant_dynamic-slice_fusion.refs_0_.refs_13_.refs_1_), channel_id=1, source_target_pairs={{0,4},{4,0},{8,12},{12,8},{1,5},{5,1},{9,13},{13,9},{2,6},{6,2},{1... | collective-permute-start | bytes 786440 | tf_op jit(solution)/shard_map/ppermute | solution.py:20
  6.3 2.6 %collective-permute-start = (bf16[256,512]{1,0:T(8,128)(2,1)S(1)}, bf16[256,512]{1,0:T(8,128)(2,1)S(1)}, u32[]{:S(2)}, u32[]{:S(2)}) collective-permute-start(bf16[256,512]{1,0:T(8,128)(2,1)S(1)} %constant_dynamic-slice_fusion.refs_0_.refs_13_.refs_1_), channel_id=1, source_target_pairs={{0,8},{4,12},{8,0},{12,4},{1,9},{5,13},{9,1},{13,5},{2,10},{6,14},... | collective-permute-start | bytes 786440 | tf_op jit(solution)/shard_map/ppermute | solution.py:20
  8.8 0.7 %reshape.10.spread_ref = bf16[1,512]{1,0:T(2,128)(2,1)S(1)} reshape(bf16[512]{0:T(512)(128)(2,1)} %param.13) | data formatting | bytes 2048 | tf_op jit(solution)/shard_map/reshape | solution.py:90
  9.5 1.0 %copy-done.1 = bf16[512,512]{1,0:T(8,128)(2,1)S(1)} copy-done((bf16[512,512]{1,0:T(8,128)(2,1)S(1)}, bf16[512,512]{1,0:T(8,128)(2,1)}, u32[]{:S(2)}) %copy-start.1) | copy-done | bytes 524312
  10.6 0.9 %copy-done.5 = bf16[512,128]{1,0:T(8,128)(2,1)S(1)} copy-done((bf16[512,128]{1,0:T(8,128)(2,1)S(1)}, bf16[512,128]{1,0:T(8,128)(2,1)}, u32[]{:S(2)}) %copy-start.5) | copy-done | bytes 131096
  11.5 0.7 %copy-done.6 = f32[128]{0:T(128)S(1)} copy-done((f32[128]{0:T(128)S(1)}, f32[128]{0:T(128)}, u32[]{:S(2)}) %copy-start.6) | copy-done | bytes 536
  13.0 1.0 %copy-done.3 = f32[1024,128]{1,0:T(8,128)S(1)} copy-done((f32[1024,128]{1,0:T(8,128)S(1)}, f32[1024,128]{1,0:T(8,128)}, u32[]{:S(2)}) %copy-start.3) | copy-done | bytes 524312
  14.0 1.0 %copy-done.4 = f32[1024,128]{1,0:T(8,128)S(1)} copy-done((f32[1024,128]{1,0:T(8,128)S(1)}, f32[1024,128]{1,0:T(8,128)}, u32[]{:S(2)}) %copy-start.4) | copy-done | bytes 524312
  15.5 3.5 %collective-permute-done.5.refs_6_ = bf16[144,512]{1,0:T(8,128)(2,1)S(1)} collective-permute-done((bf16[144,512]{1,0:T(8,128)(2,1)S(1)}, bf16[144,512]{1,0:T(8,128)(2,1)S(1)}, u32[]{:S(2)}, u32[]{:S(2)}) %collective-permute-start.5) | collective-permute-done | bytes 147488 | tf_op jit(solution)/shard_map/ppermute | solution.py:20
  19.0 1.3 %collective-permute-done.refs_0_ = bf16[256,512]{1,0:T(8,128)(2,1)S(1)} collective-permute-done((bf16[256,512]{1,0:T(8,128)(2,1)S(1)}, bf16[256,512]{1,0:T(8,128)(2,1)S(1)}, u32[]{:S(2)}, u32[]{:S(2)}) %collective-permute-start) | collective-permute-done | bytes 262176 | tf_op jit(solution)/shard_map/ppermute | solution.py:20
  20.9 0.6 collective-permute-start.20
  21.5 1.6 %collective-permute-start.1 = (bf16[256,512]{1,0:T(8,128)(2,1)S(1)}, bf16[256,512]{1,0:T(8,128)(2,1)S(1)}, u32[]{:S(2)}, u32[]{:S(2)}) collective-permute-start(bf16[256,512]{1,0:T(8,128)(2,1)S(1)} %collective-permute-done.refs_0_), channel_id=1, source_target_pairs={{0,4},{4,0},{8,12},{12,8},{1,5},{5,1},{9,13},{13,9},{2,6},{6,2},{1... | collective-permute-start | bytes 786440 | tf_op jit(solution)/shard_map/ppermute | solution.py:20
  23.1 1.3 %forward.3 = f32[256,128]{1,0:T(8,128)S(1)} custom-call(bf16[256,512]{1,0:T(8,128)(2,1)S(1)} %collective-permute-done.refs_0_, bf16[512,512]{1,0:T(8,128)(2,1)S(1)} %get-tuple-element.39.refs_1_.refs_11_.pos_ref, bf16[144,512]{1,0:T(8,128)(2,1)S(1)} %get-tuple-element.42.refs_2_, bf16[512,512]{1,0:T(8,128)(2,1)S(1)} %collective-permute-done.2.refs_3_, ...), custom_call_target="tpu_custom_call" | custom-call | flops 1 | bytes 1 | tf_op jit(solution)/shard_map/forward/pallas_call | solution.py:167
  24.4 2.7 %collective-permute-start.9 = (f32[256,128]{1,0:T(8,128)S(1)}, f32[256,128]{1,0:T(8,128)S(1)}, u32[]{:S(2)}, u32[]{:S(2)}) collective-permute-start(f32[256,128]{1,0:T(8,128)S(1)} %forward.3), channel_id=1, source_target_pairs={{0,8},{4,12},{8,0},{12,4},{1,9},{5,13},{9,1},{13,5},{2,10},{6,14},... | collective-permute-start | bytes 393224 | tf_op jit(solution)/shard_map/ppermute | solution.py:20
  27.0 1.3 %forward.4 = f32[256,128]{1,0:T(8,128)S(1)} custom-call(bf16[256,512]{1,0:T(8,128)(2,1)S(1)} %collective-permute-done.6.refs_0_, bf16[512,512]{1,0:T(8,128)(2,1)S(1)} %get-tuple-element.39.refs_1_.refs_11_.pos_ref, bf16[144,512]{1,0:T(8,128)(2,1)S(1)} %get-tuple-element.42.refs_2_, bf16[512,512]{1,0:T(8,128)(2,1)S(1)} %collective-permute-done.2.refs_3_, ...), custom_call_target="tpu_custom_call" | custom-call | flops 17179869184 | bytes 1048576 | tf_op jit(solution)/shard_map/forward/pallas_call | solution.py:167
  28.4 0.6 collective-permute-start.10
  29.0 4.4 %collective-permute-done.1.refs_0_.refs_15_.refs_3_ = bf16[256,512]{1,0:T(8,128)(2,1)S(1)} collective-permute-done((bf16[256,512]{1,0:T(8,128)(2,1)S(1)}, bf16[256,512]{1,0:T(8,128)(2,1)S(1)}, u32[]{:S(2)}, u32[]{:S(2)}) %collective-permute-start.1) | collective-permute-done | bytes 262176 | tf_op jit(solution)/shard_map/ppermute | solution.py:20
  33.4 1.3 %forward.5 = f32[256,128]{1,0:T(8,128)S(1)} custom-call(bf16[256,512]{1,0:T(8,128)(2,1)S(1)} %collective-permute-done.1.refs_0_.refs_15_.refs_3_, bf16[512,512]{1,0:T(8,128)(2,1)S(1)} %get-tuple-element.39.refs_1_.refs_11_.pos_ref, bf16[144,512]{1,0:T(8,128)(2,1)S(1)} %get-tuple-element.42.refs_2_, bf16[512,512]{1,0:T(8,128)(2,1)S(1)} %collective-permute-done.2.refs_3_, ...), custom_call_target="tpu_custom_call" | custom-call | flops 17179869184 | bytes 1048576 | tf_op jit(solution)/shard_map/forward/pallas_call | solution.py:167
  34.7 3.7 %collective-permute-start.11 = (f32[256,128]{1,0:T(8,128)S(1)}, f32[256,128]{1,0:T(8,128)S(1)}, u32[]{:S(2)}, u32[]{:S(2)}) collective-permute-start(f32[256,128]{1,0:T(8,128)S(1)} %forward.5), channel_id=1, source_target_pairs={{0,12},{4,8},{8,4},{12,0},{1,13},{5,9},{9,5},{13,1},{2,14},{6,10},... | collective-permute-start | bytes 393224 | tf_op jit(solution)/shard_map/ppermute | solution.py:20
  38.4 2.3 %own_rows.1 = (f32[256,128]{1,0:T(8,128)S(1)}, bf16[512,1024]{1,0:T(8,128)(2,1)S(1)}) custom-call(bf16[256,512]{1,0:T(8,128)(2,1)S(1)} %constant_dynamic-slice_fusion.refs_0_.refs_13_.refs_1_, bf16[512,512]{1,0:T(8,128)(2,1)S(1)} %get-tuple-element.39.refs_1_.refs_11_.pos_ref, bf16[144,512]{1,0:T(8,128)(2,1)S(1)} %get-tuple-element.42.refs_2_, ...), custom_call_target="tpu_custom_call" | custom-call | flops 17179869184 | bytes 1048576 | tf_op jit(solution)/shard_map/own_rows/pallas_call | solution.py:214
  40.7 1.0 %collective-permute-done.11.refs_1_ = f32[256,128]{1,0:T(8,128)S(1)} collective-permute-done((f32[256,128]{1,0:T(8,128)S(1)}, f32[256,128]{1,0:T(8,128)S(1)}, u32[]{:S(2)}, u32[]{:S(2)}) %collective-permute-start.11) | collective-permute-done | bytes 131104 | tf_op jit(solution)/shard_map/ppermute | solution.py:20
  41.8 0.9 %collective-permute-start.12 = (bf16[256,128]{1,0:T(8,128)(2,1)S(1)}, bf16[256,128]{1,0:T(8,128)(2,1)S(1)}, u32[]{:S(2)}, u32[]{:S(2)}) collective-permute-start(bf16[256,128]{1,0:T(8,128)(2,1)S(1)} %cotangent.1), channel_id=1, source_target_pairs={{0,4},{4,0},{8,12},{12,8},{1,5},{5,1},{9,13},{13,9},{2,6},{6,2},{1... | collective-permute-start | bytes 196616 | tf_op jit(solution)/shard_map/ppermute | solution.py:20
  42.7 2.5 %collective-permute-done.13.refs_11_.refs_3_ = bf16[256,512]{1,0:T(8,128)(2,1)S(1)} collective-permute-done((bf16[256,512]{1,0:T(8,128)(2,1)S(1)}, bf16[256,512]{1,0:T(8,128)(2,1)S(1)}, u32[]{:S(2)}, u32[]{:S(2)}) %collective-permute-start.13) | collective-permute-done | bytes 262176 | tf_op jit(solution)/shard_map/ppermute | solution.py:20
  45.2 2.0 %collective-permute-start.16 = (bf16[256,128]{1,0:T(8,128)(2,1)S(1)}, bf16[256,128]{1,0:T(8,128)(2,1)S(1)}, u32[]{:S(2)}, u32[]{:S(2)}) collective-permute-start(bf16[256,128]{1,0:T(8,128)(2,1)S(1)} %cotangent.1), channel_id=1, source_target_pairs={{0,12},{4,8},{8,4},{12,0},{1,13},{5,9},{9,5},{13,1},{2,14},{6,10},... | collective-permute-start | bytes 196616 | tf_op jit(solution)/shard_map/ppermute | solution.py:20
  47.7 1.8 %collective-permute-done.14 = bf16[256,128]{1,0:T(8,128)(2,1)S(1)} collective-permute-done((bf16[256,128]{1,0:T(8,128)(2,1)S(1)}, bf16[256,128]{1,0:T(8,128)(2,1)S(1)}, u32[]{:S(2)}, u32[]{:S(2)}) %collective-permute-start.14) | collective-permute-done | bytes 65568 | tf_op jit(solution)/shard_map/ppermute | solution.py:20
  49.5 3.2 %collective-permute-done.15 = bf16[256,128]{1,0:T(8,128)(2,1)S(1)} collective-permute-done((bf16[256,128]{1,0:T(8,128)(2,1)S(1)}, bf16[256,128]{1,0:T(8,128)(2,1)S(1)}, u32[]{:S(2)}, u32[]{:S(2)}) %collective-permute-start.15) | collective-permute-done | bytes 65568 | tf_op jit(solution)/shard_map/ppermute | solution.py:20
  53.4 2.0 %collective-permute-start.23 = (bf16[768,128]{1,0:T(8,128)(2,1)S(1)}, bf16[768,128]{1,0:T(8,128)(2,1)S(1)}, u32[]{:S(2)}, u32[]{:S(2)}) collective-permute-start(bf16[768,128]{1,0:T(8,128)(2,1)S(1)} %constant_dynamic-update-slice_fusion.2), channel_id=1, source_target_pairs={{0,2},{1,3},{2,0},{3,1},{4,6},{5,7},{6,4},{7,5},{8,10},{9,11},{10,... | collective-permute-start | bytes 589832 | tf_op jit(solution)/shard_map/ppermute | solution.py:20
  55.4 5.7 %backward.2 = (f32[512,512]{1,0:T(8,128)S(1)}, f32[512,128]{1,0:T(8,128)S(1)}, f32[512,128]{1,0:T(8,128)S(1)}, bf16[512,1024]{1,0:T(8,128)(2,1)S(1)}, bf16[512,1024]{1,0:T(8,128)(2,1)S(1)}) custom-call(bf16[512,512]{1,0:T(8,128)(2,1)S(1)} %get-tuple-element.39.refs_1_.refs_11_.pos_ref, bf16[512,128]{1,0:T(8,128)(2,1)S(1)} %get-tuple-element.40.coef_ref, ...), custom_call_target="tpu_custom_call" | custom-call | flops 17179869184 | bytes 1048576 | tf_op jit(solution)/shard_map/backward/pallas_call | solution.py:288
  61.2 1.3 %backward.3 = (f32[512,512]{1,0:T(8,128)S(1)}, f32[512,128]{1,0:T(8,128)S(1)}, f32[512,128]{1,0:T(8,128)S(1)}) custom-call(bf16[512,512]{1,0:T(8,128)(2,1)S(1)} %get-tuple-element.39.refs_1_.refs_11_.pos_ref, bf16[512,128]{1,0:T(8,128)(2,1)S(1)} %get-tuple-element.40.coef_ref, bf16[1,512]{1,0:T(2,128)(2,1)S(1)} %get-tuple-element.41.refs_12_.spread_ref, ...), custom_call_target="tpu_custom_call" | custom-call | flops 1 | bytes 1 | tf_op jit(solution)/shard_map/backward/pallas_call | solution.py:288
  62.8 2.3 %finish.1 = (f32[512,512]{1,0:T(8,128)}, f32[512,128]{1,0:T(8,128)}) custom-call(bf16[512,512]{1,0:T(8,128)(2,1)S(1)} %get-tuple-element.39.refs_1_.refs_11_.pos_ref, bf16[512,128]{1,0:T(8,128)(2,1)S(1)} %get-tuple-element.40.coef_ref, bf16[1,512]{1,0:T(2,128)(2,1)S(1)} %get-tuple-element.41.refs_12_.spread_ref, ...), custom_call_target="tpu_custom_call" | custom-call | flops 1 | bytes 1 | tf_op jit(solution)/shard_map/finish/pallas_call | solution.py:330
  (52 shorter events, 3.4 us)
Async XLA Ops:
  0.6 12.3 %copy-start = (bf16[1024,512]{1,0:T(8,128)(2,1)S(1)}, bf16[1024,512]{1,0:T(8,128)(2,1)}, u32[]{:S(2)}) copy-start(bf16[1024,512]{1,0:T(8,128)(2,1)} %refs_4_.1) | copy-start | bytes 3145732
  0.6 19.7 %collective-permute-start.4 = (bf16[512,512]{1,0:T(8,128)(2,1)}, bf16[512,512]{1,0:T(8,128)(2,1)S(1)}, u32[]{:S(2)}, u32[]{:S(2)}) collective-permute-start(bf16[512,512]{1,0:T(8,128)(2,1)} %pos_ref), channel_id=1, source_target_pairs={{0,2},{1,3},{2,0},{3,1},{4,6},{5,7},{6,4},{7,5},{8,10},{9,11},{10,... | collective-permute-start | bytes 1572872 | tf_op jit(solution)/shard_map/ppermute | solution.py:20
  4.6 14.3 %collective-permute-start.6 = (bf16[256,512]{1,0:T(8,128)(2,1)S(1)}, bf16[256,512]{1,0:T(8,128)(2,1)S(1)}, u32[]{:S(2)}, u32[]{:S(2)}) collective-permute-start(bf16[256,512]{1,0:T(8,128)(2,1)S(1)} %constant_dynamic-slice_fusion.refs_0_.refs_13_.refs_1_), channel_id=1, source_target_pairs={{0,4},{4,0},{8,12},{12,8},{1,5},{5,1},{9,13},{13,9},{2,6},{6,2},{1... | collective-permute-start | bytes 786440 | tf_op jit(solution)/shard_map/ppermute | solution.py:20
  6.3 14.0 %collective-permute-start = (bf16[256,512]{1,0:T(8,128)(2,1)S(1)}, bf16[256,512]{1,0:T(8,128)(2,1)S(1)}, u32[]{:S(2)}, u32[]{:S(2)}) collective-permute-start(bf16[256,512]{1,0:T(8,128)(2,1)S(1)} %constant_dynamic-slice_fusion.refs_0_.refs_13_.refs_1_), channel_id=1, source_target_pairs={{0,8},{4,12},{8,0},{12,4},{1,9},{5,13},{9,1},{13,5},{2,10},{6,14},... | collective-permute-start | bytes 786440 | tf_op jit(solution)/shard_map/ppermute | solution.py:20
  9.5 1.0 %copy-start.1 = (bf16[512,512]{1,0:T(8,128)(2,1)S(1)}, bf16[512,512]{1,0:T(8,128)(2,1)}, u32[]{:S(2)}) copy-start(bf16[512,512]{1,0:T(8,128)(2,1)} %pos_ref) | copy-start | bytes 1572868
  10.6 0.9 %copy-start.5 = (bf16[512,128]{1,0:T(8,128)(2,1)S(1)}, bf16[512,128]{1,0:T(8,128)(2,1)}, u32[]{:S(2)}) copy-start(bf16[512,128]{1,0:T(8,128)(2,1)} %coef_ref.1) | copy-start | bytes 393220
  11.5 0.7 %copy-start.6 = (f32[128]{0:T(128)S(1)}, f32[128]{0:T(128)}, u32[]{:S(2)}) copy-start(f32[128]{0:T(128)} %param.10) | copy-start | bytes 1540
  12.3 6.6 %copy-start.2 = (bf16[512,512]{1,0:T(8,128)(2,1)S(1)}, bf16[512,512]{1,0:T(8,128)(2,1)}, u32[]{:S(2)}) copy-start(bf16[512,512]{1,0:T(8,128)(2,1)} %pos_ref) | copy-start | bytes 1572868
  12.4 6.6 %collective-permute-start.5 = (bf16[144,512]{1,0:T(8,128)(2,1)S(1)}, bf16[144,512]{1,0:T(8,128)(2,1)S(1)}, u32[]{:S(2)}, u32[]{:S(2)}) collective-permute-start(bf16[144,512]{1,0:T(8,128)(2,1)S(1)} %get-tuple-element.42.refs_2_), channel_id=1, source_target_pairs={{0,2},{1,3},{2,0},{3,1},{4,6},{5,7},{6,4},{7,5},{8,10},{9,11},{10,... | collective-permute-start | bytes 442376 | tf_op jit(solution)/shard_map/ppermute | solution.py:20
  13.0 6.0 %collective-permute-start.3 = (bf16[144,512]{1,0:T(8,128)(2,1)S(1)}, bf16[144,512]{1,0:T(8,128)(2,1)S(1)}, u32[]{:S(2)}, u32[]{:S(2)}) collective-permute-start(bf16[144,512]{1,0:T(8,128)(2,1)S(1)} %get-tuple-element.42.refs_2_), channel_id=1, source_target_pairs={{0,1},{1,0},{2,3},{3,2},{4,5},{5,4},{6,7},{7,6},{8,9},{9,8},{10,11... | collective-permute-start | bytes 442376 | tf_op jit(solution)/shard_map/ppermute | solution.py:20
  13.0 1.0 %copy-start.3 = (f32[1024,128]{1,0:T(8,128)S(1)}, f32[1024,128]{1,0:T(8,128)}, u32[]{:S(2)}) copy-start(f32[1024,128]{1,0:T(8,128)} %refs_0_.1) | copy-start | bytes 1572868
  14.0 1.0 %copy-start.4 = (f32[1024,128]{1,0:T(8,128)S(1)}, f32[1024,128]{1,0:T(8,128)}, u32[]{:S(2)}) copy-start(f32[1024,128]{1,0:T(8,128)} %refs_1_.1) | copy-start | bytes 1572868
  18.9 4.1 %collective-permute-start.2 = (bf16[512,512]{1,0:T(8,128)(2,1)S(1)}, bf16[512,512]{1,0:T(8,128)(2,1)S(1)}, u32[]{:S(2)}, u32[]{:S(2)}) collective-permute-start(bf16[512,512]{1,0:T(8,128)(2,1)S(1)} %copy-done.2), channel_id=1, source_target_pairs={{0,1},{1,0},{2,3},{3,2},{4,5},{5,4},{6,7},{7,6},{8,9},{9,8},{10,11... | collective-permute-start | bytes 1572872 | tf_op jit(solution)/shard_map/ppermute | solution.py:20
  20.3 2.8 %collective-permute-start.7 = (bf16[512,512]{1,0:T(8,128)(2,1)S(1)}, bf16[512,512]{1,0:T(8,128)(2,1)S(1)}, u32[]{:S(2)}, u32[]{:S(2)}) collective-permute-start(bf16[512,512]{1,0:T(8,128)(2,1)S(1)} %collective-permute-done.4.refs_5_), channel_id=1, source_target_pairs={{0,1},{1,0},{2,3},{3,2},{4,5},{5,4},{6,7},{7,6},{8,9},{9,8},{10,11... | collective-permute-start | bytes 1572872 | tf_op jit(solution)/shard_map/ppermute | solution.py:20
  20.3 2.7 %collective-permute-start.8 = (bf16[144,512]{1,0:T(8,128)(2,1)S(1)}, bf16[144,512]{1,0:T(8,128)(2,1)S(1)}, u32[]{:S(2)}, u32[]{:S(2)}) collective-permute-start(bf16[144,512]{1,0:T(8,128)(2,1)S(1)} %collective-permute-done.5.refs_6_), channel_id=1, source_target_pairs={{0,1},{1,0},{2,3},{3,2},{4,5},{5,4},{6,7},{7,6},{8,9},{9,8},{10,11... | collective-permute-start | bytes 442376 | tf_op jit(solution)/shard_map/ppermute | solution.py:20
  20.9 26.3 %collective-permute-start.20 = (bf16[512,512]{1,0:T(8,128)(2,1)S(1)}, bf16[512,512]{1,0:T(8,128)(2,1)S(1)}, u32[]{:S(2)}, u32[]{:S(2)}) collective-permute-start(bf16[512,512]{1,0:T(8,128)(2,1)S(1)} %constant_dynamic-update-slice_fusion.refs_14_.refs_2_), channel_id=1, source_target_pairs={{0,2},{1,3},{2,0},{3,1},{4,6},{5,7},{6,4},{7,5},{8,10},{9,11},{10,... | collective-permute-start | bytes 1572872 | tf_op jit(solution)/shard_map/ppermute | solution.py:20
  21.5 12.0 %collective-permute-start.1 = (bf16[256,512]{1,0:T(8,128)(2,1)S(1)}, bf16[256,512]{1,0:T(8,128)(2,1)S(1)}, u32[]{:S(2)}, u32[]{:S(2)}) collective-permute-start(bf16[256,512]{1,0:T(8,128)(2,1)S(1)} %collective-permute-done.refs_0_), channel_id=1, source_target_pairs={{0,4},{4,0},{8,12},{12,8},{1,5},{5,1},{9,13},{13,9},{2,6},{6,2},{1... | collective-permute-start | bytes 786440 | tf_op jit(solution)/shard_map/ppermute | solution.py:20
  24.4 14.0 %collective-permute-start.9 = (f32[256,128]{1,0:T(8,128)S(1)}, f32[256,128]{1,0:T(8,128)S(1)}, u32[]{:S(2)}, u32[]{:S(2)}) collective-permute-start(f32[256,128]{1,0:T(8,128)S(1)} %forward.3), channel_id=1, source_target_pairs={{0,8},{4,12},{8,0},{12,4},{1,9},{5,13},{9,1},{13,5},{2,10},{6,14},... | collective-permute-start | bytes 393224 | tf_op jit(solution)/shard_map/ppermute | solution.py:20
  28.4 10.1 %collective-permute-start.10 = (f32[256,128]{1,0:T(8,128)S(1)}, f32[256,128]{1,0:T(8,128)S(1)}, u32[]{:S(2)}, u32[]{:S(2)}) collective-permute-start(f32[256,128]{1,0:T(8,128)S(1)} %forward.4), channel_id=1, source_target_pairs={{0,4},{4,0},{8,12},{12,8},{1,5},{5,1},{9,13},{13,9},{2,6},{6,2},{1... | collective-permute-start | bytes 393224 | tf_op jit(solution)/shard_map/ppermute | solution.py:20
  34.7 6.9 %collective-permute-start.11 = (f32[256,128]{1,0:T(8,128)S(1)}, f32[256,128]{1,0:T(8,128)S(1)}, u32[]{:S(2)}, u32[]{:S(2)}) collective-permute-start(f32[256,128]{1,0:T(8,128)S(1)} %forward.5), channel_id=1, source_target_pairs={{0,12},{4,8},{8,4},{12,0},{1,13},{5,9},{9,5},{13,1},{2,14},{6,10},... | collective-permute-start | bytes 393224 | tf_op jit(solution)/shard_map/ppermute | solution.py:20
  38.4 6.8 %collective-permute-start.13 = (bf16[256,512]{1,0:T(8,128)(2,1)S(1)}, bf16[256,512]{1,0:T(8,128)(2,1)S(1)}, u32[]{:S(2)}, u32[]{:S(2)}) collective-permute-start(bf16[256,512]{1,0:T(8,128)(2,1)S(1)} %collective-permute-done.1.refs_0_.refs_15_.refs_3_), channel_id=1, source_target_pairs={{0,2},{1,3},{2,0},{3,1},{4,6},{5,7},{6,4},{7,5},{8,10},{9,11},{10,... | collective-permute-start | bytes 786440 | tf_op jit(solution)/shard_map/ppermute | solution.py:20
  41.8 5.4 %collective-permute-start.12 = (bf16[256,128]{1,0:T(8,128)(2,1)S(1)}, bf16[256,128]{1,0:T(8,128)(2,1)S(1)}, u32[]{:S(2)}, u32[]{:S(2)}) collective-permute-start(bf16[256,128]{1,0:T(8,128)(2,1)S(1)} %cotangent.1), channel_id=1, source_target_pairs={{0,4},{4,0},{8,12},{12,8},{1,5},{5,1},{9,13},{13,9},{2,6},{6,2},{1... | collective-permute-start | bytes 196616 | tf_op jit(solution)/shard_map/ppermute | solution.py:20
  45.2 4.3 %collective-permute-start.14 = (bf16[256,128]{1,0:T(8,128)(2,1)S(1)}, bf16[256,128]{1,0:T(8,128)(2,1)S(1)}, u32[]{:S(2)}, u32[]{:S(2)}) collective-permute-start(bf16[256,128]{1,0:T(8,128)(2,1)S(1)} %cotangent.1), channel_id=1, source_target_pairs={{0,2},{1,3},{2,0},{3,1},{4,6},{5,7},{6,4},{7,5},{8,10},{9,11},{10,... | collective-permute-start | bytes 196616 | tf_op jit(solution)/shard_map/ppermute | solution.py:20
  45.2 7.5 %collective-permute-start.16 = (bf16[256,128]{1,0:T(8,128)(2,1)S(1)}, bf16[256,128]{1,0:T(8,128)(2,1)S(1)}, u32[]{:S(2)}, u32[]{:S(2)}) collective-permute-start(bf16[256,128]{1,0:T(8,128)(2,1)S(1)} %cotangent.1), channel_id=1, source_target_pairs={{0,12},{4,8},{8,4},{12,0},{1,13},{5,9},{9,5},{13,1},{2,14},{6,10},... | collective-permute-start | bytes 196616 | tf_op jit(solution)/shard_map/ppermute | solution.py:20
  47.2 5.5 %collective-permute-start.15 = (bf16[256,128]{1,0:T(8,128)(2,1)S(1)}, bf16[256,128]{1,0:T(8,128)(2,1)S(1)}, u32[]{:S(2)}, u32[]{:S(2)}) collective-permute-start(bf16[256,128]{1,0:T(8,128)(2,1)S(1)} %cotangent.1), channel_id=1, source_target_pairs={{0,8},{4,12},{8,0},{12,4},{1,9},{5,13},{9,1},{13,5},{2,10},{6,14},... | collective-permute-start | bytes 196616 | tf_op jit(solution)/shard_map/ppermute | solution.py:20
  47.2 6.2 %collective-permute-start.18 = (bf16[256,512]{1,0:T(8,128)(2,1)S(1)}, bf16[256,512]{1,0:T(8,128)(2,1)S(1)}, u32[]{:S(2)}, u32[]{:S(2)}) collective-permute-start(bf16[256,512]{1,0:T(8,128)(2,1)S(1)} %collective-permute-done.1.refs_0_.refs_15_.refs_3_), channel_id=1, source_target_pairs={{0,1},{1,0},{2,3},{3,2},{4,5},{5,4},{6,7},{7,6},{8,9},{9,8},{10,11... | collective-permute-start | bytes 786440 | tf_op jit(solution)/shard_map/ppermute | solution.py:20
  47.2 8.2 %collective-permute-start.17 = (bf16[512,512]{1,0:T(8,128)(2,1)S(1)}, bf16[512,512]{1,0:T(8,128)(2,1)S(1)}, u32[]{:S(2)}, u32[]{:S(2)}) collective-permute-start(bf16[512,512]{1,0:T(8,128)(2,1)S(1)} %constant_dynamic-update-slice_fusion.refs_14_.refs_2_), channel_id=1, source_target_pairs={{0,1},{1,0},{2,3},{3,2},{4,5},{5,4},{6,7},{7,6},{8,9},{9,8},{10,11... | collective-permute-start | bytes 1572872 | tf_op jit(solution)/shard_map/ppermute | solution.py:20
  49.5 5.9 %collective-permute-start.21 = (bf16[512,512]{1,0:T(8,128)(2,1)S(1)}, bf16[512,512]{1,0:T(8,128)(2,1)S(1)}, u32[]{:S(2)}, u32[]{:S(2)}) collective-permute-start(bf16[512,512]{1,0:T(8,128)(2,1)S(1)} %collective-permute-done.20.refs_10_.refs_2_), channel_id=1, source_target_pairs={{0,1},{1,0},{2,3},{3,2},{4,5},{5,4},{6,7},{7,6},{8,9},{9,8},{10,11... | collective-permute-start | bytes 1572872 | tf_op jit(solution)/shard_map/ppermute | solution.py:20
  52.7 2.7 %collective-permute-start.22 = (bf16[256,512]{1,0:T(8,128)(2,1)S(1)}, bf16[256,512]{1,0:T(8,128)(2,1)S(1)}, u32[]{:S(2)}, u32[]{:S(2)}) collective-permute-start(bf16[256,512]{1,0:T(8,128)(2,1)S(1)} %collective-permute-done.13.refs_11_.refs_3_), channel_id=1, source_target_pairs={{0,1},{1,0},{2,3},{3,2},{4,5},{5,4},{6,7},{7,6},{8,9},{9,8},{10,11... | collective-permute-start | bytes 786440 | tf_op jit(solution)/shard_map/ppermute | solution.py:20
  52.8 2.6 %collective-permute-start.19 = (bf16[1024,128]{1,0:T(8,128)(2,1)S(1)}, bf16[1024,128]{1,0:T(8,128)(2,1)S(1)}, u32[]{:S(2)}, u32[]{:S(2)}) collective-permute-start(bf16[1024,128]{1,0:T(8,128)(2,1)S(1)} %pad_maximum_fusion.refs_4_), channel_id=1, source_target_pairs={{0,1},{1,0},{2,3},{3,2},{4,5},{5,4},{6,7},{7,6},{8,9},{9,8},{10,11... | collective-permute-start | bytes 786440 | tf_op jit(solution)/shard_map/ppermute | solution.py:20
  53.4 7.7 %collective-permute-start.23 = (bf16[768,128]{1,0:T(8,128)(2,1)S(1)}, bf16[768,128]{1,0:T(8,128)(2,1)S(1)}, u32[]{:S(2)}, u32[]{:S(2)}) collective-permute-start(bf16[768,128]{1,0:T(8,128)(2,1)S(1)} %constant_dynamic-update-slice_fusion.2), channel_id=1, source_target_pairs={{0,2},{1,3},{2,0},{3,1},{4,6},{5,7},{6,4},{7,5},{8,10},{9,11},{10,... | collective-permute-start | bytes 589832 | tf_op jit(solution)/shard_map/ppermute | solution.py:20
  61.1 1.6 %collective-permute-start.24 = (bf16[1024,128]{1,0:T(8,128)(2,1)S(1)}, bf16[1024,128]{1,0:T(8,128)(2,1)S(1)}, u32[]{:S(2)}, u32[]{:S(2)}) collective-permute-start(bf16[1024,128]{1,0:T(8,128)(2,1)S(1)} %constant_dynamic-update-slice_fusion.5.refs_4_), channel_id=1, source_target_pairs={{0,1},{1,0},{2,3},{3,2},{4,5},{5,4},{6,7},{7,6},{8,9},{9,8},{10,11... | collective-permute-start | bytes 786440 | tf_op jit(solution)/shard_map/ppermute | solution.py:20

commit v16 on v14

--- a/solution.py
+++ b/solution.py
@@ -402,7 +402,7 @@
             [[local[0], early[0], late[0]]],
         )
         for d in range(2, nc, 2):
-            early[d] = swap(after(early[0], side[d]), "centers", nc, d)
+            early[d] = swap(after(early[0], side[d + 1]), "centers", nc, d)
             late[d] = swap(after(late[0], last, *soon), "centers", nc, d)
             early[d + 1] = swap(after(early[d], parts[0]), "centers", nc, 1)
         early[1] = swap(after(early[0], parts[0]), "centers", nc, 1)

time: 65.1 us -> 63.8 us (0.980)
  starting transfers between devices: 27.6 us -> 25.3 us
  waiting for transfers between devices: 13.5 us -> 14.5 us
    ppermute x25, starting transfers between devices: 27.6 us -> 25.3 us  [swap(): return lax.ppermute(a, axis, [(i, i ^ d) for i in range(size)])]
    ppermute x25, waiting for transfers between devices: 13.5 us -> 14.5 us  [swap(): return lax.ppermute(a, axis, [(i, i ^ d) for i in range(size)])]
  transfers between devices with their start and end apart: 25 -> 25, of which waited for: 8 -> 11; matrix products, arithmetic and copies ran while one was open for 3% -> 3% of each run, Pallas kernels for 22% -> 22%
where the time goes in v16:
time: 63.8 us; the launch traced here: 63.5 us
  starting transfers between devices  25.3 us (40%)
  Pallas kernels  16.4 us (26%)
  waiting for transfers between devices  14.5 us (23%)
  local copies, waits for them, and re-layouts  6.44 us (10%)
  between operations  0.82 us (1%)
    ppermute x25, starting transfers between devices, swap(): return lax.ppermute(a, axis, [(i, i ^ d) for i in range(size)])  25.3 us
    ppermute x25, waiting for transfers between devices, swap(): return lax.ppermute(a, axis, [(i, i ^ d) for i in range(size)])  14.5 us
    pallas_call x2, Pallas kernels, backward(): pl.pallas_call(body, out_shape=tuple((jax.ShapeDtypeStruct((n, width), F3...  6.08 us
    unnamed x18, local copies, waits for them, and re-layouts  4.74 us
    pallas_call x3, Pallas kernels, forward(): pl.pallas_call(body, out_shape=tuple((jax.ShapeDtypeStruct((count, out_wi...  3.95 us
    pallas_call x1, Pallas kernels, finish(): pl.pallas_call(body, out_shape=tuple((jax.ShapeDtypeStruct((n, width), F3...  2.32 us
    pallas_call x1, Pallas kernels, own_rows(): pl.pallas_call(body, out_shape=(jax.ShapeDtypeStruct((rows.shape[0], out_...  2.28 us
  transfers between devices with their start and end apart: 25, of which 11 were waited for; matrix products, arithmetic and copies ran while one was open for 3% of the time, Pallas kernels for 22%

profile of v16, /device:TPU:0, one launch (start us, length us, event | category | flops | bytes accessed | tf_op | source)
XLA Modules:
  0.0 63.5 jit_solution(3734170760022991118)
XLA Ops:
  0.6 3.0 %collective-permute-start.4 = (bf16[512,512]{1,0:T(8,128)(2,1)}, bf16[512,512]{1,0:T(8,128)(2,1)S(1)}, u32[]{:S(2)}, u32[]{:S(2)}) collective-permute-start(bf16[512,512]{1,0:T(8,128)(2,1)} %pos_ref), channel_id=1, source_target_pairs={{0,2},{1,3},{2,0},{3,1},{4,6},{5,7},{6,4},{7,5},{8,10},{9,11},{10,... | collective-permute-start | bytes 1572872 | tf_op jit(solution)/shard_map/ppermute | solution.py:20
  3.6 1.0 %constant_dynamic-slice_fusion.refs_0_.refs_13_.refs_1_ = bf16[256,512]{1,0:T(8,128)(2,1)S(1)} fusion(bf16[1024,512]{1,0:T(8,128)(2,1)} %refs_4_.1, s32[]{:T(128)S(6)} %select_n.3), kind=kLoop, calls=%fused_computation.8 | loop fusion | bytes 524292 | tf_op jit(solution)/shard_map/dynamic_slice | solution.py:354
  4.6 1.6 %collective-permute-start.6 = (bf16[256,512]{1,0:T(8,128)(2,1)S(1)}, bf16[256,512]{1,0:T(8,128)(2,1)S(1)}, u32[]{:S(2)}, u32[]{:S(2)}) collective-permute-start(bf16[256,512]{1,0:T(8,128)(2,1)S(1)} %constant_dynamic-slice_fusion.refs_0_.refs_13_.refs_1_), channel_id=1, source_target_pairs={{0,4},{4,0},{8,12},{12,8},{1,5},{5,1},{9,13},{13,9},{2,6},{6,2},{1... | collective-permute-start | bytes 786440 | tf_op jit(solution)/shard_map/ppermute | solution.py:20
  6.3 2.6 %collective-permute-start = (bf16[256,512]{1,0:T(8,128)(2,1)S(1)}, bf16[256,512]{1,0:T(8,128)(2,1)S(1)}, u32[]{:S(2)}, u32[]{:S(2)}) collective-permute-start(bf16[256,512]{1,0:T(8,128)(2,1)S(1)} %constant_dynamic-slice_fusion.refs_0_.refs_13_.refs_1_), channel_id=1, source_target_pairs={{0,8},{4,12},{8,0},{12,4},{1,9},{5,13},{9,1},{13,5},{2,10},{6,14},... | collective-permute-start | bytes 786440 | tf_op jit(solution)/shard_map/ppermute | solution.py:20
  9.5 1.0 %copy-done.1 = bf16[512,512]{1,0:T(8,128)(2,1)S(1)} copy-done((bf16[512,512]{1,0:T(8,128)(2,1)S(1)}, bf16[512,512]{1,0:T(8,128)(2,1)}, u32[]{:S(2)}) %copy-start.1) | copy-done | bytes 524312
  10.6 0.9 %copy-done.5 = bf16[512,128]{1,0:T(8,128)(2,1)S(1)} copy-done((bf16[512,128]{1,0:T(8,128)(2,1)S(1)}, bf16[512,128]{1,0:T(8,128)(2,1)}, u32[]{:S(2)}) %copy-start.5) | copy-done | bytes 131096
  13.0 1.0 %copy-done.3 = f32[1024,128]{1,0:T(8,128)S(1)} copy-done((f32[1024,128]{1,0:T(8,128)S(1)}, f32[1024,128]{1,0:T(8,128)}, u32[]{:S(2)}) %copy-start.3) | copy-done | bytes 524312
  14.0 1.0 %copy-done.4 = f32[1024,128]{1,0:T(8,128)S(1)} copy-done((f32[1024,128]{1,0:T(8,128)S(1)}, f32[1024,128]{1,0:T(8,128)}, u32[]{:S(2)}) %copy-start.4) | copy-done | bytes 524312
  15.5 3.5 %collective-permute-done.5.refs_6_ = bf16[144,512]{1,0:T(8,128)(2,1)S(1)} collective-permute-done((bf16[144,512]{1,0:T(8,128)(2,1)S(1)}, bf16[144,512]{1,0:T(8,128)(2,1)S(1)}, u32[]{:S(2)}, u32[]{:S(2)}) %collective-permute-start.5) | collective-permute-done | bytes 147488 | tf_op jit(solution)/shard_map/ppermute | solution.py:20
  19.0 1.3 %collective-permute-done.refs_0_ = bf16[256,512]{1,0:T(8,128)(2,1)S(1)} collective-permute-done((bf16[256,512]{1,0:T(8,128)(2,1)S(1)}, bf16[256,512]{1,0:T(8,128)(2,1)S(1)}, u32[]{:S(2)}, u32[]{:S(2)}) %collective-permute-start) | collective-permute-done | bytes 262176 | tf_op jit(solution)/shard_map/ppermute | solution.py:20
  21.5 0.9 %collective-permute-done.8.refs_8_ = bf16[144,512]{1,0:T(8,128)(2,1)S(1)} collective-permute-done((bf16[144,512]{1,0:T(8,128)(2,1)S(1)}, bf16[144,512]{1,0:T(8,128)(2,1)S(1)}, u32[]{:S(2)}, u32[]{:S(2)}) %collective-permute-start.8) | collective-permute-done | bytes 147488 | tf_op jit(solution)/shard_map/ppermute | solution.py:20
  22.4 1.1 %collective-permute-start.16 = (bf16[512,512]{1,0:T(8,128)(2,1)S(1)}, bf16[512,512]{1,0:T(8,128)(2,1)S(1)}, u32[]{:S(2)}, u32[]{:S(2)}) collective-permute-start(bf16[512,512]{1,0:T(8,128)(2,1)S(1)} %constant_dynamic-update-slice_fusion.refs_14_.refs_2_), channel_id=1, source_target_pairs={{0,2},{1,3},{2,0},{3,1},{4,6},{5,7},{6,4},{7,5},{8,10},{9,11},{10,... | collective-permute-start | bytes 1572872 | tf_op jit(solution)/shard_map/ppermute | solution.py:20
  23.6 1.3 %forward.3 = f32[256,128]{1,0:T(8,128)S(1)} custom-call(bf16[256,512]{1,0:T(8,128)(2,1)S(1)} %collective-permute-done.refs_0_, bf16[512,512]{1,0:T(8,128)(2,1)S(1)} %get-tuple-element.39.refs_1_.refs_11_.pos_ref, bf16[144,512]{1,0:T(8,128)(2,1)S(1)} %get-tuple-element.42.refs_2_, bf16[512,512]{1,0:T(8,128)(2,1)S(1)} %collective-permute-done.2.refs_3_, ...), custom_call_target="tpu_custom_call" | custom-call | flops 1 | bytes 1 | tf_op jit(solution)/shard_map/forward/pallas_call | solution.py:167
  24.9 2.7 %collective-permute-start.9 = (f32[256,128]{1,0:T(8,128)S(1)}, f32[256,128]{1,0:T(8,128)S(1)}, u32[]{:S(2)}, u32[]{:S(2)}) collective-permute-start(f32[256,128]{1,0:T(8,128)S(1)} %forward.3), channel_id=1, source_target_pairs={{0,8},{4,12},{8,0},{12,4},{1,9},{5,13},{9,1},{13,5},{2,10},{6,14},... | collective-permute-start | bytes 393224 | tf_op jit(solution)/shard_map/ppermute | solution.py:20
  27.5 1.3 %forward.4 = f32[256,128]{1,0:T(8,128)S(1)} custom-call(bf16[256,512]{1,0:T(8,128)(2,1)S(1)} %collective-permute-done.6.refs_0_, bf16[512,512]{1,0:T(8,128)(2,1)S(1)} %get-tuple-element.39.refs_1_.refs_11_.pos_ref, bf16[144,512]{1,0:T(8,128)(2,1)S(1)} %get-tuple-element.42.refs_2_, bf16[512,512]{1,0:T(8,128)(2,1)S(1)} %collective-permute-done.2.refs_3_, ...), custom_call_target="tpu_custom_call" | custom-call | flops 17179869184 | bytes 1048576 | tf_op jit(solution)/shard_map/forward/pallas_call | solution.py:167
  28.9 1.6 %collective-permute-start.10 = (f32[256,128]{1,0:T(8,128)S(1)}, f32[256,128]{1,0:T(8,128)S(1)}, u32[]{:S(2)}, u32[]{:S(2)}) collective-permute-start(f32[256,128]{1,0:T(8,128)S(1)} %forward.4), channel_id=1, source_target_pairs={{0,4},{4,0},{8,12},{12,8},{1,5},{5,1},{9,13},{13,9},{2,6},{6,2},{1... | collective-permute-start | bytes 393224 | tf_op jit(solution)/shard_map/ppermute | solution.py:20
  30.5 1.0 %collective-permute-done.1.refs_0_.refs_15_.refs_3_ = bf16[256,512]{1,0:T(8,128)(2,1)S(1)} collective-permute-done((bf16[256,512]{1,0:T(8,128)(2,1)S(1)}, bf16[256,512]{1,0:T(8,128)(2,1)S(1)}, u32[]{:S(2)}, u32[]{:S(2)}) %collective-permute-start.1) | collective-permute-done | bytes 262176 | tf_op jit(solution)/shard_map/ppermute | solution.py:20
  31.5 1.3 %forward.5 = f32[256,128]{1,0:T(8,128)S(1)} custom-call(bf16[256,512]{1,0:T(8,128)(2,1)S(1)} %collective-permute-done.1.refs_0_.refs_15_.refs_3_, bf16[512,512]{1,0:T(8,128)(2,1)S(1)} %get-tuple-element.39.refs_1_.refs_11_.pos_ref, bf16[144,512]{1,0:T(8,128)(2,1)S(1)} %get-tuple-element.42.refs_2_, bf16[512,512]{1,0:T(8,128)(2,1)S(1)} %collective-permute-done.2.refs_3_, ...), custom_call_target="tpu_custom_call" | custom-call | flops 17179869184 | bytes 1048576 | tf_op jit(solution)/shard_map/forward/pallas_call | solution.py:167
  32.8 0.8 %collective-permute-start.11 = (f32[256,128]{1,0:T(8,128)S(1)}, f32[256,128]{1,0:T(8,128)S(1)}, u32[]{:S(2)}, u32[]{:S(2)}) collective-permute-start(f32[256,128]{1,0:T(8,128)S(1)} %forward.5), channel_id=1, source_target_pairs={{0,12},{4,8},{8,4},{12,0},{1,13},{5,9},{9,5},{13,1},{2,14},{6,10},... | collective-permute-start | bytes 393224 | tf_op jit(solution)/shard_map/ppermute | solution.py:20
  33.6 1.0 %collective-permute-done.10.refs_10_ = f32[256,128]{1,0:T(8,128)S(1)} collective-permute-done((f32[256,128]{1,0:T(8,128)S(1)}, f32[256,128]{1,0:T(8,128)S(1)}, u32[]{:S(2)}, u32[]{:S(2)}) %collective-permute-start.10) | collective-permute-done | bytes 131104 | tf_op jit(solution)/shard_map/ppermute | solution.py:20
  34.7 1.9 %collective-permute-start.13 = (bf16[256,512]{1,0:T(8,128)(2,1)S(1)}, bf16[256,512]{1,0:T(8,128)(2,1)S(1)}, u32[]{:S(2)}, u32[]{:S(2)}) collective-permute-start(bf16[256,512]{1,0:T(8,128)(2,1)S(1)} %collective-permute-done.1.refs_0_.refs_15_.refs_3_), channel_id=1, source_target_pairs={{0,2},{1,3},{2,0},{3,1},{4,6},{5,7},{6,4},{7,5},{8,10},{9,11},{10,... | collective-permute-start | bytes 786440 | tf_op jit(solution)/shard_map/ppermute | solution.py:20
  36.5 2.3 %own_rows.1 = (f32[256,128]{1,0:T(8,128)S(1)}, bf16[512,1024]{1,0:T(8,128)(2,1)S(1)}) custom-call(bf16[256,512]{1,0:T(8,128)(2,1)S(1)} %constant_dynamic-slice_fusion.refs_0_.refs_13_.refs_1_, bf16[512,512]{1,0:T(8,128)(2,1)S(1)} %get-tuple-element.39.refs_1_.refs_11_.pos_ref, bf16[144,512]{1,0:T(8,128)(2,1)S(1)} %get-tuple-element.42.refs_2_, ...), custom_call_target="tpu_custom_call" | custom-call | flops 17179869184 | bytes 1048576 | tf_op jit(solution)/shard_map/own_rows/pallas_call | solution.py:214
  38.8 0.9 %collective-permute-done.11.refs_1_ = f32[256,128]{1,0:T(8,128)S(1)} collective-permute-done((f32[256,128]{1,0:T(8,128)S(1)}, f32[256,128]{1,0:T(8,128)S(1)}, u32[]{:S(2)}, u32[]{:S(2)}) %collective-permute-start.11) | collective-permute-done | bytes 131104 | tf_op jit(solution)/shard_map/ppermute | solution.py:20
  39.8 2.6 %collective-permute-start.15 = (bf16[256,128]{1,0:T(8,128)(2,1)S(1)}, bf16[256,128]{1,0:T(8,128)(2,1)S(1)}, u32[]{:S(2)}, u32[]{:S(2)}) collective-permute-start(bf16[256,128]{1,0:T(8,128)(2,1)S(1)} %cotangent.1), channel_id=1, source_target_pairs={{0,8},{4,12},{8,0},{12,4},{1,9},{5,13},{9,1},{13,5},{2,10},{6,14},... | collective-permute-start | bytes 196616 | tf_op jit(solution)/shard_map/ppermute | solution.py:20
  42.4 1.4 %collective-permute-start.12 = (bf16[256,128]{1,0:T(8,128)(2,1)S(1)}, bf16[256,128]{1,0:T(8,128)(2,1)S(1)}, u32[]{:S(2)}, u32[]{:S(2)}) collective-permute-start(bf16[256,128]{1,0:T(8,128)(2,1)S(1)} %cotangent.1), channel_id=1, source_target_pairs={{0,4},{4,0},{8,12},{12,8},{1,5},{5,1},{9,13},{13,9},{2,6},{6,2},{1... | collective-permute-start | bytes 196616 | tf_op jit(solution)/shard_map/ppermute | solution.py:20
  43.8 2.0 %collective-permute-start.14 = (bf16[256,128]{1,0:T(8,128)(2,1)S(1)}, bf16[256,128]{1,0:T(8,128)(2,1)S(1)}, u32[]{:S(2)}, u32[]{:S(2)}) collective-permute-start(bf16[256,128]{1,0:T(8,128)(2,1)S(1)} %cotangent.1), channel_id=1, source_target_pairs={{0,2},{1,3},{2,0},{3,1},{4,6},{5,7},{6,4},{7,5},{8,10},{9,11},{10,... | collective-permute-start | bytes 196616 | tf_op jit(solution)/shard_map/ppermute | solution.py:20
  46.3 1.1 %own_kernel.1.refs_0_ = bf16[512,1024]{1,0:T(8,128)(2,1)S(1)} custom-call(bf16[512,512]{1,0:T(8,128)(2,1)S(1)} %get-tuple-element.39.refs_1_.refs_11_.pos_ref, bf16[1,512]{1,0:T(2,128)(2,1)S(1)} %get-tuple-element.41.refs_12_.spread_ref, bf16[256,512]{1,0:T(8,128)(2,1)S(1)} %get-tuple-element.56.refs_0_.refs_1_, ...), custom_call_target="tpu_custom_call" | custom-call | flops 1 | bytes 1 | tf_op jit(solution)/shard_map/own_kernel/pallas_call | solution.py:185
  48.1 3.9 %collective-permute-done.17 = bf16[256,128]{1,0:T(8,128)(2,1)S(1)} collective-permute-done((bf16[256,128]{1,0:T(8,128)(2,1)S(1)}, bf16[256,128]{1,0:T(8,128)(2,1)S(1)}, u32[]{:S(2)}, u32[]{:S(2)}) %collective-permute-start.17) | collective-permute-done | bytes 65568 | tf_op jit(solution)/shard_map/ppermute | solution.py:20
  54.0 4.8 %backward.2 = (f32[512,512]{1,0:T(8,128)S(1)}, f32[512,128]{1,0:T(8,128)S(1)}, f32[512,128]{1,0:T(8,128)S(1)}, bf16[512,1024]{1,0:T(8,128)(2,1)S(1)}) custom-call(bf16[512,512]{1,0:T(8,128)(2,1)S(1)} %get-tuple-element.39.refs_1_.refs_11_.pos_ref, bf16[512,128]{1,0:T(8,128)(2,1)S(1)} %get-tuple-element.40.coef_ref, ...), custom_call_target="tpu_custom_call" | custom-call | flops 17179869184 | bytes 1048576 | tf_op jit(solution)/shard_map/backward/pallas_call | solution.py:288
  58.7 0.8 %collective-permute-done.23 = bf16[768,128]{1,0:T(8,128)(2,1)S(1)} collective-permute-done((bf16[768,128]{1,0:T(8,128)(2,1)S(1)}, bf16[768,128]{1,0:T(8,128)(2,1)S(1)}, u32[]{:S(2)}, u32[]{:S(2)}) %collective-permute-start.23) | collective-permute-done | bytes 196640 | tf_op jit(solution)/shard_map/ppermute | solution.py:20
  59.6 1.3 %backward.3 = (f32[512,512]{1,0:T(8,128)S(1)}, f32[512,128]{1,0:T(8,128)S(1)}, f32[512,128]{1,0:T(8,128)S(1)}) custom-call(bf16[512,512]{1,0:T(8,128)(2,1)S(1)} %get-tuple-element.39.refs_1_.refs_11_.pos_ref, bf16[512,128]{1,0:T(8,128)(2,1)S(1)} %get-tuple-element.40.coef_ref, bf16[1,512]{1,0:T(2,128)(2,1)S(1)} %get-tuple-element.41.refs_12_.spread_ref, ...), custom_call_target="tpu_custom_call" | custom-call | flops 1 | bytes 1 | tf_op jit(solution)/shard_map/backward/pallas_call | solution.py:288
  61.2 2.3 %finish.1 = (f32[512,512]{1,0:T(8,128)}, f32[512,128]{1,0:T(8,128)}) custom-call(bf16[512,512]{1,0:T(8,128)(2,1)S(1)} %get-tuple-element.39.refs_1_.refs_11_.pos_ref, bf16[512,128]{1,0:T(8,128)(2,1)S(1)} %get-tuple-element.40.coef_ref, bf16[1,512]{1,0:T(2,128)(2,1)S(1)} %get-tuple-element.41.refs_12_.spread_ref, ...), custom_call_target="tpu_custom_call" | custom-call | flops 1 | bytes 1 | tf_op jit(solution)/shard_map/finish/pallas_call | solution.py:330
  (53 shorter events, 7.3 us)
Async XLA Ops:
  0.6 12.3 %copy-start = (bf16[1024,512]{1,0:T(8,128)(2,1)S(1)}, bf16[1024,512]{1,0:T(8,128)(2,1)}, u32[]{:S(2)}) copy-start(bf16[1024,512]{1,0:T(8,128)(2,1)} %refs_4_.1) | copy-start | bytes 3145732
  0.6 19.7 %collective-permute-start.4 = (bf16[512,512]{1,0:T(8,128)(2,1)}, bf16[512,512]{1,0:T(8,128)(2,1)S(1)}, u32[]{:S(2)}, u32[]{:S(2)}) collective-permute-start(bf16[512,512]{1,0:T(8,128)(2,1)} %pos_ref), channel_id=1, source_target_pairs={{0,2},{1,3},{2,0},{3,1},{4,6},{5,7},{6,4},{7,5},{8,10},{9,11},{10,... | collective-permute-start | bytes 1572872 | tf_op jit(solution)/shard_map/ppermute | solution.py:20
  4.6 14.3 %collective-permute-start.6 = (bf16[256,512]{1,0:T(8,128)(2,1)S(1)}, bf16[256,512]{1,0:T(8,128)(2,1)S(1)}, u32[]{:S(2)}, u32[]{:S(2)}) collective-permute-start(bf16[256,512]{1,0:T(8,128)(2,1)S(1)} %constant_dynamic-slice_fusion.refs_0_.refs_13_.refs_1_), channel_id=1, source_target_pairs={{0,4},{4,0},{8,12},{12,8},{1,5},{5,1},{9,13},{13,9},{2,6},{6,2},{1... | collective-permute-start | bytes 786440 | tf_op jit(solution)/shard_map/ppermute | solution.py:20
  6.3 14.0 %collective-permute-start = (bf16[256,512]{1,0:T(8,128)(2,1)S(1)}, bf16[256,512]{1,0:T(8,128)(2,1)S(1)}, u32[]{:S(2)}, u32[]{:S(2)}) collective-permute-start(bf16[256,512]{1,0:T(8,128)(2,1)S(1)} %constant_dynamic-slice_fusion.refs_0_.refs_13_.refs_1_), channel_id=1, source_target_pairs={{0,8},{4,12},{8,0},{12,4},{1,9},{5,13},{9,1},{13,5},{2,10},{6,14},... | collective-permute-start | bytes 786440 | tf_op jit(solution)/shard_map/ppermute | solution.py:20
  9.5 1.0 %copy-start.1 = (bf16[512,512]{1,0:T(8,128)(2,1)S(1)}, bf16[512,512]{1,0:T(8,128)(2,1)}, u32[]{:S(2)}) copy-start(bf16[512,512]{1,0:T(8,128)(2,1)} %pos_ref) | copy-start | bytes 1572868
  10.6 0.9 %copy-start.5 = (bf16[512,128]{1,0:T(8,128)(2,1)S(1)}, bf16[512,128]{1,0:T(8,128)(2,1)}, u32[]{:S(2)}) copy-start(bf16[512,128]{1,0:T(8,128)(2,1)} %coef_ref.1) | copy-start | bytes 393220
  11.5 0.7 %copy-start.6 = (f32[128]{0:T(128)S(1)}, f32[128]{0:T(128)}, u32[]{:S(2)}) copy-start(f32[128]{0:T(128)} %param.10) | copy-start | bytes 1540
  12.3 6.6 %copy-start.2 = (bf16[512,512]{1,0:T(8,128)(2,1)S(1)}, bf16[512,512]{1,0:T(8,128)(2,1)}, u32[]{:S(2)}) copy-start(bf16[512,512]{1,0:T(8,128)(2,1)} %pos_ref) | copy-start | bytes 1572868
  12.4 6.6 %collective-permute-start.5 = (bf16[144,512]{1,0:T(8,128)(2,1)S(1)}, bf16[144,512]{1,0:T(8,128)(2,1)S(1)}, u32[]{:S(2)}, u32[]{:S(2)}) collective-permute-start(bf16[144,512]{1,0:T(8,128)(2,1)S(1)} %get-tuple-element.42.refs_2_), channel_id=1, source_target_pairs={{0,2},{1,3},{2,0},{3,1},{4,6},{5,7},{6,4},{7,5},{8,10},{9,11},{10,... | collective-permute-start | bytes 442376 | tf_op jit(solution)/shard_map/ppermute | solution.py:20
  13.0 6.0 %collective-permute-start.3 = (bf16[144,512]{1,0:T(8,128)(2,1)S(1)}, bf16[144,512]{1,0:T(8,128)(2,1)S(1)}, u32[]{:S(2)}, u32[]{:S(2)}) collective-permute-start(bf16[144,512]{1,0:T(8,128)(2,1)S(1)} %get-tuple-element.42.refs_2_), channel_id=1, source_target_pairs={{0,1},{1,0},{2,3},{3,2},{4,5},{5,4},{6,7},{7,6},{8,9},{9,8},{10,11... | collective-permute-start | bytes 442376 | tf_op jit(solution)/shard_map/ppermute | solution.py:20
  13.0 1.0 %copy-start.3 = (f32[1024,128]{1,0:T(8,128)S(1)}, f32[1024,128]{1,0:T(8,128)}, u32[]{:S(2)}) copy-start(f32[1024,128]{1,0:T(8,128)} %refs_0_.1) | copy-start | bytes 1572868
  14.0 1.0 %copy-start.4 = (f32[1024,128]{1,0:T(8,128)S(1)}, f32[1024,128]{1,0:T(8,128)}, u32[]{:S(2)}) copy-start(f32[1024,128]{1,0:T(8,128)} %refs_1_.1) | copy-start | bytes 1572868
  18.9 4.6 %collective-permute-start.2 = (bf16[512,512]{1,0:T(8,128)(2,1)S(1)}, bf16[512,512]{1,0:T(8,128)(2,1)S(1)}, u32[]{:S(2)}, u32[]{:S(2)}) collective-permute-start(bf16[512,512]{1,0:T(8,128)(2,1)S(1)} %copy-done.2), channel_id=1, source_target_pairs={{0,1},{1,0},{2,3},{3,2},{4,5},{5,4},{6,7},{7,6},{8,9},{9,8},{10,11... | collective-permute-start | bytes 1572872 | tf_op jit(solution)/shard_map/ppermute | solution.py:20
  20.3 3.3 %collective-permute-start.7 = (bf16[512,512]{1,0:T(8,128)(2,1)S(1)}, bf16[512,512]{1,0:T(8,128)(2,1)S(1)}, u32[]{:S(2)}, u32[]{:S(2)}) collective-permute-start(bf16[512,512]{1,0:T(8,128)(2,1)S(1)} %collective-permute-done.4.refs_5_), channel_id=1, source_target_pairs={{0,1},{1,0},{2,3},{3,2},{4,5},{5,4},{6,7},{7,6},{8,9},{9,8},{10,11... | collective-permute-start | bytes 1572872 | tf_op jit(solution)/shard_map/ppermute | solution.py:20
  20.3 2.1 %collective-permute-start.8 = (bf16[144,512]{1,0:T(8,128)(2,1)S(1)}, bf16[144,512]{1,0:T(8,128)(2,1)S(1)}, u32[]{:S(2)}, u32[]{:S(2)}) collective-permute-start(bf16[144,512]{1,0:T(8,128)(2,1)S(1)} %collective-permute-done.5.refs_6_), channel_id=1, source_target_pairs={{0,1},{1,0},{2,3},{3,2},{4,5},{5,4},{6,7},{7,6},{8,9},{9,8},{10,11... | collective-permute-start | bytes 442376 | tf_op jit(solution)/shard_map/ppermute | solution.py:20
  20.8 10.7 %collective-permute-start.1 = (bf16[256,512]{1,0:T(8,128)(2,1)S(1)}, bf16[256,512]{1,0:T(8,128)(2,1)S(1)}, u32[]{:S(2)}, u32[]{:S(2)}) collective-permute-start(bf16[256,512]{1,0:T(8,128)(2,1)S(1)} %collective-permute-done.refs_0_), channel_id=1, source_target_pairs={{0,4},{4,0},{8,12},{12,8},{1,5},{5,1},{9,13},{13,9},{2,6},{6,2},{1... | collective-permute-start | bytes 786440 | tf_op jit(solution)/shard_map/ppermute | solution.py:20
  22.4 23.4 %collective-permute-start.16 = (bf16[512,512]{1,0:T(8,128)(2,1)S(1)}, bf16[512,512]{1,0:T(8,128)(2,1)S(1)}, u32[]{:S(2)}, u32[]{:S(2)}) collective-permute-start(bf16[512,512]{1,0:T(8,128)(2,1)S(1)} %constant_dynamic-update-slice_fusion.refs_14_.refs_2_), channel_id=1, source_target_pairs={{0,2},{1,3},{2,0},{3,1},{4,6},{5,7},{6,4},{7,5},{8,10},{9,11},{10,... | collective-permute-start | bytes 1572872 | tf_op jit(solution)/shard_map/ppermute | solution.py:20
  24.9 9.8 %collective-permute-start.9 = (f32[256,128]{1,0:T(8,128)S(1)}, f32[256,128]{1,0:T(8,128)S(1)}, u32[]{:S(2)}, u32[]{:S(2)}) collective-permute-start(f32[256,128]{1,0:T(8,128)S(1)} %forward.3), channel_id=1, source_target_pairs={{0,8},{4,12},{8,0},{12,4},{1,9},{5,13},{9,1},{13,5},{2,10},{6,14},... | collective-permute-start | bytes 393224 | tf_op jit(solution)/shard_map/ppermute | solution.py:20
  28.9 5.8 %collective-permute-start.10 = (f32[256,128]{1,0:T(8,128)S(1)}, f32[256,128]{1,0:T(8,128)S(1)}, u32[]{:S(2)}, u32[]{:S(2)}) collective-permute-start(f32[256,128]{1,0:T(8,128)S(1)} %forward.4), channel_id=1, source_target_pairs={{0,4},{4,0},{8,12},{12,8},{1,5},{5,1},{9,13},{13,9},{2,6},{6,2},{1... | collective-permute-start | bytes 393224 | tf_op jit(solution)/shard_map/ppermute | solution.py:20
  32.8 6.8 %collective-permute-start.11 = (f32[256,128]{1,0:T(8,128)S(1)}, f32[256,128]{1,0:T(8,128)S(1)}, u32[]{:S(2)}, u32[]{:S(2)}) collective-permute-start(f32[256,128]{1,0:T(8,128)S(1)} %forward.5), channel_id=1, source_target_pairs={{0,12},{4,8},{8,4},{12,0},{1,13},{5,9},{9,5},{13,1},{2,14},{6,10},... | collective-permute-start | bytes 393224 | tf_op jit(solution)/shard_map/ppermute | solution.py:20
  34.7 9.1 %collective-permute-start.13 = (bf16[256,512]{1,0:T(8,128)(2,1)S(1)}, bf16[256,512]{1,0:T(8,128)(2,1)S(1)}, u32[]{:S(2)}, u32[]{:S(2)}) collective-permute-start(bf16[256,512]{1,0:T(8,128)(2,1)S(1)} %collective-permute-done.1.refs_0_.refs_15_.refs_3_), channel_id=1, source_target_pairs={{0,2},{1,3},{2,0},{3,1},{4,6},{5,7},{6,4},{7,5},{8,10},{9,11},{10,... | collective-permute-start | bytes 786440 | tf_op jit(solution)/shard_map/ppermute | solution.py:20
  39.8 7.6 %collective-permute-start.15 = (bf16[256,128]{1,0:T(8,128)(2,1)S(1)}, bf16[256,128]{1,0:T(8,128)(2,1)S(1)}, u32[]{:S(2)}, u32[]{:S(2)}) collective-permute-start(bf16[256,128]{1,0:T(8,128)(2,1)S(1)} %cotangent.1), channel_id=1, source_target_pairs={{0,8},{4,12},{8,0},{12,4},{1,9},{5,13},{9,1},{13,5},{2,10},{6,14},... | collective-permute-start | bytes 196616 | tf_op jit(solution)/shard_map/ppermute | solution.py:20
  42.4 5.0 %collective-permute-start.12 = (bf16[256,128]{1,0:T(8,128)(2,1)S(1)}, bf16[256,128]{1,0:T(8,128)(2,1)S(1)}, u32[]{:S(2)}, u32[]{:S(2)}) collective-permute-start(bf16[256,128]{1,0:T(8,128)(2,1)S(1)} %cotangent.1), channel_id=1, source_target_pairs={{0,4},{4,0},{8,12},{12,8},{1,5},{5,1},{9,13},{13,9},{2,6},{6,2},{1... | collective-permute-start | bytes 196616 | tf_op jit(solution)/shard_map/ppermute | solution.py:20
  43.8 4.3 %collective-permute-start.14 = (bf16[256,128]{1,0:T(8,128)(2,1)S(1)}, bf16[256,128]{1,0:T(8,128)(2,1)S(1)}, u32[]{:S(2)}, u32[]{:S(2)}) collective-permute-start(bf16[256,128]{1,0:T(8,128)(2,1)S(1)} %cotangent.1), channel_id=1, source_target_pairs={{0,2},{1,3},{2,0},{3,1},{4,6},{5,7},{6,4},{7,5},{8,10},{9,11},{10,... | collective-permute-start | bytes 196616 | tf_op jit(solution)/shard_map/ppermute | solution.py:20
  45.8 6.9 %collective-permute-start.19 = (bf16[256,512]{1,0:T(8,128)(2,1)S(1)}, bf16[256,512]{1,0:T(8,128)(2,1)S(1)}, u32[]{:S(2)}, u32[]{:S(2)}) collective-permute-start(bf16[256,512]{1,0:T(8,128)(2,1)S(1)} %collective-permute-done.1.refs_0_.refs_15_.refs_3_), channel_id=1, source_target_pairs={{0,1},{1,0},{2,3},{3,2},{4,5},{5,4},{6,7},{7,6},{8,9},{9,8},{10,11... | collective-permute-start | bytes 786440 | tf_op jit(solution)/shard_map/ppermute | solution.py:20
  45.8 7.2 %collective-permute-start.18 = (bf16[512,512]{1,0:T(8,128)(2,1)S(1)}, bf16[512,512]{1,0:T(8,128)(2,1)S(1)}, u32[]{:S(2)}, u32[]{:S(2)}) collective-permute-start(bf16[512,512]{1,0:T(8,128)(2,1)S(1)} %constant_dynamic-update-slice_fusion.refs_14_.refs_2_), channel_id=1, source_target_pairs={{0,1},{1,0},{2,3},{3,2},{4,5},{5,4},{6,7},{7,6},{8,9},{9,8},{10,11... | collective-permute-start | bytes 1572872 | tf_op jit(solution)/shard_map/ppermute | solution.py:20
  47.4 5.6 %collective-permute-start.21 = (bf16[512,512]{1,0:T(8,128)(2,1)S(1)}, bf16[512,512]{1,0:T(8,128)(2,1)S(1)}, u32[]{:S(2)}, u32[]{:S(2)}) collective-permute-start(bf16[512,512]{1,0:T(8,128)(2,1)S(1)} %collective-permute-done.16.refs_1_.refs_2_), channel_id=1, source_target_pairs={{0,1},{1,0},{2,3},{3,2},{4,5},{5,4},{6,7},{7,6},{8,9},{9,8},{10,11... | collective-permute-start | bytes 1572872 | tf_op jit(solution)/shard_map/ppermute | solution.py:20
  47.5 4.5 %collective-permute-start.17 = (bf16[256,128]{1,0:T(8,128)(2,1)S(1)}, bf16[256,128]{1,0:T(8,128)(2,1)S(1)}, u32[]{:S(2)}, u32[]{:S(2)}) collective-permute-start(bf16[256,128]{1,0:T(8,128)(2,1)S(1)} %collective-permute-done.15), channel_id=1, source_target_pairs={{0,4},{4,0},{8,12},{12,8},{1,5},{5,1},{9,13},{13,9},{2,6},{6,2},{1... | collective-permute-start | bytes 196616 | tf_op jit(solution)/shard_map/ppermute | solution.py:20
  52.0 1.6 %collective-permute-start.22 = (bf16[256,512]{1,0:T(8,128)(2,1)S(1)}, bf16[256,512]{1,0:T(8,128)(2,1)S(1)}, u32[]{:S(2)}, u32[]{:S(2)}) collective-permute-start(bf16[256,512]{1,0:T(8,128)(2,1)S(1)} %collective-permute-done.13.refs_2_.refs_3_), channel_id=1, source_target_pairs={{0,1},{1,0},{2,3},{3,2},{4,5},{5,4},{6,7},{7,6},{8,9},{9,8},{10,11... | collective-permute-start | bytes 786440 | tf_op jit(solution)/shard_map/ppermute | solution.py:20
  52.1 1.9 %collective-permute-start.20 = (bf16[1024,128]{1,0:T(8,128)(2,1)S(1)}, bf16[1024,128]{1,0:T(8,128)(2,1)S(1)}, u32[]{:S(2)}, u32[]{:S(2)}) collective-permute-start(bf16[1024,128]{1,0:T(8,128)(2,1)S(1)} %pad_maximum_fusion.refs_4_), channel_id=1, source_target_pairs={{0,1},{1,0},{2,3},{3,2},{4,5},{5,4},{6,7},{7,6},{8,9},{9,8},{10,11... | collective-permute-start | bytes 786440 | tf_op jit(solution)/shard_map/ppermute | solution.py:20
  52.6 6.9 %collective-permute-start.23 = (bf16[768,128]{1,0:T(8,128)(2,1)S(1)}, bf16[768,128]{1,0:T(8,128)(2,1)S(1)}, u32[]{:S(2)}, u32[]{:S(2)}) collective-permute-start(bf16[768,128]{1,0:T(8,128)(2,1)S(1)} %constant_dynamic-update-slice_fusion.2), channel_id=1, source_target_pairs={{0,2},{1,3},{2,0},{3,1},{4,6},{5,7},{6,4},{7,5},{8,10},{9,11},{10,... | collective-permute-start | bytes 589832 | tf_op jit(solution)/shard_map/ppermute | solution.py:20
  59.6 1.6 %collective-permute-start.24 = (bf16[1024,128]{1,0:T(8,128)(2,1)S(1)}, bf16[1024,128]{1,0:T(8,128)(2,1)S(1)}, u32[]{:S(2)}, u32[]{:S(2)}) collective-permute-start(bf16[1024,128]{1,0:T(8,128)(2,1)S(1)} %constant_dynamic-update-slice_fusion.5.refs_4_), channel_id=1, source_target_pairs={{0,1},{1,0},{2,3},{3,2},{4,5},{5,4},{6,7},{7,6},{8,9},{9,8},{10,11... | collective-permute-start | bytes 786440 | tf_op jit(solution)/shard_map/ppermute | solution.py:20

commit v17 on v15

--- a/solution.py
+++ b/solution.py
@@ -402,7 +402,7 @@
             [[local[0], early[0], late[0]]],
         )
         for d in range(2, nc, 2):
-            early[d] = swap(after(early[0], side[d]), "centers", nc, d)
+            early[d] = swap(after(early[0], side[d + 1]), "centers", nc, d)
             late[d] = swap(after(late[0], last, *soon), "centers", nc, d)
             early[d + 1] = swap(after(early[d], parts[0]), "centers", nc, 1)
         early[1] = swap(after(early[0], parts[0]), "centers", nc, 1)

time: 65.4 us -> 65.7 us (level)
  starting transfers between devices: 23.6 us -> 26.9 us
  waiting for transfers between devices: 17.9 us -> 15 us
    ppermute x25, starting transfers between devices: 23.6 us -> 26.9 us  [swap(): return lax.ppermute(a, axis, [(i, i ^ d) for i in range(size)])]
    ppermute x25, waiting for transfers between devices: 17.9 us -> 15 us  [swap(): return lax.ppermute(a, axis, [(i, i ^ d) for i in range(size)])]
  transfers between devices with their start and end apart: 25 -> 25, of which waited for: 8 -> 9; matrix products, arithmetic and copies ran while one was open for 3% -> 3% of each run, Pallas kernels for 21% -> 21%
where the time goes in v17:
time: 65.7 us; the launch traced here: 65.4 us
  starting transfers between devices  26.9 us (41%)
  Pallas kernels  16.2 us (25%)
  waiting for transfers between devices  15 us (23%)
  local copies, waits for them, and re-layouts  6.45 us (10%)
  between operations  0.84 us (1%)
    ppermute x25, starting transfers between devices, swap(): return lax.ppermute(a, axis, [(i, i ^ d) for i in range(size)])  26.9 us
    ppermute x25, waiting for transfers between devices, swap(): return lax.ppermute(a, axis, [(i, i ^ d) for i in range(size)])  15 us
    pallas_call x2, Pallas kernels, backward(): pl.pallas_call(body, out_shape=tuple((jax.ShapeDtypeStruct((n, width), F3...  6.98 us
    unnamed x18, local copies, waits for them, and re-layouts  4.74 us
    pallas_call x3, Pallas kernels, forward(): pl.pallas_call(body, out_shape=tuple((jax.ShapeDtypeStruct((count, out_wi...  3.94 us
    pallas_call x1, Pallas kernels, finish(): pl.pallas_call(body, out_shape=tuple((jax.ShapeDtypeStruct((n, width), F3...  2.31 us
    pallas_call x1, Pallas kernels, own_rows(): pl.pallas_call(body, out_shape=(jax.ShapeDtypeStruct((rows.shape[0], out_...  2.27 us
  transfers between devices with their start and end apart: 25, of which 9 were waited for; matrix products, arithmetic and copies ran while one was open for 3% of the time, Pallas kernels for 21%

profile of v17, /device:TPU:0, one launch (start us, length us, event | category | flops | bytes accessed | tf_op | source)
XLA Modules:
  0.0 65.4 jit_solution(4232258080074591030)
XLA Ops:
  0.6 3.0 %collective-permute-start.4 = (bf16[512,512]{1,0:T(8,128)(2,1)}, bf16[512,512]{1,0:T(8,128)(2,1)S(1)}, u32[]{:S(2)}, u32[]{:S(2)}) collective-permute-start(bf16[512,512]{1,0:T(8,128)(2,1)} %pos_ref), channel_id=1, source_target_pairs={{0,2},{1,3},{2,0},{3,1},{4,6},{5,7},{6,4},{7,5},{8,10},{9,11},{10,... | collective-permute-start | bytes 1572872 | tf_op jit(solution)/shard_map/ppermute | solution.py:20
  3.6 1.0 %constant_dynamic-slice_fusion.refs_0_.refs_13_.refs_1_ = bf16[256,512]{1,0:T(8,128)(2,1)S(1)} fusion(bf16[1024,512]{1,0:T(8,128)(2,1)} %refs_4_.1, s32[]{:T(128)S(6)} %select_n.3), kind=kLoop, calls=%fused_computation.8 | loop fusion | bytes 524292 | tf_op jit(solution)/shard_map/dynamic_slice | solution.py:354
  4.6 1.6 %collective-permute-start.6 = (bf16[256,512]{1,0:T(8,128)(2,1)S(1)}, bf16[256,512]{1,0:T(8,128)(2,1)S(1)}, u32[]{:S(2)}, u32[]{:S(2)}) collective-permute-start(bf16[256,512]{1,0:T(8,128)(2,1)S(1)} %constant_dynamic-slice_fusion.refs_0_.refs_13_.refs_1_), channel_id=1, source_target_pairs={{0,4},{4,0},{8,12},{12,8},{1,5},{5,1},{9,13},{13,9},{2,6},{6,2},{1... | collective-permute-start | bytes 786440 | tf_op jit(solution)/shard_map/ppermute | solution.py:20
  6.3 2.6 %collective-permute-start = (bf16[256,512]{1,0:T(8,128)(2,1)S(1)}, bf16[256,512]{1,0:T(8,128)(2,1)S(1)}, u32[]{:S(2)}, u32[]{:S(2)}) collective-permute-start(bf16[256,512]{1,0:T(8,128)(2,1)S(1)} %constant_dynamic-slice_fusion.refs_0_.refs_13_.refs_1_), channel_id=1, source_target_pairs={{0,8},{4,12},{8,0},{12,4},{1,9},{5,13},{9,1},{13,5},{2,10},{6,14},... | collective-permute-start | bytes 786440 | tf_op jit(solution)/shard_map/ppermute | solution.py:20
  9.5 1.0 %copy-done.1 = bf16[512,512]{1,0:T(8,128)(2,1)S(1)} copy-done((bf16[512,512]{1,0:T(8,128)(2,1)S(1)}, bf16[512,512]{1,0:T(8,128)(2,1)}, u32[]{:S(2)}) %copy-start.1) | copy-done | bytes 524312
  10.6 0.9 %copy-done.5 = bf16[512,128]{1,0:T(8,128)(2,1)S(1)} copy-done((bf16[512,128]{1,0:T(8,128)(2,1)S(1)}, bf16[512,128]{1,0:T(8,128)(2,1)}, u32[]{:S(2)}) %copy-start.5) | copy-done | bytes 131096
  13.0 1.0 %copy-done.3 = f32[1024,128]{1,0:T(8,128)S(1)} copy-done((f32[1024,128]{1,0:T(8,128)S(1)}, f32[1024,128]{1,0:T(8,128)}, u32[]{:S(2)}) %copy-start.3) | copy-done | bytes 524312
  14.0 1.0 %copy-done.4 = f32[1024,128]{1,0:T(8,128)S(1)} copy-done((f32[1024,128]{1,0:T(8,128)S(1)}, f32[1024,128]{1,0:T(8,128)}, u32[]{:S(2)}) %copy-start.4) | copy-done | bytes 524312
  15.5 3.5 %collective-permute-done.5.refs_6_ = bf16[144,512]{1,0:T(8,128)(2,1)S(1)} collective-permute-done((bf16[144,512]{1,0:T(8,128)(2,1)S(1)}, bf16[144,512]{1,0:T(8,128)(2,1)S(1)}, u32[]{:S(2)}, u32[]{:S(2)}) %collective-permute-start.5) | collective-permute-done | bytes 147488 | tf_op jit(solution)/shard_map/ppermute | solution.py:20
  19.0 1.3 %collective-permute-done.refs_0_ = bf16[256,512]{1,0:T(8,128)(2,1)S(1)} collective-permute-done((bf16[256,512]{1,0:T(8,128)(2,1)S(1)}, bf16[256,512]{1,0:T(8,128)(2,1)S(1)}, u32[]{:S(2)}, u32[]{:S(2)}) %collective-permute-start) | collective-permute-done | bytes 262176 | tf_op jit(solution)/shard_map/ppermute | solution.py:20
  21.5 0.9 %collective-permute-done.8.refs_8_ = bf16[144,512]{1,0:T(8,128)(2,1)S(1)} collective-permute-done((bf16[144,512]{1,0:T(8,128)(2,1)S(1)}, bf16[144,512]{1,0:T(8,128)(2,1)S(1)}, u32[]{:S(2)}, u32[]{:S(2)}) %collective-permute-start.8) | collective-permute-done | bytes 147488 | tf_op jit(solution)/shard_map/ppermute | solution.py:20
  22.4 1.1 %collective-permute-start.20 = (bf16[512,512]{1,0:T(8,128)(2,1)S(1)}, bf16[512,512]{1,0:T(8,128)(2,1)S(1)}, u32[]{:S(2)}, u32[]{:S(2)}) collective-permute-start(bf16[512,512]{1,0:T(8,128)(2,1)S(1)} %constant_dynamic-update-slice_fusion.refs_14_.refs_2_), channel_id=1, source_target_pairs={{0,2},{1,3},{2,0},{3,1},{4,6},{5,7},{6,4},{7,5},{8,10},{9,11},{10,... | collective-permute-start | bytes 1572872 | tf_op jit(solution)/shard_map/ppermute | solution.py:20
  23.6 1.3 %forward.3 = f32[256,128]{1,0:T(8,128)S(1)} custom-call(bf16[256,512]{1,0:T(8,128)(2,1)S(1)} %collective-permute-done.refs_0_, bf16[512,512]{1,0:T(8,128)(2,1)S(1)} %get-tuple-element.39.refs_1_.refs_11_.pos_ref, bf16[144,512]{1,0:T(8,128)(2,1)S(1)} %get-tuple-element.42.refs_2_, bf16[512,512]{1,0:T(8,128)(2,1)S(1)} %collective-permute-done.2.refs_3_, ...), custom_call_target="tpu_custom_call" | custom-call | flops 1 | bytes 1 | tf_op jit(solution)/shard_map/forward/pallas_call | solution.py:167
  24.9 2.7 %collective-permute-start.9 = (f32[256,128]{1,0:T(8,128)S(1)}, f32[256,128]{1,0:T(8,128)S(1)}, u32[]{:S(2)}, u32[]{:S(2)}) collective-permute-start(f32[256,128]{1,0:T(8,128)S(1)} %forward.3), channel_id=1, source_target_pairs={{0,8},{4,12},{8,0},{12,4},{1,9},{5,13},{9,1},{13,5},{2,10},{6,14},... | collective-permute-start | bytes 393224 | tf_op jit(solution)/shard_map/ppermute | solution.py:20
  27.5 1.3 %forward.4 = f32[256,128]{1,0:T(8,128)S(1)} custom-call(bf16[256,512]{1,0:T(8,128)(2,1)S(1)} %collective-permute-done.6.refs_0_, bf16[512,512]{1,0:T(8,128)(2,1)S(1)} %get-tuple-element.39.refs_1_.refs_11_.pos_ref, bf16[144,512]{1,0:T(8,128)(2,1)S(1)} %get-tuple-element.42.refs_2_, bf16[512,512]{1,0:T(8,128)(2,1)S(1)} %collective-permute-done.2.refs_3_, ...), custom_call_target="tpu_custom_call" | custom-call | flops 17179869184 | bytes 1048576 | tf_op jit(solution)/shard_map/forward/pallas_call | solution.py:167
  28.8 1.6 %collective-permute-start.10 = (f32[256,128]{1,0:T(8,128)S(1)}, f32[256,128]{1,0:T(8,128)S(1)}, u32[]{:S(2)}, u32[]{:S(2)}) collective-permute-start(f32[256,128]{1,0:T(8,128)S(1)} %forward.4), channel_id=1, source_target_pairs={{0,4},{4,0},{8,12},{12,8},{1,5},{5,1},{9,13},{13,9},{2,6},{6,2},{1... | collective-permute-start | bytes 393224 | tf_op jit(solution)/shard_map/ppermute | solution.py:20
  30.5 1.0 %collective-permute-done.1.refs_0_.refs_15_.refs_3_ = bf16[256,512]{1,0:T(8,128)(2,1)S(1)} collective-permute-done((bf16[256,512]{1,0:T(8,128)(2,1)S(1)}, bf16[256,512]{1,0:T(8,128)(2,1)S(1)}, u32[]{:S(2)}, u32[]{:S(2)}) %collective-permute-start.1) | collective-permute-done | bytes 262176 | tf_op jit(solution)/shard_map/ppermute | solution.py:20
  31.5 1.3 %forward.5 = f32[256,128]{1,0:T(8,128)S(1)} custom-call(bf16[256,512]{1,0:T(8,128)(2,1)S(1)} %collective-permute-done.1.refs_0_.refs_15_.refs_3_, bf16[512,512]{1,0:T(8,128)(2,1)S(1)} %get-tuple-element.39.refs_1_.refs_11_.pos_ref, bf16[144,512]{1,0:T(8,128)(2,1)S(1)} %get-tuple-element.42.refs_2_, bf16[512,512]{1,0:T(8,128)(2,1)S(1)} %collective-permute-done.2.refs_3_, ...), custom_call_target="tpu_custom_call" | custom-call | flops 17179869184 | bytes 1048576 | tf_op jit(solution)/shard_map/forward/pallas_call | solution.py:167
  32.8 0.8 %collective-permute-start.11 = (f32[256,128]{1,0:T(8,128)S(1)}, f32[256,128]{1,0:T(8,128)S(1)}, u32[]{:S(2)}, u32[]{:S(2)}) collective-permute-start(f32[256,128]{1,0:T(8,128)S(1)} %forward.5), channel_id=1, source_target_pairs={{0,12},{4,8},{8,4},{12,0},{1,13},{5,9},{9,5},{13,1},{2,14},{6,10},... | collective-permute-start | bytes 393224 | tf_op jit(solution)/shard_map/ppermute | solution.py:20
  33.6 1.0 %collective-permute-done.10.refs_10_ = f32[256,128]{1,0:T(8,128)S(1)} collective-permute-done((f32[256,128]{1,0:T(8,128)S(1)}, f32[256,128]{1,0:T(8,128)S(1)}, u32[]{:S(2)}, u32[]{:S(2)}) %collective-permute-start.10) | collective-permute-done | bytes 131104 | tf_op jit(solution)/shard_map/ppermute | solution.py:20
  34.7 1.9 %collective-permute-start.13 = (bf16[256,512]{1,0:T(8,128)(2,1)S(1)}, bf16[256,512]{1,0:T(8,128)(2,1)S(1)}, u32[]{:S(2)}, u32[]{:S(2)}) collective-permute-start(bf16[256,512]{1,0:T(8,128)(2,1)S(1)} %collective-permute-done.1.refs_0_.refs_15_.refs_3_), channel_id=1, source_target_pairs={{0,2},{1,3},{2,0},{3,1},{4,6},{5,7},{6,4},{7,5},{8,10},{9,11},{10,... | collective-permute-start | bytes 786440 | tf_op jit(solution)/shard_map/ppermute | solution.py:20
  36.5 2.3 %own_rows.1 = (f32[256,128]{1,0:T(8,128)S(1)}, bf16[512,1024]{1,0:T(8,128)(2,1)S(1)}) custom-call(bf16[256,512]{1,0:T(8,128)(2,1)S(1)} %constant_dynamic-slice_fusion.refs_0_.refs_13_.refs_1_, bf16[512,512]{1,0:T(8,128)(2,1)S(1)} %get-tuple-element.39.refs_1_.refs_11_.pos_ref, bf16[144,512]{1,0:T(8,128)(2,1)S(1)} %get-tuple-element.42.refs_2_, ...), custom_call_target="tpu_custom_call" | custom-call | flops 17179869184 | bytes 1048576 | tf_op jit(solution)/shard_map/own_rows/pallas_call | solution.py:214
  38.8 0.9 %collective-permute-done.11.refs_1_ = f32[256,128]{1,0:T(8,128)S(1)} collective-permute-done((f32[256,128]{1,0:T(8,128)S(1)}, f32[256,128]{1,0:T(8,128)S(1)}, u32[]{:S(2)}, u32[]{:S(2)}) %collective-permute-start.11) | collective-permute-done | bytes 131104 | tf_op jit(solution)/shard_map/ppermute | solution.py:20
  39.8 0.7 %collective-permute-start.12 = (bf16[256,128]{1,0:T(8,128)(2,1)S(1)}, bf16[256,128]{1,0:T(8,128)(2,1)S(1)}, u32[]{:S(2)}, u32[]{:S(2)}) collective-permute-start(bf16[256,128]{1,0:T(8,128)(2,1)S(1)} %cotangent.1), channel_id=1, source_target_pairs={{0,4},{4,0},{8,12},{12,8},{1,5},{5,1},{9,13},{13,9},{2,6},{6,2},{1... | collective-permute-start | bytes 196616 | tf_op jit(solution)/shard_map/ppermute | solution.py:20
  40.5 1.5 %collective-permute-done.13.refs_11_.refs_3_ = bf16[256,512]{1,0:T(8,128)(2,1)S(1)} collective-permute-done((bf16[256,512]{1,0:T(8,128)(2,1)S(1)}, bf16[256,512]{1,0:T(8,128)(2,1)S(1)}, u32[]{:S(2)}, u32[]{:S(2)}) %collective-permute-start.13) | collective-permute-done | bytes 262176 | tf_op jit(solution)/shard_map/ppermute | solution.py:20
  42.0 1.6 %collective-permute-start.14 = (bf16[256,128]{1,0:T(8,128)(2,1)S(1)}, bf16[256,128]{1,0:T(8,128)(2,1)S(1)}, u32[]{:S(2)}, u32[]{:S(2)}) collective-permute-start(bf16[256,128]{1,0:T(8,128)(2,1)S(1)} %cotangent.1), channel_id=1, source_target_pairs={{0,2},{1,3},{2,0},{3,1},{4,6},{5,7},{6,4},{7,5},{8,10},{9,11},{10,... | collective-permute-start | bytes 196616 | tf_op jit(solution)/shard_map/ppermute | solution.py:20
  43.7 4.2 %collective-permute-start.16 = (bf16[256,128]{1,0:T(8,128)(2,1)S(1)}, bf16[256,128]{1,0:T(8,128)(2,1)S(1)}, u32[]{:S(2)}, u32[]{:S(2)}) collective-permute-start(bf16[256,128]{1,0:T(8,128)(2,1)S(1)} %cotangent.1), channel_id=1, source_target_pairs={{0,12},{4,8},{8,4},{12,0},{1,13},{5,9},{9,5},{13,1},{2,14},{6,10},... | collective-permute-start | bytes 196616 | tf_op jit(solution)/shard_map/ppermute | solution.py:20
  48.4 4.6 %collective-permute-done.15 = bf16[256,128]{1,0:T(8,128)(2,1)S(1)} collective-permute-done((bf16[256,128]{1,0:T(8,128)(2,1)S(1)}, bf16[256,128]{1,0:T(8,128)(2,1)S(1)}, u32[]{:S(2)}, u32[]{:S(2)}) %collective-permute-start.15) | collective-permute-done | bytes 65568 | tf_op jit(solution)/shard_map/ppermute | solution.py:20
  53.7 2.0 %collective-permute-start.23 = (bf16[768,128]{1,0:T(8,128)(2,1)S(1)}, bf16[768,128]{1,0:T(8,128)(2,1)S(1)}, u32[]{:S(2)}, u32[]{:S(2)}) collective-permute-start(bf16[768,128]{1,0:T(8,128)(2,1)S(1)} %constant_dynamic-update-slice_fusion.2), channel_id=1, source_target_pairs={{0,2},{1,3},{2,0},{3,1},{4,6},{5,7},{6,4},{7,5},{8,10},{9,11},{10,... | collective-permute-start | bytes 589832 | tf_op jit(solution)/shard_map/ppermute | solution.py:20
  55.7 5.7 %backward.2 = (f32[512,512]{1,0:T(8,128)S(1)}, f32[512,128]{1,0:T(8,128)S(1)}, f32[512,128]{1,0:T(8,128)S(1)}, bf16[512,1024]{1,0:T(8,128)(2,1)S(1)}, bf16[512,1024]{1,0:T(8,128)(2,1)S(1)}) custom-call(bf16[512,512]{1,0:T(8,128)(2,1)S(1)} %get-tuple-element.39.refs_1_.refs_11_.pos_ref, bf16[512,128]{1,0:T(8,128)(2,1)S(1)} %get-tuple-element.40.coef_ref, ...), custom_call_target="tpu_custom_call" | custom-call | flops 17179869184 | bytes 1048576 | tf_op jit(solution)/shard_map/backward/pallas_call | solution.py:288
  61.5 1.3 %backward.3 = (f32[512,512]{1,0:T(8,128)S(1)}, f32[512,128]{1,0:T(8,128)S(1)}, f32[512,128]{1,0:T(8,128)S(1)}) custom-call(bf16[512,512]{1,0:T(8,128)(2,1)S(1)} %get-tuple-element.39.refs_1_.refs_11_.pos_ref, bf16[512,128]{1,0:T(8,128)(2,1)S(1)} %get-tuple-element.40.coef_ref, bf16[1,512]{1,0:T(2,128)(2,1)S(1)} %get-tuple-element.41.refs_12_.spread_ref, ...), custom_call_target="tpu_custom_call" | custom-call | flops 1 | bytes 1 | tf_op jit(solution)/shard_map/backward/pallas_call | solution.py:288
  63.1 2.3 %finish.1 = (f32[512,512]{1,0:T(8,128)}, f32[512,128]{1,0:T(8,128)}) custom-call(bf16[512,512]{1,0:T(8,128)(2,1)S(1)} %get-tuple-element.39.refs_1_.refs_11_.pos_ref, bf16[512,128]{1,0:T(8,128)(2,1)S(1)} %get-tuple-element.40.coef_ref, bf16[1,512]{1,0:T(2,128)(2,1)S(1)} %get-tuple-element.41.refs_12_.spread_ref, ...), custom_call_target="tpu_custom_call" | custom-call | flops 1 | bytes 1 | tf_op jit(solution)/shard_map/finish/pallas_call | solution.py:330
  (52 shorter events, 5.4 us)
Async XLA Ops:
  0.6 12.3 %copy-start = (bf16[1024,512]{1,0:T(8,128)(2,1)S(1)}, bf16[1024,512]{1,0:T(8,128)(2,1)}, u32[]{:S(2)}) copy-start(bf16[1024,512]{1,0:T(8,128)(2,1)} %refs_4_.1) | copy-start | bytes 3145732
  0.6 19.7 %collective-permute-start.4 = (bf16[512,512]{1,0:T(8,128)(2,1)}, bf16[512,512]{1,0:T(8,128)(2,1)S(1)}, u32[]{:S(2)}, u32[]{:S(2)}) collective-permute-start(bf16[512,512]{1,0:T(8,128)(2,1)} %pos_ref), channel_id=1, source_target_pairs={{0,2},{1,3},{2,0},{3,1},{4,6},{5,7},{6,4},{7,5},{8,10},{9,11},{10,... | collective-permute-start | bytes 1572872 | tf_op jit(solution)/shard_map/ppermute | solution.py:20
  4.6 14.3 %collective-permute-start.6 = (bf16[256,512]{1,0:T(8,128)(2,1)S(1)}, bf16[256,512]{1,0:T(8,128)(2,1)S(1)}, u32[]{:S(2)}, u32[]{:S(2)}) collective-permute-start(bf16[256,512]{1,0:T(8,128)(2,1)S(1)} %constant_dynamic-slice_fusion.refs_0_.refs_13_.refs_1_), channel_id=1, source_target_pairs={{0,4},{4,0},{8,12},{12,8},{1,5},{5,1},{9,13},{13,9},{2,6},{6,2},{1... | collective-permute-start | bytes 786440 | tf_op jit(solution)/shard_map/ppermute | solution.py:20
  6.3 14.0 %collective-permute-start = (bf16[256,512]{1,0:T(8,128)(2,1)S(1)}, bf16[256,512]{1,0:T(8,128)(2,1)S(1)}, u32[]{:S(2)}, u32[]{:S(2)}) collective-permute-start(bf16[256,512]{1,0:T(8,128)(2,1)S(1)} %constant_dynamic-slice_fusion.refs_0_.refs_13_.refs_1_), channel_id=1, source_target_pairs={{0,8},{4,12},{8,0},{12,4},{1,9},{5,13},{9,1},{13,5},{2,10},{6,14},... | collective-permute-start | bytes 786440 | tf_op jit(solution)/shard_map/ppermute | solution.py:20
  9.5 1.0 %copy-start.1 = (bf16[512,512]{1,0:T(8,128)(2,1)S(1)}, bf16[512,512]{1,0:T(8,128)(2,1)}, u32[]{:S(2)}) copy-start(bf16[512,512]{1,0:T(8,128)(2,1)} %pos_ref) | copy-start | bytes 1572868
  10.6 0.9 %copy-start.5 = (bf16[512,128]{1,0:T(8,128)(2,1)S(1)}, bf16[512,128]{1,0:T(8,128)(2,1)}, u32[]{:S(2)}) copy-start(bf16[512,128]{1,0:T(8,128)(2,1)} %coef_ref.1) | copy-start | bytes 393220
  11.5 0.7 %copy-start.6 = (f32[128]{0:T(128)S(1)}, f32[128]{0:T(128)}, u32[]{:S(2)}) copy-start(f32[128]{0:T(128)} %param.10) | copy-start | bytes 1540
  12.3 6.6 %copy-start.2 = (bf16[512,512]{1,0:T(8,128)(2,1)S(1)}, bf16[512,512]{1,0:T(8,128)(2,1)}, u32[]{:S(2)}) copy-start(bf16[512,512]{1,0:T(8,128)(2,1)} %pos_ref) | copy-start | bytes 1572868
  12.4 6.6 %collective-permute-start.5 = (bf16[144,512]{1,0:T(8,128)(2,1)S(1)}, bf16[144,512]{1,0:T(8,128)(2,1)S(1)}, u32[]{:S(2)}, u32[]{:S(2)}) collective-permute-start(bf16[144,512]{1,0:T(8,128)(2,1)S(1)} %get-tuple-element.42.refs_2_), channel_id=1, source_target_pairs={{0,2},{1,3},{2,0},{3,1},{4,6},{5,7},{6,4},{7,5},{8,10},{9,11},{10,... | collective-permute-start | bytes 442376 | tf_op jit(solution)/shard_map/ppermute | solution.py:20
  13.0 6.0 %collective-permute-start.3 = (bf16[144,512]{1,0:T(8,128)(2,1)S(1)}, bf16[144,512]{1,0:T(8,128)(2,1)S(1)}, u32[]{:S(2)}, u32[]{:S(2)}) collective-permute-start(bf16[144,512]{1,0:T(8,128)(2,1)S(1)} %get-tuple-element.42.refs_2_), channel_id=1, source_target_pairs={{0,1},{1,0},{2,3},{3,2},{4,5},{5,4},{6,7},{7,6},{8,9},{9,8},{10,11... | collective-permute-start | bytes 442376 | tf_op jit(solution)/shard_map/ppermute | solution.py:20
  13.0 1.0 %copy-start.3 = (f32[1024,128]{1,0:T(8,128)S(1)}, f32[1024,128]{1,0:T(8,128)}, u32[]{:S(2)}) copy-start(f32[1024,128]{1,0:T(8,128)} %refs_0_.1) | copy-start | bytes 1572868
  14.0 1.0 %copy-start.4 = (f32[1024,128]{1,0:T(8,128)S(1)}, f32[1024,128]{1,0:T(8,128)}, u32[]{:S(2)}) copy-start(f32[1024,128]{1,0:T(8,128)} %refs_1_.1) | copy-start | bytes 1572868
  18.9 4.6 %collective-permute-start.2 = (bf16[512,512]{1,0:T(8,128)(2,1)S(1)}, bf16[512,512]{1,0:T(8,128)(2,1)S(1)}, u32[]{:S(2)}, u32[]{:S(2)}) collective-permute-start(bf16[512,512]{1,0:T(8,128)(2,1)S(1)} %copy-done.2), channel_id=1, source_target_pairs={{0,1},{1,0},{2,3},{3,2},{4,5},{5,4},{6,7},{7,6},{8,9},{9,8},{10,11... | collective-permute-start | bytes 1572872 | tf_op jit(solution)/shard_map/ppermute | solution.py:20
  20.3 3.3 %collective-permute-start.7 = (bf16[512,512]{1,0:T(8,128)(2,1)S(1)}, bf16[512,512]{1,0:T(8,128)(2,1)S(1)}, u32[]{:S(2)}, u32[]{:S(2)}) collective-permute-start(bf16[512,512]{1,0:T(8,128)(2,1)S(1)} %collective-permute-done.4.refs_5_), channel_id=1, source_target_pairs={{0,1},{1,0},{2,3},{3,2},{4,5},{5,4},{6,7},{7,6},{8,9},{9,8},{10,11... | collective-permute-start | bytes 1572872 | tf_op jit(solution)/shard_map/ppermute | solution.py:20
  20.3 2.1 %collective-permute-start.8 = (bf16[144,512]{1,0:T(8,128)(2,1)S(1)}, bf16[144,512]{1,0:T(8,128)(2,1)S(1)}, u32[]{:S(2)}, u32[]{:S(2)}) collective-permute-start(bf16[144,512]{1,0:T(8,128)(2,1)S(1)} %collective-permute-done.5.refs_6_), channel_id=1, source_target_pairs={{0,1},{1,0},{2,3},{3,2},{4,5},{5,4},{6,7},{7,6},{8,9},{9,8},{10,11... | collective-permute-start | bytes 442376 | tf_op jit(solution)/shard_map/ppermute | solution.py:20
  20.8 10.7 %collective-permute-start.1 = (bf16[256,512]{1,0:T(8,128)(2,1)S(1)}, bf16[256,512]{1,0:T(8,128)(2,1)S(1)}, u32[]{:S(2)}, u32[]{:S(2)}) collective-permute-start(bf16[256,512]{1,0:T(8,128)(2,1)S(1)} %collective-permute-done.refs_0_), channel_id=1, source_target_pairs={{0,4},{4,0},{8,12},{12,8},{1,5},{5,1},{9,13},{13,9},{2,6},{6,2},{1... | collective-permute-start | bytes 786440 | tf_op jit(solution)/shard_map/ppermute | solution.py:20
  22.4 25.4 %collective-permute-start.20 = (bf16[512,512]{1,0:T(8,128)(2,1)S(1)}, bf16[512,512]{1,0:T(8,128)(2,1)S(1)}, u32[]{:S(2)}, u32[]{:S(2)}) collective-permute-start(bf16[512,512]{1,0:T(8,128)(2,1)S(1)} %constant_dynamic-update-slice_fusion.refs_14_.refs_2_), channel_id=1, source_target_pairs={{0,2},{1,3},{2,0},{3,1},{4,6},{5,7},{6,4},{7,5},{8,10},{9,11},{10,... | collective-permute-start | bytes 1572872 | tf_op jit(solution)/shard_map/ppermute | solution.py:20
  24.9 9.8 %collective-permute-start.9 = (f32[256,128]{1,0:T(8,128)S(1)}, f32[256,128]{1,0:T(8,128)S(1)}, u32[]{:S(2)}, u32[]{:S(2)}) collective-permute-start(f32[256,128]{1,0:T(8,128)S(1)} %forward.3), channel_id=1, source_target_pairs={{0,8},{4,12},{8,0},{12,4},{1,9},{5,13},{9,1},{13,5},{2,10},{6,14},... | collective-permute-start | bytes 393224 | tf_op jit(solution)/shard_map/ppermute | solution.py:20
  28.8 5.8 %collective-permute-start.10 = (f32[256,128]{1,0:T(8,128)S(1)}, f32[256,128]{1,0:T(8,128)S(1)}, u32[]{:S(2)}, u32[]{:S(2)}) collective-permute-start(f32[256,128]{1,0:T(8,128)S(1)} %forward.4), channel_id=1, source_target_pairs={{0,4},{4,0},{8,12},{12,8},{1,5},{5,1},{9,13},{13,9},{2,6},{6,2},{1... | collective-permute-start | bytes 393224 | tf_op jit(solution)/shard_map/ppermute | solution.py:20
  32.8 6.8 %collective-permute-start.11 = (f32[256,128]{1,0:T(8,128)S(1)}, f32[256,128]{1,0:T(8,128)S(1)}, u32[]{:S(2)}, u32[]{:S(2)}) collective-permute-start(f32[256,128]{1,0:T(8,128)S(1)} %forward.5), channel_id=1, source_target_pairs={{0,12},{4,8},{8,4},{12,0},{1,13},{5,9},{9,5},{13,1},{2,14},{6,10},... | collective-permute-start | bytes 393224 | tf_op jit(solution)/shard_map/ppermute | solution.py:20
  34.7 7.4 %collective-permute-start.13 = (bf16[256,512]{1,0:T(8,128)(2,1)S(1)}, bf16[256,512]{1,0:T(8,128)(2,1)S(1)}, u32[]{:S(2)}, u32[]{:S(2)}) collective-permute-start(bf16[256,512]{1,0:T(8,128)(2,1)S(1)} %collective-permute-done.1.refs_0_.refs_15_.refs_3_), channel_id=1, source_target_pairs={{0,2},{1,3},{2,0},{3,1},{4,6},{5,7},{6,4},{7,5},{8,10},{9,11},{10,... | collective-permute-start | bytes 786440 | tf_op jit(solution)/shard_map/ppermute | solution.py:20
  39.8 8.1 %collective-permute-start.12 = (bf16[256,128]{1,0:T(8,128)(2,1)S(1)}, bf16[256,128]{1,0:T(8,128)(2,1)S(1)}, u32[]{:S(2)}, u32[]{:S(2)}) collective-permute-start(bf16[256,128]{1,0:T(8,128)(2,1)S(1)} %cotangent.1), channel_id=1, source_target_pairs={{0,4},{4,0},{8,12},{12,8},{1,5},{5,1},{9,13},{13,9},{2,6},{6,2},{1... | collective-permute-start | bytes 196616 | tf_op jit(solution)/shard_map/ppermute | solution.py:20
  42.0 6.3 %collective-permute-start.14 = (bf16[256,128]{1,0:T(8,128)(2,1)S(1)}, bf16[256,128]{1,0:T(8,128)(2,1)S(1)}, u32[]{:S(2)}, u32[]{:S(2)}) collective-permute-start(bf16[256,128]{1,0:T(8,128)(2,1)S(1)} %cotangent.1), channel_id=1, source_target_pairs={{0,2},{1,3},{2,0},{3,1},{4,6},{5,7},{6,4},{7,5},{8,10},{9,11},{10,... | collective-permute-start | bytes 196616 | tf_op jit(solution)/shard_map/ppermute | solution.py:20
  43.7 9.3 %collective-permute-start.16 = (bf16[256,128]{1,0:T(8,128)(2,1)S(1)}, bf16[256,128]{1,0:T(8,128)(2,1)S(1)}, u32[]{:S(2)}, u32[]{:S(2)}) collective-permute-start(bf16[256,128]{1,0:T(8,128)(2,1)S(1)} %cotangent.1), channel_id=1, source_target_pairs={{0,12},{4,8},{8,4},{12,0},{1,13},{5,9},{9,5},{13,1},{2,14},{6,10},... | collective-permute-start | bytes 196616 | tf_op jit(solution)/shard_map/ppermute | solution.py:20
  47.8 5.2 %collective-permute-start.15 = (bf16[256,128]{1,0:T(8,128)(2,1)S(1)}, bf16[256,128]{1,0:T(8,128)(2,1)S(1)}, u32[]{:S(2)}, u32[]{:S(2)}) collective-permute-start(bf16[256,128]{1,0:T(8,128)(2,1)S(1)} %cotangent.1), channel_id=1, source_target_pairs={{0,8},{4,12},{8,0},{12,4},{1,9},{5,13},{9,1},{13,5},{2,10},{6,14},... | collective-permute-start | bytes 196616 | tf_op jit(solution)/shard_map/ppermute | solution.py:20
  47.8 5.9 %collective-permute-start.18 = (bf16[256,512]{1,0:T(8,128)(2,1)S(1)}, bf16[256,512]{1,0:T(8,128)(2,1)S(1)}, u32[]{:S(2)}, u32[]{:S(2)}) collective-permute-start(bf16[256,512]{1,0:T(8,128)(2,1)S(1)} %collective-permute-done.1.refs_0_.refs_15_.refs_3_), channel_id=1, source_target_pairs={{0,1},{1,0},{2,3},{3,2},{4,5},{5,4},{6,7},{7,6},{8,9},{9,8},{10,11... | collective-permute-start | bytes 786440 | tf_op jit(solution)/shard_map/ppermute | solution.py:20
  47.8 7.9 %collective-permute-start.17 = (bf16[512,512]{1,0:T(8,128)(2,1)S(1)}, bf16[512,512]{1,0:T(8,128)(2,1)S(1)}, u32[]{:S(2)}, u32[]{:S(2)}) collective-permute-start(bf16[512,512]{1,0:T(8,128)(2,1)S(1)} %constant_dynamic-update-slice_fusion.refs_14_.refs_2_), channel_id=1, source_target_pairs={{0,1},{1,0},{2,3},{3,2},{4,5},{5,4},{6,7},{7,6},{8,9},{9,8},{10,11... | collective-permute-start | bytes 1572872 | tf_op jit(solution)/shard_map/ppermute | solution.py:20
  48.3 7.4 %collective-permute-start.21 = (bf16[512,512]{1,0:T(8,128)(2,1)S(1)}, bf16[512,512]{1,0:T(8,128)(2,1)S(1)}, u32[]{:S(2)}, u32[]{:S(2)}) collective-permute-start(bf16[512,512]{1,0:T(8,128)(2,1)S(1)} %collective-permute-done.20.refs_10_.refs_2_), channel_id=1, source_target_pairs={{0,1},{1,0},{2,3},{3,2},{4,5},{5,4},{6,7},{7,6},{8,9},{9,8},{10,11... | collective-permute-start | bytes 1572872 | tf_op jit(solution)/shard_map/ppermute | solution.py:20
  53.0 2.7 %collective-permute-start.22 = (bf16[256,512]{1,0:T(8,128)(2,1)S(1)}, bf16[256,512]{1,0:T(8,128)(2,1)S(1)}, u32[]{:S(2)}, u32[]{:S(2)}) collective-permute-start(bf16[256,512]{1,0:T(8,128)(2,1)S(1)} %collective-permute-done.13.refs_11_.refs_3_), channel_id=1, source_target_pairs={{0,1},{1,0},{2,3},{3,2},{4,5},{5,4},{6,7},{7,6},{8,9},{9,8},{10,11... | collective-permute-start | bytes 786440 | tf_op jit(solution)/shard_map/ppermute | solution.py:20
  53.1 2.6 %collective-permute-start.19 = (bf16[1024,128]{1,0:T(8,128)(2,1)S(1)}, bf16[1024,128]{1,0:T(8,128)(2,1)S(1)}, u32[]{:S(2)}, u32[]{:S(2)}) collective-permute-start(bf16[1024,128]{1,0:T(8,128)(2,1)S(1)} %pad_maximum_fusion.refs_4_), channel_id=1, source_target_pairs={{0,1},{1,0},{2,3},{3,2},{4,5},{5,4},{6,7},{7,6},{8,9},{9,8},{10,11... | collective-permute-start | bytes 786440 | tf_op jit(solution)/shard_map/ppermute | solution.py:20
  53.7 7.7 %collective-permute-start.23 = (bf16[768,128]{1,0:T(8,128)(2,1)S(1)}, bf16[768,128]{1,0:T(8,128)(2,1)S(1)}, u32[]{:S(2)}, u32[]{:S(2)}) collective-permute-start(bf16[768,128]{1,0:T(8,128)(2,1)S(1)} %constant_dynamic-update-slice_fusion.2), channel_id=1, source_target_pairs={{0,2},{1,3},{2,0},{3,1},{4,6},{5,7},{6,4},{7,5},{8,10},{9,11},{10,... | collective-permute-start | bytes 589832 | tf_op jit(solution)/shard_map/ppermute | solution.py:20
  61.5 1.6 %collective-permute-start.24 = (bf16[1024,128]{1,0:T(8,128)(2,1)S(1)}, bf16[1024,128]{1,0:T(8,128)(2,1)S(1)}, u32[]{:S(2)}, u32[]{:S(2)}) collective-permute-start(bf16[1024,128]{1,0:T(8,128)(2,1)S(1)} %constant_dynamic-update-slice_fusion.5.refs_4_), channel_id=1, source_target_pairs={{0,1},{1,0},{2,3},{3,2},{4,5},{5,4},{6,7},{7,6},{8,9},{9,8},{10,11... | collective-permute-start | bytes 786440 | tf_op jit(solution)/shard_map/ppermute | solution.py:20

commit v18 on v16

--- a/solution.py
+++ b/solution.py
@@ -300,7 +300,7 @@
 def finish(center_pos, coefficients, spread, group, before):
     (n, out_width), in_width = coefficients.shape, center_pos.shape[1]
     kernel, xs, cot = group
-    step = min(n, 256)
+    step = min(n, 128)
 
     def body(pos_ref, coef_ref, spread_ref, kernel_ref, cot_ref, *refs):
         x_refs, refs = refs[: len(xs)], refs[len(xs) :]

time: 63.8 us -> 63.7 us (level)
  no operation moved by 1% of the time
where the time goes in v18:
time: 63.7 us; the launch traced here: 63.4 us
  starting transfers between devices  25.3 us (40%)
  Pallas kernels  16.3 us (26%)
  waiting for transfers between devices  14.5 us (23%)
  local copies, waits for them, and re-layouts  6.44 us (10%)
  between operations  0.82 us (1%)
    ppermute x25, starting transfers between devices, swap(): return lax.ppermute(a, axis, [(i, i ^ d) for i in range(size)])  25.3 us
    ppermute x25, waiting for transfers between devices, swap(): return lax.ppermute(a, axis, [(i, i ^ d) for i in range(size)])  14.5 us
    pallas_call x2, Pallas kernels, backward(): pl.pallas_call(body, out_shape=tuple((jax.ShapeDtypeStruct((n, width), F3...  6.08 us
    unnamed x18, local copies, waits for them, and re-layouts  4.74 us
    pallas_call x3, Pallas kernels, forward(): pl.pallas_call(body, out_shape=tuple((jax.ShapeDtypeStruct((count, out_wi...  3.95 us
    pallas_call x1, Pallas kernels, own_rows(): pl.pallas_call(body, out_shape=(jax.ShapeDtypeStruct((rows.shape[0], out_...  2.28 us
    pallas_call x1, Pallas kernels, finish(): pl.pallas_call(body, out_shape=tuple((jax.ShapeDtypeStruct((n, width), F3...  2.24 us
  transfers between devices with their start and end apart: 25, of which 11 were waited for; matrix products, arithmetic and copies ran while one was open for 3% of the time, Pallas kernels for 22%

profile of v18, /device:TPU:0, one launch (start us, length us, event | category | flops | bytes accessed | tf_op | source)
XLA Modules:
  0.0 63.4 jit_solution(2299513538643739586)
XLA Ops:
  0.6 3.0 %collective-permute-start.4 = (bf16[512,512]{1,0:T(8,128)(2,1)}, bf16[512,512]{1,0:T(8,128)(2,1)S(1)}, u32[]{:S(2)}, u32[]{:S(2)}) collective-permute-start(bf16[512,512]{1,0:T(8,128)(2,1)} %pos_ref), channel_id=1, source_target_pairs={{0,2},{1,3},{2,0},{3,1},{4,6},{5,7},{6,4},{7,5},{8,10},{9,11},{10,... | collective-permute-start | bytes 1572872 | tf_op jit(solution)/shard_map/ppermute | solution.py:20
  3.6 1.0 %constant_dynamic-slice_fusion.refs_0_.refs_13_.refs_1_ = bf16[256,512]{1,0:T(8,128)(2,1)S(1)} fusion(bf16[1024,512]{1,0:T(8,128)(2,1)} %refs_4_.1, s32[]{:T(128)S(6)} %select_n.3), kind=kLoop, calls=%fused_computation.8 | loop fusion | bytes 524292 | tf_op jit(solution)/shard_map/dynamic_slice | solution.py:354
  4.6 1.6 %collective-permute-start.6 = (bf16[256,512]{1,0:T(8,128)(2,1)S(1)}, bf16[256,512]{1,0:T(8,128)(2,1)S(1)}, u32[]{:S(2)}, u32[]{:S(2)}) collective-permute-start(bf16[256,512]{1,0:T(8,128)(2,1)S(1)} %constant_dynamic-slice_fusion.refs_0_.refs_13_.refs_1_), channel_id=1, source_target_pairs={{0,4},{4,0},{8,12},{12,8},{1,5},{5,1},{9,13},{13,9},{2,6},{6,2},{1... | collective-permute-start | bytes 786440 | tf_op jit(solution)/shard_map/ppermute | solution.py:20
  6.3 2.6 %collective-permute-start = (bf16[256,512]{1,0:T(8,128)(2,1)S(1)}, bf16[256,512]{1,0:T(8,128)(2,1)S(1)}, u32[]{:S(2)}, u32[]{:S(2)}) collective-permute-start(bf16[256,512]{1,0:T(8,128)(2,1)S(1)} %constant_dynamic-slice_fusion.refs_0_.refs_13_.refs_1_), channel_id=1, source_target_pairs={{0,8},{4,12},{8,0},{12,4},{1,9},{5,13},{9,1},{13,5},{2,10},{6,14},... | collective-permute-start | bytes 786440 | tf_op jit(solution)/shard_map/ppermute | solution.py:20
  9.5 1.0 %copy-done.1 = bf16[512,512]{1,0:T(8,128)(2,1)S(1)} copy-done((bf16[512,512]{1,0:T(8,128)(2,1)S(1)}, bf16[512,512]{1,0:T(8,128)(2,1)}, u32[]{:S(2)}) %copy-start.1) | copy-done | bytes 524312
  10.6 0.9 %copy-done.5 = bf16[512,128]{1,0:T(8,128)(2,1)S(1)} copy-done((bf16[512,128]{1,0:T(8,128)(2,1)S(1)}, bf16[512,128]{1,0:T(8,128)(2,1)}, u32[]{:S(2)}) %copy-start.5) | copy-done | bytes 131096
  13.0 1.0 %copy-done.3 = f32[1024,128]{1,0:T(8,128)S(1)} copy-done((f32[1024,128]{1,0:T(8,128)S(1)}, f32[1024,128]{1,0:T(8,128)}, u32[]{:S(2)}) %copy-start.3) | copy-done | bytes 524312
  14.0 1.0 %copy-done.4 = f32[1024,128]{1,0:T(8,128)S(1)} copy-done((f32[1024,128]{1,0:T(8,128)S(1)}, f32[1024,128]{1,0:T(8,128)}, u32[]{:S(2)}) %copy-start.4) | copy-done | bytes 524312
  15.5 3.5 %collective-permute-done.5.refs_6_ = bf16[144,512]{1,0:T(8,128)(2,1)S(1)} collective-permute-done((bf16[144,512]{1,0:T(8,128)(2,1)S(1)}, bf16[144,512]{1,0:T(8,128)(2,1)S(1)}, u32[]{:S(2)}, u32[]{:S(2)}) %collective-permute-start.5) | collective-permute-done | bytes 147488 | tf_op jit(solution)/shard_map/ppermute | solution.py:20
  19.0 1.3 %collective-permute-done.refs_0_ = bf16[256,512]{1,0:T(8,128)(2,1)S(1)} collective-permute-done((bf16[256,512]{1,0:T(8,128)(2,1)S(1)}, bf16[256,512]{1,0:T(8,128)(2,1)S(1)}, u32[]{:S(2)}, u32[]{:S(2)}) %collective-permute-start) | collective-permute-done | bytes 262176 | tf_op jit(solution)/shard_map/ppermute | solution.py:20
  21.5 0.9 %collective-permute-done.8.refs_8_ = bf16[144,512]{1,0:T(8,128)(2,1)S(1)} collective-permute-done((bf16[144,512]{1,0:T(8,128)(2,1)S(1)}, bf16[144,512]{1,0:T(8,128)(2,1)S(1)}, u32[]{:S(2)}, u32[]{:S(2)}) %collective-permute-start.8) | collective-permute-done | bytes 147488 | tf_op jit(solution)/shard_map/ppermute | solution.py:20
  22.4 1.1 %collective-permute-start.16 = (bf16[512,512]{1,0:T(8,128)(2,1)S(1)}, bf16[512,512]{1,0:T(8,128)(2,1)S(1)}, u32[]{:S(2)}, u32[]{:S(2)}) collective-permute-start(bf16[512,512]{1,0:T(8,128)(2,1)S(1)} %constant_dynamic-update-slice_fusion.refs_14_.refs_2_), channel_id=1, source_target_pairs={{0,2},{1,3},{2,0},{3,1},{4,6},{5,7},{6,4},{7,5},{8,10},{9,11},{10,... | collective-permute-start | bytes 1572872 | tf_op jit(solution)/shard_map/ppermute | solution.py:20
  23.6 1.3 %forward.3 = f32[256,128]{1,0:T(8,128)S(1)} custom-call(bf16[256,512]{1,0:T(8,128)(2,1)S(1)} %collective-permute-done.refs_0_, bf16[512,512]{1,0:T(8,128)(2,1)S(1)} %get-tuple-element.39.refs_1_.refs_11_.pos_ref, bf16[144,512]{1,0:T(8,128)(2,1)S(1)} %get-tuple-element.42.refs_2_, bf16[512,512]{1,0:T(8,128)(2,1)S(1)} %collective-permute-done.2.refs_3_, ...), custom_call_target="tpu_custom_call" | custom-call | flops 1 | bytes 1 | tf_op jit(solution)/shard_map/forward/pallas_call | solution.py:167
  24.9 2.7 %collective-permute-start.9 = (f32[256,128]{1,0:T(8,128)S(1)}, f32[256,128]{1,0:T(8,128)S(1)}, u32[]{:S(2)}, u32[]{:S(2)}) collective-permute-start(f32[256,128]{1,0:T(8,128)S(1)} %forward.3), channel_id=1, source_target_pairs={{0,8},{4,12},{8,0},{12,4},{1,9},{5,13},{9,1},{13,5},{2,10},{6,14},... | collective-permute-start | bytes 393224 | tf_op jit(solution)/shard_map/ppermute | solution.py:20
  27.5 1.3 %forward.4 = f32[256,128]{1,0:T(8,128)S(1)} custom-call(bf16[256,512]{1,0:T(8,128)(2,1)S(1)} %collective-permute-done.6.refs_0_, bf16[512,512]{1,0:T(8,128)(2,1)S(1)} %get-tuple-element.39.refs_1_.refs_11_.pos_ref, bf16[144,512]{1,0:T(8,128)(2,1)S(1)} %get-tuple-element.42.refs_2_, bf16[512,512]{1,0:T(8,128)(2,1)S(1)} %collective-permute-done.2.refs_3_, ...), custom_call_target="tpu_custom_call" | custom-call | flops 17179869184 | bytes 1048576 | tf_op jit(solution)/shard_map/forward/pallas_call | solution.py:167
  28.9 1.6 %collective-permute-start.10 = (f32[256,128]{1,0:T(8,128)S(1)}, f32[256,128]{1,0:T(8,128)S(1)}, u32[]{:S(2)}, u32[]{:S(2)}) collective-permute-start(f32[256,128]{1,0:T(8,128)S(1)} %forward.4), channel_id=1, source_target_pairs={{0,4},{4,0},{8,12},{12,8},{1,5},{5,1},{9,13},{13,9},{2,6},{6,2},{1... | collective-permute-start | bytes 393224 | tf_op jit(solution)/shard_map/ppermute | solution.py:20
  30.5 1.0 %collective-permute-done.1.refs_0_.refs_15_.refs_3_ = bf16[256,512]{1,0:T(8,128)(2,1)S(1)} collective-permute-done((bf16[256,512]{1,0:T(8,128)(2,1)S(1)}, bf16[256,512]{1,0:T(8,128)(2,1)S(1)}, u32[]{:S(2)}, u32[]{:S(2)}) %collective-permute-start.1) | collective-permute-done | bytes 262176 | tf_op jit(solution)/shard_map/ppermute | solution.py:20
  31.5 1.3 %forward.5 = f32[256,128]{1,0:T(8,128)S(1)} custom-call(bf16[256,512]{1,0:T(8,128)(2,1)S(1)} %collective-permute-done.1.refs_0_.refs_15_.refs_3_, bf16[512,512]{1,0:T(8,128)(2,1)S(1)} %get-tuple-element.39.refs_1_.refs_11_.pos_ref, bf16[144,512]{1,0:T(8,128)(2,1)S(1)} %get-tuple-element.42.refs_2_, bf16[512,512]{1,0:T(8,128)(2,1)S(1)} %collective-permute-done.2.refs_3_, ...), custom_call_target="tpu_custom_call" | custom-call | flops 17179869184 | bytes 1048576 | tf_op jit(solution)/shard_map/forward/pallas_call | solution.py:167
  32.8 0.8 %collective-permute-start.11 = (f32[256,128]{1,0:T(8,128)S(1)}, f32[256,128]{1,0:T(8,128)S(1)}, u32[]{:S(2)}, u32[]{:S(2)}) collective-permute-start(f32[256,128]{1,0:T(8,128)S(1)} %forward.5), channel_id=1, source_target_pairs={{0,12},{4,8},{8,4},{12,0},{1,13},{5,9},{9,5},{13,1},{2,14},{6,10},... | collective-permute-start | bytes 393224 | tf_op jit(solution)/shard_map/ppermute | solution.py:20
  33.6 1.0 %collective-permute-done.10.refs_10_ = f32[256,128]{1,0:T(8,128)S(1)} collective-permute-done((f32[256,128]{1,0:T(8,128)S(1)}, f32[256,128]{1,0:T(8,128)S(1)}, u32[]{:S(2)}, u32[]{:S(2)}) %collective-permute-start.10) | collective-permute-done | bytes 131104 | tf_op jit(solution)/shard_map/ppermute | solution.py:20
  34.7 1.9 %collective-permute-start.13 = (bf16[256,512]{1,0:T(8,128)(2,1)S(1)}, bf16[256,512]{1,0:T(8,128)(2,1)S(1)}, u32[]{:S(2)}, u32[]{:S(2)}) collective-permute-start(bf16[256,512]{1,0:T(8,128)(2,1)S(1)} %collective-permute-done.1.refs_0_.refs_15_.refs_3_), channel_id=1, source_target_pairs={{0,2},{1,3},{2,0},{3,1},{4,6},{5,7},{6,4},{7,5},{8,10},{9,11},{10,... | collective-permute-start | bytes 786440 | tf_op jit(solution)/shard_map/ppermute | solution.py:20
  36.5 2.3 %own_rows.1 = (f32[256,128]{1,0:T(8,128)S(1)}, bf16[512,1024]{1,0:T(8,128)(2,1)S(1)}) custom-call(bf16[256,512]{1,0:T(8,128)(2,1)S(1)} %constant_dynamic-slice_fusion.refs_0_.refs_13_.refs_1_, bf16[512,512]{1,0:T(8,128)(2,1)S(1)} %get-tuple-element.39.refs_1_.refs_11_.pos_ref, bf16[144,512]{1,0:T(8,128)(2,1)S(1)} %get-tuple-element.42.refs_2_, ...), custom_call_target="tpu_custom_call" | custom-call | flops 17179869184 | bytes 1048576 | tf_op jit(solution)/shard_map/own_rows/pallas_call | solution.py:214
  38.8 0.9 %collective-permute-done.11.refs_1_ = f32[256,128]{1,0:T(8,128)S(1)} collective-permute-done((f32[256,128]{1,0:T(8,128)S(1)}, f32[256,128]{1,0:T(8,128)S(1)}, u32[]{:S(2)}, u32[]{:S(2)}) %collective-permute-start.11) | collective-permute-done | bytes 131104 | tf_op jit(solution)/shard_map/ppermute | solution.py:20
  39.8 2.6 %collective-permute-start.15 = (bf16[256,128]{1,0:T(8,128)(2,1)S(1)}, bf16[256,128]{1,0:T(8,128)(2,1)S(1)}, u32[]{:S(2)}, u32[]{:S(2)}) collective-permute-start(bf16[256,128]{1,0:T(8,128)(2,1)S(1)} %cotangent.1), channel_id=1, source_target_pairs={{0,8},{4,12},{8,0},{12,4},{1,9},{5,13},{9,1},{13,5},{2,10},{6,14},... | collective-permute-start | bytes 196616 | tf_op jit(solution)/shard_map/ppermute | solution.py:20
  42.4 1.4 %collective-permute-start.12 = (bf16[256,128]{1,0:T(8,128)(2,1)S(1)}, bf16[256,128]{1,0:T(8,128)(2,1)S(1)}, u32[]{:S(2)}, u32[]{:S(2)}) collective-permute-start(bf16[256,128]{1,0:T(8,128)(2,1)S(1)} %cotangent.1), channel_id=1, source_target_pairs={{0,4},{4,0},{8,12},{12,8},{1,5},{5,1},{9,13},{13,9},{2,6},{6,2},{1... | collective-permute-start | bytes 196616 | tf_op jit(solution)/shard_map/ppermute | solution.py:20
  43.8 2.0 %collective-permute-start.14 = (bf16[256,128]{1,0:T(8,128)(2,1)S(1)}, bf16[256,128]{1,0:T(8,128)(2,1)S(1)}, u32[]{:S(2)}, u32[]{:S(2)}) collective-permute-start(bf16[256,128]{1,0:T(8,128)(2,1)S(1)} %cotangent.1), channel_id=1, source_target_pairs={{0,2},{1,3},{2,0},{3,1},{4,6},{5,7},{6,4},{7,5},{8,10},{9,11},{10,... | collective-permute-start | bytes 196616 | tf_op jit(solution)/shard_map/ppermute | solution.py:20
  46.3 1.1 %own_kernel.1.refs_0_ = bf16[512,1024]{1,0:T(8,128)(2,1)S(1)} custom-call(bf16[512,512]{1,0:T(8,128)(2,1)S(1)} %get-tuple-element.39.refs_1_.refs_11_.pos_ref, bf16[1,512]{1,0:T(2,128)(2,1)S(1)} %get-tuple-element.41.refs_12_.spread_ref, bf16[256,512]{1,0:T(8,128)(2,1)S(1)} %get-tuple-element.56.refs_0_.refs_1_, ...), custom_call_target="tpu_custom_call" | custom-call | flops 1 | bytes 1 | tf_op jit(solution)/shard_map/own_kernel/pallas_call | solution.py:185
  48.1 3.9 %collective-permute-done.17 = bf16[256,128]{1,0:T(8,128)(2,1)S(1)} collective-permute-done((bf16[256,128]{1,0:T(8,128)(2,1)S(1)}, bf16[256,128]{1,0:T(8,128)(2,1)S(1)}, u32[]{:S(2)}, u32[]{:S(2)}) %collective-permute-start.17) | collective-permute-done | bytes 65568 | tf_op jit(solution)/shard_map/ppermute | solution.py:20
  54.0 4.8 %backward.2 = (f32[512,512]{1,0:T(8,128)S(1)}, f32[512,128]{1,0:T(8,128)S(1)}, f32[512,128]{1,0:T(8,128)S(1)}, bf16[512,1024]{1,0:T(8,128)(2,1)S(1)}) custom-call(bf16[512,512]{1,0:T(8,128)(2,1)S(1)} %get-tuple-element.39.refs_1_.refs_11_.pos_ref, bf16[512,128]{1,0:T(8,128)(2,1)S(1)} %get-tuple-element.40.coef_ref, ...), custom_call_target="tpu_custom_call" | custom-call | flops 17179869184 | bytes 1048576 | tf_op jit(solution)/shard_map/backward/pallas_call | solution.py:288
  58.7 0.8 %collective-permute-done.23 = bf16[768,128]{1,0:T(8,128)(2,1)S(1)} collective-permute-done((bf16[768,128]{1,0:T(8,128)(2,1)S(1)}, bf16[768,128]{1,0:T(8,128)(2,1)S(1)}, u32[]{:S(2)}, u32[]{:S(2)}) %collective-permute-start.23) | collective-permute-done | bytes 196640 | tf_op jit(solution)/shard_map/ppermute | solution.py:20
  59.6 1.3 %backward.3 = (f32[512,512]{1,0:T(8,128)S(1)}, f32[512,128]{1,0:T(8,128)S(1)}, f32[512,128]{1,0:T(8,128)S(1)}) custom-call(bf16[512,512]{1,0:T(8,128)(2,1)S(1)} %get-tuple-element.39.refs_1_.refs_11_.pos_ref, bf16[512,128]{1,0:T(8,128)(2,1)S(1)} %get-tuple-element.40.coef_ref, bf16[1,512]{1,0:T(2,128)(2,1)S(1)} %get-tuple-element.41.refs_12_.spread_ref, ...), custom_call_target="tpu_custom_call" | custom-call | flops 1 | bytes 1 | tf_op jit(solution)/shard_map/backward/pallas_call | solution.py:288
  61.2 2.2 %finish.1 = (f32[512,512]{1,0:T(8,128)}, f32[512,128]{1,0:T(8,128)}) custom-call(bf16[512,512]{1,0:T(8,128)(2,1)S(1)} %get-tuple-element.39.refs_1_.refs_11_.pos_ref, bf16[512,128]{1,0:T(8,128)(2,1)S(1)} %get-tuple-element.40.coef_ref, bf16[1,512]{1,0:T(2,128)(2,1)S(1)} %get-tuple-element.41.refs_12_.spread_ref, ...), custom_call_target="tpu_custom_call" | custom-call | flops 1 | bytes 1 | tf_op jit(solution)/shard_map/finish/pallas_call | solution.py:330
  (53 shorter events, 7.3 us)
Async XLA Ops:
  0.6 12.3 %copy-start = (bf16[1024,512]{1,0:T(8,128)(2,1)S(1)}, bf16[1024,512]{1,0:T(8,128)(2,1)}, u32[]{:S(2)}) copy-start(bf16[1024,512]{1,0:T(8,128)(2,1)} %refs_4_.1) | copy-start | bytes 3145732
  0.6 19.7 %collective-permute-start.4 = (bf16[512,512]{1,0:T(8,128)(2,1)}, bf16[512,512]{1,0:T(8,128)(2,1)S(1)}, u32[]{:S(2)}, u32[]{:S(2)}) collective-permute-start(bf16[512,512]{1,0:T(8,128)(2,1)} %pos_ref), channel_id=1, source_target_pairs={{0,2},{1,3},{2,0},{3,1},{4,6},{5,7},{6,4},{7,5},{8,10},{9,11},{10,... | collective-permute-start | bytes 1572872 | tf_op jit(solution)/shard_map/ppermute | solution.py:20
  4.6 14.3 %collective-permute-start.6 = (bf16[256,512]{1,0:T(8,128)(2,1)S(1)}, bf16[256,512]{1,0:T(8,128)(2,1)S(1)}, u32[]{:S(2)}, u32[]{:S(2)}) collective-permute-start(bf16[256,512]{1,0:T(8,128)(2,1)S(1)} %constant_dynamic-slice_fusion.refs_0_.refs_13_.refs_1_), channel_id=1, source_target_pairs={{0,4},{4,0},{8,12},{12,8},{1,5},{5,1},{9,13},{13,9},{2,6},{6,2},{1... | collective-permute-start | bytes 786440 | tf_op jit(solution)/shard_map/ppermute | solution.py:20
  6.3 14.0 %collective-permute-start = (bf16[256,512]{1,0:T(8,128)(2,1)S(1)}, bf16[256,512]{1,0:T(8,128)(2,1)S(1)}, u32[]{:S(2)}, u32[]{:S(2)}) collective-permute-start(bf16[256,512]{1,0:T(8,128)(2,1)S(1)} %constant_dynamic-slice_fusion.refs_0_.refs_13_.refs_1_), channel_id=1, source_target_pairs={{0,8},{4,12},{8,0},{12,4},{1,9},{5,13},{9,1},{13,5},{2,10},{6,14},... | collective-permute-start | bytes 786440 | tf_op jit(solution)/shard_map/ppermute | solution.py:20
  9.5 1.0 %copy-start.1 = (bf16[512,512]{1,0:T(8,128)(2,1)S(1)}, bf16[512,512]{1,0:T(8,128)(2,1)}, u32[]{:S(2)}) copy-start(bf16[512,512]{1,0:T(8,128)(2,1)} %pos_ref) | copy-start | bytes 1572868
  10.6 0.9 %copy-start.5 = (bf16[512,128]{1,0:T(8,128)(2,1)S(1)}, bf16[512,128]{1,0:T(8,128)(2,1)}, u32[]{:S(2)}) copy-start(bf16[512,128]{1,0:T(8,128)(2,1)} %coef_ref.1) | copy-start | bytes 393220
  11.5 0.7 %copy-start.6 = (f32[128]{0:T(128)S(1)}, f32[128]{0:T(128)}, u32[]{:S(2)}) copy-start(f32[128]{0:T(128)} %param.10) | copy-start | bytes 1540
  12.3 6.6 %copy-start.2 = (bf16[512,512]{1,0:T(8,128)(2,1)S(1)}, bf16[512,512]{1,0:T(8,128)(2,1)}, u32[]{:S(2)}) copy-start(bf16[512,512]{1,0:T(8,128)(2,1)} %pos_ref) | copy-start | bytes 1572868
  12.4 6.6 %collective-permute-start.5 = (bf16[144,512]{1,0:T(8,128)(2,1)S(1)}, bf16[144,512]{1,0:T(8,128)(2,1)S(1)}, u32[]{:S(2)}, u32[]{:S(2)}) collective-permute-start(bf16[144,512]{1,0:T(8,128)(2,1)S(1)} %get-tuple-element.42.refs_2_), channel_id=1, source_target_pairs={{0,2},{1,3},{2,0},{3,1},{4,6},{5,7},{6,4},{7,5},{8,10},{9,11},{10,... | collective-permute-start | bytes 442376 | tf_op jit(solution)/shard_map/ppermute | solution.py:20
  13.0 6.0 %collective-permute-start.3 = (bf16[144,512]{1,0:T(8,128)(2,1)S(1)}, bf16[144,512]{1,0:T(8,128)(2,1)S(1)}, u32[]{:S(2)}, u32[]{:S(2)}) collective-permute-start(bf16[144,512]{1,0:T(8,128)(2,1)S(1)} %get-tuple-element.42.refs_2_), channel_id=1, source_target_pairs={{0,1},{1,0},{2,3},{3,2},{4,5},{5,4},{6,7},{7,6},{8,9},{9,8},{10,11... | collective-permute-start | bytes 442376 | tf_op jit(solution)/shard_map/ppermute | solution.py:20
  13.0 1.0 %copy-start.3 = (f32[1024,128]{1,0:T(8,128)S(1)}, f32[1024,128]{1,0:T(8,128)}, u32[]{:S(2)}) copy-start(f32[1024,128]{1,0:T(8,128)} %refs_0_.1) | copy-start | bytes 1572868
  14.0 1.0 %copy-start.4 = (f32[1024,128]{1,0:T(8,128)S(1)}, f32[1024,128]{1,0:T(8,128)}, u32[]{:S(2)}) copy-start(f32[1024,128]{1,0:T(8,128)} %refs_1_.1) | copy-start | bytes 1572868
  18.9 4.6 %collective-permute-start.2 = (bf16[512,512]{1,0:T(8,128)(2,1)S(1)}, bf16[512,512]{1,0:T(8,128)(2,1)S(1)}, u32[]{:S(2)}, u32[]{:S(2)}) collective-permute-start(bf16[512,512]{1,0:T(8,128)(2,1)S(1)} %copy-done.2), channel_id=1, source_target_pairs={{0,1},{1,0},{2,3},{3,2},{4,5},{5,4},{6,7},{7,6},{8,9},{9,8},{10,11... | collective-permute-start | bytes 1572872 | tf_op jit(solution)/shard_map/ppermute | solution.py:20
  20.3 3.3 %collective-permute-start.7 = (bf16[512,512]{1,0:T(8,128)(2,1)S(1)}, bf16[512,512]{1,0:T(8,128)(2,1)S(1)}, u32[]{:S(2)}, u32[]{:S(2)}) collective-permute-start(bf16[512,512]{1,0:T(8,128)(2,1)S(1)} %collective-permute-done.4.refs_5_), channel_id=1, source_target_pairs={{0,1},{1,0},{2,3},{3,2},{4,5},{5,4},{6,7},{7,6},{8,9},{9,8},{10,11... | collective-permute-start | bytes 1572872 | tf_op jit(solution)/shard_map/ppermute | solution.py:20
  20.3 2.1 %collective-permute-start.8 = (bf16[144,512]{1,0:T(8,128)(2,1)S(1)}, bf16[144,512]{1,0:T(8,128)(2,1)S(1)}, u32[]{:S(2)}, u32[]{:S(2)}) collective-permute-start(bf16[144,512]{1,0:T(8,128)(2,1)S(1)} %collective-permute-done.5.refs_6_), channel_id=1, source_target_pairs={{0,1},{1,0},{2,3},{3,2},{4,5},{5,4},{6,7},{7,6},{8,9},{9,8},{10,11... | collective-permute-start | bytes 442376 | tf_op jit(solution)/shard_map/ppermute | solution.py:20
  20.8 10.7 %collective-permute-start.1 = (bf16[256,512]{1,0:T(8,128)(2,1)S(1)}, bf16[256,512]{1,0:T(8,128)(2,1)S(1)}, u32[]{:S(2)}, u32[]{:S(2)}) collective-permute-start(bf16[256,512]{1,0:T(8,128)(2,1)S(1)} %collective-permute-done.refs_0_), channel_id=1, source_target_pairs={{0,4},{4,0},{8,12},{12,8},{1,5},{5,1},{9,13},{13,9},{2,6},{6,2},{1... | collective-permute-start | bytes 786440 | tf_op jit(solution)/shard_map/ppermute | solution.py:20
  22.4 23.4 %collective-permute-start.16 = (bf16[512,512]{1,0:T(8,128)(2,1)S(1)}, bf16[512,512]{1,0:T(8,128)(2,1)S(1)}, u32[]{:S(2)}, u32[]{:S(2)}) collective-permute-start(bf16[512,512]{1,0:T(8,128)(2,1)S(1)} %constant_dynamic-update-slice_fusion.refs_14_.refs_2_), channel_id=1, source_target_pairs={{0,2},{1,3},{2,0},{3,1},{4,6},{5,7},{6,4},{7,5},{8,10},{9,11},{10,... | collective-permute-start | bytes 1572872 | tf_op jit(solution)/shard_map/ppermute | solution.py:20
  24.9 9.8 %collective-permute-start.9 = (f32[256,128]{1,0:T(8,128)S(1)}, f32[256,128]{1,0:T(8,128)S(1)}, u32[]{:S(2)}, u32[]{:S(2)}) collective-permute-start(f32[256,128]{1,0:T(8,128)S(1)} %forward.3), channel_id=1, source_target_pairs={{0,8},{4,12},{8,0},{12,4},{1,9},{5,13},{9,1},{13,5},{2,10},{6,14},... | collective-permute-start | bytes 393224 | tf_op jit(solution)/shard_map/ppermute | solution.py:20
  28.9 5.8 %collective-permute-start.10 = (f32[256,128]{1,0:T(8,128)S(1)}, f32[256,128]{1,0:T(8,128)S(1)}, u32[]{:S(2)}, u32[]{:S(2)}) collective-permute-start(f32[256,128]{1,0:T(8,128)S(1)} %forward.4), channel_id=1, source_target_pairs={{0,4},{4,0},{8,12},{12,8},{1,5},{5,1},{9,13},{13,9},{2,6},{6,2},{1... | collective-permute-start | bytes 393224 | tf_op jit(solution)/shard_map/ppermute | solution.py:20
  32.8 6.8 %collective-permute-start.11 = (f32[256,128]{1,0:T(8,128)S(1)}, f32[256,128]{1,0:T(8,128)S(1)}, u32[]{:S(2)}, u32[]{:S(2)}) collective-permute-start(f32[256,128]{1,0:T(8,128)S(1)} %forward.5), channel_id=1, source_target_pairs={{0,12},{4,8},{8,4},{12,0},{1,13},{5,9},{9,5},{13,1},{2,14},{6,10},... | collective-permute-start | bytes 393224 | tf_op jit(solution)/shard_map/ppermute | solution.py:20
  34.7 9.1 %collective-permute-start.13 = (bf16[256,512]{1,0:T(8,128)(2,1)S(1)}, bf16[256,512]{1,0:T(8,128)(2,1)S(1)}, u32[]{:S(2)}, u32[]{:S(2)}) collective-permute-start(bf16[256,512]{1,0:T(8,128)(2,1)S(1)} %collective-permute-done.1.refs_0_.refs_15_.refs_3_), channel_id=1, source_target_pairs={{0,2},{1,3},{2,0},{3,1},{4,6},{5,7},{6,4},{7,5},{8,10},{9,11},{10,... | collective-permute-start | bytes 786440 | tf_op jit(solution)/shard_map/ppermute | solution.py:20
  39.8 7.6 %collective-permute-start.15 = (bf16[256,128]{1,0:T(8,128)(2,1)S(1)}, bf16[256,128]{1,0:T(8,128)(2,1)S(1)}, u32[]{:S(2)}, u32[]{:S(2)}) collective-permute-start(bf16[256,128]{1,0:T(8,128)(2,1)S(1)} %cotangent.1), channel_id=1, source_target_pairs={{0,8},{4,12},{8,0},{12,4},{1,9},{5,13},{9,1},{13,5},{2,10},{6,14},... | collective-permute-start | bytes 196616 | tf_op jit(solution)/shard_map/ppermute | solution.py:20
  42.4 5.0 %collective-permute-start.12 = (bf16[256,128]{1,0:T(8,128)(2,1)S(1)}, bf16[256,128]{1,0:T(8,128)(2,1)S(1)}, u32[]{:S(2)}, u32[]{:S(2)}) collective-permute-start(bf16[256,128]{1,0:T(8,128)(2,1)S(1)} %cotangent.1), channel_id=1, source_target_pairs={{0,4},{4,0},{8,12},{12,8},{1,5},{5,1},{9,13},{13,9},{2,6},{6,2},{1... | collective-permute-start | bytes 196616 | tf_op jit(solution)/shard_map/ppermute | solution.py:20
  43.8 4.3 %collective-permute-start.14 = (bf16[256,128]{1,0:T(8,128)(2,1)S(1)}, bf16[256,128]{1,0:T(8,128)(2,1)S(1)}, u32[]{:S(2)}, u32[]{:S(2)}) collective-permute-start(bf16[256,128]{1,0:T(8,128)(2,1)S(1)} %cotangent.1), channel_id=1, source_target_pairs={{0,2},{1,3},{2,0},{3,1},{4,6},{5,7},{6,4},{7,5},{8,10},{9,11},{10,... | collective-permute-start | bytes 196616 | tf_op jit(solution)/shard_map/ppermute | solution.py:20
  45.8 6.9 %collective-permute-start.19 = (bf16[256,512]{1,0:T(8,128)(2,1)S(1)}, bf16[256,512]{1,0:T(8,128)(2,1)S(1)}, u32[]{:S(2)}, u32[]{:S(2)}) collective-permute-start(bf16[256,512]{1,0:T(8,128)(2,1)S(1)} %collective-permute-done.1.refs_0_.refs_15_.refs_3_), channel_id=1, source_target_pairs={{0,1},{1,0},{2,3},{3,2},{4,5},{5,4},{6,7},{7,6},{8,9},{9,8},{10,11... | collective-permute-start | bytes 786440 | tf_op jit(solution)/shard_map/ppermute | solution.py:20
  45.8 7.2 %collective-permute-start.18 = (bf16[512,512]{1,0:T(8,128)(2,1)S(1)}, bf16[512,512]{1,0:T(8,128)(2,1)S(1)}, u32[]{:S(2)}, u32[]{:S(2)}) collective-permute-start(bf16[512,512]{1,0:T(8,128)(2,1)S(1)} %constant_dynamic-update-slice_fusion.refs_14_.refs_2_), channel_id=1, source_target_pairs={{0,1},{1,0},{2,3},{3,2},{4,5},{5,4},{6,7},{7,6},{8,9},{9,8},{10,11... | collective-permute-start | bytes 1572872 | tf_op jit(solution)/shard_map/ppermute | solution.py:20
  47.4 5.6 %collective-permute-start.21 = (bf16[512,512]{1,0:T(8,128)(2,1)S(1)}, bf16[512,512]{1,0:T(8,128)(2,1)S(1)}, u32[]{:S(2)}, u32[]{:S(2)}) collective-permute-start(bf16[512,512]{1,0:T(8,128)(2,1)S(1)} %collective-permute-done.16.refs_1_.refs_2_), channel_id=1, source_target_pairs={{0,1},{1,0},{2,3},{3,2},{4,5},{5,4},{6,7},{7,6},{8,9},{9,8},{10,11... | collective-permute-start | bytes 1572872 | tf_op jit(solution)/shard_map/ppermute | solution.py:20
  47.5 4.5 %collective-permute-start.17 = (bf16[256,128]{1,0:T(8,128)(2,1)S(1)}, bf16[256,128]{1,0:T(8,128)(2,1)S(1)}, u32[]{:S(2)}, u32[]{:S(2)}) collective-permute-start(bf16[256,128]{1,0:T(8,128)(2,1)S(1)} %collective-permute-done.15), channel_id=1, source_target_pairs={{0,4},{4,0},{8,12},{12,8},{1,5},{5,1},{9,13},{13,9},{2,6},{6,2},{1... | collective-permute-start | bytes 196616 | tf_op jit(solution)/shard_map/ppermute | solution.py:20
  52.0 1.6 %collective-permute-start.22 = (bf16[256,512]{1,0:T(8,128)(2,1)S(1)}, bf16[256,512]{1,0:T(8,128)(2,1)S(1)}, u32[]{:S(2)}, u32[]{:S(2)}) collective-permute-start(bf16[256,512]{1,0:T(8,128)(2,1)S(1)} %collective-permute-done.13.refs_2_.refs_3_), channel_id=1, source_target_pairs={{0,1},{1,0},{2,3},{3,2},{4,5},{5,4},{6,7},{7,6},{8,9},{9,8},{10,11... | collective-permute-start | bytes 786440 | tf_op jit(solution)/shard_map/ppermute | solution.py:20
  52.1 1.9 %collective-permute-start.20 = (bf16[1024,128]{1,0:T(8,128)(2,1)S(1)}, bf16[1024,128]{1,0:T(8,128)(2,1)S(1)}, u32[]{:S(2)}, u32[]{:S(2)}) collective-permute-start(bf16[1024,128]{1,0:T(8,128)(2,1)S(1)} %pad_maximum_fusion.refs_4_), channel_id=1, source_target_pairs={{0,1},{1,0},{2,3},{3,2},{4,5},{5,4},{6,7},{7,6},{8,9},{9,8},{10,11... | collective-permute-start | bytes 786440 | tf_op jit(solution)/shard_map/ppermute | solution.py:20
  52.6 6.9 %collective-permute-start.23 = (bf16[768,128]{1,0:T(8,128)(2,1)S(1)}, bf16[768,128]{1,0:T(8,128)(2,1)S(1)}, u32[]{:S(2)}, u32[]{:S(2)}) collective-permute-start(bf16[768,128]{1,0:T(8,128)(2,1)S(1)} %constant_dynamic-update-slice_fusion.2), channel_id=1, source_target_pairs={{0,2},{1,3},{2,0},{3,1},{4,6},{5,7},{6,4},{7,5},{8,10},{9,11},{10,... | collective-permute-start | bytes 589832 | tf_op jit(solution)/shard_map/ppermute | solution.py:20
  59.6 1.6 %collective-permute-start.24 = (bf16[1024,128]{1,0:T(8,128)(2,1)S(1)}, bf16[1024,128]{1,0:T(8,128)(2,1)S(1)}, u32[]{:S(2)}, u32[]{:S(2)}) collective-permute-start(bf16[1024,128]{1,0:T(8,128)(2,1)S(1)} %constant_dynamic-update-slice_fusion.5.refs_4_), channel_id=1, source_target_pairs={{0,1},{1,0},{2,3},{3,2},{4,5},{5,4},{6,7},{7,6},{8,9},{9,8},{10,11... | collective-permute-start | bytes 786440 | tf_op jit(solution)/shard_map/ppermute | solution.py:20
